TPU v7x, 32 devices: a whole 2x2x4 slice. The times are simulated.
32 devices in a mesh: fsdp: 4 (over y, core), ctx: 2 (over x), tp: 4 (over z).
Axes of the slice: x: 2, y: 2, z: 4, core: 2. Of those that a mesh axis runs over, the one named last changes fastest.
Arguments:
- hidden_in: bfloat16 [4096, 2304], P(('fsdp', 'ctx')), may hold values from -36 to 36
- cotangent: bfloat16 [4096, 2304], P(('fsdp', 'ctx')), may hold values from -6 to 6
- segment_ids: int32 [4096], P('fsdp'), may hold values from -1 to 4, as said below
- pre_attention_gain: float32 [2304], replicated, may hold values from 0.25 to 1.75
- post_attention_gain: float32 [2304], replicated, may hold values from 0.25 to 1.75
- pre_feedforward_gain: float32 [2304], replicated, may hold values from 0.25 to 1.75
- post_feedforward_gain: float32 [2304], replicated, may hold values from 0.25 to 1.75
- query_weight: bfloat16 [2304, 2048], P(('fsdp', 'ctx'), 'tp'), may hold values from -0.3125 to 0.3125
- key_weight: bfloat16 [2304, 1024], P(('fsdp', 'ctx'), 'tp'), may hold values from -0.3125 to 0.3125
- value_weight: bfloat16 [2304, 1024], P(('fsdp', 'ctx'), 'tp'), may hold values from -0.125 to 0.125
- output_weight: bfloat16 [2304, 2048], P(('fsdp', 'ctx'), 'tp'), may hold values from -0.125 to 0.125
- gate_weight: bfloat16 [2304, 9216], P(('fsdp', 'ctx'), 'tp'), may hold values from -0.125 to 0.125
- up_weight: bfloat16 [2304, 9216], P(('fsdp', 'ctx'), 'tp'), may hold values from -0.125 to 0.125
- down_weight: bfloat16 [2304, 9216], P(('fsdp', 'ctx'), 'tp'), may hold values from -0.0625 to 0.0625
Outputs:
- hidden_out: bfloat16 [4096, 2304], P(('fsdp', 'ctx'))
- grad_hidden_in: bfloat16 [4096, 2304], P(('fsdp', 'ctx'))
- grad_pre_attention_gain: float32 [2304], P(('fsdp', 'ctx'))
- grad_post_attention_gain: float32 [2304], P(('fsdp', 'ctx'))
- grad_pre_feedforward_gain: float32 [2304], P(('fsdp', 'ctx'))
- grad_post_feedforward_gain: float32 [2304], P(('fsdp', 'ctx'))
- grad_query_weight: float32 [2304, 2048], P(('fsdp', 'ctx'), 'tp')
- grad_key_weight: float32 [2304, 1024], P(('fsdp', 'ctx'), 'tp')
- grad_value_weight: float32 [2304, 1024], P(('fsdp', 'ctx'), 'tp')
- grad_output_weight: float32 [2304, 2048], P(('fsdp', 'ctx'), 'tp')
- grad_gate_weight: float32 [2304, 9216], P(('fsdp', 'ctx'), 'tp')
- grad_up_weight: float32 [2304, 9216], P(('fsdp', 'ctx'), 'tp')
- grad_down_weight: float32 [2304, 9216], P(('fsdp', 'ctx'), 'tp')
Inputs may be any that keep to these rules, and one draw needn't show every extreme that they name: `segment_ids`: within each group of 1024 tokens document ids increase in order, though some numbers (including 0) may be absent; each begins at a block's start, covers 1 to 4 blocks of 128 tokens with its padding (-1) only at the end of its last block, and never leaves its group; every group holds a document of 512 tokens and a block of padding only among its first 5 blocks.
All inputs are finite; a program needn't handle non-finite values.
Results may differ from a plain program's by a relative error of at most 0.022.
The roundings to bfloat16 on the way count: a program that leaves them out, or rounds other values in their place, can miss the bound.
Values may be sent and summed in bfloat16 or wider, within the bound.
No kernel may reach another device: no remote copies, remote signals or barrier semaphores. Data moves between devices by JAX's collectives and lax.ppermute only.
A program may use at most 256 MiB of HBM per device.

v0:
```python
import jax
import jax.numpy as jnp
from jax import lax
from jax.sharding import PartitionSpec as P

HD = 256


CAP = 50.0
EPS = 1e-06


def passed_along(block, axis, distance):
    devices = range(lax.axis_size(axis))
    route = [(i - distance, i) for i in devices if i - distance in devices]
    return lax.ppermute(block, axis, route)


def rms(value, gain):
    return value * lax.rsqrt(jnp.mean(value * value, axis=-1, keepdims=True) + EPS) * gain


def geglu(gate_value, up_value):
    return jax.nn.gelu(gate_value, approximate=True) * up_value


def product(left, right):
    return jnp.dot(left, right, preferred_element_type=jnp.float32)


def rows_product(left, right):
    return lax.dot_general(
        left, right, (((0,), (0,)), ((), ())), preferred_element_type=jnp.float32
    )


def transposed_product(left, right):
    return lax.dot_general(
        left, right, (((1,), (1,)), ((), ())), preferred_element_type=jnp.float32
    )


def attention_scores(queries, keys_all, allowed, scaling):
    scores = (
        jnp.einsum("qgrd,kgd->grqk", queries, keys_all, preferred_element_type=jnp.float32)
        * scaling
    )
    capped = CAP * jnp.tanh(scores / CAP)
    powers = jnp.where(allowed[None, None], jnp.exp(capped), 0.0)
    return (scores, powers)


def shards(
    hidden_in,
    cotangent,
    segment_ids,
    pre_attention_gain,
    post_attention_gain,
    pre_feedforward_gain,
    post_feedforward_gain,
    query_weight,
    key_weight,
    value_weight,
    output_weight,
    gate_weight,
    up_weight,
    down_weight,
):
    query_full, key_full, value_full, output_full, gate_full, up_full, down_full = (
        lax.all_gather(query_weight, ("fsdp", "ctx"), axis=0, tiled=True),
        lax.all_gather(key_weight, ("fsdp", "ctx"), axis=0, tiled=True),
        lax.all_gather(value_weight, ("fsdp", "ctx"), axis=0, tiled=True),
        lax.all_gather(output_weight, ("fsdp", "ctx"), axis=0, tiled=True),
        lax.all_gather(gate_weight, ("fsdp", "ctx"), axis=0, tiled=True),
        lax.all_gather(up_weight, ("fsdp", "ctx"), axis=0, tiled=True),
        lax.all_gather(down_weight, ("fsdp", "ctx"), axis=0, tiled=True),
    )
    length = hidden_in.shape[0]
    kv_heads = key_weight.shape[1] // HD
    repeats = query_weight.shape[1] // key_weight.shape[1]
    scaling = HD ** (-0.5)
    position = lax.axis_index("ctx")
    own_ids = lax.dynamic_slice_in_dim(segment_ids, position * length, length)
    prev_start = jnp.maximum(position - 1, 0) * length
    prev_ids = jnp.where(
        position > 0, lax.dynamic_slice_in_dim(segment_ids, prev_start, length), -2
    )
    key_ids = jnp.concatenate([prev_ids, own_ids])
    query_pos = jnp.arange(length, dtype=jnp.int32)
    key_pos = jnp.arange(2 * length, dtype=jnp.int32) - length
    allowed = (query_pos[:, None] == key_pos[None, :]) | (own_ids[:, None] == key_ids[None, :]) & (
        own_ids[:, None] >= 0
    ) & (key_pos[None, :] < query_pos[:, None])
    inputs = hidden_in.astype(jnp.float32)
    normed_one = rms(inputs, pre_attention_gain).astype(jnp.bfloat16)
    query_low = product(normed_one, query_full).astype(jnp.bfloat16)
    key_low = product(normed_one, key_full).astype(jnp.bfloat16)
    value_low = product(normed_one, value_full).astype(jnp.bfloat16)
    key_prev, value_prev = passed_along((key_low, value_low), "ctx", 1)
    keys_all = jnp.concatenate([key_prev, key_low], axis=0).reshape(2 * length, kv_heads, HD)
    values_all = jnp.concatenate([value_prev, value_low], axis=0).reshape(2 * length, kv_heads, HD)
    queries = query_low.reshape(length, kv_heads, repeats, HD)
    scores, powers = attention_scores(queries, keys_all, allowed, scaling)
    totals = jnp.sum(powers, axis=-1, keepdims=True)
    probs_low = (powers / totals).astype(jnp.bfloat16)
    attended = jnp.einsum(
        "grqk,kgd->qgrd", probs_low, values_all, preferred_element_type=jnp.float32
    )
    attended_low = attended.reshape(length, -1).astype(jnp.bfloat16)
    branch_one = lax.psum(transposed_product(attended_low, output_full), "tp")
    middle = inputs + rms(branch_one, post_attention_gain)
    normed_two = rms(middle, pre_feedforward_gain).astype(jnp.bfloat16)
    gate_value = product(normed_two, gate_full)
    up_value = product(normed_two, up_full)
    hidden_low = geglu(gate_value, up_value).astype(jnp.bfloat16)
    branch_two = lax.psum(transposed_product(hidden_low, down_full), "tp")
    result = middle + rms(branch_two, post_feedforward_gain)
    upstream = cotangent.astype(jnp.float32)
    query_full, key_full, value_full, output_full, gate_full, up_full, down_full = (
        lax.all_gather(query_weight, ("fsdp", "ctx"), axis=0, tiled=True),
        lax.all_gather(key_weight, ("fsdp", "ctx"), axis=0, tiled=True),
        lax.all_gather(value_weight, ("fsdp", "ctx"), axis=0, tiled=True),
        lax.all_gather(output_weight, ("fsdp", "ctx"), axis=0, tiled=True),
        lax.all_gather(gate_weight, ("fsdp", "ctx"), axis=0, tiled=True),
        lax.all_gather(up_weight, ("fsdp", "ctx"), axis=0, tiled=True),
        lax.all_gather(down_weight, ("fsdp", "ctx"), axis=0, tiled=True),
    )
    unused_four, pull_four = jax.vjp(rms, branch_two, post_feedforward_gain)
    grad_branch_two, grad_gain_four = pull_four(upstream)
    grad_two_low = grad_branch_two.astype(jnp.bfloat16)
    grad_hidden_units = product(grad_two_low, down_full)
    unused_glu, pull_glu = jax.vjp(geglu, gate_value, up_value)
    grad_gate, grad_up = pull_glu(grad_hidden_units)
    grad_gate_low = grad_gate.astype(jnp.bfloat16)
    grad_up_low = grad_up.astype(jnp.bfloat16)
    grad_down_full = rows_product(grad_two_low, hidden_low)
    grad_gate_full = rows_product(normed_two, grad_gate_low)
    grad_up_full = rows_product(normed_two, grad_up_low)
    grad_normed_two = lax.psum(
        transposed_product(grad_gate_low, gate_full) + transposed_product(grad_up_low, up_full),
        "tp",
    )
    unused_three, pull_three = jax.vjp(rms, middle, pre_feedforward_gain)
    grad_middle_norm, grad_gain_three = pull_three(grad_normed_two)
    grad_middle = upstream + grad_middle_norm
    unused_two, pull_two = jax.vjp(rms, branch_one, post_attention_gain)
    grad_branch_one, grad_gain_two = pull_two(grad_middle)
    grad_one_low = grad_branch_one.astype(jnp.bfloat16)
    grad_output_full = rows_product(grad_one_low, attended_low)
    grad_attended = (
        product(grad_one_low, output_full)
        .astype(jnp.bfloat16)
        .reshape(length, kv_heads, repeats, HD)
    )
    scores, powers = attention_scores(queries, keys_all, allowed, scaling)
    probs = powers / totals
    probs_low = probs.astype(jnp.bfloat16)
    grad_probs = jnp.einsum(
        "qgrd,kgd->grqk", grad_attended, values_all, preferred_element_type=jnp.float32
    )
    inner = jnp.sum(probs * grad_probs, axis=-1, keepdims=True)
    grad_capped = probs * (grad_probs - inner)
    squashed = jnp.tanh(scores / CAP)
    grad_scores = (grad_capped * (1.0 - squashed * squashed)).astype(jnp.bfloat16)
    grad_query_low = (
        (
            jnp.einsum("grqk,kgd->qgrd", grad_scores, keys_all, preferred_element_type=jnp.float32)
            * scaling
        )
        .reshape(length, -1)
        .astype(jnp.bfloat16)
    )
    grad_keys_all = (
        jnp.einsum("grqk,qgrd->kgd", grad_scores, queries, preferred_element_type=jnp.float32)
        * scaling
    )
    grad_values_all = jnp.einsum(
        "grqk,qgrd->kgd", probs_low, grad_attended, preferred_element_type=jnp.float32
    )
    grad_key_back, grad_value_back = (
        passed_along(grad_keys_all[:length].astype(jnp.bfloat16), "ctx", -1).astype(jnp.float32),
        passed_along(grad_values_all[:length].astype(jnp.bfloat16), "ctx", -1).astype(jnp.float32),
    )
    grad_key_low = (grad_keys_all[length:] + grad_key_back).reshape(length, -1).astype(jnp.bfloat16)
    grad_value_low = (
        (grad_values_all[length:] + grad_value_back).reshape(length, -1).astype(jnp.bfloat16)
    )
    grad_query_full = rows_product(normed_one, grad_query_low)
    grad_key_full = rows_product(normed_one, grad_key_low)
    grad_value_full = rows_product(normed_one, grad_value_low)
    grad_normed_one = lax.psum(
        (
            transposed_product(grad_query_low, query_full)
            + transposed_product(grad_key_low, key_full)
            + transposed_product(grad_value_low, value_full)
        ).astype(jnp.bfloat16),
        "tp",
    ).astype(jnp.float32)
    unused_one, pull_one = jax.vjp(rms, inputs, pre_attention_gain)
    grad_inputs_norm, grad_gain_one = pull_one(grad_normed_one)
    grad_inputs = grad_middle + grad_inputs_norm
    every_share = tuple(
        (
            lax.psum_scatter(
                grad_query_full.astype(jnp.bfloat16),
                ("fsdp", "ctx"),
                scatter_dimension=0,
                tiled=True,
            ).astype(jnp.float32),
            lax.psum_scatter(
                grad_key_full.astype(jnp.bfloat16), ("fsdp", "ctx"), scatter_dimension=0, tiled=True
            ).astype(jnp.float32),
            lax.psum_scatter(
                grad_value_full.astype(jnp.bfloat16),
                ("fsdp", "ctx"),
                scatter_dimension=0,
                tiled=True,
            ).astype(jnp.float32),
            lax.psum_scatter(
                grad_output_full.astype(jnp.bfloat16),
                ("fsdp", "ctx"),
                scatter_dimension=0,
                tiled=True,
            ).astype(jnp.float32),
            lax.psum_scatter(
                grad_gate_full.astype(jnp.bfloat16),
                ("fsdp", "ctx"),
                scatter_dimension=0,
                tiled=True,
            ).astype(jnp.float32),
            lax.psum_scatter(
                grad_up_full.astype(jnp.bfloat16), ("fsdp", "ctx"), scatter_dimension=0, tiled=True
            ).astype(jnp.float32),
            lax.psum_scatter(
                grad_down_full.astype(jnp.bfloat16),
                ("fsdp", "ctx"),
                scatter_dimension=0,
                tiled=True,
            ).astype(jnp.float32),
            lax.psum_scatter(
                jnp.stack([grad_gain_one, grad_gain_two, grad_gain_three, grad_gain_four]).astype(
                    jnp.bfloat16
                ),
                ("fsdp", "ctx"),
                scatter_dimension=1,
                tiled=True,
            ).astype(jnp.float32),
        )
    )
    gain_shares = every_share[7]
    weight_shares = every_share[:7]
    return (
        result.astype(jnp.bfloat16),
        grad_inputs.astype(jnp.bfloat16),
        gain_shares[0],
        gain_shares[1],
        gain_shares[2],
        gain_shares[3],
    ) + tuple(weight_shares)


def solution(mesh):
    return jax.shard_map(
        shards,
        mesh=mesh,
        in_specs=(
            P(("fsdp", "ctx"), None),
            P(("fsdp", "ctx"), None),
            P("fsdp"),
            P(),
            P(),
            P(),
            P(),
            P(("fsdp", "ctx"), "tp"),
            P(("fsdp", "ctx"), "tp"),
            P(("fsdp", "ctx"), "tp"),
            P(("fsdp", "ctx"), "tp"),
            P(("fsdp", "ctx"), "tp"),
            P(("fsdp", "ctx"), "tp"),
            P(("fsdp", "ctx"), "tp"),
        ),
        out_specs=(
            P(("fsdp", "ctx"), None),
            P(("fsdp", "ctx"), None),
            P(("fsdp", "ctx")),
            P(("fsdp", "ctx")),
            P(("fsdp", "ctx")),
            P(("fsdp", "ctx")),
            P(("fsdp", "ctx"), "tp"),
            P(("fsdp", "ctx"), "tp"),
            P(("fsdp", "ctx"), "tp"),
            P(("fsdp", "ctx"), "tp"),
            P(("fsdp", "ctx"), "tp"),
            P(("fsdp", "ctx"), "tp"),
            P(("fsdp", "ctx"), "tp"),
        ),
        check_vma=False,
    )
```

profile of v0, /device:TPU:0, one launch (start us, length us, event | category | flops | bytes accessed | tf_op | source)
XLA Modules:
  0.0 1507.4 jit_solution(7365926386257940180)
XLA Ops:
  15.4 21.2 %all-gather.8.cloned.1.call-done = bf16[2304,256]{1,0:T(8,128)(2,1)} async-done(((bf16[288,256]{1,0:T(8,128)(2,1)}), bf16[2304,256]{1,0:T(8,128)(2,1)}) %all-gather.8.cloned.1.call-update) | async-done | bytes 1179664 | tf_op jit(solution)/shard_map/all_gather | solution.py:72
  36.5 3.5 convolution_convert_fusion.10
  40.1 4.1 collective-permute-start
  44.1 19.7 %all-gather.10.cloned.1.call-done = bf16[2304,256]{1,0:T(8,128)(2,1)} async-done(((bf16[288,256]{1,0:T(8,128)(2,1)}), bf16[2304,256]{1,0:T(8,128)(2,1)}) %all-gather.10.cloned.1.call-update) | async-done | bytes 1179664 | tf_op jit(solution)/shard_map/all_gather | solution.py:71
  66.0 3.4 collective-permute-start.1
  69.4 25.6 %all-gather.12.cloned.1.call-done = bf16[2304,512]{1,0:T(8,128)(2,1)} async-done(((bf16[288,512]{1,0:T(8,128)(2,1)}), bf16[2304,512]{1,0:T(8,128)(2,1)}) %all-gather.12.cloned.1.call-update) | async-done | bytes 2359312 | tf_op jit(solution)/shard_map/all_gather | solution.py:70
  95.0 3.2 convolution_convert_fusion.8
  104.7 20.9 %all-gather.14.cloned.1.call-done = bf16[2304,512]{1,0:T(8,128)(2,1)} async-done(((bf16[288,512]{1,0:T(8,128)(2,1)}), bf16[2304,512]{1,0:T(8,128)(2,1)}) %all-gather.14.cloned.1.call-update) | async-done | bytes 2359312 | tf_op jit(solution)/shard_map/all_gather | solution.py:73
  125.6 5.3 fusion.70
  133.3 169.7 %all-reduce.5.cloned.1.call-done = f32[512,2304]{1,0:T(8,128)} async-done(((f32[512,2304]{1,0:T(8,128)}), f32[512,2304]{1,0:T(8,128)}) %all-reduce.5.cloned.1.call-update) | async-done | bytes 4718608 | tf_op jit(solution)/shard_map/psum | solution.py:110
  303.0 2.9 multiply_reduce_fusion.6
  310.6 56.9 %all-gather.16.cloned.1.call-done = bf16[2304,2304]{1,0:T(8,128)(2,1)} async-done(((bf16[288,2304]{1,0:T(8,128)(2,1)}), bf16[2304,2304]{1,0:T(8,128)(2,1)}) %all-gather.16.cloned.1.call-update) | async-done | bytes 10616848 | tf_op jit(solution)/shard_map/all_gather | solution.py:74
  367.4 11.3 fusion.71
  378.7 54.3 %all-gather.18.cloned.1.call-done = bf16[2304,2304]{1,0:T(8,128)(2,1)} async-done(((bf16[288,2304]{1,0:T(8,128)(2,1)}), bf16[2304,2304]{1,0:T(8,128)(2,1)}) %all-gather.18.cloned.1.call-update) | async-done | bytes 10616848 | tf_op jit(solution)/shard_map/all_gather | solution.py:75
  433.0 12.5 multiply_convert_fusion.1
  445.5 53.1 %all-gather.20.cloned.1.call-done = bf16[2304,2304]{1,0:T(8,128)(2,1)} async-done(((bf16[288,2304]{1,0:T(8,128)(2,1)}), bf16[2304,2304]{1,0:T(8,128)(2,1)}) %all-gather.20.cloned.1.call-update) | async-done | bytes 10616848 | tf_op jit(solution)/shard_map/all_gather | solution.py:76
  498.6 11.7 fusion.72
  510.8 171.7 %all-reduce.7.cloned.1.call-done = f32[512,2304]{1,0:T(8,128)} async-done(((f32[512,2304]{1,0:T(8,128)}), f32[512,2304]{1,0:T(8,128)}) %all-reduce.7.cloned.1.call-update) | async-done | bytes 4718608 | tf_op jit(solution)/shard_map/psum | solution.py:116
  682.5 2.9 multiply_reduce_fusion.4
  687.7 5.1 fusion.15
  692.8 14.7 multiply_convert_fusion
  707.6 7.3 fusion.73
  714.9 12.4 convolution_add_fusion.2
  727.5 170.9 %all-reduce.9.cloned.1.call-done = f32[512,2304]{1,0:T(8,128)} async-done(((f32[512,2304]{1,0:T(8,128)}), f32[512,2304]{1,0:T(8,128)}) %all-reduce.9.cloned.1.call-update) | async-done | bytes 4718608 | tf_op jit(solution)/shard_map/psum | solution.py:139
  898.4 5.1 multiply_reduce_fusion
  903.5 5.5 multiply_reduce_fusion.1
  918.5 2.8 fusion.23
  928.7 5.3 collective-permute-done.2
  937.9 3.2 convolution_convert_fusion.5
  941.2 3.1 convolution_convert_fusion.6
  944.4 86.5 %all-reduce.11.cloned.1.call-done = bf16[512,2304]{1,0:T(8,128)(2,1)} async-done(((bf16[512,2304]{1,0:T(8,128)(2,1)}), bf16[512,2304]{1,0:T(8,128)(2,1)}) %all-reduce.11.cloned.1.call-update) | async-done | bytes 2359312 | tf_op jit(solution)/shard_map/psum | solution.py:191
  1030.9 3.6 fusion.6
  1035.8 4.6 convolution_convert_fusion.3
  1040.5 3.0 convolution_convert_fusion.4
  1043.9 10.3 convolution_convert_fusion.1
  1054.3 10.4 convolution_convert_fusion.2
  1064.7 10.4 convolution_convert_fusion
  1076.8 32.9 %reduce-scatter.13.cloned.1.call-done = bf16[288,256]{1,0:T(8,128)(2,1)} async-done(((bf16[2304,256]{1,0:T(8,128)(2,1)}), bf16[288,256]{1,0:T(8,128)(2,1)}) %reduce-scatter.13.cloned.1.call-update) | async-done | bytes 147472 | tf_op jit(solution)/shard_map/reduce_scatter | solution.py:210
  1111.3 5.9 fusion.18
  1117.2 30.4 %reduce-scatter.25.cloned.1.call-done = bf16[288,4]{1,0:T(8,128)(2,1)} async-done(((bf16[2304,4]{1,0:T(8,128)(2,1)}), bf16[288,4]{1,0:T(8,128)(2,1)}) %reduce-scatter.25.cloned.1.call-update) | async-done | bytes 2320
  1149.2 44.0 %reduce-scatter.17.cloned.1.call-done = bf16[288,512]{1,0:T(8,128)(2,1)} async-done(((bf16[2304,512]{1,0:T(8,128)(2,1)}), bf16[288,512]{1,0:T(8,128)(2,1)}) %reduce-scatter.17.cloned.1.call-update) | async-done | bytes 294928 | tf_op jit(solution)/shard_map/reduce_scatter | solution.py:219
  1195.0 44.3 %reduce-scatter.11.cloned.1.call-done = bf16[288,512]{1,0:T(8,128)(2,1)} async-done(((bf16[2304,512]{1,0:T(8,128)(2,1)}), bf16[288,512]{1,0:T(8,128)(2,1)}) %reduce-scatter.11.cloned.1.call-update) | async-done | bytes 294928 | tf_op jit(solution)/shard_map/reduce_scatter | solution.py:204
  1241.2 84.1 %reduce-scatter.21.cloned.1.call-done = bf16[288,2304]{1,0:T(8,128)(2,1)} async-done(((bf16[2304,2304]{1,0:T(8,128)(2,1)}), bf16[288,2304]{1,0:T(8,128)(2,1)}) %reduce-scatter.21.cloned.1.call-update) | async-done | bytes 1327120 | tf_op jit(solution)/shard_map/reduce_scatter | solution.py:231
  1325.3 3.0 convert_element_type.193
  1328.3 83.0 %reduce-scatter.19.cloned.1.call-done = bf16[288,2304]{1,0:T(8,128)(2,1)} async-done(((bf16[2304,2304]{1,0:T(8,128)(2,1)}), bf16[288,2304]{1,0:T(8,128)(2,1)}) %reduce-scatter.19.cloned.1.call-update) | async-done | bytes 1327120 | tf_op jit(solution)/shard_map/reduce_scatter | solution.py:225
  1411.3 3.0 convert_element_type.191
  1414.3 83.2 %reduce-scatter.23.cloned.1.call-done = bf16[288,2304]{1,0:T(8,128)(2,1)} async-done(((bf16[2304,2304]{1,0:T(8,128)(2,1)}), bf16[288,2304]{1,0:T(8,128)(2,1)}) %reduce-scatter.23.cloned.1.call-update) | async-done | bytes 1327120 | tf_op jit(solution)/shard_map/reduce_scatter | solution.py:234
  1497.4 3.0 convert_element_type.195
  (184 shorter events, 57.7 us)
Async XLA Ops:
  7.2 29.4 %all-gather.8.cloned.1.call-start = ((), (), s32[]{:S(2)}) async-start(), calls=%async_computation.8 | async-start | bytes 1327104 | tf_op jit(solution)/shard_map/all_gather | solution.py:72
  7.9 55.9 %all-gather.10.cloned.1.call-start = ((), (), s32[]{:S(2)}) async-start(), calls=%async_computation.9 | async-start | bytes 1327104 | tf_op jit(solution)/shard_map/all_gather | solution.py:71
  8.7 86.3 %all-gather.12.cloned.1.call-start = ((), (), s32[]{:S(2)}) async-start(), calls=%async_computation.10 | async-start | bytes 2654208 | tf_op jit(solution)/shard_map/all_gather | solution.py:70
  9.4 116.2 %all-gather.14.cloned.1.call-start = ((), (), s32[]{:S(2)}) async-start(), calls=%async_computation.11 | async-start | bytes 2654208 | tf_op jit(solution)/shard_map/all_gather | solution.py:73
  10.0 293.0 %all-reduce.5.cloned.1.call-start = ((), (), s32[]{:S(2)}) async-start(), calls=%async_computation.12 | async-start | bytes 9437184 | tf_op jit(solution)/shard_map/psum | solution.py:110
  13.8 81.2 %copy-start.31 = (f32[512]{0:T(512)}, f32[512]{0:T(512)S(1)}, u32[]{:S(2)}) copy-start(f32[512]{0:T(512)S(1)} %fusion.50) | copy-start | bytes 6148
  15.4 48.5 %copy-start.4 = (bf16[512,2304]{1,0:T(8,128)(2,1)S(1)}, bf16[512,2304]{1,0:T(8,128)(2,1)}, u32[]{:S(2)}) copy-start(bf16[512,2304]{1,0:T(8,128)(2,1)} %param.14) | copy-start | bytes 7077892
  15.4 48.5 %copy-start.29 = (f32[2304]{0:T(1024)S(1)}, f32[2304]{0:T(1024)}, u32[]{:S(2)}) copy-start(f32[2304]{0:T(1024)} %param.17) | copy-start | bytes 27652
  40.1 59.7 %collective-permute-start = (bf16[512,256]{1,0:T(8,128)(2,1)}, bf16[512,256]{1,0:T(8,128)(2,1)}, u32[]{:S(2)}, u32[]{:S(2)}) collective-permute-start(bf16[512,256]{1,0:T(8,128)(2,1)} %convolution_convert_fusion.10), channel_id=1, source_target_pairs={{0,4},{1,5},{2,6},{3,7},{8,12},{9,13},{10,14},{11,15},{16,20},{17,... | collective-permute-start | bytes 786440 | tf_op jit(solution)/shard_map/ppermute | solution.py:16
  66.0 32.2 %copy-start.35 = (bf16[512,256]{1,0:T(8,128)(2,1)}, bf16[512,256]{1,0:T(8,128)(2,1)S(1)}, u32[]{:S(2)}) copy-start(bf16[512,256]{1,0:T(8,128)(2,1)S(1)} %convolution_convert_fusion.9) | copy-start | bytes 786436
  66.0 32.2 %collective-permute-start.1 = (bf16[512,256]{1,0:T(8,128)(2,1)S(1)}, bf16[512,256]{1,0:T(8,128)(2,1)S(1)}, u32[]{:S(2)}, u32[]{:S(2)}) collective-permute-start(bf16[512,256]{1,0:T(8,128)(2,1)S(1)} %convolution_convert_fusion.9), channel_id=1, source_target_pairs={{0,4},{1,5},{2,6},{3,7},{8,12},{9,13},{10,14},{11,15},{16,20},{17,... | collective-permute-start | bytes 786440 | tf_op jit(solution)/shard_map/ppermute | solution.py:16
  104.7 26.2 %copy-start.20 = (bf16[256,2,512]{2,0,1:T(8,128)(2,1)}, bf16[256,2,512]{2,0,1:T(8,128)(2,1)S(1)}, u32[]{:S(2)}) copy-start(bf16[256,2,512]{2,0,1:T(8,128)(2,1)S(1)} %fusion.40) | copy-start | bytes 1572868
  130.9 175.0 %copy-start.27 = (f32[2304]{0:T(1024)S(1)}, f32[2304]{0:T(1024)}, u32[]{:S(2)}) copy-start(f32[2304]{0:T(1024)} %param.18) | copy-start | bytes 27652
  130.9 236.5 %all-gather.16.cloned.1.call-start = ((), (), s32[]{:S(2)}) async-start(), calls=%async_computation.13 | async-start | bytes 11943936 | tf_op jit(solution)/shard_map/all_gather | solution.py:74
  131.5 301.5 %all-gather.18.cloned.1.call-start = ((), (), s32[]{:S(2)}) async-start(), calls=%async_computation.14 | async-start | bytes 11943936 | tf_op jit(solution)/shard_map/all_gather | solution.py:75
  132.3 366.3 %all-gather.20.cloned.1.call-start = ((), (), s32[]{:S(2)}) async-start(), calls=%async_computation.15 | async-start | bytes 11943936 | tf_op jit(solution)/shard_map/all_gather | solution.py:76
  133.0 549.5 %all-reduce.7.cloned.1.call-start = ((), (), s32[]{:S(2)}) async-start(), calls=%async_computation.16 | async-start | bytes 9437184 | tf_op jit(solution)/shard_map/psum | solution.py:116
  310.5 122.5 %copy-start.12 = (bf16[512,2304]{1,0:T(8,128)(2,1)}, bf16[512,2304]{1,0:T(8,128)(2,1)S(1)}, u32[]{:S(2)}) copy-start(bf16[512,2304]{1,0:T(8,128)(2,1)S(1)} %multiply_convert_fusion.2) | copy-start | bytes 7077892
  510.3 175.0 %copy-start.6 = (bf16[512,2304]{1,0:T(8,128)(2,1)S(1)}, bf16[512,2304]{1,0:T(8,128)(2,1)}, u32[]{:S(2)}) copy-start(bf16[512,2304]{1,0:T(8,128)(2,1)} %param.15) | copy-start | bytes 7077892
  510.3 175.0 %copy-start.28 = (f32[2304]{0:T(1024)S(1)}, f32[2304]{0:T(1024)}, u32[]{:S(2)}) copy-start(f32[2304]{0:T(1024)} %param.20) | copy-start | bytes 27652
  510.4 388.0 %all-reduce.9.cloned.1.call-start = ((), (), s32[]{:S(2)}) async-start(), calls=%async_computation.17 | async-start | bytes 9437184 | tf_op jit(solution)/shard_map/psum | solution.py:139
  686.2 6.5 slice-start.5
  687.7 5.1 slice-start.6
  687.7 19.8 %slice-start.2 = ((s8[10616832]{0:T(1024)(128)(4,1)}), s8[4194304]{0:T(1024)(128)(4,1)S(1)}, s32[]{:S(2)}) async-start(s8[10616832]{0:T(1024)(128)(4,1)} %bitcast.151), calls=%async_computation.29 | async-start | bytes 8388608
  692.8 14.8 copy-start.10
  692.8 14.8 slice-start.3
  692.8 14.8 slice-start.4
  707.5 7.3 copy-start.39
  727.3 303.7 %all-reduce.11.cloned.1.call-start = ((), (), s32[]{:S(2)}) async-start(), calls=%async_computation.18 | async-start | bytes 4718592 | tf_op jit(solution)/shard_map/psum | solution.py:191
  898.4 5.1 copy-start.7
  898.4 10.6 slice-start
  903.5 5.5 slice-start.1
  917.2 17.7 %copy-start.17 = (f32[1024,1,256]{0,2,1:T(8,128)}, f32[1024,1,256]{0,2,1:T(8,128)S(1)}, u32[]{:S(2)}) copy-start(f32[1024,1,256]{0,2,1:T(8,128)S(1)} %fusion.35) | copy-start | bytes 3145732
  917.2 17.6 %collective-permute-start.3 = (bf16[512,1,256]{0,2,1:T(8,128)(2,1)S(1)}, bf16[512,1,256]{0,2,1:T(8,128)(2,1)S(1)}, u32[]{:S(2)}, u32[]{:S(2)}) collective-permute-start(bf16[512,1,256]{0,2,1:T(8,128)(2,1)S(1)} %slice.62), channel_id=1, source_target_pairs={{4,0},{5,1},{6,2},{7,3},{12,8},{13,9},{14,10},{15,11},{20,16},{21,... | collective-permute-start | bytes 786440 | tf_op jit(solution)/shard_map/ppermute | solution.py:16
  924.1 9.8 collective-permute-start.2
  926.4 7.5 copy-start.16
  928.7 6.9 copy-start.15
  937.9 137.3 %reduce-scatter.15.cloned.1.call-start = ((), (), s32[]{:S(2)}) async-start(), calls=%async_computation.21 | async-start | bytes 1327104 | tf_op jit(solution)/shard_map/reduce_scatter | solution.py:213
  941.2 168.5 %reduce-scatter.13.cloned.1.call-start = ((), (), s32[]{:S(2)}) async-start(), calls=%async_computation.20 | async-start | bytes 1327104 | tf_op jit(solution)/shard_map/reduce_scatter | solution.py:210
  944.3 91.5 %copy-start.21 = (bf16[256,2,512]{2,0,1:T(8,128)(2,1)S(1)}, bf16[256,2,512]{2,0,1:T(8,128)(2,1)}, u32[]{:S(2)}) copy-start(bf16[256,2,512]{2,0,1:T(8,128)(2,1)} %copy-done.20) | copy-start | bytes 1572868
  944.3 203.3 %reduce-scatter.25.cloned.1.call-start = ((), (), s32[]{:S(2)}) async-start(), calls=%async_computation.26 | async-start | bytes 663552
  1035.8 4.8 copy-start.23
  1035.8 157.4 %reduce-scatter.17.cloned.1.call-start = ((), (), s32[]{:S(2)}) async-start(), calls=%async_computation.22 | async-start | bytes 2654208 | tf_op jit(solution)/shard_map/reduce_scatter | solution.py:219
  1040.5 198.8 %reduce-scatter.11.cloned.1.call-start = ((), (), s32[]{:S(2)}) async-start(), calls=%async_computation.19 | async-start | bytes 2654208 | tf_op jit(solution)/shard_map/reduce_scatter | solution.py:204
  1043.6 281.7 %reduce-scatter.21.cloned.1.call-start = ((), (), s32[]{:S(2)}) async-start(), calls=%async_computation.24 | async-start | bytes 11943936 | tf_op jit(solution)/shard_map/reduce_scatter | solution.py:231
  1054.2 357.1 %reduce-scatter.19.cloned.1.call-start = ((), (), s32[]{:S(2)}) async-start(), calls=%async_computation.23 | async-start | bytes 11943936 | tf_op jit(solution)/shard_map/reduce_scatter | solution.py:225
  1064.7 432.8 %reduce-scatter.23.cloned.1.call-start = ((), (), s32[]{:S(2)}) async-start(), calls=%async_computation.25 | async-start | bytes 11943936 | tf_op jit(solution)/shard_map/reduce_scatter | solution.py:234
  1075.1 36.2 %copy-start.34 = (f32[512]{0:T(512)S(1)}, f32[512]{0:T(512)}, u32[]{:S(2)}) copy-start(f32[512]{0:T(512)} %copy-done.33) | copy-start | bytes 6148
  (22 other events, 55.1 us)
Sparse Core Ops, SparseCore 0:
  9.9 26.6 all-gather.7
  38.4 25.3 all-gather.9
  65.7 29.1 all-gather.11
  96.7 28.8 all-gather.13
  131.0 171.9 all-reduce.4
  304.8 62.6 all-gather.15
  369.3 63.6 all-gather.17
  434.9 63.6 all-gather.19
  510.5 171.9 all-reduce.6
  727.4 170.9 all-reduce.8
  938.0 92.8 all-reduce.10
  1034.0 35.6 reduce-scatter.14
  1073.0 36.6 reduce-scatter.12
  1113.2 34.3 reduce-scatter.24
  1150.8 42.3 reduce-scatter.16
  1196.9 42.3 reduce-scatter.10
  1242.7 82.5 reduce-scatter.20
  1328.7 82.5 reduce-scatter.18
  1414.8 82.5 reduce-scatter.22
where the time goes:
time: 1520 us; the launch traced here: 1510 us
  waiting for transfers between devices  1260 us (83%)
  matrix products  145 us (10%)
  other arithmetic  57.6 us (4%)
    psum x1, waiting for transfers between devices, shards(): branch_two = lax.psum(transposed_product(hidden_low, down_full), 'tp')  172 us
    psum x1, waiting for transfers between devices, shards(): lax.psum(transposed_product(grad_gate_low, gate_full) + transposed_produc...  171 us
    psum x1, waiting for transfers between devices, shards(): branch_one = lax.psum(transposed_product(attended_low, output_full), 'tp')  170 us
    psum x1, waiting for transfers between devices, shards(): lax.psum((transposed_product(grad_query_low, query_full) + transposed_pro...  86.5 us
    reduce_scatter x1, waiting for transfers between devices, shards(): lax.psum_scatter(grad_up_full.astype(jnp.bfloat16), ('fsdp', 'ctx'), scat...  84.1 us
    reduce_scatter x1, waiting for transfers between devices, shards(): lax.psum_scatter(grad_down_full.astype(jnp.bfloat16), ('fsdp', 'ctx'), sc...  83.2 us
    reduce_scatter x1, waiting for transfers between devices, shards(): lax.psum_scatter(grad_gate_full.astype(jnp.bfloat16), ('fsdp', 'ctx'), sc...  83 us
    all_gather x1, waiting for transfers between devices, shards(): lax.all_gather(gate_weight, ('fsdp', 'ctx'), axis=0, tiled=True)  56.9 us
  transfers between devices with their start and end apart: 23, of which 19 were waited for; matrix products, arithmetic and copies ran while one was open for 8% of the time, Pallas kernels for 0%

commit v1 on v0

v1 whole, which is shorter than its diff:
```python
import jax
import jax.numpy as jnp
from jax import lax
from jax.sharding import PartitionSpec as P

HD = 256
CAP = 50.0
EPS = 1e-06
ROWS = ("fsdp", "ctx")
LOW = jnp.bfloat16
F32 = jnp.float32


def passed_along(block, axis, distance):
    devices = range(lax.axis_size(axis))
    route = [(i - distance, i) for i in devices if i - distance in devices]
    return lax.ppermute(block, axis, route)


def shift(block, distance):
    size = lax.axis_size("tp")
    return lax.ppermute(block, "tp", [(i, (i + distance) % size) for i in range(size)])


def rms(value, gain):
    return value * lax.rsqrt(jnp.mean(value * value, axis=-1, keepdims=True) + EPS) * gain


def geglu(gate_value, up_value):
    return jax.nn.gelu(gate_value, approximate=True) * up_value


def product(left, right):
    return jnp.dot(left, right, preferred_element_type=F32)


def rows_product(left, right):
    return lax.dot_general(left, right, (((0,), (0,)), ((), ())), preferred_element_type=F32)


def transposed_product(left, right):
    return lax.dot_general(left, right, (((1,), (1,)), ((), ())), preferred_element_type=F32)


def distances(size):
    return sorted(range(1, size), key=lambda k: (abs(2 * k - size), k))


def scattered(partial):
    size = lax.axis_size("tp")
    rank = lax.axis_index("tp")
    blocks = partial.reshape(size, -1, partial.shape[-1])
    total = lax.dynamic_index_in_dim(blocks, rank, 0, False).astype(F32)
    for k in distances(size):
        block = lax.dynamic_index_in_dim(blocks, (rank + k) % size, 0, False)
        total = total + shift(block, k).astype(F32)
    return total


def gathered(block):
    size = lax.axis_size("tp")
    rank = lax.axis_index("tp")
    whole = jnp.zeros((size,) + block.shape, block.dtype)
    whole = lax.dynamic_update_index_in_dim(whole, block, rank, 0)
    for k in distances(size):
        whole = lax.dynamic_update_index_in_dim(whole, shift(block, k), (rank - k) % size, 0)
    return whole.reshape(-1, block.shape[-1])


def gathered_turned(block):
    size = lax.axis_size("tp")
    pieces = {k: shift(block, k) for k in distances(size)}
    return jnp.concatenate([block] + [pieces[k] for k in range(1, size)], axis=0)


def scattered_turned(partial):
    size = lax.axis_size("tp")
    blocks = partial.reshape(size, -1, partial.shape[-1])
    total = blocks[0].astype(F32)
    for k in distances(size):
        total = total + shift(blocks[k], -k).astype(F32)
    return total


def attention_scores(queries, keys_all, allowed, scaling):
    scores = (
        jnp.einsum("qgrd,kgd->grqk", queries, keys_all, preferred_element_type=F32) * scaling
    )
    capped = CAP * jnp.tanh(scores / CAP)
    powers = jnp.where(allowed[None, None], jnp.exp(capped), 0.0)
    return (scores, powers)


def gather_rows(weight):
    return lax.all_gather(weight, ROWS, axis=0, tiled=True)


def share_rows(grad):
    return lax.psum_scatter(grad.astype(LOW), ROWS, scatter_dimension=0, tiled=True)


def shards(
    hidden_in,
    cotangent,
    segment_ids,
    pre_attention_gain,
    post_attention_gain,
    pre_feedforward_gain,
    post_feedforward_gain,
    query_weight,
    key_weight,
    value_weight,
    output_weight,
    gate_weight,
    up_weight,
    down_weight,
):
    length = hidden_in.shape[0]
    heads_width = query_weight.shape[1]
    kv_width = key_weight.shape[1]
    kv_heads = kv_width // HD
    repeats = heads_width // kv_width
    units = gate_weight.shape[1]
    qkv_width = heads_width + 2 * kv_width
    scaling = HD ** (-0.5)
    tp_size = lax.axis_size("tp")
    tp_rank = lax.axis_index("tp")
    piece = length // tp_size

    attention_full = gather_rows(
        jnp.concatenate([query_weight, key_weight, value_weight, output_weight], axis=1)
    )
    gate_up_full = gather_rows(jnp.concatenate([gate_weight, up_weight], axis=1))
    down_full = gather_rows(down_weight)
    qkv_full = attention_full[:, :qkv_width]
    output_full = attention_full[:, qkv_width:]

    position = lax.axis_index("ctx")
    own_ids = lax.dynamic_slice_in_dim(segment_ids, position * length, length)
    prev_start = jnp.maximum(position - 1, 0) * length
    prev_ids = jnp.where(
        position > 0, lax.dynamic_slice_in_dim(segment_ids, prev_start, length), -2
    )
    key_ids = jnp.concatenate([prev_ids, own_ids])
    query_pos = jnp.arange(length, dtype=jnp.int32)
    key_pos = jnp.arange(2 * length, dtype=jnp.int32) - length
    allowed = (query_pos[:, None] == key_pos[None, :]) | (own_ids[:, None] == key_ids[None, :]) & (
        own_ids[:, None] >= 0
    ) & (key_pos[None, :] < query_pos[:, None])

    normed_one = rms(hidden_in.astype(F32), pre_attention_gain).astype(LOW)
    inputs = lax.dynamic_slice_in_dim(hidden_in, tp_rank * piece, piece).astype(F32)
    upstream = lax.dynamic_slice_in_dim(cotangent, tp_rank * piece, piece).astype(F32)

    qkv_low = product(normed_one, qkv_full).astype(LOW)
    queries = qkv_low[:, :heads_width].reshape(length, kv_heads, repeats, HD)
    kv_low = qkv_low[:, heads_width:]
    kv_all = jnp.concatenate([passed_along(kv_low, "ctx", 1), kv_low], axis=0)
    keys_all = kv_all[:, :kv_width].reshape(2 * length, kv_heads, HD)
    values_all = kv_all[:, kv_width:].reshape(2 * length, kv_heads, HD)
    scores, powers = attention_scores(queries, keys_all, allowed, scaling)
    totals = jnp.sum(powers, axis=-1, keepdims=True)
    probs_low = (powers / totals).astype(LOW)
    attended = jnp.einsum("grqk,kgd->qgrd", probs_low, values_all, preferred_element_type=F32)
    attended_low = attended.reshape(length, -1).astype(LOW)

    branch_one = scattered(transposed_product(attended_low, output_full).astype(LOW))
    middle = inputs + rms(branch_one, post_attention_gain)
    normed_two_own = rms(middle, pre_feedforward_gain).astype(LOW)
    normed_two = gathered_turned(normed_two_own)

    gate_up = product(normed_two, gate_up_full)
    gate_value = gate_up[:, :units]
    up_value = gate_up[:, units:]
    hidden_low = geglu(gate_value, up_value).astype(LOW)
    branch_two = scattered_turned(transposed_product(hidden_low, down_full).astype(LOW))
    result = middle + rms(branch_two, post_feedforward_gain)

    unused_four, pull_four = jax.vjp(rms, branch_two, post_feedforward_gain)
    grad_branch_two, grad_gain_four = pull_four(upstream)
    grad_two_low = gathered_turned(grad_branch_two.astype(LOW))

    grad_down_full = rows_product(grad_two_low, hidden_low)
    down_share = share_rows(grad_down_full)
    grad_hidden_units = product(grad_two_low, down_full)
    unused_glu, pull_glu = jax.vjp(geglu, gate_value, up_value)
    grad_gate, grad_up = pull_glu(grad_hidden_units)
    grad_gate_up = jnp.concatenate([grad_gate.astype(LOW), grad_up.astype(LOW)], axis=1)
    grad_normed_two = scattered_turned(transposed_product(grad_gate_up, gate_up_full).astype(LOW))
    gate_up_share = share_rows(rows_product(normed_two, grad_gate_up))

    unused_three, pull_three = jax.vjp(rms, middle, pre_feedforward_gain)
    grad_middle_norm, grad_gain_three = pull_three(grad_normed_two)
    grad_middle = upstream + grad_middle_norm
    unused_two, pull_two = jax.vjp(rms, branch_one, post_attention_gain)
    grad_branch_one, grad_gain_two = pull_two(grad_middle)
    grad_one_low = gathered(grad_branch_one.astype(LOW))

    grad_output_full = rows_product(grad_one_low, attended_low)
    grad_attended = (
        product(grad_one_low, output_full).astype(LOW).reshape(length, kv_heads, repeats, HD)
    )
    probs = powers / totals
    grad_probs = jnp.einsum(
        "qgrd,kgd->grqk", grad_attended, values_all, preferred_element_type=F32
    )
    inner = jnp.sum(probs * grad_probs, axis=-1, keepdims=True)
    grad_capped = probs * (grad_probs - inner)
    squashed = jnp.tanh(scores / CAP)
    grad_scores = (grad_capped * (1.0 - squashed * squashed)).astype(LOW)
    grad_query_low = (
        (
            jnp.einsum("grqk,kgd->qgrd", grad_scores, keys_all, preferred_element_type=F32)
            * scaling
        )
        .reshape(length, -1)
        .astype(LOW)
    )
    grad_keys_all = (
        jnp.einsum("grqk,qgrd->kgd", grad_scores, queries, preferred_element_type=F32) * scaling
    ).reshape(2 * length, -1)
    grad_values_all = jnp.einsum(
        "grqk,qgrd->kgd", probs_low, grad_attended, preferred_element_type=F32
    ).reshape(2 * length, -1)
    grad_kv_all = jnp.concatenate([grad_keys_all, grad_values_all], axis=1)
    grad_kv_back = passed_along(grad_kv_all[:length].astype(LOW), "ctx", -1).astype(F32)
    grad_kv_low = (grad_kv_all[length:] + grad_kv_back).astype(LOW)
    grad_qkv = jnp.concatenate([grad_query_low, grad_kv_low], axis=1)
    grad_normed_one = scattered(transposed_product(grad_qkv, qkv_full).astype(LOW))
    grad_qkv_full = rows_product(normed_one, grad_qkv)

    unused_one, pull_one = jax.vjp(rms, inputs, pre_attention_gain)
    grad_inputs_norm, grad_gain_one = pull_one(grad_normed_one)
    grad_inputs = gathered((grad_middle + grad_inputs_norm).astype(LOW))
    outputs = gathered(result.astype(LOW))

    gains = jnp.stack([grad_gain_one, grad_gain_two, grad_gain_three, grad_gain_four])
    gains_all = gains
    for k in range(1, tp_size):
        gains_all = gains_all + shift(gains, k)
    attention_share = share_rows(
        jnp.concatenate(
            [grad_qkv_full.astype(LOW), grad_output_full.astype(LOW), gains_all.T.astype(LOW)],
            axis=1,
        )
    ).astype(F32)

    edges = [0, heads_width, heads_width + kv_width, qkv_width, qkv_width + heads_width]
    attention_shares = [attention_share[:, a:b] for a, b in zip(edges[:-1], edges[1:])]
    gain_shares = [attention_share[:, edges[-1] + i] for i in range(4)]
    gate_up_share = gate_up_share.astype(F32)
    return (
        (outputs, grad_inputs)
        + tuple(gain_shares)
        + tuple(attention_shares)
        + (gate_up_share[:, :units], gate_up_share[:, units:], down_share.astype(F32))
    )


def solution(mesh):
    tokens = P(ROWS, None)
    weight = P(ROWS, "tp")
    return jax.shard_map(
        shards,
        mesh=mesh,
        in_specs=(tokens, tokens, P("fsdp")) + (P(),) * 4 + (weight,) * 7,
        out_specs=(tokens, tokens) + (P(ROWS),) * 4 + (weight,) * 7,
        check_vma=False,
    )
```

time: 1520 us -> 926 us (0.61)
  waiting for transfers between devices: 1260 us -> 643 us
  starting transfers between devices: 12.1 us -> 68.4 us
  matrix products: 145 us -> 113 us
  local copies, waits for them, and re-layouts: 14.9 us -> 44.5 us
  other arithmetic: 57.6 us -> 32.9 us
    psum x4 -> x0, waiting for transfers between devices: 599 us -> none  [the longest x1 172 us: shards(): branch_two = lax.psum(transposed_product(hidden_low, down_full), 'tp')]
    ppermute x0 -> x30, waiting for transfers between devices: none -> 394 us  [shift(): lax.ppermute(block, 'tp', [(i, (i + distance) % size) for i in range(size)])]
    reduce_scatter x7 -> x2, waiting for transfers between devices: 371 us -> 151 us  [share_rows(): lax.psum_scatter(grad.astype(LOW), ROWS, scatter_dimension=0, tiled=True)]
    all_gather x7 -> x3, waiting for transfers between devices: 252 us -> 65.5 us  [gather_rows(): return lax.all_gather(weight, ROWS, axis=0, tiled=True)]
    ppermute x0 -> x30, starting transfers between devices: none -> 63.4 us  [shift(): lax.ppermute(block, 'tp', [(i, (i + distance) % size) for i in range(size)])]
    unnamed x20 -> x7, waiting for transfers between devices: 35.1 us -> 0.76 us
    ppermute x4 -> x2, waiting for transfers between devices: 5.26 us -> 31.8 us  [passed_along(): return lax.ppermute(block, axis, route)]
    convert_element_type x12 -> x7, other arithmetic: 28.3 us -> 7.91 us  [the longest x1 2.99 us: shards(): down_share.astype(F32)]
  transfers between devices with their start and end apart: 23 -> 38, of which waited for: 19 -> 26; matrix products, arithmetic and copies ran while one was open for 8% -> 11% of each run, Pallas kernels for 0% -> 0%
where the time goes in v1:
time: 926 us; the launch traced here: 918 us
  waiting for transfers between devices  643 us (69%)
  matrix products  113 us (12%)
  starting transfers between devices  68.4 us (7%)
  local copies, waits for them, and re-layouts  44.5 us (5%)
  other arithmetic  32.9 us (4%)
  between operations  15.5 us (2%)
    ppermute x30, waiting for transfers between devices, shift(): lax.ppermute(block, 'tp', [(i, (i + distance) % size) for i in range(size)])  394 us
    reduce_scatter x2, waiting for transfers between devices, share_rows(): lax.psum_scatter(grad.astype(LOW), ROWS, scatter_dimension=0, tiled=True)  151 us
    all_gather x3, waiting for transfers between devices, gather_rows(): return lax.all_gather(weight, ROWS, axis=0, tiled=True)  65.5 us
    ppermute x30, starting transfers between devices, shift(): lax.ppermute(block, 'tp', [(i, (i + distance) % size) for i in range(size)])  63.4 us
    dot_general x4, matrix products, product(): return jnp.dot(left, right, preferred_element_type=F32)  37.4 us
    dot_general x4, matrix products, rows_product(): lax.dot_general(left, right, (((0,), (0,)), ((), ())), preferred_element_...  35 us
    dot_general x4, matrix products, transposed_product(): lax.dot_general(left, right, (((1,), (1,)), ((), ())), preferred_element_...  32.6 us
    ppermute x2, waiting for transfers between devices, passed_along(): return lax.ppermute(block, axis, route)  31.8 us
  transfers between devices with their start and end apart: 38, of which 26 were waited for; matrix products, arithmetic and copies ran while one was open for 11% of the time, Pallas kernels for 0%

profile of v1, /device:TPU:0, one launch (start us, length us, event | category | flops | bytes accessed | tf_op | source)
XLA Modules:
  0.0 917.5 jit_solution(2715522698495390593)
XLA Ops:
  13.6 48.4 %all-gather.4.cloned.1.call-done = bf16[2304,1536]{1,0:T(8,128)(2,1)} async-done(((bf16[288,1536]{1,0:T(8,128)(2,1)}), bf16[2304,1536]{1,0:T(8,128)(2,1)}) %all-gather.4.cloned.1.call-update) | async-done | bytes 7077904 | tf_op jit(solution)/shard_map/all_gather | solution.py:95
  61.9 5.0 fusion.29
  67.0 3.4 collective-permute-start
  71.9 18.2 %collective-permute-done = bf16[512,512]{1,0:T(8,128)(2,1)S(1)} collective-permute-done((bf16[512,512]{1,0:T(8,128)(2,1)S(1)}, bf16[512,512]{1,0:T(8,128)(2,1)S(1)}, u32[]{:S(2)}, u32[]{:S(2)}) %collective-permute-start) | collective-permute-done | bytes 524320 | tf_op jit(solution)/shard_map/ppermute | solution.py:17
  93.6 3.3 convolution_convert_fusion.7
  98.1 3.1 collective-permute-start.3
  102.3 21.2 %collective-permute-done.3 = bf16[128,2304]{1,0:T(8,128)(2,1)S(1)} collective-permute-done((bf16[128,2304]{1,0:T(8,128)(2,1)}, bf16[128,2304]{1,0:T(8,128)(2,1)S(1)}, u32[]{:S(2)}, u32[]{:S(2)}) %collective-permute-start.3) | collective-permute-done | bytes 589856 | tf_op jit(solution)/shard_map/ppermute | solution.py:22
  123.5 5.3 collective-permute-done.2
  129.7 20.5 %collective-permute-done.1 = bf16[128,2304]{1,0:T(8,128)(2,1)} collective-permute-done((bf16[128,2304]{1,0:T(8,128)(2,1)}, bf16[128,2304]{1,0:T(8,128)(2,1)}, u32[]{:S(2)}, u32[]{:S(2)}) %collective-permute-start.1) | collective-permute-done | bytes 589856 | tf_op jit(solution)/shard_map/ppermute | solution.py:22
  157.9 12.9 %collective-permute-done.6 = bf16[128,2304]{1,0:T(8,128)(2,1)S(1)} collective-permute-done((bf16[128,2304]{1,0:T(8,128)(2,1)S(1)}, bf16[128,2304]{1,0:T(8,128)(2,1)S(1)}, u32[]{:S(2)}, u32[]{:S(2)}) %collective-permute-start.6) | collective-permute-done | bytes 589856 | tf_op jit(solution)/shard_map/ppermute | solution.py:22
  170.8 34.5 %collective-permute-done.5 = bf16[128,2304]{1,0:T(8,128)(2,1)S(1)} collective-permute-done((bf16[128,2304]{1,0:T(8,128)(2,1)S(1)}, bf16[128,2304]{1,0:T(8,128)(2,1)S(1)}, u32[]{:S(2)}, u32[]{:S(2)}) %collective-permute-start.5) | collective-permute-done | bytes 589856 | tf_op jit(solution)/shard_map/ppermute | solution.py:22
  206.1 15.0 %fusion.70 = f32[512,4608]{1,0:T(8,128)S(1)} fusion(bf16[2304,4608]{1,0:T(8,128)(2,1)} %all-gather.6.cloned.1.call-done, bf16[128,2304]{1,0:T(8,128)(2,1)} %copy-done.52, bf16[128,2304]{1,0:T(8,128)(2,1)} %copy-done.53, bf16[128,2304]{1,0:T(8,128)(2,1)} %collective-permute-done.4, bf16[128,2304]{1,0:T(8,128)(2,1)S(1)} %multiply_convert_fusion.2), kind=kOutput, calls=%fused_computation.140 | convolution fusion | flops 10881073152 | bytes 33030144 | tf_op jit(solution)/shard_map/dot_general | solution.py:34
  221.1 3.6 copy-done.2
  227.3 17.1 %all-gather.8.cloned.1.call-done = bf16[2304,2304]{1,0:T(8,128)(2,1)} async-done(((bf16[288,2304]{1,0:T(8,128)(2,1)}), bf16[2304,2304]{1,0:T(8,128)(2,1)}) %all-gather.8.cloned.1.call-update) | async-done | bytes 10616848 | tf_op jit(solution)/shard_map/all_gather | solution.py:95
  244.4 10.4 %convolution_convert_fusion.6 = bf16[512,2304]{1,0:T(8,128)(2,1)S(1)} fusion(bf16[512,2304]{1,0:T(8,128)(2,1)} %multiply_convert_fusion.1, bf16[2304,2304]{1,0:T(8,128)(2,1)} %all-gather.8.cloned.1.call-done), kind=kOutput, calls=%fused_computation.24 | convolution fusion | flops 5436997632 | bytes 15335424 | tf_op jit(solution)/shard_map/dot_general | solution.py:42
  259.4 13.6 %collective-permute-done.9 = bf16[128,2304]{1,0:T(8,128)(2,1)S(1)} collective-permute-done((bf16[128,2304]{1,0:T(8,128)(2,1)S(1)}, bf16[128,2304]{1,0:T(8,128)(2,1)S(1)}, u32[]{:S(2)}, u32[]{:S(2)}) %collective-permute-start.9) | collective-permute-done | bytes 589856 | tf_op jit(solution)/shard_map/ppermute | solution.py:22
  273.0 11.3 %collective-permute-done.8 = bf16[128,2304]{1,0:T(8,128)(2,1)S(1)} collective-permute-done((bf16[128,2304]{1,0:T(8,128)(2,1)S(1)}, bf16[128,2304]{1,0:T(8,128)(2,1)S(1)}, u32[]{:S(2)}, u32[]{:S(2)}) %collective-permute-start.8) | collective-permute-done | bytes 589856 | tf_op jit(solution)/shard_map/ppermute | solution.py:22
  284.3 25.9 %collective-permute-done.7 = bf16[128,2304]{1,0:T(8,128)(2,1)S(1)} collective-permute-done((bf16[128,2304]{1,0:T(8,128)(2,1)S(1)}, bf16[128,2304]{1,0:T(8,128)(2,1)S(1)}, u32[]{:S(2)}, u32[]{:S(2)}) %collective-permute-start.7) | collective-permute-done | bytes 589856 | tf_op jit(solution)/shard_map/ppermute | solution.py:22
  314.7 14.2 %collective-permute-done.15 = bf16[128,2304]{1,0:T(8,128)(2,1)S(1)} collective-permute-done((bf16[128,2304]{1,0:T(8,128)(2,1)S(1)}, bf16[128,2304]{1,0:T(8,128)(2,1)S(1)}, u32[]{:S(2)}, u32[]{:S(2)}) %collective-permute-start.15) | collective-permute-done | bytes 589856 | tf_op jit(solution)/shard_map/ppermute | solution.py:22
  328.8 34.3 %collective-permute-done.14 = bf16[128,2304]{1,0:T(8,128)(2,1)S(1)} collective-permute-done((bf16[128,2304]{1,0:T(8,128)(2,1)S(1)}, bf16[128,2304]{1,0:T(8,128)(2,1)S(1)}, u32[]{:S(2)}, u32[]{:S(2)}) %collective-permute-start.14) | collective-permute-done | bytes 589856 | tf_op jit(solution)/shard_map/ppermute | solution.py:22
  363.1 13.6 %fusion.9 = (bf16[512,2304]{1,0:T(8,128)(2,1)}, bf16[512,2304]{1,0:T(8,128)(2,1)}) fusion(f32[512,4608]{1,0:T(8,128)S(1)} %copy-done.3, bf16[2304,2304]{1,0:T(8,128)(2,1)} %all-gather.8.cloned.1.call-done, bf16[128,2304]{1,0:T(8,128)(2,1)S(1)} %collective-permute-done.15, bf16[128,2304]{1,0:T(8,128)(2,1)S(1)} %collective-permute-done.14, ...), kind=kOutput, calls=%fused_computation.17 | convolution fusion | flops 5473566720 | bytes 27131904 | tf_op jit(solution)/shard_map/dot_general | solution.py:34
  376.7 16.0 %convolution_convert_fusion.5 = bf16[512,2304]{1,0:T(8,128)(2,1)S(1)} fusion(bf16[2304,4608]{1,0:T(8,128)(2,1)} %all-gather.6.cloned.1.call-done, bf16[512,2304]{1,0:T(8,128)(2,1)} %get-tuple-element.68, bf16[512,2304]{1,0:T(8,128)(2,1)} %get-tuple-element.67), kind=kOutput, calls=%fused_computation.23 | convolution fusion | flops 10882252800 | bytes 28311552 | tf_op jit(solution)/shard_map/dot_general | solution.py:42
  398.4 12.5 %collective-permute-done.18 = bf16[128,2304]{1,0:T(8,128)(2,1)S(1)} collective-permute-done((bf16[128,2304]{1,0:T(8,128)(2,1)S(1)}, bf16[128,2304]{1,0:T(8,128)(2,1)S(1)}, u32[]{:S(2)}, u32[]{:S(2)}) %collective-permute-start.18) | collective-permute-done | bytes 589856 | tf_op jit(solution)/shard_map/ppermute | solution.py:22
  411.0 10.5 %collective-permute-done.17 = bf16[128,2304]{1,0:T(8,128)(2,1)S(1)} collective-permute-done((bf16[128,2304]{1,0:T(8,128)(2,1)S(1)}, bf16[128,2304]{1,0:T(8,128)(2,1)S(1)}, u32[]{:S(2)}, u32[]{:S(2)}) %collective-permute-start.17) | collective-permute-done | bytes 589856 | tf_op jit(solution)/shard_map/ppermute | solution.py:22
  421.4 25.3 %collective-permute-done.16 = bf16[128,2304]{1,0:T(8,128)(2,1)S(1)} collective-permute-done((bf16[128,2304]{1,0:T(8,128)(2,1)S(1)}, bf16[128,2304]{1,0:T(8,128)(2,1)S(1)}, u32[]{:S(2)}, u32[]{:S(2)}) %collective-permute-start.16) | collective-permute-done | bytes 589856 | tf_op jit(solution)/shard_map/ppermute | solution.py:22
  452.1 4.0 collective-permute-start.20
  456.2 37.2 %collective-permute-done.19 = bf16[128,2304]{1,0:T(8,128)(2,1)S(1)} collective-permute-done((bf16[128,2304]{1,0:T(8,128)(2,1)}, bf16[128,2304]{1,0:T(8,128)(2,1)S(1)}, u32[]{:S(2)}, u32[]{:S(2)}) %collective-permute-start.19) | collective-permute-done | bytes 589856 | tf_op jit(solution)/shard_map/ppermute | solution.py:22
  496.0 4.0 fusion.43
  508.4 13.6 %collective-permute-done.22 = bf16[512,512]{0,1:T(8,128)(2,1)S(1)} collective-permute-done((bf16[512,512]{0,1:T(8,128)(2,1)S(1)}, bf16[512,512]{0,1:T(8,128)(2,1)S(1)}, u32[]{:S(2)}, u32[]{:S(2)}) %collective-permute-start.22) | collective-permute-done | bytes 524320 | tf_op jit(solution)/shard_map/ppermute | solution.py:17
  525.5 11.5 %collective-permute-start.24 = (bf16[128,2304]{1,0:T(8,128)(2,1)S(1)}, bf16[128,2304]{1,0:T(8,128)(2,1)S(1)}, u32[]{:S(2)}, u32[]{:S(2)}) collective-permute-start(bf16[128,2304]{1,0:T(8,128)(2,1)S(1)} %get-tuple-element.73), channel_id=1, source_target_pairs={{0,1},{1,2},{2,3},{3,0},{4,5},{5,6},{6,7},{7,4},{8,9},{9,10},{10,1... | collective-permute-start | bytes 1769480 | tf_op jit(solution)/shard_map/ppermute | solution.py:22
  537.0 2.9 collective-permute-start.23
  541.5 9.0 collective-permute-done.25
  550.5 15.8 %collective-permute-done.24 = bf16[128,2304]{1,0:T(8,128)(2,1)S(1)} collective-permute-done((bf16[128,2304]{1,0:T(8,128)(2,1)S(1)}, bf16[128,2304]{1,0:T(8,128)(2,1)S(1)}, u32[]{:S(2)}, u32[]{:S(2)}) %collective-permute-start.24) | collective-permute-done | bytes 589856 | tf_op jit(solution)/shard_map/ppermute | solution.py:22
  566.3 22.4 %collective-permute-done.23 = bf16[128,2304]{1,0:T(8,128)(2,1)S(1)} collective-permute-done((bf16[128,2304]{1,0:T(8,128)(2,1)S(1)}, bf16[128,2304]{1,0:T(8,128)(2,1)S(1)}, u32[]{:S(2)}, u32[]{:S(2)}) %collective-permute-start.23) | collective-permute-done | bytes 589856 | tf_op jit(solution)/shard_map/ppermute | solution.py:22
  592.3 3.7 convolution_convert_fusion.2
  596.8 3.3 pad_maximum_fusion
  600.1 11.4 %copy.62 = bf16[2304,1540]{1,0:T(8,128)(2,1)} copy(bf16[2304,1540]{0,1:T(8,128)(2,1)} %pad_maximum_fusion) | data formatting | bytes 14192640
  611.6 10.8 %convolution_convert_fusion.1 = bf16[2304,2304]{1,0:T(8,128)(2,1)} fusion(bf16[512,2304]{1,0:T(8,128)(2,1)} %multiply_convert_fusion.1, bf16[128,2304]{1,0:T(8,128)(2,1)} %copy-done.54, bf16[128,2304]{1,0:T(8,128)(2,1)} %copy-done.55, bf16[128,2304]{1,0:T(8,128)(2,1)} %copy-done.56, bf16[128,2304]{1,0:T(8,128)(2,1)} %copy-done.18), kind=kOutput, calls=%fused_computation.1 | convolution fusion | flops 5450563584 | bytes 15335424 | tf_op jit(solution)/shard_map/dot_general | solution.py:38
  622.5 19.0 %convolution_convert_fusion = bf16[2304,4608]{1,0:T(8,128)(2,1)} fusion(bf16[512,2304]{1,0:T(8,128)(2,1)} %get-tuple-element.68, bf16[512,2304]{1,0:T(8,128)(2,1)} %get-tuple-element.67, bf16[128,2304]{1,0:T(8,128)(2,1)} %copy-done.52, bf16[128,2304]{1,0:T(8,128)(2,1)} %copy-done.53, bf16[128,2304]{1,0:T(8,128)(2,1)} %collective-permute-done.4, ...), kind=kOutput, calls=%fused_computation | convolution fusion | flops 10901127168 | bytes 28311552 | tf_op jit(solution)/shard_map/dot_general | solution.py:38
  646.8 3.5 collective-permute-start.12
  650.3 34.1 %collective-permute-done.10 = bf16[128,2304]{1,0:T(8,128)(2,1)S(1)} collective-permute-done((bf16[128,2304]{1,0:T(8,128)(2,1)S(1)}, bf16[128,2304]{1,0:T(8,128)(2,1)S(1)}, u32[]{:S(2)}, u32[]{:S(2)}) %collective-permute-start.10) | collective-permute-done | bytes 589856 | tf_op jit(solution)/shard_map/ppermute | solution.py:22
  690.1 12.2 %collective-permute-start.26 = (bf16[128,2304]{1,0:T(8,128)(2,1)S(1)}, bf16[128,2304]{1,0:T(8,128)(2,1)S(1)}, u32[]{:S(2)}, u32[]{:S(2)}) collective-permute-start(bf16[128,2304]{1,0:T(8,128)(2,1)S(1)} %get-tuple-element.52), channel_id=1, source_target_pairs={{0,2},{1,3},{2,0},{3,1},{4,6},{5,7},{6,4},{7,5},{8,10},{9,11},{10,... | collective-permute-start | bytes 1769480 | tf_op jit(solution)/shard_map/ppermute | solution.py:22
  703.2 3.8 collective-permute-start.28
  707.0 33.2 %collective-permute-done.26 = bf16[128,2304]{1,0:T(8,128)(2,1)S(1)} collective-permute-done((bf16[128,2304]{1,0:T(8,128)(2,1)S(1)}, bf16[128,2304]{1,0:T(8,128)(2,1)S(1)}, u32[]{:S(2)}, u32[]{:S(2)}) %collective-permute-start.26) | collective-permute-done | bytes 589856 | tf_op jit(solution)/shard_map/ppermute | solution.py:22
  752.3 12.5 %reduce-scatter.8.cloned.1.call-done = bf16[288,2304]{1,0:T(8,128)(2,1)} async-done(((bf16[2304,2304]{1,0:T(8,128)(2,1)}), bf16[288,2304]{1,0:T(8,128)(2,1)}) %reduce-scatter.8.cloned.1.call-update) | async-done | bytes 1327120 | tf_op jit(solution)/shard_map/reduce_scatter | solution.py:99
  764.7 3.0 convert_element_type.231
  767.7 138.1 %reduce-scatter.6.cloned.1.call-done = bf16[288,4608]{1,0:T(8,128)(2,1)} async-done(((bf16[2304,4608]{1,0:T(8,128)(2,1)}), bf16[288,4608]{1,0:T(8,128)(2,1)}) %reduce-scatter.6.cloned.1.call-update) | async-done | bytes 2654224 | tf_op jit(solution)/shard_map/reduce_scatter | solution.py:99
  905.8 4.5 fusion.99
  (248 shorter events, 89.7 us)
Async XLA Ops:
  7.2 54.7 %all-gather.4.cloned.1.call-start = ((), (), s32[]{:S(2)}) async-start(), calls=%async_computation.3 | async-start | bytes 7962624 | tf_op jit(solution)/shard_map/all_gather | solution.py:95
  9.6 196.5 %all-gather.6.cloned.1.call-start = ((), (), s32[]{:S(2)}) async-start(), calls=%async_computation.4 | async-start | bytes 23887872 | tf_op jit(solution)/shard_map/all_gather | solution.py:95
  11.4 233.0 %all-gather.8.cloned.1.call-start = ((), (), s32[]{:S(2)}) async-start(), calls=%async_computation.5 | async-start | bytes 11943936 | tf_op jit(solution)/shard_map/all_gather | solution.py:95
  12.1 730.7 %reduce-scatter.10.cloned.1.call-start = ((), (), s32[]{:S(2)}) async-start(), calls=%async_computation.8 | async-start | bytes 8626176
  13.6 56.9 %copy-start.40 = (s32[1024]{0:T(1024)S(1)}, s32[1024]{0:T(1024)}, u32[]{:S(2)}) copy-start(s32[1024]{0:T(1024)} %param.16) | copy-start | bytes 12292
  67.0 23.0 %collective-permute-start = (bf16[512,512]{1,0:T(8,128)(2,1)S(1)}, bf16[512,512]{1,0:T(8,128)(2,1)S(1)}, u32[]{:S(2)}, u32[]{:S(2)}) collective-permute-start(bf16[512,512]{1,0:T(8,128)(2,1)S(1)} %get-tuple-element.89), channel_id=1, source_target_pairs={{0,4},{1,5},{2,6},{3,7},{8,12},{9,13},{10,14},{11,15},{16,20},{17,... | collective-permute-start | bytes 1572872 | tf_op jit(solution)/shard_map/ppermute | solution.py:17
  98.1 25.4 %collective-permute-start.3 = (bf16[128,2304]{1,0:T(8,128)(2,1)}, bf16[128,2304]{1,0:T(8,128)(2,1)S(1)}, u32[]{:S(2)}, u32[]{:S(2)}) collective-permute-start(bf16[128,2304]{1,0:T(8,128)(2,1)} %get-tuple-element.82), channel_id=1, source_target_pairs={{0,3},{1,0},{2,1},{3,2},{4,7},{5,4},{6,5},{7,6},{8,11},{9,8},{10,9... | collective-permute-start | bytes 1769480 | tf_op jit(solution)/shard_map/ppermute | solution.py:22
  101.2 27.7 %collective-permute-start.2 = (bf16[128,2304]{1,0:T(8,128)(2,1)}, bf16[128,2304]{1,0:T(8,128)(2,1)S(1)}, u32[]{:S(2)}, u32[]{:S(2)}) collective-permute-start(bf16[128,2304]{1,0:T(8,128)(2,1)} %get-tuple-element.83), channel_id=1, source_target_pairs={{0,1},{1,2},{2,3},{3,0},{4,5},{5,6},{6,7},{7,4},{8,9},{9,10},{10,1... | collective-permute-start | bytes 1769480 | tf_op jit(solution)/shard_map/ppermute | solution.py:22
  101.2 49.0 %collective-permute-start.1 = (bf16[128,2304]{1,0:T(8,128)(2,1)}, bf16[128,2304]{1,0:T(8,128)(2,1)}, u32[]{:S(2)}, u32[]{:S(2)}) collective-permute-start(bf16[128,2304]{1,0:T(8,128)(2,1)} %get-tuple-element.81), channel_id=1, source_target_pairs={{0,2},{1,3},{2,0},{3,1},{4,6},{5,7},{6,4},{7,5},{8,10},{9,11},{10,... | collective-permute-start | bytes 1769480 | tf_op jit(solution)/shard_map/ppermute | solution.py:22
  154.1 66.9 %copy-start.49 = (f32[128]{0:T(128)}, f32[128]{0:T(128)S(1)}, u32[]{:S(2)}) copy-start(f32[128]{0:T(128)S(1)} %get-tuple-element.61) | copy-start | bytes 1540
  154.1 66.9 %copy-start.36 = (f32[128]{0:T(128)}, f32[128]{0:T(128)S(1)}, u32[]{:S(2)}) copy-start(f32[128]{0:T(128)S(1)} %fusion.79) | copy-start | bytes 1540
  154.3 66.8 %copy-start.17 = (bf16[128,2304]{1,0:T(8,128)(2,1)}, bf16[128,2304]{1,0:T(8,128)(2,1)S(1)}, u32[]{:S(2)}) copy-start(bf16[128,2304]{1,0:T(8,128)(2,1)S(1)} %multiply_convert_fusion.2) | copy-start | bytes 1769476
  154.3 16.5 %collective-permute-start.6 = (bf16[128,2304]{1,0:T(8,128)(2,1)S(1)}, bf16[128,2304]{1,0:T(8,128)(2,1)S(1)}, u32[]{:S(2)}, u32[]{:S(2)}) collective-permute-start(bf16[128,2304]{1,0:T(8,128)(2,1)S(1)} %multiply_convert_fusion.2), channel_id=1, source_target_pairs={{0,3},{1,0},{2,1},{3,2},{4,7},{5,4},{6,5},{7,6},{8,11},{9,8},{10,9... | collective-permute-start | bytes 1769480 | tf_op jit(solution)/shard_map/ppermute | solution.py:22
  157.0 48.2 %collective-permute-start.5 = (bf16[128,2304]{1,0:T(8,128)(2,1)S(1)}, bf16[128,2304]{1,0:T(8,128)(2,1)S(1)}, u32[]{:S(2)}, u32[]{:S(2)}) collective-permute-start(bf16[128,2304]{1,0:T(8,128)(2,1)S(1)} %multiply_convert_fusion.2), channel_id=1, source_target_pairs={{0,2},{1,3},{2,0},{3,1},{4,6},{5,7},{6,4},{7,5},{8,10},{9,11},{10,... | collective-permute-start | bytes 1769480 | tf_op jit(solution)/shard_map/ppermute | solution.py:22
  157.0 49.0 %collective-permute-start.4 = (bf16[128,2304]{1,0:T(8,128)(2,1)S(1)}, bf16[128,2304]{1,0:T(8,128)(2,1)}, u32[]{:S(2)}, u32[]{:S(2)}) collective-permute-start(bf16[128,2304]{1,0:T(8,128)(2,1)S(1)} %multiply_convert_fusion.2), channel_id=1, source_target_pairs={{0,1},{1,2},{2,3},{3,0},{4,5},{5,6},{6,7},{7,4},{8,9},{9,10},{10,1... | collective-permute-start | bytes 1769480 | tf_op jit(solution)/shard_map/ppermute | solution.py:22
  244.4 66.3 %copy-start.14 = (bf16[512,2304]{1,0:T(8,128)(2,1)S(1)}, bf16[512,2304]{1,0:T(8,128)(2,1)}, u32[]{:S(2)}) copy-start(bf16[512,2304]{1,0:T(8,128)(2,1)} %param.15) | copy-start | bytes 7077892
  244.4 66.3 %copy-start.23 = (f32[2304]{0:T(1024)S(1)}, f32[2304]{0:T(1024)}, u32[]{:S(2)}) copy-start(f32[2304]{0:T(1024)} %param.20) | copy-start | bytes 27652
  254.8 108.3 %copy-start.3 = (f32[512,4608]{1,0:T(8,128)S(1)}, f32[512,4608]{1,0:T(8,128)}, u32[]{:S(2)}) copy-start(f32[512,4608]{1,0:T(8,128)} %copy-done.2) | copy-start | bytes 28311556
  254.9 18.1 %collective-permute-start.9 = (bf16[128,2304]{1,0:T(8,128)(2,1)S(1)}, bf16[128,2304]{1,0:T(8,128)(2,1)S(1)}, u32[]{:S(2)}, u32[]{:S(2)}) collective-permute-start(bf16[128,2304]{1,0:T(8,128)(2,1)S(1)} %get-tuple-element.79), channel_id=1, source_target_pairs={{0,1},{1,2},{2,3},{3,0},{4,5},{5,6},{6,7},{7,4},{8,9},{9,10},{10,1... | collective-permute-start | bytes 1769480 | tf_op jit(solution)/shard_map/ppermute | solution.py:22
  256.5 27.8 %collective-permute-start.8 = (bf16[128,2304]{1,0:T(8,128)(2,1)S(1)}, bf16[128,2304]{1,0:T(8,128)(2,1)S(1)}, u32[]{:S(2)}, u32[]{:S(2)}) collective-permute-start(bf16[128,2304]{1,0:T(8,128)(2,1)S(1)} %get-tuple-element.80), channel_id=1, source_target_pairs={{0,3},{1,0},{2,1},{3,2},{4,7},{5,4},{6,5},{7,6},{8,11},{9,8},{10,9... | collective-permute-start | bytes 1769480 | tf_op jit(solution)/shard_map/ppermute | solution.py:22
  258.8 51.4 %collective-permute-start.7 = (bf16[128,2304]{1,0:T(8,128)(2,1)S(1)}, bf16[128,2304]{1,0:T(8,128)(2,1)S(1)}, u32[]{:S(2)}, u32[]{:S(2)}) collective-permute-start(bf16[128,2304]{1,0:T(8,128)(2,1)S(1)} %get-tuple-element.78), channel_id=1, source_target_pairs={{0,2},{1,3},{2,0},{3,1},{4,6},{5,7},{6,4},{7,5},{8,10},{9,11},{10,... | collective-permute-start | bytes 1769480 | tf_op jit(solution)/shard_map/ppermute | solution.py:22
  312.1 64.6 %copy-start.18 = (bf16[128,2304]{1,0:T(8,128)(2,1)}, bf16[128,2304]{1,0:T(8,128)(2,1)S(1)}, u32[]{:S(2)}) copy-start(bf16[128,2304]{1,0:T(8,128)(2,1)S(1)} %fusion.48) | copy-start | bytes 1769476
  312.1 16.8 %collective-permute-start.15 = (bf16[128,2304]{1,0:T(8,128)(2,1)S(1)}, bf16[128,2304]{1,0:T(8,128)(2,1)S(1)}, u32[]{:S(2)}, u32[]{:S(2)}) collective-permute-start(bf16[128,2304]{1,0:T(8,128)(2,1)S(1)} %fusion.48), channel_id=1, source_target_pairs={{0,3},{1,0},{2,1},{3,2},{4,7},{5,4},{6,5},{7,6},{8,11},{9,8},{10,9... | collective-permute-start | bytes 1769480 | tf_op jit(solution)/shard_map/ppermute | solution.py:22
  313.6 49.5 %collective-permute-start.14 = (bf16[128,2304]{1,0:T(8,128)(2,1)S(1)}, bf16[128,2304]{1,0:T(8,128)(2,1)S(1)}, u32[]{:S(2)}, u32[]{:S(2)}) collective-permute-start(bf16[128,2304]{1,0:T(8,128)(2,1)S(1)} %fusion.48), channel_id=1, source_target_pairs={{0,2},{1,3},{2,0},{3,1},{4,6},{5,7},{6,4},{7,5},{8,10},{9,11},{10,... | collective-permute-start | bytes 1769480 | tf_op jit(solution)/shard_map/ppermute | solution.py:22
  313.6 49.5 %collective-permute-start.13 = (bf16[128,2304]{1,0:T(8,128)(2,1)S(1)}, bf16[128,2304]{1,0:T(8,128)(2,1)S(1)}, u32[]{:S(2)}, u32[]{:S(2)}) collective-permute-start(bf16[128,2304]{1,0:T(8,128)(2,1)S(1)} %fusion.48), channel_id=1, source_target_pairs={{0,1},{1,2},{2,3},{3,0},{4,5},{5,6},{6,7},{7,4},{8,9},{9,10},{10,1... | collective-permute-start | bytes 1769480 | tf_op jit(solution)/shard_map/ppermute | solution.py:22
  392.8 55.0 %copy-start.50 = (f32[128]{0:T(128)S(1)}, f32[128]{0:T(128)}, u32[]{:S(2)}) copy-start(f32[128]{0:T(128)} %copy-done.49) | copy-start | bytes 1540
  392.8 55.0 %copy-start.25 = (f32[2304]{0:T(1024)S(1)}, f32[2304]{0:T(1024)}, u32[]{:S(2)}) copy-start(f32[2304]{0:T(1024)} %param.18) | copy-start | bytes 27652
  392.9 18.1 %collective-permute-start.18 = (bf16[128,2304]{1,0:T(8,128)(2,1)S(1)}, bf16[128,2304]{1,0:T(8,128)(2,1)S(1)}, u32[]{:S(2)}, u32[]{:S(2)}) collective-permute-start(bf16[128,2304]{1,0:T(8,128)(2,1)S(1)} %get-tuple-element.76), channel_id=1, source_target_pairs={{0,1},{1,2},{2,3},{3,0},{4,5},{5,6},{6,7},{7,4},{8,9},{9,10},{10,1... | collective-permute-start | bytes 1769480 | tf_op jit(solution)/shard_map/ppermute | solution.py:22
  394.5 27.0 %collective-permute-start.17 = (bf16[128,2304]{1,0:T(8,128)(2,1)S(1)}, bf16[128,2304]{1,0:T(8,128)(2,1)S(1)}, u32[]{:S(2)}, u32[]{:S(2)}) collective-permute-start(bf16[128,2304]{1,0:T(8,128)(2,1)S(1)} %get-tuple-element.77), channel_id=1, source_target_pairs={{0,3},{1,0},{2,1},{3,2},{4,7},{5,4},{6,5},{7,6},{8,11},{9,8},{10,9... | collective-permute-start | bytes 1769480 | tf_op jit(solution)/shard_map/ppermute | solution.py:22
  396.7 50.0 %collective-permute-start.16 = (bf16[128,2304]{1,0:T(8,128)(2,1)S(1)}, bf16[128,2304]{1,0:T(8,128)(2,1)S(1)}, u32[]{:S(2)}, u32[]{:S(2)}) collective-permute-start(bf16[128,2304]{1,0:T(8,128)(2,1)S(1)} %get-tuple-element.75), channel_id=1, source_target_pairs={{0,2},{1,3},{2,0},{3,1},{4,6},{5,7},{6,4},{7,5},{8,10},{9,11},{10,... | collective-permute-start | bytes 1769480 | tf_op jit(solution)/shard_map/ppermute | solution.py:22
  452.1 41.4 %collective-permute-start.19 = (bf16[128,2304]{1,0:T(8,128)(2,1)}, bf16[128,2304]{1,0:T(8,128)(2,1)S(1)}, u32[]{:S(2)}, u32[]{:S(2)}) collective-permute-start(bf16[128,2304]{1,0:T(8,128)(2,1)} %get-tuple-element.55), channel_id=1, source_target_pairs={{0,2},{1,3},{2,0},{3,1},{4,6},{5,7},{6,4},{7,5},{8,10},{9,11},{10,... | collective-permute-start | bytes 1769480 | tf_op jit(solution)/shard_map/ppermute | solution.py:22
  452.1 42.2 %collective-permute-start.20 = (bf16[128,2304]{1,0:T(8,128)(2,1)}, bf16[128,2304]{1,0:T(8,128)(2,1)S(1)}, u32[]{:S(2)}, u32[]{:S(2)}) collective-permute-start(bf16[128,2304]{1,0:T(8,128)(2,1)} %get-tuple-element.55), channel_id=1, source_target_pairs={{0,1},{1,2},{2,3},{3,0},{4,5},{5,6},{6,7},{7,4},{8,9},{9,10},{10,1... | collective-permute-start | bytes 1769480 | tf_op jit(solution)/shard_map/ppermute | solution.py:22
  456.1 39.1 %collective-permute-start.21 = (bf16[128,2304]{1,0:T(8,128)(2,1)}, bf16[128,2304]{1,0:T(8,128)(2,1)S(1)}, u32[]{:S(2)}, u32[]{:S(2)}) collective-permute-start(bf16[128,2304]{1,0:T(8,128)(2,1)} %get-tuple-element.55), channel_id=1, source_target_pairs={{0,3},{1,0},{2,1},{3,2},{4,7},{5,4},{6,5},{7,6},{8,11},{9,8},{10,9... | collective-permute-start | bytes 1769480 | tf_op jit(solution)/shard_map/ppermute | solution.py:22
  506.4 15.7 %collective-permute-start.22 = (bf16[512,512]{0,1:T(8,128)(2,1)S(1)}, bf16[512,512]{0,1:T(8,128)(2,1)S(1)}, u32[]{:S(2)}, u32[]{:S(2)}) collective-permute-start(bf16[512,512]{0,1:T(8,128)(2,1)S(1)} %fusion.63), channel_id=1, source_target_pairs={{4,0},{5,1},{6,2},{7,3},{12,8},{13,9},{14,10},{15,11},{20,16},{21,... | collective-permute-start | bytes 1572872 | tf_op jit(solution)/shard_map/ppermute | solution.py:17
  525.4 25.1 %collective-permute-start.25 = (bf16[128,2304]{1,0:T(8,128)(2,1)S(1)}, bf16[128,2304]{1,0:T(8,128)(2,1)S(1)}, u32[]{:S(2)}, u32[]{:S(2)}) collective-permute-start(bf16[128,2304]{1,0:T(8,128)(2,1)S(1)} %get-tuple-element.72), channel_id=1, source_target_pairs={{0,3},{1,0},{2,1},{3,2},{4,7},{5,4},{6,5},{7,6},{8,11},{9,8},{10,9... | collective-permute-start | bytes 1769480 | tf_op jit(solution)/shard_map/ppermute | solution.py:22
  525.5 40.8 %collective-permute-start.24 = (bf16[128,2304]{1,0:T(8,128)(2,1)S(1)}, bf16[128,2304]{1,0:T(8,128)(2,1)S(1)}, u32[]{:S(2)}, u32[]{:S(2)}) collective-permute-start(bf16[128,2304]{1,0:T(8,128)(2,1)S(1)} %get-tuple-element.73), channel_id=1, source_target_pairs={{0,1},{1,2},{2,3},{3,0},{4,5},{5,6},{6,7},{7,4},{8,9},{9,10},{10,1... | collective-permute-start | bytes 1769480 | tf_op jit(solution)/shard_map/ppermute | solution.py:22
  537.0 51.7 %collective-permute-start.23 = (bf16[128,2304]{1,0:T(8,128)(2,1)S(1)}, bf16[128,2304]{1,0:T(8,128)(2,1)S(1)}, u32[]{:S(2)}, u32[]{:S(2)}) collective-permute-start(bf16[128,2304]{1,0:T(8,128)(2,1)S(1)} %get-tuple-element.71), channel_id=1, source_target_pairs={{0,2},{1,3},{2,0},{3,1},{4,6},{5,7},{6,4},{7,5},{8,10},{9,11},{10,... | collective-permute-start | bytes 1769480 | tf_op jit(solution)/shard_map/ppermute | solution.py:22
  590.0 6.0 collective-permute-start.31
  590.1 6.0 collective-permute-start.30
  590.2 6.6 collective-permute-start.29
  611.5 153.2 %reduce-scatter.8.cloned.1.call-start = ((), (), s32[]{:S(2)}) async-start(), calls=%async_computation.7 | async-start | bytes 11943936 | tf_op jit(solution)/shard_map/reduce_scatter | solution.py:99
  622.4 283.4 %reduce-scatter.6.cloned.1.call-start = ((), (), s32[]{:S(2)}) async-start(), calls=%async_computation.6 | async-start | bytes 23887872 | tf_op jit(solution)/shard_map/reduce_scatter | solution.py:99
  644.1 40.2 %collective-permute-start.10 = (bf16[128,2304]{1,0:T(8,128)(2,1)S(1)}, bf16[128,2304]{1,0:T(8,128)(2,1)S(1)}, u32[]{:S(2)}, u32[]{:S(2)}) collective-permute-start(bf16[128,2304]{1,0:T(8,128)(2,1)S(1)} %get-tuple-element.58), channel_id=1, source_target_pairs={{0,2},{1,3},{2,0},{3,1},{4,6},{5,7},{6,4},{7,5},{8,10},{9,11},{10,... | collective-permute-start | bytes 1769480 | tf_op jit(solution)/shard_map/ppermute | solution.py:22
  646.4 38.8 %collective-permute-start.11 = (bf16[128,2304]{1,0:T(8,128)(2,1)S(1)}, bf16[128,2304]{1,0:T(8,128)(2,1)S(1)}, u32[]{:S(2)}, u32[]{:S(2)}) collective-permute-start(bf16[128,2304]{1,0:T(8,128)(2,1)S(1)} %get-tuple-element.58), channel_id=1, source_target_pairs={{0,1},{1,2},{2,3},{3,0},{4,5},{5,6},{6,7},{7,4},{8,9},{9,10},{10,1... | collective-permute-start | bytes 1769480 | tf_op jit(solution)/shard_map/ppermute | solution.py:22
  646.8 55.5 %collective-permute-start.12 = (bf16[128,2304]{1,0:T(8,128)(2,1)S(1)}, bf16[128,2304]{1,0:T(8,128)(2,1)S(1)}, u32[]{:S(2)}, u32[]{:S(2)}) collective-permute-start(bf16[128,2304]{1,0:T(8,128)(2,1)S(1)} %get-tuple-element.58), channel_id=1, source_target_pairs={{0,3},{1,0},{2,1},{3,2},{4,7},{5,4},{6,5},{7,6},{8,11},{9,8},{10,9... | collective-permute-start | bytes 1769480 | tf_op jit(solution)/shard_map/ppermute | solution.py:22
  690.1 50.1 %collective-permute-start.26 = (bf16[128,2304]{1,0:T(8,128)(2,1)S(1)}, bf16[128,2304]{1,0:T(8,128)(2,1)S(1)}, u32[]{:S(2)}, u32[]{:S(2)}) collective-permute-start(bf16[128,2304]{1,0:T(8,128)(2,1)S(1)} %get-tuple-element.52), channel_id=1, source_target_pairs={{0,2},{1,3},{2,0},{3,1},{4,6},{5,7},{6,4},{7,5},{8,10},{9,11},{10,... | collective-permute-start | bytes 1769480 | tf_op jit(solution)/shard_map/ppermute | solution.py:22
  703.2 37.9 %collective-permute-start.27 = (bf16[128,2304]{1,0:T(8,128)(2,1)S(1)}, bf16[128,2304]{1,0:T(8,128)(2,1)S(1)}, u32[]{:S(2)}, u32[]{:S(2)}) collective-permute-start(bf16[128,2304]{1,0:T(8,128)(2,1)S(1)} %get-tuple-element.52), channel_id=1, source_target_pairs={{0,1},{1,2},{2,3},{3,0},{4,5},{5,6},{6,7},{7,4},{8,9},{9,10},{10,1... | collective-permute-start | bytes 1769480 | tf_op jit(solution)/shard_map/ppermute | solution.py:22
  703.2 38.8 %collective-permute-start.28 = (bf16[128,2304]{1,0:T(8,128)(2,1)S(1)}, bf16[128,2304]{1,0:T(8,128)(2,1)S(1)}, u32[]{:S(2)}, u32[]{:S(2)}) collective-permute-start(bf16[128,2304]{1,0:T(8,128)(2,1)S(1)} %get-tuple-element.52), channel_id=1, source_target_pairs={{0,3},{1,0},{2,1},{3,2},{4,7},{5,4},{6,5},{7,6},{8,11},{9,8},{10,9... | collective-permute-start | bytes 1769480 | tf_op jit(solution)/shard_map/ppermute | solution.py:22
  (53 other events, 965.6 us)
Sparse Core Ops, SparseCore 0:
  10.5 51.4 all-gather.3
  64.4 114.3 all-gather.5
  180.7 63.6 all-gather.7
  611.7 67.0 reduce-scatter.9
  682.1 82.5 reduce-scatter.7
  768.2 137.5 reduce-scatter.5

commit v2 on v1

--- a/solution.py
+++ b/solution.py
@@ -1,7 +1,9 @@
 import jax
 import jax.numpy as jnp
 from jax import lax
+from jax.experimental.layout import Layout, with_layout_constraint
 from jax.sharding import PartitionSpec as P
+
 
 HD = 256
 CAP = 50.0
@@ -82,6 +84,15 @@
     return total
 
 
+def summed(value, axis):
+    size = lax.axis_size(axis)
+    bit = 1
+    while bit < size:
+        value = value + lax.ppermute(value, axis, [(i, i ^ bit) for i in range(size)])
+        bit *= 2
+    return value
+
+
 def attention_scores(queries, keys_all, allowed, scaling):
     scores = (
         jnp.einsum("qgrd,kgd->grqk", queries, keys_all, preferred_element_type=F32) * scaling
@@ -91,12 +102,16 @@
     return (scores, powers)
 
 
+def by_rows(value):
+    return with_layout_constraint(value, Layout(major_to_minor=(0, 1)))
+
+
 def gather_rows(weight):
     return lax.all_gather(weight, ROWS, axis=0, tiled=True)
 
 
 def share_rows(grad):
-    return lax.psum_scatter(grad.astype(LOW), ROWS, scatter_dimension=0, tiled=True)
+    return lax.psum_scatter(grad, ROWS, scatter_dimension=0, tiled=True)
 
 
 def shards(
@@ -176,25 +191,31 @@
     branch_two = scattered_turned(transposed_product(hidden_low, down_full).astype(LOW))
     result = middle + rms(branch_two, post_feedforward_gain)
 
-    unused_four, pull_four = jax.vjp(rms, branch_two, post_feedforward_gain)
+    _, pull_four = jax.vjp(rms, branch_two, post_feedforward_gain)
     grad_branch_two, grad_gain_four = pull_four(upstream)
     grad_two_low = gathered_turned(grad_branch_two.astype(LOW))
 
-    grad_down_full = rows_product(grad_two_low, hidden_low)
-    down_share = share_rows(grad_down_full)
+    grad_down_low, grad_two_low = lax.optimization_barrier(
+        (rows_product(grad_two_low, hidden_low).astype(LOW), grad_two_low)
+    )
+    down_share = share_rows(grad_down_low)
     grad_hidden_units = product(grad_two_low, down_full)
-    unused_glu, pull_glu = jax.vjp(geglu, gate_value, up_value)
+    _, pull_glu = jax.vjp(geglu, gate_value, up_value)
     grad_gate, grad_up = pull_glu(grad_hidden_units)
     grad_gate_up = jnp.concatenate([grad_gate.astype(LOW), grad_up.astype(LOW)], axis=1)
     grad_normed_two = scattered_turned(transposed_product(grad_gate_up, gate_up_full).astype(LOW))
-    gate_up_share = share_rows(rows_product(normed_two, grad_gate_up))
-
-    unused_three, pull_three = jax.vjp(rms, middle, pre_feedforward_gain)
+    grad_gate_up_low = rows_product(normed_two, grad_gate_up).astype(LOW)
+
+    _, pull_three = jax.vjp(rms, middle, pre_feedforward_gain)
     grad_middle_norm, grad_gain_three = pull_three(grad_normed_two)
     grad_middle = upstream + grad_middle_norm
-    unused_two, pull_two = jax.vjp(rms, branch_one, post_attention_gain)
+    _, pull_two = jax.vjp(rms, branch_one, post_attention_gain)
     grad_branch_one, grad_gain_two = pull_two(grad_middle)
-    grad_one_low = gathered(grad_branch_one.astype(LOW))
+    grad_one_own, grad_gate_up_low = lax.optimization_barrier(
+        (grad_branch_one.astype(LOW), grad_gate_up_low)
+    )
+    gate_up_share = share_rows(grad_gate_up_low)
+    grad_one_low = gathered(grad_one_own)
 
     grad_output_full = rows_product(grad_one_low, attended_low)
     grad_attended = (
@@ -229,29 +250,27 @@
     grad_normed_one = scattered(transposed_product(grad_qkv, qkv_full).astype(LOW))
     grad_qkv_full = rows_product(normed_one, grad_qkv)
 
-    unused_one, pull_one = jax.vjp(rms, inputs, pre_attention_gain)
+    _, pull_one = jax.vjp(rms, inputs, pre_attention_gain)
     grad_inputs_norm, grad_gain_one = pull_one(grad_normed_one)
     grad_inputs = gathered((grad_middle + grad_inputs_norm).astype(LOW))
     outputs = gathered(result.astype(LOW))
 
     gains = jnp.stack([grad_gain_one, grad_gain_two, grad_gain_three, grad_gain_four])
-    gains_all = gains
-    for k in range(1, tp_size):
-        gains_all = gains_all + shift(gains, k)
+    for axis in ("tp",) + ROWS:
+        gains = summed(gains, axis)
+    share = attention_full.shape[0] // (lax.axis_size("fsdp") * lax.axis_size("ctx"))
+    row_rank = lax.axis_index("fsdp") * lax.axis_size("ctx") + lax.axis_index("ctx")
+    gain_shares = lax.dynamic_slice_in_dim(gains, row_rank * share, share, axis=1)
     attention_share = share_rows(
-        jnp.concatenate(
-            [grad_qkv_full.astype(LOW), grad_output_full.astype(LOW), gains_all.T.astype(LOW)],
-            axis=1,
-        )
+        by_rows(jnp.concatenate([grad_qkv_full.astype(LOW), grad_output_full.astype(LOW)], axis=1))
     ).astype(F32)
 
     edges = [0, heads_width, heads_width + kv_width, qkv_width, qkv_width + heads_width]
     attention_shares = [attention_share[:, a:b] for a, b in zip(edges[:-1], edges[1:])]
-    gain_shares = [attention_share[:, edges[-1] + i] for i in range(4)]
     gate_up_share = gate_up_share.astype(F32)
     return (
         (outputs, grad_inputs)
-        + tuple(gain_shares)
+        + tuple(gain_shares[i] for i in range(4))
         + tuple(attention_shares)
         + (gate_up_share[:, :units], gate_up_share[:, units:], down_share.astype(F32))
     )

time: 926 us -> 872 us (0.942)
  waiting for transfers between devices: 643 us -> 513 us
  starting transfers between devices: 68.4 us -> 157 us
  local copies, waits for them, and re-layouts: 44.5 us -> 22.4 us
    ppermute x30 -> x27, waiting for transfers between devices: 394 us -> 275 us  [shift(): lax.ppermute(block, 'tp', [(i, (i + distance) % size) for i in range(size)])]
    ppermute x30 -> x27, starting transfers between devices: 63.4 us -> 112 us  [shift(): lax.ppermute(block, 'tp', [(i, (i + distance) % size) for i in range(size)])]
    ppermute x0 -> x5, starting transfers between devices: none -> 39.3 us  [summed(): lax.ppermute(value, axis, [(i, i ^ bit) for i in range(size)])]
    reduce_scatter x2 -> x3, waiting for transfers between devices: 151 us -> 129 us  [share_rows(): return lax.psum_scatter(grad, ROWS, scatter_dimension=0, tiled=True)]
    unnamed x132 -> x108, local copies, waits for them, and re-layouts: 25.5 us -> 8.89 us
    ppermute x0 -> x5, waiting for transfers between devices: none -> 14.3 us  [summed(): lax.ppermute(value, axis, [(i, i ^ bit) for i in range(size)])]
  transfers between devices with their start and end apart: 38 -> 40, of which waited for: 26 -> 25; matrix products, arithmetic and copies ran while one was open for 11% -> 9% of each run, Pallas kernels for 0% -> 0%
where the time goes in v2:
time: 872 us; the launch traced here: 864 us
  waiting for transfers between devices  513 us (59%)
  starting transfers between devices  157 us (18%)
  matrix products  117 us (13%)
  other arithmetic  38.6 us (4%)
  local copies, waits for them, and re-layouts  22.4 us (3%)
  between operations  15.7 us (2%)
    ppermute x27, waiting for transfers between devices, shift(): lax.ppermute(block, 'tp', [(i, (i + distance) % size) for i in range(size)])  275 us
    reduce_scatter x3, waiting for transfers between devices, share_rows(): return lax.psum_scatter(grad, ROWS, scatter_dimension=0, tiled=True)  129 us
    ppermute x27, starting transfers between devices, shift(): lax.ppermute(block, 'tp', [(i, (i + distance) % size) for i in range(size)])  112 us
    all_gather x3, waiting for transfers between devices, gather_rows(): return lax.all_gather(weight, ROWS, axis=0, tiled=True)  65.7 us
    ppermute x5, starting transfers between devices, summed(): lax.ppermute(value, axis, [(i, i ^ bit) for i in range(size)])  39.3 us
    dot_general x4, matrix products, product(): return jnp.dot(left, right, preferred_element_type=F32)  37.4 us
    dot_general x4, matrix products, rows_product(): lax.dot_general(left, right, (((0,), (0,)), ((), ())), preferred_element_...  36.3 us
    dot_general x4, matrix products, transposed_product(): lax.dot_general(left, right, (((1,), (1,)), ((), ())), preferred_element_...  35.2 us
  transfers between devices with their start and end apart: 40, of which 25 were waited for; matrix products, arithmetic and copies ran while one was open for 9% of the time, Pallas kernels for 0%

profile of v2, /device:TPU:0, one launch (start us, length us, event | category | flops | bytes accessed | tf_op | source)
XLA Modules:
  0.0 864.2 jit_solution(18034077230783873175)
XLA Ops:
  13.6 48.4 %all-gather.4.cloned.1.call-done = bf16[2304,1536]{1,0:T(8,128)(2,1)} async-done(((bf16[288,1536]{1,0:T(8,128)(2,1)}), bf16[2304,1536]{1,0:T(8,128)(2,1)}) %all-gather.4.cloned.1.call-update) | async-done | bytes 7077904 | tf_op jit(solution)/shard_map/all_gather | solution.py:110
  61.9 5.0 fusion.29
  67.0 3.4 collective-permute-start
  71.9 18.2 %collective-permute-done = bf16[512,512]{1,0:T(8,128)(2,1)S(1)} collective-permute-done((bf16[512,512]{1,0:T(8,128)(2,1)S(1)}, bf16[512,512]{1,0:T(8,128)(2,1)S(1)}, u32[]{:S(2)}, u32[]{:S(2)}) %collective-permute-start) | collective-permute-done | bytes 524320 | tf_op jit(solution)/shard_map/ppermute | solution.py:19
  93.7 3.3 convolution_convert_fusion.7
  104.2 34.4 %collective-permute-done.1 = bf16[128,2304]{1,0:T(8,128)(2,1)S(1)} collective-permute-done((bf16[128,2304]{1,0:T(8,128)(2,1)}, bf16[128,2304]{1,0:T(8,128)(2,1)S(1)}, u32[]{:S(2)}, u32[]{:S(2)}) %collective-permute-start.1) | collective-permute-done | bytes 589856 | tf_op jit(solution)/shard_map/ppermute | solution.py:24
  144.4 23.9 %collective-permute-start.4 = (bf16[128,2304]{1,0:T(8,128)(2,1)S(1)}, bf16[128,2304]{1,0:T(8,128)(2,1)S(1)}, u32[]{:S(2)}, u32[]{:S(2)}) collective-permute-start(bf16[128,2304]{1,0:T(8,128)(2,1)S(1)} %multiply_convert_fusion.2), channel_id=1, source_target_pairs={{0,1},{1,2},{2,3},{3,0},{4,5},{5,6},{6,7},{7,4},{8,9},{9,10},{10,1... | collective-permute-start | bytes 1769480 | tf_op jit(solution)/shard_map/ppermute | solution.py:24
  168.3 2.9 collective-permute-start.6
  171.3 10.8 %collective-permute-done.4 = bf16[128,2304]{1,0:T(8,128)(2,1)S(1)} collective-permute-done((bf16[128,2304]{1,0:T(8,128)(2,1)S(1)}, bf16[128,2304]{1,0:T(8,128)(2,1)S(1)}, u32[]{:S(2)}, u32[]{:S(2)}) %collective-permute-start.4) | collective-permute-done | bytes 589856 | tf_op jit(solution)/shard_map/ppermute | solution.py:24
  182.0 14.0 %collective-permute-done.5 = bf16[128,2304]{1,0:T(8,128)(2,1)S(1)} collective-permute-done((bf16[128,2304]{1,0:T(8,128)(2,1)S(1)}, bf16[128,2304]{1,0:T(8,128)(2,1)S(1)}, u32[]{:S(2)}, u32[]{:S(2)}) %collective-permute-start.5) | collective-permute-done | bytes 589856 | tf_op jit(solution)/shard_map/ppermute | solution.py:24
  196.8 8.9 %collective-permute-done.6 = bf16[128,2304]{1,0:T(8,128)(2,1)} collective-permute-done((bf16[128,2304]{1,0:T(8,128)(2,1)S(1)}, bf16[128,2304]{1,0:T(8,128)(2,1)}, u32[]{:S(2)}, u32[]{:S(2)}) %collective-permute-start.6) | collective-permute-done | bytes 589856 | tf_op jit(solution)/shard_map/ppermute | solution.py:24
  205.7 15.0 %fusion.69 = f32[512,4608]{1,0:T(8,128)S(1)} fusion(bf16[2304,4608]{1,0:T(8,128)(2,1)} %all-gather.6.cloned.1.call-done, bf16[128,2304]{1,0:T(8,128)(2,1)} %collective-permute-done.6, bf16[128,2304]{1,0:T(8,128)(2,1)} %copy-done.47, bf16[128,2304]{1,0:T(8,128)(2,1)} %copy-done.46, bf16[128,2304]{1,0:T(8,128)(2,1)S(1)} %multiply_convert_fusion.2), kind=kOutput, calls=%fused_computation.139 | convolution fusion | flops 10881073152 | bytes 33030144 | tf_op jit(solution)/shard_map/dot_general | solution.py:36
  220.7 3.6 copy-done.2
  227.0 17.4 %all-gather.8.cloned.1.call-done = bf16[2304,2304]{1,0:T(8,128)(2,1)} async-done(((bf16[288,2304]{1,0:T(8,128)(2,1)}), bf16[2304,2304]{1,0:T(8,128)(2,1)}) %all-gather.8.cloned.1.call-update) | async-done | bytes 10616848 | tf_op jit(solution)/shard_map/all_gather | solution.py:110
  244.4 10.3 %convolution_convert_fusion.6 = bf16[512,2304]{1,0:T(8,128)(2,1)S(1)} fusion(bf16[512,2304]{1,0:T(8,128)(2,1)} %multiply_convert_fusion.1, bf16[2304,2304]{1,0:T(8,128)(2,1)} %all-gather.8.cloned.1.call-done), kind=kOutput, calls=%fused_computation.24 | convolution fusion | flops 5436997632 | bytes 15335424 | tf_op jit(solution)/shard_map/dot_general | solution.py:44
  259.3 25.9 %collective-permute-done.7 = bf16[128,2304]{1,0:T(8,128)(2,1)S(1)} collective-permute-done((bf16[128,2304]{1,0:T(8,128)(2,1)S(1)}, bf16[128,2304]{1,0:T(8,128)(2,1)S(1)}, u32[]{:S(2)}, u32[]{:S(2)}) %collective-permute-start.7) | collective-permute-done | bytes 589856 | tf_op jit(solution)/shard_map/ppermute | solution.py:24
  285.2 12.4 %collective-permute-done.9 = bf16[128,2304]{1,0:T(8,128)(2,1)S(1)} collective-permute-done((bf16[128,2304]{1,0:T(8,128)(2,1)S(1)}, bf16[128,2304]{1,0:T(8,128)(2,1)S(1)}, u32[]{:S(2)}, u32[]{:S(2)}) %collective-permute-start.9) | collective-permute-done | bytes 589856 | tf_op jit(solution)/shard_map/ppermute | solution.py:24
  300.3 24.8 %collective-permute-start.13 = (bf16[128,2304]{1,0:T(8,128)(2,1)}, bf16[128,2304]{1,0:T(8,128)(2,1)}, u32[]{:S(2)}, u32[]{:S(2)}) collective-permute-start(bf16[128,2304]{1,0:T(8,128)(2,1)} %fusion.48), channel_id=1, source_target_pairs={{0,1},{1,2},{2,3},{3,0},{4,5},{5,6},{6,7},{7,4},{8,9},{9,10},{10,1... | collective-permute-start | bytes 1769480 | tf_op jit(solution)/shard_map/ppermute | solution.py:24
  327.6 11.5 %collective-permute-done.13 = bf16[128,2304]{1,0:T(8,128)(2,1)} collective-permute-done((bf16[128,2304]{1,0:T(8,128)(2,1)}, bf16[128,2304]{1,0:T(8,128)(2,1)}, u32[]{:S(2)}, u32[]{:S(2)}) %collective-permute-start.13) | collective-permute-done | bytes 589856 | tf_op jit(solution)/shard_map/ppermute | solution.py:24
  339.1 14.0 %collective-permute-done.14 = bf16[128,2304]{1,0:T(8,128)(2,1)} collective-permute-done((bf16[128,2304]{1,0:T(8,128)(2,1)}, bf16[128,2304]{1,0:T(8,128)(2,1)}, u32[]{:S(2)}, u32[]{:S(2)}) %collective-permute-start.14) | collective-permute-done | bytes 589856 | tf_op jit(solution)/shard_map/ppermute | solution.py:24
  353.1 9.8 %collective-permute-done.15 = bf16[128,2304]{1,0:T(8,128)(2,1)} collective-permute-done((bf16[128,2304]{1,0:T(8,128)(2,1)}, bf16[128,2304]{1,0:T(8,128)(2,1)}, u32[]{:S(2)}, u32[]{:S(2)}) %collective-permute-start.15) | collective-permute-done | bytes 589856 | tf_op jit(solution)/shard_map/ppermute | solution.py:24
  362.9 3.2 pad_maximum_fusion.6
  366.0 10.5 %convolution_convert_fusion.1 = bf16[2304,2304]{1,0:T(8,128)(2,1)} fusion(bf16[512,2304]{1,0:T(8,128)(2,1)S(1)} %copy-done.11, bf16[128,2304]{1,0:T(8,128)(2,1)} %collective-permute-done.15, bf16[128,2304]{1,0:T(8,128)(2,1)} %collective-permute-done.14, bf16[128,2304]{1,0:T(8,128)(2,1)} %collective-permute-done.13, bf16[128,2304]{1,0:T(8,128)(2,1)} %fusion.48), kind=kOutput, calls=%fused_computation.1 | convolution fusion | flops 5450563584 | bytes 15335424 | tf_op jit(solution)/shard_map/dot_general | solution.py:40
  376.6 14.2 %fusion.9 = (bf16[512,2304]{1,0:T(8,128)(2,1)S(1)}, bf16[512,2304]{1,0:T(8,128)(2,1)S(1)}) fusion(f32[512,4608]{1,0:T(8,128)} %copy-done.2, bf16[512,2304]{1,0:T(8,128)(2,1)} %pad_maximum_fusion.6, bf16[2304,2304]{1,0:T(8,128)(2,1)} %all-gather.8.cloned.1.call-done), kind=kOutput, calls=%fused_computation.17 | convolution fusion | flops 5464129536 | bytes 27131904 | tf_op jit(solution)/shard_map/dot_general | solution.py:36
  390.8 16.3 %convolution_convert_fusion.5 = bf16[512,2304]{1,0:T(8,128)(2,1)S(1)} fusion(bf16[2304,4608]{1,0:T(8,128)(2,1)} %all-gather.6.cloned.1.call-done, bf16[512,2304]{1,0:T(8,128)(2,1)S(1)} %get-tuple-element.48, bf16[512,2304]{1,0:T(8,128)(2,1)S(1)} %get-tuple-element.47), kind=kOutput, calls=%fused_computation.23 | convolution fusion | flops 10882252800 | bytes 28311552 | tf_op jit(solution)/shard_map/dot_general | solution.py:44
  409.8 3.5 collective-permute-start.16
  413.3 12.2 %collective-permute-start.17 = (bf16[128,2304]{1,0:T(8,128)(2,1)}, bf16[128,2304]{1,0:T(8,128)(2,1)}, u32[]{:S(2)}, u32[]{:S(2)}) collective-permute-start(bf16[128,2304]{1,0:T(8,128)(2,1)} %get-tuple-element.57), channel_id=1, source_target_pairs={{0,3},{1,0},{2,1},{3,2},{4,7},{5,4},{6,5},{7,6},{8,11},{9,8},{10,9... | collective-permute-start | bytes 1769480 | tf_op jit(solution)/shard_map/ppermute | solution.py:24
  426.2 18.2 %convolution_convert_fusion = bf16[2304,4608]{1,0:T(8,128)(2,1)} fusion(bf16[512,2304]{1,0:T(8,128)(2,1)} %copy-done.53, bf16[512,2304]{1,0:T(8,128)(2,1)} %copy-done.52, bf16[128,2304]{1,0:T(8,128)(2,1)} %collective-permute-done.6, bf16[128,2304]{1,0:T(8,128)(2,1)} %copy-done.47, bf16[128,2304]{1,0:T(8,128)(2,1)} %copy-done.46, bf16[128,2304]{1,0:T(8,128)(2,1)} %copy-done.19), kind=kOutput, calls=%fused_computation | convolution fusion | flops 10901127168 | bytes 28311552 | tf_op jit(solution)/shard_map/dot_general | solution.py:40
  444.4 19.1 %collective-permute-done.18 = bf16[128,2304]{1,0:T(8,128)(2,1)} collective-permute-done((bf16[128,2304]{1,0:T(8,128)(2,1)}, bf16[128,2304]{1,0:T(8,128)(2,1)}, u32[]{:S(2)}, u32[]{:S(2)}) %collective-permute-start.18) | collective-permute-done | bytes 589856 | tf_op jit(solution)/shard_map/ppermute | solution.py:24
  467.0 3.3 multiply_reduce_fusion.1
  470.6 3.1 collective-permute-start.19
  474.2 3.6 collective-permute-start.21
  477.9 34.8 %collective-permute-done.19 = bf16[128,2304]{1,0:T(8,128)(2,1)S(1)} collective-permute-done((bf16[128,2304]{1,0:T(8,128)(2,1)S(1)}, bf16[128,2304]{1,0:T(8,128)(2,1)S(1)}, u32[]{:S(2)}, u32[]{:S(2)}) %collective-permute-start.19) | collective-permute-done | bytes 589856 | tf_op jit(solution)/shard_map/ppermute | solution.py:24
  514.0 3.3 fusion.43
  528.7 9.4 %collective-permute-done.22 = bf16[512,512]{0,1:T(8,128)(2,1)S(1)} collective-permute-done((bf16[512,512]{0,1:T(8,128)(2,1)S(1)}, bf16[512,512]{0,1:T(8,128)(2,1)S(1)}, u32[]{:S(2)}, u32[]{:S(2)}) %collective-permute-start.22) | collective-permute-done | bytes 524320 | tf_op jit(solution)/shard_map/ppermute | solution.py:19
  538.3 4.7 convolution_convert_fusion.2
  543.0 6.5 pad_maximum_fusion
  550.8 5.3 convolution_convert_fusion.4
  556.3 12.1 %collective-permute-start.23 = (bf16[128,2304]{1,0:T(8,128)(2,1)S(1)}, bf16[128,2304]{1,0:T(8,128)(2,1)S(1)}, u32[]{:S(2)}, u32[]{:S(2)}) collective-permute-start(bf16[128,2304]{1,0:T(8,128)(2,1)S(1)} %get-tuple-element.51), channel_id=1, source_target_pairs={{0,2},{1,3},{2,0},{3,1},{4,6},{5,7},{6,4},{7,5},{8,10},{9,11},{10,... | collective-permute-start | bytes 1769480 | tf_op jit(solution)/shard_map/ppermute | solution.py:24
  575.0 33.4 %collective-permute-done.23 = bf16[128,2304]{1,0:T(8,128)(2,1)S(1)} collective-permute-done((bf16[128,2304]{1,0:T(8,128)(2,1)S(1)}, bf16[128,2304]{1,0:T(8,128)(2,1)S(1)}, u32[]{:S(2)}, u32[]{:S(2)}) %collective-permute-start.23) | collective-permute-done | bytes 589856 | tf_op jit(solution)/shard_map/ppermute | solution.py:24
  609.3 38.0 %collective-permute-start.29 = (f32[4,2304]{1,0:T(4,128)S(1)}, f32[4,2304]{1,0:T(4,128)S(1)}, u32[]{:S(2)}, u32[]{:S(2)}) collective-permute-start(f32[4,2304]{1,0:T(4,128)S(1)} %pad_maximum_fusion.15), channel_id=1, source_target_pairs={{0,1},{1,0},{2,3},{3,2},{4,5},{5,4},{6,7},{7,6},{8,9},{9,8},{10,11... | collective-permute-start | bytes 110600 | tf_op jit(solution)/shard_map/ppermute | solution.py:91
  647.2 11.3 %collective-permute-done.10 = bf16[128,2304]{1,0:T(8,128)(2,1)S(1)} collective-permute-done((bf16[128,2304]{1,0:T(8,128)(2,1)S(1)}, bf16[128,2304]{1,0:T(8,128)(2,1)S(1)}, u32[]{:S(2)}, u32[]{:S(2)}) %collective-permute-start.10) | collective-permute-done | bytes 589856 | tf_op jit(solution)/shard_map/ppermute | solution.py:24
  658.8 11.0 %collective-permute-done.30 = f32[4,2304]{1,0:T(4,128)S(1)} collective-permute-done((f32[4,2304]{1,0:T(4,128)S(1)}, f32[4,2304]{1,0:T(4,128)S(1)}, u32[]{:S(2)}, u32[]{:S(2)}) %collective-permute-start.30) | collective-permute-done | bytes 36896 | tf_op jit(solution)/shard_map/ppermute | solution.py:91
  677.2 2.9 collective-permute-start.28
  681.8 33.5 %collective-permute-done.26 = bf16[128,2304]{1,0:T(8,128)(2,1)S(1)} collective-permute-done((bf16[128,2304]{1,0:T(8,128)(2,1)S(1)}, bf16[128,2304]{1,0:T(8,128)(2,1)S(1)}, u32[]{:S(2)}, u32[]{:S(2)}) %collective-permute-start.26) | collective-permute-done | bytes 589856 | tf_op jit(solution)/shard_map/ppermute | solution.py:24
  720.5 3.1 convert_element_type.223
  723.6 128.8 %reduce-scatter.6.cloned.1.call-done = bf16[288,4608]{1,0:T(8,128)(2,1)} async-done(((bf16[2304,4608]{1,0:T(8,128)(2,1)}), bf16[288,4608]{1,0:T(8,128)(2,1)}) %reduce-scatter.6.cloned.1.call-update) | async-done | bytes 2654224 | tf_op jit(solution)/shard_map/reduce_scatter | solution.py:114
  852.4 4.5 fusion.95
  (232 shorter events, 81.1 us)
Async XLA Ops:
  7.2 54.7 %all-gather.4.cloned.1.call-start = ((), (), s32[]{:S(2)}) async-start(), calls=%async_computation.3 | async-start | bytes 7962624 | tf_op jit(solution)/shard_map/all_gather | solution.py:110
  9.6 196.1 %all-gather.6.cloned.1.call-start = ((), (), s32[]{:S(2)}) async-start(), calls=%async_computation.4 | async-start | bytes 23887872 | tf_op jit(solution)/shard_map/all_gather | solution.py:110
  11.4 50.6 %copy-start.30 = (f32[2304]{0:T(1024)S(1)}, f32[2304]{0:T(1024)}, u32[]{:S(2)}) copy-start(f32[2304]{0:T(1024)} %param.17) | copy-start | bytes 27652
  11.4 233.0 %all-gather.8.cloned.1.call-start = ((), (), s32[]{:S(2)}) async-start(), calls=%async_computation.5 | async-start | bytes 11943936 | tf_op jit(solution)/shard_map/all_gather | solution.py:110
  12.1 704.0 %reduce-scatter.4.cloned.1.call-start = ((), (), s32[]{:S(2)}) async-start(), calls=%async_computation.6 | async-start | bytes 7962624 | tf_op jit(solution)/shard_map/reduce_scatter | solution.py:114
  13.6 53.4 %copy-start.40 = (f32[512]{0:T(512)}, f32[512]{0:T(512)S(1)}, u32[]{:S(2)}) copy-start(f32[512]{0:T(512)S(1)} %add_rsqrt_fusion) | copy-start | bytes 6148
  13.6 56.9 %copy-start.39 = (s32[1024]{0:T(1024)S(1)}, s32[1024]{0:T(1024)}, u32[]{:S(2)}) copy-start(s32[1024]{0:T(1024)} %param.16) | copy-start | bytes 12292
  67.0 23.0 %collective-permute-start = (bf16[512,512]{1,0:T(8,128)(2,1)S(1)}, bf16[512,512]{1,0:T(8,128)(2,1)S(1)}, u32[]{:S(2)}, u32[]{:S(2)}) collective-permute-start(bf16[512,512]{1,0:T(8,128)(2,1)S(1)} %get-tuple-element.65), channel_id=1, source_target_pairs={{0,4},{1,5},{2,6},{3,7},{8,12},{9,13},{10,14},{11,15},{16,20},{17,... | collective-permute-start | bytes 1572872 | tf_op jit(solution)/shard_map/ppermute | solution.py:19
  98.3 43.9 %copy-start.25 = (f32[2304]{0:T(1024)S(1)}, f32[2304]{0:T(1024)}, u32[]{:S(2)}) copy-start(f32[2304]{0:T(1024)} %param.18) | copy-start | bytes 27652
  98.3 40.4 %collective-permute-start.1 = (bf16[128,2304]{1,0:T(8,128)(2,1)}, bf16[128,2304]{1,0:T(8,128)(2,1)S(1)}, u32[]{:S(2)}, u32[]{:S(2)}) collective-permute-start(bf16[128,2304]{1,0:T(8,128)(2,1)} %get-tuple-element.61), channel_id=1, source_target_pairs={{0,2},{1,3},{2,0},{3,1},{4,6},{5,7},{6,4},{7,5},{8,10},{9,11},{10,... | collective-permute-start | bytes 1769480 | tf_op jit(solution)/shard_map/ppermute | solution.py:24
  100.4 38.2 %collective-permute-start.2 = (bf16[128,2304]{1,0:T(8,128)(2,1)}, bf16[128,2304]{1,0:T(8,128)(2,1)S(1)}, u32[]{:S(2)}, u32[]{:S(2)}) collective-permute-start(bf16[128,2304]{1,0:T(8,128)(2,1)} %get-tuple-element.63), channel_id=1, source_target_pairs={{0,1},{1,2},{2,3},{3,0},{4,5},{5,6},{6,7},{7,4},{8,9},{9,10},{10,1... | collective-permute-start | bytes 1769480 | tf_op jit(solution)/shard_map/ppermute | solution.py:24
  101.9 38.4 %collective-permute-start.3 = (bf16[128,2304]{1,0:T(8,128)(2,1)}, bf16[128,2304]{1,0:T(8,128)(2,1)}, u32[]{:S(2)}, u32[]{:S(2)}) collective-permute-start(bf16[128,2304]{1,0:T(8,128)(2,1)} %get-tuple-element.62), channel_id=1, source_target_pairs={{0,3},{1,0},{2,1},{3,2},{4,7},{5,4},{6,5},{7,6},{8,11},{9,8},{10,9... | collective-permute-start | bytes 1769480 | tf_op jit(solution)/shard_map/ppermute | solution.py:24
  144.2 76.5 %copy-start.45 = (f32[128]{0:T(128)}, f32[128]{0:T(128)S(1)}, u32[]{:S(2)}) copy-start(f32[128]{0:T(128)S(1)} %get-tuple-element.41) | copy-start | bytes 1540
  144.2 76.5 %copy-start.36 = (f32[128]{0:T(128)}, f32[128]{0:T(128)S(1)}, u32[]{:S(2)}) copy-start(f32[128]{0:T(128)S(1)} %fusion.77) | copy-start | bytes 1540
  144.4 76.3 %copy-start.19 = (bf16[128,2304]{1,0:T(8,128)(2,1)}, bf16[128,2304]{1,0:T(8,128)(2,1)S(1)}, u32[]{:S(2)}) copy-start(bf16[128,2304]{1,0:T(8,128)(2,1)S(1)} %multiply_convert_fusion.2) | copy-start | bytes 1769476
  144.4 37.6 %collective-permute-start.4 = (bf16[128,2304]{1,0:T(8,128)(2,1)S(1)}, bf16[128,2304]{1,0:T(8,128)(2,1)S(1)}, u32[]{:S(2)}, u32[]{:S(2)}) collective-permute-start(bf16[128,2304]{1,0:T(8,128)(2,1)S(1)} %multiply_convert_fusion.2), channel_id=1, source_target_pairs={{0,1},{1,2},{2,3},{3,0},{4,5},{5,6},{6,7},{7,4},{8,9},{9,10},{10,1... | collective-permute-start | bytes 1769480 | tf_op jit(solution)/shard_map/ppermute | solution.py:24
  168.3 27.7 %collective-permute-start.5 = (bf16[128,2304]{1,0:T(8,128)(2,1)S(1)}, bf16[128,2304]{1,0:T(8,128)(2,1)S(1)}, u32[]{:S(2)}, u32[]{:S(2)}) collective-permute-start(bf16[128,2304]{1,0:T(8,128)(2,1)S(1)} %multiply_convert_fusion.2), channel_id=1, source_target_pairs={{0,2},{1,3},{2,0},{3,1},{4,6},{5,7},{6,4},{7,5},{8,10},{9,11},{10,... | collective-permute-start | bytes 1769480 | tf_op jit(solution)/shard_map/ppermute | solution.py:24
  168.3 37.4 %collective-permute-start.6 = (bf16[128,2304]{1,0:T(8,128)(2,1)S(1)}, bf16[128,2304]{1,0:T(8,128)(2,1)}, u32[]{:S(2)}, u32[]{:S(2)}) collective-permute-start(bf16[128,2304]{1,0:T(8,128)(2,1)S(1)} %multiply_convert_fusion.2), channel_id=1, source_target_pairs={{0,3},{1,0},{2,1},{3,2},{4,7},{5,4},{6,5},{7,6},{8,11},{9,8},{10,9... | collective-permute-start | bytes 1769480 | tf_op jit(solution)/shard_map/ppermute | solution.py:24
  254.8 43.3 %copy-start.16 = (bf16[512,2304]{1,0:T(8,128)(2,1)S(1)}, bf16[512,2304]{1,0:T(8,128)(2,1)}, u32[]{:S(2)}) copy-start(bf16[512,2304]{1,0:T(8,128)(2,1)} %param.15) | copy-start | bytes 7077892
  254.8 30.4 %collective-permute-start.7 = (bf16[128,2304]{1,0:T(8,128)(2,1)S(1)}, bf16[128,2304]{1,0:T(8,128)(2,1)S(1)}, u32[]{:S(2)}, u32[]{:S(2)}) collective-permute-start(bf16[128,2304]{1,0:T(8,128)(2,1)S(1)} %get-tuple-element.58), channel_id=1, source_target_pairs={{0,2},{1,3},{2,0},{3,1},{4,6},{5,7},{6,4},{7,5},{8,10},{9,11},{10,... | collective-permute-start | bytes 1769480 | tf_op jit(solution)/shard_map/ppermute | solution.py:24
  257.3 27.9 %collective-permute-start.8 = (bf16[128,2304]{1,0:T(8,128)(2,1)S(1)}, bf16[128,2304]{1,0:T(8,128)(2,1)S(1)}, u32[]{:S(2)}, u32[]{:S(2)}) collective-permute-start(bf16[128,2304]{1,0:T(8,128)(2,1)S(1)} %get-tuple-element.60), channel_id=1, source_target_pairs={{0,3},{1,0},{2,1},{3,2},{4,7},{5,4},{6,5},{7,6},{8,11},{9,8},{10,9... | collective-permute-start | bytes 1769480 | tf_op jit(solution)/shard_map/ppermute | solution.py:24
  258.8 38.9 %collective-permute-start.9 = (bf16[128,2304]{1,0:T(8,128)(2,1)S(1)}, bf16[128,2304]{1,0:T(8,128)(2,1)S(1)}, u32[]{:S(2)}, u32[]{:S(2)}) collective-permute-start(bf16[128,2304]{1,0:T(8,128)(2,1)S(1)} %get-tuple-element.59), channel_id=1, source_target_pairs={{0,1},{1,2},{2,3},{3,0},{4,5},{5,6},{6,7},{7,4},{8,9},{9,10},{10,1... | collective-permute-start | bytes 1769480 | tf_op jit(solution)/shard_map/ppermute | solution.py:24
  300.3 38.9 %collective-permute-start.13 = (bf16[128,2304]{1,0:T(8,128)(2,1)}, bf16[128,2304]{1,0:T(8,128)(2,1)}, u32[]{:S(2)}, u32[]{:S(2)}) collective-permute-start(bf16[128,2304]{1,0:T(8,128)(2,1)} %fusion.48), channel_id=1, source_target_pairs={{0,1},{1,2},{2,3},{3,0},{4,5},{5,6},{6,7},{7,4},{8,9},{9,10},{10,1... | collective-permute-start | bytes 1769480 | tf_op jit(solution)/shard_map/ppermute | solution.py:24
  325.1 28.0 %collective-permute-start.14 = (bf16[128,2304]{1,0:T(8,128)(2,1)}, bf16[128,2304]{1,0:T(8,128)(2,1)}, u32[]{:S(2)}, u32[]{:S(2)}) collective-permute-start(bf16[128,2304]{1,0:T(8,128)(2,1)} %fusion.48), channel_id=1, source_target_pairs={{0,2},{1,3},{2,0},{3,1},{4,6},{5,7},{6,4},{7,5},{8,10},{9,11},{10,... | collective-permute-start | bytes 1769480 | tf_op jit(solution)/shard_map/ppermute | solution.py:24
  325.1 37.8 %collective-permute-start.15 = (bf16[128,2304]{1,0:T(8,128)(2,1)}, bf16[128,2304]{1,0:T(8,128)(2,1)}, u32[]{:S(2)}, u32[]{:S(2)}) collective-permute-start(bf16[128,2304]{1,0:T(8,128)(2,1)} %fusion.48), channel_id=1, source_target_pairs={{0,3},{1,0},{2,1},{3,2},{4,7},{5,4},{6,5},{7,6},{8,11},{9,8},{10,9... | collective-permute-start | bytes 1769480 | tf_op jit(solution)/shard_map/ppermute | solution.py:24
  409.8 34.6 %collective-permute-start.16 = (bf16[128,2304]{1,0:T(8,128)(2,1)}, bf16[128,2304]{1,0:T(8,128)(2,1)}, u32[]{:S(2)}, u32[]{:S(2)}) collective-permute-start(bf16[128,2304]{1,0:T(8,128)(2,1)} %get-tuple-element.55), channel_id=1, source_target_pairs={{0,2},{1,3},{2,0},{3,1},{4,6},{5,7},{6,4},{7,5},{8,10},{9,11},{10,... | collective-permute-start | bytes 1769480 | tf_op jit(solution)/shard_map/ppermute | solution.py:24
  413.3 31.2 %collective-permute-start.17 = (bf16[128,2304]{1,0:T(8,128)(2,1)}, bf16[128,2304]{1,0:T(8,128)(2,1)}, u32[]{:S(2)}, u32[]{:S(2)}) collective-permute-start(bf16[128,2304]{1,0:T(8,128)(2,1)} %get-tuple-element.57), channel_id=1, source_target_pairs={{0,3},{1,0},{2,1},{3,2},{4,7},{5,4},{6,5},{7,6},{8,11},{9,8},{10,9... | collective-permute-start | bytes 1769480 | tf_op jit(solution)/shard_map/ppermute | solution.py:24
  425.5 38.0 %collective-permute-start.18 = (bf16[128,2304]{1,0:T(8,128)(2,1)}, bf16[128,2304]{1,0:T(8,128)(2,1)}, u32[]{:S(2)}, u32[]{:S(2)}) collective-permute-start(bf16[128,2304]{1,0:T(8,128)(2,1)} %get-tuple-element.56), channel_id=1, source_target_pairs={{0,1},{1,2},{2,3},{3,0},{4,5},{5,6},{6,7},{7,4},{8,9},{9,10},{10,1... | collective-permute-start | bytes 1769480 | tf_op jit(solution)/shard_map/ppermute | solution.py:24
  470.6 42.2 %collective-permute-start.19 = (bf16[128,2304]{1,0:T(8,128)(2,1)S(1)}, bf16[128,2304]{1,0:T(8,128)(2,1)S(1)}, u32[]{:S(2)}, u32[]{:S(2)}) collective-permute-start(bf16[128,2304]{1,0:T(8,128)(2,1)S(1)} %fusion.49), channel_id=1, source_target_pairs={{0,2},{1,3},{2,0},{3,1},{4,6},{5,7},{6,4},{7,5},{8,10},{9,11},{10,... | collective-permute-start | bytes 1769480 | tf_op jit(solution)/shard_map/ppermute | solution.py:24
  473.7 39.1 %collective-permute-start.20 = (bf16[128,2304]{1,0:T(8,128)(2,1)S(1)}, bf16[128,2304]{1,0:T(8,128)(2,1)S(1)}, u32[]{:S(2)}, u32[]{:S(2)}) collective-permute-start(bf16[128,2304]{1,0:T(8,128)(2,1)S(1)} %fusion.49), channel_id=1, source_target_pairs={{0,1},{1,2},{2,3},{3,0},{4,5},{5,6},{6,7},{7,4},{8,9},{9,10},{10,1... | collective-permute-start | bytes 1769480 | tf_op jit(solution)/shard_map/ppermute | solution.py:24
  474.2 39.7 %collective-permute-start.21 = (bf16[128,2304]{1,0:T(8,128)(2,1)S(1)}, bf16[128,2304]{1,0:T(8,128)(2,1)S(1)}, u32[]{:S(2)}, u32[]{:S(2)}) collective-permute-start(bf16[128,2304]{1,0:T(8,128)(2,1)S(1)} %fusion.49), channel_id=1, source_target_pairs={{0,3},{1,0},{2,1},{3,2},{4,7},{5,4},{6,5},{7,6},{8,11},{9,8},{10,9... | collective-permute-start | bytes 1769480 | tf_op jit(solution)/shard_map/ppermute | solution.py:24
  523.6 14.4 %collective-permute-start.22 = (bf16[512,512]{0,1:T(8,128)(2,1)S(1)}, bf16[512,512]{0,1:T(8,128)(2,1)S(1)}, u32[]{:S(2)}, u32[]{:S(2)}) collective-permute-start(bf16[512,512]{0,1:T(8,128)(2,1)S(1)} %fusion.63), channel_id=1, source_target_pairs={{4,0},{5,1},{6,2},{7,3},{12,8},{13,9},{14,10},{15,11},{20,16},{21,... | collective-permute-start | bytes 1572872 | tf_op jit(solution)/shard_map/ppermute | solution.py:19
  549.6 171.0 %reduce-scatter.8.cloned.1.call-start = ((), (), s32[]{:S(2)}) async-start(), calls=%async_computation.8 | async-start | bytes 11943936 | tf_op jit(solution)/shard_map/reduce_scatter | solution.py:114
  550.2 302.2 %reduce-scatter.6.cloned.1.call-start = ((), (), s32[]{:S(2)}) async-start(), calls=%async_computation.7 | async-start | bytes 23887872 | tf_op jit(solution)/shard_map/reduce_scatter | solution.py:114
  556.3 52.1 %collective-permute-start.23 = (bf16[128,2304]{1,0:T(8,128)(2,1)S(1)}, bf16[128,2304]{1,0:T(8,128)(2,1)S(1)}, u32[]{:S(2)}, u32[]{:S(2)}) collective-permute-start(bf16[128,2304]{1,0:T(8,128)(2,1)S(1)} %get-tuple-element.51), channel_id=1, source_target_pairs={{0,2},{1,3},{2,0},{3,1},{4,6},{5,7},{6,4},{7,5},{8,10},{9,11},{10,... | collective-permute-start | bytes 1769480 | tf_op jit(solution)/shard_map/ppermute | solution.py:24
  568.4 40.0 %collective-permute-start.24 = (bf16[128,2304]{1,0:T(8,128)(2,1)S(1)}, bf16[128,2304]{1,0:T(8,128)(2,1)S(1)}, u32[]{:S(2)}, u32[]{:S(2)}) collective-permute-start(bf16[128,2304]{1,0:T(8,128)(2,1)S(1)} %get-tuple-element.53), channel_id=1, source_target_pairs={{0,1},{1,2},{2,3},{3,0},{4,5},{5,6},{6,7},{7,4},{8,9},{9,10},{10,1... | collective-permute-start | bytes 1769480 | tf_op jit(solution)/shard_map/ppermute | solution.py:24
  569.6 38.9 %collective-permute-start.25 = (bf16[128,2304]{1,0:T(8,128)(2,1)S(1)}, bf16[128,2304]{1,0:T(8,128)(2,1)S(1)}, u32[]{:S(2)}, u32[]{:S(2)}) collective-permute-start(bf16[128,2304]{1,0:T(8,128)(2,1)S(1)} %get-tuple-element.52), channel_id=1, source_target_pairs={{0,3},{1,0},{2,1},{3,2},{4,7},{5,4},{6,5},{7,6},{8,11},{9,8},{10,9... | collective-permute-start | bytes 1769480 | tf_op jit(solution)/shard_map/ppermute | solution.py:24
  572.7 85.8 %collective-permute-start.10 = (bf16[128,2304]{1,0:T(8,128)(2,1)S(1)}, bf16[128,2304]{1,0:T(8,128)(2,1)S(1)}, u32[]{:S(2)}, u32[]{:S(2)}) collective-permute-start(bf16[128,2304]{1,0:T(8,128)(2,1)S(1)} %get-tuple-element.38), channel_id=1, source_target_pairs={{0,2},{1,3},{2,0},{3,1},{4,6},{5,7},{6,4},{7,5},{8,10},{9,11},{10,... | collective-permute-start | bytes 1769480 | tf_op jit(solution)/shard_map/ppermute | solution.py:24
  572.9 85.8 %collective-permute-start.11 = (bf16[128,2304]{1,0:T(8,128)(2,1)S(1)}, bf16[128,2304]{1,0:T(8,128)(2,1)S(1)}, u32[]{:S(2)}, u32[]{:S(2)}) collective-permute-start(bf16[128,2304]{1,0:T(8,128)(2,1)S(1)} %get-tuple-element.38), channel_id=1, source_target_pairs={{0,1},{1,2},{2,3},{3,0},{4,5},{5,6},{6,7},{7,4},{8,9},{9,10},{10,1... | collective-permute-start | bytes 1769480 | tf_op jit(solution)/shard_map/ppermute | solution.py:24
  608.4 67.8 %collective-permute-start.12 = (bf16[128,2304]{1,0:T(8,128)(2,1)S(1)}, bf16[128,2304]{1,0:T(8,128)(2,1)S(1)}, u32[]{:S(2)}, u32[]{:S(2)}) collective-permute-start(bf16[128,2304]{1,0:T(8,128)(2,1)S(1)} %get-tuple-element.38), channel_id=1, source_target_pairs={{0,3},{1,0},{2,1},{3,2},{4,7},{5,4},{6,5},{7,6},{8,11},{9,8},{10,9... | collective-permute-start | bytes 1769480 | tf_op jit(solution)/shard_map/ppermute | solution.py:24
  609.3 49.3 %collective-permute-start.29 = (f32[4,2304]{1,0:T(4,128)S(1)}, f32[4,2304]{1,0:T(4,128)S(1)}, u32[]{:S(2)}, u32[]{:S(2)}) collective-permute-start(f32[4,2304]{1,0:T(4,128)S(1)} %pad_maximum_fusion.15), channel_id=1, source_target_pairs={{0,1},{1,0},{2,3},{3,2},{4,5},{5,4},{6,7},{7,6},{8,9},{9,8},{10,11... | collective-permute-start | bytes 110600 | tf_op jit(solution)/shard_map/ppermute | solution.py:91
  658.6 11.2 %collective-permute-start.30 = (f32[4,2304]{1,0:T(4,128)S(1)}, f32[4,2304]{1,0:T(4,128)S(1)}, u32[]{:S(2)}, u32[]{:S(2)}) collective-permute-start(f32[4,2304]{1,0:T(4,128)S(1)} %fusion.89), channel_id=1, source_target_pairs={{0,2},{1,3},{2,0},{3,1},{4,6},{5,7},{6,4},{7,5},{8,10},{9,11},{10,... | collective-permute-start | bytes 110600 | tf_op jit(solution)/shard_map/ppermute | solution.py:91
  669.8 1.3 collective-permute-start.31
  671.1 5.0 collective-permute-start.32
  672.8 42.5 %collective-permute-start.26 = (bf16[128,2304]{1,0:T(8,128)(2,1)S(1)}, bf16[128,2304]{1,0:T(8,128)(2,1)S(1)}, u32[]{:S(2)}, u32[]{:S(2)}) collective-permute-start(bf16[128,2304]{1,0:T(8,128)(2,1)S(1)} %get-tuple-element.34), channel_id=1, source_target_pairs={{0,2},{1,3},{2,0},{3,1},{4,6},{5,7},{6,4},{7,5},{8,10},{9,11},{10,... | collective-permute-start | bytes 1769480 | tf_op jit(solution)/shard_map/ppermute | solution.py:24
  676.1 4.9 collective-permute-start.33
  676.3 39.0 %collective-permute-start.27 = (bf16[128,2304]{1,0:T(8,128)(2,1)S(1)}, bf16[128,2304]{1,0:T(8,128)(2,1)S(1)}, u32[]{:S(2)}, u32[]{:S(2)}) collective-permute-start(bf16[128,2304]{1,0:T(8,128)(2,1)S(1)} %get-tuple-element.34), channel_id=1, source_target_pairs={{0,1},{1,2},{2,3},{3,0},{4,5},{5,6},{6,7},{7,4},{8,9},{9,10},{10,1... | collective-permute-start | bytes 1769480 | tf_op jit(solution)/shard_map/ppermute | solution.py:24
  677.2 38.8 %collective-permute-start.28 = (bf16[128,2304]{1,0:T(8,128)(2,1)S(1)}, bf16[128,2304]{1,0:T(8,128)(2,1)S(1)}, u32[]{:S(2)}, u32[]{:S(2)}) collective-permute-start(bf16[128,2304]{1,0:T(8,128)(2,1)S(1)} %get-tuple-element.34), channel_id=1, source_target_pairs={{0,3},{1,0},{2,1},{3,2},{4,7},{5,4},{6,5},{7,6},{8,11},{9,8},{10,9... | collective-permute-start | bytes 1769480 | tf_op jit(solution)/shard_map/ppermute | solution.py:24
  (46 other events, 432.8 us)
Sparse Core Ops, SparseCore 0:
  10.5 51.4 all-gather.3
  64.4 114.3 all-gather.5
  180.7 63.6 all-gather.7
  549.7 74.7 reduce-scatter.3
  627.9 83.3 reduce-scatter.7
  714.8 137.5 reduce-scatter.5

commit v3 on v2

--- a/solution.py
+++ b/solution.py
@@ -19,11 +19,6 @@
     return lax.ppermute(block, axis, route)
 
 
-def shift(block, distance):
-    size = lax.axis_size("tp")
-    return lax.ppermute(block, "tp", [(i, (i + distance) % size) for i in range(size)])
-
-
 def rms(value, gain):
     return value * lax.rsqrt(jnp.mean(value * value, axis=-1, keepdims=True) + EPS) * gain
 
@@ -44,44 +39,61 @@
     return lax.dot_general(left, right, (((1,), (1,)), ((), ())), preferred_element_type=F32)
 
 
-def distances(size):
-    return sorted(range(1, size), key=lambda k: (abs(2 * k - size), k))
-
-
-def scattered(partial):
+def onward(block, distance, senders):
+    return lax.ppermute(block, "tp", [(i, i + distance) for i in senders])
+
+
+def scattered(blocks):
+    size = lax.axis_size("tp")
+    rising, falling = None, None
+    for step in range(1, size):
+        rise, fall = blocks[step], blocks[size - step]
+        if rising is not None:
+            rise = (rise.astype(F32) + rising.astype(F32)).astype(LOW)
+            fall = (fall.astype(F32) + falling.astype(F32)).astype(LOW)
+        rise, fall = lax.optimization_barrier((rise, fall))
+        rising = onward(rise, 1, range(step))
+        falling = onward(fall, -1, range(size - step, size))
+    return blocks[0].astype(F32) + (rising.astype(F32) + falling.astype(F32))
+
+
+def gathered(block):
+    size = lax.axis_size("tp")
+    rank = lax.axis_index("tp")
+    rising, falling = [block], [block]
+    for step in range(1, size):
+        rise = onward(rising[-1], 1, range(step - 1, size - 1))
+        fall = onward(falling[-1], -1, range(1, size - step + 1))
+        rise, fall = lax.optimization_barrier((rise, fall))
+        rising.append(rise)
+        falling.append(fall)
+    return [block] + [
+        jnp.where(rank >= k, rising[k], falling[size - k]) for k in range(1, size)
+    ]
+
+
+def turned_blocks(partial):
+    size = lax.axis_size("tp")
+    blocks = partial.reshape(size, -1, partial.shape[-1])
+    return [blocks[k] for k in range(size)]
+
+
+def ordered_blocks(partial):
     size = lax.axis_size("tp")
     rank = lax.axis_index("tp")
     blocks = partial.reshape(size, -1, partial.shape[-1])
-    total = lax.dynamic_index_in_dim(blocks, rank, 0, False).astype(F32)
-    for k in distances(size):
-        block = lax.dynamic_index_in_dim(blocks, (rank + k) % size, 0, False)
-        total = total + shift(block, k).astype(F32)
-    return total
-
-
-def gathered(block):
+    return [
+        lax.dynamic_index_in_dim(blocks, (rank - k) % size, 0, False) for k in range(size)
+    ]
+
+
+def in_order(pieces):
     size = lax.axis_size("tp")
     rank = lax.axis_index("tp")
-    whole = jnp.zeros((size,) + block.shape, block.dtype)
-    whole = lax.dynamic_update_index_in_dim(whole, block, rank, 0)
-    for k in distances(size):
-        whole = lax.dynamic_update_index_in_dim(whole, shift(block, k), (rank - k) % size, 0)
-    return whole.reshape(-1, block.shape[-1])
-
-
-def gathered_turned(block):
-    size = lax.axis_size("tp")
-    pieces = {k: shift(block, k) for k in distances(size)}
-    return jnp.concatenate([block] + [pieces[k] for k in range(1, size)], axis=0)
-
-
-def scattered_turned(partial):
-    size = lax.axis_size("tp")
-    blocks = partial.reshape(size, -1, partial.shape[-1])
-    total = blocks[0].astype(F32)
-    for k in distances(size):
-        total = total + shift(blocks[k], -k).astype(F32)
-    return total
+    whole = jnp.zeros((size,) + pieces[0].shape, pieces[0].dtype)
+    for k in range(size):
+        whole = lax.dynamic_update_index_in_dim(whole, pieces[k], (rank - k) % size, 0)
+    return whole.reshape(-1, pieces[0].shape[-1])
 
 
 def summed(value, axis):
@@ -179,31 +191,36 @@
     attended = jnp.einsum("grqk,kgd->qgrd", probs_low, values_all, preferred_element_type=F32)
     attended_low = attended.reshape(length, -1).astype(LOW)
 
-    branch_one = scattered(transposed_product(attended_low, output_full).astype(LOW))
+    branch_one = scattered(
+        ordered_blocks(transposed_product(attended_low, output_full).astype(LOW))
+    )
     middle = inputs + rms(branch_one, post_attention_gain)
     normed_two_own = rms(middle, pre_feedforward_gain).astype(LOW)
-    normed_two = gathered_turned(normed_two_own)
+    normed_two = jnp.concatenate(gathered(normed_two_own), axis=0)
 
     gate_up = product(normed_two, gate_up_full)
     gate_value = gate_up[:, :units]
     up_value = gate_up[:, units:]
     hidden_low = geglu(gate_value, up_value).astype(LOW)
-    branch_two = scattered_turned(transposed_product(hidden_low, down_full).astype(LOW))
+    branch_two = scattered(
+        turned_blocks(transposed_product(hidden_low, down_full).astype(LOW))
+    )
     result = middle + rms(branch_two, post_feedforward_gain)
 
     _, pull_four = jax.vjp(rms, branch_two, post_feedforward_gain)
     grad_branch_two, grad_gain_four = pull_four(upstream)
-    grad_two_low = gathered_turned(grad_branch_two.astype(LOW))
+    grad_two_low = jnp.concatenate(gathered(grad_branch_two.astype(LOW)), axis=0)
 
     grad_down_low, grad_two_low = lax.optimization_barrier(
         (rows_product(grad_two_low, hidden_low).astype(LOW), grad_two_low)
     )
     down_share = share_rows(grad_down_low)
-    grad_hidden_units = product(grad_two_low, down_full)
     _, pull_glu = jax.vjp(geglu, gate_value, up_value)
-    grad_gate, grad_up = pull_glu(grad_hidden_units)
+    grad_gate, grad_up = pull_glu(product(grad_two_low, down_full))
     grad_gate_up = jnp.concatenate([grad_gate.astype(LOW), grad_up.astype(LOW)], axis=1)
-    grad_normed_two = scattered_turned(transposed_product(grad_gate_up, gate_up_full).astype(LOW))
+    grad_normed_two = scattered(
+        turned_blocks(transposed_product(grad_gate_up, gate_up_full).astype(LOW))
+    )
     grad_gate_up_low = rows_product(normed_two, grad_gate_up).astype(LOW)
 
     _, pull_three = jax.vjp(rms, middle, pre_feedforward_gain)
@@ -215,7 +232,9 @@
         (grad_branch_one.astype(LOW), grad_gate_up_low)
     )
     gate_up_share = share_rows(grad_gate_up_low)
-    grad_one_low = gathered(grad_one_own)
+    grad_one_low = in_order(gathered(grad_one_own))
+    result_low, grad_one_low = lax.optimization_barrier((result.astype(LOW), grad_one_low))
+    outputs = in_order(gathered(result_low))
 
     grad_output_full = rows_product(grad_one_low, attended_low)
     grad_attended = (
@@ -247,13 +266,14 @@
     grad_kv_back = passed_along(grad_kv_all[:length].astype(LOW), "ctx", -1).astype(F32)
     grad_kv_low = (grad_kv_all[length:] + grad_kv_back).astype(LOW)
     grad_qkv = jnp.concatenate([grad_query_low, grad_kv_low], axis=1)
-    grad_normed_one = scattered(transposed_product(grad_qkv, qkv_full).astype(LOW))
+    grad_normed_one = scattered(
+        ordered_blocks(transposed_product(grad_qkv, qkv_full).astype(LOW))
+    )
     grad_qkv_full = rows_product(normed_one, grad_qkv)
 
     _, pull_one = jax.vjp(rms, inputs, pre_attention_gain)
     grad_inputs_norm, grad_gain_one = pull_one(grad_normed_one)
-    grad_inputs = gathered((grad_middle + grad_inputs_norm).astype(LOW))
-    outputs = gathered(result.astype(LOW))
+    grad_inputs = in_order(gathered((grad_middle + grad_inputs_norm).astype(LOW)))
 
     gains = jnp.stack([grad_gain_one, grad_gain_two, grad_gain_three, grad_gain_four])
     for axis in ("tp",) + ROWS:

time: 872 us -> 854 us (0.979)
  starting transfers between devices: 157 us -> 121 us
  other arithmetic: 38.6 us -> 57.3 us
    ppermute x5, starting transfers between devices: 39.3 us -> 2.13 us  [summed(): lax.ppermute(value, axis, [(i, i ^ bit) for i in range(size)])]
    reduce_scatter x3, waiting for transfers between devices: 129 us -> 164 us  [share_rows(): return lax.psum_scatter(grad, ROWS, scatter_dimension=0, tiled=True)]
    ppermute x27 -> x54, waiting for transfers between devices: 275 us -> 243 us  [onward(): return lax.ppermute(block, 'tp', [(i, i + distance) for i in senders])]
    ppermute x5, waiting for transfers between devices: 14.3 us -> 3.65 us  [summed(): lax.ppermute(value, axis, [(i, i ^ bit) for i in range(size)])]
    dynamic_update_slice x2 -> x10, other arithmetic: 0.64 us -> 9.7 us  [in_order(): lax.dynamic_update_index_in_dim(whole, pieces[k], (rank - k) % size, 0)]
    ppermute x27 -> x54, starting transfers between devices: 112 us -> 113 us  [onward(): return lax.ppermute(block, 'tp', [(i, i + distance) for i in senders])]
  transfers between devices with their start and end apart: 40 -> 67, of which waited for: 25 -> 41; matrix products, arithmetic and copies ran while one was open for 9% -> 12% of each run, Pallas kernels for 0% -> 0%
where the time goes in v3:
time: 854 us; the launch traced here: 844 us
  waiting for transfers between devices  511 us (60%)
  starting transfers between devices  121 us (14%)
  matrix products  114 us (13%)
  other arithmetic  57.3 us (7%)
  local copies, waits for them, and re-layouts  24.7 us (3%)
  between operations  16 us (2%)
    ppermute x54, waiting for transfers between devices, onward(): return lax.ppermute(block, 'tp', [(i, i + distance) for i in senders])  243 us
    reduce_scatter x3, waiting for transfers between devices, share_rows(): return lax.psum_scatter(grad, ROWS, scatter_dimension=0, tiled=True)  164 us
    ppermute x54, starting transfers between devices, onward(): return lax.ppermute(block, 'tp', [(i, i + distance) for i in senders])  113 us
    all_gather x3, waiting for transfers between devices, gather_rows(): return lax.all_gather(weight, ROWS, axis=0, tiled=True)  74.1 us
    dot_general x4, matrix products, product(): return jnp.dot(left, right, preferred_element_type=F32)  37.3 us
    dot_general x4, matrix products, transposed_product(): lax.dot_general(left, right, (((1,), (1,)), ((), ())), preferred_element_...  34.6 us
    dot_general x4, matrix products, rows_product(): lax.dot_general(left, right, (((0,), (0,)), ((), ())), preferred_element_...  34 us
    ppermute x2, waiting for transfers between devices, passed_along(): return lax.ppermute(block, axis, route)  24.3 us
  transfers between devices with their start and end apart: 67, of which 41 were waited for; matrix products, arithmetic and copies ran while one was open for 12% of the time, Pallas kernels for 0%

profile of v3, /device:TPU:0, one launch (start us, length us, event | category | flops | bytes accessed | tf_op | source)
XLA Modules:
  0.0 843.8 jit_solution(6946820080093617094)
XLA Ops:
  13.6 48.4 %all-gather.4.cloned.1.call-done = bf16[2304,1536]{1,0:T(8,128)(2,1)} async-done(((bf16[288,1536]{1,0:T(8,128)(2,1)}), bf16[2304,1536]{1,0:T(8,128)(2,1)}) %all-gather.4.cloned.1.call-update) | async-done | bytes 7077904 | tf_op jit(solution)/shard_map/all_gather | solution.py:122
  61.9 5.0 fusion.29
  71.9 18.2 %collective-permute-done = bf16[512,512]{1,0:T(8,128)(2,1)S(1)} collective-permute-done((bf16[512,512]{1,0:T(8,128)(2,1)S(1)}, bf16[512,512]{1,0:T(8,128)(2,1)S(1)}, u32[]{:S(2)}, u32[]{:S(2)}) %collective-permute-start) | collective-permute-done | bytes 524320 | tf_op jit(solution)/shard_map/ppermute | solution.py:19
  102.6 8.4 collective-permute-done.1
  113.1 5.1 collective-permute-start.3
  118.4 9.6 %collective-permute-done.3 = bf16[128,2304]{1,0:T(8,128)(2,1)S(1)} collective-permute-done((bf16[128,2304]{1,0:T(8,128)(2,1)S(1)}, bf16[128,2304]{1,0:T(8,128)(2,1)S(1)}, u32[]{:S(2)}, u32[]{:S(2)}) %collective-permute-start.3) | collective-permute-done | bytes 589856 | tf_op jit(solution)/shard_map/ppermute | solution.py:43
  128.2 5.6 collective-permute-start.5
  135.1 7.6 collective-permute-done.5
  142.7 5.0 collective-permute-done.6
  156.8 6.7 collective-permute-done.7
  163.5 5.3 collective-permute-done.8
  171.6 10.5 %collective-permute-done.10 = bf16[128,2304]{1,0:T(8,128)(2,1)} collective-permute-done((bf16[128,2304]{1,0:T(8,128)(2,1)}, bf16[128,2304]{1,0:T(8,128)(2,1)}, u32[]{:S(2)}, u32[]{:S(2)}) %collective-permute-start.10) | collective-permute-done | bytes 589856 | tf_op jit(solution)/shard_map/ppermute | solution.py:43
  185.4 9.3 %collective-permute-done.12 = bf16[128,2304]{1,0:T(8,128)(2,1)S(1)} collective-permute-done((bf16[128,2304]{1,0:T(8,128)(2,1)}, bf16[128,2304]{1,0:T(8,128)(2,1)S(1)}, u32[]{:S(2)}, u32[]{:S(2)}) %collective-permute-start.12) | collective-permute-done | bytes 589856 | tf_op jit(solution)/shard_map/ppermute | solution.py:43
  197.6 14.8 %fusion.73 = f32[512,4608]{1,0:T(8,128)S(1)} fusion(bf16[2304,4608]{1,0:T(8,128)(2,1)} %all-gather.6.cloned.1.call-done, bf16[128,2304]{1,0:T(8,128)(2,1)} %broadcast_select_fusion.1, bf16[128,2304]{1,0:T(8,128)(2,1)S(1)} %broadcast_select_fusion.3, bf16[128,2304]{1,0:T(8,128)(2,1)} %broadcast_select_fusion.5, bf16[128,2304]{1,0:T(8,128)(2,1)S(1)} %multiply_convert_fusion.2), kind=kOutput, calls=%fused_computation.163 | convolution fusion | flops 10881073152 | bytes 33030144 | tf_op jit(solution)/shard_map/dot_general | solution.py:31
  218.7 25.7 %all-gather.8.cloned.1.call-done = bf16[2304,2304]{1,0:T(8,128)(2,1)} async-done(((bf16[288,2304]{1,0:T(8,128)(2,1)}), bf16[2304,2304]{1,0:T(8,128)(2,1)}) %all-gather.8.cloned.1.call-update) | async-done | bytes 10616848 | tf_op jit(solution)/shard_map/all_gather | solution.py:122
  244.4 10.3 %convolution_convert_fusion.6 = bf16[512,2304]{1,0:T(8,128)(2,1)S(1)} fusion(bf16[512,2304]{1,0:T(8,128)(2,1)} %multiply_convert_fusion.1, bf16[2304,2304]{1,0:T(8,128)(2,1)} %all-gather.8.cloned.1.call-done), kind=kOutput, calls=%fused_computation.24 | convolution fusion | flops 5436997632 | bytes 15335424 | tf_op jit(solution)/shard_map/dot_general | solution.py:39
  258.9 12.2 %collective-permute-done.13 = bf16[128,2304]{1,0:T(8,128)(2,1)S(1)} collective-permute-done((bf16[128,2304]{1,0:T(8,128)(2,1)S(1)}, bf16[128,2304]{1,0:T(8,128)(2,1)S(1)}, u32[]{:S(2)}, u32[]{:S(2)}) %collective-permute-start.13) | collective-permute-done | bytes 589856 | tf_op jit(solution)/shard_map/ppermute | solution.py:43
  276.7 11.4 %collective-permute-done.15 = bf16[128,2304]{1,0:T(8,128)(2,1)S(1)} collective-permute-done((bf16[128,2304]{1,0:T(8,128)(2,1)S(1)}, bf16[128,2304]{1,0:T(8,128)(2,1)S(1)}, u32[]{:S(2)}, u32[]{:S(2)}) %collective-permute-start.15) | collective-permute-done | bytes 589856 | tf_op jit(solution)/shard_map/ppermute | solution.py:43
  288.4 8.2 collective-permute-start.17
  297.9 9.7 %collective-permute-done.17 = bf16[128,2304]{1,0:T(8,128)(2,1)S(1)} collective-permute-done((bf16[128,2304]{1,0:T(8,128)(2,1)S(1)}, bf16[128,2304]{1,0:T(8,128)(2,1)S(1)}, u32[]{:S(2)}, u32[]{:S(2)}) %collective-permute-start.17) | collective-permute-done | bytes 589856 | tf_op jit(solution)/shard_map/ppermute | solution.py:43
  318.2 8.8 %collective-permute-done.19 = bf16[128,2304]{1,0:T(8,128)(2,1)S(1)} collective-permute-done((bf16[128,2304]{1,0:T(8,128)(2,1)S(1)}, bf16[128,2304]{1,0:T(8,128)(2,1)S(1)}, u32[]{:S(2)}, u32[]{:S(2)}) %collective-permute-start.19) | collective-permute-done | bytes 589856 | tf_op jit(solution)/shard_map/ppermute | solution.py:43
  333.2 12.4 %collective-permute-done.22 = bf16[128,2304]{1,0:T(8,128)(2,1)S(1)} collective-permute-done((bf16[128,2304]{1,0:T(8,128)(2,1)S(1)}, bf16[128,2304]{1,0:T(8,128)(2,1)S(1)}, u32[]{:S(2)}, u32[]{:S(2)}) %collective-permute-start.22) | collective-permute-done | bytes 589856 | tf_op jit(solution)/shard_map/ppermute | solution.py:43
  348.0 11.0 %collective-permute-done.24 = bf16[128,2304]{1,0:T(8,128)(2,1)S(1)} collective-permute-done((bf16[128,2304]{1,0:T(8,128)(2,1)S(1)}, bf16[128,2304]{1,0:T(8,128)(2,1)S(1)}, u32[]{:S(2)}, u32[]{:S(2)}) %collective-permute-start.24) | collective-permute-done | bytes 589856 | tf_op jit(solution)/shard_map/ppermute | solution.py:43
  361.7 8.2 convolution_convert_fusion.1
  369.9 14.3 %fusion.9 = (bf16[512,2304]{1,0:T(8,128)(2,1)S(1)}, bf16[512,2304]{1,0:T(8,128)(2,1)S(1)}) fusion(f32[512,4608]{1,0:T(8,128)} %copy-done, bf16[512,2304]{1,0:T(8,128)(2,1)} %pad_maximum_fusion.6, bf16[2304,2304]{1,0:T(8,128)(2,1)} %all-gather.8.cloned.1.call-done), kind=kOutput, calls=%fused_computation.17 | convolution fusion | flops 5464129536 | bytes 27131904 | tf_op jit(solution)/shard_map/dot_general | solution.py:31
  385.7 14.8 %convolution_convert_fusion.5 = bf16[512,2304]{1,0:T(8,128)(2,1)S(1)} fusion(bf16[2304,4608]{1,0:T(8,128)(2,1)} %all-gather.6.cloned.1.call-done, bf16[512,2304]{1,0:T(8,128)(2,1)S(1)} %get-tuple-element.155, bf16[512,2304]{1,0:T(8,128)(2,1)S(1)} %get-tuple-element.154), kind=kOutput, calls=%fused_computation.23 | convolution fusion | flops 10882252800 | bytes 28311552 | tf_op jit(solution)/shard_map/dot_general | solution.py:39
  402.8 8.1 collective-permute-done.25
  416.3 6.6 collective-permute-done.27
  424.2 6.4 collective-permute-start.29
  432.1 18.2 %convolution_convert_fusion = bf16[2304,4608]{1,0:T(8,128)(2,1)} fusion(bf16[512,2304]{1,0:T(8,128)(2,1)} %copy-done.49, bf16[512,2304]{1,0:T(8,128)(2,1)} %copy-done.48, bf16[128,2304]{1,0:T(8,128)(2,1)} %broadcast_select_fusion.1, bf16[128,2304]{1,0:T(8,128)(2,1)} %copy-done.23, bf16[128,2304]{1,0:T(8,128)(2,1)} %broadcast_select_fusion.5, ...), kind=kOutput, calls=%fused_computation | convolution fusion | flops 10901127168 | bytes 28311552 | tf_op jit(solution)/shard_map/dot_general | solution.py:35
  456.9 4.6 collective-permute-start.31
  462.8 6.0 collective-permute-done.31
  468.9 9.3 %collective-permute-done.32 = bf16[128,2304]{1,0:T(8,128)(2,1)S(1)} collective-permute-done((bf16[128,2304]{1,0:T(8,128)(2,1)S(1)}, bf16[128,2304]{1,0:T(8,128)(2,1)S(1)}, u32[]{:S(2)}, u32[]{:S(2)}) %collective-permute-start.32) | collective-permute-done | bytes 589856 | tf_op jit(solution)/shard_map/ppermute | solution.py:43
  480.1 16.4 %collective-permute-done.34 = bf16[128,2304]{1,0:T(8,128)(2,1)S(1)} collective-permute-done((bf16[128,2304]{1,0:T(8,128)(2,1)S(1)}, bf16[128,2304]{1,0:T(8,128)(2,1)S(1)}, u32[]{:S(2)}, u32[]{:S(2)}) %collective-permute-start.34) | collective-permute-done | bytes 589856 | tf_op jit(solution)/shard_map/ppermute | solution.py:43
  499.0 10.0 %collective-permute-done.36 = bf16[128,2304]{1,0:T(8,128)(2,1)S(1)} collective-permute-done((bf16[128,2304]{1,0:T(8,128)(2,1)S(1)}, bf16[128,2304]{1,0:T(8,128)(2,1)S(1)}, u32[]{:S(2)}, u32[]{:S(2)}) %collective-permute-start.36) | collective-permute-done | bytes 589856 | tf_op jit(solution)/shard_map/ppermute | solution.py:43
  524.2 6.1 collective-permute-done.43
  531.4 4.7 convolution_convert_fusion.2
  536.1 6.5 pad_maximum_fusion
  547.6 6.3 convolution_convert_fusion.4
  554.0 4.6 collective-permute-start.44
  577.2 5.0 collective-permute-done.40
  588.4 4.7 collective-permute-start.48
  600.8 5.9 collective-permute-done.49
  624.8 4.9 collective-permute-done.51
  633.8 11.5 %collective-permute-done.53 = bf16[128,2304]{1,0:T(8,128)(2,1)S(1)} collective-permute-done((bf16[128,2304]{1,0:T(8,128)(2,1)S(1)}, bf16[128,2304]{1,0:T(8,128)(2,1)S(1)}, u32[]{:S(2)}, u32[]{:S(2)}) %collective-permute-start.53) | collective-permute-done | bytes 589856 | tf_op jit(solution)/shard_map/ppermute | solution.py:43
  650.0 7.7 collective-permute-done.55
  664.7 26.2 %reduce-scatter.8.cloned.1.call-done = bf16[288,2304]{1,0:T(8,128)(2,1)} async-done(((bf16[2304,2304]{1,0:T(8,128)(2,1)}), bf16[288,2304]{1,0:T(8,128)(2,1)}) %reduce-scatter.8.cloned.1.call-update) | async-done | bytes 1327120 | tf_op jit(solution)/shard_map/reduce_scatter | solution.py:126
  693.9 138.1 %reduce-scatter.6.cloned.1.call-done = bf16[288,4608]{1,0:T(8,128)(2,1)} async-done(((bf16[2304,4608]{1,0:T(8,128)(2,1)}), bf16[288,4608]{1,0:T(8,128)(2,1)}) %reduce-scatter.6.cloned.1.call-update) | async-done | bytes 2654224 | tf_op jit(solution)/shard_map/reduce_scatter | solution.py:126
  (294 shorter events, 203.5 us)
Async XLA Ops:
  7.2 54.7 %all-gather.4.cloned.1.call-start = ((), (), s32[]{:S(2)}) async-start(), calls=%async_computation.3 | async-start | bytes 7962624 | tf_op jit(solution)/shard_map/all_gather | solution.py:122
  9.6 188.0 %all-gather.6.cloned.1.call-start = ((), (), s32[]{:S(2)}) async-start(), calls=%async_computation.4 | async-start | bytes 23887872 | tf_op jit(solution)/shard_map/all_gather | solution.py:122
  11.4 233.0 %all-gather.8.cloned.1.call-start = ((), (), s32[]{:S(2)}) async-start(), calls=%async_computation.5 | async-start | bytes 11943936 | tf_op jit(solution)/shard_map/all_gather | solution.py:122
  12.1 648.5 %reduce-scatter.4.cloned.1.call-start = ((), (), s32[]{:S(2)}) async-start(), calls=%async_computation.6 | async-start | bytes 7962624 | tf_op jit(solution)/shard_map/reduce_scatter | solution.py:126
  67.0 23.0 %collective-permute-start = (bf16[512,512]{1,0:T(8,128)(2,1)S(1)}, bf16[512,512]{1,0:T(8,128)(2,1)S(1)}, u32[]{:S(2)}, u32[]{:S(2)}) collective-permute-start(bf16[512,512]{1,0:T(8,128)(2,1)S(1)} %get-tuple-element.182), channel_id=1, source_target_pairs={{0,4},{1,5},{2,6},{3,7},{8,12},{9,13},{10,14},{11,15},{16,20},{17,... | collective-permute-start | bytes 1572872 | tf_op jit(solution)/shard_map/ppermute | solution.py:19
  97.1 13.8 %collective-permute-start.1 = (bf16[128,2304]{1,0:T(8,128)(2,1)S(1)}, bf16[128,2304]{1,0:T(8,128)(2,1)}, u32[]{:S(2)}, u32[]{:S(2)}) collective-permute-start(bf16[128,2304]{1,0:T(8,128)(2,1)S(1)} %get-tuple-element.73), channel_id=1, source_target_pairs={{0,1},{4,5},{8,9},{12,13},{16,17},{20,21},{24,25},{28,29}} | collective-permute-start | bytes 1769480 | tf_op jit(solution)/shard_map/ppermute | solution.py:43
  113.1 14.9 %collective-permute-start.3 = (bf16[128,2304]{1,0:T(8,128)(2,1)S(1)}, bf16[128,2304]{1,0:T(8,128)(2,1)S(1)}, u32[]{:S(2)}, u32[]{:S(2)}) collective-permute-start(bf16[128,2304]{1,0:T(8,128)(2,1)S(1)} %get-tuple-element.75), channel_id=1, source_target_pairs={{0,1},{1,2},{4,5},{5,6},{8,9},{9,10},{12,13},{13,14},{16,17},{17,1... | collective-permute-start | bytes 1769480 | tf_op jit(solution)/shard_map/ppermute | solution.py:43
  128.2 14.5 %collective-permute-start.5 = (bf16[128,2304]{1,0:T(8,128)(2,1)S(1)}, bf16[128,2304]{1,0:T(8,128)(2,1)S(1)}, u32[]{:S(2)}, u32[]{:S(2)}) collective-permute-start(bf16[128,2304]{1,0:T(8,128)(2,1)S(1)} %add_convert_fusion.8), channel_id=1, source_target_pairs={{0,1},{1,2},{2,3},{4,5},{5,6},{6,7},{8,9},{9,10},{10,11},{12,13},{... | collective-permute-start | bytes 1769480 | tf_op jit(solution)/shard_map/ppermute | solution.py:43
  133.8 13.9 %collective-permute-start.6 = (bf16[128,2304]{1,0:T(8,128)(2,1)S(1)}, bf16[128,2304]{1,0:T(8,128)(2,1)S(1)}, u32[]{:S(2)}, u32[]{:S(2)}) collective-permute-start(bf16[128,2304]{1,0:T(8,128)(2,1)S(1)} %add_convert_fusion.7), channel_id=1, source_target_pairs={{1,0},{2,1},{3,2},{5,4},{6,5},{7,6},{9,8},{10,9},{11,10},{13,12},{... | collective-permute-start | bytes 1769480 | tf_op jit(solution)/shard_map/ppermute | solution.py:43
  155.5 13.3 %collective-permute-start.8 = (bf16[128,2304]{1,0:T(8,128)(2,1)S(1)}, bf16[128,2304]{1,0:T(8,128)(2,1)}, u32[]{:S(2)}, u32[]{:S(2)}) collective-permute-start(bf16[128,2304]{1,0:T(8,128)(2,1)S(1)} %multiply_convert_fusion.2), channel_id=1, source_target_pairs={{1,0},{2,1},{3,2},{5,4},{6,5},{7,6},{9,8},{10,9},{11,10},{13,12},{... | collective-permute-start | bytes 1769480 | tf_op jit(solution)/shard_map/ppermute | solution.py:43
  168.8 13.2 %collective-permute-start.10 = (bf16[128,2304]{1,0:T(8,128)(2,1)}, bf16[128,2304]{1,0:T(8,128)(2,1)}, u32[]{:S(2)}, u32[]{:S(2)}) collective-permute-start(bf16[128,2304]{1,0:T(8,128)(2,1)} %collective-permute-done.8), channel_id=1, source_target_pairs={{1,0},{2,1},{5,4},{6,5},{9,8},{10,9},{13,12},{14,13},{17,16},{18,1... | collective-permute-start | bytes 1769480 | tf_op jit(solution)/shard_map/ppermute | solution.py:43
  170.1 12.0 %collective-permute-start.9 = (bf16[128,2304]{1,0:T(8,128)(2,1)S(1)}, bf16[128,2304]{1,0:T(8,128)(2,1)}, u32[]{:S(2)}, u32[]{:S(2)}) collective-permute-start(bf16[128,2304]{1,0:T(8,128)(2,1)S(1)} %collective-permute-done.7), channel_id=1, source_target_pairs={{1,2},{2,3},{5,6},{6,7},{9,10},{10,11},{13,14},{14,15},{17,18},{18... | collective-permute-start | bytes 1769480 | tf_op jit(solution)/shard_map/ppermute | solution.py:43
  182.7 12.0 %collective-permute-start.12 = (bf16[128,2304]{1,0:T(8,128)(2,1)}, bf16[128,2304]{1,0:T(8,128)(2,1)S(1)}, u32[]{:S(2)}, u32[]{:S(2)}) collective-permute-start(bf16[128,2304]{1,0:T(8,128)(2,1)} %collective-permute-done.10), channel_id=1, source_target_pairs={{1,0},{5,4},{9,8},{13,12},{17,16},{21,20},{25,24},{29,28}} | collective-permute-start | bytes 1769480 | tf_op jit(solution)/shard_map/ppermute | solution.py:43
  254.8 16.4 %collective-permute-start.13 = (bf16[128,2304]{1,0:T(8,128)(2,1)S(1)}, bf16[128,2304]{1,0:T(8,128)(2,1)S(1)}, u32[]{:S(2)}, u32[]{:S(2)}) collective-permute-start(bf16[128,2304]{1,0:T(8,128)(2,1)S(1)} %get-tuple-element.85), channel_id=1, source_target_pairs={{0,1},{4,5},{8,9},{12,13},{16,17},{20,21},{24,25},{28,29}} | collective-permute-start | bytes 1769480 | tf_op jit(solution)/shard_map/ppermute | solution.py:43
  258.2 12.9 %collective-permute-start.14 = (bf16[128,2304]{1,0:T(8,128)(2,1)S(1)}, bf16[128,2304]{1,0:T(8,128)(2,1)S(1)}, u32[]{:S(2)}, u32[]{:S(2)}) collective-permute-start(bf16[128,2304]{1,0:T(8,128)(2,1)S(1)} %get-tuple-element.86), channel_id=1, source_target_pairs={{3,2},{7,6},{11,10},{15,14},{19,18},{23,22},{27,26},{31,30}} | collective-permute-start | bytes 1769480 | tf_op jit(solution)/shard_map/ppermute | solution.py:43
  271.4 16.6 %collective-permute-start.15 = (bf16[128,2304]{1,0:T(8,128)(2,1)S(1)}, bf16[128,2304]{1,0:T(8,128)(2,1)S(1)}, u32[]{:S(2)}, u32[]{:S(2)}) collective-permute-start(bf16[128,2304]{1,0:T(8,128)(2,1)S(1)} %get-tuple-element.87), channel_id=1, source_target_pairs={{0,1},{1,2},{4,5},{5,6},{8,9},{9,10},{12,13},{13,14},{16,17},{17,1... | collective-permute-start | bytes 1769480 | tf_op jit(solution)/shard_map/ppermute | solution.py:43
  276.0 12.1 %collective-permute-start.16 = (bf16[128,2304]{1,0:T(8,128)(2,1)S(1)}, bf16[128,2304]{1,0:T(8,128)(2,1)S(1)}, u32[]{:S(2)}, u32[]{:S(2)}) collective-permute-start(bf16[128,2304]{1,0:T(8,128)(2,1)S(1)} %get-tuple-element.88), channel_id=1, source_target_pairs={{2,1},{3,2},{6,5},{7,6},{10,9},{11,10},{14,13},{15,14},{18,17},{19... | collective-permute-start | bytes 1769480 | tf_op jit(solution)/shard_map/ppermute | solution.py:43
  288.4 19.2 %collective-permute-start.17 = (bf16[128,2304]{1,0:T(8,128)(2,1)S(1)}, bf16[128,2304]{1,0:T(8,128)(2,1)S(1)}, u32[]{:S(2)}, u32[]{:S(2)}) collective-permute-start(bf16[128,2304]{1,0:T(8,128)(2,1)S(1)} %get-tuple-element.89), channel_id=1, source_target_pairs={{0,1},{1,2},{2,3},{4,5},{5,6},{6,7},{8,9},{9,10},{10,11},{12,13},{... | collective-permute-start | bytes 1769480 | tf_op jit(solution)/shard_map/ppermute | solution.py:43
  296.6 15.1 %collective-permute-start.18 = (bf16[128,2304]{1,0:T(8,128)(2,1)S(1)}, bf16[128,2304]{1,0:T(8,128)(2,1)S(1)}, u32[]{:S(2)}, u32[]{:S(2)}) collective-permute-start(bf16[128,2304]{1,0:T(8,128)(2,1)S(1)} %get-tuple-element.90), channel_id=1, source_target_pairs={{1,0},{2,1},{3,2},{5,4},{6,5},{7,6},{9,8},{10,9},{11,10},{13,12},{... | collective-permute-start | bytes 1769480 | tf_op jit(solution)/shard_map/ppermute | solution.py:43
  314.7 12.3 %collective-permute-start.19 = (bf16[128,2304]{1,0:T(8,128)(2,1)S(1)}, bf16[128,2304]{1,0:T(8,128)(2,1)S(1)}, u32[]{:S(2)}, u32[]{:S(2)}) collective-permute-start(bf16[128,2304]{1,0:T(8,128)(2,1)S(1)} %get-tuple-element.156), channel_id=1, source_target_pairs={{0,1},{1,2},{2,3},{4,5},{5,6},{6,7},{8,9},{9,10},{10,11},{12,13},{... | collective-permute-start | bytes 1769480 | tf_op jit(solution)/shard_map/ppermute | solution.py:43
  316.9 14.2 %collective-permute-start.20 = (bf16[128,2304]{1,0:T(8,128)(2,1)S(1)}, bf16[128,2304]{1,0:T(8,128)(2,1)S(1)}, u32[]{:S(2)}, u32[]{:S(2)}) collective-permute-start(bf16[128,2304]{1,0:T(8,128)(2,1)S(1)} %get-tuple-element.156), channel_id=1, source_target_pairs={{1,0},{2,1},{3,2},{5,4},{6,5},{7,6},{9,8},{10,9},{11,10},{13,12},{... | collective-permute-start | bytes 1769480 | tf_op jit(solution)/shard_map/ppermute | solution.py:43
  331.9 13.7 %collective-permute-start.22 = (bf16[128,2304]{1,0:T(8,128)(2,1)S(1)}, bf16[128,2304]{1,0:T(8,128)(2,1)S(1)}, u32[]{:S(2)}, u32[]{:S(2)}) collective-permute-start(bf16[128,2304]{1,0:T(8,128)(2,1)S(1)} %collective-permute-done.20), channel_id=1, source_target_pairs={{1,0},{2,1},{5,4},{6,5},{9,8},{10,9},{13,12},{14,13},{17,16},{18,1... | collective-permute-start | bytes 1769480 | tf_op jit(solution)/shard_map/ppermute | solution.py:43
  346.2 12.8 %collective-permute-start.24 = (bf16[128,2304]{1,0:T(8,128)(2,1)S(1)}, bf16[128,2304]{1,0:T(8,128)(2,1)S(1)}, u32[]{:S(2)}, u32[]{:S(2)}) collective-permute-start(bf16[128,2304]{1,0:T(8,128)(2,1)S(1)} %collective-permute-done.22), channel_id=1, source_target_pairs={{1,0},{5,4},{9,8},{13,12},{17,16},{21,20},{25,24},{29,28}} | collective-permute-start | bytes 1769480 | tf_op jit(solution)/shard_map/ppermute | solution.py:43
  411.1 11.8 %collective-permute-start.27 = (bf16[128,2304]{1,0:T(8,128)(2,1)S(1)}, bf16[128,2304]{1,0:T(8,128)(2,1)S(1)}, u32[]{:S(2)}, u32[]{:S(2)}) collective-permute-start(bf16[128,2304]{1,0:T(8,128)(2,1)S(1)} %get-tuple-element.100), channel_id=1, source_target_pairs={{0,1},{1,2},{4,5},{5,6},{8,9},{9,10},{12,13},{13,14},{16,17},{17,1... | collective-permute-start | bytes 1769480 | tf_op jit(solution)/shard_map/ppermute | solution.py:43
  424.2 26.0 %collective-permute-start.29 = (bf16[128,2304]{1,0:T(8,128)(2,1)}, bf16[128,2304]{1,0:T(8,128)(2,1)S(1)}, u32[]{:S(2)}, u32[]{:S(2)}) collective-permute-start(bf16[128,2304]{1,0:T(8,128)(2,1)} %get-tuple-element.102), channel_id=1, source_target_pairs={{0,1},{1,2},{2,3},{4,5},{5,6},{6,7},{8,9},{9,10},{10,11},{12,13},{... | collective-permute-start | bytes 1769480 | tf_op jit(solution)/shard_map/ppermute | solution.py:43
  430.6 19.7 %collective-permute-start.30 = (bf16[128,2304]{1,0:T(8,128)(2,1)}, bf16[128,2304]{1,0:T(8,128)(2,1)S(1)}, u32[]{:S(2)}, u32[]{:S(2)}) collective-permute-start(bf16[128,2304]{1,0:T(8,128)(2,1)} %get-tuple-element.103), channel_id=1, source_target_pairs={{1,0},{2,1},{3,2},{5,4},{6,5},{7,6},{9,8},{10,9},{11,10},{13,12},{... | collective-permute-start | bytes 1769480 | tf_op jit(solution)/shard_map/ppermute | solution.py:43
  456.9 11.9 %collective-permute-start.31 = (bf16[128,2304]{1,0:T(8,128)(2,1)S(1)}, bf16[128,2304]{1,0:T(8,128)(2,1)S(1)}, u32[]{:S(2)}, u32[]{:S(2)}) collective-permute-start(bf16[128,2304]{1,0:T(8,128)(2,1)S(1)} %fusion.57), channel_id=1, source_target_pairs={{0,1},{1,2},{2,3},{4,5},{5,6},{6,7},{8,9},{9,10},{10,11},{12,13},{... | collective-permute-start | bytes 1769480 | tf_op jit(solution)/shard_map/ppermute | solution.py:43
  461.5 16.6 %collective-permute-start.32 = (bf16[128,2304]{1,0:T(8,128)(2,1)S(1)}, bf16[128,2304]{1,0:T(8,128)(2,1)S(1)}, u32[]{:S(2)}, u32[]{:S(2)}) collective-permute-start(bf16[128,2304]{1,0:T(8,128)(2,1)S(1)} %fusion.57), channel_id=1, source_target_pairs={{1,0},{2,1},{3,2},{5,4},{6,5},{7,6},{9,8},{10,9},{11,10},{13,12},{... | collective-permute-start | bytes 1769480 | tf_op jit(solution)/shard_map/ppermute | solution.py:43
  478.8 17.7 %collective-permute-start.34 = (bf16[128,2304]{1,0:T(8,128)(2,1)S(1)}, bf16[128,2304]{1,0:T(8,128)(2,1)S(1)}, u32[]{:S(2)}, u32[]{:S(2)}) collective-permute-start(bf16[128,2304]{1,0:T(8,128)(2,1)S(1)} %collective-permute-done.32), channel_id=1, source_target_pairs={{1,0},{2,1},{5,4},{6,5},{9,8},{10,9},{13,12},{14,13},{17,16},{18,1... | collective-permute-start | bytes 1769480 | tf_op jit(solution)/shard_map/ppermute | solution.py:43
  497.2 11.8 %collective-permute-start.36 = (bf16[128,2304]{1,0:T(8,128)(2,1)S(1)}, bf16[128,2304]{1,0:T(8,128)(2,1)S(1)}, u32[]{:S(2)}, u32[]{:S(2)}) collective-permute-start(bf16[128,2304]{1,0:T(8,128)(2,1)S(1)} %collective-permute-done.34), channel_id=1, source_target_pairs={{1,0},{5,4},{9,8},{13,12},{17,16},{21,20},{25,24},{29,28}} | collective-permute-start | bytes 1769480 | tf_op jit(solution)/shard_map/ppermute | solution.py:43
  542.6 148.3 %reduce-scatter.8.cloned.1.call-start = ((), (), s32[]{:S(2)}) async-start(), calls=%async_computation.8 | async-start | bytes 11943936 | tf_op jit(solution)/shard_map/reduce_scatter | solution.py:126
  543.2 288.8 %reduce-scatter.6.cloned.1.call-start = ((), (), s32[]{:S(2)}) async-start(), calls=%async_computation.7 | async-start | bytes 23887872 | tf_op jit(solution)/shard_map/reduce_scatter | solution.py:126
  543.8 15.5 %collective-permute-start.37 = (bf16[128,2304]{1,0:T(8,128)(2,1)}, bf16[128,2304]{1,0:T(8,128)(2,1)}, u32[]{:S(2)}, u32[]{:S(2)}) collective-permute-start(bf16[128,2304]{1,0:T(8,128)(2,1)} %get-tuple-element.111), channel_id=1, source_target_pairs={{0,1},{1,2},{2,3},{4,5},{5,6},{6,7},{8,9},{9,10},{10,11},{12,13},{... | collective-permute-start | bytes 1769480 | tf_op jit(solution)/shard_map/ppermute | solution.py:43
  546.1 17.3 %collective-permute-start.38 = (bf16[128,2304]{1,0:T(8,128)(2,1)}, bf16[128,2304]{1,0:T(8,128)(2,1)}, u32[]{:S(2)}, u32[]{:S(2)}) collective-permute-start(bf16[128,2304]{1,0:T(8,128)(2,1)} %get-tuple-element.111), channel_id=1, source_target_pairs={{1,0},{2,1},{3,2},{5,4},{6,5},{7,6},{9,8},{10,9},{11,10},{13,12},{... | collective-permute-start | bytes 1769480 | tf_op jit(solution)/shard_map/ppermute | solution.py:43
  554.0 14.0 %collective-permute-start.44 = (bf16[128,2304]{1,0:T(8,128)(2,1)S(1)}, bf16[128,2304]{1,0:T(8,128)(2,1)S(1)}, u32[]{:S(2)}, u32[]{:S(2)}) collective-permute-start(bf16[128,2304]{1,0:T(8,128)(2,1)S(1)} %get-tuple-element.119), channel_id=1, source_target_pairs={{0,1},{4,5},{8,9},{12,13},{16,17},{20,21},{24,25},{28,29}} | collective-permute-start | bytes 1769480 | tf_op jit(solution)/shard_map/ppermute | solution.py:43
  563.4 13.8 %collective-permute-start.39 = (bf16[128,2304]{1,0:T(8,128)(2,1)}, bf16[128,2304]{1,0:T(8,128)(2,1)}, u32[]{:S(2)}, u32[]{:S(2)}) collective-permute-start(bf16[128,2304]{1,0:T(8,128)(2,1)} %collective-permute-done.37), channel_id=1, source_target_pairs={{1,2},{2,3},{5,6},{6,7},{9,10},{10,11},{13,14},{14,15},{17,18},{18... | collective-permute-start | bytes 1769480 | tf_op jit(solution)/shard_map/ppermute | solution.py:43
  564.9 17.3 %collective-permute-start.40 = (bf16[128,2304]{1,0:T(8,128)(2,1)}, bf16[128,2304]{1,0:T(8,128)(2,1)}, u32[]{:S(2)}, u32[]{:S(2)}) collective-permute-start(bf16[128,2304]{1,0:T(8,128)(2,1)} %collective-permute-done.38), channel_id=1, source_target_pairs={{1,0},{2,1},{5,4},{6,5},{9,8},{10,9},{13,12},{14,13},{17,16},{18,1... | collective-permute-start | bytes 1769480 | tf_op jit(solution)/shard_map/ppermute | solution.py:43
  569.3 14.9 %collective-permute-start.47 = (bf16[128,2304]{1,0:T(8,128)(2,1)}, bf16[128,2304]{1,0:T(8,128)(2,1)}, u32[]{:S(2)}, u32[]{:S(2)}) collective-permute-start(bf16[128,2304]{1,0:T(8,128)(2,1)} %get-tuple-element.122), channel_id=1, source_target_pairs={{2,1},{3,2},{6,5},{7,6},{10,9},{11,10},{14,13},{15,14},{18,17},{19... | collective-permute-start | bytes 1769480 | tf_op jit(solution)/shard_map/ppermute | solution.py:43
  572.9 14.2 %collective-permute-start.46 = (bf16[128,2304]{1,0:T(8,128)(2,1)}, bf16[128,2304]{1,0:T(8,128)(2,1)S(1)}, u32[]{:S(2)}, u32[]{:S(2)}) collective-permute-start(bf16[128,2304]{1,0:T(8,128)(2,1)} %get-tuple-element.121), channel_id=1, source_target_pairs={{0,1},{1,2},{4,5},{5,6},{8,9},{9,10},{12,13},{13,14},{16,17},{17,1... | collective-permute-start | bytes 1769480 | tf_op jit(solution)/shard_map/ppermute | solution.py:43
  582.2 14.6 %collective-permute-start.41 = (bf16[128,2304]{1,0:T(8,128)(2,1)}, bf16[128,2304]{1,0:T(8,128)(2,1)S(1)}, u32[]{:S(2)}, u32[]{:S(2)}) collective-permute-start(bf16[128,2304]{1,0:T(8,128)(2,1)} %collective-permute-done.39), channel_id=1, source_target_pairs={{2,3},{6,7},{10,11},{14,15},{18,19},{22,23},{26,27},{30,31}} | collective-permute-start | bytes 1769480 | tf_op jit(solution)/shard_map/ppermute | solution.py:43
  582.9 17.0 %collective-permute-start.42 = (bf16[128,2304]{1,0:T(8,128)(2,1)}, bf16[128,2304]{1,0:T(8,128)(2,1)S(1)}, u32[]{:S(2)}, u32[]{:S(2)}) collective-permute-start(bf16[128,2304]{1,0:T(8,128)(2,1)} %collective-permute-done.40), channel_id=1, source_target_pairs={{1,0},{5,4},{9,8},{13,12},{17,16},{21,20},{25,24},{29,28}} | collective-permute-start | bytes 1769480 | tf_op jit(solution)/shard_map/ppermute | solution.py:43
  588.4 12.4 %collective-permute-start.48 = (bf16[128,2304]{1,0:T(8,128)(2,1)S(1)}, bf16[128,2304]{1,0:T(8,128)(2,1)S(1)}, u32[]{:S(2)}, u32[]{:S(2)}) collective-permute-start(bf16[128,2304]{1,0:T(8,128)(2,1)S(1)} %add_convert_fusion.1), channel_id=1, source_target_pairs={{0,1},{1,2},{2,3},{4,5},{5,6},{6,7},{8,9},{9,10},{10,11},{12,13},{... | collective-permute-start | bytes 1769480 | tf_op jit(solution)/shard_map/ppermute | solution.py:43
  593.1 13.5 %collective-permute-start.49 = (bf16[128,2304]{1,0:T(8,128)(2,1)S(1)}, bf16[128,2304]{1,0:T(8,128)(2,1)S(1)}, u32[]{:S(2)}, u32[]{:S(2)}) collective-permute-start(bf16[128,2304]{1,0:T(8,128)(2,1)S(1)} %add_convert_fusion), channel_id=1, source_target_pairs={{1,0},{2,1},{3,2},{5,4},{6,5},{7,6},{9,8},{10,9},{11,10},{13,12},{... | collective-permute-start | bytes 1769480 | tf_op jit(solution)/shard_map/ppermute | solution.py:43
  617.4 12.2 %collective-permute-start.51 = (bf16[128,2304]{1,0:T(8,128)(2,1)S(1)}, bf16[128,2304]{1,0:T(8,128)(2,1)S(1)}, u32[]{:S(2)}, u32[]{:S(2)}) collective-permute-start(bf16[128,2304]{1,0:T(8,128)(2,1)S(1)} %get-tuple-element.146), channel_id=1, source_target_pairs={{1,0},{2,1},{3,2},{5,4},{6,5},{7,6},{9,8},{10,9},{11,10},{13,12},{... | collective-permute-start | bytes 1769480 | tf_op jit(solution)/shard_map/ppermute | solution.py:43
  620.2 13.5 %collective-permute-start.59 = (f32[4,2304]{1,0:T(4,128)S(1)}, f32[4,2304]{1,0:T(4,128)S(1)}, u32[]{:S(2)}, u32[]{:S(2)}) collective-permute-start(f32[4,2304]{1,0:T(4,128)S(1)} %add.305), channel_id=1, source_target_pairs={{0,16},{8,24},{16,0},{24,8},{1,17},{9,25},{17,1},{25,9},{2,18},{10... | collective-permute-start | bytes 110600 | tf_op jit(solution)/shard_map/ppermute | solution.py:103
  630.4 14.9 %collective-permute-start.53 = (bf16[128,2304]{1,0:T(8,128)(2,1)S(1)}, bf16[128,2304]{1,0:T(8,128)(2,1)S(1)}, u32[]{:S(2)}, u32[]{:S(2)}) collective-permute-start(bf16[128,2304]{1,0:T(8,128)(2,1)S(1)} %collective-permute-done.51), channel_id=1, source_target_pairs={{1,0},{2,1},{5,4},{6,5},{9,8},{10,9},{13,12},{14,13},{17,16},{18,1... | collective-permute-start | bytes 1769480 | tf_op jit(solution)/shard_map/ppermute | solution.py:43
  633.7 15.6 %collective-permute-start.60 = (f32[4,2304]{1,0:T(4,128)S(1)}, f32[4,2304]{1,0:T(4,128)S(1)}, u32[]{:S(2)}, u32[]{:S(2)}) collective-permute-start(f32[4,2304]{1,0:T(4,128)S(1)} %add.306), channel_id=1, source_target_pairs={{0,4},{4,0},{1,5},{5,1},{2,6},{6,2},{3,7},{7,3},{8,12},{12,8},{9,1... | collective-permute-start | bytes 110600 | tf_op jit(solution)/shard_map/ppermute | solution.py:103
  646.0 11.8 %collective-permute-start.55 = (bf16[128,2304]{1,0:T(8,128)(2,1)S(1)}, bf16[128,2304]{1,0:T(8,128)(2,1)S(1)}, u32[]{:S(2)}, u32[]{:S(2)}) collective-permute-start(bf16[128,2304]{1,0:T(8,128)(2,1)S(1)} %collective-permute-done.53), channel_id=1, source_target_pairs={{1,0},{5,4},{9,8},{13,12},{17,16},{21,20},{25,24},{29,28}} | collective-permute-start | bytes 1769480 | tf_op jit(solution)/shard_map/ppermute | solution.py:43
  (69 other events, 747.7 us)
Sparse Core Ops, SparseCore 0:
  10.5 51.4 all-gather.3
  64.4 114.3 all-gather.5
  180.7 63.6 all-gather.7
  542.7 62.1 reduce-scatter.3
  608.2 82.6 reduce-scatter.7
  694.4 137.5 reduce-scatter.5

commit v4 on v3

--- a/solution.py
+++ b/solution.py
@@ -122,8 +122,33 @@
     return lax.all_gather(weight, ROWS, axis=0, tiled=True)
 
 
+def rows_of_core(left, core):
+    pairs = lax.axis_size("fsdp") // 2
+    split = left.reshape(left.shape[0], pairs, 2, -1)
+    return lax.dynamic_index_in_dim(split, core, 2, False).reshape(left.shape[0], -1)
+
+
+def sent_to_core(left, right):
+    other = 1 - lax.axis_index("fsdp") % 2
+    return rows_product(rows_of_core(left, other), right).astype(LOW)
+
+
+def over_cores(block):
+    return lax.ppermute(block, "fsdp", [(i, i ^ 1) for i in range(lax.axis_size("fsdp"))])
+
+
+def chip_rows(left, right, arrived):
+    own = rows_product(rows_of_core(left, lax.axis_index("fsdp") % 2), right)
+    return (own + arrived.astype(F32)).astype(LOW)
+
+
 def share_rows(grad):
-    return lax.psum_scatter(grad, ROWS, scatter_dimension=0, tiled=True)
+    width = lax.axis_size("ctx")
+    ranks = range(lax.axis_size("fsdp") * width)
+    groups = [[r for r in ranks if r // width % 2 == core] for core in range(2)]
+    return lax.psum_scatter(
+        grad, ROWS, scatter_dimension=0, tiled=True, axis_index_groups=groups
+    )
 
 
 def shards(
@@ -211,17 +236,21 @@
     grad_branch_two, grad_gain_four = pull_four(upstream)
     grad_two_low = jnp.concatenate(gathered(grad_branch_two.astype(LOW)), axis=0)
 
-    grad_down_low, grad_two_low = lax.optimization_barrier(
-        (rows_product(grad_two_low, hidden_low).astype(LOW), grad_two_low)
-    )
-    down_share = share_rows(grad_down_low)
+    down_sent, grad_two_low = lax.optimization_barrier(
+        (sent_to_core(grad_two_low, hidden_low), grad_two_low)
+    )
+    down_arrived = over_cores(down_sent)
     _, pull_glu = jax.vjp(geglu, gate_value, up_value)
     grad_gate, grad_up = pull_glu(product(grad_two_low, down_full))
     grad_gate_up = jnp.concatenate([grad_gate.astype(LOW), grad_up.astype(LOW)], axis=1)
-    grad_normed_two = scattered(
-        turned_blocks(transposed_product(grad_gate_up, gate_up_full).astype(LOW))
-    )
-    grad_gate_up_low = rows_product(normed_two, grad_gate_up).astype(LOW)
+    grad_down_low, grad_gate_up = lax.optimization_barrier(
+        (chip_rows(grad_two_low, hidden_low, down_arrived), grad_gate_up)
+    )
+    down_share = share_rows(grad_down_low)
+    grad_normed_two = transposed_product(grad_gate_up, gate_up_full).astype(LOW)
+    grad_normed_two = scattered(turned_blocks(grad_normed_two))
+    gate_up_arrived = over_cores(sent_to_core(normed_two, grad_gate_up))
+    grad_gate_up_low = chip_rows(normed_two, grad_gate_up, gate_up_arrived)
 
     _, pull_three = jax.vjp(rms, middle, pre_feedforward_gain)
     grad_middle_norm, grad_gain_three = pull_three(grad_normed_two)
@@ -236,7 +265,8 @@
     result_low, grad_one_low = lax.optimization_barrier((result.astype(LOW), grad_one_low))
     outputs = in_order(gathered(result_low))
 
-    grad_output_full = rows_product(grad_one_low, attended_low)
+    output_arrived = over_cores(sent_to_core(grad_one_low, attended_low))
+    output_share = share_rows(chip_rows(grad_one_low, attended_low, output_arrived))
     grad_attended = (
         product(grad_one_low, output_full).astype(LOW).reshape(length, kv_heads, repeats, HD)
     )
@@ -269,7 +299,8 @@
     grad_normed_one = scattered(
         ordered_blocks(transposed_product(grad_qkv, qkv_full).astype(LOW))
     )
-    grad_qkv_full = rows_product(normed_one, grad_qkv)
+    qkv_arrived = over_cores(sent_to_core(normed_one, grad_qkv))
+    qkv_share = share_rows(by_rows(chip_rows(normed_one, grad_qkv, qkv_arrived))).astype(F32)
 
     _, pull_one = jax.vjp(rms, inputs, pre_attention_gain)
     grad_inputs_norm, grad_gain_one = pull_one(grad_normed_one)
@@ -281,18 +312,14 @@
     share = attention_full.shape[0] // (lax.axis_size("fsdp") * lax.axis_size("ctx"))
     row_rank = lax.axis_index("fsdp") * lax.axis_size("ctx") + lax.axis_index("ctx")
     gain_shares = lax.dynamic_slice_in_dim(gains, row_rank * share, share, axis=1)
-    attention_share = share_rows(
-        by_rows(jnp.concatenate([grad_qkv_full.astype(LOW), grad_output_full.astype(LOW)], axis=1))
-    ).astype(F32)
-
-    edges = [0, heads_width, heads_width + kv_width, qkv_width, qkv_width + heads_width]
-    attention_shares = [attention_share[:, a:b] for a, b in zip(edges[:-1], edges[1:])]
+    edges = [0, heads_width, heads_width + kv_width, qkv_width]
+    qkv_shares = [qkv_share[:, a:b] for a, b in zip(edges[:-1], edges[1:])]
     gate_up_share = gate_up_share.astype(F32)
     return (
         (outputs, grad_inputs)
         + tuple(gain_shares[i] for i in range(4))
-        + tuple(attention_shares)
-        + (gate_up_share[:, :units], gate_up_share[:, units:], down_share.astype(F32))
+        + tuple(qkv_shares)
+        + (output_share.astype(F32), gate_up_share[:, :units], gate_up_share[:, units:], down_share.astype(F32))
     )
 
 

time: 854 us -> 777 us (0.910)
  waiting for transfers between devices: 511 us -> 407 us
  local copies, waits for them, and re-layouts: 24.7 us -> 43.5 us
  matrix products: 114 us -> 125 us
    reduce_scatter x3 -> x4, waiting for transfers between devices: 164 us -> 35.6 us  [share_rows(): lax.psum_scatter(grad, ROWS, scatter_dimension=0, tiled=True, axis_index_...]
    ppermute x54, waiting for transfers between devices: 243 us -> 270 us  [onward(): return lax.ppermute(block, 'tp', [(i, i + distance) for i in senders])]
    dot_general x4 -> x8, matrix products: 34 us -> 42.9 us  [rows_product(): lax.dot_general(left, right, (((0,), (0,)), ((), ())), preferred_element_...]
  transfers between devices with their start and end apart: 67 -> 72, of which waited for: 41 -> 42; matrix products, arithmetic and copies ran while one was open for 12% -> 22% of each run, Pallas kernels for 0% -> 0%
where the time goes in v4:
time: 777 us; the launch traced here: 767 us
  waiting for transfers between devices  407 us (52%)
  matrix products  125 us (16%)
  starting transfers between devices  120 us (15%)
  other arithmetic  54.2 us (7%)
  local copies, waits for them, and re-layouts  43.5 us (6%)
  between operations  16.1 us (2%)
    ppermute x54, waiting for transfers between devices, onward(): return lax.ppermute(block, 'tp', [(i, i + distance) for i in senders])  270 us
    ppermute x54, starting transfers between devices, onward(): return lax.ppermute(block, 'tp', [(i, i + distance) for i in senders])  110 us
    all_gather x3, waiting for transfers between devices, gather_rows(): return lax.all_gather(weight, ROWS, axis=0, tiled=True)  68.3 us
    dot_general x8, matrix products, rows_product(): lax.dot_general(left, right, (((0,), (0,)), ((), ())), preferred_element_...  42.9 us
    dot_general x4, matrix products, product(): return jnp.dot(left, right, preferred_element_type=F32)  40.3 us
    reduce_scatter x4, waiting for transfers between devices, share_rows(): lax.psum_scatter(grad, ROWS, scatter_dimension=0, tiled=True, axis_index_...  35.6 us
    dot_general x4, matrix products, transposed_product(): lax.dot_general(left, right, (((1,), (1,)), ((), ())), preferred_element_...  33.8 us
    ppermute x2, waiting for transfers between devices, passed_along(): return lax.ppermute(block, axis, route)  25.7 us
  transfers between devices with their start and end apart: 72, of which 42 were waited for; matrix products, arithmetic and copies ran while one was open for 22% of the time, Pallas kernels for 0%

profile of v4, /device:TPU:0, one launch (start us, length us, event | category | flops | bytes accessed | tf_op | source)
XLA Modules:
  0.0 766.5 jit_solution(12974406626766039471)
XLA Ops:
  17.7 44.2 %all-gather.4.cloned.1.call-done = bf16[2304,1536]{1,0:T(8,128)(2,1)} async-done(((bf16[288,1536]{1,0:T(8,128)(2,1)}), bf16[2304,1536]{1,0:T(8,128)(2,1)}) %all-gather.4.cloned.1.call-update) | async-done | bytes 7077904 | tf_op jit(solution)/shard_map/all_gather | solution.py:122
  61.9 5.7 fusion.29
  72.6 18.8 %collective-permute-done = bf16[512,512]{1,0:T(8,128)(2,1)S(1)} collective-permute-done((bf16[512,512]{1,0:T(8,128)(2,1)S(1)}, bf16[512,512]{1,0:T(8,128)(2,1)S(1)}, u32[]{:S(2)}, u32[]{:S(2)}) %collective-permute-start) | collective-permute-done | bytes 524320 | tf_op jit(solution)/shard_map/ppermute | solution.py:19
  103.9 8.4 %collective-permute-done.1 = bf16[128,2304]{1,0:T(8,128)(2,1)} collective-permute-done((bf16[128,2304]{1,0:T(8,128)(2,1)S(1)}, bf16[128,2304]{1,0:T(8,128)(2,1)}, u32[]{:S(2)}, u32[]{:S(2)}) %collective-permute-start.1) | collective-permute-done | bytes 589856 | tf_op jit(solution)/shard_map/ppermute | solution.py:43
  114.4 5.1 collective-permute-start.3
  120.5 8.8 %collective-permute-done.3 = bf16[128,2304]{1,0:T(8,128)(2,1)S(1)} collective-permute-done((bf16[128,2304]{1,0:T(8,128)(2,1)S(1)}, bf16[128,2304]{1,0:T(8,128)(2,1)S(1)}, u32[]{:S(2)}, u32[]{:S(2)}) %collective-permute-start.3) | collective-permute-done | bytes 589856 | tf_op jit(solution)/shard_map/ppermute | solution.py:43
  129.5 5.5 collective-permute-start.5
  136.4 7.8 %collective-permute-done.5 = bf16[128,2304]{1,0:T(8,128)(2,1)S(1)} collective-permute-done((bf16[128,2304]{1,0:T(8,128)(2,1)S(1)}, bf16[128,2304]{1,0:T(8,128)(2,1)S(1)}, u32[]{:S(2)}, u32[]{:S(2)}) %collective-permute-start.5) | collective-permute-done | bytes 589856 | tf_op jit(solution)/shard_map/ppermute | solution.py:43
  144.1 5.1 collective-permute-done.6
  159.6 6.1 collective-permute-done.7
  165.8 6.0 collective-permute-done.8
  174.5 10.3 %collective-permute-done.10 = bf16[128,2304]{1,0:T(8,128)(2,1)S(1)} collective-permute-done((bf16[128,2304]{1,0:T(8,128)(2,1)S(1)}, bf16[128,2304]{1,0:T(8,128)(2,1)S(1)}, u32[]{:S(2)}, u32[]{:S(2)}) %collective-permute-start.10) | collective-permute-done | bytes 589856 | tf_op jit(solution)/shard_map/ppermute | solution.py:43
  187.0 10.4 %collective-permute-done.12 = bf16[128,2304]{1,0:T(8,128)(2,1)S(1)} collective-permute-done((bf16[128,2304]{1,0:T(8,128)(2,1)S(1)}, bf16[128,2304]{1,0:T(8,128)(2,1)S(1)}, u32[]{:S(2)}, u32[]{:S(2)}) %collective-permute-start.12) | collective-permute-done | bytes 589856 | tf_op jit(solution)/shard_map/ppermute | solution.py:43
  197.6 17.7 %fusion.93 = f32[512,4608]{1,0:T(8,128)} fusion(bf16[2304,4608]{1,0:T(8,128)(2,1)} %all-gather.6.cloned.1.call-done, bf16[128,2304]{1,0:T(8,128)(2,1)S(1)} %broadcast_select_fusion.1, bf16[128,2304]{1,0:T(8,128)(2,1)S(1)} %broadcast_select_fusion.3, bf16[128,2304]{1,0:T(8,128)(2,1)S(1)} %broadcast_select_fusion.5, ...), kind=kOutput, calls=%fused_computation.210 | convolution fusion | flops 10881073152 | bytes 33030144 | tf_op jit(solution)/shard_map/dot_general | solution.py:31
  215.3 5.6 multiply_convert_fusion.1
  220.9 24.1 %all-gather.8.cloned.1.call-done = bf16[2304,2304]{1,0:T(8,128)(2,1)} async-done(((bf16[288,2304]{1,0:T(8,128)(2,1)}), bf16[2304,2304]{1,0:T(8,128)(2,1)}) %all-gather.8.cloned.1.call-update) | async-done | bytes 10616848 | tf_op jit(solution)/shard_map/all_gather | solution.py:122
  245.0 10.3 %convolution_convert_fusion.4 = bf16[512,2304]{1,0:T(8,128)(2,1)S(1)} fusion(bf16[512,2304]{1,0:T(8,128)(2,1)} %multiply_convert_fusion.1, bf16[2304,2304]{1,0:T(8,128)(2,1)} %all-gather.8.cloned.1.call-done), kind=kOutput, calls=%fused_computation.24 | convolution fusion | flops 5436997632 | bytes 15335424 | tf_op jit(solution)/shard_map/dot_general | solution.py:39
  259.6 12.2 %collective-permute-done.13 = bf16[128,2304]{1,0:T(8,128)(2,1)S(1)} collective-permute-done((bf16[128,2304]{1,0:T(8,128)(2,1)S(1)}, bf16[128,2304]{1,0:T(8,128)(2,1)S(1)}, u32[]{:S(2)}, u32[]{:S(2)}) %collective-permute-start.13) | collective-permute-done | bytes 589856 | tf_op jit(solution)/shard_map/ppermute | solution.py:43
  277.4 11.4 %collective-permute-done.15 = bf16[128,2304]{1,0:T(8,128)(2,1)S(1)} collective-permute-done((bf16[128,2304]{1,0:T(8,128)(2,1)S(1)}, bf16[128,2304]{1,0:T(8,128)(2,1)S(1)}, u32[]{:S(2)}, u32[]{:S(2)}) %collective-permute-start.15) | collective-permute-done | bytes 589856 | tf_op jit(solution)/shard_map/ppermute | solution.py:43
  289.0 8.3 %collective-permute-start.17 = (bf16[128,2304]{1,0:T(8,128)(2,1)S(1)}, bf16[128,2304]{1,0:T(8,128)(2,1)S(1)}, u32[]{:S(2)}, u32[]{:S(2)}) collective-permute-start(bf16[128,2304]{1,0:T(8,128)(2,1)S(1)} %get-tuple-element.91), channel_id=1, source_target_pairs={{0,1},{1,2},{2,3},{4,5},{5,6},{6,7},{8,9},{9,10},{10,11},{12,13},{... | collective-permute-start | bytes 1769480 | tf_op jit(solution)/shard_map/ppermute | solution.py:43
  298.6 9.7 %collective-permute-done.17 = bf16[128,2304]{1,0:T(8,128)(2,1)S(1)} collective-permute-done((bf16[128,2304]{1,0:T(8,128)(2,1)S(1)}, bf16[128,2304]{1,0:T(8,128)(2,1)S(1)}, u32[]{:S(2)}, u32[]{:S(2)}) %collective-permute-start.17) | collective-permute-done | bytes 589856 | tf_op jit(solution)/shard_map/ppermute | solution.py:43
  318.9 8.8 %collective-permute-done.19 = bf16[128,2304]{1,0:T(8,128)(2,1)S(1)} collective-permute-done((bf16[128,2304]{1,0:T(8,128)(2,1)S(1)}, bf16[128,2304]{1,0:T(8,128)(2,1)S(1)}, u32[]{:S(2)}, u32[]{:S(2)}) %collective-permute-start.19) | collective-permute-done | bytes 589856 | tf_op jit(solution)/shard_map/ppermute | solution.py:43
  333.9 12.3 %collective-permute-done.22 = bf16[128,2304]{1,0:T(8,128)(2,1)S(1)} collective-permute-done((bf16[128,2304]{1,0:T(8,128)(2,1)S(1)}, bf16[128,2304]{1,0:T(8,128)(2,1)S(1)}, u32[]{:S(2)}, u32[]{:S(2)}) %collective-permute-start.22) | collective-permute-done | bytes 589856 | tf_op jit(solution)/shard_map/ppermute | solution.py:43
  348.3 11.4 %collective-permute-done.24 = bf16[128,2304]{1,0:T(8,128)(2,1)S(1)} collective-permute-done((bf16[128,2304]{1,0:T(8,128)(2,1)S(1)}, bf16[128,2304]{1,0:T(8,128)(2,1)S(1)}, u32[]{:S(2)}, u32[]{:S(2)}) %collective-permute-start.24) | collective-permute-done | bytes 589856 | tf_op jit(solution)/shard_map/ppermute | solution.py:43
  364.7 4.6 convolution_convert_fusion.1
  383.8 13.6 %fusion.9 = (bf16[512,2304]{1,0:T(8,128)(2,1)S(1)}, bf16[512,2304]{1,0:T(8,128)(2,1)S(1)}) fusion(f32[512,4608]{1,0:T(8,128)} %fusion.93, bf16[512,2304]{1,0:T(8,128)(2,1)S(1)} %pad_maximum_fusion.3, bf16[2304,2304]{1,0:T(8,128)(2,1)} %all-gather.8.cloned.1.call-done), kind=kOutput, calls=%fused_computation.17 | convolution fusion | flops 5464129536 | bytes 27131904 | tf_op jit(solution)/shard_map/dot_general | solution.py:31
  399.9 6.6 add_convert_fusion.1
  406.5 10.7 %convolution_convert_fusion = bf16[1152,4608]{1,0:T(8,128)(2,1)} fusion(bf16[512,1152]{0,1:T(8,128)(2,1)S(1)} %bitcast.221, bf16[512,4608]{1,0:T(8,128)(2,1)} %pad_maximum_fusion), kind=kOutput, calls=%fused_computation.1 | convolution fusion | flops 5441126400 | bytes 16515072 | tf_op jit(solution)/shard_map/dot_general | solution.py:35
  417.7 14.8 %convolution_convert_fusion.3 = bf16[512,2304]{1,0:T(8,128)(2,1)S(1)} fusion(bf16[512,4608]{1,0:T(8,128)(2,1)S(1)} %copy-done.6, bf16[2304,4608]{1,0:T(8,128)(2,1)} %all-gather.6.cloned.1.call-done), kind=kOutput, calls=%fused_computation.23 | convolution fusion | flops 10872815616 | bytes 28311552 | tf_op jit(solution)/shard_map/dot_general | solution.py:39
  434.8 12.1 %collective-permute-done.26 = bf16[128,2304]{1,0:T(8,128)(2,1)S(1)} collective-permute-done((bf16[128,2304]{1,0:T(8,128)(2,1)S(1)}, bf16[128,2304]{1,0:T(8,128)(2,1)S(1)}, u32[]{:S(2)}, u32[]{:S(2)}) %collective-permute-start.26) | collective-permute-done | bytes 589856 | tf_op jit(solution)/shard_map/ppermute | solution.py:43
  452.3 11.3 %collective-permute-done.28 = bf16[128,2304]{1,0:T(8,128)(2,1)S(1)} collective-permute-done((bf16[128,2304]{1,0:T(8,128)(2,1)S(1)}, bf16[128,2304]{1,0:T(8,128)(2,1)S(1)}, u32[]{:S(2)}, u32[]{:S(2)}) %collective-permute-start.28) | collective-permute-done | bytes 589856 | tf_op jit(solution)/shard_map/ppermute | solution.py:43
  464.8 6.3 collective-permute-start.30
  472.6 10.0 %collective-permute-done.30 = bf16[128,2304]{1,0:T(8,128)(2,1)S(1)} collective-permute-done((bf16[128,2304]{1,0:T(8,128)(2,1)}, bf16[128,2304]{1,0:T(8,128)(2,1)S(1)}, u32[]{:S(2)}, u32[]{:S(2)}) %collective-permute-start.30) | collective-permute-done | bytes 589856 | tf_op jit(solution)/shard_map/ppermute | solution.py:43
  493.9 10.9 %add_convert_fusion = bf16[1152,4608]{1,0:T(8,128)(2,1)} fusion(bf16[1152,4608]{1,0:T(8,128)(2,1)} %collective-permute-done.32, bf16[512,1152]{0,1:T(8,128)(2,1)S(1)} %bitcast.218, bf16[512,4608]{1,0:T(8,128)(2,1)S(1)} %bitcast.206), kind=kOutput, calls=%fused_computation | convolution fusion | flops 5451743232 | bytes 27131904 | tf_op jit(solution)/shard_map/dot_general | solution.py:35
  508.4 8.8 %collective-permute-done.33 = bf16[128,2304]{1,0:T(8,128)(2,1)S(1)} collective-permute-done((bf16[128,2304]{1,0:T(8,128)(2,1)S(1)}, bf16[128,2304]{1,0:T(8,128)(2,1)S(1)}, u32[]{:S(2)}, u32[]{:S(2)}) %collective-permute-start.33) | collective-permute-done | bytes 589856 | tf_op jit(solution)/shard_map/ppermute | solution.py:43
  523.3 12.1 %collective-permute-done.36 = bf16[128,2304]{1,0:T(8,128)(2,1)S(1)} collective-permute-done((bf16[128,2304]{1,0:T(8,128)(2,1)S(1)}, bf16[128,2304]{1,0:T(8,128)(2,1)S(1)}, u32[]{:S(2)}, u32[]{:S(2)}) %collective-permute-start.36) | collective-permute-done | bytes 589856 | tf_op jit(solution)/shard_map/ppermute | solution.py:43
  537.6 11.1 %collective-permute-done.38 = bf16[128,2304]{1,0:T(8,128)(2,1)S(1)} collective-permute-done((bf16[128,2304]{1,0:T(8,128)(2,1)S(1)}, bf16[128,2304]{1,0:T(8,128)(2,1)S(1)}, u32[]{:S(2)}, u32[]{:S(2)}) %collective-permute-start.38) | collective-permute-done | bytes 589856 | tf_op jit(solution)/shard_map/ppermute | solution.py:43
  567.7 6.9 collective-permute-done.45
  582.5 4.7 add_convert_fusion.2
  591.6 5.4 convolution_convert_fusion.2
  597.1 4.6 collective-permute-start.46
  610.4 4.8 collective-permute-done.46
  632.1 9.0 %collective-permute-done.48 = bf16[128,2304]{1,0:T(8,128)(2,1)S(1)} collective-permute-done((bf16[128,2304]{1,0:T(8,128)(2,1)S(1)}, bf16[128,2304]{1,0:T(8,128)(2,1)S(1)}, u32[]{:S(2)}, u32[]{:S(2)}) %collective-permute-start.48) | collective-permute-done | bytes 589856 | tf_op jit(solution)/shard_map/ppermute | solution.py:43
  648.3 8.9 %collective-permute-done.50 = bf16[128,2304]{1,0:T(8,128)(2,1)S(1)} collective-permute-done((bf16[128,2304]{1,0:T(8,128)(2,1)S(1)}, bf16[128,2304]{1,0:T(8,128)(2,1)S(1)}, u32[]{:S(2)}, u32[]{:S(2)}) %collective-permute-start.50) | collective-permute-done | bytes 589856 | tf_op jit(solution)/shard_map/ppermute | solution.py:43
  675.6 5.2 collective-permute-done.52
  687.9 12.4 %collective-permute-done.55 = bf16[128,2304]{1,0:T(8,128)(2,1)S(1)} collective-permute-done((bf16[128,2304]{1,0:T(8,128)(2,1)S(1)}, bf16[128,2304]{1,0:T(8,128)(2,1)S(1)}, u32[]{:S(2)}, u32[]{:S(2)}) %collective-permute-start.55) | collective-permute-done | bytes 589856 | tf_op jit(solution)/shard_map/ppermute | solution.py:43
  707.6 5.3 collective-permute-done.57
  719.4 35.6 %reduce-scatter.9.cloned.1.call-done = bf16[288,4608]{1,0:T(8,128)(2,1)} async-done(((bf16[1152,4608]{1,0:T(8,128)(2,1)}), bf16[288,4608]{1,0:T(8,128)(2,1)}) %reduce-scatter.9.cloned.1.call-update) | async-done | bytes 2654224 | tf_op jit(solution)/shard_map/reduce_scatter | solution.py:149
  (357 shorter events, 240.6 us)
Async XLA Ops:
  7.2 54.7 %all-gather.4.cloned.1.call-start = ((), (), s32[]{:S(2)}) async-start(), calls=%async_computation.4 | async-start | bytes 7962624 | tf_op jit(solution)/shard_map/all_gather | solution.py:122
  9.6 188.0 %all-gather.6.cloned.1.call-start = ((), (), s32[]{:S(2)}) async-start(), calls=%async_computation.5 | async-start | bytes 23887872 | tf_op jit(solution)/shard_map/all_gather | solution.py:122
  11.4 233.7 %all-gather.8.cloned.1.call-start = ((), (), s32[]{:S(2)}) async-start(), calls=%async_computation.6 | async-start | bytes 11943936 | tf_op jit(solution)/shard_map/all_gather | solution.py:122
  12.1 609.2 %reduce-scatter.11.cloned.1.call-start = ((), (), s32[]{:S(2)}) async-start(), calls=%async_computation.10 | async-start | bytes 6635520 | tf_op jit(solution)/shard_map/reduce_scatter | solution.py:149
  67.7 23.7 %collective-permute-start = (bf16[512,512]{1,0:T(8,128)(2,1)S(1)}, bf16[512,512]{1,0:T(8,128)(2,1)S(1)}, u32[]{:S(2)}, u32[]{:S(2)}) collective-permute-start(bf16[512,512]{1,0:T(8,128)(2,1)S(1)} %get-tuple-element.192), channel_id=1, source_target_pairs={{0,4},{1,5},{2,6},{3,7},{8,12},{9,13},{10,14},{11,15},{16,20},{17,... | collective-permute-start | bytes 1572872 | tf_op jit(solution)/shard_map/ppermute | solution.py:19
  98.4 13.8 %collective-permute-start.1 = (bf16[128,2304]{1,0:T(8,128)(2,1)S(1)}, bf16[128,2304]{1,0:T(8,128)(2,1)}, u32[]{:S(2)}, u32[]{:S(2)}) collective-permute-start(bf16[128,2304]{1,0:T(8,128)(2,1)S(1)} %get-tuple-element.75), channel_id=1, source_target_pairs={{0,1},{4,5},{8,9},{12,13},{16,17},{20,21},{24,25},{28,29}} | collective-permute-start | bytes 1769480 | tf_op jit(solution)/shard_map/ppermute | solution.py:43
  114.4 14.9 %collective-permute-start.3 = (bf16[128,2304]{1,0:T(8,128)(2,1)S(1)}, bf16[128,2304]{1,0:T(8,128)(2,1)S(1)}, u32[]{:S(2)}, u32[]{:S(2)}) collective-permute-start(bf16[128,2304]{1,0:T(8,128)(2,1)S(1)} %get-tuple-element.77), channel_id=1, source_target_pairs={{0,1},{1,2},{4,5},{5,6},{8,9},{9,10},{12,13},{13,14},{16,17},{17,1... | collective-permute-start | bytes 1769480 | tf_op jit(solution)/shard_map/ppermute | solution.py:43
  129.5 14.6 %collective-permute-start.5 = (bf16[128,2304]{1,0:T(8,128)(2,1)S(1)}, bf16[128,2304]{1,0:T(8,128)(2,1)S(1)}, u32[]{:S(2)}, u32[]{:S(2)}) collective-permute-start(bf16[128,2304]{1,0:T(8,128)(2,1)S(1)} %add_convert_fusion.12), channel_id=1, source_target_pairs={{0,1},{1,2},{2,3},{4,5},{5,6},{6,7},{8,9},{9,10},{10,11},{12,13},{... | collective-permute-start | bytes 1769480 | tf_op jit(solution)/shard_map/ppermute | solution.py:43
  135.0 14.2 %collective-permute-start.6 = (bf16[128,2304]{1,0:T(8,128)(2,1)}, bf16[128,2304]{1,0:T(8,128)(2,1)}, u32[]{:S(2)}, u32[]{:S(2)}) collective-permute-start(bf16[128,2304]{1,0:T(8,128)(2,1)} %add_convert_fusion.11), channel_id=1, source_target_pairs={{1,0},{2,1},{3,2},{5,4},{6,5},{7,6},{9,8},{10,9},{11,10},{13,12},{... | collective-permute-start | bytes 1769480 | tf_op jit(solution)/shard_map/ppermute | solution.py:43
  158.3 13.4 %collective-permute-start.8 = (bf16[128,2304]{1,0:T(8,128)(2,1)S(1)}, bf16[128,2304]{1,0:T(8,128)(2,1)S(1)}, u32[]{:S(2)}, u32[]{:S(2)}) collective-permute-start(bf16[128,2304]{1,0:T(8,128)(2,1)S(1)} %multiply_convert_fusion.2), channel_id=1, source_target_pairs={{1,0},{2,1},{3,2},{5,4},{6,5},{7,6},{9,8},{10,9},{11,10},{13,12},{... | collective-permute-start | bytes 1769480 | tf_op jit(solution)/shard_map/ppermute | solution.py:43
  171.7 13.1 %collective-permute-start.10 = (bf16[128,2304]{1,0:T(8,128)(2,1)S(1)}, bf16[128,2304]{1,0:T(8,128)(2,1)S(1)}, u32[]{:S(2)}, u32[]{:S(2)}) collective-permute-start(bf16[128,2304]{1,0:T(8,128)(2,1)S(1)} %collective-permute-done.8), channel_id=1, source_target_pairs={{1,0},{2,1},{5,4},{6,5},{9,8},{10,9},{13,12},{14,13},{17,16},{18,1... | collective-permute-start | bytes 1769480 | tf_op jit(solution)/shard_map/ppermute | solution.py:43
  255.4 16.4 %collective-permute-start.13 = (bf16[128,2304]{1,0:T(8,128)(2,1)S(1)}, bf16[128,2304]{1,0:T(8,128)(2,1)S(1)}, u32[]{:S(2)}, u32[]{:S(2)}) collective-permute-start(bf16[128,2304]{1,0:T(8,128)(2,1)S(1)} %get-tuple-element.87), channel_id=1, source_target_pairs={{0,1},{4,5},{8,9},{12,13},{16,17},{20,21},{24,25},{28,29}} | collective-permute-start | bytes 1769480 | tf_op jit(solution)/shard_map/ppermute | solution.py:43
  258.9 12.9 %collective-permute-start.14 = (bf16[128,2304]{1,0:T(8,128)(2,1)S(1)}, bf16[128,2304]{1,0:T(8,128)(2,1)S(1)}, u32[]{:S(2)}, u32[]{:S(2)}) collective-permute-start(bf16[128,2304]{1,0:T(8,128)(2,1)S(1)} %get-tuple-element.88), channel_id=1, source_target_pairs={{3,2},{7,6},{11,10},{15,14},{19,18},{23,22},{27,26},{31,30}} | collective-permute-start | bytes 1769480 | tf_op jit(solution)/shard_map/ppermute | solution.py:43
  272.1 16.6 %collective-permute-start.15 = (bf16[128,2304]{1,0:T(8,128)(2,1)S(1)}, bf16[128,2304]{1,0:T(8,128)(2,1)S(1)}, u32[]{:S(2)}, u32[]{:S(2)}) collective-permute-start(bf16[128,2304]{1,0:T(8,128)(2,1)S(1)} %get-tuple-element.89), channel_id=1, source_target_pairs={{0,1},{1,2},{4,5},{5,6},{8,9},{9,10},{12,13},{13,14},{16,17},{17,1... | collective-permute-start | bytes 1769480 | tf_op jit(solution)/shard_map/ppermute | solution.py:43
  289.0 19.2 %collective-permute-start.17 = (bf16[128,2304]{1,0:T(8,128)(2,1)S(1)}, bf16[128,2304]{1,0:T(8,128)(2,1)S(1)}, u32[]{:S(2)}, u32[]{:S(2)}) collective-permute-start(bf16[128,2304]{1,0:T(8,128)(2,1)S(1)} %get-tuple-element.91), channel_id=1, source_target_pairs={{0,1},{1,2},{2,3},{4,5},{5,6},{6,7},{8,9},{9,10},{10,11},{12,13},{... | collective-permute-start | bytes 1769480 | tf_op jit(solution)/shard_map/ppermute | solution.py:43
  297.3 15.1 %collective-permute-start.18 = (bf16[128,2304]{1,0:T(8,128)(2,1)S(1)}, bf16[128,2304]{1,0:T(8,128)(2,1)S(1)}, u32[]{:S(2)}, u32[]{:S(2)}) collective-permute-start(bf16[128,2304]{1,0:T(8,128)(2,1)S(1)} %get-tuple-element.92), channel_id=1, source_target_pairs={{1,0},{2,1},{3,2},{5,4},{6,5},{7,6},{9,8},{10,9},{11,10},{13,12},{... | collective-permute-start | bytes 1769480 | tf_op jit(solution)/shard_map/ppermute | solution.py:43
  317.6 14.3 %collective-permute-start.20 = (bf16[128,2304]{1,0:T(8,128)(2,1)S(1)}, bf16[128,2304]{1,0:T(8,128)(2,1)S(1)}, u32[]{:S(2)}, u32[]{:S(2)}) collective-permute-start(bf16[128,2304]{1,0:T(8,128)(2,1)S(1)} %get-tuple-element.160), channel_id=1, source_target_pairs={{1,0},{2,1},{3,2},{5,4},{6,5},{7,6},{9,8},{10,9},{11,10},{13,12},{... | collective-permute-start | bytes 1769480 | tf_op jit(solution)/shard_map/ppermute | solution.py:43
  332.5 13.7 %collective-permute-start.22 = (bf16[128,2304]{1,0:T(8,128)(2,1)S(1)}, bf16[128,2304]{1,0:T(8,128)(2,1)S(1)}, u32[]{:S(2)}, u32[]{:S(2)}) collective-permute-start(bf16[128,2304]{1,0:T(8,128)(2,1)S(1)} %collective-permute-done.20), channel_id=1, source_target_pairs={{1,0},{2,1},{5,4},{6,5},{9,8},{10,9},{13,12},{14,13},{17,16},{18,1... | collective-permute-start | bytes 1769480 | tf_op jit(solution)/shard_map/ppermute | solution.py:43
  346.9 12.8 %collective-permute-start.24 = (bf16[128,2304]{1,0:T(8,128)(2,1)S(1)}, bf16[128,2304]{1,0:T(8,128)(2,1)S(1)}, u32[]{:S(2)}, u32[]{:S(2)}) collective-permute-start(bf16[128,2304]{1,0:T(8,128)(2,1)S(1)} %collective-permute-done.22), channel_id=1, source_target_pairs={{1,0},{5,4},{9,8},{13,12},{17,16},{21,20},{25,24},{29,28}} | collective-permute-start | bytes 1769480 | tf_op jit(solution)/shard_map/ppermute | solution.py:43
  369.3 30.6 %collective-permute-start.25 = (bf16[1152,2304]{1,0:T(8,128)(2,1)}, bf16[1152,2304]{1,0:T(8,128)(2,1)}, u32[]{:S(2)}, u32[]{:S(2)}) collective-permute-start(bf16[1152,2304]{1,0:T(8,128)(2,1)} %convolution_convert_fusion.1), channel_id=1, source_target_pairs={{0,8},{8,0},{16,24},{24,16},{1,9},{9,1},{17,25},{25,17},{2,10},{10... | collective-permute-start | bytes 15925256 | tf_op jit(solution)/shard_map/ppermute | solution.py:137
  417.2 75.5 %collective-permute-start.32 = (bf16[1152,4608]{1,0:T(8,128)(2,1)}, bf16[1152,4608]{1,0:T(8,128)(2,1)}, u32[]{:S(2)}, u32[]{:S(2)}) collective-permute-start(bf16[1152,4608]{1,0:T(8,128)(2,1)} %convolution_convert_fusion), channel_id=1, source_target_pairs={{0,8},{8,0},{16,24},{24,16},{1,9},{9,1},{17,25},{25,17},{2,10},{10... | collective-permute-start | bytes 31850504 | tf_op jit(solution)/shard_map/ppermute | solution.py:137
  432.6 14.3 %collective-permute-start.26 = (bf16[128,2304]{1,0:T(8,128)(2,1)S(1)}, bf16[128,2304]{1,0:T(8,128)(2,1)S(1)}, u32[]{:S(2)}, u32[]{:S(2)}) collective-permute-start(bf16[128,2304]{1,0:T(8,128)(2,1)S(1)} %get-tuple-element.102), channel_id=1, source_target_pairs={{0,1},{4,5},{8,9},{12,13},{16,17},{20,21},{24,25},{28,29}} | collective-permute-start | bytes 1769480 | tf_op jit(solution)/shard_map/ppermute | solution.py:43
  434.1 12.8 %collective-permute-start.27 = (bf16[128,2304]{1,0:T(8,128)(2,1)S(1)}, bf16[128,2304]{1,0:T(8,128)(2,1)S(1)}, u32[]{:S(2)}, u32[]{:S(2)}) collective-permute-start(bf16[128,2304]{1,0:T(8,128)(2,1)S(1)} %get-tuple-element.103), channel_id=1, source_target_pairs={{3,2},{7,6},{11,10},{15,14},{19,18},{23,22},{27,26},{31,30}} | collective-permute-start | bytes 1769480 | tf_op jit(solution)/shard_map/ppermute | solution.py:43
  447.1 16.4 %collective-permute-start.28 = (bf16[128,2304]{1,0:T(8,128)(2,1)S(1)}, bf16[128,2304]{1,0:T(8,128)(2,1)S(1)}, u32[]{:S(2)}, u32[]{:S(2)}) collective-permute-start(bf16[128,2304]{1,0:T(8,128)(2,1)S(1)} %get-tuple-element.104), channel_id=1, source_target_pairs={{0,1},{1,2},{4,5},{5,6},{8,9},{9,10},{12,13},{13,14},{16,17},{17,1... | collective-permute-start | bytes 1769480 | tf_op jit(solution)/shard_map/ppermute | solution.py:43
  464.8 17.8 %collective-permute-start.30 = (bf16[128,2304]{1,0:T(8,128)(2,1)}, bf16[128,2304]{1,0:T(8,128)(2,1)S(1)}, u32[]{:S(2)}, u32[]{:S(2)}) collective-permute-start(bf16[128,2304]{1,0:T(8,128)(2,1)} %get-tuple-element.106), channel_id=1, source_target_pairs={{0,1},{1,2},{2,3},{4,5},{5,6},{6,7},{8,9},{9,10},{10,11},{12,13},{... | collective-permute-start | bytes 1769480 | tf_op jit(solution)/shard_map/ppermute | solution.py:43
  471.2 15.5 %collective-permute-start.31 = (bf16[128,2304]{1,0:T(8,128)(2,1)}, bf16[128,2304]{1,0:T(8,128)(2,1)S(1)}, u32[]{:S(2)}, u32[]{:S(2)}) collective-permute-start(bf16[128,2304]{1,0:T(8,128)(2,1)} %get-tuple-element.107), channel_id=1, source_target_pairs={{1,0},{2,1},{3,2},{5,4},{6,5},{7,6},{9,8},{10,9},{11,10},{13,12},{... | collective-permute-start | bytes 1769480 | tf_op jit(solution)/shard_map/ppermute | solution.py:43
  472.5 233.2 %reduce-scatter.7.cloned.1.call-start = ((), (), s32[]{:S(2)}) async-start(), calls=%async_computation.8 | async-start | bytes 1474560 | tf_op jit(solution)/shard_map/reduce_scatter | solution.py:149
  507.1 14.2 %collective-permute-start.34 = (bf16[128,2304]{1,0:T(8,128)(2,1)S(1)}, bf16[128,2304]{1,0:T(8,128)(2,1)S(1)}, u32[]{:S(2)}, u32[]{:S(2)}) collective-permute-start(bf16[128,2304]{1,0:T(8,128)(2,1)S(1)} %fusion.57), channel_id=1, source_target_pairs={{1,0},{2,1},{3,2},{5,4},{6,5},{7,6},{9,8},{10,9},{11,10},{13,12},{... | collective-permute-start | bytes 1769480 | tf_op jit(solution)/shard_map/ppermute | solution.py:43
  522.0 13.4 %collective-permute-start.36 = (bf16[128,2304]{1,0:T(8,128)(2,1)S(1)}, bf16[128,2304]{1,0:T(8,128)(2,1)S(1)}, u32[]{:S(2)}, u32[]{:S(2)}) collective-permute-start(bf16[128,2304]{1,0:T(8,128)(2,1)S(1)} %collective-permute-done.34), channel_id=1, source_target_pairs={{1,0},{2,1},{5,4},{6,5},{9,8},{10,9},{13,12},{14,13},{17,16},{18,1... | collective-permute-start | bytes 1769480 | tf_op jit(solution)/shard_map/ppermute | solution.py:43
  536.1 12.6 %collective-permute-start.38 = (bf16[128,2304]{1,0:T(8,128)(2,1)S(1)}, bf16[128,2304]{1,0:T(8,128)(2,1)S(1)}, u32[]{:S(2)}, u32[]{:S(2)}) collective-permute-start(bf16[128,2304]{1,0:T(8,128)(2,1)S(1)} %collective-permute-done.36), channel_id=1, source_target_pairs={{1,0},{5,4},{9,8},{13,12},{17,16},{21,20},{25,24},{29,28}} | collective-permute-start | bytes 1769480 | tf_op jit(solution)/shard_map/ppermute | solution.py:43
  579.5 136.2 %reduce-scatter.5.cloned.1.call-start = ((), (), s32[]{:S(2)}) async-start(), calls=%async_computation.7 | async-start | bytes 2949120 | tf_op jit(solution)/shard_map/reduce_scatter | solution.py:149
  587.2 167.8 %reduce-scatter.9.cloned.1.call-start = ((), (), s32[]{:S(2)}) async-start(), calls=%async_computation.9 | async-start | bytes 13271040 | tf_op jit(solution)/shard_map/reduce_scatter | solution.py:149
  588.0 15.3 %collective-permute-start.39 = (bf16[128,2304]{1,0:T(8,128)(2,1)}, bf16[128,2304]{1,0:T(8,128)(2,1)}, u32[]{:S(2)}, u32[]{:S(2)}) collective-permute-start(bf16[128,2304]{1,0:T(8,128)(2,1)} %get-tuple-element.115), channel_id=1, source_target_pairs={{0,1},{1,2},{2,3},{4,5},{5,6},{6,7},{8,9},{9,10},{10,11},{12,13},{... | collective-permute-start | bytes 1769480 | tf_op jit(solution)/shard_map/ppermute | solution.py:43
  590.1 17.6 %collective-permute-start.40 = (bf16[128,2304]{1,0:T(8,128)(2,1)}, bf16[128,2304]{1,0:T(8,128)(2,1)}, u32[]{:S(2)}, u32[]{:S(2)}) collective-permute-start(bf16[128,2304]{1,0:T(8,128)(2,1)} %get-tuple-element.115), channel_id=1, source_target_pairs={{1,0},{2,1},{3,2},{5,4},{6,5},{7,6},{9,8},{10,9},{11,10},{13,12},{... | collective-permute-start | bytes 1769480 | tf_op jit(solution)/shard_map/ppermute | solution.py:43
  597.1 18.1 %collective-permute-start.46 = (bf16[128,2304]{1,0:T(8,128)(2,1)S(1)}, bf16[128,2304]{1,0:T(8,128)(2,1)S(1)}, u32[]{:S(2)}, u32[]{:S(2)}) collective-permute-start(bf16[128,2304]{1,0:T(8,128)(2,1)S(1)} %get-tuple-element.123), channel_id=1, source_target_pairs={{0,1},{4,5},{8,9},{12,13},{16,17},{20,21},{24,25},{28,29}} | collective-permute-start | bytes 1769480 | tf_op jit(solution)/shard_map/ppermute | solution.py:43
  601.7 13.6 %collective-permute-start.47 = (bf16[128,2304]{1,0:T(8,128)(2,1)S(1)}, bf16[128,2304]{1,0:T(8,128)(2,1)S(1)}, u32[]{:S(2)}, u32[]{:S(2)}) collective-permute-start(bf16[128,2304]{1,0:T(8,128)(2,1)S(1)} %get-tuple-element.124), channel_id=1, source_target_pairs={{3,2},{7,6},{11,10},{15,14},{19,18},{23,22},{27,26},{31,30}} | collective-permute-start | bytes 1769480 | tf_op jit(solution)/shard_map/ppermute | solution.py:43
  607.7 21.1 %collective-permute-start.41 = (bf16[128,2304]{1,0:T(8,128)(2,1)}, bf16[128,2304]{1,0:T(8,128)(2,1)}, u32[]{:S(2)}, u32[]{:S(2)}) collective-permute-start(bf16[128,2304]{1,0:T(8,128)(2,1)} %collective-permute-done.39), channel_id=1, source_target_pairs={{1,2},{2,3},{5,6},{6,7},{9,10},{10,11},{13,14},{14,15},{17,18},{18... | collective-permute-start | bytes 1769480 | tf_op jit(solution)/shard_map/ppermute | solution.py:43
  609.1 19.6 %collective-permute-start.42 = (bf16[128,2304]{1,0:T(8,128)(2,1)}, bf16[128,2304]{1,0:T(8,128)(2,1)}, u32[]{:S(2)}, u32[]{:S(2)}) collective-permute-start(bf16[128,2304]{1,0:T(8,128)(2,1)} %collective-permute-done.40), channel_id=1, source_target_pairs={{1,0},{2,1},{5,4},{6,5},{9,8},{10,9},{13,12},{14,13},{17,16},{18,1... | collective-permute-start | bytes 1769480 | tf_op jit(solution)/shard_map/ppermute | solution.py:43
  616.5 14.3 %collective-permute-start.49 = (bf16[128,2304]{1,0:T(8,128)(2,1)}, bf16[128,2304]{1,0:T(8,128)(2,1)}, u32[]{:S(2)}, u32[]{:S(2)}) collective-permute-start(bf16[128,2304]{1,0:T(8,128)(2,1)} %get-tuple-element.126), channel_id=1, source_target_pairs={{2,1},{3,2},{6,5},{7,6},{10,9},{11,10},{14,13},{15,14},{18,17},{19... | collective-permute-start | bytes 1769480 | tf_op jit(solution)/shard_map/ppermute | solution.py:43
  624.5 16.6 %collective-permute-start.48 = (bf16[128,2304]{1,0:T(8,128)(2,1)S(1)}, bf16[128,2304]{1,0:T(8,128)(2,1)S(1)}, u32[]{:S(2)}, u32[]{:S(2)}) collective-permute-start(bf16[128,2304]{1,0:T(8,128)(2,1)S(1)} %copy-done.34), channel_id=1, source_target_pairs={{0,1},{1,2},{4,5},{5,6},{8,9},{9,10},{12,13},{13,14},{16,17},{17,1... | collective-permute-start | bytes 1769480 | tf_op jit(solution)/shard_map/ppermute | solution.py:43
  628.8 19.5 %collective-permute-start.43 = (bf16[128,2304]{1,0:T(8,128)(2,1)}, bf16[128,2304]{1,0:T(8,128)(2,1)S(1)}, u32[]{:S(2)}, u32[]{:S(2)}) collective-permute-start(bf16[128,2304]{1,0:T(8,128)(2,1)} %collective-permute-done.41), channel_id=1, source_target_pairs={{2,3},{6,7},{10,11},{14,15},{18,19},{22,23},{26,27},{30,31}} | collective-permute-start | bytes 1769480 | tf_op jit(solution)/shard_map/ppermute | solution.py:43
  629.5 18.8 %collective-permute-start.44 = (bf16[128,2304]{1,0:T(8,128)(2,1)}, bf16[128,2304]{1,0:T(8,128)(2,1)S(1)}, u32[]{:S(2)}, u32[]{:S(2)}) collective-permute-start(bf16[128,2304]{1,0:T(8,128)(2,1)} %collective-permute-done.42), channel_id=1, source_target_pairs={{1,0},{5,4},{9,8},{13,12},{17,16},{21,20},{25,24},{29,28}} | collective-permute-start | bytes 1769480 | tf_op jit(solution)/shard_map/ppermute | solution.py:43
  641.3 16.0 %collective-permute-start.50 = (bf16[128,2304]{1,0:T(8,128)(2,1)S(1)}, bf16[128,2304]{1,0:T(8,128)(2,1)S(1)}, u32[]{:S(2)}, u32[]{:S(2)}) collective-permute-start(bf16[128,2304]{1,0:T(8,128)(2,1)S(1)} %add_convert_fusion.5), channel_id=1, source_target_pairs={{0,1},{1,2},{2,3},{4,5},{5,6},{6,7},{8,9},{9,10},{10,11},{12,13},{... | collective-permute-start | bytes 1769480 | tf_op jit(solution)/shard_map/ppermute | solution.py:43
  645.7 16.0 %collective-permute-start.51 = (bf16[128,2304]{1,0:T(8,128)(2,1)S(1)}, bf16[128,2304]{1,0:T(8,128)(2,1)S(1)}, u32[]{:S(2)}, u32[]{:S(2)}) collective-permute-start(bf16[128,2304]{1,0:T(8,128)(2,1)S(1)} %add_convert_fusion.4), channel_id=1, source_target_pairs={{1,0},{2,1},{3,2},{5,4},{6,5},{7,6},{9,8},{10,9},{11,10},{13,12},{... | collective-permute-start | bytes 1769480 | tf_op jit(solution)/shard_map/ppermute | solution.py:43
  671.2 13.4 %collective-permute-start.53 = (bf16[128,2304]{1,0:T(8,128)(2,1)S(1)}, bf16[128,2304]{1,0:T(8,128)(2,1)S(1)}, u32[]{:S(2)}, u32[]{:S(2)}) collective-permute-start(bf16[128,2304]{1,0:T(8,128)(2,1)S(1)} %get-tuple-element.150), channel_id=1, source_target_pairs={{1,0},{2,1},{3,2},{5,4},{6,5},{7,6},{9,8},{10,9},{11,10},{13,12},{... | collective-permute-start | bytes 1769480 | tf_op jit(solution)/shard_map/ppermute | solution.py:43
  673.8 14.0 %collective-permute-start.61 = (f32[4,2304]{1,0:T(4,128)S(1)}, f32[4,2304]{1,0:T(4,128)S(1)}, u32[]{:S(2)}, u32[]{:S(2)}) collective-permute-start(f32[4,2304]{1,0:T(4,128)S(1)} %add.348), channel_id=1, source_target_pairs={{0,16},{8,24},{16,0},{24,8},{1,17},{9,25},{17,1},{25,9},{2,18},{10... | collective-permute-start | bytes 110600 | tf_op jit(solution)/shard_map/ppermute | solution.py:103
  685.3 15.1 %collective-permute-start.55 = (bf16[128,2304]{1,0:T(8,128)(2,1)S(1)}, bf16[128,2304]{1,0:T(8,128)(2,1)S(1)}, u32[]{:S(2)}, u32[]{:S(2)}) collective-permute-start(bf16[128,2304]{1,0:T(8,128)(2,1)S(1)} %collective-permute-done.53), channel_id=1, source_target_pairs={{1,0},{2,1},{5,4},{6,5},{9,8},{10,9},{13,12},{14,13},{17,16},{18,1... | collective-permute-start | bytes 1769480 | tf_op jit(solution)/shard_map/ppermute | solution.py:43
  687.9 15.8 %collective-permute-start.62 = (f32[4,2304]{1,0:T(4,128)S(1)}, f32[4,2304]{1,0:T(4,128)S(1)}, u32[]{:S(2)}, u32[]{:S(2)}) collective-permute-start(f32[4,2304]{1,0:T(4,128)S(1)} %add.349), channel_id=1, source_target_pairs={{0,4},{4,0},{1,5},{5,1},{2,6},{6,2},{3,7},{7,3},{8,12},{12,8},{9,1... | collective-permute-start | bytes 110600 | tf_op jit(solution)/shard_map/ppermute | solution.py:103
  (91 other events, 972.0 us)
Sparse Core Ops, SparseCore 0:
  10.5 51.4 all-gather.3
  64.4 115.0 all-gather.5
  181.3 63.6 all-gather.7
  472.6 61.1 reduce-scatter.10
  579.6 26.0 reduce-scatter.6
  609.2 37.3 reduce-scatter.4
  649.7 105.3 reduce-scatter.8

commit v5 on v4

--- a/solution.py
+++ b/solution.py
@@ -41,6 +41,30 @@
 
 def onward(block, distance, senders):
     return lax.ppermute(block, "tp", [(i, i + distance) for i in senders])
+
+
+def shift(block, distance):
+    size = lax.axis_size("tp")
+    return lax.ppermute(block, "tp", [(i, (i + distance) % size) for i in range(size)])
+
+
+def distances(size):
+    return sorted(range(1, size), key=lambda k: (abs(2 * k - size), k))
+
+
+def sent_scattered(blocks):
+    blocks = lax.optimization_barrier(tuple(blocks))
+    arrived = [shift(blocks[k], -k) for k in distances(len(blocks))]
+    total = blocks[0].astype(F32)
+    for block in arrived:
+        total = total + block.astype(F32)
+    return total
+
+
+def sent_gathered(block):
+    size = lax.axis_size("tp")
+    pieces = {k: shift(block, k) for k in distances(size)}
+    return [block] + [pieces[k] for k in range(1, size)]
 
 
 def scattered(blocks):
@@ -118,14 +142,36 @@
     return with_layout_constraint(value, Layout(major_to_minor=(0, 1)))
 
 
+def row_groups():
+    width = lax.axis_size("ctx")
+    ranks = range(lax.axis_size("fsdp") * width)
+    return [[r for r in ranks if r // width % 2 == core] for core in range(2)]
+
+
+def swapped(value, first, second):
+    part = value.shape[-1] // (first * second)
+    order = [i * second + j for j in range(second) for i in range(first)]
+    return jnp.concatenate([value[..., k * part : (k + 1) * part] for k in order], axis=-1)
+
+
+def by_core(value):
+    return swapped(value, lax.axis_size("fsdp") // 2, 2)
+
+
+def by_chip(value):
+    return swapped(value, 2, lax.axis_size("fsdp") // 2)
+
+
 def gather_rows(weight):
-    return lax.all_gather(weight, ROWS, axis=0, tiled=True)
+    first, second = row_groups()
+    return lax.all_gather(
+        weight, ROWS, axis=0, tiled=True, axis_index_groups=[first + second]
+    )
 
 
 def rows_of_core(left, core):
-    pairs = lax.axis_size("fsdp") // 2
-    split = left.reshape(left.shape[0], pairs, 2, -1)
-    return lax.dynamic_index_in_dim(split, core, 2, False).reshape(left.shape[0], -1)
+    half = left.shape[-1] // 2
+    return lax.dynamic_slice_in_dim(left, core * half, half, axis=left.ndim - 1)
 
 
 def sent_to_core(left, right):
@@ -143,11 +189,8 @@
 
 
 def share_rows(grad):
-    width = lax.axis_size("ctx")
-    ranks = range(lax.axis_size("fsdp") * width)
-    groups = [[r for r in ranks if r // width % 2 == core] for core in range(2)]
     return lax.psum_scatter(
-        grad, ROWS, scatter_dimension=0, tiled=True, axis_index_groups=groups
+        grad, ROWS, scatter_dimension=0, tiled=True, axis_index_groups=row_groups()
     )
 
 
@@ -200,9 +243,21 @@
         own_ids[:, None] >= 0
     ) & (key_pos[None, :] < query_pos[:, None])
 
+    pre_attention_gain, post_attention_gain, pre_feedforward_gain, post_feedforward_gain = (
+        by_core(gain)
+        for gain in (
+            pre_attention_gain,
+            post_attention_gain,
+            pre_feedforward_gain,
+            post_feedforward_gain,
+        )
+    )
+    hidden_in = by_core(hidden_in)
     normed_one = rms(hidden_in.astype(F32), pre_attention_gain).astype(LOW)
     inputs = lax.dynamic_slice_in_dim(hidden_in, tp_rank * piece, piece).astype(F32)
-    upstream = lax.dynamic_slice_in_dim(cotangent, tp_rank * piece, piece).astype(F32)
+    upstream = by_core(
+        lax.dynamic_slice_in_dim(cotangent, tp_rank * piece, piece)
+    ).astype(F32)
 
     qkv_low = product(normed_one, qkv_full).astype(LOW)
     queries = qkv_low[:, :heads_width].reshape(length, kv_heads, repeats, HD)
@@ -236,10 +291,14 @@
     grad_branch_two, grad_gain_four = pull_four(upstream)
     grad_two_low = jnp.concatenate(gathered(grad_branch_two.astype(LOW)), axis=0)
 
+    result_low, grad_two_low = lax.optimization_barrier(
+        (by_chip(result.astype(LOW)), grad_two_low)
+    )
     down_sent, grad_two_low = lax.optimization_barrier(
         (sent_to_core(grad_two_low, hidden_low), grad_two_low)
     )
     down_arrived = over_cores(down_sent)
+    outputs = in_order(sent_gathered(result_low))
     _, pull_glu = jax.vjp(geglu, gate_value, up_value)
     grad_gate, grad_up = pull_glu(product(grad_two_low, down_full))
     grad_gate_up = jnp.concatenate([grad_gate.astype(LOW), grad_up.astype(LOW)], axis=1)
@@ -248,24 +307,22 @@
     )
     down_share = share_rows(grad_down_low)
     grad_normed_two = transposed_product(grad_gate_up, gate_up_full).astype(LOW)
-    grad_normed_two = scattered(turned_blocks(grad_normed_two))
-    gate_up_arrived = over_cores(sent_to_core(normed_two, grad_gate_up))
+    grad_normed_two = sent_scattered(turned_blocks(grad_normed_two))
+    gate_up_sent = sent_to_core(normed_two, grad_gate_up)
+    gate_up_arrived = over_cores(gate_up_sent)
     grad_gate_up_low = chip_rows(normed_two, grad_gate_up, gate_up_arrived)
+
+    gate_up_share = share_rows(grad_gate_up_low)
 
     _, pull_three = jax.vjp(rms, middle, pre_feedforward_gain)
     grad_middle_norm, grad_gain_three = pull_three(grad_normed_two)
     grad_middle = upstream + grad_middle_norm
     _, pull_two = jax.vjp(rms, branch_one, post_attention_gain)
     grad_branch_one, grad_gain_two = pull_two(grad_middle)
-    grad_one_own, grad_gate_up_low = lax.optimization_barrier(
-        (grad_branch_one.astype(LOW), grad_gate_up_low)
-    )
-    gate_up_share = share_rows(grad_gate_up_low)
-    grad_one_low = in_order(gathered(grad_one_own))
-    result_low, grad_one_low = lax.optimization_barrier((result.astype(LOW), grad_one_low))
-    outputs = in_order(gathered(result_low))
-
-    output_arrived = over_cores(sent_to_core(grad_one_low, attended_low))
+    grad_one_low = in_order(sent_gathered(grad_branch_one.astype(LOW)))
+
+    output_sent = sent_to_core(grad_one_low, attended_low)
+    output_arrived = over_cores(output_sent)
     output_share = share_rows(chip_rows(grad_one_low, attended_low, output_arrived))
     grad_attended = (
         product(grad_one_low, output_full).astype(LOW).reshape(length, kv_heads, repeats, HD)
@@ -296,17 +353,21 @@
     grad_kv_back = passed_along(grad_kv_all[:length].astype(LOW), "ctx", -1).astype(F32)
     grad_kv_low = (grad_kv_all[length:] + grad_kv_back).astype(LOW)
     grad_qkv = jnp.concatenate([grad_query_low, grad_kv_low], axis=1)
-    grad_normed_one = scattered(
-        ordered_blocks(transposed_product(grad_qkv, qkv_full).astype(LOW))
-    )
-    qkv_arrived = over_cores(sent_to_core(normed_one, grad_qkv))
-    qkv_share = share_rows(by_rows(chip_rows(normed_one, grad_qkv, qkv_arrived))).astype(F32)
+    grad_normed_one = transposed_product(grad_qkv, qkv_full).astype(LOW)
+    grad_normed_one = sent_scattered(ordered_blocks(grad_normed_one))
+    qkv_sent = sent_to_core(normed_one, grad_qkv)
+    qkv_arrived = over_cores(qkv_sent)
+    grad_qkv_low = by_rows(chip_rows(normed_one, grad_qkv, qkv_arrived))
+    qkv_share = share_rows(grad_qkv_low).astype(F32)
 
     _, pull_one = jax.vjp(rms, inputs, pre_attention_gain)
     grad_inputs_norm, grad_gain_one = pull_one(grad_normed_one)
-    grad_inputs = in_order(gathered((grad_middle + grad_inputs_norm).astype(LOW)))
-
-    gains = jnp.stack([grad_gain_one, grad_gain_two, grad_gain_three, grad_gain_four])
+    grad_inputs_own, grad_qkv_low = lax.optimization_barrier(
+        (by_chip((grad_middle + grad_inputs_norm).astype(LOW)), grad_qkv_low)
+    )
+    grad_inputs = in_order(sent_gathered(grad_inputs_own))
+
+    gains = by_chip(jnp.stack([grad_gain_one, grad_gain_two, grad_gain_three, grad_gain_four]))
     for axis in ("tp",) + ROWS:
         gains = summed(gains, axis)
     share = attention_full.shape[0] // (lax.axis_size("fsdp") * lax.axis_size("ctx"))

time: 777 us -> 834 us (1.073)
  waiting for transfers between devices: 407 us -> 435 us
  starting transfers between devices: 120 us -> 143 us
  matrix products: 125 us -> 136 us
    ppermute x0 -> x15, waiting for transfers between devices: none -> 189 us  [shift(): lax.ppermute(block, 'tp', [(i, (i + distance) % size) for i in range(size)])]
    ppermute x54 -> x24, waiting for transfers between devices: 270 us -> 113 us  [onward(): return lax.ppermute(block, 'tp', [(i, i + distance) for i in senders])]
    ppermute x0 -> x15, starting transfers between devices: none -> 57.3 us  [shift(): lax.ppermute(block, 'tp', [(i, (i + distance) % size) for i in range(size)])]
    ppermute x54 -> x24, starting transfers between devices: 110 us -> 64.2 us  [onward(): return lax.ppermute(block, 'tp', [(i, i + distance) for i in senders])]
    reduce_scatter x4, waiting for transfers between devices: 35.6 us -> 10.3 us  [share_rows(): lax.psum_scatter(grad, ROWS, scatter_dimension=0, tiled=True, axis_index_...]
    ppermute x4, waiting for transfers between devices: 2.95 us -> 19.4 us  [over_cores(): lax.ppermute(block, 'fsdp', [(i, i ^ 1) for i in range(lax.axis_size('fsd...]
    slice x0 -> x9, local copies, waits for them, and re-layouts: none -> 10.1 us  [swapped(): value[..., k * part:(k + 1) * part]]
    ppermute x5, starting transfers between devices: 5.25 us -> 15.3 us  [summed(): lax.ppermute(value, axis, [(i, i ^ bit) for i in range(size)])]
  transfers between devices with their start and end apart: 72 -> 57, of which waited for: 42 -> 37; matrix products, arithmetic and copies ran while one was open for 22% -> 20% of each run, Pallas kernels for 0% -> 0%
where the time goes in v5:
time: 834 us; the launch traced here: 824 us
  waiting for transfers between devices  435 us (52%)
  starting transfers between devices  143 us (17%)
  matrix products  136 us (16%)
  local copies, waits for them, and re-layouts  48.6 us (6%)
  other arithmetic  45.9 us (6%)
  between operations  16 us (2%)
    ppermute x15, waiting for transfers between devices, shift(): lax.ppermute(block, 'tp', [(i, (i + distance) % size) for i in range(size)])  189 us
    ppermute x24, waiting for transfers between devices, onward(): return lax.ppermute(block, 'tp', [(i, i + distance) for i in senders])  113 us
    ppermute x24, starting transfers between devices, onward(): return lax.ppermute(block, 'tp', [(i, i + distance) for i in senders])  64.2 us
    all_gather x3, waiting for transfers between devices, gather_rows(): lax.all_gather(weight, ROWS, axis=0, tiled=True, axis_index_groups=[first...  60.2 us
    ppermute x15, starting transfers between devices, shift(): lax.ppermute(block, 'tp', [(i, (i + distance) % size) for i in range(size)])  57.3 us
    dot_general x8, matrix products, rows_product(): lax.dot_general(left, right, (((0,), (0,)), ((), ())), preferred_element_...  46.6 us
    dot_general x4, matrix products, product(): return jnp.dot(left, right, preferred_element_type=F32)  41.1 us
    dot_general x4, matrix products, transposed_product(): lax.dot_general(left, right, (((1,), (1,)), ((), ())), preferred_element_...  34.9 us
  transfers between devices with their start and end apart: 57, of which 37 were waited for; matrix products, arithmetic and copies ran while one was open for 20% of the time, Pallas kernels for 0%

profile of v5, /device:TPU:0, one launch (start us, length us, event | category | flops | bytes accessed | tf_op | source)
XLA Modules:
  0.0 824.0 jit_solution(5294786399130721126)
XLA Ops:
  21.9 40.0 %all-gather.4.cloned.1.call-done = bf16[2304,1536]{1,0:T(8,128)(2,1)} async-done(((bf16[288,1536]{1,0:T(8,128)(2,1)}), bf16[2304,1536]{1,0:T(8,128)(2,1)}) %all-gather.4.cloned.1.call-update) | async-done | bytes 7077904 | tf_op jit(solution)/shard_map/all_gather | solution.py:167
  61.9 5.7 fusion.30
  75.6 18.3 %collective-permute-done = bf16[512,512]{1,0:T(8,128)(2,1)} collective-permute-done((bf16[512,512]{1,0:T(8,128)(2,1)}, bf16[512,512]{1,0:T(8,128)(2,1)}, u32[]{:S(2)}, u32[]{:S(2)}) %collective-permute-start) | collective-permute-done | bytes 524320 | tf_op jit(solution)/shard_map/ppermute | solution.py:19
  109.8 8.4 %collective-permute-done.1 = bf16[128,2304]{1,0:T(8,128)(2,1)} collective-permute-done((bf16[128,2304]{1,0:T(8,128)(2,1)S(1)}, bf16[128,2304]{1,0:T(8,128)(2,1)}, u32[]{:S(2)}, u32[]{:S(2)}) %collective-permute-start.1) | collective-permute-done | bytes 589856 | tf_op jit(solution)/shard_map/ppermute | solution.py:43
  121.2 5.1 collective-permute-start.3
  127.3 8.2 collective-permute-done.3
  135.6 5.7 collective-permute-start.5
  150.0 5.1 collective-permute-done.6
  163.7 6.2 collective-permute-done.7
  169.8 6.0 collective-permute-done.8
  178.7 11.2 %collective-permute-done.10 = bf16[128,2304]{1,0:T(8,128)(2,1)S(1)} collective-permute-done((bf16[128,2304]{1,0:T(8,128)(2,1)S(1)}, bf16[128,2304]{1,0:T(8,128)(2,1)S(1)}, u32[]{:S(2)}, u32[]{:S(2)}) %collective-permute-start.10) | collective-permute-done | bytes 589856 | tf_op jit(solution)/shard_map/ppermute | solution.py:43
  192.0 10.4 %collective-permute-done.12 = bf16[128,2304]{1,0:T(8,128)(2,1)S(1)} collective-permute-done((bf16[128,2304]{1,0:T(8,128)(2,1)S(1)}, bf16[128,2304]{1,0:T(8,128)(2,1)S(1)}, u32[]{:S(2)}, u32[]{:S(2)}) %collective-permute-start.12) | collective-permute-done | bytes 589856 | tf_op jit(solution)/shard_map/ppermute | solution.py:43
  202.5 17.9 %fusion.113 = f32[512,4608]{1,0:T(8,128)} fusion(bf16[2304,4608]{1,0:T(8,128)(2,1)} %all-gather.6.cloned.1.call-done, bf16[128,2304]{1,0:T(8,128)(2,1)S(1)} %broadcast_select_fusion.1, bf16[128,2304]{1,0:T(8,128)(2,1)S(1)} %broadcast_select_fusion.3, bf16[128,2304]{1,0:T(8,128)(2,1)S(1)} %broadcast_select_fusion.5, ...), kind=kOutput, calls=%fused_computation.211 | convolution fusion | flops 10881073152 | bytes 33030144 | tf_op jit(solution)/shard_map/dot_general | solution.py:31
  220.5 5.6 multiply_convert_fusion.1
  226.1 20.1 %all-gather.8.cloned.1.call-done = bf16[2304,2304]{1,0:T(8,128)(2,1)} async-done(((bf16[288,2304]{1,0:T(8,128)(2,1)}), bf16[2304,2304]{1,0:T(8,128)(2,1)}) %all-gather.8.cloned.1.call-update) | async-done | bytes 10616848 | tf_op jit(solution)/shard_map/all_gather | solution.py:167
  246.2 10.3 %convolution_convert_fusion.4 = bf16[512,2304]{1,0:T(8,128)(2,1)S(1)} fusion(bf16[512,2304]{1,0:T(8,128)(2,1)} %multiply_convert_fusion.1, bf16[2304,2304]{1,0:T(8,128)(2,1)} %all-gather.8.cloned.1.call-done), kind=kOutput, calls=%fused_computation.24 | convolution fusion | flops 5436997632 | bytes 15335424 | tf_op jit(solution)/shard_map/dot_general | solution.py:39
  260.7 12.2 %collective-permute-done.13 = bf16[128,2304]{1,0:T(8,128)(2,1)S(1)} collective-permute-done((bf16[128,2304]{1,0:T(8,128)(2,1)S(1)}, bf16[128,2304]{1,0:T(8,128)(2,1)S(1)}, u32[]{:S(2)}, u32[]{:S(2)}) %collective-permute-start.13) | collective-permute-done | bytes 589856 | tf_op jit(solution)/shard_map/ppermute | solution.py:43
  273.2 4.4 collective-permute-start.15
  278.4 11.4 %collective-permute-done.15 = bf16[128,2304]{1,0:T(8,128)(2,1)S(1)} collective-permute-done((bf16[128,2304]{1,0:T(8,128)(2,1)S(1)}, bf16[128,2304]{1,0:T(8,128)(2,1)S(1)}, u32[]{:S(2)}, u32[]{:S(2)}) %collective-permute-start.15) | collective-permute-done | bytes 589856 | tf_op jit(solution)/shard_map/ppermute | solution.py:43
  291.1 9.0 %collective-permute-start.17 = (bf16[128,2304]{1,0:T(8,128)(2,1)}, bf16[128,2304]{1,0:T(8,128)(2,1)}, u32[]{:S(2)}, u32[]{:S(2)}) collective-permute-start(bf16[128,2304]{1,0:T(8,128)(2,1)} %get-tuple-element.68), channel_id=1, source_target_pairs={{0,1},{1,2},{2,3},{4,5},{5,6},{6,7},{8,9},{9,10},{10,11},{12,13},{... | collective-permute-start | bytes 1769480 | tf_op jit(solution)/shard_map/ppermute | solution.py:43
  310.6 4.9 collective-permute-done.18
  325.2 8.7 %collective-permute-done.19 = bf16[128,2304]{1,0:T(8,128)(2,1)S(1)} collective-permute-done((bf16[128,2304]{1,0:T(8,128)(2,1)S(1)}, bf16[128,2304]{1,0:T(8,128)(2,1)S(1)}, u32[]{:S(2)}, u32[]{:S(2)}) %collective-permute-start.19) | collective-permute-done | bytes 589856 | tf_op jit(solution)/shard_map/ppermute | solution.py:43
  343.4 10.0 %collective-permute-done.22 = bf16[128,2304]{1,0:T(8,128)(2,1)} collective-permute-done((bf16[128,2304]{1,0:T(8,128)(2,1)S(1)}, bf16[128,2304]{1,0:T(8,128)(2,1)}, u32[]{:S(2)}, u32[]{:S(2)}) %collective-permute-start.22) | collective-permute-done | bytes 589856 | tf_op jit(solution)/shard_map/ppermute | solution.py:43
  354.0 10.0 %collective-permute-start.24 = (bf16[128,2304]{1,0:T(8,128)(2,1)}, bf16[128,2304]{1,0:T(8,128)(2,1)S(1)}, u32[]{:S(2)}, u32[]{:S(2)}) collective-permute-start(bf16[128,2304]{1,0:T(8,128)(2,1)} %collective-permute-done.22), channel_id=1, source_target_pairs={{1,0},{5,4},{9,8},{13,12},{17,16},{21,20},{25,24},{29,28}} | collective-permute-start | bytes 1769480 | tf_op jit(solution)/shard_map/ppermute | solution.py:43
  368.9 5.0 convolution_convert_fusion.1
  373.9 14.3 %fusion.9 = (bf16[512,2304]{1,0:T(8,128)(2,1)S(1)}, bf16[512,2304]{1,0:T(8,128)(2,1)S(1)}) fusion(f32[512,4608]{1,0:T(8,128)} %fusion.113, bf16[512,2304]{1,0:T(8,128)(2,1)} %copy-done.31, bf16[2304,2304]{1,0:T(8,128)(2,1)} %all-gather.8.cloned.1.call-done), kind=kOutput, calls=%fused_computation.17 | convolution fusion | flops 5464129536 | bytes 27131904 | tf_op jit(solution)/shard_map/dot_general | solution.py:31
  392.3 6.9 add_convert_fusion.1
  399.1 15.9 %convolution_convert_fusion.3 = bf16[512,2304]{1,0:T(8,128)(2,1)S(1)} fusion(bf16[512,4608]{1,0:T(8,128)(2,1)} %pad_maximum_fusion, bf16[2304,4608]{1,0:T(8,128)(2,1)} %all-gather.6.cloned.1.call-done), kind=kOutput, calls=%fused_computation.23 | convolution fusion | flops 10872815616 | bytes 28311552 | tf_op jit(solution)/shard_map/dot_general | solution.py:39
  418.7 26.9 %collective-permute-done.29 = bf16[128,2304]{1,0:T(8,128)(2,1)S(1)} collective-permute-done((bf16[128,2304]{1,0:T(8,128)(2,1)S(1)}, bf16[128,2304]{1,0:T(8,128)(2,1)S(1)}, u32[]{:S(2)}, u32[]{:S(2)}) %collective-permute-start.29) | collective-permute-done | bytes 589856 | tf_op jit(solution)/shard_map/ppermute | solution.py:48
  445.6 12.2 %collective-permute-done.31 = bf16[128,2304]{1,0:T(8,128)(2,1)S(1)} collective-permute-done((bf16[128,2304]{1,0:T(8,128)(2,1)S(1)}, bf16[128,2304]{1,0:T(8,128)(2,1)S(1)}, u32[]{:S(2)}, u32[]{:S(2)}) %collective-permute-start.31) | collective-permute-done | bytes 589856 | tf_op jit(solution)/shard_map/ppermute | solution.py:48
  461.1 25.4 %collective-permute-start.32 = (bf16[128,2304]{1,0:T(8,128)(2,1)S(1)}, bf16[128,2304]{1,0:T(8,128)(2,1)S(1)}, u32[]{:S(2)}, u32[]{:S(2)}) collective-permute-start(bf16[128,2304]{1,0:T(8,128)(2,1)S(1)} %get-tuple-element.104), channel_id=1, source_target_pairs={{0,1},{1,2},{2,3},{3,0},{4,5},{5,6},{6,7},{7,4},{8,9},{9,10},{10,1... | collective-permute-start | bytes 1769480 | tf_op jit(solution)/shard_map/ppermute | solution.py:48
  489.1 11.1 %collective-permute-done.32 = bf16[128,2304]{1,0:T(8,128)(2,1)S(1)} collective-permute-done((bf16[128,2304]{1,0:T(8,128)(2,1)S(1)}, bf16[128,2304]{1,0:T(8,128)(2,1)S(1)}, u32[]{:S(2)}, u32[]{:S(2)}) %collective-permute-start.32) | collective-permute-done | bytes 589856 | tf_op jit(solution)/shard_map/ppermute | solution.py:48
  500.2 14.3 %collective-permute-done.33 = bf16[128,2304]{1,0:T(8,128)(2,1)S(1)} collective-permute-done((bf16[128,2304]{1,0:T(8,128)(2,1)S(1)}, bf16[128,2304]{1,0:T(8,128)(2,1)S(1)}, u32[]{:S(2)}, u32[]{:S(2)}) %collective-permute-start.33) | collective-permute-done | bytes 589856 | tf_op jit(solution)/shard_map/ppermute | solution.py:48
  514.5 9.7 %collective-permute-done.34 = bf16[128,2304]{1,0:T(8,128)(2,1)S(1)} collective-permute-done((bf16[128,2304]{1,0:T(8,128)(2,1)S(1)}, bf16[128,2304]{1,0:T(8,128)(2,1)S(1)}, u32[]{:S(2)}, u32[]{:S(2)}) %collective-permute-start.34) | collective-permute-done | bytes 589856 | tf_op jit(solution)/shard_map/ppermute | solution.py:48
  539.3 13.0 %collective-permute-done.35 = bf16[512,512]{0,1:T(8,128)(2,1)S(1)} collective-permute-done((bf16[512,512]{0,1:T(8,128)(2,1)S(1)}, bf16[512,512]{0,1:T(8,128)(2,1)S(1)}, u32[]{:S(2)}, u32[]{:S(2)}) %collective-permute-start.35) | collective-permute-done | bytes 524320 | tf_op jit(solution)/shard_map/ppermute | solution.py:19
  560.2 4.9 add_convert_fusion.2
  566.8 11.1 %convolution_convert_fusion = bf16[1152,4608]{1,0:T(8,128)(2,1)} fusion(bf16[512,4608]{1,0:T(8,128)(2,1)} %pad_maximum_fusion, bf16[512,2304]{1,0:T(8,128)(2,1)S(1)} %pad_maximum_fusion.2, s32[]{:T(128)S(6)} %select_n.192), kind=kOutput, calls=%fused_computation.1 | convolution fusion | flops 5441126400 | bytes 16515076 | tf_op jit(solution)/shard_map/dot_general | solution.py:35
  578.1 16.5 %collective-permute-done.49 = bf16[1152,4608]{1,0:T(8,128)(2,1)} collective-permute-done((bf16[1152,4608]{1,0:T(8,128)(2,1)}, bf16[1152,4608]{1,0:T(8,128)(2,1)}, u32[]{:S(2)}, u32[]{:S(2)}) %collective-permute-start.49) | collective-permute-done | bytes 10616864 | tf_op jit(solution)/shard_map/ppermute | solution.py:183
  594.6 13.3 %add_convert_fusion = bf16[1152,4608]{1,0:T(8,128)(2,1)} fusion(bf16[1152,4608]{1,0:T(8,128)(2,1)} %collective-permute-done.49, bf16[512,4608]{1,0:T(8,128)(2,1)} %pad_maximum_fusion, bf16[512,2304]{1,0:T(8,128)(2,1)S(1)} %copy-done.34, s32[]{:T(128)S(6)} %select_n.193), kind=kOutput, calls=%fused_computation | convolution fusion | flops 5451743232 | bytes 27131908 | tf_op jit(solution)/shard_map/dot_general | solution.py:35
  608.6 13.7 %collective-permute-start.25 = (bf16[128,2304]{1,0:T(8,128)(2,1)}, bf16[128,2304]{1,0:T(8,128)(2,1)S(1)}, u32[]{:S(2)}, u32[]{:S(2)}) collective-permute-start(bf16[128,2304]{1,0:T(8,128)(2,1)} %concatenate.64), channel_id=1, source_target_pairs={{0,1},{1,2},{2,3},{3,0},{4,5},{5,6},{6,7},{7,4},{8,9},{9,10},{10,1... | collective-permute-start | bytes 1769480 | tf_op jit(solution)/shard_map/ppermute | solution.py:48
  627.1 5.4 convolution_convert_fusion.2
  639.9 75.2 %collective-permute-done.36 = bf16[128,2304]{1,0:T(8,128)(2,1)S(1)} collective-permute-done((bf16[128,2304]{1,0:T(8,128)(2,1)S(1)}, bf16[128,2304]{1,0:T(8,128)(2,1)S(1)}, u32[]{:S(2)}, u32[]{:S(2)}) %collective-permute-start.36) | collective-permute-done | bytes 589856 | tf_op jit(solution)/shard_map/ppermute | solution.py:48
  718.6 13.2 %collective-permute-start.43 = (f32[4,2304]{1,0:T(4,128)}, f32[4,2304]{1,0:T(4,128)S(1)}, u32[]{:S(2)}, u32[]{:S(2)}) collective-permute-start(f32[4,2304]{1,0:T(4,128)} %concatenate.71), channel_id=1, source_target_pairs={{0,1},{1,0},{2,3},{3,2},{4,5},{5,4},{6,7},{7,6},{8,9},{9,8},{10,11... | collective-permute-start | bytes 110600 | tf_op jit(solution)/shard_map/ppermute | solution.py:127
  746.9 4.3 collective-permute-done.47
  756.2 13.8 %collective-permute-done.40 = bf16[128,2304]{1,0:T(8,128)(2,1)S(1)} collective-permute-done((bf16[128,2304]{1,0:T(8,128)(2,1)S(1)}, bf16[128,2304]{1,0:T(8,128)(2,1)S(1)}, u32[]{:S(2)}, u32[]{:S(2)}) %collective-permute-start.40) | collective-permute-done | bytes 589856 | tf_op jit(solution)/shard_map/ppermute | solution.py:48
  770.0 23.1 %collective-permute-done.41 = bf16[128,2304]{1,0:T(8,128)(2,1)S(1)} collective-permute-done((bf16[128,2304]{1,0:T(8,128)(2,1)S(1)}, bf16[128,2304]{1,0:T(8,128)(2,1)S(1)}, u32[]{:S(2)}, u32[]{:S(2)}) %collective-permute-start.41) | collective-permute-done | bytes 589856 | tf_op jit(solution)/shard_map/ppermute | solution.py:48
  802.0 10.2 %reduce-scatter.9.cloned.1.call-done = bf16[288,4608]{1,0:T(8,128)(2,1)} async-done(((bf16[1152,4608]{1,0:T(8,128)(2,1)}), bf16[288,4608]{1,0:T(8,128)(2,1)}) %reduce-scatter.9.cloned.1.call-update) | async-done | bytes 2654224 | tf_op jit(solution)/shard_map/reduce_scatter | solution.py:192
  812.2 4.5 fusion.115
  (349 shorter events, 189.6 us)
Async XLA Ops:
  7.2 54.7 %all-gather.4.cloned.1.call-start = ((), (), s32[]{:S(2)}) async-start(), calls=%async_computation.4 | async-start | bytes 7962624 | tf_op jit(solution)/shard_map/all_gather | solution.py:167
  9.6 192.9 %all-gather.6.cloned.1.call-start = ((), (), s32[]{:S(2)}) async-start(), calls=%async_computation.5 | async-start | bytes 23887872 | tf_op jit(solution)/shard_map/all_gather | solution.py:167
  11.4 234.8 %all-gather.8.cloned.1.call-start = ((), (), s32[]{:S(2)}) async-start(), calls=%async_computation.6 | async-start | bytes 11943936 | tf_op jit(solution)/shard_map/all_gather | solution.py:167
  12.1 781.1 %reduce-scatter.7.cloned.1.call-start = ((), (), s32[]{:S(2)}) async-start(), calls=%async_computation.8 | async-start | bytes 1474560 | tf_op jit(solution)/shard_map/reduce_scatter | solution.py:192
  68.7 25.2 %collective-permute-start = (bf16[512,512]{1,0:T(8,128)(2,1)}, bf16[512,512]{1,0:T(8,128)(2,1)}, u32[]{:S(2)}, u32[]{:S(2)}) collective-permute-start(bf16[512,512]{1,0:T(8,128)(2,1)} %get-tuple-element.146), channel_id=1, source_target_pairs={{0,4},{1,5},{2,6},{3,7},{8,12},{9,13},{10,14},{11,15},{16,20},{17,... | collective-permute-start | bytes 1572872 | tf_op jit(solution)/shard_map/ppermute | solution.py:19
  104.4 13.8 %collective-permute-start.1 = (bf16[128,2304]{1,0:T(8,128)(2,1)S(1)}, bf16[128,2304]{1,0:T(8,128)(2,1)}, u32[]{:S(2)}, u32[]{:S(2)}) collective-permute-start(bf16[128,2304]{1,0:T(8,128)(2,1)S(1)} %get-tuple-element.52), channel_id=1, source_target_pairs={{0,1},{4,5},{8,9},{12,13},{16,17},{20,21},{24,25},{28,29}} | collective-permute-start | bytes 1769480 | tf_op jit(solution)/shard_map/ppermute | solution.py:43
  121.2 14.2 %collective-permute-start.3 = (bf16[128,2304]{1,0:T(8,128)(2,1)S(1)}, bf16[128,2304]{1,0:T(8,128)(2,1)S(1)}, u32[]{:S(2)}, u32[]{:S(2)}) collective-permute-start(bf16[128,2304]{1,0:T(8,128)(2,1)S(1)} %get-tuple-element.54), channel_id=1, source_target_pairs={{0,1},{1,2},{4,5},{5,6},{8,9},{9,10},{12,13},{13,14},{16,17},{17,1... | collective-permute-start | bytes 1769480 | tf_op jit(solution)/shard_map/ppermute | solution.py:43
  135.6 14.4 %collective-permute-start.5 = (bf16[128,2304]{1,0:T(8,128)(2,1)S(1)}, bf16[128,2304]{1,0:T(8,128)(2,1)S(1)}, u32[]{:S(2)}, u32[]{:S(2)}) collective-permute-start(bf16[128,2304]{1,0:T(8,128)(2,1)S(1)} %add_convert_fusion.7), channel_id=1, source_target_pairs={{0,1},{1,2},{2,3},{4,5},{5,6},{6,7},{8,9},{9,10},{10,11},{12,13},{... | collective-permute-start | bytes 1769480 | tf_op jit(solution)/shard_map/ppermute | solution.py:43
  141.3 13.8 %collective-permute-start.6 = (bf16[128,2304]{1,0:T(8,128)(2,1)}, bf16[128,2304]{1,0:T(8,128)(2,1)}, u32[]{:S(2)}, u32[]{:S(2)}) collective-permute-start(bf16[128,2304]{1,0:T(8,128)(2,1)} %add_convert_fusion.6), channel_id=1, source_target_pairs={{1,0},{2,1},{3,2},{5,4},{6,5},{7,6},{9,8},{10,9},{11,10},{13,12},{... | collective-permute-start | bytes 1769480 | tf_op jit(solution)/shard_map/ppermute | solution.py:43
  158.7 11.2 %collective-permute-start.7 = (bf16[128,2304]{1,0:T(8,128)(2,1)S(1)}, bf16[128,2304]{1,0:T(8,128)(2,1)S(1)}, u32[]{:S(2)}, u32[]{:S(2)}) collective-permute-start(bf16[128,2304]{1,0:T(8,128)(2,1)S(1)} %multiply_convert_fusion.2), channel_id=1, source_target_pairs={{0,1},{1,2},{2,3},{4,5},{5,6},{6,7},{8,9},{9,10},{10,11},{12,13},{... | collective-permute-start | bytes 1769480 | tf_op jit(solution)/shard_map/ppermute | solution.py:43
  162.4 13.5 %collective-permute-start.8 = (bf16[128,2304]{1,0:T(8,128)(2,1)S(1)}, bf16[128,2304]{1,0:T(8,128)(2,1)S(1)}, u32[]{:S(2)}, u32[]{:S(2)}) collective-permute-start(bf16[128,2304]{1,0:T(8,128)(2,1)S(1)} %multiply_convert_fusion.2), channel_id=1, source_target_pairs={{1,0},{2,1},{3,2},{5,4},{6,5},{7,6},{9,8},{10,9},{11,10},{13,12},{... | collective-permute-start | bytes 1769480 | tf_op jit(solution)/shard_map/ppermute | solution.py:43
  175.9 13.9 %collective-permute-start.10 = (bf16[128,2304]{1,0:T(8,128)(2,1)S(1)}, bf16[128,2304]{1,0:T(8,128)(2,1)S(1)}, u32[]{:S(2)}, u32[]{:S(2)}) collective-permute-start(bf16[128,2304]{1,0:T(8,128)(2,1)S(1)} %collective-permute-done.8), channel_id=1, source_target_pairs={{1,0},{2,1},{5,4},{6,5},{9,8},{10,9},{13,12},{14,13},{17,16},{18,1... | collective-permute-start | bytes 1769480 | tf_op jit(solution)/shard_map/ppermute | solution.py:43
  177.2 12.7 %collective-permute-start.9 = (bf16[128,2304]{1,0:T(8,128)(2,1)S(1)}, bf16[128,2304]{1,0:T(8,128)(2,1)}, u32[]{:S(2)}, u32[]{:S(2)}) collective-permute-start(bf16[128,2304]{1,0:T(8,128)(2,1)S(1)} %collective-permute-done.7), channel_id=1, source_target_pairs={{1,2},{2,3},{5,6},{6,7},{9,10},{10,11},{13,14},{14,15},{17,18},{18... | collective-permute-start | bytes 1769480 | tf_op jit(solution)/shard_map/ppermute | solution.py:43
  190.5 11.8 %collective-permute-start.12 = (bf16[128,2304]{1,0:T(8,128)(2,1)S(1)}, bf16[128,2304]{1,0:T(8,128)(2,1)S(1)}, u32[]{:S(2)}, u32[]{:S(2)}) collective-permute-start(bf16[128,2304]{1,0:T(8,128)(2,1)S(1)} %collective-permute-done.10), channel_id=1, source_target_pairs={{1,0},{5,4},{9,8},{13,12},{17,16},{21,20},{25,24},{29,28}} | collective-permute-start | bytes 1769480 | tf_op jit(solution)/shard_map/ppermute | solution.py:43
  256.6 16.4 %collective-permute-start.13 = (bf16[128,2304]{1,0:T(8,128)(2,1)S(1)}, bf16[128,2304]{1,0:T(8,128)(2,1)S(1)}, u32[]{:S(2)}, u32[]{:S(2)}) collective-permute-start(bf16[128,2304]{1,0:T(8,128)(2,1)S(1)} %get-tuple-element.64), channel_id=1, source_target_pairs={{0,1},{4,5},{8,9},{12,13},{16,17},{20,21},{24,25},{28,29}} | collective-permute-start | bytes 1769480 | tf_op jit(solution)/shard_map/ppermute | solution.py:43
  260.0 12.9 %collective-permute-start.14 = (bf16[128,2304]{1,0:T(8,128)(2,1)S(1)}, bf16[128,2304]{1,0:T(8,128)(2,1)S(1)}, u32[]{:S(2)}, u32[]{:S(2)}) collective-permute-start(bf16[128,2304]{1,0:T(8,128)(2,1)S(1)} %get-tuple-element.65), channel_id=1, source_target_pairs={{3,2},{7,6},{11,10},{15,14},{19,18},{23,22},{27,26},{31,30}} | collective-permute-start | bytes 1769480 | tf_op jit(solution)/shard_map/ppermute | solution.py:43
  273.2 16.5 %collective-permute-start.15 = (bf16[128,2304]{1,0:T(8,128)(2,1)S(1)}, bf16[128,2304]{1,0:T(8,128)(2,1)S(1)}, u32[]{:S(2)}, u32[]{:S(2)}) collective-permute-start(bf16[128,2304]{1,0:T(8,128)(2,1)S(1)} %get-tuple-element.66), channel_id=1, source_target_pairs={{0,1},{1,2},{4,5},{5,6},{8,9},{9,10},{12,13},{13,14},{16,17},{17,1... | collective-permute-start | bytes 1769480 | tf_op jit(solution)/shard_map/ppermute | solution.py:43
  277.7 12.1 %collective-permute-start.16 = (bf16[128,2304]{1,0:T(8,128)(2,1)S(1)}, bf16[128,2304]{1,0:T(8,128)(2,1)S(1)}, u32[]{:S(2)}, u32[]{:S(2)}) collective-permute-start(bf16[128,2304]{1,0:T(8,128)(2,1)S(1)} %get-tuple-element.67), channel_id=1, source_target_pairs={{2,1},{3,2},{6,5},{7,6},{10,9},{11,10},{14,13},{15,14},{18,17},{19... | collective-permute-start | bytes 1769480 | tf_op jit(solution)/shard_map/ppermute | solution.py:43
  291.1 19.5 %collective-permute-start.17 = (bf16[128,2304]{1,0:T(8,128)(2,1)}, bf16[128,2304]{1,0:T(8,128)(2,1)}, u32[]{:S(2)}, u32[]{:S(2)}) collective-permute-start(bf16[128,2304]{1,0:T(8,128)(2,1)} %get-tuple-element.68), channel_id=1, source_target_pairs={{0,1},{1,2},{2,3},{4,5},{5,6},{6,7},{8,9},{9,10},{10,11},{12,13},{... | collective-permute-start | bytes 1769480 | tf_op jit(solution)/shard_map/ppermute | solution.py:43
  300.1 15.4 %collective-permute-start.18 = (bf16[128,2304]{1,0:T(8,128)(2,1)}, bf16[128,2304]{1,0:T(8,128)(2,1)}, u32[]{:S(2)}, u32[]{:S(2)}) collective-permute-start(bf16[128,2304]{1,0:T(8,128)(2,1)} %get-tuple-element.69), channel_id=1, source_target_pairs={{1,0},{2,1},{3,2},{5,4},{6,5},{7,6},{9,8},{10,9},{11,10},{13,12},{... | collective-permute-start | bytes 1769480 | tf_op jit(solution)/shard_map/ppermute | solution.py:43
  322.4 11.5 %collective-permute-start.19 = (bf16[128,2304]{1,0:T(8,128)(2,1)S(1)}, bf16[128,2304]{1,0:T(8,128)(2,1)S(1)}, u32[]{:S(2)}, u32[]{:S(2)}) collective-permute-start(bf16[128,2304]{1,0:T(8,128)(2,1)S(1)} %get-tuple-element.114), channel_id=1, source_target_pairs={{0,1},{1,2},{2,3},{4,5},{5,6},{6,7},{8,9},{9,10},{10,11},{12,13},{... | collective-permute-start | bytes 1769480 | tf_op jit(solution)/shard_map/ppermute | solution.py:43
  323.9 14.2 %collective-permute-start.20 = (bf16[128,2304]{1,0:T(8,128)(2,1)S(1)}, bf16[128,2304]{1,0:T(8,128)(2,1)S(1)}, u32[]{:S(2)}, u32[]{:S(2)}) collective-permute-start(bf16[128,2304]{1,0:T(8,128)(2,1)S(1)} %get-tuple-element.114), channel_id=1, source_target_pairs={{1,0},{2,1},{3,2},{5,4},{6,5},{7,6},{9,8},{10,9},{11,10},{13,12},{... | collective-permute-start | bytes 1769480 | tf_op jit(solution)/shard_map/ppermute | solution.py:43
  339.6 13.8 %collective-permute-start.22 = (bf16[128,2304]{1,0:T(8,128)(2,1)S(1)}, bf16[128,2304]{1,0:T(8,128)(2,1)}, u32[]{:S(2)}, u32[]{:S(2)}) collective-permute-start(bf16[128,2304]{1,0:T(8,128)(2,1)S(1)} %collective-permute-done.20), channel_id=1, source_target_pairs={{1,0},{2,1},{5,4},{6,5},{9,8},{10,9},{13,12},{14,13},{17,16},{18,1... | collective-permute-start | bytes 1769480 | tf_op jit(solution)/shard_map/ppermute | solution.py:43
  353.3 12.0 %collective-permute-start.23 = (bf16[128,2304]{1,0:T(8,128)(2,1)}, bf16[128,2304]{1,0:T(8,128)(2,1)S(1)}, u32[]{:S(2)}, u32[]{:S(2)}) collective-permute-start(bf16[128,2304]{1,0:T(8,128)(2,1)} %collective-permute-done.21), channel_id=1, source_target_pairs={{2,3},{6,7},{10,11},{14,15},{18,19},{22,23},{26,27},{30,31}} | collective-permute-start | bytes 1769480 | tf_op jit(solution)/shard_map/ppermute | solution.py:43
  354.0 13.0 %collective-permute-start.24 = (bf16[128,2304]{1,0:T(8,128)(2,1)}, bf16[128,2304]{1,0:T(8,128)(2,1)S(1)}, u32[]{:S(2)}, u32[]{:S(2)}) collective-permute-start(bf16[128,2304]{1,0:T(8,128)(2,1)} %collective-permute-done.22), channel_id=1, source_target_pairs={{1,0},{5,4},{9,8},{13,12},{17,16},{21,20},{25,24},{29,28}} | collective-permute-start | bytes 1769480 | tf_op jit(solution)/shard_map/ppermute | solution.py:43
  373.9 17.0 %collective-permute-start.28 = (bf16[1152,2304]{1,0:T(8,128)(2,1)}, bf16[1152,2304]{1,0:T(8,128)(2,1)}, u32[]{:S(2)}, u32[]{:S(2)}) collective-permute-start(bf16[1152,2304]{1,0:T(8,128)(2,1)} %convolution_convert_fusion.1), channel_id=1, source_target_pairs={{0,8},{8,0},{16,24},{24,16},{1,9},{9,1},{17,25},{25,17},{2,10},{10... | collective-permute-start | bytes 15925256 | tf_op jit(solution)/shard_map/ppermute | solution.py:183
  415.3 30.3 %collective-permute-start.29 = (bf16[128,2304]{1,0:T(8,128)(2,1)S(1)}, bf16[128,2304]{1,0:T(8,128)(2,1)S(1)}, u32[]{:S(2)}, u32[]{:S(2)}) collective-permute-start(bf16[128,2304]{1,0:T(8,128)(2,1)S(1)} %get-tuple-element.82), channel_id=1, source_target_pairs={{0,2},{1,3},{2,0},{3,1},{4,6},{5,7},{6,4},{7,5},{8,10},{9,11},{10,... | collective-permute-start | bytes 1769480 | tf_op jit(solution)/shard_map/ppermute | solution.py:48
  415.4 30.2 %collective-permute-start.30 = (bf16[128,2304]{1,0:T(8,128)(2,1)S(1)}, bf16[128,2304]{1,0:T(8,128)(2,1)S(1)}, u32[]{:S(2)}, u32[]{:S(2)}) collective-permute-start(bf16[128,2304]{1,0:T(8,128)(2,1)S(1)} %get-tuple-element.83), channel_id=1, source_target_pairs={{0,3},{1,0},{2,1},{3,2},{4,7},{5,4},{6,5},{7,6},{8,11},{9,8},{10,9... | collective-permute-start | bytes 1769480 | tf_op jit(solution)/shard_map/ppermute | solution.py:48
  418.7 39.1 %collective-permute-start.31 = (bf16[128,2304]{1,0:T(8,128)(2,1)S(1)}, bf16[128,2304]{1,0:T(8,128)(2,1)S(1)}, u32[]{:S(2)}, u32[]{:S(2)}) collective-permute-start(bf16[128,2304]{1,0:T(8,128)(2,1)S(1)} %get-tuple-element.84), channel_id=1, source_target_pairs={{0,1},{1,2},{2,3},{3,0},{4,5},{5,6},{6,7},{7,4},{8,9},{9,10},{10,1... | collective-permute-start | bytes 1769480 | tf_op jit(solution)/shard_map/ppermute | solution.py:48
  461.1 39.1 %collective-permute-start.32 = (bf16[128,2304]{1,0:T(8,128)(2,1)S(1)}, bf16[128,2304]{1,0:T(8,128)(2,1)S(1)}, u32[]{:S(2)}, u32[]{:S(2)}) collective-permute-start(bf16[128,2304]{1,0:T(8,128)(2,1)S(1)} %get-tuple-element.104), channel_id=1, source_target_pairs={{0,1},{1,2},{2,3},{3,0},{4,5},{5,6},{6,7},{7,4},{8,9},{9,10},{10,1... | collective-permute-start | bytes 1769480 | tf_op jit(solution)/shard_map/ppermute | solution.py:48
  486.4 28.1 %collective-permute-start.33 = (bf16[128,2304]{1,0:T(8,128)(2,1)S(1)}, bf16[128,2304]{1,0:T(8,128)(2,1)S(1)}, u32[]{:S(2)}, u32[]{:S(2)}) collective-permute-start(bf16[128,2304]{1,0:T(8,128)(2,1)S(1)} %get-tuple-element.104), channel_id=1, source_target_pairs={{0,2},{1,3},{2,0},{3,1},{4,6},{5,7},{6,4},{7,5},{8,10},{9,11},{10,... | collective-permute-start | bytes 1769480 | tf_op jit(solution)/shard_map/ppermute | solution.py:48
  486.4 37.8 %collective-permute-start.34 = (bf16[128,2304]{1,0:T(8,128)(2,1)S(1)}, bf16[128,2304]{1,0:T(8,128)(2,1)S(1)}, u32[]{:S(2)}, u32[]{:S(2)}) collective-permute-start(bf16[128,2304]{1,0:T(8,128)(2,1)S(1)} %get-tuple-element.104), channel_id=1, source_target_pairs={{0,3},{1,0},{2,1},{3,2},{4,7},{5,4},{6,5},{7,6},{8,11},{9,8},{10,9... | collective-permute-start | bytes 1769480 | tf_op jit(solution)/shard_map/ppermute | solution.py:48
  525.1 30.2 %collective-permute-start.48 = (bf16[1152,512]{1,0:T(8,128)(2,1)S(1)}, bf16[1152,512]{1,0:T(8,128)(2,1)S(1)}, u32[]{:S(2)}, u32[]{:S(2)}) collective-permute-start(bf16[1152,512]{1,0:T(8,128)(2,1)S(1)} %convolution_convert_fusion.7), channel_id=1, source_target_pairs={{0,8},{8,0},{16,24},{24,16},{1,9},{9,1},{17,25},{25,17},{2,10},{10... | collective-permute-start | bytes 3538952 | tf_op jit(solution)/shard_map/ppermute | solution.py:183
  536.2 16.1 %collective-permute-start.35 = (bf16[512,512]{0,1:T(8,128)(2,1)S(1)}, bf16[512,512]{0,1:T(8,128)(2,1)S(1)}, u32[]{:S(2)}, u32[]{:S(2)}) collective-permute-start(bf16[512,512]{0,1:T(8,128)(2,1)S(1)} %fusion.81), channel_id=1, source_target_pairs={{4,0},{5,1},{6,2},{7,3},{12,8},{13,9},{14,10},{15,11},{20,16},{21,... | collective-permute-start | bytes 1572872 | tf_op jit(solution)/shard_map/ppermute | solution.py:19
  557.2 238.1 %reduce-scatter.5.cloned.1.call-start = ((), (), s32[]{:S(2)}) async-start(), calls=%async_computation.7 | async-start | bytes 2949120 | tf_op jit(solution)/shard_map/reduce_scatter | solution.py:192
  565.1 233.9 %reduce-scatter.11.cloned.1.call-start = ((), (), s32[]{:S(2)}) async-start(), calls=%async_computation.10 | async-start | bytes 6635520 | tf_op jit(solution)/shard_map/reduce_scatter | solution.py:192
  577.9 16.7 %collective-permute-start.49 = (bf16[1152,4608]{1,0:T(8,128)(2,1)}, bf16[1152,4608]{1,0:T(8,128)(2,1)}, u32[]{:S(2)}, u32[]{:S(2)}) collective-permute-start(bf16[1152,4608]{1,0:T(8,128)(2,1)} %convolution_convert_fusion), channel_id=1, source_target_pairs={{0,8},{8,0},{16,24},{24,16},{1,9},{9,1},{17,25},{25,17},{2,10},{10... | collective-permute-start | bytes 31850504 | tf_op jit(solution)/shard_map/ppermute | solution.py:183
  578.1 234.2 %reduce-scatter.9.cloned.1.call-start = ((), (), s32[]{:S(2)}) async-start(), calls=%async_computation.9 | async-start | bytes 13271040 | tf_op jit(solution)/shard_map/reduce_scatter | solution.py:192
  608.6 31.2 %collective-permute-start.25 = (bf16[128,2304]{1,0:T(8,128)(2,1)}, bf16[128,2304]{1,0:T(8,128)(2,1)S(1)}, u32[]{:S(2)}, u32[]{:S(2)}) collective-permute-start(bf16[128,2304]{1,0:T(8,128)(2,1)} %concatenate.64), channel_id=1, source_target_pairs={{0,1},{1,2},{2,3},{3,0},{4,5},{5,6},{6,7},{7,4},{8,9},{9,10},{10,1... | collective-permute-start | bytes 1769480 | tf_op jit(solution)/shard_map/ppermute | solution.py:48
  622.2 109.5 %collective-permute-start.26 = (bf16[128,2304]{1,0:T(8,128)(2,1)}, bf16[128,2304]{1,0:T(8,128)(2,1)}, u32[]{:S(2)}, u32[]{:S(2)}) collective-permute-start(bf16[128,2304]{1,0:T(8,128)(2,1)} %concatenate.64), channel_id=1, source_target_pairs={{0,2},{1,3},{2,0},{3,1},{4,6},{5,7},{6,4},{7,5},{8,10},{9,11},{10,... | collective-permute-start | bytes 1769480 | tf_op jit(solution)/shard_map/ppermute | solution.py:48
  625.8 110.0 %collective-permute-start.27 = (bf16[128,2304]{1,0:T(8,128)(2,1)}, bf16[128,2304]{1,0:T(8,128)(2,1)}, u32[]{:S(2)}, u32[]{:S(2)}) collective-permute-start(bf16[128,2304]{1,0:T(8,128)(2,1)} %concatenate.64), channel_id=1, source_target_pairs={{0,3},{1,0},{2,1},{3,2},{4,7},{5,4},{6,5},{7,6},{8,11},{9,8},{10,9... | collective-permute-start | bytes 1769480 | tf_op jit(solution)/shard_map/ppermute | solution.py:48
  632.7 82.4 %collective-permute-start.36 = (bf16[128,2304]{1,0:T(8,128)(2,1)S(1)}, bf16[128,2304]{1,0:T(8,128)(2,1)S(1)}, u32[]{:S(2)}, u32[]{:S(2)}) collective-permute-start(bf16[128,2304]{1,0:T(8,128)(2,1)S(1)} %get-tuple-element.86), channel_id=1, source_target_pairs={{0,2},{1,3},{2,0},{3,1},{4,6},{5,7},{6,4},{7,5},{8,10},{9,11},{10,... | collective-permute-start | bytes 1769480 | tf_op jit(solution)/shard_map/ppermute | solution.py:48
  634.3 80.8 %collective-permute-start.37 = (bf16[128,2304]{1,0:T(8,128)(2,1)S(1)}, bf16[128,2304]{1,0:T(8,128)(2,1)S(1)}, u32[]{:S(2)}, u32[]{:S(2)}) collective-permute-start(bf16[128,2304]{1,0:T(8,128)(2,1)S(1)} %get-tuple-element.87), channel_id=1, source_target_pairs={{0,3},{1,0},{2,1},{3,2},{4,7},{5,4},{6,5},{7,6},{8,11},{9,8},{10,9... | collective-permute-start | bytes 1769480 | tf_op jit(solution)/shard_map/ppermute | solution.py:48
  639.8 75.4 %collective-permute-start.38 = (bf16[128,2304]{1,0:T(8,128)(2,1)S(1)}, bf16[128,2304]{1,0:T(8,128)(2,1)S(1)}, u32[]{:S(2)}, u32[]{:S(2)}) collective-permute-start(bf16[128,2304]{1,0:T(8,128)(2,1)S(1)} %get-tuple-element.88), channel_id=1, source_target_pairs={{0,1},{1,2},{2,3},{3,0},{4,5},{5,6},{6,7},{7,4},{8,9},{9,10},{10,1... | collective-permute-start | bytes 1769480 | tf_op jit(solution)/shard_map/ppermute | solution.py:48
  718.6 15.3 %collective-permute-start.43 = (f32[4,2304]{1,0:T(4,128)}, f32[4,2304]{1,0:T(4,128)S(1)}, u32[]{:S(2)}, u32[]{:S(2)}) collective-permute-start(f32[4,2304]{1,0:T(4,128)} %concatenate.71), channel_id=1, source_target_pairs={{0,1},{1,0},{2,3},{3,2},{4,5},{5,4},{6,7},{7,6},{8,9},{9,8},{10,11... | collective-permute-start | bytes 110600 | tf_op jit(solution)/shard_map/ppermute | solution.py:127
  751.8 18.1 %collective-permute-start.40 = (bf16[128,2304]{1,0:T(8,128)(2,1)S(1)}, bf16[128,2304]{1,0:T(8,128)(2,1)S(1)}, u32[]{:S(2)}, u32[]{:S(2)}) collective-permute-start(bf16[128,2304]{1,0:T(8,128)(2,1)S(1)} %concatenate.70), channel_id=1, source_target_pairs={{0,1},{1,2},{2,3},{3,0},{4,5},{5,6},{6,7},{7,4},{8,9},{9,10},{10,1... | collective-permute-start | bytes 1769480 | tf_op jit(solution)/shard_map/ppermute | solution.py:48
  753.6 39.5 %collective-permute-start.41 = (bf16[128,2304]{1,0:T(8,128)(2,1)S(1)}, bf16[128,2304]{1,0:T(8,128)(2,1)S(1)}, u32[]{:S(2)}, u32[]{:S(2)}) collective-permute-start(bf16[128,2304]{1,0:T(8,128)(2,1)S(1)} %concatenate.70), channel_id=1, source_target_pairs={{0,2},{1,3},{2,0},{3,1},{4,6},{5,7},{6,4},{7,5},{8,10},{9,11},{10,... | collective-permute-start | bytes 1769480 | tf_op jit(solution)/shard_map/ppermute | solution.py:48
  753.6 39.5 %collective-permute-start.42 = (bf16[128,2304]{1,0:T(8,128)(2,1)S(1)}, bf16[128,2304]{1,0:T(8,128)(2,1)S(1)}, u32[]{:S(2)}, u32[]{:S(2)}) collective-permute-start(bf16[128,2304]{1,0:T(8,128)(2,1)S(1)} %concatenate.70), channel_id=1, source_target_pairs={{0,3},{1,0},{2,1},{3,2},{4,7},{5,4},{6,5},{7,6},{8,11},{9,8},{10,9... | collective-permute-start | bytes 1769480 | tf_op jit(solution)/shard_map/ppermute | solution.py:48
  (86 other events, 1484.5 us)
Sparse Core Ops, SparseCore 0:
  10.5 51.4 all-gather.3
  64.4 116.1 all-gather.5
  182.5 63.6 all-gather.7
  557.3 40.7 reduce-scatter.6
  601.6 37.3 reduce-scatter.4
  641.9 61.8 reduce-scatter.10
  706.9 105.3 reduce-scatter.8

commit v6 on v5

--- a/solution.py
+++ b/solution.py
@@ -6,6 +6,8 @@
 
 
 HD = 256
+BLOCK_TOKENS = 128
+MAX_DOC_BLOCKS = 4
 CAP = 50.0
 EPS = 1e-06
 ROWS = ("fsdp", "ctx")
@@ -167,6 +169,31 @@
     return lax.all_gather(
         weight, ROWS, axis=0, tiled=True, axis_index_groups=[first + second]
     )
+
+
+def sent_rows(weight, after=()):
+    ranks = lax.axis_size("fsdp") * lax.axis_size("ctx")
+    if (lax.axis_size("fsdp"), lax.axis_size("ctx")) != (4, 2):
+        return gather_rows(weight), ()
+    core, pair, width = 2, 4, 1
+
+    def sent(block, bits):
+        return lax.ppermute(block, ROWS, [(r, r ^ bits) for r in range(ranks)])
+
+    weight, after = lax.optimization_barrier((weight, after))
+    held = {0: weight}
+    for bits in (pair | width, width, pair):
+        held[bits] = sent(weight, bits)
+    for bits in (0, width, pair, pair | width):
+        held[bits | core] = sent(held[bits], core)
+    place = {0: 0, width: 1, pair: 2, core: 4}
+    rank = lax.axis_index("fsdp") * 2 + lax.axis_index("ctx")
+    own = (rank // core) % 2 * 4 + rank // pair * 2 + rank % 2
+    whole = jnp.zeros((ranks,) + weight.shape, weight.dtype)
+    for bits in held:
+        at = own ^ (place[bits & width] | place[bits & pair] | place[bits & core])
+        whole = lax.dynamic_update_index_in_dim(whole, held[bits], at, 0)
+    return whole.reshape(-1, weight.shape[1]), (held[pair | width],)
 
 
 def rows_of_core(left, core):
@@ -222,23 +249,23 @@
     tp_rank = lax.axis_index("tp")
     piece = length // tp_size
 
-    attention_full = gather_rows(
-        jnp.concatenate([query_weight, key_weight, value_weight, output_weight], axis=1)
-    )
+    qkv_full, first_sent = sent_rows(
+        jnp.concatenate([query_weight, key_weight, value_weight], axis=1)
+    )
+    output_full, _ = sent_rows(output_weight, first_sent)
     gate_up_full = gather_rows(jnp.concatenate([gate_weight, up_weight], axis=1))
     down_full = gather_rows(down_weight)
-    qkv_full = attention_full[:, :qkv_width]
-    output_full = attention_full[:, qkv_width:]
 
     position = lax.axis_index("ctx")
     own_ids = lax.dynamic_slice_in_dim(segment_ids, position * length, length)
-    prev_start = jnp.maximum(position - 1, 0) * length
+    before = min(length, (MAX_DOC_BLOCKS - 1) * BLOCK_TOKENS)
+    prev_start = jnp.maximum(position * length - before, 0)
     prev_ids = jnp.where(
-        position > 0, lax.dynamic_slice_in_dim(segment_ids, prev_start, length), -2
+        position > 0, lax.dynamic_slice_in_dim(segment_ids, prev_start, before), -2
     )
     key_ids = jnp.concatenate([prev_ids, own_ids])
     query_pos = jnp.arange(length, dtype=jnp.int32)
-    key_pos = jnp.arange(2 * length, dtype=jnp.int32) - length
+    key_pos = jnp.arange(before + length, dtype=jnp.int32) - before
     allowed = (query_pos[:, None] == key_pos[None, :]) | (own_ids[:, None] == key_ids[None, :]) & (
         own_ids[:, None] >= 0
     ) & (key_pos[None, :] < query_pos[:, None])
@@ -262,9 +289,9 @@
     qkv_low = product(normed_one, qkv_full).astype(LOW)
     queries = qkv_low[:, :heads_width].reshape(length, kv_heads, repeats, HD)
     kv_low = qkv_low[:, heads_width:]
-    kv_all = jnp.concatenate([passed_along(kv_low, "ctx", 1), kv_low], axis=0)
-    keys_all = kv_all[:, :kv_width].reshape(2 * length, kv_heads, HD)
-    values_all = kv_all[:, kv_width:].reshape(2 * length, kv_heads, HD)
+    kv_all = jnp.concatenate([passed_along(kv_low[-before:], "ctx", 1), kv_low], axis=0)
+    keys_all = kv_all[:, :kv_width].reshape(before + length, kv_heads, HD)
+    values_all = kv_all[:, kv_width:].reshape(before + length, kv_heads, HD)
     scores, powers = attention_scores(queries, keys_all, allowed, scaling)
     totals = jnp.sum(powers, axis=-1, keepdims=True)
     probs_low = (powers / totals).astype(LOW)
@@ -291,27 +318,20 @@
     grad_branch_two, grad_gain_four = pull_four(upstream)
     grad_two_low = jnp.concatenate(gathered(grad_branch_two.astype(LOW)), axis=0)
 
-    result_low, grad_two_low = lax.optimization_barrier(
-        (by_chip(result.astype(LOW)), grad_two_low)
-    )
     down_sent, grad_two_low = lax.optimization_barrier(
         (sent_to_core(grad_two_low, hidden_low), grad_two_low)
     )
     down_arrived = over_cores(down_sent)
-    outputs = in_order(sent_gathered(result_low))
     _, pull_glu = jax.vjp(geglu, gate_value, up_value)
     grad_gate, grad_up = pull_glu(product(grad_two_low, down_full))
     grad_gate_up = jnp.concatenate([grad_gate.astype(LOW), grad_up.astype(LOW)], axis=1)
-    grad_down_low, grad_gate_up = lax.optimization_barrier(
-        (chip_rows(grad_two_low, hidden_low, down_arrived), grad_gate_up)
-    )
-    down_share = share_rows(grad_down_low)
     grad_normed_two = transposed_product(grad_gate_up, gate_up_full).astype(LOW)
     grad_normed_two = sent_scattered(turned_blocks(grad_normed_two))
+    grad_down_low = chip_rows(grad_two_low, hidden_low, down_arrived)
+    down_share = share_rows(grad_down_low)
     gate_up_sent = sent_to_core(normed_two, grad_gate_up)
     gate_up_arrived = over_cores(gate_up_sent)
     grad_gate_up_low = chip_rows(normed_two, grad_gate_up, gate_up_arrived)
-
     gate_up_share = share_rows(grad_gate_up_low)
 
     _, pull_three = jax.vjp(rms, middle, pre_feedforward_gain)
@@ -320,13 +340,16 @@
     _, pull_two = jax.vjp(rms, branch_one, post_attention_gain)
     grad_branch_one, grad_gain_two = pull_two(grad_middle)
     grad_one_low = in_order(sent_gathered(grad_branch_one.astype(LOW)))
+    result_low, grad_one_low = lax.optimization_barrier(
+        (by_chip(result.astype(LOW)), grad_one_low)
+    )
+    outputs = in_order(sent_gathered(result_low))
 
     output_sent = sent_to_core(grad_one_low, attended_low)
     output_arrived = over_cores(output_sent)
     output_share = share_rows(chip_rows(grad_one_low, attended_low, output_arrived))
-    grad_attended = (
-        product(grad_one_low, output_full).astype(LOW).reshape(length, kv_heads, repeats, HD)
-    )
+    grad_attended = product(grad_one_low, output_full).astype(LOW)
+    grad_attended = grad_attended.reshape(length, kv_heads, repeats, HD)
     probs = powers / totals
     grad_probs = jnp.einsum(
         "qgrd,kgd->grqk", grad_attended, values_all, preferred_element_type=F32
@@ -345,13 +368,14 @@
     )
     grad_keys_all = (
         jnp.einsum("grqk,qgrd->kgd", grad_scores, queries, preferred_element_type=F32) * scaling
-    ).reshape(2 * length, -1)
+    ).reshape(before + length, -1)
     grad_values_all = jnp.einsum(
         "grqk,qgrd->kgd", probs_low, grad_attended, preferred_element_type=F32
-    ).reshape(2 * length, -1)
+    ).reshape(before + length, -1)
     grad_kv_all = jnp.concatenate([grad_keys_all, grad_values_all], axis=1)
-    grad_kv_back = passed_along(grad_kv_all[:length].astype(LOW), "ctx", -1).astype(F32)
-    grad_kv_low = (grad_kv_all[length:] + grad_kv_back).astype(LOW)
+    grad_kv_back = passed_along(grad_kv_all[:before].astype(LOW), "ctx", -1)
+    grad_kv_back = jnp.pad(grad_kv_back, ((length - before, 0), (0, 0))).astype(F32)
+    grad_kv_low = (grad_kv_all[before:] + grad_kv_back).astype(LOW)
     grad_qkv = jnp.concatenate([grad_query_low, grad_kv_low], axis=1)
     grad_normed_one = transposed_product(grad_qkv, qkv_full).astype(LOW)
     grad_normed_one = sent_scattered(ordered_blocks(grad_normed_one))
@@ -362,15 +386,13 @@
 
     _, pull_one = jax.vjp(rms, inputs, pre_attention_gain)
     grad_inputs_norm, grad_gain_one = pull_one(grad_normed_one)
-    grad_inputs_own, grad_qkv_low = lax.optimization_barrier(
-        (by_chip((grad_middle + grad_inputs_norm).astype(LOW)), grad_qkv_low)
-    )
-    grad_inputs = in_order(sent_gathered(grad_inputs_own))
+    grad_inputs_low = by_chip((grad_middle + grad_inputs_norm).astype(LOW))
+    grad_inputs = in_order(sent_gathered(grad_inputs_low))
 
     gains = by_chip(jnp.stack([grad_gain_one, grad_gain_two, grad_gain_three, grad_gain_four]))
     for axis in ("tp",) + ROWS:
         gains = summed(gains, axis)
-    share = attention_full.shape[0] // (lax.axis_size("fsdp") * lax.axis_size("ctx"))
+    share = qkv_full.shape[0] // (lax.axis_size("fsdp") * lax.axis_size("ctx"))
     row_rank = lax.axis_index("fsdp") * lax.axis_size("ctx") + lax.axis_index("ctx")
     gain_shares = lax.dynamic_slice_in_dim(gains, row_rank * share, share, axis=1)
     edges = [0, heads_width, heads_width + kv_width, qkv_width]

time: 834 us -> 788 us (0.945)
  waiting for transfers between devices: 435 us -> 395 us
  local copies, waits for them, and re-layouts: 48.6 us -> 78.6 us
  starting transfers between devices: 143 us -> 119 us
    all_gather x3 -> x2, waiting for transfers between devices: 60.2 us -> 0.02 us  [gather_rows(): lax.all_gather(weight, ROWS, axis=0, tiled=True, axis_index_groups=[first...]
    ppermute x0 -> x14, waiting for transfers between devices: none -> 35.7 us  [sent(): return lax.ppermute(block, ROWS, [(r, r ^ bits) for r in range(ranks)])]
    dynamic_update_slice x0 -> x16, local copies, waits for them, and re-layouts: none -> 24.1 us  [sent_rows(): whole = lax.dynamic_update_index_in_dim(whole, held[bits], at, 0)]
    ppermute x15, starting transfers between devices: 57.3 us -> 37.5 us  [shift(): lax.ppermute(block, 'tp', [(i, (i + distance) % size) for i in range(size)])]
    ppermute x15, waiting for transfers between devices: 189 us -> 174 us  [shift(): lax.ppermute(block, 'tp', [(i, (i + distance) % size) for i in range(size)])]
    ppermute x24, starting transfers between devices: 64.2 us -> 50.6 us  [onward(): return lax.ppermute(block, 'tp', [(i, i + distance) for i in senders])]
    ppermute x24, waiting for transfers between devices: 113 us -> 124 us  [onward(): return lax.ppermute(block, 'tp', [(i, i + distance) for i in senders])]
    ppermute x0 -> x14, starting transfers between devices: none -> 9.44 us  [sent(): return lax.ppermute(block, ROWS, [(r, r ^ bits) for r in range(ranks)])]
  transfers between devices with their start and end apart: 57 -> 70, of which waited for: 37 -> 36; matrix products, arithmetic and copies ran while one was open for 20% -> 22% of each run, Pallas kernels for 0% -> 0%
where the time goes in v6:
time: 788 us; the launch traced here: 779 us
  waiting for transfers between devices  395 us (50%)
  matrix products  128 us (16%)
  starting transfers between devices  119 us (15%)
  local copies, waits for them, and re-layouts  78.6 us (10%)
  other arithmetic  42.7 us (5%)
  between operations  15.9 us (2%)
    ppermute x15, waiting for transfers between devices, shift(): lax.ppermute(block, 'tp', [(i, (i + distance) % size) for i in range(size)])  174 us
    ppermute x24, waiting for transfers between devices, onward(): return lax.ppermute(block, 'tp', [(i, i + distance) for i in senders])  124 us
    ppermute x24, starting transfers between devices, onward(): return lax.ppermute(block, 'tp', [(i, i + distance) for i in senders])  50.6 us
    dot_general x8, matrix products, rows_product(): lax.dot_general(left, right, (((0,), (0,)), ((), ())), preferred_element_...  49.4 us
    ppermute x15, starting transfers between devices, shift(): lax.ppermute(block, 'tp', [(i, (i + distance) % size) for i in range(size)])  37.5 us
    dot_general x4, matrix products, product(): return jnp.dot(left, right, preferred_element_type=F32)  36 us
    ppermute x14, waiting for transfers between devices, sent(): return lax.ppermute(block, ROWS, [(r, r ^ bits) for r in range(ranks)])  35.7 us
    dot_general x4, matrix products, transposed_product(): lax.dot_general(left, right, (((1,), (1,)), ((), ())), preferred_element_...  33.7 us
  transfers between devices with their start and end apart: 70, of which 36 were waited for; matrix products, arithmetic and copies ran while one was open for 22% of the time, Pallas kernels for 0%

profile of v6, /device:TPU:0, one launch (start us, length us, event | category | flops | bytes accessed | tf_op | source)
XLA Modules:
  0.0 779.5 jit_solution(15548135769788527022)
XLA Ops:
  32.7 4.6 collective-permute-done
  42.6 20.0 %collective-permute-done.1 = bf16[288,1024]{1,0:T(8,128)(2,1)} collective-permute-done((bf16[288,1024]{1,0:T(8,128)(2,1)}, bf16[288,1024]{1,0:T(8,128)(2,1)}, u32[]{:S(2)}, u32[]{:S(2)}) %collective-permute-start.1) | collective-permute-done | bytes 589856 | tf_op jit(solution)/shard_map/ppermute | solution.py:181
  76.8 7.4 collective-permute-done.9
  92.1 6.4 convolution_convert_fusion.8
  109.1 12.6 %collective-permute-done.7 = bf16[384,512]{1,0:T(8,128)(2,1)S(1)} collective-permute-done((bf16[384,512]{1,0:T(8,128)(2,1)}, bf16[384,512]{1,0:T(8,128)(2,1)S(1)}, u32[]{:S(2)}, u32[]{:S(2)}) %collective-permute-start.7) | collective-permute-done | bytes 393248 | tf_op jit(solution)/shard_map/ppermute | solution.py:21
  131.3 4.3 collective-permute-start.15
  137.1 9.6 %collective-permute-done.15 = bf16[128,2304]{1,0:T(8,128)(2,1)} collective-permute-done((bf16[128,2304]{1,0:T(8,128)(2,1)S(1)}, bf16[128,2304]{1,0:T(8,128)(2,1)}, u32[]{:S(2)}, u32[]{:S(2)}) %collective-permute-start.15) | collective-permute-done | bytes 589856 | tf_op jit(solution)/shard_map/ppermute | solution.py:45
  149.1 5.1 collective-permute-start.17
  155.2 10.1 %collective-permute-done.17 = bf16[128,2304]{1,0:T(8,128)(2,1)S(1)} collective-permute-done((bf16[128,2304]{1,0:T(8,128)(2,1)S(1)}, bf16[128,2304]{1,0:T(8,128)(2,1)S(1)}, u32[]{:S(2)}, u32[]{:S(2)}) %collective-permute-start.17) | collective-permute-done | bytes 589856 | tf_op jit(solution)/shard_map/ppermute | solution.py:45
  165.4 5.6 collective-permute-start.19
  176.7 4.6 collective-permute-done.19
  181.3 5.1 collective-permute-done.20
  195.0 7.8 collective-permute-done.21
  208.9 11.9 %collective-permute-done.24 = bf16[128,2304]{1,0:T(8,128)(2,1)} collective-permute-done((bf16[128,2304]{1,0:T(8,128)(2,1)S(1)}, bf16[128,2304]{1,0:T(8,128)(2,1)}, u32[]{:S(2)}, u32[]{:S(2)}) %collective-permute-start.24) | collective-permute-done | bytes 589856 | tf_op jit(solution)/shard_map/ppermute | solution.py:45
  224.2 9.7 %collective-permute-done.26 = bf16[128,2304]{1,0:T(8,128)(2,1)S(1)} collective-permute-done((bf16[128,2304]{1,0:T(8,128)(2,1)}, bf16[128,2304]{1,0:T(8,128)(2,1)S(1)}, u32[]{:S(2)}, u32[]{:S(2)}) %collective-permute-start.26) | collective-permute-done | bytes 589856 | tf_op jit(solution)/shard_map/ppermute | solution.py:45
  234.1 14.8 %fusion.104 = f32[512,4608]{1,0:T(8,128)S(1)} fusion(bf16[2304,4608]{1,0:T(8,128)(2,1)} %all-gather.3.cloned.1.call-done, bf16[128,2304]{1,0:T(8,128)(2,1)S(1)} %broadcast_select_fusion.1, bf16[128,2304]{1,0:T(8,128)(2,1)S(1)} %broadcast_select_fusion.3, bf16[128,2304]{1,0:T(8,128)(2,1)S(1)} %broadcast_select_fusion.5, ...), kind=kOutput, calls=%fused_computation.224 | convolution fusion | flops 10881073152 | bytes 33030144 | tf_op jit(solution)/shard_map/dot_general | solution.py:33
  255.2 10.3 %convolution_convert_fusion.4 = bf16[512,2304]{1,0:T(8,128)(2,1)S(1)} fusion(bf16[512,2304]{1,0:T(8,128)(2,1)} %multiply_convert_fusion.1, bf16[2304,2304]{1,0:T(8,128)(2,1)} %all-gather.5.cloned.1.call-done), kind=kOutput, calls=%fused_computation.24 | convolution fusion | flops 5436997632 | bytes 15335424 | tf_op jit(solution)/shard_map/dot_general | solution.py:41
  267.9 8.8 %collective-permute-done.27 = bf16[128,2304]{1,0:T(8,128)(2,1)S(1)} collective-permute-done((bf16[128,2304]{1,0:T(8,128)(2,1)S(1)}, bf16[128,2304]{1,0:T(8,128)(2,1)S(1)}, u32[]{:S(2)}, u32[]{:S(2)}) %collective-permute-start.27) | collective-permute-done | bytes 589856 | tf_op jit(solution)/shard_map/ppermute | solution.py:45
  277.0 4.4 collective-permute-start.29
  282.1 8.7 %collective-permute-done.29 = bf16[128,2304]{1,0:T(8,128)(2,1)S(1)} collective-permute-done((bf16[128,2304]{1,0:T(8,128)(2,1)S(1)}, bf16[128,2304]{1,0:T(8,128)(2,1)S(1)}, u32[]{:S(2)}, u32[]{:S(2)}) %collective-permute-start.29) | collective-permute-done | bytes 589856 | tf_op jit(solution)/shard_map/ppermute | solution.py:45
  292.1 7.1 collective-permute-start.31
  321.0 6.0 collective-permute-done.33
  327.1 9.3 %collective-permute-done.34 = bf16[128,2304]{1,0:T(8,128)(2,1)S(1)} collective-permute-done((bf16[128,2304]{1,0:T(8,128)(2,1)S(1)}, bf16[128,2304]{1,0:T(8,128)(2,1)S(1)}, u32[]{:S(2)}, u32[]{:S(2)}) %collective-permute-start.34) | collective-permute-done | bytes 589856 | tf_op jit(solution)/shard_map/ppermute | solution.py:45
  338.4 14.5 %collective-permute-done.36 = bf16[128,2304]{1,0:T(8,128)(2,1)S(1)} collective-permute-done((bf16[128,2304]{1,0:T(8,128)(2,1)S(1)}, bf16[128,2304]{1,0:T(8,128)(2,1)S(1)}, u32[]{:S(2)}, u32[]{:S(2)}) %collective-permute-start.36) | collective-permute-done | bytes 589856 | tf_op jit(solution)/shard_map/ppermute | solution.py:45
  355.4 10.0 %collective-permute-done.38 = bf16[128,2304]{1,0:T(8,128)(2,1)S(1)} collective-permute-done((bf16[128,2304]{1,0:T(8,128)(2,1)S(1)}, bf16[128,2304]{1,0:T(8,128)(2,1)S(1)}, u32[]{:S(2)}, u32[]{:S(2)}) %collective-permute-start.38) | collective-permute-done | bytes 589856 | tf_op jit(solution)/shard_map/ppermute | solution.py:45
  367.1 5.1 convolution_convert_fusion.1
  372.2 11.6 %fusion.9 = (bf16[512,2304]{1,0:T(8,128)(2,1)S(1)}, bf16[512,2304]{1,0:T(8,128)(2,1)S(1)}) fusion(f32[512,4608]{1,0:T(8,128)S(1)} %bitcast.204, bf16[512,2304]{1,0:T(8,128)(2,1)S(1)} %pad_maximum_fusion.3, bf16[2304,2304]{1,0:T(8,128)(2,1)} %all-gather.5.cloned.1.call-done), kind=kOutput, calls=%fused_computation.17 | convolution fusion | flops 5464129536 | bytes 27131904 | tf_op jit(solution)/shard_map/dot_general | solution.py:33
  385.3 14.7 %convolution_convert_fusion.3 = bf16[512,2304]{1,0:T(8,128)(2,1)S(1)} fusion(bf16[2304,4608]{1,0:T(8,128)(2,1)} %all-gather.3.cloned.1.call-done, bf16[512,2304]{1,0:T(8,128)(2,1)S(1)} %get-tuple-element.109, bf16[512,2304]{1,0:T(8,128)(2,1)S(1)} %get-tuple-element.108), kind=kOutput, calls=%fused_computation.23 | convolution fusion | flops 10882252800 | bytes 28311552 | tf_op jit(solution)/shard_map/dot_general | solution.py:41
  402.4 36.3 %collective-permute-done.39 = bf16[128,2304]{1,0:T(8,128)(2,1)S(1)} collective-permute-done((bf16[128,2304]{1,0:T(8,128)(2,1)S(1)}, bf16[128,2304]{1,0:T(8,128)(2,1)S(1)}, u32[]{:S(2)}, u32[]{:S(2)}) %collective-permute-start.39) | collective-permute-done | bytes 589856 | tf_op jit(solution)/shard_map/ppermute | solution.py:50
  442.9 6.9 collective-permute-start.42
  453.9 9.9 %collective-permute-done.42 = bf16[128,2304]{1,0:T(8,128)(2,1)} collective-permute-done((bf16[128,2304]{1,0:T(8,128)(2,1)}, bf16[128,2304]{1,0:T(8,128)(2,1)}, u32[]{:S(2)}, u32[]{:S(2)}) %collective-permute-start.42) | collective-permute-done | bytes 589856 | tf_op jit(solution)/shard_map/ppermute | solution.py:50
  464.9 14.8 %collective-permute-done.43 = bf16[128,2304]{1,0:T(8,128)(2,1)S(1)} collective-permute-done((bf16[128,2304]{1,0:T(8,128)(2,1)}, bf16[128,2304]{1,0:T(8,128)(2,1)S(1)}, u32[]{:S(2)}, u32[]{:S(2)}) %collective-permute-start.43) | collective-permute-done | bytes 589856 | tf_op jit(solution)/shard_map/ppermute | solution.py:50
  494.8 12.2 %collective-permute-done.48 = bf16[384,512]{0,1:T(8,128)(2,1)S(1)} collective-permute-done((bf16[384,512]{0,1:T(8,128)(2,1)S(1)}, bf16[384,512]{0,1:T(8,128)(2,1)S(1)}, u32[]{:S(2)}, u32[]{:S(2)}) %collective-permute-start.48) | collective-permute-done | bytes 393248 | tf_op jit(solution)/shard_map/ppermute | solution.py:21
  514.9 4.7 add_convert_fusion.2
  521.3 11.2 %convolution_convert_fusion = bf16[1152,4608]{1,0:T(8,128)(2,1)} fusion(bf16[512,2304]{1,0:T(8,128)(2,1)} %copy-done.80, bf16[512,2304]{1,0:T(8,128)(2,1)} %copy-done.79, bf16[512,2304]{1,0:T(8,128)(2,1)S(1)} %pad_maximum_fusion.2, s32[]{:T(128)S(6)} %select_n.256), kind=kOutput, calls=%fused_computation.1 | convolution fusion | flops 5450563584 | bytes 16515076 | tf_op jit(solution)/shard_map/dot_general | solution.py:37
  532.7 6.8 add_convert_fusion.1
  539.6 9.6 %collective-permute-done.62 = bf16[1152,4608]{1,0:T(8,128)(2,1)} collective-permute-done((bf16[1152,4608]{1,0:T(8,128)(2,1)}, bf16[1152,4608]{1,0:T(8,128)(2,1)}, u32[]{:S(2)}, u32[]{:S(2)}) %collective-permute-start.62) | collective-permute-done | bytes 10616864 | tf_op jit(solution)/shard_map/ppermute | solution.py:210
  549.2 13.3 %add_convert_fusion = bf16[1152,4608]{1,0:T(8,128)(2,1)} fusion(bf16[1152,4608]{1,0:T(8,128)(2,1)} %collective-permute-done.62, bf16[512,2304]{1,0:T(8,128)(2,1)} %copy-done.80, bf16[512,2304]{1,0:T(8,128)(2,1)} %copy-done.79, bf16[512,2304]{1,0:T(8,128)(2,1)S(1)} %copy-done.35, s32[]{:T(128)S(6)} %select_n.258), kind=kOutput, calls=%fused_computation | convolution fusion | flops 5461180416 | bytes 27131908 | tf_op jit(solution)/shard_map/dot_general | solution.py:37
  563.3 13.3 %collective-permute-start.45 = (bf16[128,2304]{1,0:T(8,128)(2,1)}, bf16[128,2304]{1,0:T(8,128)(2,1)S(1)}, u32[]{:S(2)}, u32[]{:S(2)}) collective-permute-start(bf16[128,2304]{1,0:T(8,128)(2,1)} %concatenate.64), channel_id=1, source_target_pairs={{0,1},{1,2},{2,3},{3,0},{4,5},{5,6},{6,7},{7,4},{8,9},{9,10},{10,1... | collective-permute-start | bytes 1769480 | tf_op jit(solution)/shard_map/ppermute | solution.py:50
  581.6 5.3 convolution_convert_fusion.2
  594.3 25.2 %collective-permute-done.46 = bf16[128,2304]{1,0:T(8,128)(2,1)S(1)} collective-permute-done((bf16[128,2304]{1,0:T(8,128)(2,1)}, bf16[128,2304]{1,0:T(8,128)(2,1)S(1)}, u32[]{:S(2)}, u32[]{:S(2)}) %collective-permute-start.46) | collective-permute-done | bytes 589856 | tf_op jit(solution)/shard_map/ppermute | solution.py:50
  619.6 50.3 %collective-permute-done.49 = bf16[128,2304]{1,0:T(8,128)(2,1)S(1)} collective-permute-done((bf16[128,2304]{1,0:T(8,128)(2,1)S(1)}, bf16[128,2304]{1,0:T(8,128)(2,1)S(1)}, u32[]{:S(2)}, u32[]{:S(2)}) %collective-permute-start.49) | collective-permute-done | bytes 589856 | tf_op jit(solution)/shard_map/ppermute | solution.py:50
  673.4 13.2 %collective-permute-start.55 = (f32[4,2304]{1,0:T(4,128)}, f32[4,2304]{1,0:T(4,128)S(1)}, u32[]{:S(2)}, u32[]{:S(2)}) collective-permute-start(f32[4,2304]{1,0:T(4,128)} %concatenate.71), channel_id=1, source_target_pairs={{0,1},{1,0},{2,3},{3,2},{4,5},{5,4},{6,7},{7,6},{8,9},{9,8},{10,11... | collective-permute-start | bytes 110600 | tf_op jit(solution)/shard_map/ppermute | solution.py:129
  702.6 4.5 collective-permute-done.59
  707.8 8.5 %collective-permute-done.52 = bf16[128,2304]{1,0:T(8,128)(2,1)S(1)} collective-permute-done((bf16[128,2304]{1,0:T(8,128)(2,1)S(1)}, bf16[128,2304]{1,0:T(8,128)(2,1)S(1)}, u32[]{:S(2)}, u32[]{:S(2)}) %collective-permute-start.52) | collective-permute-done | bytes 589856 | tf_op jit(solution)/shard_map/ppermute | solution.py:50
  716.4 24.3 %collective-permute-done.53 = bf16[128,2304]{1,0:T(8,128)(2,1)S(1)} collective-permute-done((bf16[128,2304]{1,0:T(8,128)(2,1)S(1)}, bf16[128,2304]{1,0:T(8,128)(2,1)S(1)}, u32[]{:S(2)}, u32[]{:S(2)}) %collective-permute-start.53) | collective-permute-done | bytes 589856 | tf_op jit(solution)/shard_map/ppermute | solution.py:50
  749.7 18.2 %reduce-scatter.9.cloned.1.call-done = bf16[288,4608]{1,0:T(8,128)(2,1)} async-done(((bf16[1152,4608]{1,0:T(8,128)(2,1)}), bf16[288,4608]{1,0:T(8,128)(2,1)}) %reduce-scatter.9.cloned.1.call-update) | async-done | bytes 2654224 | tf_op jit(solution)/shard_map/reduce_scatter | solution.py:219
  767.9 4.5 fusion.106
  (407 shorter events, 220.3 us)
Async XLA Ops:
  7.2 226.9 %all-gather.3.cloned.1.call-start = ((), (), s32[]{:S(2)}) async-start(), calls=%async_computation.4 | async-start | bytes 23887872 | tf_op jit(solution)/shard_map/all_gather | solution.py:169
  10.7 244.5 %all-gather.5.cloned.1.call-start = ((), (), s32[]{:S(2)}) async-start(), calls=%async_computation.5 | async-start | bytes 11943936 | tf_op jit(solution)/shard_map/all_gather | solution.py:169
  12.6 24.7 %collective-permute-start = (bf16[288,1024]{1,0:T(8,128)(2,1)}, bf16[288,1024]{1,0:T(8,128)(2,1)}, u32[]{:S(2)}, u32[]{:S(2)}) collective-permute-start(bf16[288,1024]{1,0:T(8,128)(2,1)} %pad_maximum_fusion.11), channel_id=1, source_target_pairs={{0,20},{4,16},{8,28},{12,24},{16,4},{20,0},{24,12},{28,8},{1,21},{... | collective-permute-start | bytes 1769480 | tf_op jit(solution)/shard_map/ppermute | solution.py:181
  16.5 46.1 %collective-permute-start.1 = (bf16[288,1024]{1,0:T(8,128)(2,1)}, bf16[288,1024]{1,0:T(8,128)(2,1)}, u32[]{:S(2)}, u32[]{:S(2)}) collective-permute-start(bf16[288,1024]{1,0:T(8,128)(2,1)} %pad_maximum_fusion.11), channel_id=1, source_target_pairs={{0,4},{4,0},{8,12},{12,8},{16,20},{20,16},{24,28},{28,24},{1,5},{5... | collective-permute-start | bytes 1769480 | tf_op jit(solution)/shard_map/ppermute | solution.py:181
  17.0 47.5 %collective-permute-start.2 = (bf16[288,1024]{1,0:T(8,128)(2,1)}, bf16[288,1024]{1,0:T(8,128)(2,1)}, u32[]{:S(2)}, u32[]{:S(2)}) collective-permute-start(bf16[288,1024]{1,0:T(8,128)(2,1)} %pad_maximum_fusion.11), channel_id=1, source_target_pairs={{0,16},{4,20},{8,24},{12,28},{16,0},{20,4},{24,8},{28,12},{1,17},{... | collective-permute-start | bytes 1769480 | tf_op jit(solution)/shard_map/ppermute | solution.py:181
  17.1 49.4 %collective-permute-start.3 = (bf16[288,1024]{1,0:T(8,128)(2,1)}, bf16[288,1024]{1,0:T(8,128)(2,1)}, u32[]{:S(2)}, u32[]{:S(2)}) collective-permute-start(bf16[288,1024]{1,0:T(8,128)(2,1)} %pad_maximum_fusion.11), channel_id=1, source_target_pairs={{0,8},{4,12},{8,0},{12,4},{16,24},{20,28},{24,16},{28,20},{1,9},{5... | collective-permute-start | bytes 1769480 | tf_op jit(solution)/shard_map/ppermute | solution.py:181
  17.1 723.7 %reduce-scatter.7.cloned.1.call-start = ((), (), s32[]{:S(2)}) async-start(), calls=%async_computation.7 | async-start | bytes 1474560 | tf_op jit(solution)/shard_map/reduce_scatter | solution.py:219
  37.3 37.8 %collective-permute-start.8 = (bf16[288,512]{1,0:T(8,128)(2,1)S(1)}, bf16[288,512]{1,0:T(8,128)(2,1)}, u32[]{:S(2)}, u32[]{:S(2)}) collective-permute-start(bf16[288,512]{1,0:T(8,128)(2,1)S(1)} %copy-done.47), channel_id=1, source_target_pairs={{0,20},{4,16},{8,28},{12,24},{16,4},{20,0},{24,12},{28,8},{1,21},{... | collective-permute-start | bytes 884744 | tf_op jit(solution)/shard_map/ppermute | solution.py:181
  40.7 43.5 %collective-permute-start.9 = (bf16[288,512]{1,0:T(8,128)(2,1)S(1)}, bf16[288,512]{1,0:T(8,128)(2,1)}, u32[]{:S(2)}, u32[]{:S(2)}) collective-permute-start(bf16[288,512]{1,0:T(8,128)(2,1)S(1)} %copy-done.47), channel_id=1, source_target_pairs={{0,4},{4,0},{8,12},{12,8},{16,20},{20,16},{24,28},{28,24},{1,5},{5... | collective-permute-start | bytes 884744 | tf_op jit(solution)/shard_map/ppermute | solution.py:181
  62.6 23.3 %collective-permute-start.10 = (bf16[288,512]{1,0:T(8,128)(2,1)S(1)}, bf16[288,512]{1,0:T(8,128)(2,1)}, u32[]{:S(2)}, u32[]{:S(2)}) collective-permute-start(bf16[288,512]{1,0:T(8,128)(2,1)S(1)} %copy-done.47), channel_id=1, source_target_pairs={{0,16},{4,20},{8,24},{12,28},{16,0},{20,4},{24,8},{28,12},{1,17},{... | collective-permute-start | bytes 884744 | tf_op jit(solution)/shard_map/ppermute | solution.py:181
  64.5 23.7 %collective-permute-start.11 = (bf16[288,512]{1,0:T(8,128)(2,1)S(1)}, bf16[288,512]{1,0:T(8,128)(2,1)S(1)}, u32[]{:S(2)}, u32[]{:S(2)}) collective-permute-start(bf16[288,512]{1,0:T(8,128)(2,1)S(1)} %copy-done.47), channel_id=1, source_target_pairs={{0,8},{4,12},{8,0},{12,4},{16,24},{20,28},{24,16},{28,20},{1,9},{5... | collective-permute-start | bytes 884744 | tf_op jit(solution)/shard_map/ppermute | solution.py:181
  66.5 22.6 %collective-permute-start.4 = (bf16[288,1024]{1,0:T(8,128)(2,1)}, bf16[288,1024]{1,0:T(8,128)(2,1)S(1)}, u32[]{:S(2)}, u32[]{:S(2)}) collective-permute-start(bf16[288,1024]{1,0:T(8,128)(2,1)} %collective-permute-done.1), channel_id=1, source_target_pairs={{0,8},{4,12},{8,0},{12,4},{16,24},{20,28},{24,16},{28,20},{1,9},{5... | collective-permute-start | bytes 1769480 | tf_op jit(solution)/shard_map/ppermute | solution.py:181
  75.1 15.3 %collective-permute-start.5 = (bf16[288,1024]{1,0:T(8,128)(2,1)}, bf16[288,1024]{1,0:T(8,128)(2,1)S(1)}, u32[]{:S(2)}, u32[]{:S(2)}) collective-permute-start(bf16[288,1024]{1,0:T(8,128)(2,1)} %collective-permute-done.2), channel_id=1, source_target_pairs={{0,8},{4,12},{8,0},{12,4},{16,24},{20,28},{24,16},{28,20},{1,9},{5... | collective-permute-start | bytes 1769480 | tf_op jit(solution)/shard_map/ppermute | solution.py:181
  85.9 18.2 %collective-permute-start.12 = (bf16[288,512]{1,0:T(8,128)(2,1)}, bf16[288,512]{1,0:T(8,128)(2,1)}, u32[]{:S(2)}, u32[]{:S(2)}) collective-permute-start(bf16[288,512]{1,0:T(8,128)(2,1)} %collective-permute-done.9), channel_id=1, source_target_pairs={{0,8},{4,12},{8,0},{12,4},{16,24},{20,28},{24,16},{28,20},{1,9},{5... | collective-permute-start | bytes 884744 | tf_op jit(solution)/shard_map/ppermute | solution.py:181
  88.3 17.5 %collective-permute-start.13 = (bf16[288,512]{1,0:T(8,128)(2,1)}, bf16[288,512]{1,0:T(8,128)(2,1)}, u32[]{:S(2)}, u32[]{:S(2)}) collective-permute-start(bf16[288,512]{1,0:T(8,128)(2,1)} %collective-permute-done.10), channel_id=1, source_target_pairs={{0,8},{4,12},{8,0},{12,4},{16,24},{20,28},{24,16},{28,20},{1,9},{5... | collective-permute-start | bytes 884744 | tf_op jit(solution)/shard_map/ppermute | solution.py:181
  89.0 18.4 %collective-permute-start.14 = (bf16[288,512]{1,0:T(8,128)(2,1)}, bf16[288,512]{1,0:T(8,128)(2,1)}, u32[]{:S(2)}, u32[]{:S(2)}) collective-permute-start(bf16[288,512]{1,0:T(8,128)(2,1)} %collective-permute-done.8), channel_id=1, source_target_pairs={{0,8},{4,12},{8,0},{12,4},{16,24},{20,28},{24,16},{28,20},{1,9},{5... | collective-permute-start | bytes 884744 | tf_op jit(solution)/shard_map/ppermute | solution.py:181
  100.4 21.4 %collective-permute-start.7 = (bf16[384,512]{1,0:T(8,128)(2,1)}, bf16[384,512]{1,0:T(8,128)(2,1)S(1)}, u32[]{:S(2)}, u32[]{:S(2)}) collective-permute-start(bf16[384,512]{1,0:T(8,128)(2,1)} %slice.258), channel_id=1, source_target_pairs={{0,4},{1,5},{2,6},{3,7},{8,12},{9,13},{10,14},{11,15},{16,20},{17,... | collective-permute-start | bytes 1179656 | tf_op jit(solution)/shard_map/ppermute | solution.py:21
  131.3 15.4 %collective-permute-start.15 = (bf16[128,2304]{1,0:T(8,128)(2,1)S(1)}, bf16[128,2304]{1,0:T(8,128)(2,1)}, u32[]{:S(2)}, u32[]{:S(2)}) collective-permute-start(bf16[128,2304]{1,0:T(8,128)(2,1)S(1)} %get-tuple-element.51), channel_id=1, source_target_pairs={{0,1},{4,5},{8,9},{12,13},{16,17},{20,21},{24,25},{28,29}} | collective-permute-start | bytes 1769480 | tf_op jit(solution)/shard_map/ppermute | solution.py:45
  149.1 16.2 %collective-permute-start.17 = (bf16[128,2304]{1,0:T(8,128)(2,1)S(1)}, bf16[128,2304]{1,0:T(8,128)(2,1)S(1)}, u32[]{:S(2)}, u32[]{:S(2)}) collective-permute-start(bf16[128,2304]{1,0:T(8,128)(2,1)S(1)} %get-tuple-element.53), channel_id=1, source_target_pairs={{0,1},{1,2},{4,5},{5,6},{8,9},{9,10},{12,13},{13,14},{16,17},{17,1... | collective-permute-start | bytes 1769480 | tf_op jit(solution)/shard_map/ppermute | solution.py:45
  165.4 15.9 %collective-permute-start.19 = (bf16[128,2304]{1,0:T(8,128)(2,1)S(1)}, bf16[128,2304]{1,0:T(8,128)(2,1)S(1)}, u32[]{:S(2)}, u32[]{:S(2)}) collective-permute-start(bf16[128,2304]{1,0:T(8,128)(2,1)S(1)} %add_convert_fusion.8), channel_id=1, source_target_pairs={{0,1},{1,2},{2,3},{4,5},{5,6},{6,7},{8,9},{9,10},{10,11},{12,13},{... | collective-permute-start | bytes 1769480 | tf_op jit(solution)/shard_map/ppermute | solution.py:45
  171.1 15.4 %collective-permute-start.20 = (bf16[128,2304]{1,0:T(8,128)(2,1)}, bf16[128,2304]{1,0:T(8,128)(2,1)}, u32[]{:S(2)}, u32[]{:S(2)}) collective-permute-start(bf16[128,2304]{1,0:T(8,128)(2,1)} %add_convert_fusion.7), channel_id=1, source_target_pairs={{1,0},{2,1},{3,2},{5,4},{6,5},{7,6},{9,8},{10,9},{11,10},{13,12},{... | collective-permute-start | bytes 1769480 | tf_op jit(solution)/shard_map/ppermute | solution.py:45
  277.0 13.8 %collective-permute-start.29 = (bf16[128,2304]{1,0:T(8,128)(2,1)S(1)}, bf16[128,2304]{1,0:T(8,128)(2,1)S(1)}, u32[]{:S(2)}, u32[]{:S(2)}) collective-permute-start(bf16[128,2304]{1,0:T(8,128)(2,1)S(1)} %get-tuple-element.65), channel_id=1, source_target_pairs={{0,1},{1,2},{4,5},{5,6},{8,9},{9,10},{12,13},{13,14},{16,17},{17,1... | collective-permute-start | bytes 1769480 | tf_op jit(solution)/shard_map/ppermute | solution.py:45
  292.1 15.5 %collective-permute-start.31 = (bf16[128,2304]{1,0:T(8,128)(2,1)}, bf16[128,2304]{1,0:T(8,128)(2,1)}, u32[]{:S(2)}, u32[]{:S(2)}) collective-permute-start(bf16[128,2304]{1,0:T(8,128)(2,1)} %get-tuple-element.67), channel_id=1, source_target_pairs={{0,1},{1,2},{2,3},{4,5},{5,6},{6,7},{8,9},{9,10},{10,11},{12,13},{... | collective-permute-start | bytes 1769480 | tf_op jit(solution)/shard_map/ppermute | solution.py:45
  319.7 16.7 %collective-permute-start.34 = (bf16[128,2304]{1,0:T(8,128)(2,1)S(1)}, bf16[128,2304]{1,0:T(8,128)(2,1)S(1)}, u32[]{:S(2)}, u32[]{:S(2)}) collective-permute-start(bf16[128,2304]{1,0:T(8,128)(2,1)S(1)} %get-tuple-element.110), channel_id=1, source_target_pairs={{1,0},{2,1},{3,2},{5,4},{6,5},{7,6},{9,8},{10,9},{11,10},{13,12},{... | collective-permute-start | bytes 1769480 | tf_op jit(solution)/shard_map/ppermute | solution.py:45
  337.1 15.8 %collective-permute-start.36 = (bf16[128,2304]{1,0:T(8,128)(2,1)S(1)}, bf16[128,2304]{1,0:T(8,128)(2,1)S(1)}, u32[]{:S(2)}, u32[]{:S(2)}) collective-permute-start(bf16[128,2304]{1,0:T(8,128)(2,1)S(1)} %collective-permute-done.34), channel_id=1, source_target_pairs={{1,0},{2,1},{5,4},{6,5},{9,8},{10,9},{13,12},{14,13},{17,16},{18,1... | collective-permute-start | bytes 1769480 | tf_op jit(solution)/shard_map/ppermute | solution.py:45
  400.2 38.5 %collective-permute-start.39 = (bf16[128,2304]{1,0:T(8,128)(2,1)S(1)}, bf16[128,2304]{1,0:T(8,128)(2,1)S(1)}, u32[]{:S(2)}, u32[]{:S(2)}) collective-permute-start(bf16[128,2304]{1,0:T(8,128)(2,1)S(1)} %get-tuple-element.77), channel_id=1, source_target_pairs={{0,2},{1,3},{2,0},{3,1},{4,6},{5,7},{6,4},{7,5},{8,10},{9,11},{10,... | collective-permute-start | bytes 1769480 | tf_op jit(solution)/shard_map/ppermute | solution.py:50
  400.3 38.4 %collective-permute-start.40 = (bf16[128,2304]{1,0:T(8,128)(2,1)S(1)}, bf16[128,2304]{1,0:T(8,128)(2,1)S(1)}, u32[]{:S(2)}, u32[]{:S(2)}) collective-permute-start(bf16[128,2304]{1,0:T(8,128)(2,1)S(1)} %get-tuple-element.78), channel_id=1, source_target_pairs={{0,3},{1,0},{2,1},{3,2},{4,7},{5,4},{6,5},{7,6},{8,11},{9,8},{10,9... | collective-permute-start | bytes 1769480 | tf_op jit(solution)/shard_map/ppermute | solution.py:50
  402.2 36.5 %collective-permute-start.41 = (bf16[128,2304]{1,0:T(8,128)(2,1)S(1)}, bf16[128,2304]{1,0:T(8,128)(2,1)S(1)}, u32[]{:S(2)}, u32[]{:S(2)}) collective-permute-start(bf16[128,2304]{1,0:T(8,128)(2,1)S(1)} %get-tuple-element.79), channel_id=1, source_target_pairs={{0,1},{1,2},{2,3},{3,0},{4,5},{5,6},{6,7},{7,4},{8,9},{9,10},{10,1... | collective-permute-start | bytes 1769480 | tf_op jit(solution)/shard_map/ppermute | solution.py:50
  442.9 20.9 %collective-permute-start.42 = (bf16[128,2304]{1,0:T(8,128)(2,1)}, bf16[128,2304]{1,0:T(8,128)(2,1)}, u32[]{:S(2)}, u32[]{:S(2)}) collective-permute-start(bf16[128,2304]{1,0:T(8,128)(2,1)} %get-tuple-element.100), channel_id=1, source_target_pairs={{0,1},{1,2},{2,3},{3,0},{4,5},{5,6},{6,7},{7,4},{8,9},{9,10},{10,1... | collective-permute-start | bytes 1769480 | tf_op jit(solution)/shard_map/ppermute | solution.py:50
  451.0 28.6 %collective-permute-start.43 = (bf16[128,2304]{1,0:T(8,128)(2,1)}, bf16[128,2304]{1,0:T(8,128)(2,1)S(1)}, u32[]{:S(2)}, u32[]{:S(2)}) collective-permute-start(bf16[128,2304]{1,0:T(8,128)(2,1)} %get-tuple-element.100), channel_id=1, source_target_pairs={{0,2},{1,3},{2,0},{3,1},{4,6},{5,7},{6,4},{7,5},{8,10},{9,11},{10,... | collective-permute-start | bytes 1769480 | tf_op jit(solution)/shard_map/ppermute | solution.py:50
  451.0 30.5 %collective-permute-start.44 = (bf16[128,2304]{1,0:T(8,128)(2,1)}, bf16[128,2304]{1,0:T(8,128)(2,1)S(1)}, u32[]{:S(2)}, u32[]{:S(2)}) collective-permute-start(bf16[128,2304]{1,0:T(8,128)(2,1)} %get-tuple-element.100), channel_id=1, source_target_pairs={{0,3},{1,0},{2,1},{3,2},{4,7},{5,4},{6,5},{7,6},{8,11},{9,8},{10,9... | collective-permute-start | bytes 1769480 | tf_op jit(solution)/shard_map/ppermute | solution.py:50
  486.8 23.2 %collective-permute-start.61 = (bf16[1152,512]{1,0:T(8,128)(2,1)}, bf16[1152,512]{1,0:T(8,128)(2,1)}, u32[]{:S(2)}, u32[]{:S(2)}) collective-permute-start(bf16[1152,512]{1,0:T(8,128)(2,1)} %convolution_convert_fusion.7), channel_id=1, source_target_pairs={{0,8},{8,0},{16,24},{24,16},{1,9},{9,1},{17,25},{25,17},{2,10},{10... | collective-permute-start | bytes 3538952 | tf_op jit(solution)/shard_map/ppermute | solution.py:210
  492.6 14.3 %collective-permute-start.48 = (bf16[384,512]{0,1:T(8,128)(2,1)S(1)}, bf16[384,512]{0,1:T(8,128)(2,1)S(1)}, u32[]{:S(2)}, u32[]{:S(2)}) collective-permute-start(bf16[384,512]{0,1:T(8,128)(2,1)S(1)} %fusion.69), channel_id=1, source_target_pairs={{4,0},{5,1},{6,2},{7,3},{12,8},{13,9},{14,10},{15,11},{20,16},{21,... | collective-permute-start | bytes 1179656 | tf_op jit(solution)/shard_map/ppermute | solution.py:21
  513.5 229.4 %reduce-scatter.5.cloned.1.call-start = ((), (), s32[]{:S(2)}) async-start(), calls=%async_computation.6 | async-start | bytes 2949120 | tf_op jit(solution)/shard_map/reduce_scatter | solution.py:219
  513.5 19.2 %collective-permute-start.63 = (bf16[1152,2304]{1,0:T(8,128)(2,1)}, bf16[1152,2304]{1,0:T(8,128)(2,1)}, u32[]{:S(2)}, u32[]{:S(2)}) collective-permute-start(bf16[1152,2304]{1,0:T(8,128)(2,1)} %convolution_convert_fusion.1), channel_id=1, source_target_pairs={{0,8},{8,0},{16,24},{24,16},{1,9},{9,1},{17,25},{25,17},{2,10},{10... | collective-permute-start | bytes 15925256 | tf_op jit(solution)/shard_map/ppermute | solution.py:210
  519.6 227.0 %reduce-scatter.11.cloned.1.call-start = ((), (), s32[]{:S(2)}) async-start(), calls=%async_computation.9 | async-start | bytes 6635520 | tf_op jit(solution)/shard_map/reduce_scatter | solution.py:219
  532.6 16.7 %collective-permute-start.62 = (bf16[1152,4608]{1,0:T(8,128)(2,1)}, bf16[1152,4608]{1,0:T(8,128)(2,1)}, u32[]{:S(2)}, u32[]{:S(2)}) collective-permute-start(bf16[1152,4608]{1,0:T(8,128)(2,1)} %convolution_convert_fusion), channel_id=1, source_target_pairs={{0,8},{8,0},{16,24},{24,16},{1,9},{9,1},{17,25},{25,17},{2,10},{10... | collective-permute-start | bytes 31850504 | tf_op jit(solution)/shard_map/ppermute | solution.py:210
  539.6 228.3 %reduce-scatter.9.cloned.1.call-start = ((), (), s32[]{:S(2)}) async-start(), calls=%async_computation.8 | async-start | bytes 13271040 | tf_op jit(solution)/shard_map/reduce_scatter | solution.py:219
  563.3 31.0 %collective-permute-start.45 = (bf16[128,2304]{1,0:T(8,128)(2,1)}, bf16[128,2304]{1,0:T(8,128)(2,1)S(1)}, u32[]{:S(2)}, u32[]{:S(2)}) collective-permute-start(bf16[128,2304]{1,0:T(8,128)(2,1)} %concatenate.64), channel_id=1, source_target_pairs={{0,1},{1,2},{2,3},{3,0},{4,5},{5,6},{6,7},{7,4},{8,9},{9,10},{10,1... | collective-permute-start | bytes 1769480 | tf_op jit(solution)/shard_map/ppermute | solution.py:50
  576.6 42.9 %collective-permute-start.46 = (bf16[128,2304]{1,0:T(8,128)(2,1)}, bf16[128,2304]{1,0:T(8,128)(2,1)S(1)}, u32[]{:S(2)}, u32[]{:S(2)}) collective-permute-start(bf16[128,2304]{1,0:T(8,128)(2,1)} %concatenate.64), channel_id=1, source_target_pairs={{0,2},{1,3},{2,0},{3,1},{4,6},{5,7},{6,4},{7,5},{8,10},{9,11},{10,... | collective-permute-start | bytes 1769480 | tf_op jit(solution)/shard_map/ppermute | solution.py:50
  580.3 106.2 %collective-permute-start.47 = (bf16[128,2304]{1,0:T(8,128)(2,1)}, bf16[128,2304]{1,0:T(8,128)(2,1)}, u32[]{:S(2)}, u32[]{:S(2)}) collective-permute-start(bf16[128,2304]{1,0:T(8,128)(2,1)} %concatenate.64), channel_id=1, source_target_pairs={{0,3},{1,0},{2,1},{3,2},{4,7},{5,4},{6,5},{7,6},{8,11},{9,8},{10,9... | collective-permute-start | bytes 1769480 | tf_op jit(solution)/shard_map/ppermute | solution.py:50
  587.2 82.8 %collective-permute-start.49 = (bf16[128,2304]{1,0:T(8,128)(2,1)S(1)}, bf16[128,2304]{1,0:T(8,128)(2,1)S(1)}, u32[]{:S(2)}, u32[]{:S(2)}) collective-permute-start(bf16[128,2304]{1,0:T(8,128)(2,1)S(1)} %get-tuple-element.83), channel_id=1, source_target_pairs={{0,2},{1,3},{2,0},{3,1},{4,6},{5,7},{6,4},{7,5},{8,10},{9,11},{10,... | collective-permute-start | bytes 1769480 | tf_op jit(solution)/shard_map/ppermute | solution.py:50
  588.8 81.1 %collective-permute-start.50 = (bf16[128,2304]{1,0:T(8,128)(2,1)S(1)}, bf16[128,2304]{1,0:T(8,128)(2,1)S(1)}, u32[]{:S(2)}, u32[]{:S(2)}) collective-permute-start(bf16[128,2304]{1,0:T(8,128)(2,1)S(1)} %get-tuple-element.84), channel_id=1, source_target_pairs={{0,3},{1,0},{2,1},{3,2},{4,7},{5,4},{6,5},{7,6},{8,11},{9,8},{10,9... | collective-permute-start | bytes 1769480 | tf_op jit(solution)/shard_map/ppermute | solution.py:50
  594.3 75.6 %collective-permute-start.51 = (bf16[128,2304]{1,0:T(8,128)(2,1)S(1)}, bf16[128,2304]{1,0:T(8,128)(2,1)S(1)}, u32[]{:S(2)}, u32[]{:S(2)}) collective-permute-start(bf16[128,2304]{1,0:T(8,128)(2,1)S(1)} %get-tuple-element.85), channel_id=1, source_target_pairs={{0,1},{1,2},{2,3},{3,0},{4,5},{5,6},{6,7},{7,4},{8,9},{9,10},{10,1... | collective-permute-start | bytes 1769480 | tf_op jit(solution)/shard_map/ppermute | solution.py:50
  673.4 15.3 %collective-permute-start.55 = (f32[4,2304]{1,0:T(4,128)}, f32[4,2304]{1,0:T(4,128)S(1)}, u32[]{:S(2)}, u32[]{:S(2)}) collective-permute-start(f32[4,2304]{1,0:T(4,128)} %concatenate.71), channel_id=1, source_target_pairs={{0,1},{1,0},{2,3},{3,2},{4,5},{5,4},{6,7},{7,6},{8,9},{9,8},{10,11... | collective-permute-start | bytes 110600 | tf_op jit(solution)/shard_map/ppermute | solution.py:129
  698.1 18.2 %collective-permute-start.52 = (bf16[128,2304]{1,0:T(8,128)(2,1)S(1)}, bf16[128,2304]{1,0:T(8,128)(2,1)S(1)}, u32[]{:S(2)}, u32[]{:S(2)}) collective-permute-start(bf16[128,2304]{1,0:T(8,128)(2,1)S(1)} %concatenate.70), channel_id=1, source_target_pairs={{0,1},{1,2},{2,3},{3,0},{4,5},{5,6},{6,7},{7,4},{8,9},{9,10},{10,1... | collective-permute-start | bytes 1769480 | tf_op jit(solution)/shard_map/ppermute | solution.py:50
  699.8 40.8 %collective-permute-start.53 = (bf16[128,2304]{1,0:T(8,128)(2,1)S(1)}, bf16[128,2304]{1,0:T(8,128)(2,1)S(1)}, u32[]{:S(2)}, u32[]{:S(2)}) collective-permute-start(bf16[128,2304]{1,0:T(8,128)(2,1)S(1)} %concatenate.70), channel_id=1, source_target_pairs={{0,2},{1,3},{2,0},{3,1},{4,6},{5,7},{6,4},{7,5},{8,10},{9,11},{10,... | collective-permute-start | bytes 1769480 | tf_op jit(solution)/shard_map/ppermute | solution.py:50
  699.8 40.9 %collective-permute-start.54 = (bf16[128,2304]{1,0:T(8,128)(2,1)S(1)}, bf16[128,2304]{1,0:T(8,128)(2,1)S(1)}, u32[]{:S(2)}, u32[]{:S(2)}) collective-permute-start(bf16[128,2304]{1,0:T(8,128)(2,1)S(1)} %concatenate.70), channel_id=1, source_target_pairs={{0,3},{1,0},{2,1},{3,2},{4,7},{5,4},{6,5},{7,6},{8,11},{9,8},{10,9... | collective-permute-start | bytes 1769480 | tf_op jit(solution)/shard_map/ppermute | solution.py:50
  (106 other events, 1470.2 us)
Sparse Core Ops, SparseCore 0:
  10.8 145.2 all-gather.2
  158.0 67.6 all-gather.4
  513.6 40.3 reduce-scatter.6
  557.5 37.3 reduce-scatter.4
  597.7 61.8 reduce-scatter.10
  662.6 105.3 reduce-scatter.8

commit v7 on v6

--- a/solution.py
+++ b/solution.py
@@ -122,6 +122,20 @@
     return whole.reshape(-1, pieces[0].shape[-1])
 
 
+def exchanged(value):
+    size = lax.axis_size("tp")
+    rank = lax.axis_index("tp")
+    width = value.shape[1] // size
+    pieces = [value[:, k * width : (k + 1) * width] for k in range(size)]
+    pieces = lax.optimization_barrier(tuple(pieces))
+    whole = jnp.zeros((size,) + pieces[0].shape, value.dtype)
+    whole = lax.dynamic_update_index_in_dim(whole, pieces[0], rank, 0)
+    for k in distances(size):
+        arrived = shift(pieces[k], -k)
+        whole = lax.dynamic_update_index_in_dim(whole, arrived, (rank + k) % size, 0)
+    return whole.reshape(-1, width)
+
+
 def summed(value, axis):
     size = lax.axis_size(axis)
     bit = 1
@@ -169,31 +183,6 @@
     return lax.all_gather(
         weight, ROWS, axis=0, tiled=True, axis_index_groups=[first + second]
     )
-
-
-def sent_rows(weight, after=()):
-    ranks = lax.axis_size("fsdp") * lax.axis_size("ctx")
-    if (lax.axis_size("fsdp"), lax.axis_size("ctx")) != (4, 2):
-        return gather_rows(weight), ()
-    core, pair, width = 2, 4, 1
-
-    def sent(block, bits):
-        return lax.ppermute(block, ROWS, [(r, r ^ bits) for r in range(ranks)])
-
-    weight, after = lax.optimization_barrier((weight, after))
-    held = {0: weight}
-    for bits in (pair | width, width, pair):
-        held[bits] = sent(weight, bits)
-    for bits in (0, width, pair, pair | width):
-        held[bits | core] = sent(held[bits], core)
-    place = {0: 0, width: 1, pair: 2, core: 4}
-    rank = lax.axis_index("fsdp") * 2 + lax.axis_index("ctx")
-    own = (rank // core) % 2 * 4 + rank // pair * 2 + rank % 2
-    whole = jnp.zeros((ranks,) + weight.shape, weight.dtype)
-    for bits in held:
-        at = own ^ (place[bits & width] | place[bits & pair] | place[bits & core])
-        whole = lax.dynamic_update_index_in_dim(whole, held[bits], at, 0)
-    return whole.reshape(-1, weight.shape[1]), (held[pair | width],)
 
 
 def rows_of_core(left, core):
@@ -249,12 +238,16 @@
     tp_rank = lax.axis_index("tp")
     piece = length // tp_size
 
-    qkv_full, first_sent = sent_rows(
-        jnp.concatenate([query_weight, key_weight, value_weight], axis=1)
-    )
-    output_full, _ = sent_rows(output_weight, first_sent)
-    gate_up_full = gather_rows(jnp.concatenate([gate_weight, up_weight], axis=1))
-    down_full = gather_rows(down_weight)
+    attention_full = gather_rows(
+        jnp.concatenate([query_weight, key_weight, value_weight, output_weight], axis=1)
+    )
+    qkv_full = attention_full[:, :qkv_width]
+    output_full = attention_full[:, qkv_width:]
+    units_full = gather_rows(jnp.concatenate([gate_weight, up_weight, down_weight], axis=1))
+    gate_up_full = units_full[:, : 2 * units]
+    down_full = units_full[:, 2 * units :]
+    output_pieces = jnp.concatenate(sent_gathered(output_weight), axis=1)
+    output_all = gather_rows(output_pieces)
 
     position = lax.axis_index("ctx")
     own_ids = lax.dynamic_slice_in_dim(segment_ids, position * length, length)
@@ -318,6 +311,10 @@
     grad_branch_two, grad_gain_four = pull_four(upstream)
     grad_two_low = jnp.concatenate(gathered(grad_branch_two.astype(LOW)), axis=0)
 
+    result_low, grad_two_low = lax.optimization_barrier(
+        (by_chip(result.astype(LOW)), grad_two_low)
+    )
+    outputs = lax.all_gather(result_low, "tp", axis=0, tiled=True)
     down_sent, grad_two_low = lax.optimization_barrier(
         (sent_to_core(grad_two_low, hidden_low), grad_two_low)
     )
@@ -339,17 +336,16 @@
     grad_middle = upstream + grad_middle_norm
     _, pull_two = jax.vjp(rms, branch_one, post_attention_gain)
     grad_branch_one, grad_gain_two = pull_two(grad_middle)
-    grad_one_low = in_order(sent_gathered(grad_branch_one.astype(LOW)))
-    result_low, grad_one_low = lax.optimization_barrier(
-        (by_chip(result.astype(LOW)), grad_one_low)
-    )
-    outputs = in_order(sent_gathered(result_low))
-
+    grad_one_own = grad_branch_one.astype(LOW)
+    grad_attended = product(grad_one_own, output_all).astype(LOW)
+    grad_attended, grad_one_own = lax.optimization_barrier(
+        (exchanged(grad_attended), grad_one_own)
+    )
+    grad_attended = grad_attended.reshape(length, kv_heads, repeats, HD)
+    grad_one_low = in_order(sent_gathered(grad_one_own))
     output_sent = sent_to_core(grad_one_low, attended_low)
     output_arrived = over_cores(output_sent)
     output_share = share_rows(chip_rows(grad_one_low, attended_low, output_arrived))
-    grad_attended = product(grad_one_low, output_full).astype(LOW)
-    grad_attended = grad_attended.reshape(length, kv_heads, repeats, HD)
     probs = powers / totals
     grad_probs = jnp.einsum(
         "qgrd,kgd->grqk", grad_attended, values_all, preferred_element_type=F32
@@ -392,7 +388,7 @@
     gains = by_chip(jnp.stack([grad_gain_one, grad_gain_two, grad_gain_three, grad_gain_four]))
     for axis in ("tp",) + ROWS:
         gains = summed(gains, axis)
-    share = qkv_full.shape[0] // (lax.axis_size("fsdp") * lax.axis_size("ctx"))
+    share = hidden_in.shape[1] // (lax.axis_size("fsdp") * lax.axis_size("ctx"))
     row_rank = lax.axis_index("fsdp") * lax.axis_size("ctx") + lax.axis_index("ctx")
     gain_shares = lax.dynamic_slice_in_dim(gains, row_rank * share, share, axis=1)
     edges = [0, heads_width, heads_width + kv_width, qkv_width]

time: 788 us -> 847 us (1.075)
  waiting for transfers between devices: 395 us -> 483 us
  local copies, waits for them, and re-layouts: 78.6 us -> 51.7 us
  starting transfers between devices: 119 us -> 95.5 us
  matrix products: 128 us -> 139 us
  other arithmetic: 42.7 us -> 52.1 us
    ppermute x15 -> x18, waiting for transfers between devices: 174 us -> 229 us  [shift(): lax.ppermute(block, 'tp', [(i, (i + distance) % size) for i in range(size)])]
    reduce_scatter x4, waiting for transfers between devices: 18.2 us -> 62.8 us  [share_rows(): lax.psum_scatter(grad, ROWS, scatter_dimension=0, tiled=True, axis_index_...]
    all_gather x2 -> x3, waiting for transfers between devices: 0.02 us -> 38.3 us  [gather_rows(): lax.all_gather(weight, ROWS, axis=0, tiled=True, axis_index_groups=[first...]
    ppermute x14 -> x0, waiting for transfers between devices: 35.7 us -> none  [sent(): return lax.ppermute(block, ROWS, [(r, r ^ bits) for r in range(ranks)])]
    dynamic_update_slice x16 -> x4, local copies, waits for them, and re-layouts: 24.1 us -> 0.06 us  [the longest x3 0.04 us: exchanged(): lax.dynamic_update_index_in_dim(whole, arrived, (rank + k) % size, 0)]
    ppermute x24, waiting for transfers between devices: 124 us -> 108 us  [onward(): return lax.ppermute(block, 'tp', [(i, i + distance) for i in senders])]
    ppermute x5, starting transfers between devices: 14.9 us -> 0.29 us  [summed(): lax.ppermute(value, axis, [(i, i ^ bit) for i in range(size)])]
    ppermute x14 -> x0, starting transfers between devices: 9.44 us -> none  [sent(): return lax.ppermute(block, ROWS, [(r, r ^ bits) for r in range(ranks)])]
  transfers between devices with their start and end apart: 70 -> 61, of which waited for: 36 -> 37; matrix products, arithmetic and copies ran while one was open for 22% -> 27% of each run, Pallas kernels for 0% -> 0%
where the time goes in v7:
time: 847 us; the launch traced here: 837 us
  waiting for transfers between devices  483 us (57%)
  matrix products  139 us (16%)
  starting transfers between devices  95.5 us (11%)
  other arithmetic  52.1 us (6%)
  local copies, waits for them, and re-layouts  51.7 us (6%)
  between operations  16.2 us (2%)
    ppermute x18, waiting for transfers between devices, shift(): lax.ppermute(block, 'tp', [(i, (i + distance) % size) for i in range(size)])  229 us
    ppermute x24, waiting for transfers between devices, onward(): return lax.ppermute(block, 'tp', [(i, i + distance) for i in senders])  108 us
    reduce_scatter x4, waiting for transfers between devices, share_rows(): lax.psum_scatter(grad, ROWS, scatter_dimension=0, tiled=True, axis_index_...  62.8 us
    ppermute x24, starting transfers between devices, onward(): return lax.ppermute(block, 'tp', [(i, i + distance) for i in senders])  55.5 us
    dot_general x8, matrix products, rows_product(): lax.dot_general(left, right, (((0,), (0,)), ((), ())), preferred_element_...  50.2 us
    dot_general x4, matrix products, product(): return jnp.dot(left, right, preferred_element_type=F32)  40.2 us
    all_gather x3, waiting for transfers between devices, gather_rows(): lax.all_gather(weight, ROWS, axis=0, tiled=True, axis_index_groups=[first...  38.3 us
    dot_general x4, matrix products, transposed_product(): lax.dot_general(left, right, (((1,), (1,)), ((), ())), preferred_element_...  34.3 us
  transfers between devices with their start and end apart: 61, of which 37 were waited for; matrix products, arithmetic and copies ran while one was open for 27% of the time, Pallas kernels for 0%

profile of v7, /device:TPU:0, one launch (start us, length us, event | category | flops | bytes accessed | tf_op | source)
XLA Modules:
  0.0 837.3 jit_solution(11604669681372259661)
XLA Ops:
  23.7 38.3 %all-gather.5.cloned.1.call-done = bf16[2304,1536]{1,0:T(8,128)(2,1)} async-done(((bf16[288,1536]{1,0:T(8,128)(2,1)}), bf16[2304,1536]{1,0:T(8,128)(2,1)}) %all-gather.5.cloned.1.call-update) | async-done | bytes 7077904 | tf_op jit(solution)/shard_map/all_gather | solution.py:183
  61.9 5.7 fusion.42
  75.2 11.5 %collective-permute-done = bf16[384,512]{1,0:T(8,128)(2,1)} collective-permute-done((bf16[384,512]{1,0:T(8,128)(2,1)}, bf16[384,512]{1,0:T(8,128)(2,1)}, u32[]{:S(2)}, u32[]{:S(2)}) %collective-permute-start) | collective-permute-done | bytes 393248 | tf_op jit(solution)/shard_map/ppermute | solution.py:21
  102.3 9.8 %collective-permute-done.1 = bf16[128,2304]{1,0:T(8,128)(2,1)} collective-permute-done((bf16[128,2304]{1,0:T(8,128)(2,1)S(1)}, bf16[128,2304]{1,0:T(8,128)(2,1)}, u32[]{:S(2)}, u32[]{:S(2)}) %collective-permute-start.1) | collective-permute-done | bytes 589856 | tf_op jit(solution)/shard_map/ppermute | solution.py:45
  113.8 4.5 collective-permute-start.3
  119.1 9.1 %collective-permute-done.3 = bf16[128,2304]{1,0:T(8,128)(2,1)S(1)} collective-permute-done((bf16[128,2304]{1,0:T(8,128)(2,1)S(1)}, bf16[128,2304]{1,0:T(8,128)(2,1)S(1)}, u32[]{:S(2)}, u32[]{:S(2)}) %collective-permute-start.3) | collective-permute-done | bytes 589856 | tf_op jit(solution)/shard_map/ppermute | solution.py:45
  130.5 7.0 collective-permute-start.5
  149.6 4.4 collective-permute-start.7
  155.3 6.8 collective-permute-done.7
  169.4 4.9 collective-permute-start.29
  176.4 16.0 %collective-permute-done.30 = bf16[288,512]{1,0:T(8,128)(2,1)} collective-permute-done((bf16[288,512]{1,0:T(8,128)(2,1)}, bf16[288,512]{1,0:T(8,128)(2,1)}, u32[]{:S(2)}, u32[]{:S(2)}) %collective-permute-start.30) | collective-permute-done | bytes 294944 | tf_op jit(solution)/shard_map/ppermute | solution.py:50
  192.3 13.8 %collective-permute-done.29 = bf16[288,512]{1,0:T(8,128)(2,1)} collective-permute-done((bf16[288,512]{1,0:T(8,128)(2,1)}, bf16[288,512]{1,0:T(8,128)(2,1)}, u32[]{:S(2)}, u32[]{:S(2)}) %collective-permute-start.29) | collective-permute-done | bytes 294944 | tf_op jit(solution)/shard_map/ppermute | solution.py:50
  211.9 9.5 %collective-permute-done.12 = bf16[128,2304]{1,0:T(8,128)(2,1)S(1)} collective-permute-done((bf16[128,2304]{1,0:T(8,128)(2,1)}, bf16[128,2304]{1,0:T(8,128)(2,1)S(1)}, u32[]{:S(2)}, u32[]{:S(2)}) %collective-permute-start.12) | collective-permute-done | bytes 589856 | tf_op jit(solution)/shard_map/ppermute | solution.py:45
  221.5 17.7 %fusion.2 = f32[512,4608]{1,0:T(8,128)} fusion(bf16[2304,6912]{1,0:T(8,128)(2,1)} %all-gather.7.cloned.1.call-done, bf16[128,2304]{1,0:T(8,128)(2,1)S(1)} %broadcast_select_fusion.1, bf16[128,2304]{1,0:T(8,128)(2,1)S(1)} %broadcast_select_fusion.3, bf16[128,2304]{1,0:T(8,128)(2,1)S(1)} %broadcast_select_fusion.5, ...), kind=kOutput, calls=%fused_computation.4 | convolution fusion | flops 10881073152 | bytes 33030144 | tf_op jit(solution)/shard_map/dot_general | solution.py:33
  239.3 4.6 multiply_convert_fusion.1
  243.9 10.8 %fusion.18 = bf16[512,2304]{1,0:T(8,128)(2,1)S(1)} fusion(bf16[512,2304]{1,0:T(8,128)(2,1)S(1)} %multiply_convert_fusion.1, bf16[2304,6912]{1,0:T(8,128)(2,1)} %all-gather.7.cloned.1.call-done), kind=kOutput, calls=%fused_computation.30 | convolution fusion | flops 5436997632 | bytes 15335424 | tf_op jit(solution)/shard_map/dot_general | solution.py:41
  258.0 12.9 %collective-permute-done.13 = bf16[128,2304]{1,0:T(8,128)(2,1)S(1)} collective-permute-done((bf16[128,2304]{1,0:T(8,128)(2,1)S(1)}, bf16[128,2304]{1,0:T(8,128)(2,1)S(1)}, u32[]{:S(2)}, u32[]{:S(2)}) %collective-permute-start.13) | collective-permute-done | bytes 589856 | tf_op jit(solution)/shard_map/ppermute | solution.py:45
  271.9 5.0 collective-permute-start.15
  276.9 12.2 %collective-permute-done.15 = bf16[128,2304]{1,0:T(8,128)(2,1)S(1)} collective-permute-done((bf16[128,2304]{1,0:T(8,128)(2,1)S(1)}, bf16[128,2304]{1,0:T(8,128)(2,1)S(1)}, u32[]{:S(2)}, u32[]{:S(2)}) %collective-permute-start.15) | collective-permute-done | bytes 589856 | tf_op jit(solution)/shard_map/ppermute | solution.py:45
  291.7 6.3 collective-permute-start.17
  315.3 4.4 collective-permute-start.19
  321.1 9.2 %collective-permute-done.19 = bf16[128,2304]{1,0:T(8,128)(2,1)S(1)} collective-permute-done((bf16[128,2304]{1,0:T(8,128)(2,1)S(1)}, bf16[128,2304]{1,0:T(8,128)(2,1)S(1)}, u32[]{:S(2)}, u32[]{:S(2)}) %collective-permute-start.19) | collective-permute-done | bytes 589856 | tf_op jit(solution)/shard_map/ppermute | solution.py:45
  339.7 12.8 %collective-permute-done.22 = bf16[128,2304]{1,0:T(8,128)(2,1)} collective-permute-done((bf16[128,2304]{1,0:T(8,128)(2,1)S(1)}, bf16[128,2304]{1,0:T(8,128)(2,1)}, u32[]{:S(2)}, u32[]{:S(2)}) %collective-permute-start.22) | collective-permute-done | bytes 589856 | tf_op jit(solution)/shard_map/ppermute | solution.py:45
  355.6 10.1 %collective-permute-done.24 = bf16[128,2304]{1,0:T(8,128)(2,1)S(1)} collective-permute-done((bf16[128,2304]{1,0:T(8,128)(2,1)}, bf16[128,2304]{1,0:T(8,128)(2,1)S(1)}, u32[]{:S(2)}, u32[]{:S(2)}) %collective-permute-start.24) | collective-permute-done | bytes 589856 | tf_op jit(solution)/shard_map/ppermute | solution.py:45
  367.5 5.1 convolution_convert_fusion.1
  372.6 11.7 %fusion.17 = (bf16[512,2304]{1,0:T(8,128)(2,1)S(1)}, bf16[512,2304]{1,0:T(8,128)(2,1)S(1)}) fusion(f32[512,4608]{1,0:T(8,128)S(1)} %bitcast.163, bf16[512,2304]{1,0:T(8,128)(2,1)S(1)} %pad_maximum_fusion.3, bf16[2304,6912]{1,0:T(8,128)(2,1)} %all-gather.7.cloned.1.call-done), kind=kOutput, calls=%fused_computation.25 | convolution fusion | flops 5464129536 | bytes 27131904 | tf_op jit(solution)/shard_map/dot_general | solution.py:33
  385.9 14.7 %fusion.21 = bf16[512,2304]{1,0:T(8,128)(2,1)S(1)} fusion(bf16[2304,6912]{1,0:T(8,128)(2,1)} %all-gather.7.cloned.1.call-done, bf16[512,2304]{1,0:T(8,128)(2,1)S(1)} %get-tuple-element.117, bf16[512,2304]{1,0:T(8,128)(2,1)S(1)} %get-tuple-element.116), kind=kOutput, calls=%fused_computation.31 | convolution fusion | flops 10882252800 | bytes 28311552 | tf_op jit(solution)/shard_map/dot_general | solution.py:41
  405.9 16.4 %collective-permute-done.27 = bf16[128,2304]{1,0:T(8,128)(2,1)S(1)} collective-permute-done((bf16[128,2304]{1,0:T(8,128)(2,1)}, bf16[128,2304]{1,0:T(8,128)(2,1)S(1)}, u32[]{:S(2)}, u32[]{:S(2)}) %collective-permute-start.27) | collective-permute-done | bytes 589856 | tf_op jit(solution)/shard_map/ppermute | solution.py:50
  422.3 20.9 %collective-permute-done.26 = bf16[128,2304]{1,0:T(8,128)(2,1)} collective-permute-done((bf16[128,2304]{1,0:T(8,128)(2,1)}, bf16[128,2304]{1,0:T(8,128)(2,1)}, u32[]{:S(2)}, u32[]{:S(2)}) %collective-permute-start.26) | collective-permute-done | bytes 589856 | tf_op jit(solution)/shard_map/ppermute | solution.py:50
  443.2 45.0 %collective-permute-done.25 = bf16[128,2304]{1,0:T(8,128)(2,1)} collective-permute-done((bf16[128,2304]{1,0:T(8,128)(2,1)}, bf16[128,2304]{1,0:T(8,128)(2,1)}, u32[]{:S(2)}, u32[]{:S(2)}) %collective-permute-start.25) | collective-permute-done | bytes 589856 | tf_op jit(solution)/shard_map/ppermute | solution.py:50
  494.9 5.1 convolution_convert_fusion.6
  502.2 18.4 %collective-permute-done.31 = bf16[128,512]{1,0:T(8,128)(2,1)S(1)} collective-permute-done((bf16[128,512]{1,0:T(8,128)(2,1)S(1)}, bf16[128,512]{1,0:T(8,128)(2,1)S(1)}, u32[]{:S(2)}, u32[]{:S(2)}) %collective-permute-start.31) | collective-permute-done | bytes 131104 | tf_op jit(solution)/shard_map/ppermute | solution.py:50
  537.1 14.6 %collective-permute-done.48 = bf16[128,2304]{1,0:T(8,128)(2,1)} collective-permute-done((bf16[128,2304]{1,0:T(8,128)(2,1)S(1)}, bf16[128,2304]{1,0:T(8,128)(2,1)}, u32[]{:S(2)}, u32[]{:S(2)}) %collective-permute-start.48) | collective-permute-done | bytes 589856 | tf_op jit(solution)/shard_map/ppermute | solution.py:50
  560.0 10.2 %collective-permute-done.34 = bf16[384,512]{0,1:T(8,128)(2,1)S(1)} collective-permute-done((bf16[384,512]{0,1:T(8,128)(2,1)S(1)}, bf16[384,512]{0,1:T(8,128)(2,1)S(1)}, u32[]{:S(2)}, u32[]{:S(2)}) %collective-permute-start.34) | collective-permute-done | bytes 393248 | tf_op jit(solution)/shard_map/ppermute | solution.py:21
  578.1 4.9 add_convert_fusion.2
  584.8 11.4 %convolution_convert_fusion = bf16[1152,4608]{1,0:T(8,128)(2,1)} fusion(bf16[512,2304]{1,0:T(8,128)(2,1)} %copy-done.75, bf16[512,2304]{1,0:T(8,128)(2,1)} %copy-done.74, bf16[512,2304]{1,0:T(8,128)(2,1)S(1)} %pad_maximum_fusion.2, s32[]{:T(128)S(6)} %select_n.202), kind=kOutput, calls=%fused_computation.1 | convolution fusion | flops 5450563584 | bytes 16515076 | tf_op jit(solution)/shard_map/dot_general | solution.py:37
  596.3 6.8 add_convert_fusion.1
  603.2 9.6 %collective-permute-done.51 = bf16[1152,4608]{1,0:T(8,128)(2,1)} collective-permute-done((bf16[1152,4608]{1,0:T(8,128)(2,1)}, bf16[1152,4608]{1,0:T(8,128)(2,1)}, u32[]{:S(2)}, u32[]{:S(2)}) %collective-permute-start.51) | collective-permute-done | bytes 10616864 | tf_op jit(solution)/shard_map/ppermute | solution.py:199
  612.9 13.4 %add_convert_fusion = bf16[1152,4608]{1,0:T(8,128)(2,1)} fusion(bf16[1152,4608]{1,0:T(8,128)(2,1)} %collective-permute-done.51, bf16[512,2304]{1,0:T(8,128)(2,1)} %copy-done.75, bf16[512,2304]{1,0:T(8,128)(2,1)} %copy-done.74, bf16[512,2304]{1,0:T(8,128)(2,1)S(1)} %copy-done.31, s32[]{:T(128)S(6)} %select_n.211), kind=kOutput, calls=%fused_computation | convolution fusion | flops 5461180416 | bytes 27131908 | tf_op jit(solution)/shard_map/dot_general | solution.py:37
  627.5 5.5 convolution_convert_fusion.2
  633.2 6.1 collective-permute-start.37
  642.3 13.3 %collective-permute-done.37 = bf16[128,2304]{1,0:T(8,128)(2,1)S(1)} collective-permute-done((bf16[128,2304]{1,0:T(8,128)(2,1)S(1)}, bf16[128,2304]{1,0:T(8,128)(2,1)S(1)}, u32[]{:S(2)}, u32[]{:S(2)}) %collective-permute-start.37) | collective-permute-done | bytes 589856 | tf_op jit(solution)/shard_map/ppermute | solution.py:50
  655.5 12.0 %collective-permute-done.36 = bf16[128,2304]{1,0:T(8,128)(2,1)S(1)} collective-permute-done((bf16[128,2304]{1,0:T(8,128)(2,1)S(1)}, bf16[128,2304]{1,0:T(8,128)(2,1)S(1)}, u32[]{:S(2)}, u32[]{:S(2)}) %collective-permute-start.36) | collective-permute-done | bytes 589856 | tf_op jit(solution)/shard_map/ppermute | solution.py:50
  667.5 25.6 %collective-permute-done.35 = bf16[128,2304]{1,0:T(8,128)(2,1)S(1)} collective-permute-done((bf16[128,2304]{1,0:T(8,128)(2,1)S(1)}, bf16[128,2304]{1,0:T(8,128)(2,1)S(1)}, u32[]{:S(2)}, u32[]{:S(2)}) %collective-permute-start.35) | collective-permute-done | bytes 589856 | tf_op jit(solution)/shard_map/ppermute | solution.py:50
  718.7 9.0 %collective-permute-done.38 = bf16[128,2304]{1,0:T(8,128)(2,1)S(1)} collective-permute-done((bf16[128,2304]{1,0:T(8,128)(2,1)S(1)}, bf16[128,2304]{1,0:T(8,128)(2,1)S(1)}, u32[]{:S(2)}, u32[]{:S(2)}) %collective-permute-start.38) | collective-permute-done | bytes 589856 | tf_op jit(solution)/shard_map/ppermute | solution.py:50
  727.8 24.3 %collective-permute-done.39 = bf16[128,2304]{1,0:T(8,128)(2,1)S(1)} collective-permute-done((bf16[128,2304]{1,0:T(8,128)(2,1)S(1)}, bf16[128,2304]{1,0:T(8,128)(2,1)S(1)}, u32[]{:S(2)}, u32[]{:S(2)}) %collective-permute-start.39) | collective-permute-done | bytes 589856 | tf_op jit(solution)/shard_map/ppermute | solution.py:50
  761.2 62.8 %reduce-scatter.9.cloned.1.call-done = bf16[288,4608]{1,0:T(8,128)(2,1)} async-done(((bf16[1152,4608]{1,0:T(8,128)(2,1)}), bf16[288,4608]{1,0:T(8,128)(2,1)}) %reduce-scatter.9.cloned.1.call-update) | async-done | bytes 2654224 | tf_op jit(solution)/shard_map/reduce_scatter | solution.py:208
  823.9 4.6 fusion.123
  (368 shorter events, 202.4 us)
Async XLA Ops:
  7.2 54.7 %all-gather.5.cloned.1.call-start = ((), (), s32[]{:S(2)}) async-start(), calls=%async_computation.4 | async-start | bytes 7962624 | tf_op jit(solution)/shard_map/all_gather | solution.py:183
  9.6 211.9 %all-gather.7.cloned.1.call-start = ((), (), s32[]{:S(2)}) async-start(), calls=%async_computation.5 | async-start | bytes 35831808 | tf_op jit(solution)/shard_map/all_gather | solution.py:183
  12.9 482.0 %all-gather.11.cloned.1.call-start = ((), (), s32[]{:S(2)}) async-start(), calls=%async_computation.7 | async-start | bytes 10616832 | tf_op jit(solution)/shard_map/all_gather | solution.py:183
  68.4 18.3 %collective-permute-start = (bf16[384,512]{1,0:T(8,128)(2,1)}, bf16[384,512]{1,0:T(8,128)(2,1)}, u32[]{:S(2)}, u32[]{:S(2)}) collective-permute-start(bf16[384,512]{1,0:T(8,128)(2,1)} %slice.291), channel_id=1, source_target_pairs={{0,4},{1,5},{2,6},{3,7},{8,12},{9,13},{10,14},{11,15},{16,20},{17,... | collective-permute-start | bytes 1179656 | tf_op jit(solution)/shard_map/ppermute | solution.py:21
  98.3 13.8 %collective-permute-start.1 = (bf16[128,2304]{1,0:T(8,128)(2,1)S(1)}, bf16[128,2304]{1,0:T(8,128)(2,1)}, u32[]{:S(2)}, u32[]{:S(2)}) collective-permute-start(bf16[128,2304]{1,0:T(8,128)(2,1)S(1)} %get-tuple-element.55), channel_id=1, source_target_pairs={{0,1},{4,5},{8,9},{12,13},{16,17},{20,21},{24,25},{28,29}} | collective-permute-start | bytes 1769480 | tf_op jit(solution)/shard_map/ppermute | solution.py:45
  113.8 14.3 %collective-permute-start.3 = (bf16[128,2304]{1,0:T(8,128)(2,1)S(1)}, bf16[128,2304]{1,0:T(8,128)(2,1)S(1)}, u32[]{:S(2)}, u32[]{:S(2)}) collective-permute-start(bf16[128,2304]{1,0:T(8,128)(2,1)S(1)} %get-tuple-element.57), channel_id=1, source_target_pairs={{0,1},{1,2},{4,5},{5,6},{8,9},{9,10},{12,13},{13,14},{16,17},{17,1... | collective-permute-start | bytes 1769480 | tf_op jit(solution)/shard_map/ppermute | solution.py:45
  129.2 15.1 %collective-permute-start.6 = (bf16[128,2304]{1,0:T(8,128)(2,1)S(1)}, bf16[128,2304]{1,0:T(8,128)(2,1)S(1)}, u32[]{:S(2)}, u32[]{:S(2)}) collective-permute-start(bf16[128,2304]{1,0:T(8,128)(2,1)S(1)} %add_convert_fusion.6), channel_id=1, source_target_pairs={{1,0},{2,1},{3,2},{5,4},{6,5},{7,6},{9,8},{10,9},{11,10},{13,12},{... | collective-permute-start | bytes 1769480 | tf_op jit(solution)/shard_map/ppermute | solution.py:45
  130.5 15.3 %collective-permute-start.5 = (bf16[128,2304]{1,0:T(8,128)(2,1)}, bf16[128,2304]{1,0:T(8,128)(2,1)}, u32[]{:S(2)}, u32[]{:S(2)}) collective-permute-start(bf16[128,2304]{1,0:T(8,128)(2,1)} %add_convert_fusion.7), channel_id=1, source_target_pairs={{0,1},{1,2},{2,3},{4,5},{5,6},{6,7},{8,9},{9,10},{10,11},{12,13},{... | collective-permute-start | bytes 1769480 | tf_op jit(solution)/shard_map/ppermute | solution.py:45
  149.6 12.5 %collective-permute-start.7 = (bf16[128,2304]{1,0:T(8,128)(2,1)S(1)}, bf16[128,2304]{1,0:T(8,128)(2,1)S(1)}, u32[]{:S(2)}, u32[]{:S(2)}) collective-permute-start(bf16[128,2304]{1,0:T(8,128)(2,1)S(1)} %multiply_convert_fusion.2), channel_id=1, source_target_pairs={{0,1},{1,2},{2,3},{4,5},{5,6},{6,7},{8,9},{9,10},{10,11},{12,13},{... | collective-permute-start | bytes 1769480 | tf_op jit(solution)/shard_map/ppermute | solution.py:45
  154.0 12.2 %collective-permute-start.8 = (bf16[128,2304]{1,0:T(8,128)(2,1)S(1)}, bf16[128,2304]{1,0:T(8,128)(2,1)S(1)}, u32[]{:S(2)}, u32[]{:S(2)}) collective-permute-start(bf16[128,2304]{1,0:T(8,128)(2,1)S(1)} %multiply_convert_fusion.2), channel_id=1, source_target_pairs={{1,0},{2,1},{3,2},{5,4},{6,5},{7,6},{9,8},{10,9},{11,10},{13,12},{... | collective-permute-start | bytes 1769480 | tf_op jit(solution)/shard_map/ppermute | solution.py:45
  166.2 42.4 %collective-permute-start.9 = (bf16[128,2304]{1,0:T(8,128)(2,1)S(1)}, bf16[128,2304]{1,0:T(8,128)(2,1)S(1)}, u32[]{:S(2)}, u32[]{:S(2)}) collective-permute-start(bf16[128,2304]{1,0:T(8,128)(2,1)S(1)} %collective-permute-done.7), channel_id=1, source_target_pairs={{1,2},{2,3},{5,6},{6,7},{9,10},{10,11},{13,14},{14,15},{17,18},{18... | collective-permute-start | bytes 1769480 | tf_op jit(solution)/shard_map/ppermute | solution.py:45
  166.9 41.7 %collective-permute-start.10 = (bf16[128,2304]{1,0:T(8,128)(2,1)S(1)}, bf16[128,2304]{1,0:T(8,128)(2,1)}, u32[]{:S(2)}, u32[]{:S(2)}) collective-permute-start(bf16[128,2304]{1,0:T(8,128)(2,1)S(1)} %collective-permute-done.8), channel_id=1, source_target_pairs={{1,0},{2,1},{5,4},{6,5},{9,8},{10,9},{13,12},{14,13},{17,16},{18,1... | collective-permute-start | bytes 1769480 | tf_op jit(solution)/shard_map/ppermute | solution.py:45
  168.2 24.1 %collective-permute-start.30 = (bf16[288,512]{1,0:T(8,128)(2,1)}, bf16[288,512]{1,0:T(8,128)(2,1)}, u32[]{:S(2)}, u32[]{:S(2)}) collective-permute-start(bf16[288,512]{1,0:T(8,128)(2,1)} %param.24), channel_id=1, source_target_pairs={{0,3},{1,0},{2,1},{3,2},{4,7},{5,4},{6,5},{7,6},{8,11},{9,8},{10,9... | collective-permute-start | bytes 884744 | tf_op jit(solution)/shard_map/ppermute | solution.py:50
  169.4 36.8 %collective-permute-start.29 = (bf16[288,512]{1,0:T(8,128)(2,1)}, bf16[288,512]{1,0:T(8,128)(2,1)}, u32[]{:S(2)}, u32[]{:S(2)}) collective-permute-start(bf16[288,512]{1,0:T(8,128)(2,1)} %param.24), channel_id=1, source_target_pairs={{0,2},{1,3},{2,0},{3,1},{4,6},{5,7},{6,4},{7,5},{8,10},{9,11},{10,... | collective-permute-start | bytes 884744 | tf_op jit(solution)/shard_map/ppermute | solution.py:50
  174.3 31.8 %collective-permute-start.28 = (bf16[288,512]{1,0:T(8,128)(2,1)}, bf16[288,512]{1,0:T(8,128)(2,1)}, u32[]{:S(2)}, u32[]{:S(2)}) collective-permute-start(bf16[288,512]{1,0:T(8,128)(2,1)} %param.24), channel_id=1, source_target_pairs={{0,1},{1,2},{2,3},{3,0},{4,5},{5,6},{6,7},{7,4},{8,9},{9,10},{10,1... | collective-permute-start | bytes 884744 | tf_op jit(solution)/shard_map/ppermute | solution.py:50
  208.6 543.7 %all-gather.9.cloned.1.call-start = ((), (), s32[]{:S(2)}) async-start(), calls=%async_computation.6 | async-start | bytes 2949120 | tf_op jit(solution)/shard_map/all_gather | solution.py:317
  209.4 12.0 %collective-permute-start.12 = (bf16[128,2304]{1,0:T(8,128)(2,1)}, bf16[128,2304]{1,0:T(8,128)(2,1)S(1)}, u32[]{:S(2)}, u32[]{:S(2)}) collective-permute-start(bf16[128,2304]{1,0:T(8,128)(2,1)} %collective-permute-done.10), channel_id=1, source_target_pairs={{1,0},{5,4},{9,8},{13,12},{17,16},{21,20},{25,24},{29,28}} | collective-permute-start | bytes 1769480 | tf_op jit(solution)/shard_map/ppermute | solution.py:45
  255.5 15.4 %collective-permute-start.13 = (bf16[128,2304]{1,0:T(8,128)(2,1)S(1)}, bf16[128,2304]{1,0:T(8,128)(2,1)S(1)}, u32[]{:S(2)}, u32[]{:S(2)}) collective-permute-start(bf16[128,2304]{1,0:T(8,128)(2,1)S(1)} %get-tuple-element.67), channel_id=1, source_target_pairs={{0,1},{4,5},{8,9},{12,13},{16,17},{20,21},{24,25},{28,29}} | collective-permute-start | bytes 1769480 | tf_op jit(solution)/shard_map/ppermute | solution.py:45
  271.9 17.2 %collective-permute-start.15 = (bf16[128,2304]{1,0:T(8,128)(2,1)S(1)}, bf16[128,2304]{1,0:T(8,128)(2,1)S(1)}, u32[]{:S(2)}, u32[]{:S(2)}) collective-permute-start(bf16[128,2304]{1,0:T(8,128)(2,1)S(1)} %get-tuple-element.69), channel_id=1, source_target_pairs={{0,1},{1,2},{4,5},{5,6},{8,9},{9,10},{12,13},{13,14},{16,17},{17,1... | collective-permute-start | bytes 1769480 | tf_op jit(solution)/shard_map/ppermute | solution.py:45
  290.4 16.8 %collective-permute-start.18 = (bf16[128,2304]{1,0:T(8,128)(2,1)}, bf16[128,2304]{1,0:T(8,128)(2,1)}, u32[]{:S(2)}, u32[]{:S(2)}) collective-permute-start(bf16[128,2304]{1,0:T(8,128)(2,1)} %get-tuple-element.72), channel_id=1, source_target_pairs={{1,0},{2,1},{3,2},{5,4},{6,5},{7,6},{9,8},{10,9},{11,10},{13,12},{... | collective-permute-start | bytes 1769480 | tf_op jit(solution)/shard_map/ppermute | solution.py:45
  291.7 16.7 %collective-permute-start.17 = (bf16[128,2304]{1,0:T(8,128)(2,1)}, bf16[128,2304]{1,0:T(8,128)(2,1)}, u32[]{:S(2)}, u32[]{:S(2)}) collective-permute-start(bf16[128,2304]{1,0:T(8,128)(2,1)} %get-tuple-element.71), channel_id=1, source_target_pairs={{0,1},{1,2},{2,3},{4,5},{5,6},{6,7},{8,9},{9,10},{10,11},{12,13},{... | collective-permute-start | bytes 1769480 | tf_op jit(solution)/shard_map/ppermute | solution.py:45
  315.3 14.9 %collective-permute-start.19 = (bf16[128,2304]{1,0:T(8,128)(2,1)S(1)}, bf16[128,2304]{1,0:T(8,128)(2,1)S(1)}, u32[]{:S(2)}, u32[]{:S(2)}) collective-permute-start(bf16[128,2304]{1,0:T(8,128)(2,1)S(1)} %get-tuple-element.118), channel_id=1, source_target_pairs={{0,1},{1,2},{2,3},{4,5},{5,6},{6,7},{8,9},{9,10},{10,11},{12,13},{... | collective-permute-start | bytes 1769480 | tf_op jit(solution)/shard_map/ppermute | solution.py:45
  319.8 14.7 %collective-permute-start.20 = (bf16[128,2304]{1,0:T(8,128)(2,1)S(1)}, bf16[128,2304]{1,0:T(8,128)(2,1)S(1)}, u32[]{:S(2)}, u32[]{:S(2)}) collective-permute-start(bf16[128,2304]{1,0:T(8,128)(2,1)S(1)} %get-tuple-element.118), channel_id=1, source_target_pairs={{1,0},{2,1},{3,2},{5,4},{6,5},{7,6},{9,8},{10,9},{11,10},{13,12},{... | collective-permute-start | bytes 1769480 | tf_op jit(solution)/shard_map/ppermute | solution.py:45
  335.9 16.6 %collective-permute-start.22 = (bf16[128,2304]{1,0:T(8,128)(2,1)S(1)}, bf16[128,2304]{1,0:T(8,128)(2,1)}, u32[]{:S(2)}, u32[]{:S(2)}) collective-permute-start(bf16[128,2304]{1,0:T(8,128)(2,1)S(1)} %collective-permute-done.20), channel_id=1, source_target_pairs={{1,0},{2,1},{5,4},{6,5},{9,8},{10,9},{13,12},{14,13},{17,16},{18,1... | collective-permute-start | bytes 1769480 | tf_op jit(solution)/shard_map/ppermute | solution.py:45
  353.2 12.6 %collective-permute-start.24 = (bf16[128,2304]{1,0:T(8,128)(2,1)}, bf16[128,2304]{1,0:T(8,128)(2,1)S(1)}, u32[]{:S(2)}, u32[]{:S(2)}) collective-permute-start(bf16[128,2304]{1,0:T(8,128)(2,1)} %collective-permute-done.22), channel_id=1, source_target_pairs={{1,0},{5,4},{9,8},{13,12},{17,16},{21,20},{25,24},{29,28}} | collective-permute-start | bytes 1769480 | tf_op jit(solution)/shard_map/ppermute | solution.py:45
  401.8 20.5 %collective-permute-start.27 = (bf16[128,2304]{1,0:T(8,128)(2,1)}, bf16[128,2304]{1,0:T(8,128)(2,1)S(1)}, u32[]{:S(2)}, u32[]{:S(2)}) collective-permute-start(bf16[128,2304]{1,0:T(8,128)(2,1)} %get-tuple-element.85), channel_id=1, source_target_pairs={{0,1},{1,2},{2,3},{3,0},{4,5},{5,6},{6,7},{7,4},{8,9},{9,10},{10,1... | collective-permute-start | bytes 1769480 | tf_op jit(solution)/shard_map/ppermute | solution.py:50
  401.8 41.3 %collective-permute-start.26 = (bf16[128,2304]{1,0:T(8,128)(2,1)}, bf16[128,2304]{1,0:T(8,128)(2,1)}, u32[]{:S(2)}, u32[]{:S(2)}) collective-permute-start(bf16[128,2304]{1,0:T(8,128)(2,1)} %get-tuple-element.84), channel_id=1, source_target_pairs={{0,3},{1,0},{2,1},{3,2},{4,7},{5,4},{6,5},{7,6},{8,11},{9,8},{10,9... | collective-permute-start | bytes 1769480 | tf_op jit(solution)/shard_map/ppermute | solution.py:50
  405.7 82.5 %collective-permute-start.25 = (bf16[128,2304]{1,0:T(8,128)(2,1)}, bf16[128,2304]{1,0:T(8,128)(2,1)}, u32[]{:S(2)}, u32[]{:S(2)}) collective-permute-start(bf16[128,2304]{1,0:T(8,128)(2,1)} %get-tuple-element.83), channel_id=1, source_target_pairs={{0,2},{1,3},{2,0},{3,1},{4,6},{5,7},{6,4},{7,5},{8,10},{9,11},{10,... | collective-permute-start | bytes 1769480 | tf_op jit(solution)/shard_map/ppermute | solution.py:50
  405.7 346.6 %reduce-scatter.7.cloned.1.call-start = ((), (), s32[]{:S(2)}) async-start(), calls=%async_computation.9 | async-start | bytes 1474560 | tf_op jit(solution)/shard_map/reduce_scatter | solution.py:208
  500.0 20.7 %collective-permute-start.31 = (bf16[128,512]{1,0:T(8,128)(2,1)S(1)}, bf16[128,512]{1,0:T(8,128)(2,1)S(1)}, u32[]{:S(2)}, u32[]{:S(2)}) collective-permute-start(bf16[128,512]{1,0:T(8,128)(2,1)S(1)} %get-tuple-element.87), channel_id=1, source_target_pairs={{0,2},{1,3},{2,0},{3,1},{4,6},{5,7},{6,4},{7,5},{8,10},{9,11},{10,... | collective-permute-start | bytes 393224 | tf_op jit(solution)/shard_map/ppermute | solution.py:50
  500.1 20.6 %collective-permute-start.32 = (bf16[128,512]{1,0:T(8,128)(2,1)S(1)}, bf16[128,512]{1,0:T(8,128)(2,1)S(1)}, u32[]{:S(2)}, u32[]{:S(2)}) collective-permute-start(bf16[128,512]{1,0:T(8,128)(2,1)S(1)} %get-tuple-element.88), channel_id=1, source_target_pairs={{0,3},{1,0},{2,1},{3,2},{4,7},{5,4},{6,5},{7,6},{8,11},{9,8},{10,9... | collective-permute-start | bytes 393224 | tf_op jit(solution)/shard_map/ppermute | solution.py:50
  500.3 20.5 %collective-permute-start.33 = (bf16[128,512]{1,0:T(8,128)(2,1)S(1)}, bf16[128,512]{1,0:T(8,128)(2,1)S(1)}, u32[]{:S(2)}, u32[]{:S(2)}) collective-permute-start(bf16[128,512]{1,0:T(8,128)(2,1)S(1)} %get-tuple-element.89), channel_id=1, source_target_pairs={{0,1},{1,2},{2,3},{3,0},{4,5},{5,6},{6,7},{7,4},{8,9},{9,10},{10,1... | collective-permute-start | bytes 393224 | tf_op jit(solution)/shard_map/ppermute | solution.py:50
  520.8 15.1 %collective-permute-start.47 = (bf16[128,2304]{1,0:T(8,128)(2,1)S(1)}, bf16[128,2304]{1,0:T(8,128)(2,1)}, u32[]{:S(2)}, u32[]{:S(2)}) collective-permute-start(bf16[128,2304]{1,0:T(8,128)(2,1)S(1)} %fusion.64), channel_id=1, source_target_pairs={{0,1},{1,2},{2,3},{3,0},{4,5},{5,6},{6,7},{7,4},{8,9},{9,10},{10,1... | collective-permute-start | bytes 1769480 | tf_op jit(solution)/shard_map/ppermute | solution.py:50
  524.1 27.6 %collective-permute-start.48 = (bf16[128,2304]{1,0:T(8,128)(2,1)S(1)}, bf16[128,2304]{1,0:T(8,128)(2,1)}, u32[]{:S(2)}, u32[]{:S(2)}) collective-permute-start(bf16[128,2304]{1,0:T(8,128)(2,1)S(1)} %fusion.64), channel_id=1, source_target_pairs={{0,2},{1,3},{2,0},{3,1},{4,6},{5,7},{6,4},{7,5},{8,10},{9,11},{10,... | collective-permute-start | bytes 1769480 | tf_op jit(solution)/shard_map/ppermute | solution.py:50
  524.1 28.7 %collective-permute-start.49 = (bf16[128,2304]{1,0:T(8,128)(2,1)S(1)}, bf16[128,2304]{1,0:T(8,128)(2,1)}, u32[]{:S(2)}, u32[]{:S(2)}) collective-permute-start(bf16[128,2304]{1,0:T(8,128)(2,1)S(1)} %fusion.64), channel_id=1, source_target_pairs={{0,3},{1,0},{2,1},{3,2},{4,7},{5,4},{6,5},{7,6},{8,11},{9,8},{10,9... | collective-permute-start | bytes 1769480 | tf_op jit(solution)/shard_map/ppermute | solution.py:50
  555.9 17.4 %collective-permute-start.50 = (bf16[1152,512]{1,0:T(8,128)(2,1)}, bf16[1152,512]{1,0:T(8,128)(2,1)}, u32[]{:S(2)}, u32[]{:S(2)}) collective-permute-start(bf16[1152,512]{1,0:T(8,128)(2,1)} %convolution_convert_fusion.5), channel_id=1, source_target_pairs={{0,8},{8,0},{16,24},{24,16},{1,9},{9,1},{17,25},{25,17},{2,10},{10... | collective-permute-start | bytes 3538952 | tf_op jit(solution)/shard_map/ppermute | solution.py:199
  556.7 13.5 %collective-permute-start.34 = (bf16[384,512]{0,1:T(8,128)(2,1)S(1)}, bf16[384,512]{0,1:T(8,128)(2,1)S(1)}, u32[]{:S(2)}, u32[]{:S(2)}) collective-permute-start(bf16[384,512]{0,1:T(8,128)(2,1)S(1)} %fusion.88), channel_id=1, source_target_pairs={{4,0},{5,1},{6,2},{7,3},{12,8},{13,9},{14,10},{15,11},{20,16},{21,... | collective-permute-start | bytes 1179656 | tf_op jit(solution)/shard_map/ppermute | solution.py:21
  577.2 177.2 %reduce-scatter.5.cloned.1.call-start = ((), (), s32[]{:S(2)}) async-start(), calls=%async_computation.8 | async-start | bytes 2949120 | tf_op jit(solution)/shard_map/reduce_scatter | solution.py:208
  577.2 19.1 %collective-permute-start.52 = (bf16[1152,2304]{1,0:T(8,128)(2,1)}, bf16[1152,2304]{1,0:T(8,128)(2,1)}, u32[]{:S(2)}, u32[]{:S(2)}) collective-permute-start(bf16[1152,2304]{1,0:T(8,128)(2,1)} %convolution_convert_fusion.1), channel_id=1, source_target_pairs={{0,8},{8,0},{16,24},{24,16},{1,9},{9,1},{17,25},{25,17},{2,10},{10... | collective-permute-start | bytes 15925256 | tf_op jit(solution)/shard_map/ppermute | solution.py:199
  583.0 175.0 %reduce-scatter.11.cloned.1.call-start = ((), (), s32[]{:S(2)}) async-start(), calls=%async_computation.11 | async-start | bytes 6635520 | tf_op jit(solution)/shard_map/reduce_scatter | solution.py:208
  596.2 16.7 %collective-permute-start.51 = (bf16[1152,4608]{1,0:T(8,128)(2,1)}, bf16[1152,4608]{1,0:T(8,128)(2,1)}, u32[]{:S(2)}, u32[]{:S(2)}) collective-permute-start(bf16[1152,4608]{1,0:T(8,128)(2,1)} %convolution_convert_fusion), channel_id=1, source_target_pairs={{0,8},{8,0},{16,24},{24,16},{1,9},{9,1},{17,25},{25,17},{2,10},{10... | collective-permute-start | bytes 31850504 | tf_op jit(solution)/shard_map/ppermute | solution.py:199
  603.2 220.7 %reduce-scatter.9.cloned.1.call-start = ((), (), s32[]{:S(2)}) async-start(), calls=%async_computation.10 | async-start | bytes 13271040 | tf_op jit(solution)/shard_map/reduce_scatter | solution.py:208
  633.2 22.3 %collective-permute-start.37 = (bf16[128,2304]{1,0:T(8,128)(2,1)S(1)}, bf16[128,2304]{1,0:T(8,128)(2,1)S(1)}, u32[]{:S(2)}, u32[]{:S(2)}) collective-permute-start(bf16[128,2304]{1,0:T(8,128)(2,1)S(1)} %get-tuple-element.94), channel_id=1, source_target_pairs={{0,1},{1,2},{2,3},{3,0},{4,5},{5,6},{6,7},{7,4},{8,9},{9,10},{10,1... | collective-permute-start | bytes 1769480 | tf_op jit(solution)/shard_map/ppermute | solution.py:50
  639.4 28.1 %collective-permute-start.36 = (bf16[128,2304]{1,0:T(8,128)(2,1)S(1)}, bf16[128,2304]{1,0:T(8,128)(2,1)S(1)}, u32[]{:S(2)}, u32[]{:S(2)}) collective-permute-start(bf16[128,2304]{1,0:T(8,128)(2,1)S(1)} %get-tuple-element.93), channel_id=1, source_target_pairs={{0,3},{1,0},{2,1},{3,2},{4,7},{5,4},{6,5},{7,6},{8,11},{9,8},{10,9... | collective-permute-start | bytes 1769480 | tf_op jit(solution)/shard_map/ppermute | solution.py:50
  641.6 51.5 %collective-permute-start.35 = (bf16[128,2304]{1,0:T(8,128)(2,1)S(1)}, bf16[128,2304]{1,0:T(8,128)(2,1)S(1)}, u32[]{:S(2)}, u32[]{:S(2)}) collective-permute-start(bf16[128,2304]{1,0:T(8,128)(2,1)S(1)} %get-tuple-element.92), channel_id=1, source_target_pairs={{0,2},{1,3},{2,0},{3,1},{4,6},{5,7},{6,4},{7,5},{8,10},{9,11},{10,... | collective-permute-start | bytes 1769480 | tf_op jit(solution)/shard_map/ppermute | solution.py:50
  709.5 18.2 %collective-permute-start.38 = (bf16[128,2304]{1,0:T(8,128)(2,1)S(1)}, bf16[128,2304]{1,0:T(8,128)(2,1)S(1)}, u32[]{:S(2)}, u32[]{:S(2)}) collective-permute-start(bf16[128,2304]{1,0:T(8,128)(2,1)S(1)} %concatenate.74), channel_id=1, source_target_pairs={{0,1},{1,2},{2,3},{3,0},{4,5},{5,6},{6,7},{7,4},{8,9},{9,10},{10,1... | collective-permute-start | bytes 1769480 | tf_op jit(solution)/shard_map/ppermute | solution.py:50
  709.6 42.5 %collective-permute-start.39 = (bf16[128,2304]{1,0:T(8,128)(2,1)S(1)}, bf16[128,2304]{1,0:T(8,128)(2,1)S(1)}, u32[]{:S(2)}, u32[]{:S(2)}) collective-permute-start(bf16[128,2304]{1,0:T(8,128)(2,1)S(1)} %concatenate.74), channel_id=1, source_target_pairs={{0,2},{1,3},{2,0},{3,1},{4,6},{5,7},{6,4},{7,5},{8,10},{9,11},{10,... | collective-permute-start | bytes 1769480 | tf_op jit(solution)/shard_map/ppermute | solution.py:50
  710.6 41.5 %collective-permute-start.40 = (bf16[128,2304]{1,0:T(8,128)(2,1)S(1)}, bf16[128,2304]{1,0:T(8,128)(2,1)S(1)}, u32[]{:S(2)}, u32[]{:S(2)}) collective-permute-start(bf16[128,2304]{1,0:T(8,128)(2,1)S(1)} %concatenate.74), channel_id=1, source_target_pairs={{0,3},{1,0},{2,1},{3,2},{4,7},{5,4},{6,5},{7,6},{8,11},{9,8},{10,9... | collective-permute-start | bytes 1769480 | tf_op jit(solution)/shard_map/ppermute | solution.py:50
  (92 other events, 1481.1 us)
Sparse Core Ops, SparseCore 0:
  10.5 51.4 all-gather.4
  63.8 157.0 all-gather.6
  223.3 58.6 all-gather.10
  405.8 81.9 all-gather.8
  577.3 32.3 reduce-scatter.6
  613.2 37.3 reduce-scatter.4
  653.6 62.6 reduce-scatter.10
  719.4 104.5 reduce-scatter.8

commit v8 on v7

--- a/solution.py
+++ b/solution.py
@@ -235,7 +235,6 @@
     qkv_width = heads_width + 2 * kv_width
     scaling = HD ** (-0.5)
     tp_size = lax.axis_size("tp")
-    tp_rank = lax.axis_index("tp")
     piece = length // tp_size
 
     attention_full = gather_rows(
@@ -274,10 +273,10 @@
     )
     hidden_in = by_core(hidden_in)
     normed_one = rms(hidden_in.astype(F32), pre_attention_gain).astype(LOW)
-    inputs = lax.dynamic_slice_in_dim(hidden_in, tp_rank * piece, piece).astype(F32)
-    upstream = by_core(
-        lax.dynamic_slice_in_dim(cotangent, tp_rank * piece, piece)
-    ).astype(F32)
+    inputs_turned = jnp.concatenate(ordered_blocks(hidden_in), axis=0)
+    upstream_turned = by_core(jnp.concatenate(ordered_blocks(cotangent), axis=0))
+    inputs = inputs_turned[:piece].astype(F32)
+    upstream = upstream_turned[:piece].astype(F32)
 
     qkv_low = product(normed_one, qkv_full).astype(LOW)
     queries = qkv_low[:, :heads_width].reshape(length, kv_heads, repeats, HD)
@@ -294,9 +293,10 @@
     branch_one = scattered(
         ordered_blocks(transposed_product(attended_low, output_full).astype(LOW))
     )
-    middle = inputs + rms(branch_one, post_attention_gain)
-    normed_two_own = rms(middle, pre_feedforward_gain).astype(LOW)
-    normed_two = jnp.concatenate(gathered(normed_two_own), axis=0)
+    branch_one_low = jnp.concatenate(gathered(branch_one.astype(LOW)), axis=0).astype(F32)
+    middle_turned = inputs_turned.astype(F32) + rms(branch_one_low, post_attention_gain)
+    middle = middle_turned[:piece]
+    normed_two = rms(middle_turned, pre_feedforward_gain).astype(LOW)
 
     gate_up = product(normed_two, gate_up_full)
     gate_value = gate_up[:, :units]
@@ -305,16 +305,12 @@
     branch_two = scattered(
         turned_blocks(transposed_product(hidden_low, down_full).astype(LOW))
     )
-    result = middle + rms(branch_two, post_feedforward_gain)
-
-    _, pull_four = jax.vjp(rms, branch_two, post_feedforward_gain)
-    grad_branch_two, grad_gain_four = pull_four(upstream)
-    grad_two_low = jnp.concatenate(gathered(grad_branch_two.astype(LOW)), axis=0)
-
-    result_low, grad_two_low = lax.optimization_barrier(
-        (by_chip(result.astype(LOW)), grad_two_low)
-    )
-    outputs = lax.all_gather(result_low, "tp", axis=0, tiled=True)
+    branch_two_low = jnp.concatenate(gathered(branch_two.astype(LOW)), axis=0).astype(F32)
+    unused_four, pull_four = jax.vjp(rms, branch_two_low, post_feedforward_gain)
+    grad_two_low = pull_four(upstream_turned.astype(F32))[0].astype(LOW)
+    unused_four, pull_four = jax.vjp(rms, branch_two, post_feedforward_gain)
+    grad_gain_four = pull_four(upstream)[1]
+
     down_sent, grad_two_low = lax.optimization_barrier(
         (sent_to_core(grad_two_low, hidden_low), grad_two_low)
     )
@@ -324,6 +320,8 @@
     grad_gate_up = jnp.concatenate([grad_gate.astype(LOW), grad_up.astype(LOW)], axis=1)
     grad_normed_two = transposed_product(grad_gate_up, gate_up_full).astype(LOW)
     grad_normed_two = sent_scattered(turned_blocks(grad_normed_two))
+    result = (middle_turned + rms(branch_two_low, post_feedforward_gain)).astype(LOW)
+    outputs = in_order(turned_blocks(by_chip(result)))
     grad_down_low = chip_rows(grad_two_low, hidden_low, down_arrived)
     down_share = share_rows(grad_down_low)
     gate_up_sent = sent_to_core(normed_two, grad_gate_up)
@@ -345,7 +343,7 @@
     grad_one_low = in_order(sent_gathered(grad_one_own))
     output_sent = sent_to_core(grad_one_low, attended_low)
     output_arrived = over_cores(output_sent)
-    output_share = share_rows(chip_rows(grad_one_low, attended_low, output_arrived))
+    grad_output_low = chip_rows(grad_one_low, attended_low, output_arrived)
     probs = powers / totals
     grad_probs = jnp.einsum(
         "qgrd,kgd->grqk", grad_attended, values_all, preferred_element_type=F32
@@ -377,8 +375,9 @@
     grad_normed_one = sent_scattered(ordered_blocks(grad_normed_one))
     qkv_sent = sent_to_core(normed_one, grad_qkv)
     qkv_arrived = over_cores(qkv_sent)
-    grad_qkv_low = by_rows(chip_rows(normed_one, grad_qkv, qkv_arrived))
-    qkv_share = share_rows(grad_qkv_low).astype(F32)
+    grad_qkv_low = chip_rows(normed_one, grad_qkv, qkv_arrived)
+    grad_attention = by_rows(jnp.concatenate([grad_qkv_low, grad_output_low], axis=1))
+    attention_share = share_rows(grad_attention).astype(F32)
 
     _, pull_one = jax.vjp(rms, inputs, pre_attention_gain)
     grad_inputs_norm, grad_gain_one = pull_one(grad_normed_one)
@@ -391,14 +390,14 @@
     share = hidden_in.shape[1] // (lax.axis_size("fsdp") * lax.axis_size("ctx"))
     row_rank = lax.axis_index("fsdp") * lax.axis_size("ctx") + lax.axis_index("ctx")
     gain_shares = lax.dynamic_slice_in_dim(gains, row_rank * share, share, axis=1)
-    edges = [0, heads_width, heads_width + kv_width, qkv_width]
-    qkv_shares = [qkv_share[:, a:b] for a, b in zip(edges[:-1], edges[1:])]
+    edges = [0, heads_width, heads_width + kv_width, qkv_width, qkv_width + heads_width]
+    attention_shares = [attention_share[:, a:b] for a, b in zip(edges[:-1], edges[1:])]
     gate_up_share = gate_up_share.astype(F32)
     return (
         (outputs, grad_inputs)
         + tuple(gain_shares[i] for i in range(4))
-        + tuple(qkv_shares)
-        + (output_share.astype(F32), gate_up_share[:, :units], gate_up_share[:, units:], down_share.astype(F32))
+        + tuple(attention_shares)
+        + (gate_up_share[:, :units], gate_up_share[:, units:], down_share.astype(F32))
     )
 
 

time: 847 us -> 811 us (0.957)
  waiting for transfers between devices: 483 us -> 421 us
  starting transfers between devices: 95.5 us -> 114 us
  local copies, waits for them, and re-layouts: 51.7 us -> 60.5 us
    ppermute x18, waiting for transfers between devices: 229 us -> 169 us  [shift(): lax.ppermute(block, 'tp', [(i, (i + distance) % size) for i in range(size)])]
    reduce_scatter x4 -> x3, waiting for transfers between devices: 62.8 us -> 41.2 us  [share_rows(): lax.psum_scatter(grad, ROWS, scatter_dimension=0, tiled=True, axis_index_...]
    all_gather x3, waiting for transfers between devices: 38.3 us -> 59.8 us  [gather_rows(): lax.all_gather(weight, ROWS, axis=0, tiled=True, axis_index_groups=[first...]
    ppermute x18, starting transfers between devices: 32.7 us -> 46.4 us  [shift(): lax.ppermute(block, 'tp', [(i, (i + distance) % size) for i in range(size)])]
  transfers between devices with their start and end apart: 61 -> 59, of which waited for: 37 -> 36; matrix products, arithmetic and copies ran while one was open for 27% -> 23% of each run, Pallas kernels for 0% -> 0%
where the time goes in v8:
time: 811 us; the launch traced here: 800 us
  waiting for transfers between devices  421 us (52%)
  matrix products  134 us (17%)
  starting transfers between devices  114 us (14%)
  local copies, waits for them, and re-layouts  60.5 us (7%)
  other arithmetic  54.8 us (7%)
  between operations  16.2 us (2%)
    ppermute x18, waiting for transfers between devices, shift(): lax.ppermute(block, 'tp', [(i, (i + distance) % size) for i in range(size)])  169 us
    ppermute x24, waiting for transfers between devices, onward(): return lax.ppermute(block, 'tp', [(i, i + distance) for i in senders])  112 us
    all_gather x3, waiting for transfers between devices, gather_rows(): lax.all_gather(weight, ROWS, axis=0, tiled=True, axis_index_groups=[first...  59.8 us
    ppermute x24, starting transfers between devices, onward(): return lax.ppermute(block, 'tp', [(i, i + distance) for i in senders])  58.2 us
    ppermute x18, starting transfers between devices, shift(): lax.ppermute(block, 'tp', [(i, (i + distance) % size) for i in range(size)])  46.4 us
    dot_general x8, matrix products, rows_product(): lax.dot_general(left, right, (((0,), (0,)), ((), ())), preferred_element_...  46.3 us
    reduce_scatter x3, waiting for transfers between devices, share_rows(): lax.psum_scatter(grad, ROWS, scatter_dimension=0, tiled=True, axis_index_...  41.2 us
    dot_general x4, matrix products, product(): return jnp.dot(left, right, preferred_element_type=F32)  38.6 us
  transfers between devices with their start and end apart: 59, of which 36 were waited for; matrix products, arithmetic and copies ran while one was open for 23% of the time, Pallas kernels for 0%

profile of v8, /device:TPU:0, one launch (start us, length us, event | category | flops | bytes accessed | tf_op | source)
XLA Modules:
  0.0 800.4 jit_solution(9002514685451459281)
XLA Ops:
  23.3 38.7 %all-gather.4.cloned.1.call-done = bf16[2304,1536]{1,0:T(8,128)(2,1)} async-done(((bf16[288,1536]{1,0:T(8,128)(2,1)}), bf16[2304,1536]{1,0:T(8,128)(2,1)}) %all-gather.4.cloned.1.call-update) | async-done | bytes 7077904 | tf_op jit(solution)/shard_map/all_gather | solution.py:183
  61.9 5.7 fusion.51
  75.2 11.5 %collective-permute-done = bf16[384,512]{1,0:T(8,128)(2,1)} collective-permute-done((bf16[384,512]{1,0:T(8,128)(2,1)}, bf16[384,512]{1,0:T(8,128)(2,1)}, u32[]{:S(2)}, u32[]{:S(2)}) %collective-permute-start) | collective-permute-done | bytes 393248 | tf_op jit(solution)/shard_map/ppermute | solution.py:21
  100.7 10.6 %collective-permute-done.1 = bf16[128,2304]{1,0:T(8,128)(2,1)S(1)} collective-permute-done((bf16[128,2304]{1,0:T(8,128)(2,1)S(1)}, bf16[128,2304]{1,0:T(8,128)(2,1)S(1)}, u32[]{:S(2)}, u32[]{:S(2)}) %collective-permute-start.1) | collective-permute-done | bytes 589856 | tf_op jit(solution)/shard_map/ppermute | solution.py:45
  116.7 9.2 %collective-permute-done.3 = bf16[128,2304]{1,0:T(8,128)(2,1)S(1)} collective-permute-done((bf16[128,2304]{1,0:T(8,128)(2,1)S(1)}, bf16[128,2304]{1,0:T(8,128)(2,1)S(1)}, u32[]{:S(2)}, u32[]{:S(2)}) %collective-permute-start.3) | collective-permute-done | bytes 589856 | tf_op jit(solution)/shard_map/ppermute | solution.py:45
  127.5 7.3 collective-permute-start.5
  134.9 7.6 collective-permute-done.6
  145.6 5.2 collective-permute-start.7
  153.0 5.0 collective-permute-done.7
  158.0 5.0 collective-permute-done.8
  169.5 8.7 %collective-permute-done.10 = bf16[128,2304]{1,0:T(8,128)(2,1)} collective-permute-done((bf16[128,2304]{1,0:T(8,128)(2,1)}, bf16[128,2304]{1,0:T(8,128)(2,1)}, u32[]{:S(2)}, u32[]{:S(2)}) %collective-permute-start.10) | collective-permute-done | bytes 589856 | tf_op jit(solution)/shard_map/ppermute | solution.py:45
  181.4 9.5 %collective-permute-done.12 = bf16[128,2304]{1,0:T(8,128)(2,1)S(1)} collective-permute-done((bf16[128,2304]{1,0:T(8,128)(2,1)}, bf16[128,2304]{1,0:T(8,128)(2,1)S(1)}, u32[]{:S(2)}, u32[]{:S(2)}) %collective-permute-start.12) | collective-permute-done | bytes 589856 | tf_op jit(solution)/shard_map/ppermute | solution.py:45
  199.7 21.1 %all-gather.6.cloned.1.call-done = bf16[2304,6912]{1,0:T(8,128)(2,1)} async-done(((bf16[288,6912]{1,0:T(8,128)(2,1)}), bf16[2304,6912]{1,0:T(8,128)(2,1)}) %all-gather.6.cloned.1.call-update) | async-done | bytes 31850512 | tf_op jit(solution)/shard_map/all_gather | solution.py:183
  220.9 14.5 %fusion.2 = f32[512,4608]{1,0:T(8,128)S(1)} fusion(bf16[512,2304]{1,0:T(8,128)(2,1)S(1)} %multiply_convert_fusion.2, bf16[2304,6912]{1,0:T(8,128)(2,1)} %all-gather.6.cloned.1.call-done), kind=kOutput, calls=%fused_computation.4 | convolution fusion | flops 10871635968 | bytes 33030144 | tf_op jit(solution)/shard_map/dot_general | solution.py:33
  239.0 10.8 %fusion.27 = bf16[512,2304]{1,0:T(8,128)(2,1)S(1)} fusion(bf16[512,2304]{1,0:T(8,128)(2,1)S(1)} %multiply_convert_fusion.1, bf16[2304,6912]{1,0:T(8,128)(2,1)} %all-gather.6.cloned.1.call-done), kind=kOutput, calls=%fused_computation.49 | convolution fusion | flops 5436997632 | bytes 15335424 | tf_op jit(solution)/shard_map/dot_general | solution.py:41
  254.2 12.9 %collective-permute-done.13 = bf16[128,2304]{1,0:T(8,128)(2,1)S(1)} collective-permute-done((bf16[128,2304]{1,0:T(8,128)(2,1)S(1)}, bf16[128,2304]{1,0:T(8,128)(2,1)S(1)}, u32[]{:S(2)}, u32[]{:S(2)}) %collective-permute-start.13) | collective-permute-done | bytes 589856 | tf_op jit(solution)/shard_map/ppermute | solution.py:45
  269.9 5.1 collective-permute-start.15
  278.3 16.1 %collective-permute-done.30 = bf16[288,512]{1,0:T(8,128)(2,1)S(1)} collective-permute-done((bf16[288,512]{1,0:T(8,128)(2,1)S(1)}, bf16[288,512]{1,0:T(8,128)(2,1)S(1)}, u32[]{:S(2)}, u32[]{:S(2)}) %collective-permute-start.30) | collective-permute-done | bytes 294944 | tf_op jit(solution)/shard_map/ppermute | solution.py:50
  294.4 18.0 %collective-permute-done.29 = bf16[288,512]{1,0:T(8,128)(2,1)S(1)} collective-permute-done((bf16[288,512]{1,0:T(8,128)(2,1)S(1)}, bf16[288,512]{1,0:T(8,128)(2,1)S(1)}, u32[]{:S(2)}, u32[]{:S(2)}) %collective-permute-start.29) | collective-permute-done | bytes 294944 | tf_op jit(solution)/shard_map/ppermute | solution.py:50
  317.7 5.4 collective-permute-start.17
  337.9 5.2 collective-permute-start.19
  344.4 8.0 %collective-permute-done.19 = bf16[128,2304]{1,0:T(8,128)(2,1)} collective-permute-done((bf16[128,2304]{1,0:T(8,128)(2,1)S(1)}, bf16[128,2304]{1,0:T(8,128)(2,1)}, u32[]{:S(2)}, u32[]{:S(2)}) %collective-permute-start.19) | collective-permute-done | bytes 589856 | tf_op jit(solution)/shard_map/ppermute | solution.py:45
  352.4 5.0 collective-permute-done.20
  360.5 14.8 %collective-permute-done.22 = bf16[128,2304]{1,0:T(8,128)(2,1)} collective-permute-done((bf16[128,2304]{1,0:T(8,128)(2,1)}, bf16[128,2304]{1,0:T(8,128)(2,1)}, u32[]{:S(2)}, u32[]{:S(2)}) %collective-permute-start.22) | collective-permute-done | bytes 589856 | tf_op jit(solution)/shard_map/ppermute | solution.py:45
  378.8 9.6 %collective-permute-done.24 = bf16[128,2304]{1,0:T(8,128)(2,1)S(1)} collective-permute-done((bf16[128,2304]{1,0:T(8,128)(2,1)}, bf16[128,2304]{1,0:T(8,128)(2,1)S(1)}, u32[]{:S(2)}, u32[]{:S(2)}) %collective-permute-start.24) | collective-permute-done | bytes 589856 | tf_op jit(solution)/shard_map/ppermute | solution.py:45
  391.0 5.7 fusion.21
  398.1 5.1 convolution_convert_fusion.1
  403.2 13.4 %fusion.20 = (bf16[512,2304]{1,0:T(8,128)(2,1)S(1)}, bf16[512,2304]{1,0:T(8,128)(2,1)}) fusion(f32[512,4608]{1,0:T(8,128)S(1)} %bitcast.204, bf16[512,2304]{1,0:T(8,128)(2,1)} %copy-done.28, bf16[2304,6912]{1,0:T(8,128)(2,1)} %all-gather.6.cloned.1.call-done), kind=kOutput, calls=%fused_computation.35 | convolution fusion | flops 5464129536 | bytes 27131904 | tf_op jit(solution)/shard_map/dot_general | solution.py:33
  418.0 15.3 %fusion.30 = bf16[512,2304]{1,0:T(8,128)(2,1)S(1)} fusion(bf16[2304,6912]{1,0:T(8,128)(2,1)} %all-gather.6.cloned.1.call-done, bf16[512,2304]{1,0:T(8,128)(2,1)} %get-tuple-element.115, bf16[512,2304]{1,0:T(8,128)(2,1)S(1)} %get-tuple-element.114), kind=kOutput, calls=%fused_computation.50 | convolution fusion | flops 10882252800 | bytes 28311552 | tf_op jit(solution)/shard_map/dot_general | solution.py:41
  437.7 13.8 %collective-permute-done.27 = bf16[128,2304]{1,0:T(8,128)(2,1)S(1)} collective-permute-done((bf16[128,2304]{1,0:T(8,128)(2,1)S(1)}, bf16[128,2304]{1,0:T(8,128)(2,1)S(1)}, u32[]{:S(2)}, u32[]{:S(2)}) %collective-permute-start.27) | collective-permute-done | bytes 589856 | tf_op jit(solution)/shard_map/ppermute | solution.py:50
  451.6 8.7 %collective-permute-done.26 = bf16[128,2304]{1,0:T(8,128)(2,1)S(1)} collective-permute-done((bf16[128,2304]{1,0:T(8,128)(2,1)S(1)}, bf16[128,2304]{1,0:T(8,128)(2,1)S(1)}, u32[]{:S(2)}, u32[]{:S(2)}) %collective-permute-start.26) | collective-permute-done | bytes 589856 | tf_op jit(solution)/shard_map/ppermute | solution.py:50
  460.3 21.1 %collective-permute-done.25 = bf16[128,2304]{1,0:T(8,128)(2,1)S(1)} collective-permute-done((bf16[128,2304]{1,0:T(8,128)(2,1)S(1)}, bf16[128,2304]{1,0:T(8,128)(2,1)S(1)}, u32[]{:S(2)}, u32[]{:S(2)}) %collective-permute-start.25) | collective-permute-done | bytes 589856 | tf_op jit(solution)/shard_map/ppermute | solution.py:50
  485.4 5.1 convolution_convert_fusion.6
  492.8 7.9 collective-permute-done.31
  500.9 21.5 %collective-permute-start.47 = (bf16[128,2304]{1,0:T(8,128)(2,1)S(1)}, bf16[128,2304]{1,0:T(8,128)(2,1)}, u32[]{:S(2)}, u32[]{:S(2)}) collective-permute-start(bf16[128,2304]{1,0:T(8,128)(2,1)S(1)} %fusion.69), channel_id=1, source_target_pairs={{0,1},{1,2},{2,3},{3,0},{4,5},{5,6},{6,7},{7,4},{8,9},{9,10},{10,1... | collective-permute-start | bytes 1769480 | tf_op jit(solution)/shard_map/ppermute | solution.py:50
  537.4 6.1 collective-permute-done.34
  564.7 10.7 %convolution_convert_fusion = bf16[1152,4608]{1,0:T(8,128)(2,1)} fusion(bf16[512,2304]{1,0:T(8,128)(2,1)} %get-tuple-element.115, bf16[512,2304]{1,0:T(8,128)(2,1)} %copy-done.64, bf16[512,2304]{1,0:T(8,128)(2,1)S(1)} %copy-done.24, s32[]{:T(128)S(6)} %select_n.233), kind=kOutput, calls=%fused_computation.1 | convolution fusion | flops 5450563584 | bytes 16515076 | tf_op jit(solution)/shard_map/dot_general | solution.py:37
  575.8 6.8 add_convert_fusion.1
  583.0 9.1 %collective-permute-done.51 = bf16[1152,4608]{1,0:T(8,128)(2,1)} collective-permute-done((bf16[1152,4608]{1,0:T(8,128)(2,1)}, bf16[1152,4608]{1,0:T(8,128)(2,1)}, u32[]{:S(2)}, u32[]{:S(2)}) %collective-permute-start.51) | collective-permute-done | bytes 10616864 | tf_op jit(solution)/shard_map/ppermute | solution.py:199
  592.1 13.3 %add_convert_fusion = bf16[1152,4608]{1,0:T(8,128)(2,1)} fusion(bf16[1152,4608]{1,0:T(8,128)(2,1)} %collective-permute-done.51, bf16[512,2304]{1,0:T(8,128)(2,1)} %get-tuple-element.115, bf16[512,2304]{1,0:T(8,128)(2,1)} %copy-done.64, bf16[512,2304]{1,0:T(8,128)(2,1)S(1)} %copy-done.24, s32[]{:T(128)S(6)} %select_n.242), kind=kOutput, calls=%fused_computation | convolution fusion | flops 5461180416 | bytes 27131908 | tf_op jit(solution)/shard_map/dot_general | solution.py:37
  614.4 5.4 convolution_convert_fusion.2
  620.0 5.9 collective-permute-start.37
  630.3 12.5 %collective-permute-done.37 = bf16[128,2304]{1,0:T(8,128)(2,1)S(1)} collective-permute-done((bf16[128,2304]{1,0:T(8,128)(2,1)S(1)}, bf16[128,2304]{1,0:T(8,128)(2,1)S(1)}, u32[]{:S(2)}, u32[]{:S(2)}) %collective-permute-start.37) | collective-permute-done | bytes 589856 | tf_op jit(solution)/shard_map/ppermute | solution.py:50
  642.8 10.9 %collective-permute-done.36 = bf16[128,2304]{1,0:T(8,128)(2,1)S(1)} collective-permute-done((bf16[128,2304]{1,0:T(8,128)(2,1)S(1)}, bf16[128,2304]{1,0:T(8,128)(2,1)S(1)}, u32[]{:S(2)}, u32[]{:S(2)}) %collective-permute-start.36) | collective-permute-done | bytes 589856 | tf_op jit(solution)/shard_map/ppermute | solution.py:50
  653.7 26.5 %collective-permute-done.35 = bf16[128,2304]{1,0:T(8,128)(2,1)S(1)} collective-permute-done((bf16[128,2304]{1,0:T(8,128)(2,1)S(1)}, bf16[128,2304]{1,0:T(8,128)(2,1)S(1)}, u32[]{:S(2)}, u32[]{:S(2)}) %collective-permute-start.35) | collective-permute-done | bytes 589856 | tf_op jit(solution)/shard_map/ppermute | solution.py:50
  706.8 8.8 %collective-permute-done.38 = bf16[128,2304]{1,0:T(8,128)(2,1)S(1)} collective-permute-done((bf16[128,2304]{1,0:T(8,128)(2,1)S(1)}, bf16[128,2304]{1,0:T(8,128)(2,1)S(1)}, u32[]{:S(2)}, u32[]{:S(2)}) %collective-permute-start.38) | collective-permute-done | bytes 589856 | tf_op jit(solution)/shard_map/ppermute | solution.py:50
  715.6 24.3 %collective-permute-done.39 = bf16[128,2304]{1,0:T(8,128)(2,1)S(1)} collective-permute-done((bf16[128,2304]{1,0:T(8,128)(2,1)S(1)}, bf16[128,2304]{1,0:T(8,128)(2,1)S(1)}, u32[]{:S(2)}, u32[]{:S(2)}) %collective-permute-start.39) | collective-permute-done | bytes 589856 | tf_op jit(solution)/shard_map/ppermute | solution.py:50
  747.5 41.2 %reduce-scatter.6.cloned.1.call-done = bf16[288,4608]{1,0:T(8,128)(2,1)} async-done(((bf16[1152,4608]{1,0:T(8,128)(2,1)}), bf16[288,4608]{1,0:T(8,128)(2,1)}) %reduce-scatter.6.cloned.1.call-update) | async-done | bytes 2654224 | tf_op jit(solution)/shard_map/reduce_scatter | solution.py:208
  (357 shorter events, 214.5 us)
Async XLA Ops:
  7.2 54.7 %all-gather.4.cloned.1.call-start = ((), (), s32[]{:S(2)}) async-start(), calls=%async_computation.3 | async-start | bytes 7962624 | tf_op jit(solution)/shard_map/all_gather | solution.py:183
  9.6 211.3 %all-gather.6.cloned.1.call-start = ((), (), s32[]{:S(2)}) async-start(), calls=%async_computation.4 | async-start | bytes 35831808 | tf_op jit(solution)/shard_map/all_gather | solution.py:183
  12.9 472.6 %all-gather.8.cloned.1.call-start = ((), (), s32[]{:S(2)}) async-start(), calls=%async_computation.5 | async-start | bytes 10616832 | tf_op jit(solution)/shard_map/all_gather | solution.py:183
  68.4 18.3 %collective-permute-start = (bf16[384,512]{1,0:T(8,128)(2,1)}, bf16[384,512]{1,0:T(8,128)(2,1)}, u32[]{:S(2)}, u32[]{:S(2)}) collective-permute-start(bf16[384,512]{1,0:T(8,128)(2,1)} %slice.335), channel_id=1, source_target_pairs={{0,4},{1,5},{2,6},{3,7},{8,12},{9,13},{10,14},{11,15},{16,20},{17,... | collective-permute-start | bytes 1179656 | tf_op jit(solution)/shard_map/ppermute | solution.py:21
  97.5 13.8 %collective-permute-start.1 = (bf16[128,2304]{1,0:T(8,128)(2,1)S(1)}, bf16[128,2304]{1,0:T(8,128)(2,1)S(1)}, u32[]{:S(2)}, u32[]{:S(2)}) collective-permute-start(bf16[128,2304]{1,0:T(8,128)(2,1)S(1)} %get-tuple-element.53), channel_id=1, source_target_pairs={{0,1},{4,5},{8,9},{12,13},{16,17},{20,21},{24,25},{28,29}} | collective-permute-start | bytes 1769480 | tf_op jit(solution)/shard_map/ppermute | solution.py:45
  111.5 14.3 %collective-permute-start.3 = (bf16[128,2304]{1,0:T(8,128)(2,1)S(1)}, bf16[128,2304]{1,0:T(8,128)(2,1)S(1)}, u32[]{:S(2)}, u32[]{:S(2)}) collective-permute-start(bf16[128,2304]{1,0:T(8,128)(2,1)S(1)} %get-tuple-element.55), channel_id=1, source_target_pairs={{0,1},{1,2},{4,5},{5,6},{8,9},{9,10},{12,13},{13,14},{16,17},{17,1... | collective-permute-start | bytes 1769480 | tf_op jit(solution)/shard_map/ppermute | solution.py:45
  116.0 10.0 %collective-permute-start.4 = (bf16[128,2304]{1,0:T(8,128)(2,1)S(1)}, bf16[128,2304]{1,0:T(8,128)(2,1)S(1)}, u32[]{:S(2)}, u32[]{:S(2)}) collective-permute-start(bf16[128,2304]{1,0:T(8,128)(2,1)S(1)} %get-tuple-element.56), channel_id=1, source_target_pairs={{2,1},{3,2},{6,5},{7,6},{10,9},{11,10},{14,13},{15,14},{18,17},{19... | collective-permute-start | bytes 1769480 | tf_op jit(solution)/shard_map/ppermute | solution.py:45
  126.2 16.2 %collective-permute-start.6 = (bf16[128,2304]{1,0:T(8,128)(2,1)S(1)}, bf16[128,2304]{1,0:T(8,128)(2,1)S(1)}, u32[]{:S(2)}, u32[]{:S(2)}) collective-permute-start(bf16[128,2304]{1,0:T(8,128)(2,1)S(1)} %add_convert_fusion.5), channel_id=1, source_target_pairs={{1,0},{2,1},{3,2},{5,4},{6,5},{7,6},{9,8},{10,9},{11,10},{13,12},{... | collective-permute-start | bytes 1769480 | tf_op jit(solution)/shard_map/ppermute | solution.py:45
  127.5 16.1 %collective-permute-start.5 = (bf16[128,2304]{1,0:T(8,128)(2,1)S(1)}, bf16[128,2304]{1,0:T(8,128)(2,1)S(1)}, u32[]{:S(2)}, u32[]{:S(2)}) collective-permute-start(bf16[128,2304]{1,0:T(8,128)(2,1)S(1)} %add_convert_fusion.6), channel_id=1, source_target_pairs={{0,1},{1,2},{2,3},{4,5},{5,6},{6,7},{8,9},{9,10},{10,11},{12,13},{... | collective-permute-start | bytes 1769480 | tf_op jit(solution)/shard_map/ppermute | solution.py:45
  145.6 12.4 %collective-permute-start.7 = (bf16[128,2304]{1,0:T(8,128)(2,1)S(1)}, bf16[128,2304]{1,0:T(8,128)(2,1)}, u32[]{:S(2)}, u32[]{:S(2)}) collective-permute-start(bf16[128,2304]{1,0:T(8,128)(2,1)S(1)} %convert_element_type.298), channel_id=1, source_target_pairs={{0,1},{1,2},{2,3},{4,5},{5,6},{6,7},{8,9},{9,10},{10,11},{12,13},{... | collective-permute-start | bytes 1769480 | tf_op jit(solution)/shard_map/ppermute | solution.py:45
  150.8 12.3 %collective-permute-start.8 = (bf16[128,2304]{1,0:T(8,128)(2,1)S(1)}, bf16[128,2304]{1,0:T(8,128)(2,1)}, u32[]{:S(2)}, u32[]{:S(2)}) collective-permute-start(bf16[128,2304]{1,0:T(8,128)(2,1)S(1)} %convert_element_type.298), channel_id=1, source_target_pairs={{1,0},{2,1},{3,2},{5,4},{6,5},{7,6},{9,8},{10,9},{11,10},{13,12},{... | collective-permute-start | bytes 1769480 | tf_op jit(solution)/shard_map/ppermute | solution.py:45
  163.0 6.4 collective-permute-start.9
  164.5 13.7 %collective-permute-start.10 = (bf16[128,2304]{1,0:T(8,128)(2,1)}, bf16[128,2304]{1,0:T(8,128)(2,1)}, u32[]{:S(2)}, u32[]{:S(2)}) collective-permute-start(bf16[128,2304]{1,0:T(8,128)(2,1)} %collective-permute-done.8), channel_id=1, source_target_pairs={{1,0},{2,1},{5,4},{6,5},{9,8},{10,9},{13,12},{14,13},{17,16},{18,1... | collective-permute-start | bytes 1769480 | tf_op jit(solution)/shard_map/ppermute | solution.py:45
  178.9 12.0 %collective-permute-start.12 = (bf16[128,2304]{1,0:T(8,128)(2,1)}, bf16[128,2304]{1,0:T(8,128)(2,1)S(1)}, u32[]{:S(2)}, u32[]{:S(2)}) collective-permute-start(bf16[128,2304]{1,0:T(8,128)(2,1)} %collective-permute-done.10), channel_id=1, source_target_pairs={{1,0},{5,4},{9,8},{13,12},{17,16},{21,20},{25,24},{29,28}} | collective-permute-start | bytes 1769480 | tf_op jit(solution)/shard_map/ppermute | solution.py:45
  250.8 16.4 %collective-permute-start.13 = (bf16[128,2304]{1,0:T(8,128)(2,1)S(1)}, bf16[128,2304]{1,0:T(8,128)(2,1)S(1)}, u32[]{:S(2)}, u32[]{:S(2)}) collective-permute-start(bf16[128,2304]{1,0:T(8,128)(2,1)S(1)} %get-tuple-element.65), channel_id=1, source_target_pairs={{0,1},{4,5},{8,9},{12,13},{16,17},{20,21},{24,25},{28,29}} | collective-permute-start | bytes 1769480 | tf_op jit(solution)/shard_map/ppermute | solution.py:45
  268.5 45.2 %collective-permute-start.16 = (bf16[128,2304]{1,0:T(8,128)(2,1)}, bf16[128,2304]{1,0:T(8,128)(2,1)}, u32[]{:S(2)}, u32[]{:S(2)}) collective-permute-start(bf16[128,2304]{1,0:T(8,128)(2,1)} %get-tuple-element.68), channel_id=1, source_target_pairs={{2,1},{3,2},{6,5},{7,6},{10,9},{11,10},{14,13},{15,14},{18,17},{19... | collective-permute-start | bytes 1769480 | tf_op jit(solution)/shard_map/ppermute | solution.py:45
  269.9 43.8 %collective-permute-start.15 = (bf16[128,2304]{1,0:T(8,128)(2,1)}, bf16[128,2304]{1,0:T(8,128)(2,1)}, u32[]{:S(2)}, u32[]{:S(2)}) collective-permute-start(bf16[128,2304]{1,0:T(8,128)(2,1)} %get-tuple-element.67), channel_id=1, source_target_pairs={{0,1},{1,2},{4,5},{5,6},{8,9},{9,10},{12,13},{13,14},{16,17},{17,1... | collective-permute-start | bytes 1769480 | tf_op jit(solution)/shard_map/ppermute | solution.py:45
  275.0 19.4 %collective-permute-start.30 = (bf16[288,512]{1,0:T(8,128)(2,1)S(1)}, bf16[288,512]{1,0:T(8,128)(2,1)S(1)}, u32[]{:S(2)}, u32[]{:S(2)}) collective-permute-start(bf16[288,512]{1,0:T(8,128)(2,1)S(1)} %copy-done.36), channel_id=1, source_target_pairs={{0,3},{1,0},{2,1},{3,2},{4,7},{5,4},{6,5},{7,6},{8,11},{9,8},{10,9... | collective-permute-start | bytes 884744 | tf_op jit(solution)/shard_map/ppermute | solution.py:50
  276.8 35.6 %collective-permute-start.29 = (bf16[288,512]{1,0:T(8,128)(2,1)S(1)}, bf16[288,512]{1,0:T(8,128)(2,1)S(1)}, u32[]{:S(2)}, u32[]{:S(2)}) collective-permute-start(bf16[288,512]{1,0:T(8,128)(2,1)S(1)} %copy-done.36), channel_id=1, source_target_pairs={{0,2},{1,3},{2,0},{3,1},{4,6},{5,7},{6,4},{7,5},{8,10},{9,11},{10,... | collective-permute-start | bytes 884744 | tf_op jit(solution)/shard_map/ppermute | solution.py:50
  278.3 34.1 %collective-permute-start.28 = (bf16[288,512]{1,0:T(8,128)(2,1)S(1)}, bf16[288,512]{1,0:T(8,128)(2,1)S(1)}, u32[]{:S(2)}, u32[]{:S(2)}) collective-permute-start(bf16[288,512]{1,0:T(8,128)(2,1)S(1)} %copy-done.36), channel_id=1, source_target_pairs={{0,1},{1,2},{2,3},{3,0},{4,5},{5,6},{6,7},{7,4},{8,9},{9,10},{10,1... | collective-permute-start | bytes 884744 | tf_op jit(solution)/shard_map/ppermute | solution.py:50
  313.6 426.5 %reduce-scatter.4.cloned.1.call-start = ((), (), s32[]{:S(2)}) async-start(), calls=%async_computation.6 | async-start | bytes 4423680 | tf_op jit(solution)/shard_map/reduce_scatter | solution.py:208
  316.4 16.0 %collective-permute-start.18 = (bf16[128,2304]{1,0:T(8,128)(2,1)}, bf16[128,2304]{1,0:T(8,128)(2,1)}, u32[]{:S(2)}, u32[]{:S(2)}) collective-permute-start(bf16[128,2304]{1,0:T(8,128)(2,1)} %get-tuple-element.70), channel_id=1, source_target_pairs={{1,0},{2,1},{3,2},{5,4},{6,5},{7,6},{9,8},{10,9},{11,10},{13,12},{... | collective-permute-start | bytes 1769480 | tf_op jit(solution)/shard_map/ppermute | solution.py:45
  317.7 15.9 %collective-permute-start.17 = (bf16[128,2304]{1,0:T(8,128)(2,1)}, bf16[128,2304]{1,0:T(8,128)(2,1)}, u32[]{:S(2)}, u32[]{:S(2)}) collective-permute-start(bf16[128,2304]{1,0:T(8,128)(2,1)} %get-tuple-element.69), channel_id=1, source_target_pairs={{0,1},{1,2},{2,3},{4,5},{5,6},{6,7},{8,9},{9,10},{10,11},{12,13},{... | collective-permute-start | bytes 1769480 | tf_op jit(solution)/shard_map/ppermute | solution.py:45
  337.9 14.5 %collective-permute-start.19 = (bf16[128,2304]{1,0:T(8,128)(2,1)S(1)}, bf16[128,2304]{1,0:T(8,128)(2,1)}, u32[]{:S(2)}, u32[]{:S(2)}) collective-permute-start(bf16[128,2304]{1,0:T(8,128)(2,1)S(1)} %get-tuple-element.117), channel_id=1, source_target_pairs={{0,1},{1,2},{2,3},{4,5},{5,6},{6,7},{8,9},{9,10},{10,11},{12,13},{... | collective-permute-start | bytes 1769480 | tf_op jit(solution)/shard_map/ppermute | solution.py:45
  343.1 14.3 %collective-permute-start.20 = (bf16[128,2304]{1,0:T(8,128)(2,1)S(1)}, bf16[128,2304]{1,0:T(8,128)(2,1)}, u32[]{:S(2)}, u32[]{:S(2)}) collective-permute-start(bf16[128,2304]{1,0:T(8,128)(2,1)S(1)} %get-tuple-element.117), channel_id=1, source_target_pairs={{1,0},{2,1},{3,2},{5,4},{6,5},{7,6},{9,8},{10,9},{11,10},{13,12},{... | collective-permute-start | bytes 1769480 | tf_op jit(solution)/shard_map/ppermute | solution.py:45
  359.0 16.3 %collective-permute-start.22 = (bf16[128,2304]{1,0:T(8,128)(2,1)}, bf16[128,2304]{1,0:T(8,128)(2,1)}, u32[]{:S(2)}, u32[]{:S(2)}) collective-permute-start(bf16[128,2304]{1,0:T(8,128)(2,1)} %collective-permute-done.20), channel_id=1, source_target_pairs={{1,0},{2,1},{5,4},{6,5},{9,8},{10,9},{13,12},{14,13},{17,16},{18,1... | collective-permute-start | bytes 1769480 | tf_op jit(solution)/shard_map/ppermute | solution.py:45
  376.0 12.5 %collective-permute-start.24 = (bf16[128,2304]{1,0:T(8,128)(2,1)}, bf16[128,2304]{1,0:T(8,128)(2,1)S(1)}, u32[]{:S(2)}, u32[]{:S(2)}) collective-permute-start(bf16[128,2304]{1,0:T(8,128)(2,1)} %collective-permute-done.22), channel_id=1, source_target_pairs={{1,0},{5,4},{9,8},{13,12},{17,16},{21,20},{25,24},{29,28}} | collective-permute-start | bytes 1769480 | tf_op jit(solution)/shard_map/ppermute | solution.py:45
  433.5 18.1 %collective-permute-start.27 = (bf16[128,2304]{1,0:T(8,128)(2,1)S(1)}, bf16[128,2304]{1,0:T(8,128)(2,1)S(1)}, u32[]{:S(2)}, u32[]{:S(2)}) collective-permute-start(bf16[128,2304]{1,0:T(8,128)(2,1)S(1)} %get-tuple-element.81), channel_id=1, source_target_pairs={{0,1},{1,2},{2,3},{3,0},{4,5},{5,6},{6,7},{7,4},{8,9},{9,10},{10,1... | collective-permute-start | bytes 1769480 | tf_op jit(solution)/shard_map/ppermute | solution.py:50
  434.3 26.0 %collective-permute-start.26 = (bf16[128,2304]{1,0:T(8,128)(2,1)S(1)}, bf16[128,2304]{1,0:T(8,128)(2,1)S(1)}, u32[]{:S(2)}, u32[]{:S(2)}) collective-permute-start(bf16[128,2304]{1,0:T(8,128)(2,1)S(1)} %get-tuple-element.80), channel_id=1, source_target_pairs={{0,3},{1,0},{2,1},{3,2},{4,7},{5,4},{6,5},{7,6},{8,11},{9,8},{10,9... | collective-permute-start | bytes 1769480 | tf_op jit(solution)/shard_map/ppermute | solution.py:50
  437.5 43.9 %collective-permute-start.25 = (bf16[128,2304]{1,0:T(8,128)(2,1)S(1)}, bf16[128,2304]{1,0:T(8,128)(2,1)S(1)}, u32[]{:S(2)}, u32[]{:S(2)}) collective-permute-start(bf16[128,2304]{1,0:T(8,128)(2,1)S(1)} %get-tuple-element.79), channel_id=1, source_target_pairs={{0,2},{1,3},{2,0},{3,1},{4,6},{5,7},{6,4},{7,5},{8,10},{9,11},{10,... | collective-permute-start | bytes 1769480 | tf_op jit(solution)/shard_map/ppermute | solution.py:50
  490.6 10.2 %collective-permute-start.31 = (bf16[128,512]{1,0:T(8,128)(2,1)S(1)}, bf16[128,512]{1,0:T(8,128)(2,1)S(1)}, u32[]{:S(2)}, u32[]{:S(2)}) collective-permute-start(bf16[128,512]{1,0:T(8,128)(2,1)S(1)} %get-tuple-element.83), channel_id=1, source_target_pairs={{0,2},{1,3},{2,0},{3,1},{4,6},{5,7},{6,4},{7,5},{8,10},{9,11},{10,... | collective-permute-start | bytes 393224 | tf_op jit(solution)/shard_map/ppermute | solution.py:50
  490.7 10.1 %collective-permute-start.32 = (bf16[128,512]{1,0:T(8,128)(2,1)S(1)}, bf16[128,512]{1,0:T(8,128)(2,1)S(1)}, u32[]{:S(2)}, u32[]{:S(2)}) collective-permute-start(bf16[128,512]{1,0:T(8,128)(2,1)S(1)} %get-tuple-element.84), channel_id=1, source_target_pairs={{0,3},{1,0},{2,1},{3,2},{4,7},{5,4},{6,5},{7,6},{8,11},{9,8},{10,9... | collective-permute-start | bytes 393224 | tf_op jit(solution)/shard_map/ppermute | solution.py:50
  491.7 9.1 %collective-permute-start.33 = (bf16[128,512]{1,0:T(8,128)(2,1)S(1)}, bf16[128,512]{1,0:T(8,128)(2,1)S(1)}, u32[]{:S(2)}, u32[]{:S(2)}) collective-permute-start(bf16[128,512]{1,0:T(8,128)(2,1)S(1)} %get-tuple-element.85), channel_id=1, source_target_pairs={{0,1},{1,2},{2,3},{3,0},{4,5},{5,6},{6,7},{7,4},{8,9},{9,10},{10,1... | collective-permute-start | bytes 393224 | tf_op jit(solution)/shard_map/ppermute | solution.py:50
  500.9 45.6 %collective-permute-start.47 = (bf16[128,2304]{1,0:T(8,128)(2,1)S(1)}, bf16[128,2304]{1,0:T(8,128)(2,1)}, u32[]{:S(2)}, u32[]{:S(2)}) collective-permute-start(bf16[128,2304]{1,0:T(8,128)(2,1)S(1)} %fusion.69), channel_id=1, source_target_pairs={{0,1},{1,2},{2,3},{3,0},{4,5},{5,6},{6,7},{7,4},{8,9},{9,10},{10,1... | collective-permute-start | bytes 1769480 | tf_op jit(solution)/shard_map/ppermute | solution.py:50
  522.4 25.3 %collective-permute-start.48 = (bf16[128,2304]{1,0:T(8,128)(2,1)S(1)}, bf16[128,2304]{1,0:T(8,128)(2,1)}, u32[]{:S(2)}, u32[]{:S(2)}) collective-permute-start(bf16[128,2304]{1,0:T(8,128)(2,1)S(1)} %fusion.69), channel_id=1, source_target_pairs={{0,2},{1,3},{2,0},{3,1},{4,6},{5,7},{6,4},{7,5},{8,10},{9,11},{10,... | collective-permute-start | bytes 1769480 | tf_op jit(solution)/shard_map/ppermute | solution.py:50
  522.4 26.4 %collective-permute-start.49 = (bf16[128,2304]{1,0:T(8,128)(2,1)S(1)}, bf16[128,2304]{1,0:T(8,128)(2,1)S(1)}, u32[]{:S(2)}, u32[]{:S(2)}) collective-permute-start(bf16[128,2304]{1,0:T(8,128)(2,1)S(1)} %fusion.69), channel_id=1, source_target_pairs={{0,3},{1,0},{2,1},{3,2},{4,7},{5,4},{6,5},{7,6},{8,11},{9,8},{10,9... | collective-permute-start | bytes 1769480 | tf_op jit(solution)/shard_map/ppermute | solution.py:50
  533.8 9.7 %collective-permute-start.34 = (bf16[384,512]{0,1:T(8,128)(2,1)S(1)}, bf16[384,512]{0,1:T(8,128)(2,1)S(1)}, u32[]{:S(2)}, u32[]{:S(2)}) collective-permute-start(bf16[384,512]{0,1:T(8,128)(2,1)S(1)} %fusion.93), channel_id=1, source_target_pairs={{4,0},{5,1},{6,2},{7,3},{12,8},{13,9},{14,10},{15,11},{20,16},{21,... | collective-permute-start | bytes 1179656 | tf_op jit(solution)/shard_map/ppermute | solution.py:21
  546.5 11.4 %collective-permute-start.46 = (bf16[1152,1024]{1,0:T(8,128)(2,1)}, bf16[1152,1024]{1,0:T(8,128)(2,1)}, u32[]{:S(2)}, u32[]{:S(2)}) collective-permute-start(bf16[1152,1024]{1,0:T(8,128)(2,1)} %convolution_convert_fusion.4), channel_id=1, source_target_pairs={{0,8},{8,0},{16,24},{24,16},{1,9},{9,1},{17,25},{25,17},{2,10},{10... | collective-permute-start | bytes 7077896 | tf_op jit(solution)/shard_map/ppermute | solution.py:199
  563.1 181.4 %reduce-scatter.8.cloned.1.call-start = ((), (), s32[]{:S(2)}) async-start(), calls=%async_computation.8 | async-start | bytes 6635520 | tf_op jit(solution)/shard_map/reduce_scatter | solution.py:208
  563.1 12.7 %collective-permute-start.52 = (bf16[1152,2304]{1,0:T(8,128)(2,1)}, bf16[1152,2304]{1,0:T(8,128)(2,1)}, u32[]{:S(2)}, u32[]{:S(2)}) collective-permute-start(bf16[1152,2304]{1,0:T(8,128)(2,1)} %convolution_convert_fusion.1), channel_id=1, source_target_pairs={{0,8},{8,0},{16,24},{24,16},{1,9},{9,1},{17,25},{25,17},{2,10},{10... | collective-permute-start | bytes 15925256 | tf_op jit(solution)/shard_map/ppermute | solution.py:199
  575.4 16.7 %collective-permute-start.51 = (bf16[1152,4608]{1,0:T(8,128)(2,1)}, bf16[1152,4608]{1,0:T(8,128)(2,1)}, u32[]{:S(2)}, u32[]{:S(2)}) collective-permute-start(bf16[1152,4608]{1,0:T(8,128)(2,1)} %convolution_convert_fusion), channel_id=1, source_target_pairs={{0,8},{8,0},{16,24},{24,16},{1,9},{9,1},{17,25},{25,17},{2,10},{10... | collective-permute-start | bytes 31850504 | tf_op jit(solution)/shard_map/ppermute | solution.py:199
  582.7 206.0 %reduce-scatter.6.cloned.1.call-start = ((), (), s32[]{:S(2)}) async-start(), calls=%async_computation.7 | async-start | bytes 13271040 | tf_op jit(solution)/shard_map/reduce_scatter | solution.py:208
  620.0 22.8 %collective-permute-start.37 = (bf16[128,2304]{1,0:T(8,128)(2,1)S(1)}, bf16[128,2304]{1,0:T(8,128)(2,1)S(1)}, u32[]{:S(2)}, u32[]{:S(2)}) collective-permute-start(bf16[128,2304]{1,0:T(8,128)(2,1)S(1)} %get-tuple-element.90), channel_id=1, source_target_pairs={{0,1},{1,2},{2,3},{3,0},{4,5},{5,6},{6,7},{7,4},{8,9},{9,10},{10,1... | collective-permute-start | bytes 1769480 | tf_op jit(solution)/shard_map/ppermute | solution.py:50
  626.0 27.7 %collective-permute-start.36 = (bf16[128,2304]{1,0:T(8,128)(2,1)S(1)}, bf16[128,2304]{1,0:T(8,128)(2,1)S(1)}, u32[]{:S(2)}, u32[]{:S(2)}) collective-permute-start(bf16[128,2304]{1,0:T(8,128)(2,1)S(1)} %get-tuple-element.89), channel_id=1, source_target_pairs={{0,3},{1,0},{2,1},{3,2},{4,7},{5,4},{6,5},{7,6},{8,11},{9,8},{10,9... | collective-permute-start | bytes 1769480 | tf_op jit(solution)/shard_map/ppermute | solution.py:50
  628.7 51.5 %collective-permute-start.35 = (bf16[128,2304]{1,0:T(8,128)(2,1)S(1)}, bf16[128,2304]{1,0:T(8,128)(2,1)S(1)}, u32[]{:S(2)}, u32[]{:S(2)}) collective-permute-start(bf16[128,2304]{1,0:T(8,128)(2,1)S(1)} %get-tuple-element.88), channel_id=1, source_target_pairs={{0,2},{1,3},{2,0},{3,1},{4,6},{5,7},{6,4},{7,5},{8,10},{9,11},{10,... | collective-permute-start | bytes 1769480 | tf_op jit(solution)/shard_map/ppermute | solution.py:50
  697.4 18.2 %collective-permute-start.38 = (bf16[128,2304]{1,0:T(8,128)(2,1)S(1)}, bf16[128,2304]{1,0:T(8,128)(2,1)S(1)}, u32[]{:S(2)}, u32[]{:S(2)}) collective-permute-start(bf16[128,2304]{1,0:T(8,128)(2,1)S(1)} %concatenate.85), channel_id=1, source_target_pairs={{0,1},{1,2},{2,3},{3,0},{4,5},{5,6},{6,7},{7,4},{8,9},{9,10},{10,1... | collective-permute-start | bytes 1769480 | tf_op jit(solution)/shard_map/ppermute | solution.py:50
  697.5 42.5 %collective-permute-start.39 = (bf16[128,2304]{1,0:T(8,128)(2,1)S(1)}, bf16[128,2304]{1,0:T(8,128)(2,1)S(1)}, u32[]{:S(2)}, u32[]{:S(2)}) collective-permute-start(bf16[128,2304]{1,0:T(8,128)(2,1)S(1)} %concatenate.85), channel_id=1, source_target_pairs={{0,2},{1,3},{2,0},{3,1},{4,6},{5,7},{6,4},{7,5},{8,10},{9,11},{10,... | collective-permute-start | bytes 1769480 | tf_op jit(solution)/shard_map/ppermute | solution.py:50
  698.1 41.9 %collective-permute-start.40 = (bf16[128,2304]{1,0:T(8,128)(2,1)S(1)}, bf16[128,2304]{1,0:T(8,128)(2,1)S(1)}, u32[]{:S(2)}, u32[]{:S(2)}) collective-permute-start(bf16[128,2304]{1,0:T(8,128)(2,1)S(1)} %concatenate.85), channel_id=1, source_target_pairs={{0,3},{1,0},{2,1},{3,2},{4,7},{5,4},{6,5},{7,6},{8,11},{9,8},{10,9... | collective-permute-start | bytes 1769480 | tf_op jit(solution)/shard_map/ppermute | solution.py:50
  (81 other events, 1093.4 us)
Sparse Core Ops, SparseCore 0:
  10.5 51.4 all-gather.3
  63.8 157.0 all-gather.5
  313.7 58.9 all-gather.7
  563.2 52.3 reduce-scatter.3
  618.5 61.8 reduce-scatter.7
  683.3 105.3 reduce-scatter.5

commit v9 on v8

--- a/solution.py
+++ b/solution.py
@@ -96,12 +96,6 @@
     return [block] + [
         jnp.where(rank >= k, rising[k], falling[size - k]) for k in range(1, size)
     ]
-
-
-def turned_blocks(partial):
-    size = lax.axis_size("tp")
-    blocks = partial.reshape(size, -1, partial.shape[-1])
-    return [blocks[k] for k in range(size)]
 
 
 def ordered_blocks(partial):
@@ -235,6 +229,7 @@
     qkv_width = heads_width + 2 * kv_width
     scaling = HD ** (-0.5)
     tp_size = lax.axis_size("tp")
+    tp_rank = lax.axis_index("tp")
     piece = length // tp_size
 
     attention_full = gather_rows(
@@ -273,10 +268,9 @@
     )
     hidden_in = by_core(hidden_in)
     normed_one = rms(hidden_in.astype(F32), pre_attention_gain).astype(LOW)
-    inputs_turned = jnp.concatenate(ordered_blocks(hidden_in), axis=0)
-    upstream_turned = by_core(jnp.concatenate(ordered_blocks(cotangent), axis=0))
-    inputs = inputs_turned[:piece].astype(F32)
-    upstream = upstream_turned[:piece].astype(F32)
+    upstream_all = by_core(cotangent)
+    inputs = lax.dynamic_slice_in_dim(hidden_in, tp_rank * piece, piece).astype(F32)
+    upstream = lax.dynamic_slice_in_dim(upstream_all, tp_rank * piece, piece).astype(F32)
 
     qkv_low = product(normed_one, qkv_full).astype(LOW)
     queries = qkv_low[:, :heads_width].reshape(length, kv_heads, repeats, HD)
@@ -293,23 +287,21 @@
     branch_one = scattered(
         ordered_blocks(transposed_product(attended_low, output_full).astype(LOW))
     )
-    branch_one_low = jnp.concatenate(gathered(branch_one.astype(LOW)), axis=0).astype(F32)
-    middle_turned = inputs_turned.astype(F32) + rms(branch_one_low, post_attention_gain)
-    middle = middle_turned[:piece]
-    normed_two = rms(middle_turned, pre_feedforward_gain).astype(LOW)
+    branch_one_all = in_order(gathered(branch_one.astype(LOW))).astype(F32)
+    middle_all = hidden_in.astype(F32) + rms(branch_one_all, post_attention_gain)
+    middle = lax.dynamic_slice_in_dim(middle_all, tp_rank * piece, piece)
+    normed_two = rms(middle_all, pre_feedforward_gain).astype(LOW)
 
     gate_up = product(normed_two, gate_up_full)
     gate_value = gate_up[:, :units]
     up_value = gate_up[:, units:]
     hidden_low = geglu(gate_value, up_value).astype(LOW)
-    branch_two = scattered(
-        turned_blocks(transposed_product(hidden_low, down_full).astype(LOW))
-    )
-    branch_two_low = jnp.concatenate(gathered(branch_two.astype(LOW)), axis=0).astype(F32)
-    unused_four, pull_four = jax.vjp(rms, branch_two_low, post_feedforward_gain)
-    grad_two_low = pull_four(upstream_turned.astype(F32))[0].astype(LOW)
-    unused_four, pull_four = jax.vjp(rms, branch_two, post_feedforward_gain)
-    grad_gain_four = pull_four(upstream)[1]
+    branch_two = lax.psum(transposed_product(hidden_low, down_full).astype(LOW), "tp")
+    branch_two = branch_two.astype(F32)
+    _, pull_four = jax.vjp(rms, branch_two, post_feedforward_gain)
+    grad_branch_two, grad_gain_four = pull_four(upstream_all.astype(F32))
+    grad_gain_four = grad_gain_four / tp_size
+    grad_two_low = grad_branch_two.astype(LOW)
 
     down_sent, grad_two_low = lax.optimization_barrier(
         (sent_to_core(grad_two_low, hidden_low), grad_two_low)
@@ -319,9 +311,8 @@
     grad_gate, grad_up = pull_glu(product(grad_two_low, down_full))
     grad_gate_up = jnp.concatenate([grad_gate.astype(LOW), grad_up.astype(LOW)], axis=1)
     grad_normed_two = transposed_product(grad_gate_up, gate_up_full).astype(LOW)
-    grad_normed_two = sent_scattered(turned_blocks(grad_normed_two))
-    result = (middle_turned + rms(branch_two_low, post_feedforward_gain)).astype(LOW)
-    outputs = in_order(turned_blocks(by_chip(result)))
+    grad_normed_two = sent_scattered(ordered_blocks(grad_normed_two))
+    outputs = by_chip((middle_all + rms(branch_two, post_feedforward_gain)).astype(LOW))
     grad_down_low = chip_rows(grad_two_low, hidden_low, down_arrived)
     down_share = share_rows(grad_down_low)
     gate_up_sent = sent_to_core(normed_two, grad_gate_up)
@@ -372,6 +363,12 @@
     grad_kv_low = (grad_kv_all[before:] + grad_kv_back).astype(LOW)
     grad_qkv = jnp.concatenate([grad_query_low, grad_kv_low], axis=1)
     grad_normed_one = transposed_product(grad_qkv, qkv_full).astype(LOW)
+    unused_one, pull_one = jax.vjp(rms, hidden_in.astype(F32), pre_attention_gain)
+    grad_gain_one = pull_one(grad_normed_one.astype(F32))[1]
+    gains = by_chip(jnp.stack([grad_gain_one, grad_gain_two, grad_gain_three, grad_gain_four]))
+    for axis in ROWS:
+        gains = summed(gains, axis)
+    gains = sum((shift(gains, k) for k in range(1, tp_size)), gains)
     grad_normed_one = sent_scattered(ordered_blocks(grad_normed_one))
     qkv_sent = sent_to_core(normed_one, grad_qkv)
     qkv_arrived = over_cores(qkv_sent)
@@ -379,14 +376,10 @@
     grad_attention = by_rows(jnp.concatenate([grad_qkv_low, grad_output_low], axis=1))
     attention_share = share_rows(grad_attention).astype(F32)
 
-    _, pull_one = jax.vjp(rms, inputs, pre_attention_gain)
-    grad_inputs_norm, grad_gain_one = pull_one(grad_normed_one)
-    grad_inputs_low = by_chip((grad_middle + grad_inputs_norm).astype(LOW))
+    unused_one, pull_one = jax.vjp(rms, inputs, pre_attention_gain)
+    grad_inputs_low = by_chip((grad_middle + pull_one(grad_normed_one)[0]).astype(LOW))
     grad_inputs = in_order(sent_gathered(grad_inputs_low))
 
-    gains = by_chip(jnp.stack([grad_gain_one, grad_gain_two, grad_gain_three, grad_gain_four]))
-    for axis in ("tp",) + ROWS:
-        gains = summed(gains, axis)
     share = hidden_in.shape[1] // (lax.axis_size("fsdp") * lax.axis_size("ctx"))
     row_rank = lax.axis_index("fsdp") * lax.axis_size("ctx") + lax.axis_index("ctx")
     gain_shares = lax.dynamic_slice_in_dim(gains, row_rank * share, share, axis=1)

time: 811 us -> 805 us (level)
  waiting for transfers between devices: 421 us -> 400 us
  other arithmetic: 54.8 us -> 67.2 us
    ppermute x24 -> x12, waiting for transfers between devices: 112 us -> 51.3 us  [onward(): return lax.ppermute(block, 'tp', [(i, i + distance) for i in senders])]
    psum x0 -> x1, waiting for transfers between devices: none -> 52.5 us  [shards(): lax.psum(transposed_product(hidden_low, down_full).astype(LOW), 'tp')]
    ppermute x24 -> x12, starting transfers between devices: 58.2 us -> 30.3 us  [onward(): return lax.ppermute(block, 'tp', [(i, i + distance) for i in senders])]
    ppermute x18 -> x21, starting transfers between devices: 46.4 us -> 68.1 us  [shift(): lax.ppermute(block, 'tp', [(i, (i + distance) % size) for i in range(size)])]
    all_gather x3, waiting for transfers between devices: 59.8 us -> 47.7 us  [gather_rows(): lax.all_gather(weight, ROWS, axis=0, tiled=True, axis_index_groups=[first...]
    ppermute x18 -> x21, waiting for transfers between devices: 169 us -> 176 us  [shift(): lax.ppermute(block, 'tp', [(i, (i + distance) % size) for i in range(size)])]
    concatenate x9 -> x10, local copies, waits for them, and re-layouts: 16.1 us -> 23.1 us  [swapped(): jnp.concatenate([value[..., k * part:(k + 1) * part] for k in order], axi...]
    unnamed x140 -> x132, local copies, waits for them, and re-layouts: 16.3 us -> 12.4 us
  transfers between devices with their start and end apart: 59 -> 49, of which waited for: 36 -> 28; matrix products, arithmetic and copies ran while one was open for 23% -> 27% of each run, Pallas kernels for 0% -> 0%
where the time goes in v9:
time: 805 us; the launch traced here: 795 us
  waiting for transfers between devices  400 us (50%)
  matrix products  138 us (17%)
  starting transfers between devices  108 us (13%)
  other arithmetic  67.2 us (8%)
  local copies, waits for them, and re-layouts  65.6 us (8%)
  between operations  15.8 us (2%)
    ppermute x21, waiting for transfers between devices, shift(): lax.ppermute(block, 'tp', [(i, (i + distance) % size) for i in range(size)])  176 us
    ppermute x21, starting transfers between devices, shift(): lax.ppermute(block, 'tp', [(i, (i + distance) % size) for i in range(size)])  68.1 us
    psum x1, waiting for transfers between devices, shards(): lax.psum(transposed_product(hidden_low, down_full).astype(LOW), 'tp')  52.5 us
    ppermute x12, waiting for transfers between devices, onward(): return lax.ppermute(block, 'tp', [(i, i + distance) for i in senders])  51.3 us
    all_gather x3, waiting for transfers between devices, gather_rows(): lax.all_gather(weight, ROWS, axis=0, tiled=True, axis_index_groups=[first...  47.7 us
    dot_general x8, matrix products, rows_product(): lax.dot_general(left, right, (((0,), (0,)), ((), ())), preferred_element_...  46.9 us
    reduce_scatter x3, waiting for transfers between devices, share_rows(): lax.psum_scatter(grad, ROWS, scatter_dimension=0, tiled=True, axis_index_...  39.2 us
    dot_general x4, matrix products, product(): return jnp.dot(left, right, preferred_element_type=F32)  38.7 us
  transfers between devices with their start and end apart: 49, of which 28 were waited for; matrix products, arithmetic and copies ran while one was open for 27% of the time, Pallas kernels for 0%

profile of v9, /device:TPU:0, one launch (start us, length us, event | category | flops | bytes accessed | tf_op | source)
XLA Modules:
  0.0 794.7 jit_solution(6919009710136904240)
XLA Ops:
  16.3 4.2 concatenate.65
  23.4 38.5 %all-gather.4.cloned.1.call-done = bf16[2304,1536]{1,0:T(8,128)(2,1)} async-done(((bf16[288,1536]{1,0:T(8,128)(2,1)}), bf16[2304,1536]{1,0:T(8,128)(2,1)}) %all-gather.4.cloned.1.call-update) | async-done | bytes 7077904 | tf_op jit(solution)/shard_map/all_gather | solution.py:177
  61.9 5.7 fusion.53
  68.4 4.1 collective-permute-start
  75.2 11.4 %collective-permute-done = bf16[384,512]{1,0:T(8,128)(2,1)} collective-permute-done((bf16[384,512]{1,0:T(8,128)(2,1)}, bf16[384,512]{1,0:T(8,128)(2,1)}, u32[]{:S(2)}, u32[]{:S(2)}) %collective-permute-start) | collective-permute-done | bytes 393248 | tf_op jit(solution)/shard_map/ppermute | solution.py:21
  98.3 4.0 collective-permute-start.1
  102.3 9.8 %collective-permute-done.1 = bf16[128,2304]{1,0:T(8,128)(2,1)} collective-permute-done((bf16[128,2304]{1,0:T(8,128)(2,1)S(1)}, bf16[128,2304]{1,0:T(8,128)(2,1)}, u32[]{:S(2)}, u32[]{:S(2)}) %collective-permute-start.1) | collective-permute-done | bytes 589856 | tf_op jit(solution)/shard_map/ppermute | solution.py:45
  113.8 4.5 collective-permute-start.3
  119.0 9.1 %collective-permute-done.3 = bf16[128,2304]{1,0:T(8,128)(2,1)S(1)} collective-permute-done((bf16[128,2304]{1,0:T(8,128)(2,1)S(1)}, bf16[128,2304]{1,0:T(8,128)(2,1)S(1)}, u32[]{:S(2)}, u32[]{:S(2)}) %collective-permute-start.3) | collective-permute-done | bytes 589856 | tf_op jit(solution)/shard_map/ppermute | solution.py:45
  130.5 6.8 collective-permute-start.5
  137.3 7.0 collective-permute-done.6
  150.5 4.4 collective-permute-start.7
  156.5 6.6 collective-permute-done.7
  163.0 4.1 collective-permute-done.8
  170.0 12.0 %collective-permute-done.10 = bf16[128,2304]{1,0:T(8,128)(2,1)} collective-permute-done((bf16[128,2304]{1,0:T(8,128)(2,1)S(1)}, bf16[128,2304]{1,0:T(8,128)(2,1)}, u32[]{:S(2)}, u32[]{:S(2)}) %collective-permute-start.10) | collective-permute-done | bytes 589856 | tf_op jit(solution)/shard_map/ppermute | solution.py:45
  186.8 5.2 concatenate.75
  205.8 5.9 multiply_convert_fusion.2
  211.7 9.2 %all-gather.6.cloned.1.call-done = bf16[2304,6912]{1,0:T(8,128)(2,1)} async-done(((bf16[288,6912]{1,0:T(8,128)(2,1)}), bf16[2304,6912]{1,0:T(8,128)(2,1)}) %all-gather.6.cloned.1.call-update) | async-done | bytes 31850512 | tf_op jit(solution)/shard_map/all_gather | solution.py:177
  220.9 15.2 %fusion.2 = f32[512,4608]{1,0:T(8,128)S(1)} fusion(bf16[512,2304]{1,0:T(8,128)(2,1)} %get-tuple-element.84, bf16[2304,6912]{1,0:T(8,128)(2,1)} %all-gather.6.cloned.1.call-done), kind=kOutput, calls=%fused_computation.4 | convolution fusion | flops 10871635968 | bytes 33030144 | tf_op jit(solution)/shard_map/dot_general | solution.py:33
  241.1 11.0 %fusion.29 = bf16[512,2304]{1,0:T(8,128)(2,1)} fusion(bf16[512,2304]{1,0:T(8,128)(2,1)S(1)} %multiply_convert_fusion.1, bf16[2304,6912]{1,0:T(8,128)(2,1)} %all-gather.6.cloned.1.call-done), kind=kOutput, calls=%fused_computation.53 | convolution fusion | flops 5436997632 | bytes 15335424 | tf_op jit(solution)/shard_map/dot_general | solution.py:41
  256.6 12.4 %collective-permute-done.18 = bf16[288,512]{1,0:T(8,128)(2,1)S(1)} collective-permute-done((bf16[288,512]{1,0:T(8,128)(2,1)}, bf16[288,512]{1,0:T(8,128)(2,1)S(1)}, u32[]{:S(2)}, u32[]{:S(2)}) %collective-permute-start.18) | collective-permute-done | bytes 294944 | tf_op jit(solution)/shard_map/ppermute | solution.py:50
  269.0 35.7 %collective-permute-done.17 = bf16[288,512]{1,0:T(8,128)(2,1)S(1)} collective-permute-done((bf16[288,512]{1,0:T(8,128)(2,1)}, bf16[288,512]{1,0:T(8,128)(2,1)S(1)}, u32[]{:S(2)}, u32[]{:S(2)}) %collective-permute-start.17) | collective-permute-done | bytes 294944 | tf_op jit(solution)/shard_map/ppermute | solution.py:50
  309.4 4.1 concatenate.80
  316.4 52.5 %all-reduce.3.cloned.1.call-done = bf16[512,2304]{1,0:T(8,128)(2,1)} async-done(((bf16[512,2304]{1,0:T(8,128)(2,1)}), bf16[512,2304]{1,0:T(8,128)(2,1)}) %all-reduce.3.cloned.1.call-update) | async-done | bytes 2359312 | tf_op jit(solution)/shard_map/psum | solution.py:299
  374.7 5.3 fusion.25
  380.0 5.1 convolution_convert_fusion.1
  385.2 12.8 %fusion.23 = (bf16[512,2304]{1,0:T(8,128)(2,1)S(1)}, bf16[512,2304]{1,0:T(8,128)(2,1)}) fusion(f32[512,4608]{1,0:T(8,128)S(1)} %bitcast.196, bf16[512,2304]{1,0:T(8,128)(2,1)S(1)} %get-tuple-element.53, bf16[2304,6912]{1,0:T(8,128)(2,1)} %all-gather.6.cloned.1.call-done), kind=kOutput, calls=%fused_computation.39 | convolution fusion | flops 5464129536 | bytes 27131904 | tf_op jit(solution)/shard_map/dot_general | solution.py:33
  398.0 17.2 %fusion.32 = bf16[512,2304]{1,0:T(8,128)(2,1)S(1)} fusion(bf16[2304,6912]{1,0:T(8,128)(2,1)} %all-gather.6.cloned.1.call-done, bf16[512,2304]{1,0:T(8,128)(2,1)} %get-tuple-element.91, bf16[512,2304]{1,0:T(8,128)(2,1)S(1)} %get-tuple-element.90), kind=kOutput, calls=%fused_computation.54 | convolution fusion | flops 10882252800 | bytes 28311552 | tf_op jit(solution)/shard_map/dot_general | solution.py:41
  422.4 12.6 %collective-permute-done.15 = bf16[128,2304]{1,0:T(8,128)(2,1)} collective-permute-done((bf16[128,2304]{1,0:T(8,128)(2,1)}, bf16[128,2304]{1,0:T(8,128)(2,1)}, u32[]{:S(2)}, u32[]{:S(2)}) %collective-permute-start.15) | collective-permute-done | bytes 589856 | tf_op jit(solution)/shard_map/ppermute | solution.py:50
  435.0 10.0 %collective-permute-done.14 = bf16[128,2304]{1,0:T(8,128)(2,1)} collective-permute-done((bf16[128,2304]{1,0:T(8,128)(2,1)}, bf16[128,2304]{1,0:T(8,128)(2,1)}, u32[]{:S(2)}, u32[]{:S(2)}) %collective-permute-start.14) | collective-permute-done | bytes 589856 | tf_op jit(solution)/shard_map/ppermute | solution.py:50
  445.0 26.2 %collective-permute-done.13 = bf16[128,2304]{1,0:T(8,128)(2,1)} collective-permute-done((bf16[128,2304]{1,0:T(8,128)(2,1)}, bf16[128,2304]{1,0:T(8,128)(2,1)}, u32[]{:S(2)}, u32[]{:S(2)}) %collective-permute-start.13) | collective-permute-done | bytes 589856 | tf_op jit(solution)/shard_map/ppermute | solution.py:50
  478.9 5.1 convolution_convert_fusion.6
  486.3 8.0 %collective-permute-done.19 = bf16[128,512]{1,0:T(8,128)(2,1)S(1)} collective-permute-done((bf16[128,512]{1,0:T(8,128)(2,1)S(1)}, bf16[128,512]{1,0:T(8,128)(2,1)S(1)}, u32[]{:S(2)}, u32[]{:S(2)}) %collective-permute-start.19) | collective-permute-done | bytes 131104 | tf_op jit(solution)/shard_map/ppermute | solution.py:50
  494.7 21.5 %collective-permute-start.36 = (bf16[128,2304]{1,0:T(8,128)(2,1)S(1)}, bf16[128,2304]{1,0:T(8,128)(2,1)S(1)}, u32[]{:S(2)}, u32[]{:S(2)}) collective-permute-start(bf16[128,2304]{1,0:T(8,128)(2,1)S(1)} %fusion.69), channel_id=1, source_target_pairs={{0,1},{1,2},{2,3},{3,0},{4,5},{5,6},{6,7},{7,4},{8,9},{9,10},{10,1... | collective-permute-start | bytes 1769480 | tf_op jit(solution)/shard_map/ppermute | solution.py:50
  532.2 6.1 collective-permute-done.22
  557.4 10.7 %convolution_convert_fusion = bf16[1152,4608]{1,0:T(8,128)(2,1)} fusion(bf16[512,2304]{1,0:T(8,128)(2,1)} %get-tuple-element.91, bf16[512,2304]{1,0:T(8,128)(2,1)} %copy-done.62, bf16[512,2304]{1,0:T(8,128)(2,1)S(1)} %copy-done.18, s32[]{:T(128)S(6)} %select_n.212), kind=kOutput, calls=%fused_computation.1 | convolution fusion | flops 5450563584 | bytes 16515076 | tf_op jit(solution)/shard_map/dot_general | solution.py:37
  568.5 7.3 add_convert_fusion.1
  576.1 8.7 %collective-permute-done.40 = bf16[1152,4608]{1,0:T(8,128)(2,1)} collective-permute-done((bf16[1152,4608]{1,0:T(8,128)(2,1)}, bf16[1152,4608]{1,0:T(8,128)(2,1)}, u32[]{:S(2)}, u32[]{:S(2)}) %collective-permute-start.40) | collective-permute-done | bytes 10616864 | tf_op jit(solution)/shard_map/ppermute | solution.py:193
  584.8 13.4 %add_convert_fusion = bf16[1152,4608]{1,0:T(8,128)(2,1)} fusion(bf16[1152,4608]{1,0:T(8,128)(2,1)} %collective-permute-done.40, bf16[512,2304]{1,0:T(8,128)(2,1)} %get-tuple-element.91, bf16[512,2304]{1,0:T(8,128)(2,1)} %copy-done.62, bf16[512,2304]{1,0:T(8,128)(2,1)S(1)} %copy-done.18, s32[]{:T(128)S(6)} %select_n.221), kind=kOutput, calls=%fused_computation | convolution fusion | flops 5461180416 | bytes 27131908 | tf_op jit(solution)/shard_map/dot_general | solution.py:37
  600.0 6.9 fusion.15
  615.6 8.5 %collective-permute-start.25 = (bf16[128,2304]{1,0:T(8,128)(2,1)}, bf16[128,2304]{1,0:T(8,128)(2,1)S(1)}, u32[]{:S(2)}, u32[]{:S(2)}) collective-permute-start(bf16[128,2304]{1,0:T(8,128)(2,1)} %get-tuple-element.66), channel_id=1, source_target_pairs={{0,1},{1,2},{2,3},{3,0},{4,5},{5,6},{6,7},{7,4},{8,9},{9,10},{10,1... | collective-permute-start | bytes 1769480 | tf_op jit(solution)/shard_map/ppermute | solution.py:50
  629.7 33.0 %collective-permute-done.34 = f32[4,2304]{1,0:T(4,128)} collective-permute-done((f32[4,2304]{1,0:T(4,128)}, f32[4,2304]{1,0:T(4,128)}, u32[]{:S(2)}, u32[]{:S(2)}) %collective-permute-start.34) | collective-permute-done | bytes 36896 | tf_op jit(solution)/shard_map/ppermute | solution.py:50
  662.7 16.0 %collective-permute-start.33 = (f32[4,2304]{1,0:T(4,128)}, f32[4,2304]{1,0:T(4,128)}, u32[]{:S(2)}, u32[]{:S(2)}) collective-permute-start(f32[4,2304]{1,0:T(4,128)} %add.367), channel_id=1, source_target_pairs={{0,2},{1,3},{2,0},{3,1},{4,6},{5,7},{6,4},{7,5},{8,10},{9,11},{10,... | collective-permute-start | bytes 110600 | tf_op jit(solution)/shard_map/ppermute | solution.py:50
  682.6 5.4 concatenate.79
  698.2 14.0 %collective-permute-done.26 = bf16[128,2304]{1,0:T(8,128)(2,1)S(1)} collective-permute-done((bf16[128,2304]{1,0:T(8,128)(2,1)S(1)}, bf16[128,2304]{1,0:T(8,128)(2,1)S(1)}, u32[]{:S(2)}, u32[]{:S(2)}) %collective-permute-start.26) | collective-permute-done | bytes 589856 | tf_op jit(solution)/shard_map/ppermute | solution.py:50
  712.3 23.9 %collective-permute-done.27 = bf16[128,2304]{1,0:T(8,128)(2,1)S(1)} collective-permute-done((bf16[128,2304]{1,0:T(8,128)(2,1)S(1)}, bf16[128,2304]{1,0:T(8,128)(2,1)S(1)}, u32[]{:S(2)}, u32[]{:S(2)}) %collective-permute-start.27) | collective-permute-done | bytes 589856 | tf_op jit(solution)/shard_map/ppermute | solution.py:50
  743.7 39.2 %reduce-scatter.6.cloned.1.call-done = bf16[288,4608]{1,0:T(8,128)(2,1)} async-done(((bf16[1152,4608]{1,0:T(8,128)(2,1)}), bf16[288,4608]{1,0:T(8,128)(2,1)}) %reduce-scatter.6.cloned.1.call-update) | async-done | bytes 2654224 | tf_op jit(solution)/shard_map/reduce_scatter | solution.py:202
  783.0 4.5 fusion.130
  (314 shorter events, 174.0 us)
Async XLA Ops:
  7.2 54.7 %all-gather.4.cloned.1.call-start = ((), (), s32[]{:S(2)}) async-start(), calls=%async_computation.3 | async-start | bytes 7962624 | tf_op jit(solution)/shard_map/all_gather | solution.py:177
  9.6 211.3 %all-gather.6.cloned.1.call-start = ((), (), s32[]{:S(2)}) async-start(), calls=%async_computation.4 | async-start | bytes 35831808 | tf_op jit(solution)/shard_map/all_gather | solution.py:177
  12.8 356.1 %all-reduce.3.cloned.1.call-start = ((), (), s32[]{:S(2)}) async-start(), calls=%async_computation.5 | async-start | bytes 4718592 | tf_op jit(solution)/shard_map/psum | solution.py:299
  68.4 18.3 %collective-permute-start = (bf16[384,512]{1,0:T(8,128)(2,1)}, bf16[384,512]{1,0:T(8,128)(2,1)}, u32[]{:S(2)}, u32[]{:S(2)}) collective-permute-start(bf16[384,512]{1,0:T(8,128)(2,1)} %slice.255), channel_id=1, source_target_pairs={{0,4},{1,5},{2,6},{3,7},{8,12},{9,13},{10,14},{11,15},{16,20},{17,... | collective-permute-start | bytes 1179656 | tf_op jit(solution)/shard_map/ppermute | solution.py:21
  96.9 5.4 collective-permute-start.2
  98.3 13.8 %collective-permute-start.1 = (bf16[128,2304]{1,0:T(8,128)(2,1)S(1)}, bf16[128,2304]{1,0:T(8,128)(2,1)}, u32[]{:S(2)}, u32[]{:S(2)}) collective-permute-start(bf16[128,2304]{1,0:T(8,128)(2,1)S(1)} %get-tuple-element.41), channel_id=1, source_target_pairs={{0,1},{4,5},{8,9},{12,13},{16,17},{20,21},{24,25},{28,29}} | collective-permute-start | bytes 1769480 | tf_op jit(solution)/shard_map/ppermute | solution.py:45
  113.8 14.3 %collective-permute-start.3 = (bf16[128,2304]{1,0:T(8,128)(2,1)S(1)}, bf16[128,2304]{1,0:T(8,128)(2,1)S(1)}, u32[]{:S(2)}, u32[]{:S(2)}) collective-permute-start(bf16[128,2304]{1,0:T(8,128)(2,1)S(1)} %get-tuple-element.43), channel_id=1, source_target_pairs={{0,1},{1,2},{4,5},{5,6},{8,9},{9,10},{12,13},{13,14},{16,17},{17,1... | collective-permute-start | bytes 1769480 | tf_op jit(solution)/shard_map/ppermute | solution.py:45
  118.3 10.7 %collective-permute-start.4 = (bf16[128,2304]{1,0:T(8,128)(2,1)S(1)}, bf16[128,2304]{1,0:T(8,128)(2,1)S(1)}, u32[]{:S(2)}, u32[]{:S(2)}) collective-permute-start(bf16[128,2304]{1,0:T(8,128)(2,1)S(1)} %get-tuple-element.44), channel_id=1, source_target_pairs={{2,1},{3,2},{6,5},{7,6},{10,9},{11,10},{14,13},{15,14},{18,17},{19... | collective-permute-start | bytes 1769480 | tf_op jit(solution)/shard_map/ppermute | solution.py:45
  129.2 15.1 %collective-permute-start.6 = (bf16[128,2304]{1,0:T(8,128)(2,1)S(1)}, bf16[128,2304]{1,0:T(8,128)(2,1)S(1)}, u32[]{:S(2)}, u32[]{:S(2)}) collective-permute-start(bf16[128,2304]{1,0:T(8,128)(2,1)S(1)} %add_convert_fusion.3), channel_id=1, source_target_pairs={{1,0},{2,1},{3,2},{5,4},{6,5},{7,6},{9,8},{10,9},{11,10},{13,12},{... | collective-permute-start | bytes 1769480 | tf_op jit(solution)/shard_map/ppermute | solution.py:45
  130.5 15.3 %collective-permute-start.5 = (bf16[128,2304]{1,0:T(8,128)(2,1)}, bf16[128,2304]{1,0:T(8,128)(2,1)}, u32[]{:S(2)}, u32[]{:S(2)}) collective-permute-start(bf16[128,2304]{1,0:T(8,128)(2,1)} %add_convert_fusion.4), channel_id=1, source_target_pairs={{0,1},{1,2},{2,3},{4,5},{5,6},{6,7},{8,9},{9,10},{10,11},{12,13},{... | collective-permute-start | bytes 1769480 | tf_op jit(solution)/shard_map/ppermute | solution.py:45
  150.5 12.5 %collective-permute-start.7 = (bf16[128,2304]{1,0:T(8,128)(2,1)S(1)}, bf16[128,2304]{1,0:T(8,128)(2,1)S(1)}, u32[]{:S(2)}, u32[]{:S(2)}) collective-permute-start(bf16[128,2304]{1,0:T(8,128)(2,1)S(1)} %get-tuple-element.87), channel_id=1, source_target_pairs={{0,1},{1,2},{2,3},{4,5},{5,6},{6,7},{8,9},{9,10},{10,11},{12,13},{... | collective-permute-start | bytes 1769480 | tf_op jit(solution)/shard_map/ppermute | solution.py:45
  154.9 12.2 %collective-permute-start.8 = (bf16[128,2304]{1,0:T(8,128)(2,1)S(1)}, bf16[128,2304]{1,0:T(8,128)(2,1)S(1)}, u32[]{:S(2)}, u32[]{:S(2)}) collective-permute-start(bf16[128,2304]{1,0:T(8,128)(2,1)S(1)} %get-tuple-element.87), channel_id=1, source_target_pairs={{1,0},{2,1},{3,2},{5,4},{6,5},{7,6},{9,8},{10,9},{11,10},{13,12},{... | collective-permute-start | bytes 1769480 | tf_op jit(solution)/shard_map/ppermute | solution.py:45
  167.2 2.8 collective-permute-start.9
  168.7 13.3 %collective-permute-start.10 = (bf16[128,2304]{1,0:T(8,128)(2,1)S(1)}, bf16[128,2304]{1,0:T(8,128)(2,1)}, u32[]{:S(2)}, u32[]{:S(2)}) collective-permute-start(bf16[128,2304]{1,0:T(8,128)(2,1)S(1)} %collective-permute-done.8), channel_id=1, source_target_pairs={{1,0},{2,1},{5,4},{6,5},{9,8},{10,9},{13,12},{14,13},{17,16},{18,1... | collective-permute-start | bytes 1769480 | tf_op jit(solution)/shard_map/ppermute | solution.py:45
  182.0 11.5 %collective-permute-start.11 = (bf16[128,2304]{1,0:T(8,128)(2,1)}, bf16[128,2304]{1,0:T(8,128)(2,1)}, u32[]{:S(2)}, u32[]{:S(2)}) collective-permute-start(bf16[128,2304]{1,0:T(8,128)(2,1)} %collective-permute-done.9), channel_id=1, source_target_pairs={{2,3},{6,7},{10,11},{14,15},{18,19},{22,23},{26,27},{30,31}} | collective-permute-start | bytes 1769480 | tf_op jit(solution)/shard_map/ppermute | solution.py:45
  183.5 12.1 %collective-permute-start.12 = (bf16[128,2304]{1,0:T(8,128)(2,1)}, bf16[128,2304]{1,0:T(8,128)(2,1)}, u32[]{:S(2)}, u32[]{:S(2)}) collective-permute-start(bf16[128,2304]{1,0:T(8,128)(2,1)} %collective-permute-done.10), channel_id=1, source_target_pairs={{1,0},{5,4},{9,8},{13,12},{17,16},{21,20},{25,24},{29,28}} | collective-permute-start | bytes 1769480 | tf_op jit(solution)/shard_map/ppermute | solution.py:45
  252.1 226.8 %all-gather.8.cloned.1.call-start = ((), (), s32[]{:S(2)}) async-start(), calls=%async_computation.6 | async-start | bytes 10616832 | tf_op jit(solution)/shard_map/all_gather | solution.py:177
  252.1 16.9 %collective-permute-start.18 = (bf16[288,512]{1,0:T(8,128)(2,1)}, bf16[288,512]{1,0:T(8,128)(2,1)S(1)}, u32[]{:S(2)}, u32[]{:S(2)}) collective-permute-start(bf16[288,512]{1,0:T(8,128)(2,1)} %param.24), channel_id=1, source_target_pairs={{0,3},{1,0},{2,1},{3,2},{4,7},{5,4},{6,5},{7,6},{8,11},{9,8},{10,9... | collective-permute-start | bytes 884744 | tf_op jit(solution)/shard_map/ppermute | solution.py:50
  255.5 49.2 %collective-permute-start.17 = (bf16[288,512]{1,0:T(8,128)(2,1)}, bf16[288,512]{1,0:T(8,128)(2,1)S(1)}, u32[]{:S(2)}, u32[]{:S(2)}) collective-permute-start(bf16[288,512]{1,0:T(8,128)(2,1)} %param.24), channel_id=1, source_target_pairs={{0,2},{1,3},{2,0},{3,1},{4,6},{5,7},{6,4},{7,5},{8,10},{9,11},{10,... | collective-permute-start | bytes 884744 | tf_op jit(solution)/shard_map/ppermute | solution.py:50
  255.5 49.2 %collective-permute-start.16 = (bf16[288,512]{1,0:T(8,128)(2,1)}, bf16[288,512]{1,0:T(8,128)(2,1)S(1)}, u32[]{:S(2)}, u32[]{:S(2)}) collective-permute-start(bf16[288,512]{1,0:T(8,128)(2,1)} %param.24), channel_id=1, source_target_pairs={{0,1},{1,2},{2,3},{3,0},{4,5},{5,6},{6,7},{7,4},{8,9},{9,10},{10,1... | collective-permute-start | bytes 884744 | tf_op jit(solution)/shard_map/ppermute | solution.py:50
  306.9 429.5 %reduce-scatter.4.cloned.1.call-start = ((), (), s32[]{:S(2)}) async-start(), calls=%async_computation.7 | async-start | bytes 4423680 | tf_op jit(solution)/shard_map/reduce_scatter | solution.py:202
  416.7 18.3 %collective-permute-start.15 = (bf16[128,2304]{1,0:T(8,128)(2,1)}, bf16[128,2304]{1,0:T(8,128)(2,1)}, u32[]{:S(2)}, u32[]{:S(2)}) collective-permute-start(bf16[128,2304]{1,0:T(8,128)(2,1)} %get-tuple-element.57), channel_id=1, source_target_pairs={{0,1},{1,2},{2,3},{3,0},{4,5},{5,6},{6,7},{7,4},{8,9},{9,10},{10,1... | collective-permute-start | bytes 1769480 | tf_op jit(solution)/shard_map/ppermute | solution.py:50
  417.1 27.9 %collective-permute-start.14 = (bf16[128,2304]{1,0:T(8,128)(2,1)}, bf16[128,2304]{1,0:T(8,128)(2,1)}, u32[]{:S(2)}, u32[]{:S(2)}) collective-permute-start(bf16[128,2304]{1,0:T(8,128)(2,1)} %get-tuple-element.56), channel_id=1, source_target_pairs={{0,3},{1,0},{2,1},{3,2},{4,7},{5,4},{6,5},{7,6},{8,11},{9,8},{10,9... | collective-permute-start | bytes 1769480 | tf_op jit(solution)/shard_map/ppermute | solution.py:50
  420.7 50.5 %collective-permute-start.13 = (bf16[128,2304]{1,0:T(8,128)(2,1)}, bf16[128,2304]{1,0:T(8,128)(2,1)}, u32[]{:S(2)}, u32[]{:S(2)}) collective-permute-start(bf16[128,2304]{1,0:T(8,128)(2,1)} %get-tuple-element.55), channel_id=1, source_target_pairs={{0,2},{1,3},{2,0},{3,1},{4,6},{5,7},{6,4},{7,5},{8,10},{9,11},{10,... | collective-permute-start | bytes 1769480 | tf_op jit(solution)/shard_map/ppermute | solution.py:50
  484.0 10.2 %collective-permute-start.19 = (bf16[128,512]{1,0:T(8,128)(2,1)S(1)}, bf16[128,512]{1,0:T(8,128)(2,1)S(1)}, u32[]{:S(2)}, u32[]{:S(2)}) collective-permute-start(bf16[128,512]{1,0:T(8,128)(2,1)S(1)} %get-tuple-element.59), channel_id=1, source_target_pairs={{0,2},{1,3},{2,0},{3,1},{4,6},{5,7},{6,4},{7,5},{8,10},{9,11},{10,... | collective-permute-start | bytes 393224 | tf_op jit(solution)/shard_map/ppermute | solution.py:50
  484.1 10.6 %collective-permute-start.20 = (bf16[128,512]{1,0:T(8,128)(2,1)S(1)}, bf16[128,512]{1,0:T(8,128)(2,1)S(1)}, u32[]{:S(2)}, u32[]{:S(2)}) collective-permute-start(bf16[128,512]{1,0:T(8,128)(2,1)S(1)} %get-tuple-element.60), channel_id=1, source_target_pairs={{0,3},{1,0},{2,1},{3,2},{4,7},{5,4},{6,5},{7,6},{8,11},{9,8},{10,9... | collective-permute-start | bytes 393224 | tf_op jit(solution)/shard_map/ppermute | solution.py:50
  485.2 9.5 %collective-permute-start.21 = (bf16[128,512]{1,0:T(8,128)(2,1)S(1)}, bf16[128,512]{1,0:T(8,128)(2,1)S(1)}, u32[]{:S(2)}, u32[]{:S(2)}) collective-permute-start(bf16[128,512]{1,0:T(8,128)(2,1)S(1)} %get-tuple-element.61), channel_id=1, source_target_pairs={{0,1},{1,2},{2,3},{3,0},{4,5},{5,6},{6,7},{7,4},{8,9},{9,10},{10,1... | collective-permute-start | bytes 393224 | tf_op jit(solution)/shard_map/ppermute | solution.py:50
  494.7 46.6 %collective-permute-start.36 = (bf16[128,2304]{1,0:T(8,128)(2,1)S(1)}, bf16[128,2304]{1,0:T(8,128)(2,1)S(1)}, u32[]{:S(2)}, u32[]{:S(2)}) collective-permute-start(bf16[128,2304]{1,0:T(8,128)(2,1)S(1)} %fusion.69), channel_id=1, source_target_pairs={{0,1},{1,2},{2,3},{3,0},{4,5},{5,6},{6,7},{7,4},{8,9},{9,10},{10,1... | collective-permute-start | bytes 1769480 | tf_op jit(solution)/shard_map/ppermute | solution.py:50
  516.2 25.2 %collective-permute-start.37 = (bf16[128,2304]{1,0:T(8,128)(2,1)S(1)}, bf16[128,2304]{1,0:T(8,128)(2,1)S(1)}, u32[]{:S(2)}, u32[]{:S(2)}) collective-permute-start(bf16[128,2304]{1,0:T(8,128)(2,1)S(1)} %fusion.69), channel_id=1, source_target_pairs={{0,2},{1,3},{2,0},{3,1},{4,6},{5,7},{6,4},{7,5},{8,10},{9,11},{10,... | collective-permute-start | bytes 1769480 | tf_op jit(solution)/shard_map/ppermute | solution.py:50
  516.2 25.2 %collective-permute-start.38 = (bf16[128,2304]{1,0:T(8,128)(2,1)S(1)}, bf16[128,2304]{1,0:T(8,128)(2,1)S(1)}, u32[]{:S(2)}, u32[]{:S(2)}) collective-permute-start(bf16[128,2304]{1,0:T(8,128)(2,1)S(1)} %fusion.69), channel_id=1, source_target_pairs={{0,3},{1,0},{2,1},{3,2},{4,7},{5,4},{6,5},{7,6},{8,11},{9,8},{10,9... | collective-permute-start | bytes 1769480 | tf_op jit(solution)/shard_map/ppermute | solution.py:50
  528.6 9.7 %collective-permute-start.22 = (bf16[384,512]{0,1:T(8,128)(2,1)S(1)}, bf16[384,512]{0,1:T(8,128)(2,1)S(1)}, u32[]{:S(2)}, u32[]{:S(2)}) collective-permute-start(bf16[384,512]{0,1:T(8,128)(2,1)S(1)} %fusion.91), channel_id=1, source_target_pairs={{4,0},{5,1},{6,2},{7,3},{12,8},{13,9},{14,10},{15,11},{20,16},{21,... | collective-permute-start | bytes 1179656 | tf_op jit(solution)/shard_map/ppermute | solution.py:21
  541.3 9.2 %collective-permute-start.35 = (bf16[1152,1024]{1,0:T(8,128)(2,1)}, bf16[1152,1024]{1,0:T(8,128)(2,1)}, u32[]{:S(2)}, u32[]{:S(2)}) collective-permute-start(bf16[1152,1024]{1,0:T(8,128)(2,1)} %convolution_convert_fusion.4), channel_id=1, source_target_pairs={{0,8},{8,0},{16,24},{24,16},{1,9},{9,1},{17,25},{25,17},{2,10},{10... | collective-permute-start | bytes 7077896 | tf_op jit(solution)/shard_map/ppermute | solution.py:193
  544.8 3.3 collective-permute-start.39
  555.8 185.0 %reduce-scatter.8.cloned.1.call-start = ((), (), s32[]{:S(2)}) async-start(), calls=%async_computation.9 | async-start | bytes 6635520 | tf_op jit(solution)/shard_map/reduce_scatter | solution.py:202
  555.8 12.7 %collective-permute-start.41 = (bf16[1152,2304]{1,0:T(8,128)(2,1)}, bf16[1152,2304]{1,0:T(8,128)(2,1)}, u32[]{:S(2)}, u32[]{:S(2)}) collective-permute-start(bf16[1152,2304]{1,0:T(8,128)(2,1)} %convolution_convert_fusion.1), channel_id=1, source_target_pairs={{0,8},{8,0},{16,24},{24,16},{1,9},{9,1},{17,25},{25,17},{2,10},{10... | collective-permute-start | bytes 15925256 | tf_op jit(solution)/shard_map/ppermute | solution.py:193
  568.1 16.7 %collective-permute-start.40 = (bf16[1152,4608]{1,0:T(8,128)(2,1)}, bf16[1152,4608]{1,0:T(8,128)(2,1)}, u32[]{:S(2)}, u32[]{:S(2)}) collective-permute-start(bf16[1152,4608]{1,0:T(8,128)(2,1)} %convolution_convert_fusion), channel_id=1, source_target_pairs={{0,8},{8,0},{16,24},{24,16},{1,9},{9,1},{17,25},{25,17},{2,10},{10... | collective-permute-start | bytes 31850504 | tf_op jit(solution)/shard_map/ppermute | solution.py:193
  575.8 207.1 %reduce-scatter.6.cloned.1.call-start = ((), (), s32[]{:S(2)}) async-start(), calls=%async_computation.8 | async-start | bytes 13271040 | tf_op jit(solution)/shard_map/reduce_scatter | solution.py:202
  608.6 4.0 collective-permute-start.30
  612.6 14.4 %collective-permute-start.31 = (f32[4,2304]{1,0:T(4,128)S(1)}, f32[4,2304]{1,0:T(4,128)S(1)}, u32[]{:S(2)}, u32[]{:S(2)}) collective-permute-start(f32[4,2304]{1,0:T(4,128)S(1)} %add.366), channel_id=1, source_target_pairs={{0,4},{4,0},{1,5},{5,1},{2,6},{6,2},{3,7},{7,3},{8,12},{12,8},{9,1... | collective-permute-start | bytes 110600 | tf_op jit(solution)/shard_map/ppermute | solution.py:137
  615.6 74.0 %collective-permute-start.25 = (bf16[128,2304]{1,0:T(8,128)(2,1)}, bf16[128,2304]{1,0:T(8,128)(2,1)S(1)}, u32[]{:S(2)}, u32[]{:S(2)}) collective-permute-start(bf16[128,2304]{1,0:T(8,128)(2,1)} %get-tuple-element.66), channel_id=1, source_target_pairs={{0,1},{1,2},{2,3},{3,0},{4,5},{5,6},{6,7},{7,4},{8,9},{9,10},{10,1... | collective-permute-start | bytes 1769480 | tf_op jit(solution)/shard_map/ppermute | solution.py:50
  624.1 65.5 %collective-permute-start.24 = (bf16[128,2304]{1,0:T(8,128)(2,1)}, bf16[128,2304]{1,0:T(8,128)(2,1)}, u32[]{:S(2)}, u32[]{:S(2)}) collective-permute-start(bf16[128,2304]{1,0:T(8,128)(2,1)} %get-tuple-element.65), channel_id=1, source_target_pairs={{0,3},{1,0},{2,1},{3,2},{4,7},{5,4},{6,5},{7,6},{8,11},{9,8},{10,9... | collective-permute-start | bytes 1769480 | tf_op jit(solution)/shard_map/ppermute | solution.py:50
  626.5 63.1 %collective-permute-start.23 = (bf16[128,2304]{1,0:T(8,128)(2,1)}, bf16[128,2304]{1,0:T(8,128)(2,1)}, u32[]{:S(2)}, u32[]{:S(2)}) collective-permute-start(bf16[128,2304]{1,0:T(8,128)(2,1)} %get-tuple-element.64), channel_id=1, source_target_pairs={{0,2},{1,3},{2,0},{3,1},{4,6},{5,7},{6,4},{7,5},{8,10},{9,11},{10,... | collective-permute-start | bytes 1769480 | tf_op jit(solution)/shard_map/ppermute | solution.py:50
  627.7 35.0 %collective-permute-start.34 = (f32[4,2304]{1,0:T(4,128)}, f32[4,2304]{1,0:T(4,128)}, u32[]{:S(2)}, u32[]{:S(2)}) collective-permute-start(f32[4,2304]{1,0:T(4,128)} %add.367), channel_id=1, source_target_pairs={{0,3},{1,0},{2,1},{3,2},{4,7},{5,4},{6,5},{7,6},{8,11},{9,8},{10,9... | collective-permute-start | bytes 110600 | tf_op jit(solution)/shard_map/ppermute | solution.py:50
  629.1 58.9 %collective-permute-start.32 = (f32[4,2304]{1,0:T(4,128)}, f32[4,2304]{1,0:T(4,128)}, u32[]{:S(2)}, u32[]{:S(2)}) collective-permute-start(f32[4,2304]{1,0:T(4,128)} %add.367), channel_id=1, source_target_pairs={{0,1},{1,2},{2,3},{3,0},{4,5},{5,6},{6,7},{7,4},{8,9},{9,10},{10,1... | collective-permute-start | bytes 110600 | tf_op jit(solution)/shard_map/ppermute | solution.py:50
  662.7 25.3 %collective-permute-start.33 = (f32[4,2304]{1,0:T(4,128)}, f32[4,2304]{1,0:T(4,128)}, u32[]{:S(2)}, u32[]{:S(2)}) collective-permute-start(f32[4,2304]{1,0:T(4,128)} %add.367), channel_id=1, source_target_pairs={{0,2},{1,3},{2,0},{3,1},{4,6},{5,7},{6,4},{7,5},{8,10},{9,11},{10,... | collective-permute-start | bytes 110600 | tf_op jit(solution)/shard_map/ppermute | solution.py:50
  694.0 18.2 %collective-permute-start.26 = (bf16[128,2304]{1,0:T(8,128)(2,1)S(1)}, bf16[128,2304]{1,0:T(8,128)(2,1)S(1)}, u32[]{:S(2)}, u32[]{:S(2)}) collective-permute-start(bf16[128,2304]{1,0:T(8,128)(2,1)S(1)} %concatenate.85), channel_id=1, source_target_pairs={{0,1},{1,2},{2,3},{3,0},{4,5},{5,6},{6,7},{7,4},{8,9},{9,10},{10,1... | collective-permute-start | bytes 1769480 | tf_op jit(solution)/shard_map/ppermute | solution.py:50
  694.9 41.3 %collective-permute-start.27 = (bf16[128,2304]{1,0:T(8,128)(2,1)S(1)}, bf16[128,2304]{1,0:T(8,128)(2,1)S(1)}, u32[]{:S(2)}, u32[]{:S(2)}) collective-permute-start(bf16[128,2304]{1,0:T(8,128)(2,1)S(1)} %concatenate.85), channel_id=1, source_target_pairs={{0,2},{1,3},{2,0},{3,1},{4,6},{5,7},{6,4},{7,5},{8,10},{9,11},{10,... | collective-permute-start | bytes 1769480 | tf_op jit(solution)/shard_map/ppermute | solution.py:50
  698.0 38.2 %collective-permute-start.28 = (bf16[128,2304]{1,0:T(8,128)(2,1)S(1)}, bf16[128,2304]{1,0:T(8,128)(2,1)S(1)}, u32[]{:S(2)}, u32[]{:S(2)}) collective-permute-start(bf16[128,2304]{1,0:T(8,128)(2,1)S(1)} %concatenate.85), channel_id=1, source_target_pairs={{0,3},{1,0},{2,1},{3,2},{4,7},{5,4},{6,5},{7,6},{8,11},{9,8},{10,9... | collective-permute-start | bytes 1769480 | tf_op jit(solution)/shard_map/ppermute | solution.py:50
  (67 other events, 733.6 us)
Sparse Core Ops, SparseCore 0:
  10.5 51.4 all-gather.3
  63.8 157.0 all-gather.5
  252.2 116.6 all-reduce.2
  370.7 57.7 all-gather.7
  555.9 53.8 reduce-scatter.3
  612.7 62.5 reduce-scatter.7
  678.4 104.5 reduce-scatter.5

commit v10 on v9

--- a/solution.py
+++ b/solution.py
@@ -43,6 +43,13 @@
 
 def onward(block, distance, senders):
     return lax.ppermute(block, "tp", [(i, i + distance) for i in senders])
+
+
+def returned(grads, length):
+    before = grads.shape[0] - length
+    back = passed_along(grads[:before].astype(LOW), "ctx", -1)
+    back = jnp.pad(back, ((length - before, 0), (0, 0))).astype(F32)
+    return (grads[before:] + back).astype(LOW)
 
 
 def shift(block, distance):
@@ -177,6 +184,30 @@
     return lax.all_gather(
         weight, ROWS, axis=0, tiled=True, axis_index_groups=[first + second]
     )
+
+
+def sent_rows(weight):
+    ranks = lax.axis_size("fsdp") * lax.axis_size("ctx")
+    if (lax.axis_size("fsdp"), lax.axis_size("ctx")) != (4, 2):
+        return gather_rows(weight)
+    core, pair, width = 2, 4, 1
+
+    def sent(block, bits):
+        return lax.ppermute(block, ROWS, [(r, r ^ bits) for r in range(ranks)])
+
+    held = {0: weight}
+    for bits in (pair | width, width, pair):
+        held[bits] = sent(weight, bits)
+    for bits in (0, width, pair, pair | width):
+        held[bits | core] = sent(held[bits], core)
+    place = {0: 0, width: 1, pair: 2, core: 4}
+    rank = lax.axis_index("fsdp") * 2 + lax.axis_index("ctx")
+    own = (rank // core) % 2 * 4 + rank // pair * 2 + rank % 2
+    whole = jnp.zeros((ranks,) + weight.shape, weight.dtype)
+    for bits in held:
+        at = own ^ (place[bits & width] | place[bits & pair] | place[bits & core])
+        whole = lax.dynamic_update_index_in_dim(whole, held[bits], at, 0)
+    return whole.reshape(-1, weight.shape[1])
 
 
 def rows_of_core(left, core):
@@ -241,7 +272,6 @@
     gate_up_full = units_full[:, : 2 * units]
     down_full = units_full[:, 2 * units :]
     output_pieces = jnp.concatenate(sent_gathered(output_weight), axis=1)
-    output_all = gather_rows(output_pieces)
 
     position = lax.axis_index("ctx")
     own_ids = lax.dynamic_slice_in_dim(segment_ids, position * length, length)
@@ -297,6 +327,7 @@
     up_value = gate_up[:, units:]
     hidden_low = geglu(gate_value, up_value).astype(LOW)
     branch_two = lax.psum(transposed_product(hidden_low, down_full).astype(LOW), "tp")
+    output_all = sent_rows(output_pieces)
     branch_two = branch_two.astype(F32)
     _, pull_four = jax.vjp(rms, branch_two, post_feedforward_gain)
     grad_branch_two, grad_gain_four = pull_four(upstream_all.astype(F32))
@@ -310,27 +341,28 @@
     _, pull_glu = jax.vjp(geglu, gate_value, up_value)
     grad_gate, grad_up = pull_glu(product(grad_two_low, down_full))
     grad_gate_up = jnp.concatenate([grad_gate.astype(LOW), grad_up.astype(LOW)], axis=1)
+    grad_down_low = chip_rows(grad_two_low, hidden_low, down_arrived)
+    down_share = share_rows(grad_down_low)
     grad_normed_two = transposed_product(grad_gate_up, gate_up_full).astype(LOW)
     grad_normed_two = sent_scattered(ordered_blocks(grad_normed_two))
     outputs = by_chip((middle_all + rms(branch_two, post_feedforward_gain)).astype(LOW))
-    grad_down_low = chip_rows(grad_two_low, hidden_low, down_arrived)
-    down_share = share_rows(grad_down_low)
     gate_up_sent = sent_to_core(normed_two, grad_gate_up)
     gate_up_arrived = over_cores(gate_up_sent)
     grad_gate_up_low = chip_rows(normed_two, grad_gate_up, gate_up_arrived)
     gate_up_share = share_rows(grad_gate_up_low)
 
     _, pull_three = jax.vjp(rms, middle, pre_feedforward_gain)
-    grad_middle_norm, grad_gain_three = pull_three(grad_normed_two)
-    grad_middle = upstream + grad_middle_norm
+    grad_middle = upstream + pull_three(grad_normed_two)[0]
     _, pull_two = jax.vjp(rms, branch_one, post_attention_gain)
-    grad_branch_one, grad_gain_two = pull_two(grad_middle)
+    grad_branch_one = pull_two(grad_middle)[0]
     grad_one_own = grad_branch_one.astype(LOW)
     grad_attended = product(grad_one_own, output_all).astype(LOW)
     grad_attended, grad_one_own = lax.optimization_barrier(
         (exchanged(grad_attended), grad_one_own)
     )
     grad_attended = grad_attended.reshape(length, kv_heads, repeats, HD)
+    later = (middle, grad_normed_two, branch_one, grad_middle, grad_one_own)
+    middle_kept, normed_kept, branch_kept, grad_kept, grad_one_own = lax.optimization_barrier(later)
     grad_one_low = in_order(sent_gathered(grad_one_own))
     output_sent = sent_to_core(grad_one_low, attended_low)
     output_arrived = over_cores(output_sent)
@@ -357,18 +389,19 @@
     grad_values_all = jnp.einsum(
         "grqk,qgrd->kgd", probs_low, grad_attended, preferred_element_type=F32
     ).reshape(before + length, -1)
-    grad_kv_all = jnp.concatenate([grad_keys_all, grad_values_all], axis=1)
-    grad_kv_back = passed_along(grad_kv_all[:before].astype(LOW), "ctx", -1)
-    grad_kv_back = jnp.pad(grad_kv_back, ((length - before, 0), (0, 0))).astype(F32)
-    grad_kv_low = (grad_kv_all[before:] + grad_kv_back).astype(LOW)
+    grad_value_low = returned(grad_values_all, length)
+    grad_key_low = returned(grad_keys_all, length)
+    grad_kv_low = jnp.concatenate([grad_key_low, grad_value_low], axis=1)
     grad_qkv = jnp.concatenate([grad_query_low, grad_kv_low], axis=1)
     grad_normed_one = transposed_product(grad_qkv, qkv_full).astype(LOW)
     unused_one, pull_one = jax.vjp(rms, hidden_in.astype(F32), pre_attention_gain)
     grad_gain_one = pull_one(grad_normed_one.astype(F32))[1]
+    grad_gain_three = jax.vjp(rms, middle_kept, pre_feedforward_gain)[1](normed_kept)[1]
+    grad_gain_two = jax.vjp(rms, branch_kept, post_attention_gain)[1](grad_kept)[1]
     gains = by_chip(jnp.stack([grad_gain_one, grad_gain_two, grad_gain_three, grad_gain_four]))
+    gains = sum((shift(gains, k) for k in range(1, tp_size)), gains)
     for axis in ROWS:
         gains = summed(gains, axis)
-    gains = sum((shift(gains, k) for k in range(1, tp_size)), gains)
     grad_normed_one = sent_scattered(ordered_blocks(grad_normed_one))
     qkv_sent = sent_to_core(normed_one, grad_qkv)
     qkv_arrived = over_cores(qkv_sent)

time: 805 us -> 843 us (1.047)
  waiting for transfers between devices: 400 us -> 434 us
  local copies, waits for them, and re-layouts: 65.6 us -> 95.5 us
  starting transfers between devices: 108 us -> 88.2 us
    ppermute x0 -> x7, waiting for transfers between devices: none -> 35.2 us  [sent(): return lax.ppermute(block, ROWS, [(r, r ^ bits) for r in range(ranks)])]
    psum x1, waiting for transfers between devices: 52.5 us -> 82 us  [shards(): lax.psum(transposed_product(hidden_low, down_full).astype(LOW), 'tp')]
    ppermute x21, starting transfers between devices: 68.1 us -> 43.1 us  [shift(): lax.ppermute(block, 'tp', [(i, (i + distance) % size) for i in range(size)])]
    dynamic_update_slice x0 -> x8, local copies, waits for them, and re-layouts: none -> 19.8 us  [sent_rows(): whole = lax.dynamic_update_index_in_dim(whole, held[bits], at, 0)]
    ppermute x12, waiting for transfers between devices: 51.3 us -> 34.3 us  [onward(): return lax.ppermute(block, 'tp', [(i, i + distance) for i in senders])]
    all_gather x3 -> x2, waiting for transfers between devices: 47.7 us -> 38.3 us  [gather_rows(): lax.all_gather(weight, ROWS, axis=0, tiled=True, axis_index_groups=[first...]
    ppermute x21, waiting for transfers between devices: 176 us -> 167 us  [shift(): lax.ppermute(block, 'tp', [(i, (i + distance) % size) for i in range(size)])]
    unnamed x132 -> x155, local copies, waits for them, and re-layouts: 12.4 us -> 17 us
  transfers between devices with their start and end apart: 49 -> 56, of which waited for: 28 -> 30; matrix products, arithmetic and copies ran while one was open for 27% -> 31% of each run, Pallas kernels for 0% -> 0%
where the time goes in v10:
time: 843 us; the launch traced here: 832 us
  waiting for transfers between devices  434 us (51%)
  matrix products  138 us (16%)
  local copies, waits for them, and re-layouts  95.5 us (11%)
  starting transfers between devices  88.2 us (10%)
  other arithmetic  61.3 us (7%)
  between operations  15.8 us (2%)
    ppermute x21, waiting for transfers between devices, shift(): lax.ppermute(block, 'tp', [(i, (i + distance) % size) for i in range(size)])  167 us
    psum x1, waiting for transfers between devices, shards(): lax.psum(transposed_product(hidden_low, down_full).astype(LOW), 'tp')  82 us
    dot_general x8, matrix products, rows_product(): lax.dot_general(left, right, (((0,), (0,)), ((), ())), preferred_element_...  46.7 us
    reduce_scatter x3, waiting for transfers between devices, share_rows(): lax.psum_scatter(grad, ROWS, scatter_dimension=0, tiled=True, axis_index_...  45.6 us
    ppermute x21, starting transfers between devices, shift(): lax.ppermute(block, 'tp', [(i, (i + distance) % size) for i in range(size)])  43.1 us
    dot_general x4, matrix products, product(): return jnp.dot(left, right, preferred_element_type=F32)  38.7 us
    all_gather x2, waiting for transfers between devices, gather_rows(): lax.all_gather(weight, ROWS, axis=0, tiled=True, axis_index_groups=[first...  38.3 us
    dot_general x4, matrix products, transposed_product(): lax.dot_general(left, right, (((1,), (1,)), ((), ())), preferred_element_...  37.9 us
  transfers between devices with their start and end apart: 56, of which 30 were waited for; matrix products, arithmetic and copies ran while one was open for 31% of the time, Pallas kernels for 0%

profile of v10, /device:TPU:0, one launch (start us, length us, event | category | flops | bytes accessed | tf_op | source)
XLA Modules:
  0.0 832.5 jit_solution(14298020081082912277)
XLA Ops:
  16.5 4.2 concatenate.62
  23.7 38.3 %all-gather.3.cloned.1.call-done = bf16[2304,1536]{1,0:T(8,128)(2,1)} async-done(((bf16[288,1536]{1,0:T(8,128)(2,1)}), bf16[2304,1536]{1,0:T(8,128)(2,1)}) %all-gather.3.cloned.1.call-update) | async-done | bytes 7077904 | tf_op jit(solution)/shard_map/all_gather | solution.py:184
  61.9 5.7 fusion.53
  68.4 4.1 collective-permute-start
  75.2 11.5 %collective-permute-done = bf16[384,512]{1,0:T(8,128)(2,1)} collective-permute-done((bf16[384,512]{1,0:T(8,128)(2,1)}, bf16[384,512]{1,0:T(8,128)(2,1)}, u32[]{:S(2)}, u32[]{:S(2)}) %collective-permute-start) | collective-permute-done | bytes 393248 | tf_op jit(solution)/shard_map/ppermute | solution.py:21
  98.4 4.0 collective-permute-start.1
  102.4 9.8 %collective-permute-done.1 = bf16[128,2304]{1,0:T(8,128)(2,1)} collective-permute-done((bf16[128,2304]{1,0:T(8,128)(2,1)S(1)}, bf16[128,2304]{1,0:T(8,128)(2,1)}, u32[]{:S(2)}, u32[]{:S(2)}) %collective-permute-start.1) | collective-permute-done | bytes 589856 | tf_op jit(solution)/shard_map/ppermute | solution.py:45
  113.9 4.5 collective-permute-start.3
  119.1 9.1 %collective-permute-done.3 = bf16[128,2304]{1,0:T(8,128)(2,1)S(1)} collective-permute-done((bf16[128,2304]{1,0:T(8,128)(2,1)S(1)}, bf16[128,2304]{1,0:T(8,128)(2,1)S(1)}, u32[]{:S(2)}, u32[]{:S(2)}) %collective-permute-start.3) | collective-permute-done | bytes 589856 | tf_op jit(solution)/shard_map/ppermute | solution.py:45
  131.4 6.0 collective-permute-start.5
  137.4 7.9 collective-permute-done.6
  151.6 4.3 collective-permute-start.7
  165.1 16.2 %collective-permute-done.16 = bf16[288,512]{1,0:T(8,128)(2,1)S(1)} collective-permute-done((bf16[288,512]{1,0:T(8,128)(2,1)S(1)}, bf16[288,512]{1,0:T(8,128)(2,1)S(1)}, u32[]{:S(2)}, u32[]{:S(2)}) %collective-permute-start.16) | collective-permute-done | bytes 294944 | tf_op jit(solution)/shard_map/ppermute | solution.py:57
  182.0 9.3 %collective-permute-done.17 = bf16[288,512]{1,0:T(8,128)(2,1)S(1)} collective-permute-done((bf16[288,512]{1,0:T(8,128)(2,1)S(1)}, bf16[288,512]{1,0:T(8,128)(2,1)S(1)}, u32[]{:S(2)}, u32[]{:S(2)}) %collective-permute-start.17) | collective-permute-done | bytes 294944 | tf_op jit(solution)/shard_map/ppermute | solution.py:57
  202.4 6.1 collective-permute-done.10
  212.0 5.2 concatenate.77
  217.8 5.5 concatenate.72
  225.5 4.8 broadcast_in_dim.149
  232.8 16.0 %collective-permute-done.19 = bf16[288,2048]{1,0:T(8,128)(2,1)} collective-permute-done((bf16[288,2048]{1,0:T(8,128)(2,1)}, bf16[288,2048]{1,0:T(8,128)(2,1)}, u32[]{:S(2)}, u32[]{:S(2)}) %collective-permute-start.19) | collective-permute-done | bytes 1179680 | tf_op jit(solution)/shard_map/ppermute | solution.py:196
  248.8 19.2 %collective-permute-done.20 = bf16[288,2048]{1,0:T(8,128)(2,1)} collective-permute-done((bf16[288,2048]{1,0:T(8,128)(2,1)}, bf16[288,2048]{1,0:T(8,128)(2,1)}, u32[]{:S(2)}, u32[]{:S(2)}) %collective-permute-start.20) | collective-permute-done | bytes 1179680 | tf_op jit(solution)/shard_map/ppermute | solution.py:196
  279.0 5.9 multiply_convert_fusion.2
  284.9 15.2 %fusion.2 = f32[512,4608]{1,0:T(8,128)S(1)} fusion(bf16[512,2304]{1,0:T(8,128)(2,1)} %get-tuple-element.94, bf16[2304,6912]{1,0:T(8,128)(2,1)} %all-gather.5.cloned.1.call-done), kind=kOutput, calls=%fused_computation.4 | convolution fusion | flops 10871635968 | bytes 33030144 | tf_op jit(solution)/shard_map/dot_general | solution.py:33
  305.1 11.0 %fusion.29 = bf16[512,2304]{1,0:T(8,128)(2,1)} fusion(bf16[512,2304]{1,0:T(8,128)(2,1)S(1)} %multiply_convert_fusion.1, bf16[2304,6912]{1,0:T(8,128)(2,1)} %all-gather.5.cloned.1.call-done), kind=kOutput, calls=%fused_computation.53 | convolution fusion | flops 5436997632 | bytes 15335424 | tf_op jit(solution)/shard_map/dot_general | solution.py:41
  328.9 82.0 %all-reduce.4.cloned.1.call-done = bf16[512,2304]{1,0:T(8,128)(2,1)} async-done(((bf16[512,2304]{1,0:T(8,128)(2,1)}), bf16[512,2304]{1,0:T(8,128)(2,1)}) %all-reduce.4.cloned.1.call-update) | async-done | bytes 2359312 | tf_op jit(solution)/shard_map/psum | solution.py:329
  416.7 5.1 fusion.25
  421.8 5.1 convolution_convert_fusion.1
  427.0 12.8 %fusion.23 = (bf16[512,2304]{1,0:T(8,128)(2,1)S(1)}, bf16[512,2304]{1,0:T(8,128)(2,1)}) fusion(f32[512,4608]{1,0:T(8,128)S(1)} %bitcast.225, bf16[512,2304]{1,0:T(8,128)(2,1)S(1)} %get-tuple-element.58, bf16[2304,6912]{1,0:T(8,128)(2,1)} %all-gather.5.cloned.1.call-done), kind=kOutput, calls=%fused_computation.39 | convolution fusion | flops 5464129536 | bytes 27131904 | tf_op jit(solution)/shard_map/dot_general | solution.py:33
  439.7 16.1 %fusion.32 = bf16[512,2304]{1,0:T(8,128)(2,1)S(1)} fusion(bf16[2304,6912]{1,0:T(8,128)(2,1)} %all-gather.5.cloned.1.call-done, bf16[512,2304]{1,0:T(8,128)(2,1)} %get-tuple-element.102, bf16[512,2304]{1,0:T(8,128)(2,1)S(1)} %get-tuple-element.101), kind=kOutput, calls=%fused_computation.54 | convolution fusion | flops 10882252800 | bytes 28311552 | tf_op jit(solution)/shard_map/dot_general | solution.py:41
  465.0 9.1 %collective-permute-done.15 = bf16[128,2304]{1,0:T(8,128)(2,1)S(1)} collective-permute-done((bf16[128,2304]{1,0:T(8,128)(2,1)S(1)}, bf16[128,2304]{1,0:T(8,128)(2,1)S(1)}, u32[]{:S(2)}, u32[]{:S(2)}) %collective-permute-start.15) | collective-permute-done | bytes 589856 | tf_op jit(solution)/shard_map/ppermute | solution.py:57
  474.1 9.8 %collective-permute-done.14 = bf16[128,2304]{1,0:T(8,128)(2,1)S(1)} collective-permute-done((bf16[128,2304]{1,0:T(8,128)(2,1)S(1)}, bf16[128,2304]{1,0:T(8,128)(2,1)S(1)}, u32[]{:S(2)}, u32[]{:S(2)}) %collective-permute-start.14) | collective-permute-done | bytes 589856 | tf_op jit(solution)/shard_map/ppermute | solution.py:57
  483.9 26.4 %collective-permute-done.13 = bf16[128,2304]{1,0:T(8,128)(2,1)S(1)} collective-permute-done((bf16[128,2304]{1,0:T(8,128)(2,1)S(1)}, bf16[128,2304]{1,0:T(8,128)(2,1)S(1)}, u32[]{:S(2)}, u32[]{:S(2)}) %collective-permute-start.13) | collective-permute-done | bytes 589856 | tf_op jit(solution)/shard_map/ppermute | solution.py:57
  514.8 5.1 convolution_convert_fusion.6
  522.2 8.0 collective-permute-done.26
  551.6 3.9 collective-permute-done.29
  559.8 11.4 %collective-permute-done.45 = bf16[128,2304]{1,0:T(8,128)(2,1)} collective-permute-done((bf16[128,2304]{1,0:T(8,128)(2,1)S(1)}, bf16[128,2304]{1,0:T(8,128)(2,1)}, u32[]{:S(2)}, u32[]{:S(2)}) %collective-permute-start.45) | collective-permute-done | bytes 589856 | tf_op jit(solution)/shard_map/ppermute | solution.py:57
  588.4 10.7 %convolution_convert_fusion = bf16[1152,4608]{1,0:T(8,128)(2,1)} fusion(bf16[512,2304]{1,0:T(8,128)(2,1)} %get-tuple-element.102, bf16[512,2304]{1,0:T(8,128)(2,1)} %copy-done.72, bf16[512,2304]{1,0:T(8,128)(2,1)S(1)} %copy-done.24, s32[]{:T(128)S(6)} %select_n.252), kind=kOutput, calls=%fused_computation.1 | convolution fusion | flops 5450563584 | bytes 16515076 | tf_op jit(solution)/shard_map/dot_general | solution.py:37
  599.3 6.8 add_convert_fusion.1
  606.4 9.4 %collective-permute-done.48 = bf16[1152,4608]{1,0:T(8,128)(2,1)} collective-permute-done((bf16[1152,4608]{1,0:T(8,128)(2,1)}, bf16[1152,4608]{1,0:T(8,128)(2,1)}, u32[]{:S(2)}, u32[]{:S(2)}) %collective-permute-start.48) | collective-permute-done | bytes 10616864 | tf_op jit(solution)/shard_map/ppermute | solution.py:224
  615.8 13.5 %add_convert_fusion = bf16[1152,4608]{1,0:T(8,128)(2,1)} fusion(bf16[1152,4608]{1,0:T(8,128)(2,1)} %collective-permute-done.48, bf16[512,2304]{1,0:T(8,128)(2,1)} %get-tuple-element.102, bf16[512,2304]{1,0:T(8,128)(2,1)} %copy-done.72, bf16[512,2304]{1,0:T(8,128)(2,1)S(1)} %copy-done.24, s32[]{:T(128)S(6)} %select_n.273), kind=kOutput, calls=%fused_computation | convolution fusion | flops 5461180416 | bytes 27131908 | tf_op jit(solution)/shard_map/dot_general | solution.py:37
  633.2 7.5 fusion.15
  641.0 15.6 %collective-permute-start.39 = (f32[4,2304]{1,0:T(4,128)S(1)}, f32[4,2304]{1,0:T(4,128)S(1)}, u32[]{:S(2)}, u32[]{:S(2)}) collective-permute-start(f32[4,2304]{1,0:T(4,128)S(1)} %concatenate.82), channel_id=1, source_target_pairs={{0,3},{1,0},{2,1},{3,2},{4,7},{5,4},{6,5},{7,6},{8,11},{9,8},{10,9... | collective-permute-start | bytes 110600 | tf_op jit(solution)/shard_map/ppermute | solution.py:57
  680.1 5.1 concatenate.76
  686.8 8.0 collective-permute-done.32
  694.8 25.6 %collective-permute-done.31 = bf16[128,2304]{1,0:T(8,128)(2,1)} collective-permute-done((bf16[128,2304]{1,0:T(8,128)(2,1)}, bf16[128,2304]{1,0:T(8,128)(2,1)}, u32[]{:S(2)}, u32[]{:S(2)}) %collective-permute-start.31) | collective-permute-done | bytes 589856 | tf_op jit(solution)/shard_map/ppermute | solution.py:57
  729.5 14.1 %collective-permute-done.34 = bf16[128,2304]{1,0:T(8,128)(2,1)S(1)} collective-permute-done((bf16[128,2304]{1,0:T(8,128)(2,1)S(1)}, bf16[128,2304]{1,0:T(8,128)(2,1)S(1)}, u32[]{:S(2)}, u32[]{:S(2)}) %collective-permute-start.34) | collective-permute-done | bytes 589856 | tf_op jit(solution)/shard_map/ppermute | solution.py:57
  743.6 23.9 %collective-permute-done.35 = bf16[128,2304]{1,0:T(8,128)(2,1)S(1)} collective-permute-done((bf16[128,2304]{1,0:T(8,128)(2,1)S(1)}, bf16[128,2304]{1,0:T(8,128)(2,1)S(1)}, u32[]{:S(2)}, u32[]{:S(2)}) %collective-permute-start.35) | collective-permute-done | bytes 589856 | tf_op jit(solution)/shard_map/ppermute | solution.py:57
  775.1 45.6 %reduce-scatter.6.cloned.1.call-done = bf16[288,4608]{1,0:T(8,128)(2,1)} async-done(((bf16[1152,4608]{1,0:T(8,128)(2,1)}), bf16[288,4608]{1,0:T(8,128)(2,1)}) %reduce-scatter.6.cloned.1.call-update) | async-done | bytes 2654224 | tf_op jit(solution)/shard_map/reduce_scatter | solution.py:233
  820.7 4.5 fusion.127
  (363 shorter events, 207.8 us)
Async XLA Ops:
  7.2 54.7 %all-gather.3.cloned.1.call-start = ((), (), s32[]{:S(2)}) async-start(), calls=%async_computation.3 | async-start | bytes 7962624 | tf_op jit(solution)/shard_map/all_gather | solution.py:184
  9.5 275.4 %all-gather.5.cloned.1.call-start = ((), (), s32[]{:S(2)}) async-start(), calls=%async_computation.4 | async-start | bytes 35831808 | tf_op jit(solution)/shard_map/all_gather | solution.py:184
  12.9 398.0 %all-reduce.4.cloned.1.call-start = ((), (), s32[]{:S(2)}) async-start(), calls=%async_computation.5 | async-start | bytes 4718592 | tf_op jit(solution)/shard_map/psum | solution.py:329
  68.4 18.3 %collective-permute-start = (bf16[384,512]{1,0:T(8,128)(2,1)}, bf16[384,512]{1,0:T(8,128)(2,1)}, u32[]{:S(2)}, u32[]{:S(2)}) collective-permute-start(bf16[384,512]{1,0:T(8,128)(2,1)} %slice.274), channel_id=1, source_target_pairs={{0,4},{1,5},{2,6},{3,7},{8,12},{9,13},{10,14},{11,15},{16,20},{17,... | collective-permute-start | bytes 1179656 | tf_op jit(solution)/shard_map/ppermute | solution.py:21
  98.4 13.8 %collective-permute-start.1 = (bf16[128,2304]{1,0:T(8,128)(2,1)S(1)}, bf16[128,2304]{1,0:T(8,128)(2,1)}, u32[]{:S(2)}, u32[]{:S(2)}) collective-permute-start(bf16[128,2304]{1,0:T(8,128)(2,1)S(1)} %get-tuple-element.46), channel_id=1, source_target_pairs={{0,1},{4,5},{8,9},{12,13},{16,17},{20,21},{24,25},{28,29}} | collective-permute-start | bytes 1769480 | tf_op jit(solution)/shard_map/ppermute | solution.py:45
  113.9 14.3 %collective-permute-start.3 = (bf16[128,2304]{1,0:T(8,128)(2,1)S(1)}, bf16[128,2304]{1,0:T(8,128)(2,1)S(1)}, u32[]{:S(2)}, u32[]{:S(2)}) collective-permute-start(bf16[128,2304]{1,0:T(8,128)(2,1)S(1)} %get-tuple-element.48), channel_id=1, source_target_pairs={{0,1},{1,2},{4,5},{5,6},{8,9},{9,10},{12,13},{13,14},{16,17},{17,1... | collective-permute-start | bytes 1769480 | tf_op jit(solution)/shard_map/ppermute | solution.py:45
  118.4 10.7 %collective-permute-start.4 = (bf16[128,2304]{1,0:T(8,128)(2,1)S(1)}, bf16[128,2304]{1,0:T(8,128)(2,1)S(1)}, u32[]{:S(2)}, u32[]{:S(2)}) collective-permute-start(bf16[128,2304]{1,0:T(8,128)(2,1)S(1)} %get-tuple-element.49), channel_id=1, source_target_pairs={{2,1},{3,2},{6,5},{7,6},{10,9},{11,10},{14,13},{15,14},{18,17},{19... | collective-permute-start | bytes 1769480 | tf_op jit(solution)/shard_map/ppermute | solution.py:45
  130.1 15.3 %collective-permute-start.6 = (bf16[128,2304]{1,0:T(8,128)(2,1)}, bf16[128,2304]{1,0:T(8,128)(2,1)S(1)}, u32[]{:S(2)}, u32[]{:S(2)}) collective-permute-start(bf16[128,2304]{1,0:T(8,128)(2,1)} %add_convert_fusion.3), channel_id=1, source_target_pairs={{1,0},{2,1},{3,2},{5,4},{6,5},{7,6},{9,8},{10,9},{11,10},{13,12},{... | collective-permute-start | bytes 1769480 | tf_op jit(solution)/shard_map/ppermute | solution.py:45
  131.4 15.3 %collective-permute-start.5 = (bf16[128,2304]{1,0:T(8,128)(2,1)}, bf16[128,2304]{1,0:T(8,128)(2,1)S(1)}, u32[]{:S(2)}, u32[]{:S(2)}) collective-permute-start(bf16[128,2304]{1,0:T(8,128)(2,1)} %add_convert_fusion.4), channel_id=1, source_target_pairs={{0,1},{1,2},{2,3},{4,5},{5,6},{6,7},{8,9},{9,10},{10,11},{12,13},{... | collective-permute-start | bytes 1769480 | tf_op jit(solution)/shard_map/ppermute | solution.py:45
  151.6 40.4 %collective-permute-start.7 = (bf16[128,2304]{1,0:T(8,128)(2,1)S(1)}, bf16[128,2304]{1,0:T(8,128)(2,1)S(1)}, u32[]{:S(2)}, u32[]{:S(2)}) collective-permute-start(bf16[128,2304]{1,0:T(8,128)(2,1)S(1)} %get-tuple-element.97), channel_id=1, source_target_pairs={{0,1},{1,2},{2,3},{4,5},{5,6},{6,7},{8,9},{9,10},{10,11},{12,13},{... | collective-permute-start | bytes 1769480 | tf_op jit(solution)/shard_map/ppermute | solution.py:45
  155.9 36.1 %collective-permute-start.8 = (bf16[128,2304]{1,0:T(8,128)(2,1)S(1)}, bf16[128,2304]{1,0:T(8,128)(2,1)S(1)}, u32[]{:S(2)}, u32[]{:S(2)}) collective-permute-start(bf16[128,2304]{1,0:T(8,128)(2,1)S(1)} %get-tuple-element.97), channel_id=1, source_target_pairs={{1,0},{2,1},{3,2},{5,4},{6,5},{7,6},{9,8},{10,9},{11,10},{13,12},{... | collective-permute-start | bytes 1769480 | tf_op jit(solution)/shard_map/ppermute | solution.py:45
  157.3 24.0 %collective-permute-start.16 = (bf16[288,512]{1,0:T(8,128)(2,1)S(1)}, bf16[288,512]{1,0:T(8,128)(2,1)S(1)}, u32[]{:S(2)}, u32[]{:S(2)}) collective-permute-start(bf16[288,512]{1,0:T(8,128)(2,1)S(1)} %copy-done.35), channel_id=1, source_target_pairs={{0,1},{1,2},{2,3},{3,0},{4,5},{5,6},{6,7},{7,4},{8,9},{9,10},{10,1... | collective-permute-start | bytes 884744 | tf_op jit(solution)/shard_map/ppermute | solution.py:57
  160.2 31.1 %collective-permute-start.17 = (bf16[288,512]{1,0:T(8,128)(2,1)S(1)}, bf16[288,512]{1,0:T(8,128)(2,1)S(1)}, u32[]{:S(2)}, u32[]{:S(2)}) collective-permute-start(bf16[288,512]{1,0:T(8,128)(2,1)S(1)} %copy-done.35), channel_id=1, source_target_pairs={{0,2},{1,3},{2,0},{3,1},{4,6},{5,7},{6,4},{7,5},{8,10},{9,11},{10,... | collective-permute-start | bytes 884744 | tf_op jit(solution)/shard_map/ppermute | solution.py:57
  161.6 33.2 %collective-permute-start.18 = (bf16[288,512]{1,0:T(8,128)(2,1)S(1)}, bf16[288,512]{1,0:T(8,128)(2,1)S(1)}, u32[]{:S(2)}, u32[]{:S(2)}) collective-permute-start(bf16[288,512]{1,0:T(8,128)(2,1)S(1)} %copy-done.35), channel_id=1, source_target_pairs={{0,3},{1,0},{2,1},{3,2},{4,7},{5,4},{6,5},{7,6},{8,11},{9,8},{10,9... | collective-permute-start | bytes 884744 | tf_op jit(solution)/shard_map/ppermute | solution.py:57
  192.1 10.3 %collective-permute-start.9 = (bf16[128,2304]{1,0:T(8,128)(2,1)S(1)}, bf16[128,2304]{1,0:T(8,128)(2,1)}, u32[]{:S(2)}, u32[]{:S(2)}) collective-permute-start(bf16[128,2304]{1,0:T(8,128)(2,1)S(1)} %collective-permute-done.7), channel_id=1, source_target_pairs={{1,2},{2,3},{5,6},{6,7},{9,10},{10,11},{13,14},{14,15},{17,18},{18... | collective-permute-start | bytes 1769480 | tf_op jit(solution)/shard_map/ppermute | solution.py:45
  193.6 14.9 %collective-permute-start.10 = (bf16[128,2304]{1,0:T(8,128)(2,1)S(1)}, bf16[128,2304]{1,0:T(8,128)(2,1)}, u32[]{:S(2)}, u32[]{:S(2)}) collective-permute-start(bf16[128,2304]{1,0:T(8,128)(2,1)S(1)} %collective-permute-done.8), channel_id=1, source_target_pairs={{1,0},{2,1},{5,4},{6,5},{9,8},{10,9},{13,12},{14,13},{17,16},{18,1... | collective-permute-start | bytes 1769480 | tf_op jit(solution)/shard_map/ppermute | solution.py:45
  195.6 53.2 %collective-permute-start.19 = (bf16[288,2048]{1,0:T(8,128)(2,1)}, bf16[288,2048]{1,0:T(8,128)(2,1)}, u32[]{:S(2)}, u32[]{:S(2)}) collective-permute-start(bf16[288,2048]{1,0:T(8,128)(2,1)} %constant_dynamic-update-slice_fusion), channel_id=1, source_target_pairs={{0,20},{4,16},{8,28},{12,24},{16,4},{20,0},{24,12},{28,8},{1,21},{... | collective-permute-start | bytes 3538952 | tf_op jit(solution)/shard_map/ppermute | solution.py:196
  197.2 70.8 %collective-permute-start.20 = (bf16[288,2048]{1,0:T(8,128)(2,1)}, bf16[288,2048]{1,0:T(8,128)(2,1)}, u32[]{:S(2)}, u32[]{:S(2)}) collective-permute-start(bf16[288,2048]{1,0:T(8,128)(2,1)} %constant_dynamic-update-slice_fusion), channel_id=1, source_target_pairs={{0,4},{4,0},{8,12},{12,8},{16,20},{20,16},{24,28},{28,24},{1,5},{5... | collective-permute-start | bytes 3538952 | tf_op jit(solution)/shard_map/ppermute | solution.py:196
  198.1 69.9 %collective-permute-start.21 = (bf16[288,2048]{1,0:T(8,128)(2,1)}, bf16[288,2048]{1,0:T(8,128)(2,1)}, u32[]{:S(2)}, u32[]{:S(2)}) collective-permute-start(bf16[288,2048]{1,0:T(8,128)(2,1)} %constant_dynamic-update-slice_fusion), channel_id=1, source_target_pairs={{0,16},{4,20},{8,24},{12,28},{16,0},{20,4},{24,8},{28,12},{1,17},{... | collective-permute-start | bytes 3538952 | tf_op jit(solution)/shard_map/ppermute | solution.py:196
  208.5 60.0 %collective-permute-start.11 = (bf16[128,2304]{1,0:T(8,128)(2,1)}, bf16[128,2304]{1,0:T(8,128)(2,1)}, u32[]{:S(2)}, u32[]{:S(2)}) collective-permute-start(bf16[128,2304]{1,0:T(8,128)(2,1)} %collective-permute-done.9), channel_id=1, source_target_pairs={{2,3},{6,7},{10,11},{14,15},{18,19},{22,23},{26,27},{30,31}} | collective-permute-start | bytes 1769480 | tf_op jit(solution)/shard_map/ppermute | solution.py:45
  210.0 58.6 %collective-permute-start.12 = (bf16[128,2304]{1,0:T(8,128)(2,1)}, bf16[128,2304]{1,0:T(8,128)(2,1)}, u32[]{:S(2)}, u32[]{:S(2)}) collective-permute-start(bf16[128,2304]{1,0:T(8,128)(2,1)} %collective-permute-done.10), channel_id=1, source_target_pairs={{1,0},{5,4},{9,8},{13,12},{17,16},{21,20},{25,24},{29,28}} | collective-permute-start | bytes 1769480 | tf_op jit(solution)/shard_map/ppermute | solution.py:45
  248.8 75.1 %collective-permute-start.22 = (bf16[288,2048]{1,0:T(8,128)(2,1)}, bf16[288,2048]{1,0:T(8,128)(2,1)}, u32[]{:S(2)}, u32[]{:S(2)}) collective-permute-start(bf16[288,2048]{1,0:T(8,128)(2,1)} %constant_dynamic-update-slice_fusion), channel_id=1, source_target_pairs={{0,8},{4,12},{8,0},{12,4},{16,24},{20,28},{24,16},{28,20},{1,9},{5... | collective-permute-start | bytes 3538952 | tf_op jit(solution)/shard_map/ppermute | solution.py:196
  268.0 58.3 %collective-permute-start.23 = (bf16[288,2048]{1,0:T(8,128)(2,1)}, bf16[288,2048]{1,0:T(8,128)(2,1)}, u32[]{:S(2)}, u32[]{:S(2)}) collective-permute-start(bf16[288,2048]{1,0:T(8,128)(2,1)} %collective-permute-done.20), channel_id=1, source_target_pairs={{0,8},{4,12},{8,0},{12,4},{16,24},{20,28},{24,16},{28,20},{1,9},{5... | collective-permute-start | bytes 3538952 | tf_op jit(solution)/shard_map/ppermute | solution.py:196
  268.0 192.1 %collective-permute-start.24 = (bf16[288,2048]{1,0:T(8,128)(2,1)}, bf16[288,2048]{1,0:T(8,128)(2,1)}, u32[]{:S(2)}, u32[]{:S(2)}) collective-permute-start(bf16[288,2048]{1,0:T(8,128)(2,1)} %collective-permute-done.21), channel_id=1, source_target_pairs={{0,8},{4,12},{8,0},{12,4},{16,24},{20,28},{24,16},{28,20},{1,9},{5... | collective-permute-start | bytes 3538952 | tf_op jit(solution)/shard_map/ppermute | solution.py:196
  268.5 194.0 %collective-permute-start.25 = (bf16[288,2048]{1,0:T(8,128)(2,1)}, bf16[288,2048]{1,0:T(8,128)(2,1)}, u32[]{:S(2)}, u32[]{:S(2)}) collective-permute-start(bf16[288,2048]{1,0:T(8,128)(2,1)} %collective-permute-done.19), channel_id=1, source_target_pairs={{0,8},{4,12},{8,0},{12,4},{16,24},{20,28},{24,16},{28,20},{1,9},{5... | collective-permute-start | bytes 3538952 | tf_op jit(solution)/shard_map/ppermute | solution.py:196
  316.1 451.6 %reduce-scatter.4.cloned.1.call-start = ((), (), s32[]{:S(2)}) async-start(), calls=%async_computation.6 | async-start | bytes 4423680 | tf_op jit(solution)/shard_map/reduce_scatter | solution.py:233
  456.1 18.1 %collective-permute-start.15 = (bf16[128,2304]{1,0:T(8,128)(2,1)S(1)}, bf16[128,2304]{1,0:T(8,128)(2,1)S(1)}, u32[]{:S(2)}, u32[]{:S(2)}) collective-permute-start(bf16[128,2304]{1,0:T(8,128)(2,1)S(1)} %get-tuple-element.62), channel_id=1, source_target_pairs={{0,1},{1,2},{2,3},{3,0},{4,5},{5,6},{6,7},{7,4},{8,9},{9,10},{10,1... | collective-permute-start | bytes 1769480 | tf_op jit(solution)/shard_map/ppermute | solution.py:57
  456.3 27.6 %collective-permute-start.14 = (bf16[128,2304]{1,0:T(8,128)(2,1)S(1)}, bf16[128,2304]{1,0:T(8,128)(2,1)S(1)}, u32[]{:S(2)}, u32[]{:S(2)}) collective-permute-start(bf16[128,2304]{1,0:T(8,128)(2,1)S(1)} %get-tuple-element.61), channel_id=1, source_target_pairs={{0,3},{1,0},{2,1},{3,2},{4,7},{5,4},{6,5},{7,6},{8,11},{9,8},{10,9... | collective-permute-start | bytes 1769480 | tf_op jit(solution)/shard_map/ppermute | solution.py:57
  460.1 50.2 %collective-permute-start.13 = (bf16[128,2304]{1,0:T(8,128)(2,1)S(1)}, bf16[128,2304]{1,0:T(8,128)(2,1)S(1)}, u32[]{:S(2)}, u32[]{:S(2)}) collective-permute-start(bf16[128,2304]{1,0:T(8,128)(2,1)S(1)} %get-tuple-element.60), channel_id=1, source_target_pairs={{0,2},{1,3},{2,0},{3,1},{4,6},{5,7},{6,4},{7,5},{8,10},{9,11},{10,... | collective-permute-start | bytes 1769480 | tf_op jit(solution)/shard_map/ppermute | solution.py:57
  520.0 10.2 %collective-permute-start.26 = (bf16[128,512]{1,0:T(8,128)(2,1)S(1)}, bf16[128,512]{1,0:T(8,128)(2,1)S(1)}, u32[]{:S(2)}, u32[]{:S(2)}) collective-permute-start(bf16[128,512]{1,0:T(8,128)(2,1)S(1)} %get-tuple-element.64), channel_id=1, source_target_pairs={{0,2},{1,3},{2,0},{3,1},{4,6},{5,7},{6,4},{7,5},{8,10},{9,11},{10,... | collective-permute-start | bytes 393224 | tf_op jit(solution)/shard_map/ppermute | solution.py:57
  520.1 10.6 %collective-permute-start.27 = (bf16[128,512]{1,0:T(8,128)(2,1)S(1)}, bf16[128,512]{1,0:T(8,128)(2,1)S(1)}, u32[]{:S(2)}, u32[]{:S(2)}) collective-permute-start(bf16[128,512]{1,0:T(8,128)(2,1)S(1)} %get-tuple-element.65), channel_id=1, source_target_pairs={{0,3},{1,0},{2,1},{3,2},{4,7},{5,4},{6,5},{7,6},{8,11},{9,8},{10,9... | collective-permute-start | bytes 393224 | tf_op jit(solution)/shard_map/ppermute | solution.py:57
  530.7 27.9 %collective-permute-start.44 = (bf16[128,2304]{1,0:T(8,128)(2,1)S(1)}, bf16[128,2304]{1,0:T(8,128)(2,1)}, u32[]{:S(2)}, u32[]{:S(2)}) collective-permute-start(bf16[128,2304]{1,0:T(8,128)(2,1)S(1)} %fusion.69), channel_id=1, source_target_pairs={{0,1},{1,2},{2,3},{3,0},{4,5},{5,6},{6,7},{7,4},{8,9},{9,10},{10,1... | collective-permute-start | bytes 1769480 | tf_op jit(solution)/shard_map/ppermute | solution.py:57
  533.2 38.0 %collective-permute-start.45 = (bf16[128,2304]{1,0:T(8,128)(2,1)S(1)}, bf16[128,2304]{1,0:T(8,128)(2,1)}, u32[]{:S(2)}, u32[]{:S(2)}) collective-permute-start(bf16[128,2304]{1,0:T(8,128)(2,1)S(1)} %fusion.69), channel_id=1, source_target_pairs={{0,2},{1,3},{2,0},{3,1},{4,6},{5,7},{6,4},{7,5},{8,10},{9,11},{10,... | collective-permute-start | bytes 1769480 | tf_op jit(solution)/shard_map/ppermute | solution.py:57
  534.1 38.2 %collective-permute-start.46 = (bf16[128,2304]{1,0:T(8,128)(2,1)S(1)}, bf16[128,2304]{1,0:T(8,128)(2,1)S(1)}, u32[]{:S(2)}, u32[]{:S(2)}) collective-permute-start(bf16[128,2304]{1,0:T(8,128)(2,1)S(1)} %fusion.69), channel_id=1, source_target_pairs={{0,3},{1,0},{2,1},{3,2},{4,7},{5,4},{6,5},{7,6},{8,11},{9,8},{10,9... | collective-permute-start | bytes 1769480 | tf_op jit(solution)/shard_map/ppermute | solution.py:57
  541.7 9.9 %collective-permute-start.30 = (bf16[384,256]{0,1:T(8,128)(2,1)S(1)}, bf16[384,256]{0,1:T(8,128)(2,1)S(1)}, u32[]{:S(2)}, u32[]{:S(2)}) collective-permute-start(bf16[384,256]{0,1:T(8,128)(2,1)S(1)} %fusion.96), channel_id=1, source_target_pairs={{4,0},{5,1},{6,2},{7,3},{12,8},{13,9},{14,10},{15,11},{20,16},{21,... | collective-permute-start | bytes 589832 | tf_op jit(solution)/shard_map/ppermute | solution.py:21
  558.5 23.0 %collective-permute-start.43 = (bf16[1152,1024]{1,0:T(8,128)(2,1)}, bf16[1152,1024]{1,0:T(8,128)(2,1)}, u32[]{:S(2)}, u32[]{:S(2)}) collective-permute-start(bf16[1152,1024]{1,0:T(8,128)(2,1)} %convolution_convert_fusion.4), channel_id=1, source_target_pairs={{0,8},{8,0},{16,24},{24,16},{1,9},{9,1},{17,25},{25,17},{2,10},{10... | collective-permute-start | bytes 7077896 | tf_op jit(solution)/shard_map/ppermute | solution.py:224
  586.8 185.3 %reduce-scatter.8.cloned.1.call-start = ((), (), s32[]{:S(2)}) async-start(), calls=%async_computation.8 | async-start | bytes 6635520 | tf_op jit(solution)/shard_map/reduce_scatter | solution.py:233
  586.8 12.4 %collective-permute-start.49 = (bf16[1152,2304]{1,0:T(8,128)(2,1)}, bf16[1152,2304]{1,0:T(8,128)(2,1)}, u32[]{:S(2)}, u32[]{:S(2)}) collective-permute-start(bf16[1152,2304]{1,0:T(8,128)(2,1)} %convolution_convert_fusion.1), channel_id=1, source_target_pairs={{0,8},{8,0},{16,24},{24,16},{1,9},{9,1},{17,25},{25,17},{2,10},{10... | collective-permute-start | bytes 15925256 | tf_op jit(solution)/shard_map/ppermute | solution.py:224
  599.1 16.7 %collective-permute-start.48 = (bf16[1152,4608]{1,0:T(8,128)(2,1)}, bf16[1152,4608]{1,0:T(8,128)(2,1)}, u32[]{:S(2)}, u32[]{:S(2)}) collective-permute-start(bf16[1152,4608]{1,0:T(8,128)(2,1)} %convolution_convert_fusion), channel_id=1, source_target_pairs={{0,8},{8,0},{16,24},{24,16},{1,9},{9,1},{17,25},{25,17},{2,10},{10... | collective-permute-start | bytes 31850504 | tf_op jit(solution)/shard_map/ppermute | solution.py:224
  606.1 214.6 %reduce-scatter.6.cloned.1.call-start = ((), (), s32[]{:S(2)}) async-start(), calls=%async_computation.7 | async-start | bytes 13271040 | tf_op jit(solution)/shard_map/reduce_scatter | solution.py:233
  641.0 17.4 %collective-permute-start.39 = (f32[4,2304]{1,0:T(4,128)S(1)}, f32[4,2304]{1,0:T(4,128)S(1)}, u32[]{:S(2)}, u32[]{:S(2)}) collective-permute-start(f32[4,2304]{1,0:T(4,128)S(1)} %concatenate.82), channel_id=1, source_target_pairs={{0,3},{1,0},{2,1},{3,2},{4,7},{5,4},{6,5},{7,6},{8,11},{9,8},{10,9... | collective-permute-start | bytes 110600 | tf_op jit(solution)/shard_map/ppermute | solution.py:57
  665.6 21.2 %collective-permute-start.33 = (bf16[128,2304]{1,0:T(8,128)(2,1)}, bf16[128,2304]{1,0:T(8,128)(2,1)}, u32[]{:S(2)}, u32[]{:S(2)}) collective-permute-start(bf16[128,2304]{1,0:T(8,128)(2,1)} %get-tuple-element.71), channel_id=1, source_target_pairs={{0,1},{1,2},{2,3},{3,0},{4,5},{5,6},{6,7},{7,4},{8,9},{9,10},{10,1... | collective-permute-start | bytes 1769480 | tf_op jit(solution)/shard_map/ppermute | solution.py:57
  665.6 29.2 %collective-permute-start.32 = (bf16[128,2304]{1,0:T(8,128)(2,1)}, bf16[128,2304]{1,0:T(8,128)(2,1)}, u32[]{:S(2)}, u32[]{:S(2)}) collective-permute-start(bf16[128,2304]{1,0:T(8,128)(2,1)} %get-tuple-element.70), channel_id=1, source_target_pairs={{0,3},{1,0},{2,1},{3,2},{4,7},{5,4},{6,5},{7,6},{8,11},{9,8},{10,9... | collective-permute-start | bytes 1769480 | tf_op jit(solution)/shard_map/ppermute | solution.py:57
  669.4 51.0 %collective-permute-start.31 = (bf16[128,2304]{1,0:T(8,128)(2,1)}, bf16[128,2304]{1,0:T(8,128)(2,1)}, u32[]{:S(2)}, u32[]{:S(2)}) collective-permute-start(bf16[128,2304]{1,0:T(8,128)(2,1)} %get-tuple-element.69), channel_id=1, source_target_pairs={{0,2},{1,3},{2,0},{3,1},{4,6},{5,7},{6,4},{7,5},{8,10},{9,11},{10,... | collective-permute-start | bytes 1769480 | tf_op jit(solution)/shard_map/ppermute | solution.py:57
  675.1 10.2 %collective-permute-start.42 = (f32[4,2304]{1,0:T(4,128)}, f32[4,2304]{1,0:T(4,128)}, u32[]{:S(2)}, u32[]{:S(2)}) collective-permute-start(f32[4,2304]{1,0:T(4,128)} %add.446), channel_id=1, source_target_pairs={{0,4},{4,0},{1,5},{5,1},{2,6},{6,2},{3,7},{7,3},{8,12},{12,8},{9,1... | collective-permute-start | bytes 110600 | tf_op jit(solution)/shard_map/ppermute | solution.py:144
  725.4 18.1 %collective-permute-start.34 = (bf16[128,2304]{1,0:T(8,128)(2,1)S(1)}, bf16[128,2304]{1,0:T(8,128)(2,1)S(1)}, u32[]{:S(2)}, u32[]{:S(2)}) collective-permute-start(bf16[128,2304]{1,0:T(8,128)(2,1)S(1)} %concatenate.81), channel_id=1, source_target_pairs={{0,1},{1,2},{2,3},{3,0},{4,5},{5,6},{6,7},{7,4},{8,9},{9,10},{10,1... | collective-permute-start | bytes 1769480 | tf_op jit(solution)/shard_map/ppermute | solution.py:57
  725.5 42.0 %collective-permute-start.35 = (bf16[128,2304]{1,0:T(8,128)(2,1)S(1)}, bf16[128,2304]{1,0:T(8,128)(2,1)S(1)}, u32[]{:S(2)}, u32[]{:S(2)}) collective-permute-start(bf16[128,2304]{1,0:T(8,128)(2,1)S(1)} %concatenate.81), channel_id=1, source_target_pairs={{0,2},{1,3},{2,0},{3,1},{4,6},{5,7},{6,4},{7,5},{8,10},{9,11},{10,... | collective-permute-start | bytes 1769480 | tf_op jit(solution)/shard_map/ppermute | solution.py:57
  727.0 40.5 %collective-permute-start.36 = (bf16[128,2304]{1,0:T(8,128)(2,1)S(1)}, bf16[128,2304]{1,0:T(8,128)(2,1)S(1)}, u32[]{:S(2)}, u32[]{:S(2)}) collective-permute-start(bf16[128,2304]{1,0:T(8,128)(2,1)S(1)} %concatenate.81), channel_id=1, source_target_pairs={{0,3},{1,0},{2,1},{3,2},{4,7},{5,4},{6,5},{7,6},{8,11},{9,8},{10,9... | collective-permute-start | bytes 1769480 | tf_op jit(solution)/shard_map/ppermute | solution.py:57
  (84 other events, 1093.9 us)
Sparse Core Ops, SparseCore 0:
  10.5 51.4 all-gather.2
  63.8 209.6 all-gather.4
  316.2 94.6 all-reduce.3
  586.9 60.6 reduce-scatter.3
  650.5 62.6 reduce-scatter.7
  716.1 104.5 reduce-scatter.5

commit v11 on v10

--- a/solution.py
+++ b/solution.py
@@ -338,13 +338,31 @@
         (sent_to_core(grad_two_low, hidden_low), grad_two_low)
     )
     down_arrived = over_cores(down_sent)
-    _, pull_glu = jax.vjp(geglu, gate_value, up_value)
-    grad_gate, grad_up = pull_glu(product(grad_two_low, down_full))
-    grad_gate_up = jnp.concatenate([grad_gate.astype(LOW), grad_up.astype(LOW)], axis=1)
+    order = distances(tp_size) + [0]
+    halves = (order[: tp_size // 2], order[tp_size // 2 :])
+    rows = {k: (tp_rank - k) % tp_size * piece for k in order}
+
+    def rows_of(value, offsets):
+        blocks = [lax.dynamic_slice_in_dim(value, rows[k], piece) for k in offsets]
+        return jnp.concatenate(blocks, axis=0)
+
+    def hidden_back(offsets):
+        _, pull_glu = jax.vjp(geglu, rows_of(gate_value, offsets), rows_of(up_value, offsets))
+        grad_gate, grad_up = pull_glu(product(rows_of(grad_two_low, offsets), down_full))
+        grads = jnp.concatenate([grad_gate.astype(LOW), grad_up.astype(LOW)], axis=1)
+        normed = transposed_product(grads, gate_up_full).astype(LOW)
+        return grads, [normed[i * piece : (i + 1) * piece] for i in range(len(offsets))]
+
+    first_grads, blocks = hidden_back(halves[0])
+    arrived = [shift(block, -k) for k, block in zip(halves[0], blocks)]
     grad_down_low = chip_rows(grad_two_low, hidden_low, down_arrived)
     down_share = share_rows(grad_down_low)
-    grad_normed_two = transposed_product(grad_gate_up, gate_up_full).astype(LOW)
-    grad_normed_two = sent_scattered(ordered_blocks(grad_normed_two))
+    second_grads, blocks = hidden_back(halves[1])
+    arrived += [shift(block, -k) for k, block in zip(halves[1][:-1], blocks[:-1])]
+    grad_normed_two = sum((block.astype(F32) for block in arrived), blocks[-1].astype(F32))
+    grad_gate_up = jnp.concatenate([first_grads, second_grads], axis=0)
+    normed_two = rows_of(normed_two, order)
+
     outputs = by_chip((middle_all + rms(branch_two, post_feedforward_gain)).astype(LOW))
     gate_up_sent = sent_to_core(normed_two, grad_gate_up)
     gate_up_arrived = over_cores(gate_up_sent)

time: 843 us -> 866 us (1.027)
  matrix products: 138 us -> 153 us
    ppermute x21, waiting for transfers between devices: 167 us -> 150 us  [shift(): lax.ppermute(block, 'tp', [(i, (i + distance) % size) for i in range(size)])]
    ppermute x7, waiting for transfers between devices: 35.2 us -> 49.1 us  [sent(): return lax.ppermute(block, ROWS, [(r, r ^ bits) for r in range(ranks)])]
    dot_general x4 -> x5, matrix products: 37.9 us -> 44.5 us  [transposed_product(): lax.dot_general(left, right, (((1,), (1,)), ((), ())), preferred_element_...]
    dot_general x4 -> x5, matrix products: 38.7 us -> 42.6 us  [product(): return jnp.dot(left, right, preferred_element_type=F32)]
    unnamed x155 -> x151, local copies, waits for them, and re-layouts: 17 us -> 19.6 us
  transfers between devices with their start and end apart: 56 -> 56, of which waited for: 30 -> 27; matrix products, arithmetic and copies ran while one was open for 31% -> 34% of each run, Pallas kernels for 0% -> 0%
where the time goes in v11:
time: 866 us; the launch traced here: 856 us
  waiting for transfers between devices  426 us (49%)
  matrix products  153 us (18%)
  local copies, waits for them, and re-layouts  104 us (12%)
  starting transfers between devices  88.2 us (10%)
  other arithmetic  68.6 us (8%)
  between operations  16 us (2%)
    ppermute x21, waiting for transfers between devices, shift(): lax.ppermute(block, 'tp', [(i, (i + distance) % size) for i in range(size)])  150 us
    psum x1, waiting for transfers between devices, shards(): lax.psum(transposed_product(hidden_low, down_full).astype(LOW), 'tp')  82.5 us
    dot_general x8, matrix products, rows_product(): lax.dot_general(left, right, (((0,), (0,)), ((), ())), preferred_element_...  51.8 us
    ppermute x7, waiting for transfers between devices, sent(): return lax.ppermute(block, ROWS, [(r, r ^ bits) for r in range(ranks)])  49.1 us
    dot_general x5, matrix products, transposed_product(): lax.dot_general(left, right, (((1,), (1,)), ((), ())), preferred_element_...  44.5 us
    dot_general x5, matrix products, product(): return jnp.dot(left, right, preferred_element_type=F32)  42.6 us
    reduce_scatter x3, waiting for transfers between devices, share_rows(): lax.psum_scatter(grad, ROWS, scatter_dimension=0, tiled=True, axis_index_...  42.5 us
    ppermute x21, starting transfers between devices, shift(): lax.ppermute(block, 'tp', [(i, (i + distance) % size) for i in range(size)])  41.9 us
  transfers between devices with their start and end apart: 56, of which 27 were waited for; matrix products, arithmetic and copies ran while one was open for 34% of the time, Pallas kernels for 0%

profile of v11, /device:TPU:0, one launch (start us, length us, event | category | flops | bytes accessed | tf_op | source)
XLA Modules:
  0.0 855.9 jit_solution(8134641458040917432)
XLA Ops:
  23.8 38.1 %all-gather.3.cloned.1.call-done = bf16[2304,1536]{1,0:T(8,128)(2,1)} async-done(((bf16[288,1536]{1,0:T(8,128)(2,1)}), bf16[2304,1536]{1,0:T(8,128)(2,1)}) %all-gather.3.cloned.1.call-update) | async-done | bytes 7077904 | tf_op jit(solution)/shard_map/all_gather | solution.py:184
  61.9 5.7 fusion.82
  68.4 4.1 collective-permute-start
  76.4 10.2 %collective-permute-done = bf16[384,512]{1,0:T(8,128)(2,1)} collective-permute-done((bf16[384,512]{1,0:T(8,128)(2,1)}, bf16[384,512]{1,0:T(8,128)(2,1)}, u32[]{:S(2)}, u32[]{:S(2)}) %collective-permute-start) | collective-permute-done | bytes 393248 | tf_op jit(solution)/shard_map/ppermute | solution.py:21
  103.4 10.2 %collective-permute-done.1 = bf16[128,2304]{1,0:T(8,128)(2,1)} collective-permute-done((bf16[128,2304]{1,0:T(8,128)(2,1)}, bf16[128,2304]{1,0:T(8,128)(2,1)}, u32[]{:S(2)}, u32[]{:S(2)}) %collective-permute-start.1) | collective-permute-done | bytes 589856 | tf_op jit(solution)/shard_map/ppermute | solution.py:45
  115.2 4.6 collective-permute-start.3
  120.5 9.1 %collective-permute-done.3 = bf16[128,2304]{1,0:T(8,128)(2,1)S(1)} collective-permute-done((bf16[128,2304]{1,0:T(8,128)(2,1)S(1)}, bf16[128,2304]{1,0:T(8,128)(2,1)S(1)}, u32[]{:S(2)}, u32[]{:S(2)}) %collective-permute-start.3) | collective-permute-done | bytes 589856 | tf_op jit(solution)/shard_map/ppermute | solution.py:45
  135.2 5.9 collective-permute-start.5
  146.6 13.9 %collective-permute-done.16 = bf16[288,512]{1,0:T(8,128)(2,1)} collective-permute-done((bf16[288,512]{1,0:T(8,128)(2,1)S(1)}, bf16[288,512]{1,0:T(8,128)(2,1)}, u32[]{:S(2)}, u32[]{:S(2)}) %collective-permute-start.16) | collective-permute-done | bytes 294944 | tf_op jit(solution)/shard_map/ppermute | solution.py:57
  162.2 9.1 %collective-permute-done.17 = bf16[288,512]{1,0:T(8,128)(2,1)} collective-permute-done((bf16[288,512]{1,0:T(8,128)(2,1)S(1)}, bf16[288,512]{1,0:T(8,128)(2,1)}, u32[]{:S(2)}, u32[]{:S(2)}) %collective-permute-start.17) | collective-permute-done | bytes 294944 | tf_op jit(solution)/shard_map/ppermute | solution.py:57
  177.6 7.5 collective-permute-start.7
  200.0 5.2 concatenate.104
  205.9 5.1 concatenate.99
  211.7 4.8 broadcast_in_dim.149
  218.9 49.1 %collective-permute-done.20 = bf16[288,2048]{1,0:T(8,128)(2,1)} collective-permute-done((bf16[288,2048]{1,0:T(8,128)(2,1)}, bf16[288,2048]{1,0:T(8,128)(2,1)}, u32[]{:S(2)}, u32[]{:S(2)}) %collective-permute-start.20) | collective-permute-done | bytes 1179680 | tf_op jit(solution)/shard_map/ppermute | solution.py:196
  275.9 10.7 %collective-permute-done.12 = bf16[128,2304]{1,0:T(8,128)(2,1)S(1)} collective-permute-done((bf16[128,2304]{1,0:T(8,128)(2,1)}, bf16[128,2304]{1,0:T(8,128)(2,1)S(1)}, u32[]{:S(2)}, u32[]{:S(2)}) %collective-permute-start.12) | collective-permute-done | bytes 589856 | tf_op jit(solution)/shard_map/ppermute | solution.py:45
  297.0 5.9 multiply_convert_fusion
  302.9 15.2 %fusion.4 = f32[512,4608]{1,0:T(8,128)S(1)} fusion(bf16[512,2304]{1,0:T(8,128)(2,1)} %get-tuple-element.86, bf16[2304,6912]{1,0:T(8,128)(2,1)} %all-gather.5.cloned.1.call-done), kind=kOutput, calls=%fused_computation.6 | convolution fusion | flops 10871635968 | bytes 33030144 | tf_op jit(solution)/shard_map/dot_general | solution.py:33
  318.1 4.5 fusion.167
  323.9 11.0 %fusion.35 = bf16[512,2304]{1,0:T(8,128)(2,1)} fusion(bf16[512,2304]{1,0:T(8,128)(2,1)S(1)} %get-tuple-element.94, bf16[2304,6912]{1,0:T(8,128)(2,1)} %all-gather.5.cloned.1.call-done), kind=kOutput, calls=%fused_computation.56 | convolution fusion | flops 5436997632 | bytes 15335424 | tf_op jit(solution)/shard_map/dot_general | solution.py:41
  346.5 82.5 %all-reduce.4.cloned.1.call-done = bf16[512,2304]{1,0:T(8,128)(2,1)} async-done(((bf16[512,2304]{1,0:T(8,128)(2,1)}), bf16[512,2304]{1,0:T(8,128)(2,1)}) %all-reduce.4.cloned.1.call-update) | async-done | bytes 2359312 | tf_op jit(solution)/shard_map/psum | solution.py:329
  431.2 4.4 fusion.20
  435.7 5.1 fusion.31
  440.8 5.1 convolution_convert_fusion.1
  448.6 8.0 fusion.59
  456.7 12.1 %fusion.41 = bf16[256,2304]{1,0:T(8,128)(2,1)} fusion(bf16[2304,6912]{1,0:T(8,128)(2,1)} %all-gather.5.cloned.1.call-done, bf16[256,2304]{1,0:T(8,128)(2,1)} %get-tuple-element.107, bf16[256,2304]{1,0:T(8,128)(2,1)} %get-tuple-element.106), kind=kOutput, calls=%fused_computation.63 | convolution fusion | flops 5441126400 | bytes 24772608 | tf_op jit(solution)/shard_map/dot_general | solution.py:41
  471.3 8.7 %fusion.66 = (bf16[256,2304]{1,0:T(8,128)(2,1)}, bf16[256,2304]{1,0:T(8,128)(2,1)}) fusion(f32[128,2304]{1,0:T(8,128)S(1)} %copy-done.35, f32[128,2304]{1,0:T(8,128)S(1)} %get-tuple-element.98, f32[128,2304]{1,0:T(8,128)} %get-tuple-element.105, f32[128,2304]{1,0:T(8,128)S(1)} %copy-done.36, bf16[2304,6912]{1,0:T(8,128)(2,1)} %all-gather.5.cloned.1.call-done, ...), kind=kOutput, calls=%fused_computation.98 | convolution fusion | flops 2735603712 | bytes 18874368 | tf_op jit(solution)/shard_map/dot_general | solution.py:33
  480.0 11.2 %fusion.44 = bf16[256,2304]{1,0:T(8,128)(2,1)S(1)} fusion(bf16[2304,6912]{1,0:T(8,128)(2,1)} %all-gather.5.cloned.1.call-done, bf16[256,2304]{1,0:T(8,128)(2,1)} %get-tuple-element.97, bf16[256,2304]{1,0:T(8,128)(2,1)} %get-tuple-element.96), kind=kOutput, calls=%fused_computation.64 | convolution fusion | flops 5441126400 | bytes 24772608 | tf_op jit(solution)/shard_map/dot_general | solution.py:41
  499.8 8.8 %collective-permute-done.14 = bf16[128,2304]{1,0:T(8,128)(2,1)S(1)} collective-permute-done((bf16[128,2304]{1,0:T(8,128)(2,1)S(1)}, bf16[128,2304]{1,0:T(8,128)(2,1)S(1)}, u32[]{:S(2)}, u32[]{:S(2)}) %collective-permute-start.14) | collective-permute-done | bytes 589856 | tf_op jit(solution)/shard_map/ppermute | solution.py:57
  508.6 23.8 %collective-permute-done.13 = bf16[128,2304]{1,0:T(8,128)(2,1)S(1)} collective-permute-done((bf16[128,2304]{1,0:T(8,128)(2,1)S(1)}, bf16[128,2304]{1,0:T(8,128)(2,1)S(1)}, u32[]{:S(2)}, u32[]{:S(2)}) %collective-permute-start.13) | collective-permute-done | bytes 589856 | tf_op jit(solution)/shard_map/ppermute | solution.py:57
  537.0 5.1 convolution_convert_fusion.6
  546.2 6.4 collective-permute-done.26
  574.4 4.3 collective-permute-done.29
  582.9 12.7 %collective-permute-done.45 = bf16[128,2304]{1,0:T(8,128)(2,1)} collective-permute-done((bf16[128,2304]{1,0:T(8,128)(2,1)S(1)}, bf16[128,2304]{1,0:T(8,128)(2,1)}, u32[]{:S(2)}, u32[]{:S(2)}) %collective-permute-start.45) | collective-permute-done | bytes 589856 | tf_op jit(solution)/shard_map/ppermute | solution.py:57
  613.1 12.2 %convolution_convert_fusion = bf16[1152,4608]{1,0:T(8,128)(2,1)} fusion(bf16[512,2304]{1,0:T(8,128)(2,1)S(1)} %pad_maximum_fusion.4, s32[]{:T(128)S(6)} %select_n.272, bf16[256,2304]{1,0:T(8,128)(2,1)} %get-tuple-element.107, bf16[256,2304]{1,0:T(8,128)(2,1)} %get-tuple-element.106, bf16[256,2304]{1,0:T(8,128)(2,1)} %get-tuple-element.97, ...), kind=kOutput, calls=%fused_computation.1 | convolution fusion | flops 5460000768 | bytes 16515076 | tf_op jit(solution)/shard_map/dot_general | solution.py:37
  625.5 8.6 %add_convert_fusion.1 = bf16[1152,2304]{1,0:T(8,128)(2,1)} fusion(bf16[1152,2304]{1,0:T(8,128)(2,1)} %collective-permute-done.49, bf16[512,2304]{1,0:T(8,128)(2,1)} %copy-done.27, bf16[512,2304]{1,0:T(8,128)(2,1)S(1)} %copy-done.16, s32[]{:T(128)S(6)} %select_n.297), kind=kOutput, calls=%fused_computation.9 | convolution fusion | flops 2725871616 | bytes 14155780 | tf_op jit(solution)/shard_map/dot_general | solution.py:37
  634.4 7.6 collective-permute-done.48
  642.0 15.5 %add_convert_fusion = bf16[1152,4608]{1,0:T(8,128)(2,1)} fusion(bf16[1152,4608]{1,0:T(8,128)(2,1)} %collective-permute-done.48, bf16[512,2304]{1,0:T(8,128)(2,1)S(1)} %pad_maximum_fusion.4, s32[]{:T(128)S(6)} %select_n.297, bf16[256,2304]{1,0:T(8,128)(2,1)} %get-tuple-element.107, bf16[256,2304]{1,0:T(8,128)(2,1)} %get-tuple-element.106, ...), kind=kOutput, calls=%fused_computation | convolution fusion | flops 5470617600 | bytes 27131908 | tf_op jit(solution)/shard_map/dot_general | solution.py:37
  661.8 7.0 fusion.19
  669.0 14.9 %collective-permute-start.39 = (f32[4,2304]{1,0:T(4,128)S(1)}, f32[4,2304]{1,0:T(4,128)S(1)}, u32[]{:S(2)}, u32[]{:S(2)}) collective-permute-start(f32[4,2304]{1,0:T(4,128)S(1)} %concatenate.116), channel_id=1, source_target_pairs={{0,3},{1,0},{2,1},{3,2},{4,7},{5,4},{6,5},{7,6},{8,11},{9,8},{10,9... | collective-permute-start | bytes 110600 | tf_op jit(solution)/shard_map/ppermute | solution.py:57
  692.6 4.1 collective-permute-start.32
  709.4 5.3 concatenate.103
  716.2 5.7 collective-permute-done.32
  721.9 25.7 %collective-permute-done.31 = bf16[128,2304]{1,0:T(8,128)(2,1)} collective-permute-done((bf16[128,2304]{1,0:T(8,128)(2,1)}, bf16[128,2304]{1,0:T(8,128)(2,1)}, u32[]{:S(2)}, u32[]{:S(2)}) %collective-permute-start.31) | collective-permute-done | bytes 589856 | tf_op jit(solution)/shard_map/ppermute | solution.py:57
  756.3 14.1 %collective-permute-done.34 = bf16[128,2304]{1,0:T(8,128)(2,1)S(1)} collective-permute-done((bf16[128,2304]{1,0:T(8,128)(2,1)S(1)}, bf16[128,2304]{1,0:T(8,128)(2,1)S(1)}, u32[]{:S(2)}, u32[]{:S(2)}) %collective-permute-start.34) | collective-permute-done | bytes 589856 | tf_op jit(solution)/shard_map/ppermute | solution.py:57
  770.4 23.7 %collective-permute-done.35 = bf16[128,2304]{1,0:T(8,128)(2,1)S(1)} collective-permute-done((bf16[128,2304]{1,0:T(8,128)(2,1)S(1)}, bf16[128,2304]{1,0:T(8,128)(2,1)S(1)}, u32[]{:S(2)}, u32[]{:S(2)}) %collective-permute-start.35) | collective-permute-done | bytes 589856 | tf_op jit(solution)/shard_map/ppermute | solution.py:57
  801.6 42.5 %reduce-scatter.6.cloned.1.call-done = bf16[288,4608]{1,0:T(8,128)(2,1)} async-done(((bf16[1152,4608]{1,0:T(8,128)(2,1)}), bf16[288,4608]{1,0:T(8,128)(2,1)}) %reduce-scatter.6.cloned.1.call-update) | async-done | bytes 2654224 | tf_op jit(solution)/shard_map/reduce_scatter | solution.py:233
  844.1 4.5 fusion.168
  (367 shorter events, 220.9 us)
Async XLA Ops:
  7.2 54.7 %all-gather.3.cloned.1.call-start = ((), (), s32[]{:S(2)}) async-start(), calls=%async_computation.3 | async-start | bytes 7962624 | tf_op jit(solution)/shard_map/all_gather | solution.py:184
  9.6 293.3 %all-gather.5.cloned.1.call-start = ((), (), s32[]{:S(2)}) async-start(), calls=%async_computation.4 | async-start | bytes 35831808 | tf_op jit(solution)/shard_map/all_gather | solution.py:184
  12.8 416.2 %all-reduce.4.cloned.1.call-start = ((), (), s32[]{:S(2)}) async-start(), calls=%async_computation.5 | async-start | bytes 4718592 | tf_op jit(solution)/shard_map/psum | solution.py:329
  68.4 18.3 %collective-permute-start = (bf16[384,512]{1,0:T(8,128)(2,1)}, bf16[384,512]{1,0:T(8,128)(2,1)}, u32[]{:S(2)}, u32[]{:S(2)}) collective-permute-start(bf16[384,512]{1,0:T(8,128)(2,1)} %slice.290), channel_id=1, source_target_pairs={{0,4},{1,5},{2,6},{3,7},{8,12},{9,13},{10,14},{11,15},{16,20},{17,... | collective-permute-start | bytes 1179656 | tf_op jit(solution)/shard_map/ppermute | solution.py:21
  99.4 14.1 %collective-permute-start.1 = (bf16[128,2304]{1,0:T(8,128)(2,1)}, bf16[128,2304]{1,0:T(8,128)(2,1)}, u32[]{:S(2)}, u32[]{:S(2)}) collective-permute-start(bf16[128,2304]{1,0:T(8,128)(2,1)} %get-tuple-element.42), channel_id=1, source_target_pairs={{0,1},{4,5},{8,9},{12,13},{16,17},{20,21},{24,25},{28,29}} | collective-permute-start | bytes 1769480 | tf_op jit(solution)/shard_map/ppermute | solution.py:45
  115.2 14.3 %collective-permute-start.3 = (bf16[128,2304]{1,0:T(8,128)(2,1)S(1)}, bf16[128,2304]{1,0:T(8,128)(2,1)S(1)}, u32[]{:S(2)}, u32[]{:S(2)}) collective-permute-start(bf16[128,2304]{1,0:T(8,128)(2,1)S(1)} %get-tuple-element.44), channel_id=1, source_target_pairs={{0,1},{1,2},{4,5},{5,6},{8,9},{9,10},{12,13},{13,14},{16,17},{17,1... | collective-permute-start | bytes 1769480 | tf_op jit(solution)/shard_map/ppermute | solution.py:45
  119.8 12.0 %collective-permute-start.4 = (bf16[128,2304]{1,0:T(8,128)(2,1)S(1)}, bf16[128,2304]{1,0:T(8,128)(2,1)S(1)}, u32[]{:S(2)}, u32[]{:S(2)}) collective-permute-start(bf16[128,2304]{1,0:T(8,128)(2,1)S(1)} %get-tuple-element.45), channel_id=1, source_target_pairs={{2,1},{3,2},{6,5},{7,6},{10,9},{11,10},{14,13},{15,14},{18,17},{19... | collective-permute-start | bytes 1769480 | tf_op jit(solution)/shard_map/ppermute | solution.py:45
  134.0 39.1 %collective-permute-start.6 = (bf16[128,2304]{1,0:T(8,128)(2,1)}, bf16[128,2304]{1,0:T(8,128)(2,1)}, u32[]{:S(2)}, u32[]{:S(2)}) collective-permute-start(bf16[128,2304]{1,0:T(8,128)(2,1)} %add_convert_fusion.3), channel_id=1, source_target_pairs={{1,0},{2,1},{3,2},{5,4},{6,5},{7,6},{9,8},{10,9},{11,10},{13,12},{... | collective-permute-start | bytes 1769480 | tf_op jit(solution)/shard_map/ppermute | solution.py:45
  135.2 37.8 %collective-permute-start.5 = (bf16[128,2304]{1,0:T(8,128)(2,1)}, bf16[128,2304]{1,0:T(8,128)(2,1)}, u32[]{:S(2)}, u32[]{:S(2)}) collective-permute-start(bf16[128,2304]{1,0:T(8,128)(2,1)} %add_convert_fusion.4), channel_id=1, source_target_pairs={{0,1},{1,2},{2,3},{4,5},{5,6},{6,7},{8,9},{9,10},{10,11},{12,13},{... | collective-permute-start | bytes 1769480 | tf_op jit(solution)/shard_map/ppermute | solution.py:45
  141.1 19.4 %collective-permute-start.16 = (bf16[288,512]{1,0:T(8,128)(2,1)S(1)}, bf16[288,512]{1,0:T(8,128)(2,1)}, u32[]{:S(2)}, u32[]{:S(2)}) collective-permute-start(bf16[288,512]{1,0:T(8,128)(2,1)S(1)} %copy-done.42), channel_id=1, source_target_pairs={{0,1},{1,2},{2,3},{3,0},{4,5},{5,6},{6,7},{7,4},{8,9},{9,10},{10,1... | collective-permute-start | bytes 884744 | tf_op jit(solution)/shard_map/ppermute | solution.py:57
  142.4 29.0 %collective-permute-start.17 = (bf16[288,512]{1,0:T(8,128)(2,1)S(1)}, bf16[288,512]{1,0:T(8,128)(2,1)}, u32[]{:S(2)}, u32[]{:S(2)}) collective-permute-start(bf16[288,512]{1,0:T(8,128)(2,1)S(1)} %copy-done.42), channel_id=1, source_target_pairs={{0,2},{1,3},{2,0},{3,1},{4,6},{5,7},{6,4},{7,5},{8,10},{9,11},{10,... | collective-permute-start | bytes 884744 | tf_op jit(solution)/shard_map/ppermute | solution.py:57
  142.8 43.6 %collective-permute-start.18 = (bf16[288,512]{1,0:T(8,128)(2,1)S(1)}, bf16[288,512]{1,0:T(8,128)(2,1)}, u32[]{:S(2)}, u32[]{:S(2)}) collective-permute-start(bf16[288,512]{1,0:T(8,128)(2,1)S(1)} %copy-done.42), channel_id=1, source_target_pairs={{0,3},{1,0},{2,1},{3,2},{4,7},{5,4},{6,5},{7,6},{8,11},{9,8},{10,9... | collective-permute-start | bytes 884744 | tf_op jit(solution)/shard_map/ppermute | solution.py:57
  177.6 15.5 %collective-permute-start.7 = (bf16[128,2304]{1,0:T(8,128)(2,1)S(1)}, bf16[128,2304]{1,0:T(8,128)(2,1)}, u32[]{:S(2)}, u32[]{:S(2)}) collective-permute-start(bf16[128,2304]{1,0:T(8,128)(2,1)S(1)} %get-tuple-element.89), channel_id=1, source_target_pairs={{0,1},{1,2},{2,3},{4,5},{5,6},{6,7},{8,9},{9,10},{10,11},{12,13},{... | collective-permute-start | bytes 1769480 | tf_op jit(solution)/shard_map/ppermute | solution.py:45
  185.1 11.9 %collective-permute-start.8 = (bf16[128,2304]{1,0:T(8,128)(2,1)S(1)}, bf16[128,2304]{1,0:T(8,128)(2,1)}, u32[]{:S(2)}, u32[]{:S(2)}) collective-permute-start(bf16[128,2304]{1,0:T(8,128)(2,1)S(1)} %get-tuple-element.89), channel_id=1, source_target_pairs={{1,0},{2,1},{3,2},{5,4},{6,5},{7,6},{9,8},{10,9},{11,10},{13,12},{... | collective-permute-start | bytes 1769480 | tf_op jit(solution)/shard_map/ppermute | solution.py:45
  188.2 81.0 %collective-permute-start.19 = (bf16[288,2048]{1,0:T(8,128)(2,1)}, bf16[288,2048]{1,0:T(8,128)(2,1)}, u32[]{:S(2)}, u32[]{:S(2)}) collective-permute-start(bf16[288,2048]{1,0:T(8,128)(2,1)} %constant_dynamic-update-slice_fusion), channel_id=1, source_target_pairs={{0,20},{4,16},{8,28},{12,24},{16,4},{20,0},{24,12},{28,8},{1,21},{... | collective-permute-start | bytes 3538952 | tf_op jit(solution)/shard_map/ppermute | solution.py:196
  189.7 78.3 %collective-permute-start.20 = (bf16[288,2048]{1,0:T(8,128)(2,1)}, bf16[288,2048]{1,0:T(8,128)(2,1)}, u32[]{:S(2)}, u32[]{:S(2)}) collective-permute-start(bf16[288,2048]{1,0:T(8,128)(2,1)} %constant_dynamic-update-slice_fusion), channel_id=1, source_target_pairs={{0,4},{4,0},{8,12},{12,8},{16,20},{20,16},{24,28},{28,24},{1,5},{5... | collective-permute-start | bytes 3538952 | tf_op jit(solution)/shard_map/ppermute | solution.py:196
  197.0 71.0 %collective-permute-start.9 = (bf16[128,2304]{1,0:T(8,128)(2,1)}, bf16[128,2304]{1,0:T(8,128)(2,1)}, u32[]{:S(2)}, u32[]{:S(2)}) collective-permute-start(bf16[128,2304]{1,0:T(8,128)(2,1)} %collective-permute-done.7), channel_id=1, source_target_pairs={{1,2},{2,3},{5,6},{6,7},{9,10},{10,11},{13,14},{14,15},{17,18},{18... | collective-permute-start | bytes 1769480 | tf_op jit(solution)/shard_map/ppermute | solution.py:45
  198.5 70.1 %collective-permute-start.10 = (bf16[128,2304]{1,0:T(8,128)(2,1)}, bf16[128,2304]{1,0:T(8,128)(2,1)}, u32[]{:S(2)}, u32[]{:S(2)}) collective-permute-start(bf16[128,2304]{1,0:T(8,128)(2,1)} %collective-permute-done.8), channel_id=1, source_target_pairs={{1,0},{2,1},{5,4},{6,5},{9,8},{10,9},{13,12},{14,13},{17,16},{18,1... | collective-permute-start | bytes 1769480 | tf_op jit(solution)/shard_map/ppermute | solution.py:45
  211.7 63.7 %collective-permute-start.21 = (bf16[288,2048]{1,0:T(8,128)(2,1)}, bf16[288,2048]{1,0:T(8,128)(2,1)}, u32[]{:S(2)}, u32[]{:S(2)}) collective-permute-start(bf16[288,2048]{1,0:T(8,128)(2,1)} %constant_dynamic-update-slice_fusion), channel_id=1, source_target_pairs={{0,16},{4,20},{8,24},{12,28},{16,0},{20,4},{24,8},{28,12},{1,17},{... | collective-permute-start | bytes 3538952 | tf_op jit(solution)/shard_map/ppermute | solution.py:196
  268.0 69.6 %collective-permute-start.22 = (bf16[288,2048]{1,0:T(8,128)(2,1)}, bf16[288,2048]{1,0:T(8,128)(2,1)}, u32[]{:S(2)}, u32[]{:S(2)}) collective-permute-start(bf16[288,2048]{1,0:T(8,128)(2,1)} %constant_dynamic-update-slice_fusion), channel_id=1, source_target_pairs={{0,8},{4,12},{8,0},{12,4},{16,24},{20,28},{24,16},{28,20},{1,9},{5... | collective-permute-start | bytes 3538952 | tf_op jit(solution)/shard_map/ppermute | solution.py:196
  268.0 72.2 %collective-permute-start.23 = (bf16[288,2048]{1,0:T(8,128)(2,1)}, bf16[288,2048]{1,0:T(8,128)(2,1)S(1)}, u32[]{:S(2)}, u32[]{:S(2)}) collective-permute-start(bf16[288,2048]{1,0:T(8,128)(2,1)} %collective-permute-done.20), channel_id=1, source_target_pairs={{0,8},{4,12},{8,0},{12,4},{16,24},{20,28},{24,16},{28,20},{1,9},{5... | collective-permute-start | bytes 3538952 | tf_op jit(solution)/shard_map/ppermute | solution.py:196
  269.2 17.4 %collective-permute-start.12 = (bf16[128,2304]{1,0:T(8,128)(2,1)}, bf16[128,2304]{1,0:T(8,128)(2,1)S(1)}, u32[]{:S(2)}, u32[]{:S(2)}) collective-permute-start(bf16[128,2304]{1,0:T(8,128)(2,1)} %collective-permute-done.10), channel_id=1, source_target_pairs={{1,0},{5,4},{9,8},{13,12},{17,16},{21,20},{25,24},{29,28}} | collective-permute-start | bytes 1769480 | tf_op jit(solution)/shard_map/ppermute | solution.py:45
  275.4 222.0 %collective-permute-start.25 = (bf16[288,2048]{1,0:T(8,128)(2,1)}, bf16[288,2048]{1,0:T(8,128)(2,1)}, u32[]{:S(2)}, u32[]{:S(2)}) collective-permute-start(bf16[288,2048]{1,0:T(8,128)(2,1)} %collective-permute-done.19), channel_id=1, source_target_pairs={{0,8},{4,12},{8,0},{12,4},{16,24},{20,28},{24,16},{28,20},{1,9},{5... | collective-permute-start | bytes 3538952 | tf_op jit(solution)/shard_map/ppermute | solution.py:196
  275.4 219.5 %collective-permute-start.24 = (bf16[288,2048]{1,0:T(8,128)(2,1)}, bf16[288,2048]{1,0:T(8,128)(2,1)}, u32[]{:S(2)}, u32[]{:S(2)}) collective-permute-start(bf16[288,2048]{1,0:T(8,128)(2,1)} %collective-permute-done.21), channel_id=1, source_target_pairs={{0,8},{4,12},{8,0},{12,4},{16,24},{20,28},{24,16},{28,20},{1,9},{5... | collective-permute-start | bytes 3538952 | tf_op jit(solution)/shard_map/ppermute | solution.py:196
  334.9 459.3 %reduce-scatter.4.cloned.1.call-start = ((), (), s32[]{:S(2)}) async-start(), calls=%async_computation.6 | async-start | bytes 4423680 | tf_op jit(solution)/shard_map/reduce_scatter | solution.py:233
  470.7 29.1 %collective-permute-start.15 = (bf16[128,2304]{1,0:T(8,128)(2,1)}, bf16[128,2304]{1,0:T(8,128)(2,1)S(1)}, u32[]{:S(2)}, u32[]{:S(2)}) collective-permute-start(bf16[128,2304]{1,0:T(8,128)(2,1)} %slice.307), channel_id=1, source_target_pairs={{0,1},{1,2},{2,3},{3,0},{4,5},{5,6},{6,7},{7,4},{8,9},{9,10},{10,1... | collective-permute-start | bytes 1769480 | tf_op jit(solution)/shard_map/ppermute | solution.py:57
  491.2 17.4 %collective-permute-start.14 = (bf16[128,2304]{1,0:T(8,128)(2,1)S(1)}, bf16[128,2304]{1,0:T(8,128)(2,1)S(1)}, u32[]{:S(2)}, u32[]{:S(2)}) collective-permute-start(bf16[128,2304]{1,0:T(8,128)(2,1)S(1)} %get-tuple-element.141), channel_id=1, source_target_pairs={{0,3},{1,0},{2,1},{3,2},{4,7},{5,4},{6,5},{7,6},{8,11},{9,8},{10,9... | collective-permute-start | bytes 1769480 | tf_op jit(solution)/shard_map/ppermute | solution.py:57
  494.9 37.5 %collective-permute-start.13 = (bf16[128,2304]{1,0:T(8,128)(2,1)S(1)}, bf16[128,2304]{1,0:T(8,128)(2,1)S(1)}, u32[]{:S(2)}, u32[]{:S(2)}) collective-permute-start(bf16[128,2304]{1,0:T(8,128)(2,1)S(1)} %get-tuple-element.140), channel_id=1, source_target_pairs={{0,2},{1,3},{2,0},{3,1},{4,6},{5,7},{6,4},{7,5},{8,10},{9,11},{10,... | collective-permute-start | bytes 1769480 | tf_op jit(solution)/shard_map/ppermute | solution.py:57
  542.1 10.5 %collective-permute-start.26 = (bf16[128,512]{1,0:T(8,128)(2,1)S(1)}, bf16[128,512]{1,0:T(8,128)(2,1)S(1)}, u32[]{:S(2)}, u32[]{:S(2)}) collective-permute-start(bf16[128,512]{1,0:T(8,128)(2,1)S(1)} %get-tuple-element.56), channel_id=1, source_target_pairs={{0,2},{1,3},{2,0},{3,1},{4,6},{5,7},{6,4},{7,5},{8,10},{9,11},{10,... | collective-permute-start | bytes 393224 | tf_op jit(solution)/shard_map/ppermute | solution.py:57
  542.2 10.4 %collective-permute-start.27 = (bf16[128,512]{1,0:T(8,128)(2,1)S(1)}, bf16[128,512]{1,0:T(8,128)(2,1)S(1)}, u32[]{:S(2)}, u32[]{:S(2)}) collective-permute-start(bf16[128,512]{1,0:T(8,128)(2,1)S(1)} %get-tuple-element.57), channel_id=1, source_target_pairs={{0,3},{1,0},{2,1},{3,2},{4,7},{5,4},{6,5},{7,6},{8,11},{9,8},{10,9... | collective-permute-start | bytes 393224 | tf_op jit(solution)/shard_map/ppermute | solution.py:57
  545.6 8.4 collective-permute-start.28
  554.1 27.6 %collective-permute-start.44 = (bf16[128,2304]{1,0:T(8,128)(2,1)S(1)}, bf16[128,2304]{1,0:T(8,128)(2,1)}, u32[]{:S(2)}, u32[]{:S(2)}) collective-permute-start(bf16[128,2304]{1,0:T(8,128)(2,1)S(1)} %fusion.97), channel_id=1, source_target_pairs={{0,1},{1,2},{2,3},{3,0},{4,5},{5,6},{6,7},{7,4},{8,9},{9,10},{10,1... | collective-permute-start | bytes 1769480 | tf_op jit(solution)/shard_map/ppermute | solution.py:57
  556.1 39.5 %collective-permute-start.45 = (bf16[128,2304]{1,0:T(8,128)(2,1)S(1)}, bf16[128,2304]{1,0:T(8,128)(2,1)}, u32[]{:S(2)}, u32[]{:S(2)}) collective-permute-start(bf16[128,2304]{1,0:T(8,128)(2,1)S(1)} %fusion.97), channel_id=1, source_target_pairs={{0,2},{1,3},{2,0},{3,1},{4,6},{5,7},{6,4},{7,5},{8,10},{9,11},{10,... | collective-permute-start | bytes 1769480 | tf_op jit(solution)/shard_map/ppermute | solution.py:57
  557.6 39.1 %collective-permute-start.46 = (bf16[128,2304]{1,0:T(8,128)(2,1)S(1)}, bf16[128,2304]{1,0:T(8,128)(2,1)S(1)}, u32[]{:S(2)}, u32[]{:S(2)}) collective-permute-start(bf16[128,2304]{1,0:T(8,128)(2,1)S(1)} %fusion.97), channel_id=1, source_target_pairs={{0,3},{1,0},{2,1},{3,2},{4,7},{5,4},{6,5},{7,6},{8,11},{9,8},{10,9... | collective-permute-start | bytes 1769480 | tf_op jit(solution)/shard_map/ppermute | solution.py:57
  564.5 9.8 %collective-permute-start.30 = (bf16[384,256]{0,1:T(8,128)(2,1)S(1)}, bf16[384,256]{0,1:T(8,128)(2,1)S(1)}, u32[]{:S(2)}, u32[]{:S(2)}) collective-permute-start(bf16[384,256]{0,1:T(8,128)(2,1)S(1)} %fusion.133), channel_id=1, source_target_pairs={{4,0},{5,1},{6,2},{7,3},{12,8},{13,9},{14,10},{15,11},{20,16},{21,... | collective-permute-start | bytes 589832 | tf_op jit(solution)/shard_map/ppermute | solution.py:21
  581.6 24.3 %collective-permute-start.43 = (bf16[1152,1024]{1,0:T(8,128)(2,1)}, bf16[1152,1024]{1,0:T(8,128)(2,1)}, u32[]{:S(2)}, u32[]{:S(2)}) collective-permute-start(bf16[1152,1024]{1,0:T(8,128)(2,1)} %convolution_convert_fusion.4), channel_id=1, source_target_pairs={{0,8},{8,0},{16,24},{24,16},{1,9},{9,1},{17,25},{25,17},{2,10},{10... | collective-permute-start | bytes 7077896 | tf_op jit(solution)/shard_map/ppermute | solution.py:224
  611.1 187.5 %reduce-scatter.8.cloned.1.call-start = ((), (), s32[]{:S(2)}) async-start(), calls=%async_computation.8 | async-start | bytes 6635520 | tf_op jit(solution)/shard_map/reduce_scatter | solution.py:233
  611.4 14.1 %collective-permute-start.49 = (bf16[1152,2304]{1,0:T(8,128)(2,1)}, bf16[1152,2304]{1,0:T(8,128)(2,1)}, u32[]{:S(2)}, u32[]{:S(2)}) collective-permute-start(bf16[1152,2304]{1,0:T(8,128)(2,1)} %convolution_convert_fusion.1), channel_id=1, source_target_pairs={{0,8},{8,0},{16,24},{24,16},{1,9},{9,1},{17,25},{25,17},{2,10},{10... | collective-permute-start | bytes 15925256 | tf_op jit(solution)/shard_map/ppermute | solution.py:224
  625.3 16.7 %collective-permute-start.48 = (bf16[1152,4608]{1,0:T(8,128)(2,1)}, bf16[1152,4608]{1,0:T(8,128)(2,1)}, u32[]{:S(2)}, u32[]{:S(2)}) collective-permute-start(bf16[1152,4608]{1,0:T(8,128)(2,1)} %convolution_convert_fusion), channel_id=1, source_target_pairs={{0,8},{8,0},{16,24},{24,16},{1,9},{9,1},{17,25},{25,17},{2,10},{10... | collective-permute-start | bytes 31850504 | tf_op jit(solution)/shard_map/ppermute | solution.py:224
  634.1 210.0 %reduce-scatter.6.cloned.1.call-start = ((), (), s32[]{:S(2)}) async-start(), calls=%async_computation.7 | async-start | bytes 13271040 | tf_op jit(solution)/shard_map/reduce_scatter | solution.py:233
  669.0 16.8 %collective-permute-start.39 = (f32[4,2304]{1,0:T(4,128)S(1)}, f32[4,2304]{1,0:T(4,128)S(1)}, u32[]{:S(2)}, u32[]{:S(2)}) collective-permute-start(f32[4,2304]{1,0:T(4,128)S(1)} %concatenate.116), channel_id=1, source_target_pairs={{0,3},{1,0},{2,1},{3,2},{4,7},{5,4},{6,5},{7,6},{8,11},{9,8},{10,9... | collective-permute-start | bytes 110600 | tf_op jit(solution)/shard_map/ppermute | solution.py:57
  692.6 23.6 %collective-permute-start.33 = (bf16[128,2304]{1,0:T(8,128)(2,1)}, bf16[128,2304]{1,0:T(8,128)(2,1)S(1)}, u32[]{:S(2)}, u32[]{:S(2)}) collective-permute-start(bf16[128,2304]{1,0:T(8,128)(2,1)} %get-tuple-element.63), channel_id=1, source_target_pairs={{0,1},{1,2},{2,3},{3,0},{4,5},{5,6},{6,7},{7,4},{8,9},{9,10},{10,1... | collective-permute-start | bytes 1769480 | tf_op jit(solution)/shard_map/ppermute | solution.py:57
  692.6 29.3 %collective-permute-start.32 = (bf16[128,2304]{1,0:T(8,128)(2,1)}, bf16[128,2304]{1,0:T(8,128)(2,1)}, u32[]{:S(2)}, u32[]{:S(2)}) collective-permute-start(bf16[128,2304]{1,0:T(8,128)(2,1)} %get-tuple-element.62), channel_id=1, source_target_pairs={{0,3},{1,0},{2,1},{3,2},{4,7},{5,4},{6,5},{7,6},{8,11},{9,8},{10,9... | collective-permute-start | bytes 1769480 | tf_op jit(solution)/shard_map/ppermute | solution.py:57
  696.7 51.0 %collective-permute-start.31 = (bf16[128,2304]{1,0:T(8,128)(2,1)}, bf16[128,2304]{1,0:T(8,128)(2,1)}, u32[]{:S(2)}, u32[]{:S(2)}) collective-permute-start(bf16[128,2304]{1,0:T(8,128)(2,1)} %get-tuple-element.61), channel_id=1, source_target_pairs={{0,2},{1,3},{2,0},{3,1},{4,6},{5,7},{6,4},{7,5},{8,10},{9,11},{10,... | collective-permute-start | bytes 1769480 | tf_op jit(solution)/shard_map/ppermute | solution.py:57
  704.0 10.7 %collective-permute-start.42 = (f32[4,2304]{1,0:T(4,128)}, f32[4,2304]{1,0:T(4,128)}, u32[]{:S(2)}, u32[]{:S(2)}) collective-permute-start(f32[4,2304]{1,0:T(4,128)} %add.489), channel_id=1, source_target_pairs={{0,4},{4,0},{1,5},{5,1},{2,6},{6,2},{3,7},{7,3},{8,12},{12,8},{9,1... | collective-permute-start | bytes 110600 | tf_op jit(solution)/shard_map/ppermute | solution.py:144
  752.2 18.2 %collective-permute-start.34 = (bf16[128,2304]{1,0:T(8,128)(2,1)S(1)}, bf16[128,2304]{1,0:T(8,128)(2,1)S(1)}, u32[]{:S(2)}, u32[]{:S(2)}) collective-permute-start(bf16[128,2304]{1,0:T(8,128)(2,1)S(1)} %concatenate.115), channel_id=1, source_target_pairs={{0,1},{1,2},{2,3},{3,0},{4,5},{5,6},{6,7},{7,4},{8,9},{9,10},{10,1... | collective-permute-start | bytes 1769480 | tf_op jit(solution)/shard_map/ppermute | solution.py:57
  752.2 41.8 %collective-permute-start.35 = (bf16[128,2304]{1,0:T(8,128)(2,1)S(1)}, bf16[128,2304]{1,0:T(8,128)(2,1)S(1)}, u32[]{:S(2)}, u32[]{:S(2)}) collective-permute-start(bf16[128,2304]{1,0:T(8,128)(2,1)S(1)} %concatenate.115), channel_id=1, source_target_pairs={{0,2},{1,3},{2,0},{3,1},{4,6},{5,7},{6,4},{7,5},{8,10},{9,11},{10,... | collective-permute-start | bytes 1769480 | tf_op jit(solution)/shard_map/ppermute | solution.py:57
  753.8 40.3 %collective-permute-start.36 = (bf16[128,2304]{1,0:T(8,128)(2,1)S(1)}, bf16[128,2304]{1,0:T(8,128)(2,1)S(1)}, u32[]{:S(2)}, u32[]{:S(2)}) collective-permute-start(bf16[128,2304]{1,0:T(8,128)(2,1)S(1)} %concatenate.115), channel_id=1, source_target_pairs={{0,3},{1,0},{2,1},{3,2},{4,7},{5,4},{6,5},{7,6},{8,11},{9,8},{10,9... | collective-permute-start | bytes 1769480 | tf_op jit(solution)/shard_map/ppermute | solution.py:57
  (82 other events, 1005.9 us)
Sparse Core Ops, SparseCore 0:
  10.5 51.4 all-gather.2
  63.8 200.2 all-gather.4
  335.0 93.9 all-reduce.3
  611.3 59.7 reduce-scatter.3
  673.9 62.6 reduce-scatter.7
  739.5 104.5 reduce-scatter.5

commit v12 on v10

--- a/solution.py
+++ b/solution.py
@@ -341,11 +341,11 @@
     _, pull_glu = jax.vjp(geglu, gate_value, up_value)
     grad_gate, grad_up = pull_glu(product(grad_two_low, down_full))
     grad_gate_up = jnp.concatenate([grad_gate.astype(LOW), grad_up.astype(LOW)], axis=1)
-    grad_down_low = chip_rows(grad_two_low, hidden_low, down_arrived)
-    down_share = share_rows(grad_down_low)
     grad_normed_two = transposed_product(grad_gate_up, gate_up_full).astype(LOW)
     grad_normed_two = sent_scattered(ordered_blocks(grad_normed_two))
     outputs = by_chip((middle_all + rms(branch_two, post_feedforward_gain)).astype(LOW))
+    grad_down_low = chip_rows(grad_two_low, hidden_low, down_arrived)
+    down_share = share_rows(grad_down_low)
     gate_up_sent = sent_to_core(normed_two, grad_gate_up)
     gate_up_arrived = over_cores(gate_up_sent)
     grad_gate_up_low = chip_rows(normed_two, grad_gate_up, gate_up_arrived)
@@ -407,7 +407,7 @@
     qkv_arrived = over_cores(qkv_sent)
     grad_qkv_low = chip_rows(normed_one, grad_qkv, qkv_arrived)
     grad_attention = by_rows(jnp.concatenate([grad_qkv_low, grad_output_low], axis=1))
-    attention_share = share_rows(grad_attention).astype(F32)
+    attention_share = share_rows(grad_attention)
 
     unused_one, pull_one = jax.vjp(rms, inputs, pre_attention_gain)
     grad_inputs_low = by_chip((grad_middle + pull_one(grad_normed_one)[0]).astype(LOW))
@@ -417,13 +417,15 @@
     row_rank = lax.axis_index("fsdp") * lax.axis_size("ctx") + lax.axis_index("ctx")
     gain_shares = lax.dynamic_slice_in_dim(gains, row_rank * share, share, axis=1)
     edges = [0, heads_width, heads_width + kv_width, qkv_width, qkv_width + heads_width]
-    attention_shares = [attention_share[:, a:b] for a, b in zip(edges[:-1], edges[1:])]
-    gate_up_share = gate_up_share.astype(F32)
+    attention_shares = [attention_share[:, a:b].astype(F32) for a, b in zip(edges[:-1], edges[1:])]
+    gate_share = gate_up_share[:, :units].astype(F32)
+    up_share = gate_up_share[:, units:].astype(F32)
+    down_share = down_share.astype(F32)
     return (
         (outputs, grad_inputs)
         + tuple(gain_shares[i] for i in range(4))
         + tuple(attention_shares)
-        + (gate_up_share[:, :units], gate_up_share[:, units:], down_share.astype(F32))
+        + (gate_share, up_share, down_share)
     )
 
 

time: 843 us -> 843 us (level)
  other arithmetic: 61.3 us -> 70.2 us
  local copies, waits for them, and re-layouts: 95.5 us -> 86.6 us
    convert_element_type x1 -> x4, other arithmetic: 3.06 us -> 12 us  [the longest x1 4.49 us: shards(): up_share = gate_up_share[:, units:].astype(F32)]
    slice x3 -> x0, local copies, waits for them, and re-layouts: 8.89 us -> none  [the longest x1 4.49 us: shards(): gate_up_share[:, units:]]
where the time goes in v12:
time: 843 us; the launch traced here: 832 us
  waiting for transfers between devices  434 us (51%)
  matrix products  138 us (16%)
  starting transfers between devices  88.2 us (10%)
  local copies, waits for them, and re-layouts  86.6 us (10%)
  other arithmetic  70.2 us (8%)
  between operations  15.8 us (2%)
    ppermute x21, waiting for transfers between devices, shift(): lax.ppermute(block, 'tp', [(i, (i + distance) % size) for i in range(size)])  167 us
    psum x1, waiting for transfers between devices, shards(): lax.psum(transposed_product(hidden_low, down_full).astype(LOW), 'tp')  82 us
    dot_general x8, matrix products, rows_product(): lax.dot_general(left, right, (((0,), (0,)), ((), ())), preferred_element_...  46.7 us
    reduce_scatter x3, waiting for transfers between devices, share_rows(): lax.psum_scatter(grad, ROWS, scatter_dimension=0, tiled=True, axis_index_...  45.6 us
    ppermute x21, starting transfers between devices, shift(): lax.ppermute(block, 'tp', [(i, (i + distance) % size) for i in range(size)])  43.1 us
    dot_general x4, matrix products, product(): return jnp.dot(left, right, preferred_element_type=F32)  38.7 us
    all_gather x2, waiting for transfers between devices, gather_rows(): lax.all_gather(weight, ROWS, axis=0, tiled=True, axis_index_groups=[first...  38.3 us
    dot_general x4, matrix products, transposed_product(): lax.dot_general(left, right, (((1,), (1,)), ((), ())), preferred_element_...  37.9 us
  transfers between devices with their start and end apart: 56, of which 30 were waited for; matrix products, arithmetic and copies ran while one was open for 31% of the time, Pallas kernels for 0%

profile of v12, /device:TPU:0, one launch (start us, length us, event | category | flops | bytes accessed | tf_op | source)
XLA Modules:
  0.0 832.5 jit_solution(14298020081082912277)
XLA Ops:
  16.5 4.2 concatenate.62
  23.7 38.3 %all-gather.3.cloned.1.call-done = bf16[2304,1536]{1,0:T(8,128)(2,1)} async-done(((bf16[288,1536]{1,0:T(8,128)(2,1)}), bf16[2304,1536]{1,0:T(8,128)(2,1)}) %all-gather.3.cloned.1.call-update) | async-done | bytes 7077904 | tf_op jit(solution)/shard_map/all_gather | solution.py:184
  61.9 5.7 fusion.53
  68.4 4.1 collective-permute-start
  75.2 11.5 %collective-permute-done = bf16[384,512]{1,0:T(8,128)(2,1)} collective-permute-done((bf16[384,512]{1,0:T(8,128)(2,1)}, bf16[384,512]{1,0:T(8,128)(2,1)}, u32[]{:S(2)}, u32[]{:S(2)}) %collective-permute-start) | collective-permute-done | bytes 393248 | tf_op jit(solution)/shard_map/ppermute | solution.py:21
  98.4 4.0 collective-permute-start.1
  102.4 9.8 %collective-permute-done.1 = bf16[128,2304]{1,0:T(8,128)(2,1)} collective-permute-done((bf16[128,2304]{1,0:T(8,128)(2,1)S(1)}, bf16[128,2304]{1,0:T(8,128)(2,1)}, u32[]{:S(2)}, u32[]{:S(2)}) %collective-permute-start.1) | collective-permute-done | bytes 589856 | tf_op jit(solution)/shard_map/ppermute | solution.py:45
  113.9 4.5 collective-permute-start.3
  119.1 9.1 %collective-permute-done.3 = bf16[128,2304]{1,0:T(8,128)(2,1)S(1)} collective-permute-done((bf16[128,2304]{1,0:T(8,128)(2,1)S(1)}, bf16[128,2304]{1,0:T(8,128)(2,1)S(1)}, u32[]{:S(2)}, u32[]{:S(2)}) %collective-permute-start.3) | collective-permute-done | bytes 589856 | tf_op jit(solution)/shard_map/ppermute | solution.py:45
  131.4 6.0 collective-permute-start.5
  137.4 7.9 collective-permute-done.6
  151.6 4.3 collective-permute-start.7
  165.1 16.2 %collective-permute-done.16 = bf16[288,512]{1,0:T(8,128)(2,1)S(1)} collective-permute-done((bf16[288,512]{1,0:T(8,128)(2,1)S(1)}, bf16[288,512]{1,0:T(8,128)(2,1)S(1)}, u32[]{:S(2)}, u32[]{:S(2)}) %collective-permute-start.16) | collective-permute-done | bytes 294944 | tf_op jit(solution)/shard_map/ppermute | solution.py:57
  182.0 9.3 %collective-permute-done.17 = bf16[288,512]{1,0:T(8,128)(2,1)S(1)} collective-permute-done((bf16[288,512]{1,0:T(8,128)(2,1)S(1)}, bf16[288,512]{1,0:T(8,128)(2,1)S(1)}, u32[]{:S(2)}, u32[]{:S(2)}) %collective-permute-start.17) | collective-permute-done | bytes 294944 | tf_op jit(solution)/shard_map/ppermute | solution.py:57
  202.4 6.1 collective-permute-done.10
  212.0 5.2 concatenate.77
  217.8 5.5 concatenate.72
  225.5 4.8 broadcast_in_dim.149
  232.8 16.0 %collective-permute-done.19 = bf16[288,2048]{1,0:T(8,128)(2,1)} collective-permute-done((bf16[288,2048]{1,0:T(8,128)(2,1)}, bf16[288,2048]{1,0:T(8,128)(2,1)}, u32[]{:S(2)}, u32[]{:S(2)}) %collective-permute-start.19) | collective-permute-done | bytes 1179680 | tf_op jit(solution)/shard_map/ppermute | solution.py:196
  248.8 19.2 %collective-permute-done.20 = bf16[288,2048]{1,0:T(8,128)(2,1)} collective-permute-done((bf16[288,2048]{1,0:T(8,128)(2,1)}, bf16[288,2048]{1,0:T(8,128)(2,1)}, u32[]{:S(2)}, u32[]{:S(2)}) %collective-permute-start.20) | collective-permute-done | bytes 1179680 | tf_op jit(solution)/shard_map/ppermute | solution.py:196
  279.0 5.9 multiply_convert_fusion.2
  284.9 15.2 %fusion.2 = f32[512,4608]{1,0:T(8,128)S(1)} fusion(bf16[512,2304]{1,0:T(8,128)(2,1)} %get-tuple-element.94, bf16[2304,6912]{1,0:T(8,128)(2,1)} %all-gather.5.cloned.1.call-done), kind=kOutput, calls=%fused_computation.4 | convolution fusion | flops 10871635968 | bytes 33030144 | tf_op jit(solution)/shard_map/dot_general | solution.py:33
  305.1 11.0 %fusion.29 = bf16[512,2304]{1,0:T(8,128)(2,1)} fusion(bf16[512,2304]{1,0:T(8,128)(2,1)S(1)} %multiply_convert_fusion.1, bf16[2304,6912]{1,0:T(8,128)(2,1)} %all-gather.5.cloned.1.call-done), kind=kOutput, calls=%fused_computation.53 | convolution fusion | flops 5436997632 | bytes 15335424 | tf_op jit(solution)/shard_map/dot_general | solution.py:41
  328.9 82.0 %all-reduce.4.cloned.1.call-done = bf16[512,2304]{1,0:T(8,128)(2,1)} async-done(((bf16[512,2304]{1,0:T(8,128)(2,1)}), bf16[512,2304]{1,0:T(8,128)(2,1)}) %all-reduce.4.cloned.1.call-update) | async-done | bytes 2359312 | tf_op jit(solution)/shard_map/psum | solution.py:329
  416.7 5.1 fusion.25
  421.8 5.1 convolution_convert_fusion.1
  427.0 12.8 %fusion.23 = (bf16[512,2304]{1,0:T(8,128)(2,1)S(1)}, bf16[512,2304]{1,0:T(8,128)(2,1)}) fusion(f32[512,4608]{1,0:T(8,128)S(1)} %bitcast.225, bf16[512,2304]{1,0:T(8,128)(2,1)S(1)} %get-tuple-element.58, bf16[2304,6912]{1,0:T(8,128)(2,1)} %all-gather.5.cloned.1.call-done), kind=kOutput, calls=%fused_computation.39 | convolution fusion | flops 5464129536 | bytes 27131904 | tf_op jit(solution)/shard_map/dot_general | solution.py:33
  439.7 16.1 %fusion.32 = bf16[512,2304]{1,0:T(8,128)(2,1)S(1)} fusion(bf16[2304,6912]{1,0:T(8,128)(2,1)} %all-gather.5.cloned.1.call-done, bf16[512,2304]{1,0:T(8,128)(2,1)} %get-tuple-element.102, bf16[512,2304]{1,0:T(8,128)(2,1)S(1)} %get-tuple-element.101), kind=kOutput, calls=%fused_computation.54 | convolution fusion | flops 10882252800 | bytes 28311552 | tf_op jit(solution)/shard_map/dot_general | solution.py:41
  465.0 9.1 %collective-permute-done.15 = bf16[128,2304]{1,0:T(8,128)(2,1)S(1)} collective-permute-done((bf16[128,2304]{1,0:T(8,128)(2,1)S(1)}, bf16[128,2304]{1,0:T(8,128)(2,1)S(1)}, u32[]{:S(2)}, u32[]{:S(2)}) %collective-permute-start.15) | collective-permute-done | bytes 589856 | tf_op jit(solution)/shard_map/ppermute | solution.py:57
  474.1 9.8 %collective-permute-done.14 = bf16[128,2304]{1,0:T(8,128)(2,1)S(1)} collective-permute-done((bf16[128,2304]{1,0:T(8,128)(2,1)S(1)}, bf16[128,2304]{1,0:T(8,128)(2,1)S(1)}, u32[]{:S(2)}, u32[]{:S(2)}) %collective-permute-start.14) | collective-permute-done | bytes 589856 | tf_op jit(solution)/shard_map/ppermute | solution.py:57
  483.9 26.4 %collective-permute-done.13 = bf16[128,2304]{1,0:T(8,128)(2,1)S(1)} collective-permute-done((bf16[128,2304]{1,0:T(8,128)(2,1)S(1)}, bf16[128,2304]{1,0:T(8,128)(2,1)S(1)}, u32[]{:S(2)}, u32[]{:S(2)}) %collective-permute-start.13) | collective-permute-done | bytes 589856 | tf_op jit(solution)/shard_map/ppermute | solution.py:57
  514.8 5.1 convolution_convert_fusion.6
  522.2 8.0 collective-permute-done.26
  551.6 3.9 collective-permute-done.29
  559.8 11.4 %collective-permute-done.45 = bf16[128,2304]{1,0:T(8,128)(2,1)} collective-permute-done((bf16[128,2304]{1,0:T(8,128)(2,1)S(1)}, bf16[128,2304]{1,0:T(8,128)(2,1)}, u32[]{:S(2)}, u32[]{:S(2)}) %collective-permute-start.45) | collective-permute-done | bytes 589856 | tf_op jit(solution)/shard_map/ppermute | solution.py:57
  588.4 10.7 %convolution_convert_fusion = bf16[1152,4608]{1,0:T(8,128)(2,1)} fusion(bf16[512,2304]{1,0:T(8,128)(2,1)} %get-tuple-element.102, bf16[512,2304]{1,0:T(8,128)(2,1)} %copy-done.72, bf16[512,2304]{1,0:T(8,128)(2,1)S(1)} %copy-done.24, s32[]{:T(128)S(6)} %select_n.252), kind=kOutput, calls=%fused_computation.1 | convolution fusion | flops 5450563584 | bytes 16515076 | tf_op jit(solution)/shard_map/dot_general | solution.py:37
  599.3 6.8 add_convert_fusion.1
  606.4 9.4 %collective-permute-done.48 = bf16[1152,4608]{1,0:T(8,128)(2,1)} collective-permute-done((bf16[1152,4608]{1,0:T(8,128)(2,1)}, bf16[1152,4608]{1,0:T(8,128)(2,1)}, u32[]{:S(2)}, u32[]{:S(2)}) %collective-permute-start.48) | collective-permute-done | bytes 10616864 | tf_op jit(solution)/shard_map/ppermute | solution.py:224
  615.8 13.5 %add_convert_fusion = bf16[1152,4608]{1,0:T(8,128)(2,1)} fusion(bf16[1152,4608]{1,0:T(8,128)(2,1)} %collective-permute-done.48, bf16[512,2304]{1,0:T(8,128)(2,1)} %get-tuple-element.102, bf16[512,2304]{1,0:T(8,128)(2,1)} %copy-done.72, bf16[512,2304]{1,0:T(8,128)(2,1)S(1)} %copy-done.24, s32[]{:T(128)S(6)} %select_n.273), kind=kOutput, calls=%fused_computation | convolution fusion | flops 5461180416 | bytes 27131908 | tf_op jit(solution)/shard_map/dot_general | solution.py:37
  633.2 7.5 fusion.15
  641.0 15.6 %collective-permute-start.39 = (f32[4,2304]{1,0:T(4,128)S(1)}, f32[4,2304]{1,0:T(4,128)S(1)}, u32[]{:S(2)}, u32[]{:S(2)}) collective-permute-start(f32[4,2304]{1,0:T(4,128)S(1)} %concatenate.82), channel_id=1, source_target_pairs={{0,3},{1,0},{2,1},{3,2},{4,7},{5,4},{6,5},{7,6},{8,11},{9,8},{10,9... | collective-permute-start | bytes 110600 | tf_op jit(solution)/shard_map/ppermute | solution.py:57
  680.1 5.1 concatenate.76
  686.8 8.0 collective-permute-done.32
  694.8 25.6 %collective-permute-done.31 = bf16[128,2304]{1,0:T(8,128)(2,1)} collective-permute-done((bf16[128,2304]{1,0:T(8,128)(2,1)}, bf16[128,2304]{1,0:T(8,128)(2,1)}, u32[]{:S(2)}, u32[]{:S(2)}) %collective-permute-start.31) | collective-permute-done | bytes 589856 | tf_op jit(solution)/shard_map/ppermute | solution.py:57
  729.5 14.1 %collective-permute-done.34 = bf16[128,2304]{1,0:T(8,128)(2,1)S(1)} collective-permute-done((bf16[128,2304]{1,0:T(8,128)(2,1)S(1)}, bf16[128,2304]{1,0:T(8,128)(2,1)S(1)}, u32[]{:S(2)}, u32[]{:S(2)}) %collective-permute-start.34) | collective-permute-done | bytes 589856 | tf_op jit(solution)/shard_map/ppermute | solution.py:57
  743.6 23.9 %collective-permute-done.35 = bf16[128,2304]{1,0:T(8,128)(2,1)S(1)} collective-permute-done((bf16[128,2304]{1,0:T(8,128)(2,1)S(1)}, bf16[128,2304]{1,0:T(8,128)(2,1)S(1)}, u32[]{:S(2)}, u32[]{:S(2)}) %collective-permute-start.35) | collective-permute-done | bytes 589856 | tf_op jit(solution)/shard_map/ppermute | solution.py:57
  775.1 45.6 %reduce-scatter.6.cloned.1.call-done = bf16[288,4608]{1,0:T(8,128)(2,1)} async-done(((bf16[1152,4608]{1,0:T(8,128)(2,1)}), bf16[288,4608]{1,0:T(8,128)(2,1)}) %reduce-scatter.6.cloned.1.call-update) | async-done | bytes 2654224 | tf_op jit(solution)/shard_map/reduce_scatter | solution.py:233
  820.7 4.5 slice_convert_fusion
  (363 shorter events, 207.8 us)
Async XLA Ops:
  7.2 54.7 %all-gather.3.cloned.1.call-start = ((), (), s32[]{:S(2)}) async-start(), calls=%async_computation.3 | async-start | bytes 7962624 | tf_op jit(solution)/shard_map/all_gather | solution.py:184
  9.5 275.4 %all-gather.5.cloned.1.call-start = ((), (), s32[]{:S(2)}) async-start(), calls=%async_computation.4 | async-start | bytes 35831808 | tf_op jit(solution)/shard_map/all_gather | solution.py:184
  12.9 398.0 %all-reduce.4.cloned.1.call-start = ((), (), s32[]{:S(2)}) async-start(), calls=%async_computation.5 | async-start | bytes 4718592 | tf_op jit(solution)/shard_map/psum | solution.py:329
  68.4 18.3 %collective-permute-start = (bf16[384,512]{1,0:T(8,128)(2,1)}, bf16[384,512]{1,0:T(8,128)(2,1)}, u32[]{:S(2)}, u32[]{:S(2)}) collective-permute-start(bf16[384,512]{1,0:T(8,128)(2,1)} %slice.274), channel_id=1, source_target_pairs={{0,4},{1,5},{2,6},{3,7},{8,12},{9,13},{10,14},{11,15},{16,20},{17,... | collective-permute-start | bytes 1179656 | tf_op jit(solution)/shard_map/ppermute | solution.py:21
  98.4 13.8 %collective-permute-start.1 = (bf16[128,2304]{1,0:T(8,128)(2,1)S(1)}, bf16[128,2304]{1,0:T(8,128)(2,1)}, u32[]{:S(2)}, u32[]{:S(2)}) collective-permute-start(bf16[128,2304]{1,0:T(8,128)(2,1)S(1)} %get-tuple-element.46), channel_id=1, source_target_pairs={{0,1},{4,5},{8,9},{12,13},{16,17},{20,21},{24,25},{28,29}} | collective-permute-start | bytes 1769480 | tf_op jit(solution)/shard_map/ppermute | solution.py:45
  113.9 14.3 %collective-permute-start.3 = (bf16[128,2304]{1,0:T(8,128)(2,1)S(1)}, bf16[128,2304]{1,0:T(8,128)(2,1)S(1)}, u32[]{:S(2)}, u32[]{:S(2)}) collective-permute-start(bf16[128,2304]{1,0:T(8,128)(2,1)S(1)} %get-tuple-element.48), channel_id=1, source_target_pairs={{0,1},{1,2},{4,5},{5,6},{8,9},{9,10},{12,13},{13,14},{16,17},{17,1... | collective-permute-start | bytes 1769480 | tf_op jit(solution)/shard_map/ppermute | solution.py:45
  118.4 10.7 %collective-permute-start.4 = (bf16[128,2304]{1,0:T(8,128)(2,1)S(1)}, bf16[128,2304]{1,0:T(8,128)(2,1)S(1)}, u32[]{:S(2)}, u32[]{:S(2)}) collective-permute-start(bf16[128,2304]{1,0:T(8,128)(2,1)S(1)} %get-tuple-element.49), channel_id=1, source_target_pairs={{2,1},{3,2},{6,5},{7,6},{10,9},{11,10},{14,13},{15,14},{18,17},{19... | collective-permute-start | bytes 1769480 | tf_op jit(solution)/shard_map/ppermute | solution.py:45
  130.1 15.3 %collective-permute-start.6 = (bf16[128,2304]{1,0:T(8,128)(2,1)}, bf16[128,2304]{1,0:T(8,128)(2,1)S(1)}, u32[]{:S(2)}, u32[]{:S(2)}) collective-permute-start(bf16[128,2304]{1,0:T(8,128)(2,1)} %add_convert_fusion.3), channel_id=1, source_target_pairs={{1,0},{2,1},{3,2},{5,4},{6,5},{7,6},{9,8},{10,9},{11,10},{13,12},{... | collective-permute-start | bytes 1769480 | tf_op jit(solution)/shard_map/ppermute | solution.py:45
  131.4 15.3 %collective-permute-start.5 = (bf16[128,2304]{1,0:T(8,128)(2,1)}, bf16[128,2304]{1,0:T(8,128)(2,1)S(1)}, u32[]{:S(2)}, u32[]{:S(2)}) collective-permute-start(bf16[128,2304]{1,0:T(8,128)(2,1)} %add_convert_fusion.4), channel_id=1, source_target_pairs={{0,1},{1,2},{2,3},{4,5},{5,6},{6,7},{8,9},{9,10},{10,11},{12,13},{... | collective-permute-start | bytes 1769480 | tf_op jit(solution)/shard_map/ppermute | solution.py:45
  151.6 40.4 %collective-permute-start.7 = (bf16[128,2304]{1,0:T(8,128)(2,1)S(1)}, bf16[128,2304]{1,0:T(8,128)(2,1)S(1)}, u32[]{:S(2)}, u32[]{:S(2)}) collective-permute-start(bf16[128,2304]{1,0:T(8,128)(2,1)S(1)} %get-tuple-element.97), channel_id=1, source_target_pairs={{0,1},{1,2},{2,3},{4,5},{5,6},{6,7},{8,9},{9,10},{10,11},{12,13},{... | collective-permute-start | bytes 1769480 | tf_op jit(solution)/shard_map/ppermute | solution.py:45
  155.9 36.1 %collective-permute-start.8 = (bf16[128,2304]{1,0:T(8,128)(2,1)S(1)}, bf16[128,2304]{1,0:T(8,128)(2,1)S(1)}, u32[]{:S(2)}, u32[]{:S(2)}) collective-permute-start(bf16[128,2304]{1,0:T(8,128)(2,1)S(1)} %get-tuple-element.97), channel_id=1, source_target_pairs={{1,0},{2,1},{3,2},{5,4},{6,5},{7,6},{9,8},{10,9},{11,10},{13,12},{... | collective-permute-start | bytes 1769480 | tf_op jit(solution)/shard_map/ppermute | solution.py:45
  157.3 24.0 %collective-permute-start.16 = (bf16[288,512]{1,0:T(8,128)(2,1)S(1)}, bf16[288,512]{1,0:T(8,128)(2,1)S(1)}, u32[]{:S(2)}, u32[]{:S(2)}) collective-permute-start(bf16[288,512]{1,0:T(8,128)(2,1)S(1)} %copy-done.35), channel_id=1, source_target_pairs={{0,1},{1,2},{2,3},{3,0},{4,5},{5,6},{6,7},{7,4},{8,9},{9,10},{10,1... | collective-permute-start | bytes 884744 | tf_op jit(solution)/shard_map/ppermute | solution.py:57
  160.2 31.1 %collective-permute-start.17 = (bf16[288,512]{1,0:T(8,128)(2,1)S(1)}, bf16[288,512]{1,0:T(8,128)(2,1)S(1)}, u32[]{:S(2)}, u32[]{:S(2)}) collective-permute-start(bf16[288,512]{1,0:T(8,128)(2,1)S(1)} %copy-done.35), channel_id=1, source_target_pairs={{0,2},{1,3},{2,0},{3,1},{4,6},{5,7},{6,4},{7,5},{8,10},{9,11},{10,... | collective-permute-start | bytes 884744 | tf_op jit(solution)/shard_map/ppermute | solution.py:57
  161.6 33.2 %collective-permute-start.18 = (bf16[288,512]{1,0:T(8,128)(2,1)S(1)}, bf16[288,512]{1,0:T(8,128)(2,1)S(1)}, u32[]{:S(2)}, u32[]{:S(2)}) collective-permute-start(bf16[288,512]{1,0:T(8,128)(2,1)S(1)} %copy-done.35), channel_id=1, source_target_pairs={{0,3},{1,0},{2,1},{3,2},{4,7},{5,4},{6,5},{7,6},{8,11},{9,8},{10,9... | collective-permute-start | bytes 884744 | tf_op jit(solution)/shard_map/ppermute | solution.py:57
  192.1 10.3 %collective-permute-start.9 = (bf16[128,2304]{1,0:T(8,128)(2,1)S(1)}, bf16[128,2304]{1,0:T(8,128)(2,1)}, u32[]{:S(2)}, u32[]{:S(2)}) collective-permute-start(bf16[128,2304]{1,0:T(8,128)(2,1)S(1)} %collective-permute-done.7), channel_id=1, source_target_pairs={{1,2},{2,3},{5,6},{6,7},{9,10},{10,11},{13,14},{14,15},{17,18},{18... | collective-permute-start | bytes 1769480 | tf_op jit(solution)/shard_map/ppermute | solution.py:45
  193.6 14.9 %collective-permute-start.10 = (bf16[128,2304]{1,0:T(8,128)(2,1)S(1)}, bf16[128,2304]{1,0:T(8,128)(2,1)}, u32[]{:S(2)}, u32[]{:S(2)}) collective-permute-start(bf16[128,2304]{1,0:T(8,128)(2,1)S(1)} %collective-permute-done.8), channel_id=1, source_target_pairs={{1,0},{2,1},{5,4},{6,5},{9,8},{10,9},{13,12},{14,13},{17,16},{18,1... | collective-permute-start | bytes 1769480 | tf_op jit(solution)/shard_map/ppermute | solution.py:45
  195.6 53.2 %collective-permute-start.19 = (bf16[288,2048]{1,0:T(8,128)(2,1)}, bf16[288,2048]{1,0:T(8,128)(2,1)}, u32[]{:S(2)}, u32[]{:S(2)}) collective-permute-start(bf16[288,2048]{1,0:T(8,128)(2,1)} %constant_dynamic-update-slice_fusion), channel_id=1, source_target_pairs={{0,20},{4,16},{8,28},{12,24},{16,4},{20,0},{24,12},{28,8},{1,21},{... | collective-permute-start | bytes 3538952 | tf_op jit(solution)/shard_map/ppermute | solution.py:196
  197.2 70.8 %collective-permute-start.20 = (bf16[288,2048]{1,0:T(8,128)(2,1)}, bf16[288,2048]{1,0:T(8,128)(2,1)}, u32[]{:S(2)}, u32[]{:S(2)}) collective-permute-start(bf16[288,2048]{1,0:T(8,128)(2,1)} %constant_dynamic-update-slice_fusion), channel_id=1, source_target_pairs={{0,4},{4,0},{8,12},{12,8},{16,20},{20,16},{24,28},{28,24},{1,5},{5... | collective-permute-start | bytes 3538952 | tf_op jit(solution)/shard_map/ppermute | solution.py:196
  198.1 69.9 %collective-permute-start.21 = (bf16[288,2048]{1,0:T(8,128)(2,1)}, bf16[288,2048]{1,0:T(8,128)(2,1)}, u32[]{:S(2)}, u32[]{:S(2)}) collective-permute-start(bf16[288,2048]{1,0:T(8,128)(2,1)} %constant_dynamic-update-slice_fusion), channel_id=1, source_target_pairs={{0,16},{4,20},{8,24},{12,28},{16,0},{20,4},{24,8},{28,12},{1,17},{... | collective-permute-start | bytes 3538952 | tf_op jit(solution)/shard_map/ppermute | solution.py:196
  208.5 60.0 %collective-permute-start.11 = (bf16[128,2304]{1,0:T(8,128)(2,1)}, bf16[128,2304]{1,0:T(8,128)(2,1)}, u32[]{:S(2)}, u32[]{:S(2)}) collective-permute-start(bf16[128,2304]{1,0:T(8,128)(2,1)} %collective-permute-done.9), channel_id=1, source_target_pairs={{2,3},{6,7},{10,11},{14,15},{18,19},{22,23},{26,27},{30,31}} | collective-permute-start | bytes 1769480 | tf_op jit(solution)/shard_map/ppermute | solution.py:45
  210.0 58.6 %collective-permute-start.12 = (bf16[128,2304]{1,0:T(8,128)(2,1)}, bf16[128,2304]{1,0:T(8,128)(2,1)}, u32[]{:S(2)}, u32[]{:S(2)}) collective-permute-start(bf16[128,2304]{1,0:T(8,128)(2,1)} %collective-permute-done.10), channel_id=1, source_target_pairs={{1,0},{5,4},{9,8},{13,12},{17,16},{21,20},{25,24},{29,28}} | collective-permute-start | bytes 1769480 | tf_op jit(solution)/shard_map/ppermute | solution.py:45
  248.8 75.1 %collective-permute-start.22 = (bf16[288,2048]{1,0:T(8,128)(2,1)}, bf16[288,2048]{1,0:T(8,128)(2,1)}, u32[]{:S(2)}, u32[]{:S(2)}) collective-permute-start(bf16[288,2048]{1,0:T(8,128)(2,1)} %constant_dynamic-update-slice_fusion), channel_id=1, source_target_pairs={{0,8},{4,12},{8,0},{12,4},{16,24},{20,28},{24,16},{28,20},{1,9},{5... | collective-permute-start | bytes 3538952 | tf_op jit(solution)/shard_map/ppermute | solution.py:196
  268.0 58.3 %collective-permute-start.23 = (bf16[288,2048]{1,0:T(8,128)(2,1)}, bf16[288,2048]{1,0:T(8,128)(2,1)}, u32[]{:S(2)}, u32[]{:S(2)}) collective-permute-start(bf16[288,2048]{1,0:T(8,128)(2,1)} %collective-permute-done.20), channel_id=1, source_target_pairs={{0,8},{4,12},{8,0},{12,4},{16,24},{20,28},{24,16},{28,20},{1,9},{5... | collective-permute-start | bytes 3538952 | tf_op jit(solution)/shard_map/ppermute | solution.py:196
  268.0 192.1 %collective-permute-start.24 = (bf16[288,2048]{1,0:T(8,128)(2,1)}, bf16[288,2048]{1,0:T(8,128)(2,1)}, u32[]{:S(2)}, u32[]{:S(2)}) collective-permute-start(bf16[288,2048]{1,0:T(8,128)(2,1)} %collective-permute-done.21), channel_id=1, source_target_pairs={{0,8},{4,12},{8,0},{12,4},{16,24},{20,28},{24,16},{28,20},{1,9},{5... | collective-permute-start | bytes 3538952 | tf_op jit(solution)/shard_map/ppermute | solution.py:196
  268.5 194.0 %collective-permute-start.25 = (bf16[288,2048]{1,0:T(8,128)(2,1)}, bf16[288,2048]{1,0:T(8,128)(2,1)}, u32[]{:S(2)}, u32[]{:S(2)}) collective-permute-start(bf16[288,2048]{1,0:T(8,128)(2,1)} %collective-permute-done.19), channel_id=1, source_target_pairs={{0,8},{4,12},{8,0},{12,4},{16,24},{20,28},{24,16},{28,20},{1,9},{5... | collective-permute-start | bytes 3538952 | tf_op jit(solution)/shard_map/ppermute | solution.py:196
  316.1 451.6 %reduce-scatter.4.cloned.1.call-start = ((), (), s32[]{:S(2)}) async-start(), calls=%async_computation.6 | async-start | bytes 4423680 | tf_op jit(solution)/shard_map/reduce_scatter | solution.py:233
  456.1 18.1 %collective-permute-start.15 = (bf16[128,2304]{1,0:T(8,128)(2,1)S(1)}, bf16[128,2304]{1,0:T(8,128)(2,1)S(1)}, u32[]{:S(2)}, u32[]{:S(2)}) collective-permute-start(bf16[128,2304]{1,0:T(8,128)(2,1)S(1)} %get-tuple-element.62), channel_id=1, source_target_pairs={{0,1},{1,2},{2,3},{3,0},{4,5},{5,6},{6,7},{7,4},{8,9},{9,10},{10,1... | collective-permute-start | bytes 1769480 | tf_op jit(solution)/shard_map/ppermute | solution.py:57
  456.3 27.6 %collective-permute-start.14 = (bf16[128,2304]{1,0:T(8,128)(2,1)S(1)}, bf16[128,2304]{1,0:T(8,128)(2,1)S(1)}, u32[]{:S(2)}, u32[]{:S(2)}) collective-permute-start(bf16[128,2304]{1,0:T(8,128)(2,1)S(1)} %get-tuple-element.61), channel_id=1, source_target_pairs={{0,3},{1,0},{2,1},{3,2},{4,7},{5,4},{6,5},{7,6},{8,11},{9,8},{10,9... | collective-permute-start | bytes 1769480 | tf_op jit(solution)/shard_map/ppermute | solution.py:57
  460.1 50.2 %collective-permute-start.13 = (bf16[128,2304]{1,0:T(8,128)(2,1)S(1)}, bf16[128,2304]{1,0:T(8,128)(2,1)S(1)}, u32[]{:S(2)}, u32[]{:S(2)}) collective-permute-start(bf16[128,2304]{1,0:T(8,128)(2,1)S(1)} %get-tuple-element.60), channel_id=1, source_target_pairs={{0,2},{1,3},{2,0},{3,1},{4,6},{5,7},{6,4},{7,5},{8,10},{9,11},{10,... | collective-permute-start | bytes 1769480 | tf_op jit(solution)/shard_map/ppermute | solution.py:57
  520.0 10.2 %collective-permute-start.26 = (bf16[128,512]{1,0:T(8,128)(2,1)S(1)}, bf16[128,512]{1,0:T(8,128)(2,1)S(1)}, u32[]{:S(2)}, u32[]{:S(2)}) collective-permute-start(bf16[128,512]{1,0:T(8,128)(2,1)S(1)} %get-tuple-element.64), channel_id=1, source_target_pairs={{0,2},{1,3},{2,0},{3,1},{4,6},{5,7},{6,4},{7,5},{8,10},{9,11},{10,... | collective-permute-start | bytes 393224 | tf_op jit(solution)/shard_map/ppermute | solution.py:57
  520.1 10.6 %collective-permute-start.27 = (bf16[128,512]{1,0:T(8,128)(2,1)S(1)}, bf16[128,512]{1,0:T(8,128)(2,1)S(1)}, u32[]{:S(2)}, u32[]{:S(2)}) collective-permute-start(bf16[128,512]{1,0:T(8,128)(2,1)S(1)} %get-tuple-element.65), channel_id=1, source_target_pairs={{0,3},{1,0},{2,1},{3,2},{4,7},{5,4},{6,5},{7,6},{8,11},{9,8},{10,9... | collective-permute-start | bytes 393224 | tf_op jit(solution)/shard_map/ppermute | solution.py:57
  530.7 27.9 %collective-permute-start.44 = (bf16[128,2304]{1,0:T(8,128)(2,1)S(1)}, bf16[128,2304]{1,0:T(8,128)(2,1)}, u32[]{:S(2)}, u32[]{:S(2)}) collective-permute-start(bf16[128,2304]{1,0:T(8,128)(2,1)S(1)} %fusion.69), channel_id=1, source_target_pairs={{0,1},{1,2},{2,3},{3,0},{4,5},{5,6},{6,7},{7,4},{8,9},{9,10},{10,1... | collective-permute-start | bytes 1769480 | tf_op jit(solution)/shard_map/ppermute | solution.py:57
  533.2 38.0 %collective-permute-start.45 = (bf16[128,2304]{1,0:T(8,128)(2,1)S(1)}, bf16[128,2304]{1,0:T(8,128)(2,1)}, u32[]{:S(2)}, u32[]{:S(2)}) collective-permute-start(bf16[128,2304]{1,0:T(8,128)(2,1)S(1)} %fusion.69), channel_id=1, source_target_pairs={{0,2},{1,3},{2,0},{3,1},{4,6},{5,7},{6,4},{7,5},{8,10},{9,11},{10,... | collective-permute-start | bytes 1769480 | tf_op jit(solution)/shard_map/ppermute | solution.py:57
  534.1 38.2 %collective-permute-start.46 = (bf16[128,2304]{1,0:T(8,128)(2,1)S(1)}, bf16[128,2304]{1,0:T(8,128)(2,1)S(1)}, u32[]{:S(2)}, u32[]{:S(2)}) collective-permute-start(bf16[128,2304]{1,0:T(8,128)(2,1)S(1)} %fusion.69), channel_id=1, source_target_pairs={{0,3},{1,0},{2,1},{3,2},{4,7},{5,4},{6,5},{7,6},{8,11},{9,8},{10,9... | collective-permute-start | bytes 1769480 | tf_op jit(solution)/shard_map/ppermute | solution.py:57
  541.7 9.9 %collective-permute-start.30 = (bf16[384,256]{0,1:T(8,128)(2,1)S(1)}, bf16[384,256]{0,1:T(8,128)(2,1)S(1)}, u32[]{:S(2)}, u32[]{:S(2)}) collective-permute-start(bf16[384,256]{0,1:T(8,128)(2,1)S(1)} %fusion.96), channel_id=1, source_target_pairs={{4,0},{5,1},{6,2},{7,3},{12,8},{13,9},{14,10},{15,11},{20,16},{21,... | collective-permute-start | bytes 589832 | tf_op jit(solution)/shard_map/ppermute | solution.py:21
  558.5 23.0 %collective-permute-start.43 = (bf16[1152,1024]{1,0:T(8,128)(2,1)}, bf16[1152,1024]{1,0:T(8,128)(2,1)}, u32[]{:S(2)}, u32[]{:S(2)}) collective-permute-start(bf16[1152,1024]{1,0:T(8,128)(2,1)} %convolution_convert_fusion.4), channel_id=1, source_target_pairs={{0,8},{8,0},{16,24},{24,16},{1,9},{9,1},{17,25},{25,17},{2,10},{10... | collective-permute-start | bytes 7077896 | tf_op jit(solution)/shard_map/ppermute | solution.py:224
  586.8 185.3 %reduce-scatter.8.cloned.1.call-start = ((), (), s32[]{:S(2)}) async-start(), calls=%async_computation.8 | async-start | bytes 6635520 | tf_op jit(solution)/shard_map/reduce_scatter | solution.py:233
  586.8 12.4 %collective-permute-start.49 = (bf16[1152,2304]{1,0:T(8,128)(2,1)}, bf16[1152,2304]{1,0:T(8,128)(2,1)}, u32[]{:S(2)}, u32[]{:S(2)}) collective-permute-start(bf16[1152,2304]{1,0:T(8,128)(2,1)} %convolution_convert_fusion.1), channel_id=1, source_target_pairs={{0,8},{8,0},{16,24},{24,16},{1,9},{9,1},{17,25},{25,17},{2,10},{10... | collective-permute-start | bytes 15925256 | tf_op jit(solution)/shard_map/ppermute | solution.py:224
  599.1 16.7 %collective-permute-start.48 = (bf16[1152,4608]{1,0:T(8,128)(2,1)}, bf16[1152,4608]{1,0:T(8,128)(2,1)}, u32[]{:S(2)}, u32[]{:S(2)}) collective-permute-start(bf16[1152,4608]{1,0:T(8,128)(2,1)} %convolution_convert_fusion), channel_id=1, source_target_pairs={{0,8},{8,0},{16,24},{24,16},{1,9},{9,1},{17,25},{25,17},{2,10},{10... | collective-permute-start | bytes 31850504 | tf_op jit(solution)/shard_map/ppermute | solution.py:224
  606.1 214.6 %reduce-scatter.6.cloned.1.call-start = ((), (), s32[]{:S(2)}) async-start(), calls=%async_computation.7 | async-start | bytes 13271040 | tf_op jit(solution)/shard_map/reduce_scatter | solution.py:233
  641.0 17.4 %collective-permute-start.39 = (f32[4,2304]{1,0:T(4,128)S(1)}, f32[4,2304]{1,0:T(4,128)S(1)}, u32[]{:S(2)}, u32[]{:S(2)}) collective-permute-start(f32[4,2304]{1,0:T(4,128)S(1)} %concatenate.82), channel_id=1, source_target_pairs={{0,3},{1,0},{2,1},{3,2},{4,7},{5,4},{6,5},{7,6},{8,11},{9,8},{10,9... | collective-permute-start | bytes 110600 | tf_op jit(solution)/shard_map/ppermute | solution.py:57
  665.6 21.2 %collective-permute-start.33 = (bf16[128,2304]{1,0:T(8,128)(2,1)}, bf16[128,2304]{1,0:T(8,128)(2,1)}, u32[]{:S(2)}, u32[]{:S(2)}) collective-permute-start(bf16[128,2304]{1,0:T(8,128)(2,1)} %get-tuple-element.71), channel_id=1, source_target_pairs={{0,1},{1,2},{2,3},{3,0},{4,5},{5,6},{6,7},{7,4},{8,9},{9,10},{10,1... | collective-permute-start | bytes 1769480 | tf_op jit(solution)/shard_map/ppermute | solution.py:57
  665.6 29.2 %collective-permute-start.32 = (bf16[128,2304]{1,0:T(8,128)(2,1)}, bf16[128,2304]{1,0:T(8,128)(2,1)}, u32[]{:S(2)}, u32[]{:S(2)}) collective-permute-start(bf16[128,2304]{1,0:T(8,128)(2,1)} %get-tuple-element.70), channel_id=1, source_target_pairs={{0,3},{1,0},{2,1},{3,2},{4,7},{5,4},{6,5},{7,6},{8,11},{9,8},{10,9... | collective-permute-start | bytes 1769480 | tf_op jit(solution)/shard_map/ppermute | solution.py:57
  669.4 51.0 %collective-permute-start.31 = (bf16[128,2304]{1,0:T(8,128)(2,1)}, bf16[128,2304]{1,0:T(8,128)(2,1)}, u32[]{:S(2)}, u32[]{:S(2)}) collective-permute-start(bf16[128,2304]{1,0:T(8,128)(2,1)} %get-tuple-element.69), channel_id=1, source_target_pairs={{0,2},{1,3},{2,0},{3,1},{4,6},{5,7},{6,4},{7,5},{8,10},{9,11},{10,... | collective-permute-start | bytes 1769480 | tf_op jit(solution)/shard_map/ppermute | solution.py:57
  675.1 10.2 %collective-permute-start.42 = (f32[4,2304]{1,0:T(4,128)}, f32[4,2304]{1,0:T(4,128)}, u32[]{:S(2)}, u32[]{:S(2)}) collective-permute-start(f32[4,2304]{1,0:T(4,128)} %add.446), channel_id=1, source_target_pairs={{0,4},{4,0},{1,5},{5,1},{2,6},{6,2},{3,7},{7,3},{8,12},{12,8},{9,1... | collective-permute-start | bytes 110600 | tf_op jit(solution)/shard_map/ppermute | solution.py:144
  725.4 18.1 %collective-permute-start.34 = (bf16[128,2304]{1,0:T(8,128)(2,1)S(1)}, bf16[128,2304]{1,0:T(8,128)(2,1)S(1)}, u32[]{:S(2)}, u32[]{:S(2)}) collective-permute-start(bf16[128,2304]{1,0:T(8,128)(2,1)S(1)} %concatenate.81), channel_id=1, source_target_pairs={{0,1},{1,2},{2,3},{3,0},{4,5},{5,6},{6,7},{7,4},{8,9},{9,10},{10,1... | collective-permute-start | bytes 1769480 | tf_op jit(solution)/shard_map/ppermute | solution.py:57
  725.5 42.0 %collective-permute-start.35 = (bf16[128,2304]{1,0:T(8,128)(2,1)S(1)}, bf16[128,2304]{1,0:T(8,128)(2,1)S(1)}, u32[]{:S(2)}, u32[]{:S(2)}) collective-permute-start(bf16[128,2304]{1,0:T(8,128)(2,1)S(1)} %concatenate.81), channel_id=1, source_target_pairs={{0,2},{1,3},{2,0},{3,1},{4,6},{5,7},{6,4},{7,5},{8,10},{9,11},{10,... | collective-permute-start | bytes 1769480 | tf_op jit(solution)/shard_map/ppermute | solution.py:57
  727.0 40.5 %collective-permute-start.36 = (bf16[128,2304]{1,0:T(8,128)(2,1)S(1)}, bf16[128,2304]{1,0:T(8,128)(2,1)S(1)}, u32[]{:S(2)}, u32[]{:S(2)}) collective-permute-start(bf16[128,2304]{1,0:T(8,128)(2,1)S(1)} %concatenate.81), channel_id=1, source_target_pairs={{0,3},{1,0},{2,1},{3,2},{4,7},{5,4},{6,5},{7,6},{8,11},{9,8},{10,9... | collective-permute-start | bytes 1769480 | tf_op jit(solution)/shard_map/ppermute | solution.py:57
  (84 other events, 1093.9 us)
Sparse Core Ops, SparseCore 0:
  10.5 51.4 all-gather.2
  63.8 209.6 all-gather.4
  316.2 94.6 all-reduce.3
  586.9 60.6 reduce-scatter.3
  650.5 62.6 reduce-scatter.7
  716.1 104.5 reduce-scatter.5

commit v13 on v12

--- a/solution.py
+++ b/solution.py
@@ -232,6 +232,13 @@
 def share_rows(grad):
     return lax.psum_scatter(
         grad, ROWS, scatter_dimension=0, tiled=True, axis_index_groups=row_groups()
+    )
+
+
+def share_all_rows(grad):
+    first, second = row_groups()
+    return lax.psum_scatter(
+        grad, ROWS, scatter_dimension=0, tiled=True, axis_index_groups=[first + second]
     )
 
 
@@ -334,18 +341,16 @@
     grad_gain_four = grad_gain_four / tp_size
     grad_two_low = grad_branch_two.astype(LOW)
 
-    down_sent, grad_two_low = lax.optimization_barrier(
-        (sent_to_core(grad_two_low, hidden_low), grad_two_low)
-    )
-    down_arrived = over_cores(down_sent)
+    grad_down_low, grad_two_low = lax.optimization_barrier(
+        (rows_product(grad_two_low, hidden_low).astype(LOW), grad_two_low)
+    )
+    down_share = share_all_rows(grad_down_low)
     _, pull_glu = jax.vjp(geglu, gate_value, up_value)
     grad_gate, grad_up = pull_glu(product(grad_two_low, down_full))
     grad_gate_up = jnp.concatenate([grad_gate.astype(LOW), grad_up.astype(LOW)], axis=1)
     grad_normed_two = transposed_product(grad_gate_up, gate_up_full).astype(LOW)
     grad_normed_two = sent_scattered(ordered_blocks(grad_normed_two))
     outputs = by_chip((middle_all + rms(branch_two, post_feedforward_gain)).astype(LOW))
-    grad_down_low = chip_rows(grad_two_low, hidden_low, down_arrived)
-    down_share = share_rows(grad_down_low)
     gate_up_sent = sent_to_core(normed_two, grad_gate_up)
     gate_up_arrived = over_cores(gate_up_sent)
     grad_gate_up_low = chip_rows(normed_two, grad_gate_up, gate_up_arrived)
@@ -399,9 +404,7 @@
     grad_gain_three = jax.vjp(rms, middle_kept, pre_feedforward_gain)[1](normed_kept)[1]
     grad_gain_two = jax.vjp(rms, branch_kept, post_attention_gain)[1](grad_kept)[1]
     gains = by_chip(jnp.stack([grad_gain_one, grad_gain_two, grad_gain_three, grad_gain_four]))
-    gains = sum((shift(gains, k) for k in range(1, tp_size)), gains)
-    for axis in ROWS:
-        gains = summed(gains, axis)
+    gains_arrived = [shift(gains, k) for k in range(1, tp_size)]
     grad_normed_one = sent_scattered(ordered_blocks(grad_normed_one))
     qkv_sent = sent_to_core(normed_one, grad_qkv)
     qkv_arrived = over_cores(qkv_sent)
@@ -413,11 +416,17 @@
     grad_inputs_low = by_chip((grad_middle + pull_one(grad_normed_one)[0]).astype(LOW))
     grad_inputs = in_order(sent_gathered(grad_inputs_low))
 
+    gains_arrived, _ = lax.optimization_barrier((gains_arrived, grad_inputs_low))
+    gains = sum(gains_arrived, gains)
+    for axis in ROWS:
+        gains = summed(gains, axis)
     share = hidden_in.shape[1] // (lax.axis_size("fsdp") * lax.axis_size("ctx"))
     row_rank = lax.axis_index("fsdp") * lax.axis_size("ctx") + lax.axis_index("ctx")
     gain_shares = lax.dynamic_slice_in_dim(gains, row_rank * share, share, axis=1)
     edges = [0, heads_width, heads_width + kv_width, qkv_width, qkv_width + heads_width]
-    attention_shares = [attention_share[:, a:b].astype(F32) for a, b in zip(edges[:-1], edges[1:])]
+    attention_shares = [
+        attention_share[:, a:b].astype(F32) for a, b in zip(edges[:-1], edges[1:])
+    ]
     gate_share = gate_up_share[:, :units].astype(F32)
     up_share = gate_up_share[:, units:].astype(F32)
     down_share = down_share.astype(F32)

time: 843 us -> 871 us (1.033)
  waiting for transfers between devices: 434 us -> 450 us
  starting transfers between devices: 88.2 us -> 102 us
    reduce_scatter x3 -> x2, waiting for transfers between devices: 45.6 us -> 64.2 us  [share_rows(): lax.psum_scatter(grad, ROWS, scatter_dimension=0, tiled=True, axis_index_...]
    ppermute x21, starting transfers between devices: 43.1 us -> 57.6 us  [shift(): lax.ppermute(block, 'tp', [(i, (i + distance) % size) for i in range(size)])]
    ppermute x21, waiting for transfers between devices: 167 us -> 158 us  [shift(): lax.ppermute(block, 'tp', [(i, (i + distance) % size) for i in range(size)])]
    ppermute x4 -> x3, waiting for transfers between devices: 12.6 us -> 19.7 us  [over_cores(): lax.ppermute(block, 'fsdp', [(i, i ^ 1) for i in range(lax.axis_size('fsd...]
    dot_general x8 -> x7, matrix products: 46.7 us -> 42.7 us  [rows_product(): lax.dot_general(left, right, (((0,), (0,)), ((), ())), preferred_element_...]
  transfers between devices with their start and end apart: 56 -> 55, of which waited for: 30 -> 28; matrix products, arithmetic and copies ran while one was open for 31% -> 30% of each run, Pallas kernels for 0% -> 0%
where the time goes in v13:
time: 871 us; the launch traced here: 860 us
  waiting for transfers between devices  450 us (52%)
  matrix products  134 us (15%)
  starting transfers between devices  102 us (12%)
  local copies, waits for them, and re-layouts  85.2 us (10%)
  other arithmetic  72.8 us (8%)
  between operations  15.7 us (2%)
    ppermute x21, waiting for transfers between devices, shift(): lax.ppermute(block, 'tp', [(i, (i + distance) % size) for i in range(size)])  158 us
    psum x1, waiting for transfers between devices, shards(): lax.psum(transposed_product(hidden_low, down_full).astype(LOW), 'tp')  82 us
    reduce_scatter x2, waiting for transfers between devices, share_rows(): lax.psum_scatter(grad, ROWS, scatter_dimension=0, tiled=True, axis_index_...  64.2 us
    ppermute x21, starting transfers between devices, shift(): lax.ppermute(block, 'tp', [(i, (i + distance) % size) for i in range(size)])  57.6 us
    dot_general x7, matrix products, rows_product(): lax.dot_general(left, right, (((0,), (0,)), ((), ())), preferred_element_...  42.7 us
    dot_general x4, matrix products, product(): return jnp.dot(left, right, preferred_element_type=F32)  40.3 us
    all_gather x2, waiting for transfers between devices, gather_rows(): lax.all_gather(weight, ROWS, axis=0, tiled=True, axis_index_groups=[first...  38.3 us
    dot_general x4, matrix products, transposed_product(): lax.dot_general(left, right, (((1,), (1,)), ((), ())), preferred_element_...  36.4 us
  transfers between devices with their start and end apart: 55, of which 28 were waited for; matrix products, arithmetic and copies ran while one was open for 30% of the time, Pallas kernels for 0%

profile of v13, /device:TPU:0, one launch (start us, length us, event | category | flops | bytes accessed | tf_op | source)
XLA Modules:
  0.0 860.0 jit_solution(18337760599340406059)
XLA Ops:
  16.5 4.2 concatenate.62
  23.7 38.3 %all-gather.3.cloned.1.call-done = bf16[2304,1536]{1,0:T(8,128)(2,1)} async-done(((bf16[288,1536]{1,0:T(8,128)(2,1)}), bf16[2304,1536]{1,0:T(8,128)(2,1)}) %all-gather.3.cloned.1.call-update) | async-done | bytes 7077904 | tf_op jit(solution)/shard_map/all_gather | solution.py:184
  61.9 5.7 fusion.53
  68.4 4.1 collective-permute-start
  75.2 11.4 %collective-permute-done = bf16[384,512]{1,0:T(8,128)(2,1)} collective-permute-done((bf16[384,512]{1,0:T(8,128)(2,1)}, bf16[384,512]{1,0:T(8,128)(2,1)}, u32[]{:S(2)}, u32[]{:S(2)}) %collective-permute-start) | collective-permute-done | bytes 393248 | tf_op jit(solution)/shard_map/ppermute | solution.py:21
  98.4 4.0 collective-permute-start.1
  102.4 9.8 %collective-permute-done.1 = bf16[128,2304]{1,0:T(8,128)(2,1)} collective-permute-done((bf16[128,2304]{1,0:T(8,128)(2,1)S(1)}, bf16[128,2304]{1,0:T(8,128)(2,1)}, u32[]{:S(2)}, u32[]{:S(2)}) %collective-permute-start.1) | collective-permute-done | bytes 589856 | tf_op jit(solution)/shard_map/ppermute | solution.py:45
  113.9 4.5 collective-permute-start.3
  119.1 9.1 %collective-permute-done.3 = bf16[128,2304]{1,0:T(8,128)(2,1)S(1)} collective-permute-done((bf16[128,2304]{1,0:T(8,128)(2,1)S(1)}, bf16[128,2304]{1,0:T(8,128)(2,1)S(1)}, u32[]{:S(2)}, u32[]{:S(2)}) %collective-permute-start.3) | collective-permute-done | bytes 589856 | tf_op jit(solution)/shard_map/ppermute | solution.py:45
  131.4 6.0 collective-permute-start.5
  137.4 7.9 collective-permute-done.6
  151.6 4.3 collective-permute-start.7
  165.0 16.2 %collective-permute-done.16 = bf16[288,512]{1,0:T(8,128)(2,1)S(1)} collective-permute-done((bf16[288,512]{1,0:T(8,128)(2,1)S(1)}, bf16[288,512]{1,0:T(8,128)(2,1)S(1)}, u32[]{:S(2)}, u32[]{:S(2)}) %collective-permute-start.16) | collective-permute-done | bytes 294944 | tf_op jit(solution)/shard_map/ppermute | solution.py:57
  182.1 9.2 %collective-permute-done.17 = bf16[288,512]{1,0:T(8,128)(2,1)S(1)} collective-permute-done((bf16[288,512]{1,0:T(8,128)(2,1)S(1)}, bf16[288,512]{1,0:T(8,128)(2,1)S(1)}, u32[]{:S(2)}, u32[]{:S(2)}) %collective-permute-start.17) | collective-permute-done | bytes 294944 | tf_op jit(solution)/shard_map/ppermute | solution.py:57
  202.4 6.2 collective-permute-done.10
  212.0 5.2 concatenate.77
  217.9 5.4 concatenate.72
  225.4 4.7 broadcast_in_dim.149
  232.7 16.1 %collective-permute-done.19 = bf16[288,2048]{1,0:T(8,128)(2,1)} collective-permute-done((bf16[288,2048]{1,0:T(8,128)(2,1)}, bf16[288,2048]{1,0:T(8,128)(2,1)}, u32[]{:S(2)}, u32[]{:S(2)}) %collective-permute-start.19) | collective-permute-done | bytes 1179680 | tf_op jit(solution)/shard_map/ppermute | solution.py:196
  248.8 19.2 %collective-permute-done.20 = bf16[288,2048]{1,0:T(8,128)(2,1)} collective-permute-done((bf16[288,2048]{1,0:T(8,128)(2,1)}, bf16[288,2048]{1,0:T(8,128)(2,1)}, u32[]{:S(2)}, u32[]{:S(2)}) %collective-permute-start.20) | collective-permute-done | bytes 1179680 | tf_op jit(solution)/shard_map/ppermute | solution.py:196
  279.0 5.9 multiply_convert_fusion.2
  284.9 15.2 %fusion.2 = f32[512,4608]{1,0:T(8,128)S(1)} fusion(bf16[512,2304]{1,0:T(8,128)(2,1)} %get-tuple-element.100, bf16[2304,6912]{1,0:T(8,128)(2,1)} %all-gather.5.cloned.1.call-done), kind=kOutput, calls=%fused_computation.4 | convolution fusion | flops 10871635968 | bytes 33030144 | tf_op jit(solution)/shard_map/dot_general | solution.py:33
  305.2 11.0 %fusion.29 = bf16[512,2304]{1,0:T(8,128)(2,1)} fusion(bf16[512,2304]{1,0:T(8,128)(2,1)S(1)} %multiply_convert_fusion.1, bf16[2304,6912]{1,0:T(8,128)(2,1)} %all-gather.5.cloned.1.call-done), kind=kOutput, calls=%fused_computation.52 | convolution fusion | flops 5436997632 | bytes 15335424 | tf_op jit(solution)/shard_map/dot_general | solution.py:41
  329.0 82.0 %all-reduce.4.cloned.1.call-done = bf16[512,2304]{1,0:T(8,128)(2,1)} async-done(((bf16[512,2304]{1,0:T(8,128)(2,1)}), bf16[512,2304]{1,0:T(8,128)(2,1)}) %all-reduce.4.cloned.1.call-update) | async-done | bytes 2359312 | tf_op jit(solution)/shard_map/psum | solution.py:336
  416.8 5.1 fusion.25
  423.3 8.3 convolution_convert_fusion.1
  431.6 14.4 %fusion.23 = (bf16[512,2304]{1,0:T(8,128)(2,1)S(1)}, bf16[512,2304]{1,0:T(8,128)(2,1)S(1)}) fusion(f32[512,4608]{1,0:T(8,128)} %copy-done.11, bf16[512,2304]{1,0:T(8,128)(2,1)} %copy-done.26, bf16[2304,6912]{1,0:T(8,128)(2,1)} %all-gather.5.cloned.1.call-done), kind=kOutput, calls=%fused_computation.38 | convolution fusion | flops 5464129536 | bytes 27131904 | tf_op jit(solution)/shard_map/dot_general | solution.py:33
  446.0 16.3 %fusion.32 = bf16[512,2304]{1,0:T(8,128)(2,1)S(1)} fusion(bf16[2304,6912]{1,0:T(8,128)(2,1)} %all-gather.5.cloned.1.call-done, bf16[512,2304]{1,0:T(8,128)(2,1)S(1)} %get-tuple-element.108, bf16[512,2304]{1,0:T(8,128)(2,1)S(1)} %get-tuple-element.107), kind=kOutput, calls=%fused_computation.53 | convolution fusion | flops 10882252800 | bytes 28311552 | tf_op jit(solution)/shard_map/dot_general | solution.py:41
  471.4 9.2 %collective-permute-done.15 = bf16[128,2304]{1,0:T(8,128)(2,1)S(1)} collective-permute-done((bf16[128,2304]{1,0:T(8,128)(2,1)S(1)}, bf16[128,2304]{1,0:T(8,128)(2,1)S(1)}, u32[]{:S(2)}, u32[]{:S(2)}) %collective-permute-start.15) | collective-permute-done | bytes 589856 | tf_op jit(solution)/shard_map/ppermute | solution.py:57
  480.6 9.8 %collective-permute-done.14 = bf16[128,2304]{1,0:T(8,128)(2,1)S(1)} collective-permute-done((bf16[128,2304]{1,0:T(8,128)(2,1)S(1)}, bf16[128,2304]{1,0:T(8,128)(2,1)S(1)}, u32[]{:S(2)}, u32[]{:S(2)}) %collective-permute-start.14) | collective-permute-done | bytes 589856 | tf_op jit(solution)/shard_map/ppermute | solution.py:57
  490.3 26.4 %collective-permute-done.13 = bf16[128,2304]{1,0:T(8,128)(2,1)S(1)} collective-permute-done((bf16[128,2304]{1,0:T(8,128)(2,1)S(1)}, bf16[128,2304]{1,0:T(8,128)(2,1)S(1)}, u32[]{:S(2)}, u32[]{:S(2)}) %collective-permute-start.13) | collective-permute-done | bytes 589856 | tf_op jit(solution)/shard_map/ppermute | solution.py:57
  521.3 5.1 convolution_convert_fusion.6
  528.6 8.0 collective-permute-done.26
  557.9 4.1 collective-permute-done.29
  566.3 11.3 %collective-permute-done.45 = bf16[128,2304]{1,0:T(8,128)(2,1)} collective-permute-done((bf16[128,2304]{1,0:T(8,128)(2,1)S(1)}, bf16[128,2304]{1,0:T(8,128)(2,1)}, u32[]{:S(2)}, u32[]{:S(2)}) %collective-permute-start.45) | collective-permute-done | bytes 589856 | tf_op jit(solution)/shard_map/ppermute | solution.py:57
  594.8 10.3 %convolution_convert_fusion = bf16[1152,4608]{1,0:T(8,128)(2,1)} fusion(bf16[512,2304]{1,0:T(8,128)(2,1)} %copy-done.67, bf16[512,2304]{1,0:T(8,128)(2,1)} %copy-done.66, bf16[512,2304]{1,0:T(8,128)(2,1)S(1)} %copy-done.23, s32[]{:T(128)S(6)} %select_n.267), kind=kOutput, calls=%fused_computation.1 | convolution fusion | flops 5450563584 | bytes 16515076 | tf_op jit(solution)/shard_map/dot_general | solution.py:37
  605.3 16.5 %collective-permute-done.48 = bf16[1152,4608]{1,0:T(8,128)(2,1)} collective-permute-done((bf16[1152,4608]{1,0:T(8,128)(2,1)}, bf16[1152,4608]{1,0:T(8,128)(2,1)}, u32[]{:S(2)}, u32[]{:S(2)}) %collective-permute-start.48) | collective-permute-done | bytes 10616864 | tf_op jit(solution)/shard_map/ppermute | solution.py:224
  621.8 13.6 %add_convert_fusion = bf16[1152,4608]{1,0:T(8,128)(2,1)} fusion(bf16[1152,4608]{1,0:T(8,128)(2,1)} %collective-permute-done.48, bf16[512,2304]{1,0:T(8,128)(2,1)} %copy-done.67, bf16[512,2304]{1,0:T(8,128)(2,1)} %copy-done.66, bf16[512,2304]{1,0:T(8,128)(2,1)S(1)} %copy-done.23, s32[]{:T(128)S(6)} %select_n.266), kind=kOutput, calls=%fused_computation | convolution fusion | flops 5461180416 | bytes 27131908 | tf_op jit(solution)/shard_map/dot_general | solution.py:37
  638.3 5.9 fusion.15
  645.7 13.5 %collective-permute-start.33 = (bf16[128,2304]{1,0:T(8,128)(2,1)}, bf16[128,2304]{1,0:T(8,128)(2,1)}, u32[]{:S(2)}, u32[]{:S(2)}) collective-permute-start(bf16[128,2304]{1,0:T(8,128)(2,1)} %get-tuple-element.74), channel_id=1, source_target_pairs={{0,1},{1,2},{2,3},{3,0},{4,5},{5,6},{6,7},{7,4},{8,9},{9,10},{10,1... | collective-permute-start | bytes 1769480 | tf_op jit(solution)/shard_map/ppermute | solution.py:57
  665.4 10.9 %collective-permute-done.33 = bf16[128,2304]{1,0:T(8,128)(2,1)} collective-permute-done((bf16[128,2304]{1,0:T(8,128)(2,1)}, bf16[128,2304]{1,0:T(8,128)(2,1)}, u32[]{:S(2)}, u32[]{:S(2)}) %collective-permute-start.33) | collective-permute-done | bytes 589856 | tf_op jit(solution)/shard_map/ppermute | solution.py:57
  676.4 15.4 %collective-permute-start.39 = (f32[4,2304]{1,0:T(4,128)S(1)}, f32[4,2304]{1,0:T(4,128)}, u32[]{:S(2)}, u32[]{:S(2)}) collective-permute-start(f32[4,2304]{1,0:T(4,128)S(1)} %concatenate.82), channel_id=1, source_target_pairs={{0,3},{1,0},{2,1},{3,2},{4,7},{5,4},{6,5},{7,6},{8,11},{9,8},{10,9... | collective-permute-start | bytes 110600 | tf_op jit(solution)/shard_map/ppermute | solution.py:57
  691.8 23.5 %collective-permute-done.31 = bf16[128,2304]{1,0:T(8,128)(2,1)} collective-permute-done((bf16[128,2304]{1,0:T(8,128)(2,1)}, bf16[128,2304]{1,0:T(8,128)(2,1)}, u32[]{:S(2)}, u32[]{:S(2)}) %collective-permute-start.31) | collective-permute-done | bytes 589856 | tf_op jit(solution)/shard_map/ppermute | solution.py:57
  728.9 5.1 concatenate.76
  743.3 9.0 %collective-permute-done.34 = bf16[128,2304]{1,0:T(8,128)(2,1)S(1)} collective-permute-done((bf16[128,2304]{1,0:T(8,128)(2,1)}, bf16[128,2304]{1,0:T(8,128)(2,1)S(1)}, u32[]{:S(2)}, u32[]{:S(2)}) %collective-permute-start.34) | collective-permute-done | bytes 589856 | tf_op jit(solution)/shard_map/ppermute | solution.py:57
  752.3 24.2 %collective-permute-done.35 = bf16[128,2304]{1,0:T(8,128)(2,1)S(1)} collective-permute-done((bf16[128,2304]{1,0:T(8,128)(2,1)}, bf16[128,2304]{1,0:T(8,128)(2,1)S(1)}, u32[]{:S(2)}, u32[]{:S(2)}) %collective-permute-start.35) | collective-permute-done | bytes 589856 | tf_op jit(solution)/shard_map/ppermute | solution.py:57
  784.1 64.1 %reduce-scatter.6.cloned.1.call-done = bf16[288,4608]{1,0:T(8,128)(2,1)} async-done(((bf16[1152,4608]{1,0:T(8,128)(2,1)}), bf16[288,4608]{1,0:T(8,128)(2,1)}) %reduce-scatter.6.cloned.1.call-update) | async-done | bytes 2654224 | tf_op jit(solution)/shard_map/reduce_scatter | solution.py:233
  848.3 4.5 slice_convert_fusion
  (343 shorter events, 204.2 us)
Async XLA Ops:
  7.2 54.7 %all-gather.3.cloned.1.call-start = ((), (), s32[]{:S(2)}) async-start(), calls=%async_computation.3 | async-start | bytes 7962624 | tf_op jit(solution)/shard_map/all_gather | solution.py:184
  9.5 275.4 %all-gather.5.cloned.1.call-start = ((), (), s32[]{:S(2)}) async-start(), calls=%async_computation.4 | async-start | bytes 35831808 | tf_op jit(solution)/shard_map/all_gather | solution.py:184
  13.0 398.0 %all-reduce.4.cloned.1.call-start = ((), (), s32[]{:S(2)}) async-start(), calls=%async_computation.5 | async-start | bytes 4718592 | tf_op jit(solution)/shard_map/psum | solution.py:336
  68.4 18.3 %collective-permute-start = (bf16[384,512]{1,0:T(8,128)(2,1)}, bf16[384,512]{1,0:T(8,128)(2,1)}, u32[]{:S(2)}, u32[]{:S(2)}) collective-permute-start(bf16[384,512]{1,0:T(8,128)(2,1)} %slice.274), channel_id=1, source_target_pairs={{0,4},{1,5},{2,6},{3,7},{8,12},{9,13},{10,14},{11,15},{16,20},{17,... | collective-permute-start | bytes 1179656 | tf_op jit(solution)/shard_map/ppermute | solution.py:21
  98.4 13.8 %collective-permute-start.1 = (bf16[128,2304]{1,0:T(8,128)(2,1)S(1)}, bf16[128,2304]{1,0:T(8,128)(2,1)}, u32[]{:S(2)}, u32[]{:S(2)}) collective-permute-start(bf16[128,2304]{1,0:T(8,128)(2,1)S(1)} %get-tuple-element.49), channel_id=1, source_target_pairs={{0,1},{4,5},{8,9},{12,13},{16,17},{20,21},{24,25},{28,29}} | collective-permute-start | bytes 1769480 | tf_op jit(solution)/shard_map/ppermute | solution.py:45
  113.9 14.3 %collective-permute-start.3 = (bf16[128,2304]{1,0:T(8,128)(2,1)S(1)}, bf16[128,2304]{1,0:T(8,128)(2,1)S(1)}, u32[]{:S(2)}, u32[]{:S(2)}) collective-permute-start(bf16[128,2304]{1,0:T(8,128)(2,1)S(1)} %get-tuple-element.51), channel_id=1, source_target_pairs={{0,1},{1,2},{4,5},{5,6},{8,9},{9,10},{12,13},{13,14},{16,17},{17,1... | collective-permute-start | bytes 1769480 | tf_op jit(solution)/shard_map/ppermute | solution.py:45
  118.4 10.7 %collective-permute-start.4 = (bf16[128,2304]{1,0:T(8,128)(2,1)S(1)}, bf16[128,2304]{1,0:T(8,128)(2,1)S(1)}, u32[]{:S(2)}, u32[]{:S(2)}) collective-permute-start(bf16[128,2304]{1,0:T(8,128)(2,1)S(1)} %get-tuple-element.52), channel_id=1, source_target_pairs={{2,1},{3,2},{6,5},{7,6},{10,9},{11,10},{14,13},{15,14},{18,17},{19... | collective-permute-start | bytes 1769480 | tf_op jit(solution)/shard_map/ppermute | solution.py:45
  130.1 15.3 %collective-permute-start.6 = (bf16[128,2304]{1,0:T(8,128)(2,1)}, bf16[128,2304]{1,0:T(8,128)(2,1)S(1)}, u32[]{:S(2)}, u32[]{:S(2)}) collective-permute-start(bf16[128,2304]{1,0:T(8,128)(2,1)} %add_convert_fusion.2), channel_id=1, source_target_pairs={{1,0},{2,1},{3,2},{5,4},{6,5},{7,6},{9,8},{10,9},{11,10},{13,12},{... | collective-permute-start | bytes 1769480 | tf_op jit(solution)/shard_map/ppermute | solution.py:45
  131.4 15.3 %collective-permute-start.5 = (bf16[128,2304]{1,0:T(8,128)(2,1)}, bf16[128,2304]{1,0:T(8,128)(2,1)S(1)}, u32[]{:S(2)}, u32[]{:S(2)}) collective-permute-start(bf16[128,2304]{1,0:T(8,128)(2,1)} %add_convert_fusion.3), channel_id=1, source_target_pairs={{0,1},{1,2},{2,3},{4,5},{5,6},{6,7},{8,9},{9,10},{10,11},{12,13},{... | collective-permute-start | bytes 1769480 | tf_op jit(solution)/shard_map/ppermute | solution.py:45
  151.6 40.4 %collective-permute-start.7 = (bf16[128,2304]{1,0:T(8,128)(2,1)S(1)}, bf16[128,2304]{1,0:T(8,128)(2,1)S(1)}, u32[]{:S(2)}, u32[]{:S(2)}) collective-permute-start(bf16[128,2304]{1,0:T(8,128)(2,1)S(1)} %get-tuple-element.103), channel_id=1, source_target_pairs={{0,1},{1,2},{2,3},{4,5},{5,6},{6,7},{8,9},{9,10},{10,11},{12,13},{... | collective-permute-start | bytes 1769480 | tf_op jit(solution)/shard_map/ppermute | solution.py:45
  155.9 36.1 %collective-permute-start.8 = (bf16[128,2304]{1,0:T(8,128)(2,1)S(1)}, bf16[128,2304]{1,0:T(8,128)(2,1)S(1)}, u32[]{:S(2)}, u32[]{:S(2)}) collective-permute-start(bf16[128,2304]{1,0:T(8,128)(2,1)S(1)} %get-tuple-element.103), channel_id=1, source_target_pairs={{1,0},{2,1},{3,2},{5,4},{6,5},{7,6},{9,8},{10,9},{11,10},{13,12},{... | collective-permute-start | bytes 1769480 | tf_op jit(solution)/shard_map/ppermute | solution.py:45
  157.3 24.0 %collective-permute-start.16 = (bf16[288,512]{1,0:T(8,128)(2,1)S(1)}, bf16[288,512]{1,0:T(8,128)(2,1)S(1)}, u32[]{:S(2)}, u32[]{:S(2)}) collective-permute-start(bf16[288,512]{1,0:T(8,128)(2,1)S(1)} %copy-done.32), channel_id=1, source_target_pairs={{0,1},{1,2},{2,3},{3,0},{4,5},{5,6},{6,7},{7,4},{8,9},{9,10},{10,1... | collective-permute-start | bytes 884744 | tf_op jit(solution)/shard_map/ppermute | solution.py:57
  160.1 31.2 %collective-permute-start.17 = (bf16[288,512]{1,0:T(8,128)(2,1)S(1)}, bf16[288,512]{1,0:T(8,128)(2,1)S(1)}, u32[]{:S(2)}, u32[]{:S(2)}) collective-permute-start(bf16[288,512]{1,0:T(8,128)(2,1)S(1)} %copy-done.32), channel_id=1, source_target_pairs={{0,2},{1,3},{2,0},{3,1},{4,6},{5,7},{6,4},{7,5},{8,10},{9,11},{10,... | collective-permute-start | bytes 884744 | tf_op jit(solution)/shard_map/ppermute | solution.py:57
  161.6 33.3 %collective-permute-start.18 = (bf16[288,512]{1,0:T(8,128)(2,1)S(1)}, bf16[288,512]{1,0:T(8,128)(2,1)S(1)}, u32[]{:S(2)}, u32[]{:S(2)}) collective-permute-start(bf16[288,512]{1,0:T(8,128)(2,1)S(1)} %copy-done.32), channel_id=1, source_target_pairs={{0,3},{1,0},{2,1},{3,2},{4,7},{5,4},{6,5},{7,6},{8,11},{9,8},{10,9... | collective-permute-start | bytes 884744 | tf_op jit(solution)/shard_map/ppermute | solution.py:57
  192.1 10.3 %collective-permute-start.9 = (bf16[128,2304]{1,0:T(8,128)(2,1)S(1)}, bf16[128,2304]{1,0:T(8,128)(2,1)}, u32[]{:S(2)}, u32[]{:S(2)}) collective-permute-start(bf16[128,2304]{1,0:T(8,128)(2,1)S(1)} %collective-permute-done.7), channel_id=1, source_target_pairs={{1,2},{2,3},{5,6},{6,7},{9,10},{10,11},{13,14},{14,15},{17,18},{18... | collective-permute-start | bytes 1769480 | tf_op jit(solution)/shard_map/ppermute | solution.py:45
  193.6 15.0 %collective-permute-start.10 = (bf16[128,2304]{1,0:T(8,128)(2,1)S(1)}, bf16[128,2304]{1,0:T(8,128)(2,1)}, u32[]{:S(2)}, u32[]{:S(2)}) collective-permute-start(bf16[128,2304]{1,0:T(8,128)(2,1)S(1)} %collective-permute-done.8), channel_id=1, source_target_pairs={{1,0},{2,1},{5,4},{6,5},{9,8},{10,9},{13,12},{14,13},{17,16},{18,1... | collective-permute-start | bytes 1769480 | tf_op jit(solution)/shard_map/ppermute | solution.py:45
  195.7 53.1 %collective-permute-start.19 = (bf16[288,2048]{1,0:T(8,128)(2,1)}, bf16[288,2048]{1,0:T(8,128)(2,1)}, u32[]{:S(2)}, u32[]{:S(2)}) collective-permute-start(bf16[288,2048]{1,0:T(8,128)(2,1)} %constant_dynamic-update-slice_fusion), channel_id=1, source_target_pairs={{0,20},{4,16},{8,28},{12,24},{16,4},{20,0},{24,12},{28,8},{1,21},{... | collective-permute-start | bytes 3538952 | tf_op jit(solution)/shard_map/ppermute | solution.py:196
  197.2 70.8 %collective-permute-start.20 = (bf16[288,2048]{1,0:T(8,128)(2,1)}, bf16[288,2048]{1,0:T(8,128)(2,1)}, u32[]{:S(2)}, u32[]{:S(2)}) collective-permute-start(bf16[288,2048]{1,0:T(8,128)(2,1)} %constant_dynamic-update-slice_fusion), channel_id=1, source_target_pairs={{0,4},{4,0},{8,12},{12,8},{16,20},{20,16},{24,28},{28,24},{1,5},{5... | collective-permute-start | bytes 3538952 | tf_op jit(solution)/shard_map/ppermute | solution.py:196
  198.2 69.8 %collective-permute-start.21 = (bf16[288,2048]{1,0:T(8,128)(2,1)}, bf16[288,2048]{1,0:T(8,128)(2,1)}, u32[]{:S(2)}, u32[]{:S(2)}) collective-permute-start(bf16[288,2048]{1,0:T(8,128)(2,1)} %constant_dynamic-update-slice_fusion), channel_id=1, source_target_pairs={{0,16},{4,20},{8,24},{12,28},{16,0},{20,4},{24,8},{28,12},{1,17},{... | collective-permute-start | bytes 3538952 | tf_op jit(solution)/shard_map/ppermute | solution.py:196
  208.6 59.9 %collective-permute-start.11 = (bf16[128,2304]{1,0:T(8,128)(2,1)}, bf16[128,2304]{1,0:T(8,128)(2,1)}, u32[]{:S(2)}, u32[]{:S(2)}) collective-permute-start(bf16[128,2304]{1,0:T(8,128)(2,1)} %collective-permute-done.9), channel_id=1, source_target_pairs={{2,3},{6,7},{10,11},{14,15},{18,19},{22,23},{26,27},{30,31}} | collective-permute-start | bytes 1769480 | tf_op jit(solution)/shard_map/ppermute | solution.py:45
  210.0 58.5 %collective-permute-start.12 = (bf16[128,2304]{1,0:T(8,128)(2,1)}, bf16[128,2304]{1,0:T(8,128)(2,1)}, u32[]{:S(2)}, u32[]{:S(2)}) collective-permute-start(bf16[128,2304]{1,0:T(8,128)(2,1)} %collective-permute-done.10), channel_id=1, source_target_pairs={{1,0},{5,4},{9,8},{13,12},{17,16},{21,20},{25,24},{29,28}} | collective-permute-start | bytes 1769480 | tf_op jit(solution)/shard_map/ppermute | solution.py:45
  248.8 75.2 %collective-permute-start.22 = (bf16[288,2048]{1,0:T(8,128)(2,1)}, bf16[288,2048]{1,0:T(8,128)(2,1)}, u32[]{:S(2)}, u32[]{:S(2)}) collective-permute-start(bf16[288,2048]{1,0:T(8,128)(2,1)} %constant_dynamic-update-slice_fusion), channel_id=1, source_target_pairs={{0,8},{4,12},{8,0},{12,4},{16,24},{20,28},{24,16},{28,20},{1,9},{5... | collective-permute-start | bytes 3538952 | tf_op jit(solution)/shard_map/ppermute | solution.py:196
  268.0 58.5 %collective-permute-start.23 = (bf16[288,2048]{1,0:T(8,128)(2,1)}, bf16[288,2048]{1,0:T(8,128)(2,1)}, u32[]{:S(2)}, u32[]{:S(2)}) collective-permute-start(bf16[288,2048]{1,0:T(8,128)(2,1)} %collective-permute-done.20), channel_id=1, source_target_pairs={{0,8},{4,12},{8,0},{12,4},{16,24},{20,28},{24,16},{28,20},{1,9},{5... | collective-permute-start | bytes 3538952 | tf_op jit(solution)/shard_map/ppermute | solution.py:196
  268.0 198.5 %collective-permute-start.24 = (bf16[288,2048]{1,0:T(8,128)(2,1)}, bf16[288,2048]{1,0:T(8,128)(2,1)}, u32[]{:S(2)}, u32[]{:S(2)}) collective-permute-start(bf16[288,2048]{1,0:T(8,128)(2,1)} %collective-permute-done.21), channel_id=1, source_target_pairs={{0,8},{4,12},{8,0},{12,4},{16,24},{20,28},{24,16},{28,20},{1,9},{5... | collective-permute-start | bytes 3538952 | tf_op jit(solution)/shard_map/ppermute | solution.py:196
  268.5 200.5 %collective-permute-start.25 = (bf16[288,2048]{1,0:T(8,128)(2,1)}, bf16[288,2048]{1,0:T(8,128)(2,1)}, u32[]{:S(2)}, u32[]{:S(2)}) collective-permute-start(bf16[288,2048]{1,0:T(8,128)(2,1)} %collective-permute-done.19), channel_id=1, source_target_pairs={{0,8},{4,12},{8,0},{12,4},{16,24},{20,28},{24,16},{28,20},{1,9},{5... | collective-permute-start | bytes 3538952 | tf_op jit(solution)/shard_map/ppermute | solution.py:196
  316.2 460.5 %reduce-scatter.4.cloned.1.call-start = ((), (), s32[]{:S(2)}) async-start(), calls=%async_computation.6 | async-start | bytes 4423680 | tf_op jit(solution)/shard_map/reduce_scatter | solution.py:233
  462.5 18.1 %collective-permute-start.15 = (bf16[128,2304]{1,0:T(8,128)(2,1)S(1)}, bf16[128,2304]{1,0:T(8,128)(2,1)S(1)}, u32[]{:S(2)}, u32[]{:S(2)}) collective-permute-start(bf16[128,2304]{1,0:T(8,128)(2,1)S(1)} %get-tuple-element.65), channel_id=1, source_target_pairs={{0,1},{1,2},{2,3},{3,0},{4,5},{5,6},{6,7},{7,4},{8,9},{9,10},{10,1... | collective-permute-start | bytes 1769480 | tf_op jit(solution)/shard_map/ppermute | solution.py:57
  462.8 27.6 %collective-permute-start.14 = (bf16[128,2304]{1,0:T(8,128)(2,1)S(1)}, bf16[128,2304]{1,0:T(8,128)(2,1)S(1)}, u32[]{:S(2)}, u32[]{:S(2)}) collective-permute-start(bf16[128,2304]{1,0:T(8,128)(2,1)S(1)} %get-tuple-element.64), channel_id=1, source_target_pairs={{0,3},{1,0},{2,1},{3,2},{4,7},{5,4},{6,5},{7,6},{8,11},{9,8},{10,9... | collective-permute-start | bytes 1769480 | tf_op jit(solution)/shard_map/ppermute | solution.py:57
  466.5 50.2 %collective-permute-start.13 = (bf16[128,2304]{1,0:T(8,128)(2,1)S(1)}, bf16[128,2304]{1,0:T(8,128)(2,1)S(1)}, u32[]{:S(2)}, u32[]{:S(2)}) collective-permute-start(bf16[128,2304]{1,0:T(8,128)(2,1)S(1)} %get-tuple-element.63), channel_id=1, source_target_pairs={{0,2},{1,3},{2,0},{3,1},{4,6},{5,7},{6,4},{7,5},{8,10},{9,11},{10,... | collective-permute-start | bytes 1769480 | tf_op jit(solution)/shard_map/ppermute | solution.py:57
  526.4 10.2 %collective-permute-start.26 = (bf16[128,512]{1,0:T(8,128)(2,1)S(1)}, bf16[128,512]{1,0:T(8,128)(2,1)S(1)}, u32[]{:S(2)}, u32[]{:S(2)}) collective-permute-start(bf16[128,512]{1,0:T(8,128)(2,1)S(1)} %get-tuple-element.67), channel_id=1, source_target_pairs={{0,2},{1,3},{2,0},{3,1},{4,6},{5,7},{6,4},{7,5},{8,10},{9,11},{10,... | collective-permute-start | bytes 393224 | tf_op jit(solution)/shard_map/ppermute | solution.py:57
  526.5 10.6 %collective-permute-start.27 = (bf16[128,512]{1,0:T(8,128)(2,1)S(1)}, bf16[128,512]{1,0:T(8,128)(2,1)S(1)}, u32[]{:S(2)}, u32[]{:S(2)}) collective-permute-start(bf16[128,512]{1,0:T(8,128)(2,1)S(1)} %get-tuple-element.68), channel_id=1, source_target_pairs={{0,3},{1,0},{2,1},{3,2},{4,7},{5,4},{6,5},{7,6},{8,11},{9,8},{10,9... | collective-permute-start | bytes 393224 | tf_op jit(solution)/shard_map/ppermute | solution.py:57
  537.2 28.0 %collective-permute-start.44 = (bf16[128,2304]{1,0:T(8,128)(2,1)S(1)}, bf16[128,2304]{1,0:T(8,128)(2,1)}, u32[]{:S(2)}, u32[]{:S(2)}) collective-permute-start(bf16[128,2304]{1,0:T(8,128)(2,1)S(1)} %fusion.69), channel_id=1, source_target_pairs={{0,1},{1,2},{2,3},{3,0},{4,5},{5,6},{6,7},{7,4},{8,9},{9,10},{10,1... | collective-permute-start | bytes 1769480 | tf_op jit(solution)/shard_map/ppermute | solution.py:57
  539.6 38.0 %collective-permute-start.45 = (bf16[128,2304]{1,0:T(8,128)(2,1)S(1)}, bf16[128,2304]{1,0:T(8,128)(2,1)}, u32[]{:S(2)}, u32[]{:S(2)}) collective-permute-start(bf16[128,2304]{1,0:T(8,128)(2,1)S(1)} %fusion.69), channel_id=1, source_target_pairs={{0,2},{1,3},{2,0},{3,1},{4,6},{5,7},{6,4},{7,5},{8,10},{9,11},{10,... | collective-permute-start | bytes 1769480 | tf_op jit(solution)/shard_map/ppermute | solution.py:57
  540.5 38.2 %collective-permute-start.46 = (bf16[128,2304]{1,0:T(8,128)(2,1)S(1)}, bf16[128,2304]{1,0:T(8,128)(2,1)S(1)}, u32[]{:S(2)}, u32[]{:S(2)}) collective-permute-start(bf16[128,2304]{1,0:T(8,128)(2,1)S(1)} %fusion.69), channel_id=1, source_target_pairs={{0,3},{1,0},{2,1},{3,2},{4,7},{5,4},{6,5},{7,6},{8,11},{9,8},{10,9... | collective-permute-start | bytes 1769480 | tf_op jit(solution)/shard_map/ppermute | solution.py:57
  565.0 22.8 %collective-permute-start.43 = (bf16[1152,1024]{1,0:T(8,128)(2,1)}, bf16[1152,1024]{1,0:T(8,128)(2,1)}, u32[]{:S(2)}, u32[]{:S(2)}) collective-permute-start(bf16[1152,1024]{1,0:T(8,128)(2,1)} %convolution_convert_fusion.4), channel_id=1, source_target_pairs={{0,8},{8,0},{16,24},{24,16},{1,9},{9,1},{17,25},{25,17},{2,10},{10... | collective-permute-start | bytes 7077896 | tf_op jit(solution)/shard_map/ppermute | solution.py:224
  593.2 188.0 %reduce-scatter.8.cloned.1.call-start = ((), (), s32[]{:S(2)}) async-start(), calls=%async_computation.8 | async-start | bytes 11943936 | tf_op jit(solution)/shard_map/reduce_scatter | solution.py:240
  593.8 254.5 %reduce-scatter.6.cloned.1.call-start = ((), (), s32[]{:S(2)}) async-start(), calls=%async_computation.7 | async-start | bytes 13271040 | tf_op jit(solution)/shard_map/reduce_scatter | solution.py:233
  605.2 16.7 %collective-permute-start.48 = (bf16[1152,4608]{1,0:T(8,128)(2,1)}, bf16[1152,4608]{1,0:T(8,128)(2,1)}, u32[]{:S(2)}, u32[]{:S(2)}) collective-permute-start(bf16[1152,4608]{1,0:T(8,128)(2,1)} %convolution_convert_fusion), channel_id=1, source_target_pairs={{0,8},{8,0},{16,24},{24,16},{1,9},{9,1},{17,25},{25,17},{2,10},{10... | collective-permute-start | bytes 31850504 | tf_op jit(solution)/shard_map/ppermute | solution.py:224
  645.7 30.7 %collective-permute-start.33 = (bf16[128,2304]{1,0:T(8,128)(2,1)}, bf16[128,2304]{1,0:T(8,128)(2,1)}, u32[]{:S(2)}, u32[]{:S(2)}) collective-permute-start(bf16[128,2304]{1,0:T(8,128)(2,1)} %get-tuple-element.74), channel_id=1, source_target_pairs={{0,1},{1,2},{2,3},{3,0},{4,5},{5,6},{6,7},{7,4},{8,9},{9,10},{10,1... | collective-permute-start | bytes 1769480 | tf_op jit(solution)/shard_map/ppermute | solution.py:57
  659.2 32.6 %collective-permute-start.32 = (bf16[128,2304]{1,0:T(8,128)(2,1)}, bf16[128,2304]{1,0:T(8,128)(2,1)}, u32[]{:S(2)}, u32[]{:S(2)}) collective-permute-start(bf16[128,2304]{1,0:T(8,128)(2,1)} %get-tuple-element.73), channel_id=1, source_target_pairs={{0,3},{1,0},{2,1},{3,2},{4,7},{5,4},{6,5},{7,6},{8,11},{9,8},{10,9... | collective-permute-start | bytes 1769480 | tf_op jit(solution)/shard_map/ppermute | solution.py:57
  661.8 53.5 %collective-permute-start.31 = (bf16[128,2304]{1,0:T(8,128)(2,1)}, bf16[128,2304]{1,0:T(8,128)(2,1)}, u32[]{:S(2)}, u32[]{:S(2)}) collective-permute-start(bf16[128,2304]{1,0:T(8,128)(2,1)} %get-tuple-element.72), channel_id=1, source_target_pairs={{0,2},{1,3},{2,0},{3,1},{4,6},{5,7},{6,4},{7,5},{8,10},{9,11},{10,... | collective-permute-start | bytes 1769480 | tf_op jit(solution)/shard_map/ppermute | solution.py:57
  662.9 59.8 %collective-permute-start.37 = (f32[4,2304]{1,0:T(4,128)S(1)}, f32[4,2304]{1,0:T(4,128)S(1)}, u32[]{:S(2)}, u32[]{:S(2)}) collective-permute-start(f32[4,2304]{1,0:T(4,128)S(1)} %concatenate.82), channel_id=1, source_target_pairs={{0,1},{1,2},{2,3},{3,0},{4,5},{5,6},{6,7},{7,4},{8,9},{9,10},{10,1... | collective-permute-start | bytes 110600 | tf_op jit(solution)/shard_map/ppermute | solution.py:57
  665.0 57.8 %collective-permute-start.38 = (f32[4,2304]{1,0:T(4,128)S(1)}, f32[4,2304]{1,0:T(4,128)}, u32[]{:S(2)}, u32[]{:S(2)}) collective-permute-start(f32[4,2304]{1,0:T(4,128)S(1)} %concatenate.82), channel_id=1, source_target_pairs={{0,2},{1,3},{2,0},{3,1},{4,6},{5,7},{6,4},{7,5},{8,10},{9,11},{10,... | collective-permute-start | bytes 110600 | tf_op jit(solution)/shard_map/ppermute | solution.py:57
  676.4 46.4 %collective-permute-start.39 = (f32[4,2304]{1,0:T(4,128)S(1)}, f32[4,2304]{1,0:T(4,128)}, u32[]{:S(2)}, u32[]{:S(2)}) collective-permute-start(f32[4,2304]{1,0:T(4,128)S(1)} %concatenate.82), channel_id=1, source_target_pairs={{0,3},{1,0},{2,1},{3,2},{4,7},{5,4},{6,5},{7,6},{8,11},{9,8},{10,9... | collective-permute-start | bytes 110600 | tf_op jit(solution)/shard_map/ppermute | solution.py:57
  725.5 12.3 %collective-permute-start.41 = (f32[4,2304]{1,0:T(4,128)}, f32[4,2304]{1,0:T(4,128)}, u32[]{:S(2)}, u32[]{:S(2)}) collective-permute-start(f32[4,2304]{1,0:T(4,128)} %add.436), channel_id=1, source_target_pairs={{0,16},{8,24},{16,0},{24,8},{1,17},{9,25},{17,1},{25,9},{2,18},{10... | collective-permute-start | bytes 110600 | tf_op jit(solution)/shard_map/ppermute | solution.py:144
  734.0 18.3 %collective-permute-start.34 = (bf16[128,2304]{1,0:T(8,128)(2,1)}, bf16[128,2304]{1,0:T(8,128)(2,1)S(1)}, u32[]{:S(2)}, u32[]{:S(2)}) collective-permute-start(bf16[128,2304]{1,0:T(8,128)(2,1)} %concatenate.81), channel_id=1, source_target_pairs={{0,1},{1,2},{2,3},{3,0},{4,5},{5,6},{6,7},{7,4},{8,9},{9,10},{10,1... | collective-permute-start | bytes 1769480 | tf_op jit(solution)/shard_map/ppermute | solution.py:57
  734.0 42.5 %collective-permute-start.35 = (bf16[128,2304]{1,0:T(8,128)(2,1)}, bf16[128,2304]{1,0:T(8,128)(2,1)S(1)}, u32[]{:S(2)}, u32[]{:S(2)}) collective-permute-start(bf16[128,2304]{1,0:T(8,128)(2,1)} %concatenate.81), channel_id=1, source_target_pairs={{0,2},{1,3},{2,0},{3,1},{4,6},{5,7},{6,4},{7,5},{8,10},{9,11},{10,... | collective-permute-start | bytes 1769480 | tf_op jit(solution)/shard_map/ppermute | solution.py:57
  734.8 41.7 %collective-permute-start.36 = (bf16[128,2304]{1,0:T(8,128)(2,1)}, bf16[128,2304]{1,0:T(8,128)(2,1)S(1)}, u32[]{:S(2)}, u32[]{:S(2)}) collective-permute-start(bf16[128,2304]{1,0:T(8,128)(2,1)} %concatenate.81), channel_id=1, source_target_pairs={{0,3},{1,0},{2,1},{3,2},{4,7},{5,4},{6,5},{7,6},{8,11},{9,8},{10,9... | collective-permute-start | bytes 1769480 | tf_op jit(solution)/shard_map/ppermute | solution.py:57
  (75 other events, 1026.5 us)
Sparse Core Ops, SparseCore 0:
  10.5 51.4 all-gather.2
  63.8 209.5 all-gather.4
  316.3 94.6 all-reduce.3
  593.3 60.6 reduce-scatter.3
  657.3 83.3 reduce-scatter.7
  743.7 104.5 reduce-scatter.5

commit v14 on v13

--- a/solution.py
+++ b/solution.py
@@ -70,9 +70,10 @@
     return total
 
 
-def sent_gathered(block):
-    size = lax.axis_size("tp")
-    pieces = {k: shift(block, k) for k in distances(size)}
+def sent_gathered(block, pieces=None):
+    size = lax.axis_size("tp")
+    pieces = dict(pieces or {})
+    pieces.update({k: shift(block, k) for k in distances(size) if k not in pieces})
     return [block] + [pieces[k] for k in range(1, size)]
 
 
@@ -361,6 +362,7 @@
     _, pull_two = jax.vjp(rms, branch_one, post_attention_gain)
     grad_branch_one = pull_two(grad_middle)[0]
     grad_one_own = grad_branch_one.astype(LOW)
+    early = {1: shift(grad_one_own, 1)}
     grad_attended = product(grad_one_own, output_all).astype(LOW)
     grad_attended, grad_one_own = lax.optimization_barrier(
         (exchanged(grad_attended), grad_one_own)
@@ -368,7 +370,7 @@
     grad_attended = grad_attended.reshape(length, kv_heads, repeats, HD)
     later = (middle, grad_normed_two, branch_one, grad_middle, grad_one_own)
     middle_kept, normed_kept, branch_kept, grad_kept, grad_one_own = lax.optimization_barrier(later)
-    grad_one_low = in_order(sent_gathered(grad_one_own))
+    grad_one_low = in_order(sent_gathered(grad_one_own, early))
     output_sent = sent_to_core(grad_one_low, attended_low)
     output_arrived = over_cores(output_sent)
     grad_output_low = chip_rows(grad_one_low, attended_low, output_arrived)

time: 871 us -> 869 us (level)
  transfers between devices with their start and end apart: 55 -> 55, of which waited for: 28 -> 27; matrix products, arithmetic and copies ran while one was open for 30% -> 31% of each run, Pallas kernels for 0% -> 0%
where the time goes in v14:
time: 869 us; the launch traced here: 858 us
  waiting for transfers between devices  448 us (52%)
  matrix products  134 us (15%)
  starting transfers between devices  102 us (12%)
  local copies, waits for them, and re-layouts  85.1 us (10%)
  other arithmetic  72.8 us (8%)
  between operations  15.7 us (2%)
    ppermute x21, waiting for transfers between devices, shift(): lax.ppermute(block, 'tp', [(i, (i + distance) % size) for i in range(size)])  155 us
    psum x1, waiting for transfers between devices, shards(): lax.psum(transposed_product(hidden_low, down_full).astype(LOW), 'tp')  82 us
    reduce_scatter x2, waiting for transfers between devices, share_rows(): lax.psum_scatter(grad, ROWS, scatter_dimension=0, tiled=True, axis_index_...  64.2 us
    ppermute x21, starting transfers between devices, shift(): lax.ppermute(block, 'tp', [(i, (i + distance) % size) for i in range(size)])  57.6 us
    dot_general x7, matrix products, rows_product(): lax.dot_general(left, right, (((0,), (0,)), ((), ())), preferred_element_...  42.8 us
    dot_general x4, matrix products, product(): return jnp.dot(left, right, preferred_element_type=F32)  40.3 us
    all_gather x2, waiting for transfers between devices, gather_rows(): lax.all_gather(weight, ROWS, axis=0, tiled=True, axis_index_groups=[first...  38.3 us
    dot_general x4, matrix products, transposed_product(): lax.dot_general(left, right, (((1,), (1,)), ((), ())), preferred_element_...  37 us
  transfers between devices with their start and end apart: 55, of which 27 were waited for; matrix products, arithmetic and copies ran while one was open for 31% of the time, Pallas kernels for 0%

profile of v14, /device:TPU:0, one launch (start us, length us, event | category | flops | bytes accessed | tf_op | source)
XLA Modules:
  0.0 858.5 jit_solution(16910795776305961987)
XLA Ops:
  16.5 4.2 concatenate.62
  23.7 38.3 %all-gather.3.cloned.1.call-done = bf16[2304,1536]{1,0:T(8,128)(2,1)} async-done(((bf16[288,1536]{1,0:T(8,128)(2,1)}), bf16[2304,1536]{1,0:T(8,128)(2,1)}) %all-gather.3.cloned.1.call-update) | async-done | bytes 7077904 | tf_op jit(solution)/shard_map/all_gather | solution.py:185
  61.9 5.7 fusion.53
  68.4 4.1 collective-permute-start
  75.2 11.4 %collective-permute-done = bf16[384,512]{1,0:T(8,128)(2,1)} collective-permute-done((bf16[384,512]{1,0:T(8,128)(2,1)}, bf16[384,512]{1,0:T(8,128)(2,1)}, u32[]{:S(2)}, u32[]{:S(2)}) %collective-permute-start) | collective-permute-done | bytes 393248 | tf_op jit(solution)/shard_map/ppermute | solution.py:21
  98.4 4.0 collective-permute-start.1
  102.4 9.8 %collective-permute-done.1 = bf16[128,2304]{1,0:T(8,128)(2,1)} collective-permute-done((bf16[128,2304]{1,0:T(8,128)(2,1)S(1)}, bf16[128,2304]{1,0:T(8,128)(2,1)}, u32[]{:S(2)}, u32[]{:S(2)}) %collective-permute-start.1) | collective-permute-done | bytes 589856 | tf_op jit(solution)/shard_map/ppermute | solution.py:45
  113.9 4.5 collective-permute-start.3
  119.1 9.1 %collective-permute-done.3 = bf16[128,2304]{1,0:T(8,128)(2,1)S(1)} collective-permute-done((bf16[128,2304]{1,0:T(8,128)(2,1)S(1)}, bf16[128,2304]{1,0:T(8,128)(2,1)S(1)}, u32[]{:S(2)}, u32[]{:S(2)}) %collective-permute-start.3) | collective-permute-done | bytes 589856 | tf_op jit(solution)/shard_map/ppermute | solution.py:45
  131.4 6.0 collective-permute-start.5
  137.4 7.9 collective-permute-done.6
  151.6 4.3 collective-permute-start.7
  165.0 16.2 %collective-permute-done.16 = bf16[288,512]{1,0:T(8,128)(2,1)S(1)} collective-permute-done((bf16[288,512]{1,0:T(8,128)(2,1)S(1)}, bf16[288,512]{1,0:T(8,128)(2,1)S(1)}, u32[]{:S(2)}, u32[]{:S(2)}) %collective-permute-start.16) | collective-permute-done | bytes 294944 | tf_op jit(solution)/shard_map/ppermute | solution.py:57
  182.1 9.2 %collective-permute-done.17 = bf16[288,512]{1,0:T(8,128)(2,1)S(1)} collective-permute-done((bf16[288,512]{1,0:T(8,128)(2,1)S(1)}, bf16[288,512]{1,0:T(8,128)(2,1)S(1)}, u32[]{:S(2)}, u32[]{:S(2)}) %collective-permute-start.17) | collective-permute-done | bytes 294944 | tf_op jit(solution)/shard_map/ppermute | solution.py:57
  202.4 6.2 collective-permute-done.10
  212.0 5.2 concatenate.77
  217.9 5.4 concatenate.72
  225.4 4.7 broadcast_in_dim.149
  232.7 16.1 %collective-permute-done.19 = bf16[288,2048]{1,0:T(8,128)(2,1)} collective-permute-done((bf16[288,2048]{1,0:T(8,128)(2,1)}, bf16[288,2048]{1,0:T(8,128)(2,1)}, u32[]{:S(2)}, u32[]{:S(2)}) %collective-permute-start.19) | collective-permute-done | bytes 1179680 | tf_op jit(solution)/shard_map/ppermute | solution.py:197
  248.8 19.2 %collective-permute-done.20 = bf16[288,2048]{1,0:T(8,128)(2,1)} collective-permute-done((bf16[288,2048]{1,0:T(8,128)(2,1)}, bf16[288,2048]{1,0:T(8,128)(2,1)}, u32[]{:S(2)}, u32[]{:S(2)}) %collective-permute-start.20) | collective-permute-done | bytes 1179680 | tf_op jit(solution)/shard_map/ppermute | solution.py:197
  279.0 5.9 multiply_convert_fusion.2
  284.9 15.2 %fusion.2 = f32[512,4608]{1,0:T(8,128)S(1)} fusion(bf16[512,2304]{1,0:T(8,128)(2,1)} %get-tuple-element.100, bf16[2304,6912]{1,0:T(8,128)(2,1)} %all-gather.5.cloned.1.call-done), kind=kOutput, calls=%fused_computation.4 | convolution fusion | flops 10871635968 | bytes 33030144 | tf_op jit(solution)/shard_map/dot_general | solution.py:33
  305.2 11.0 %fusion.29 = bf16[512,2304]{1,0:T(8,128)(2,1)} fusion(bf16[512,2304]{1,0:T(8,128)(2,1)S(1)} %multiply_convert_fusion.1, bf16[2304,6912]{1,0:T(8,128)(2,1)} %all-gather.5.cloned.1.call-done), kind=kOutput, calls=%fused_computation.52 | convolution fusion | flops 5436997632 | bytes 15335424 | tf_op jit(solution)/shard_map/dot_general | solution.py:41
  329.0 82.0 %all-reduce.4.cloned.1.call-done = bf16[512,2304]{1,0:T(8,128)(2,1)} async-done(((bf16[512,2304]{1,0:T(8,128)(2,1)}), bf16[512,2304]{1,0:T(8,128)(2,1)}) %all-reduce.4.cloned.1.call-update) | async-done | bytes 2359312 | tf_op jit(solution)/shard_map/psum | solution.py:337
  416.8 5.1 fusion.25
  423.3 8.3 convolution_convert_fusion.1
  431.6 14.4 %fusion.23 = (bf16[512,2304]{1,0:T(8,128)(2,1)S(1)}, bf16[512,2304]{1,0:T(8,128)(2,1)S(1)}) fusion(f32[512,4608]{1,0:T(8,128)} %copy-done.11, bf16[512,2304]{1,0:T(8,128)(2,1)} %copy-done.26, bf16[2304,6912]{1,0:T(8,128)(2,1)} %all-gather.5.cloned.1.call-done), kind=kOutput, calls=%fused_computation.38 | convolution fusion | flops 5464129536 | bytes 27131904 | tf_op jit(solution)/shard_map/dot_general | solution.py:33
  446.0 16.3 %fusion.32 = bf16[512,2304]{1,0:T(8,128)(2,1)S(1)} fusion(bf16[2304,6912]{1,0:T(8,128)(2,1)} %all-gather.5.cloned.1.call-done, bf16[512,2304]{1,0:T(8,128)(2,1)S(1)} %get-tuple-element.108, bf16[512,2304]{1,0:T(8,128)(2,1)S(1)} %get-tuple-element.107), kind=kOutput, calls=%fused_computation.53 | convolution fusion | flops 10882252800 | bytes 28311552 | tf_op jit(solution)/shard_map/dot_general | solution.py:41
  471.2 9.3 %collective-permute-done.15 = bf16[128,2304]{1,0:T(8,128)(2,1)S(1)} collective-permute-done((bf16[128,2304]{1,0:T(8,128)(2,1)S(1)}, bf16[128,2304]{1,0:T(8,128)(2,1)S(1)}, u32[]{:S(2)}, u32[]{:S(2)}) %collective-permute-start.15) | collective-permute-done | bytes 589856 | tf_op jit(solution)/shard_map/ppermute | solution.py:57
  480.6 9.6 %collective-permute-done.14 = bf16[128,2304]{1,0:T(8,128)(2,1)S(1)} collective-permute-done((bf16[128,2304]{1,0:T(8,128)(2,1)S(1)}, bf16[128,2304]{1,0:T(8,128)(2,1)S(1)}, u32[]{:S(2)}, u32[]{:S(2)}) %collective-permute-start.14) | collective-permute-done | bytes 589856 | tf_op jit(solution)/shard_map/ppermute | solution.py:57
  490.2 26.4 %collective-permute-done.13 = bf16[128,2304]{1,0:T(8,128)(2,1)S(1)} collective-permute-done((bf16[128,2304]{1,0:T(8,128)(2,1)S(1)}, bf16[128,2304]{1,0:T(8,128)(2,1)S(1)}, u32[]{:S(2)}, u32[]{:S(2)}) %collective-permute-start.13) | collective-permute-done | bytes 589856 | tf_op jit(solution)/shard_map/ppermute | solution.py:57
  521.4 5.1 convolution_convert_fusion.6
  531.0 15.3 %collective-permute-done.26 = bf16[128,512]{1,0:T(8,128)(2,1)S(1)} collective-permute-done((bf16[128,512]{1,0:T(8,128)(2,1)S(1)}, bf16[128,512]{1,0:T(8,128)(2,1)S(1)}, u32[]{:S(2)}, u32[]{:S(2)}) %collective-permute-start.26) | collective-permute-done | bytes 131104 | tf_op jit(solution)/shard_map/ppermute | solution.py:57
  553.1 3.9 fusion.57
  566.8 4.8 collective-permute-done.29
  594.6 10.3 %convolution_convert_fusion = bf16[1152,4608]{1,0:T(8,128)(2,1)} fusion(bf16[512,2304]{1,0:T(8,128)(2,1)} %copy-done.67, bf16[512,2304]{1,0:T(8,128)(2,1)} %copy-done.66, bf16[512,2304]{1,0:T(8,128)(2,1)S(1)} %copy-done.23, s32[]{:T(128)S(6)} %select_n.267), kind=kOutput, calls=%fused_computation.1 | convolution fusion | flops 5450563584 | bytes 16515076 | tf_op jit(solution)/shard_map/dot_general | solution.py:37
  605.1 16.5 %collective-permute-done.48 = bf16[1152,4608]{1,0:T(8,128)(2,1)} collective-permute-done((bf16[1152,4608]{1,0:T(8,128)(2,1)}, bf16[1152,4608]{1,0:T(8,128)(2,1)}, u32[]{:S(2)}, u32[]{:S(2)}) %collective-permute-start.48) | collective-permute-done | bytes 10616864 | tf_op jit(solution)/shard_map/ppermute | solution.py:225
  621.6 13.6 %add_convert_fusion = bf16[1152,4608]{1,0:T(8,128)(2,1)} fusion(bf16[1152,4608]{1,0:T(8,128)(2,1)} %collective-permute-done.48, bf16[512,2304]{1,0:T(8,128)(2,1)} %copy-done.67, bf16[512,2304]{1,0:T(8,128)(2,1)} %copy-done.66, bf16[512,2304]{1,0:T(8,128)(2,1)S(1)} %copy-done.23, s32[]{:T(128)S(6)} %select_n.266), kind=kOutput, calls=%fused_computation | convolution fusion | flops 5461180416 | bytes 27131908 | tf_op jit(solution)/shard_map/dot_general | solution.py:37
  638.2 6.5 fusion.15
  646.1 11.6 %collective-permute-start.33 = (bf16[128,2304]{1,0:T(8,128)(2,1)}, bf16[128,2304]{1,0:T(8,128)(2,1)}, u32[]{:S(2)}, u32[]{:S(2)}) collective-permute-start(bf16[128,2304]{1,0:T(8,128)(2,1)} %get-tuple-element.74), channel_id=1, source_target_pairs={{0,1},{1,2},{2,3},{3,0},{4,5},{5,6},{6,7},{7,4},{8,9},{9,10},{10,1... | collective-permute-start | bytes 1769480 | tf_op jit(solution)/shard_map/ppermute | solution.py:57
  663.9 10.9 %collective-permute-done.33 = bf16[128,2304]{1,0:T(8,128)(2,1)} collective-permute-done((bf16[128,2304]{1,0:T(8,128)(2,1)}, bf16[128,2304]{1,0:T(8,128)(2,1)}, u32[]{:S(2)}, u32[]{:S(2)}) %collective-permute-start.33) | collective-permute-done | bytes 589856 | tf_op jit(solution)/shard_map/ppermute | solution.py:57
  674.9 15.4 %collective-permute-start.39 = (f32[4,2304]{1,0:T(4,128)S(1)}, f32[4,2304]{1,0:T(4,128)}, u32[]{:S(2)}, u32[]{:S(2)}) collective-permute-start(f32[4,2304]{1,0:T(4,128)S(1)} %concatenate.82), channel_id=1, source_target_pairs={{0,3},{1,0},{2,1},{3,2},{4,7},{5,4},{6,5},{7,6},{8,11},{9,8},{10,9... | collective-permute-start | bytes 110600 | tf_op jit(solution)/shard_map/ppermute | solution.py:57
  690.3 23.5 %collective-permute-done.31 = bf16[128,2304]{1,0:T(8,128)(2,1)} collective-permute-done((bf16[128,2304]{1,0:T(8,128)(2,1)}, bf16[128,2304]{1,0:T(8,128)(2,1)}, u32[]{:S(2)}, u32[]{:S(2)}) %collective-permute-start.31) | collective-permute-done | bytes 589856 | tf_op jit(solution)/shard_map/ppermute | solution.py:57
  727.3 5.1 concatenate.76
  741.8 9.0 %collective-permute-done.34 = bf16[128,2304]{1,0:T(8,128)(2,1)S(1)} collective-permute-done((bf16[128,2304]{1,0:T(8,128)(2,1)}, bf16[128,2304]{1,0:T(8,128)(2,1)S(1)}, u32[]{:S(2)}, u32[]{:S(2)}) %collective-permute-start.34) | collective-permute-done | bytes 589856 | tf_op jit(solution)/shard_map/ppermute | solution.py:57
  750.8 24.2 %collective-permute-done.35 = bf16[128,2304]{1,0:T(8,128)(2,1)S(1)} collective-permute-done((bf16[128,2304]{1,0:T(8,128)(2,1)}, bf16[128,2304]{1,0:T(8,128)(2,1)S(1)}, u32[]{:S(2)}, u32[]{:S(2)}) %collective-permute-start.35) | collective-permute-done | bytes 589856 | tf_op jit(solution)/shard_map/ppermute | solution.py:57
  782.6 64.2 %reduce-scatter.6.cloned.1.call-done = bf16[288,4608]{1,0:T(8,128)(2,1)} async-done(((bf16[1152,4608]{1,0:T(8,128)(2,1)}), bf16[288,4608]{1,0:T(8,128)(2,1)}) %reduce-scatter.6.cloned.1.call-update) | async-done | bytes 2654224 | tf_op jit(solution)/shard_map/reduce_scatter | solution.py:234
  846.8 4.5 slice_convert_fusion
  (343 shorter events, 203.4 us)
Async XLA Ops:
  7.2 54.7 %all-gather.3.cloned.1.call-start = ((), (), s32[]{:S(2)}) async-start(), calls=%async_computation.3 | async-start | bytes 7962624 | tf_op jit(solution)/shard_map/all_gather | solution.py:185
  9.5 275.4 %all-gather.5.cloned.1.call-start = ((), (), s32[]{:S(2)}) async-start(), calls=%async_computation.4 | async-start | bytes 35831808 | tf_op jit(solution)/shard_map/all_gather | solution.py:185
  13.0 398.0 %all-reduce.4.cloned.1.call-start = ((), (), s32[]{:S(2)}) async-start(), calls=%async_computation.5 | async-start | bytes 4718592 | tf_op jit(solution)/shard_map/psum | solution.py:337
  68.4 18.3 %collective-permute-start = (bf16[384,512]{1,0:T(8,128)(2,1)}, bf16[384,512]{1,0:T(8,128)(2,1)}, u32[]{:S(2)}, u32[]{:S(2)}) collective-permute-start(bf16[384,512]{1,0:T(8,128)(2,1)} %slice.274), channel_id=1, source_target_pairs={{0,4},{1,5},{2,6},{3,7},{8,12},{9,13},{10,14},{11,15},{16,20},{17,... | collective-permute-start | bytes 1179656 | tf_op jit(solution)/shard_map/ppermute | solution.py:21
  98.4 13.8 %collective-permute-start.1 = (bf16[128,2304]{1,0:T(8,128)(2,1)S(1)}, bf16[128,2304]{1,0:T(8,128)(2,1)}, u32[]{:S(2)}, u32[]{:S(2)}) collective-permute-start(bf16[128,2304]{1,0:T(8,128)(2,1)S(1)} %get-tuple-element.49), channel_id=1, source_target_pairs={{0,1},{4,5},{8,9},{12,13},{16,17},{20,21},{24,25},{28,29}} | collective-permute-start | bytes 1769480 | tf_op jit(solution)/shard_map/ppermute | solution.py:45
  113.9 14.3 %collective-permute-start.3 = (bf16[128,2304]{1,0:T(8,128)(2,1)S(1)}, bf16[128,2304]{1,0:T(8,128)(2,1)S(1)}, u32[]{:S(2)}, u32[]{:S(2)}) collective-permute-start(bf16[128,2304]{1,0:T(8,128)(2,1)S(1)} %get-tuple-element.51), channel_id=1, source_target_pairs={{0,1},{1,2},{4,5},{5,6},{8,9},{9,10},{12,13},{13,14},{16,17},{17,1... | collective-permute-start | bytes 1769480 | tf_op jit(solution)/shard_map/ppermute | solution.py:45
  118.4 10.7 %collective-permute-start.4 = (bf16[128,2304]{1,0:T(8,128)(2,1)S(1)}, bf16[128,2304]{1,0:T(8,128)(2,1)S(1)}, u32[]{:S(2)}, u32[]{:S(2)}) collective-permute-start(bf16[128,2304]{1,0:T(8,128)(2,1)S(1)} %get-tuple-element.52), channel_id=1, source_target_pairs={{2,1},{3,2},{6,5},{7,6},{10,9},{11,10},{14,13},{15,14},{18,17},{19... | collective-permute-start | bytes 1769480 | tf_op jit(solution)/shard_map/ppermute | solution.py:45
  130.1 15.3 %collective-permute-start.6 = (bf16[128,2304]{1,0:T(8,128)(2,1)}, bf16[128,2304]{1,0:T(8,128)(2,1)S(1)}, u32[]{:S(2)}, u32[]{:S(2)}) collective-permute-start(bf16[128,2304]{1,0:T(8,128)(2,1)} %add_convert_fusion.2), channel_id=1, source_target_pairs={{1,0},{2,1},{3,2},{5,4},{6,5},{7,6},{9,8},{10,9},{11,10},{13,12},{... | collective-permute-start | bytes 1769480 | tf_op jit(solution)/shard_map/ppermute | solution.py:45
  131.4 15.3 %collective-permute-start.5 = (bf16[128,2304]{1,0:T(8,128)(2,1)}, bf16[128,2304]{1,0:T(8,128)(2,1)S(1)}, u32[]{:S(2)}, u32[]{:S(2)}) collective-permute-start(bf16[128,2304]{1,0:T(8,128)(2,1)} %add_convert_fusion.3), channel_id=1, source_target_pairs={{0,1},{1,2},{2,3},{4,5},{5,6},{6,7},{8,9},{9,10},{10,11},{12,13},{... | collective-permute-start | bytes 1769480 | tf_op jit(solution)/shard_map/ppermute | solution.py:45
  151.6 40.4 %collective-permute-start.7 = (bf16[128,2304]{1,0:T(8,128)(2,1)S(1)}, bf16[128,2304]{1,0:T(8,128)(2,1)S(1)}, u32[]{:S(2)}, u32[]{:S(2)}) collective-permute-start(bf16[128,2304]{1,0:T(8,128)(2,1)S(1)} %get-tuple-element.103), channel_id=1, source_target_pairs={{0,1},{1,2},{2,3},{4,5},{5,6},{6,7},{8,9},{9,10},{10,11},{12,13},{... | collective-permute-start | bytes 1769480 | tf_op jit(solution)/shard_map/ppermute | solution.py:45
  155.9 36.1 %collective-permute-start.8 = (bf16[128,2304]{1,0:T(8,128)(2,1)S(1)}, bf16[128,2304]{1,0:T(8,128)(2,1)S(1)}, u32[]{:S(2)}, u32[]{:S(2)}) collective-permute-start(bf16[128,2304]{1,0:T(8,128)(2,1)S(1)} %get-tuple-element.103), channel_id=1, source_target_pairs={{1,0},{2,1},{3,2},{5,4},{6,5},{7,6},{9,8},{10,9},{11,10},{13,12},{... | collective-permute-start | bytes 1769480 | tf_op jit(solution)/shard_map/ppermute | solution.py:45
  157.3 24.0 %collective-permute-start.16 = (bf16[288,512]{1,0:T(8,128)(2,1)S(1)}, bf16[288,512]{1,0:T(8,128)(2,1)S(1)}, u32[]{:S(2)}, u32[]{:S(2)}) collective-permute-start(bf16[288,512]{1,0:T(8,128)(2,1)S(1)} %copy-done.32), channel_id=1, source_target_pairs={{0,1},{1,2},{2,3},{3,0},{4,5},{5,6},{6,7},{7,4},{8,9},{9,10},{10,1... | collective-permute-start | bytes 884744 | tf_op jit(solution)/shard_map/ppermute | solution.py:57
  160.1 31.2 %collective-permute-start.17 = (bf16[288,512]{1,0:T(8,128)(2,1)S(1)}, bf16[288,512]{1,0:T(8,128)(2,1)S(1)}, u32[]{:S(2)}, u32[]{:S(2)}) collective-permute-start(bf16[288,512]{1,0:T(8,128)(2,1)S(1)} %copy-done.32), channel_id=1, source_target_pairs={{0,2},{1,3},{2,0},{3,1},{4,6},{5,7},{6,4},{7,5},{8,10},{9,11},{10,... | collective-permute-start | bytes 884744 | tf_op jit(solution)/shard_map/ppermute | solution.py:57
  161.6 33.3 %collective-permute-start.18 = (bf16[288,512]{1,0:T(8,128)(2,1)S(1)}, bf16[288,512]{1,0:T(8,128)(2,1)S(1)}, u32[]{:S(2)}, u32[]{:S(2)}) collective-permute-start(bf16[288,512]{1,0:T(8,128)(2,1)S(1)} %copy-done.32), channel_id=1, source_target_pairs={{0,3},{1,0},{2,1},{3,2},{4,7},{5,4},{6,5},{7,6},{8,11},{9,8},{10,9... | collective-permute-start | bytes 884744 | tf_op jit(solution)/shard_map/ppermute | solution.py:57
  193.6 15.0 %collective-permute-start.10 = (bf16[128,2304]{1,0:T(8,128)(2,1)S(1)}, bf16[128,2304]{1,0:T(8,128)(2,1)}, u32[]{:S(2)}, u32[]{:S(2)}) collective-permute-start(bf16[128,2304]{1,0:T(8,128)(2,1)S(1)} %collective-permute-done.8), channel_id=1, source_target_pairs={{1,0},{2,1},{5,4},{6,5},{9,8},{10,9},{13,12},{14,13},{17,16},{18,1... | collective-permute-start | bytes 1769480 | tf_op jit(solution)/shard_map/ppermute | solution.py:45
  195.7 53.1 %collective-permute-start.19 = (bf16[288,2048]{1,0:T(8,128)(2,1)}, bf16[288,2048]{1,0:T(8,128)(2,1)}, u32[]{:S(2)}, u32[]{:S(2)}) collective-permute-start(bf16[288,2048]{1,0:T(8,128)(2,1)} %constant_dynamic-update-slice_fusion), channel_id=1, source_target_pairs={{0,20},{4,16},{8,28},{12,24},{16,4},{20,0},{24,12},{28,8},{1,21},{... | collective-permute-start | bytes 3538952 | tf_op jit(solution)/shard_map/ppermute | solution.py:197
  197.2 70.8 %collective-permute-start.20 = (bf16[288,2048]{1,0:T(8,128)(2,1)}, bf16[288,2048]{1,0:T(8,128)(2,1)}, u32[]{:S(2)}, u32[]{:S(2)}) collective-permute-start(bf16[288,2048]{1,0:T(8,128)(2,1)} %constant_dynamic-update-slice_fusion), channel_id=1, source_target_pairs={{0,4},{4,0},{8,12},{12,8},{16,20},{20,16},{24,28},{28,24},{1,5},{5... | collective-permute-start | bytes 3538952 | tf_op jit(solution)/shard_map/ppermute | solution.py:197
  198.2 69.8 %collective-permute-start.21 = (bf16[288,2048]{1,0:T(8,128)(2,1)}, bf16[288,2048]{1,0:T(8,128)(2,1)}, u32[]{:S(2)}, u32[]{:S(2)}) collective-permute-start(bf16[288,2048]{1,0:T(8,128)(2,1)} %constant_dynamic-update-slice_fusion), channel_id=1, source_target_pairs={{0,16},{4,20},{8,24},{12,28},{16,0},{20,4},{24,8},{28,12},{1,17},{... | collective-permute-start | bytes 3538952 | tf_op jit(solution)/shard_map/ppermute | solution.py:197
  208.6 59.9 %collective-permute-start.11 = (bf16[128,2304]{1,0:T(8,128)(2,1)}, bf16[128,2304]{1,0:T(8,128)(2,1)}, u32[]{:S(2)}, u32[]{:S(2)}) collective-permute-start(bf16[128,2304]{1,0:T(8,128)(2,1)} %collective-permute-done.9), channel_id=1, source_target_pairs={{2,3},{6,7},{10,11},{14,15},{18,19},{22,23},{26,27},{30,31}} | collective-permute-start | bytes 1769480 | tf_op jit(solution)/shard_map/ppermute | solution.py:45
  210.0 58.5 %collective-permute-start.12 = (bf16[128,2304]{1,0:T(8,128)(2,1)}, bf16[128,2304]{1,0:T(8,128)(2,1)}, u32[]{:S(2)}, u32[]{:S(2)}) collective-permute-start(bf16[128,2304]{1,0:T(8,128)(2,1)} %collective-permute-done.10), channel_id=1, source_target_pairs={{1,0},{5,4},{9,8},{13,12},{17,16},{21,20},{25,24},{29,28}} | collective-permute-start | bytes 1769480 | tf_op jit(solution)/shard_map/ppermute | solution.py:45
  248.8 75.2 %collective-permute-start.22 = (bf16[288,2048]{1,0:T(8,128)(2,1)}, bf16[288,2048]{1,0:T(8,128)(2,1)}, u32[]{:S(2)}, u32[]{:S(2)}) collective-permute-start(bf16[288,2048]{1,0:T(8,128)(2,1)} %constant_dynamic-update-slice_fusion), channel_id=1, source_target_pairs={{0,8},{4,12},{8,0},{12,4},{16,24},{20,28},{24,16},{28,20},{1,9},{5... | collective-permute-start | bytes 3538952 | tf_op jit(solution)/shard_map/ppermute | solution.py:197
  268.0 58.5 %collective-permute-start.23 = (bf16[288,2048]{1,0:T(8,128)(2,1)}, bf16[288,2048]{1,0:T(8,128)(2,1)}, u32[]{:S(2)}, u32[]{:S(2)}) collective-permute-start(bf16[288,2048]{1,0:T(8,128)(2,1)} %collective-permute-done.20), channel_id=1, source_target_pairs={{0,8},{4,12},{8,0},{12,4},{16,24},{20,28},{24,16},{28,20},{1,9},{5... | collective-permute-start | bytes 3538952 | tf_op jit(solution)/shard_map/ppermute | solution.py:197
  268.0 198.4 %collective-permute-start.24 = (bf16[288,2048]{1,0:T(8,128)(2,1)}, bf16[288,2048]{1,0:T(8,128)(2,1)}, u32[]{:S(2)}, u32[]{:S(2)}) collective-permute-start(bf16[288,2048]{1,0:T(8,128)(2,1)} %collective-permute-done.21), channel_id=1, source_target_pairs={{0,8},{4,12},{8,0},{12,4},{16,24},{20,28},{24,16},{28,20},{1,9},{5... | collective-permute-start | bytes 3538952 | tf_op jit(solution)/shard_map/ppermute | solution.py:197
  268.5 200.3 %collective-permute-start.25 = (bf16[288,2048]{1,0:T(8,128)(2,1)}, bf16[288,2048]{1,0:T(8,128)(2,1)}, u32[]{:S(2)}, u32[]{:S(2)}) collective-permute-start(bf16[288,2048]{1,0:T(8,128)(2,1)} %collective-permute-done.19), channel_id=1, source_target_pairs={{0,8},{4,12},{8,0},{12,4},{16,24},{20,28},{24,16},{28,20},{1,9},{5... | collective-permute-start | bytes 3538952 | tf_op jit(solution)/shard_map/ppermute | solution.py:197
  316.2 459.0 %reduce-scatter.4.cloned.1.call-start = ((), (), s32[]{:S(2)}) async-start(), calls=%async_computation.6 | async-start | bytes 4423680 | tf_op jit(solution)/shard_map/reduce_scatter | solution.py:234
  462.5 18.1 %collective-permute-start.15 = (bf16[128,2304]{1,0:T(8,128)(2,1)S(1)}, bf16[128,2304]{1,0:T(8,128)(2,1)S(1)}, u32[]{:S(2)}, u32[]{:S(2)}) collective-permute-start(bf16[128,2304]{1,0:T(8,128)(2,1)S(1)} %get-tuple-element.65), channel_id=1, source_target_pairs={{0,1},{1,2},{2,3},{3,0},{4,5},{5,6},{6,7},{7,4},{8,9},{9,10},{10,1... | collective-permute-start | bytes 1769480 | tf_op jit(solution)/shard_map/ppermute | solution.py:57
  462.8 27.4 %collective-permute-start.14 = (bf16[128,2304]{1,0:T(8,128)(2,1)S(1)}, bf16[128,2304]{1,0:T(8,128)(2,1)S(1)}, u32[]{:S(2)}, u32[]{:S(2)}) collective-permute-start(bf16[128,2304]{1,0:T(8,128)(2,1)S(1)} %get-tuple-element.64), channel_id=1, source_target_pairs={{0,3},{1,0},{2,1},{3,2},{4,7},{5,4},{6,5},{7,6},{8,11},{9,8},{10,9... | collective-permute-start | bytes 1769480 | tf_op jit(solution)/shard_map/ppermute | solution.py:57
  466.4 50.2 %collective-permute-start.13 = (bf16[128,2304]{1,0:T(8,128)(2,1)S(1)}, bf16[128,2304]{1,0:T(8,128)(2,1)S(1)}, u32[]{:S(2)}, u32[]{:S(2)}) collective-permute-start(bf16[128,2304]{1,0:T(8,128)(2,1)S(1)} %get-tuple-element.63), channel_id=1, source_target_pairs={{0,2},{1,3},{2,0},{3,1},{4,6},{5,7},{6,4},{7,5},{8,10},{9,11},{10,... | collective-permute-start | bytes 1769480 | tf_op jit(solution)/shard_map/ppermute | solution.py:57
  521.1 53.5 %collective-permute-start.44 = (bf16[128,2304]{1,0:T(8,128)(2,1)S(1)}, bf16[128,2304]{1,0:T(8,128)(2,1)S(1)}, u32[]{:S(2)}, u32[]{:S(2)}) collective-permute-start(bf16[128,2304]{1,0:T(8,128)(2,1)S(1)} %fusion.69), channel_id=1, source_target_pairs={{0,1},{1,2},{2,3},{3,0},{4,5},{5,6},{6,7},{7,4},{8,9},{9,10},{10,1... | collective-permute-start | bytes 1769480 | tf_op jit(solution)/shard_map/ppermute | solution.py:57
  526.5 19.8 %collective-permute-start.26 = (bf16[128,512]{1,0:T(8,128)(2,1)S(1)}, bf16[128,512]{1,0:T(8,128)(2,1)S(1)}, u32[]{:S(2)}, u32[]{:S(2)}) collective-permute-start(bf16[128,512]{1,0:T(8,128)(2,1)S(1)} %get-tuple-element.67), channel_id=1, source_target_pairs={{0,2},{1,3},{2,0},{3,1},{4,6},{5,7},{6,4},{7,5},{8,10},{9,11},{10,... | collective-permute-start | bytes 393224 | tf_op jit(solution)/shard_map/ppermute | solution.py:57
  528.3 18.0 %collective-permute-start.27 = (bf16[128,512]{1,0:T(8,128)(2,1)S(1)}, bf16[128,512]{1,0:T(8,128)(2,1)S(1)}, u32[]{:S(2)}, u32[]{:S(2)}) collective-permute-start(bf16[128,512]{1,0:T(8,128)(2,1)S(1)} %get-tuple-element.68), channel_id=1, source_target_pairs={{0,3},{1,0},{2,1},{3,2},{4,7},{5,4},{6,5},{7,6},{8,11},{9,8},{10,9... | collective-permute-start | bytes 393224 | tf_op jit(solution)/shard_map/ppermute | solution.py:57
  530.4 15.9 %collective-permute-start.28 = (bf16[128,512]{1,0:T(8,128)(2,1)S(1)}, bf16[128,512]{1,0:T(8,128)(2,1)S(1)}, u32[]{:S(2)}, u32[]{:S(2)}) collective-permute-start(bf16[128,512]{1,0:T(8,128)(2,1)S(1)} %get-tuple-element.69), channel_id=1, source_target_pairs={{0,1},{1,2},{2,3},{3,0},{4,5},{5,6},{6,7},{7,4},{8,9},{9,10},{10,1... | collective-permute-start | bytes 393224 | tf_op jit(solution)/shard_map/ppermute | solution.py:57
  546.4 29.9 %collective-permute-start.45 = (bf16[128,2304]{1,0:T(8,128)(2,1)S(1)}, bf16[128,2304]{1,0:T(8,128)(2,1)}, u32[]{:S(2)}, u32[]{:S(2)}) collective-permute-start(bf16[128,2304]{1,0:T(8,128)(2,1)S(1)} %fusion.69), channel_id=1, source_target_pairs={{0,2},{1,3},{2,0},{3,1},{4,6},{5,7},{6,4},{7,5},{8,10},{9,11},{10,... | collective-permute-start | bytes 1769480 | tf_op jit(solution)/shard_map/ppermute | solution.py:57
  548.7 28.7 %collective-permute-start.46 = (bf16[128,2304]{1,0:T(8,128)(2,1)S(1)}, bf16[128,2304]{1,0:T(8,128)(2,1)}, u32[]{:S(2)}, u32[]{:S(2)}) collective-permute-start(bf16[128,2304]{1,0:T(8,128)(2,1)S(1)} %fusion.69), channel_id=1, source_target_pairs={{0,3},{1,0},{2,1},{3,2},{4,7},{5,4},{6,5},{7,6},{8,11},{9,8},{10,9... | collective-permute-start | bytes 1769480 | tf_op jit(solution)/shard_map/ppermute | solution.py:57
  574.5 13.1 %collective-permute-start.43 = (bf16[1152,1024]{1,0:T(8,128)(2,1)}, bf16[1152,1024]{1,0:T(8,128)(2,1)}, u32[]{:S(2)}, u32[]{:S(2)}) collective-permute-start(bf16[1152,1024]{1,0:T(8,128)(2,1)} %convolution_convert_fusion.4), channel_id=1, source_target_pairs={{0,8},{8,0},{16,24},{24,16},{1,9},{9,1},{17,25},{25,17},{2,10},{10... | collective-permute-start | bytes 7077896 | tf_op jit(solution)/shard_map/ppermute | solution.py:225
  593.0 186.7 %reduce-scatter.8.cloned.1.call-start = ((), (), s32[]{:S(2)}) async-start(), calls=%async_computation.8 | async-start | bytes 11943936 | tf_op jit(solution)/shard_map/reduce_scatter | solution.py:241
  593.5 253.2 %reduce-scatter.6.cloned.1.call-start = ((), (), s32[]{:S(2)}) async-start(), calls=%async_computation.7 | async-start | bytes 13271040 | tf_op jit(solution)/shard_map/reduce_scatter | solution.py:234
  604.9 16.7 %collective-permute-start.48 = (bf16[1152,4608]{1,0:T(8,128)(2,1)}, bf16[1152,4608]{1,0:T(8,128)(2,1)}, u32[]{:S(2)}, u32[]{:S(2)}) collective-permute-start(bf16[1152,4608]{1,0:T(8,128)(2,1)} %convolution_convert_fusion), channel_id=1, source_target_pairs={{0,8},{8,0},{16,24},{24,16},{1,9},{9,1},{17,25},{25,17},{2,10},{10... | collective-permute-start | bytes 31850504 | tf_op jit(solution)/shard_map/ppermute | solution.py:225
  646.1 28.7 %collective-permute-start.33 = (bf16[128,2304]{1,0:T(8,128)(2,1)}, bf16[128,2304]{1,0:T(8,128)(2,1)}, u32[]{:S(2)}, u32[]{:S(2)}) collective-permute-start(bf16[128,2304]{1,0:T(8,128)(2,1)} %get-tuple-element.74), channel_id=1, source_target_pairs={{0,1},{1,2},{2,3},{3,0},{4,5},{5,6},{6,7},{7,4},{8,9},{9,10},{10,1... | collective-permute-start | bytes 1769480 | tf_op jit(solution)/shard_map/ppermute | solution.py:57
  657.7 32.6 %collective-permute-start.32 = (bf16[128,2304]{1,0:T(8,128)(2,1)}, bf16[128,2304]{1,0:T(8,128)(2,1)}, u32[]{:S(2)}, u32[]{:S(2)}) collective-permute-start(bf16[128,2304]{1,0:T(8,128)(2,1)} %get-tuple-element.73), channel_id=1, source_target_pairs={{0,3},{1,0},{2,1},{3,2},{4,7},{5,4},{6,5},{7,6},{8,11},{9,8},{10,9... | collective-permute-start | bytes 1769480 | tf_op jit(solution)/shard_map/ppermute | solution.py:57
  660.3 53.5 %collective-permute-start.31 = (bf16[128,2304]{1,0:T(8,128)(2,1)}, bf16[128,2304]{1,0:T(8,128)(2,1)}, u32[]{:S(2)}, u32[]{:S(2)}) collective-permute-start(bf16[128,2304]{1,0:T(8,128)(2,1)} %get-tuple-element.72), channel_id=1, source_target_pairs={{0,2},{1,3},{2,0},{3,1},{4,6},{5,7},{6,4},{7,5},{8,10},{9,11},{10,... | collective-permute-start | bytes 1769480 | tf_op jit(solution)/shard_map/ppermute | solution.py:57
  661.4 59.9 %collective-permute-start.37 = (f32[4,2304]{1,0:T(4,128)S(1)}, f32[4,2304]{1,0:T(4,128)S(1)}, u32[]{:S(2)}, u32[]{:S(2)}) collective-permute-start(f32[4,2304]{1,0:T(4,128)S(1)} %concatenate.82), channel_id=1, source_target_pairs={{0,1},{1,2},{2,3},{3,0},{4,5},{5,6},{6,7},{7,4},{8,9},{9,10},{10,1... | collective-permute-start | bytes 110600 | tf_op jit(solution)/shard_map/ppermute | solution.py:57
  663.5 57.8 %collective-permute-start.38 = (f32[4,2304]{1,0:T(4,128)S(1)}, f32[4,2304]{1,0:T(4,128)}, u32[]{:S(2)}, u32[]{:S(2)}) collective-permute-start(f32[4,2304]{1,0:T(4,128)S(1)} %concatenate.82), channel_id=1, source_target_pairs={{0,2},{1,3},{2,0},{3,1},{4,6},{5,7},{6,4},{7,5},{8,10},{9,11},{10,... | collective-permute-start | bytes 110600 | tf_op jit(solution)/shard_map/ppermute | solution.py:57
  674.9 46.4 %collective-permute-start.39 = (f32[4,2304]{1,0:T(4,128)S(1)}, f32[4,2304]{1,0:T(4,128)}, u32[]{:S(2)}, u32[]{:S(2)}) collective-permute-start(f32[4,2304]{1,0:T(4,128)S(1)} %concatenate.82), channel_id=1, source_target_pairs={{0,3},{1,0},{2,1},{3,2},{4,7},{5,4},{6,5},{7,6},{8,11},{9,8},{10,9... | collective-permute-start | bytes 110600 | tf_op jit(solution)/shard_map/ppermute | solution.py:57
  724.0 12.3 %collective-permute-start.41 = (f32[4,2304]{1,0:T(4,128)}, f32[4,2304]{1,0:T(4,128)}, u32[]{:S(2)}, u32[]{:S(2)}) collective-permute-start(f32[4,2304]{1,0:T(4,128)} %add.436), channel_id=1, source_target_pairs={{0,16},{8,24},{16,0},{24,8},{1,17},{9,25},{17,1},{25,9},{2,18},{10... | collective-permute-start | bytes 110600 | tf_op jit(solution)/shard_map/ppermute | solution.py:145
  732.5 18.3 %collective-permute-start.34 = (bf16[128,2304]{1,0:T(8,128)(2,1)}, bf16[128,2304]{1,0:T(8,128)(2,1)S(1)}, u32[]{:S(2)}, u32[]{:S(2)}) collective-permute-start(bf16[128,2304]{1,0:T(8,128)(2,1)} %concatenate.81), channel_id=1, source_target_pairs={{0,1},{1,2},{2,3},{3,0},{4,5},{5,6},{6,7},{7,4},{8,9},{9,10},{10,1... | collective-permute-start | bytes 1769480 | tf_op jit(solution)/shard_map/ppermute | solution.py:57
  732.5 42.5 %collective-permute-start.35 = (bf16[128,2304]{1,0:T(8,128)(2,1)}, bf16[128,2304]{1,0:T(8,128)(2,1)S(1)}, u32[]{:S(2)}, u32[]{:S(2)}) collective-permute-start(bf16[128,2304]{1,0:T(8,128)(2,1)} %concatenate.81), channel_id=1, source_target_pairs={{0,2},{1,3},{2,0},{3,1},{4,6},{5,7},{6,4},{7,5},{8,10},{9,11},{10,... | collective-permute-start | bytes 1769480 | tf_op jit(solution)/shard_map/ppermute | solution.py:57
  733.3 41.7 %collective-permute-start.36 = (bf16[128,2304]{1,0:T(8,128)(2,1)}, bf16[128,2304]{1,0:T(8,128)(2,1)S(1)}, u32[]{:S(2)}, u32[]{:S(2)}) collective-permute-start(bf16[128,2304]{1,0:T(8,128)(2,1)} %concatenate.81), channel_id=1, source_target_pairs={{0,3},{1,0},{2,1},{3,2},{4,7},{5,4},{6,5},{7,6},{8,11},{9,8},{10,9... | collective-permute-start | bytes 1769480 | tf_op jit(solution)/shard_map/ppermute | solution.py:57
  (75 other events, 1033.5 us)
Sparse Core Ops, SparseCore 0:
  10.5 51.4 all-gather.2
  63.8 209.5 all-gather.4
  316.3 94.6 all-reduce.3
  593.1 59.3 reduce-scatter.3
  655.8 83.3 reduce-scatter.7
  742.2 104.5 reduce-scatter.5

commit v15 on v14

--- a/solution.py
+++ b/solution.py
@@ -364,9 +364,8 @@
     grad_one_own = grad_branch_one.astype(LOW)
     early = {1: shift(grad_one_own, 1)}
     grad_attended = product(grad_one_own, output_all).astype(LOW)
-    grad_attended, grad_one_own = lax.optimization_barrier(
-        (exchanged(grad_attended), grad_one_own)
-    )
+    grad_attended = exchanged(grad_attended)
+    grad_attended, grad_one_own = lax.optimization_barrier((grad_attended, grad_one_own))
     grad_attended = grad_attended.reshape(length, kv_heads, repeats, HD)
     later = (middle, grad_normed_two, branch_one, grad_middle, grad_one_own)
     middle_kept, normed_kept, branch_kept, grad_kept, grad_one_own = lax.optimization_barrier(later)

time: 869 us -> 869 us (level)
  no operation moved by 1% of the time
where the time goes in v15:
time: 869 us; the launch traced here: 858 us
  waiting for transfers between devices  448 us (52%)
  matrix products  134 us (15%)
  starting transfers between devices  102 us (12%)
  local copies, waits for them, and re-layouts  85.1 us (10%)
  other arithmetic  72.8 us (8%)
  between operations  15.7 us (2%)
    ppermute x21, waiting for transfers between devices, shift(): lax.ppermute(block, 'tp', [(i, (i + distance) % size) for i in range(size)])  155 us
    psum x1, waiting for transfers between devices, shards(): lax.psum(transposed_product(hidden_low, down_full).astype(LOW), 'tp')  82 us
    reduce_scatter x2, waiting for transfers between devices, share_rows(): lax.psum_scatter(grad, ROWS, scatter_dimension=0, tiled=True, axis_index_...  64.2 us
    ppermute x21, starting transfers between devices, shift(): lax.ppermute(block, 'tp', [(i, (i + distance) % size) for i in range(size)])  57.6 us
    dot_general x7, matrix products, rows_product(): lax.dot_general(left, right, (((0,), (0,)), ((), ())), preferred_element_...  42.8 us
    dot_general x4, matrix products, product(): return jnp.dot(left, right, preferred_element_type=F32)  40.3 us
    all_gather x2, waiting for transfers between devices, gather_rows(): lax.all_gather(weight, ROWS, axis=0, tiled=True, axis_index_groups=[first...  38.3 us
    dot_general x4, matrix products, transposed_product(): lax.dot_general(left, right, (((1,), (1,)), ((), ())), preferred_element_...  37 us
  transfers between devices with their start and end apart: 55, of which 27 were waited for; matrix products, arithmetic and copies ran while one was open for 31% of the time, Pallas kernels for 0%

profile of v15, /device:TPU:0, one launch (start us, length us, event | category | flops | bytes accessed | tf_op | source)
XLA Modules:
  0.0 858.5 jit_solution(16910795776305961987)
XLA Ops:
  16.5 4.2 concatenate.62
  23.7 38.3 %all-gather.3.cloned.1.call-done = bf16[2304,1536]{1,0:T(8,128)(2,1)} async-done(((bf16[288,1536]{1,0:T(8,128)(2,1)}), bf16[2304,1536]{1,0:T(8,128)(2,1)}) %all-gather.3.cloned.1.call-update) | async-done | bytes 7077904 | tf_op jit(solution)/shard_map/all_gather | solution.py:185
  61.9 5.7 fusion.53
  68.4 4.1 collective-permute-start
  75.2 11.4 %collective-permute-done = bf16[384,512]{1,0:T(8,128)(2,1)} collective-permute-done((bf16[384,512]{1,0:T(8,128)(2,1)}, bf16[384,512]{1,0:T(8,128)(2,1)}, u32[]{:S(2)}, u32[]{:S(2)}) %collective-permute-start) | collective-permute-done | bytes 393248 | tf_op jit(solution)/shard_map/ppermute | solution.py:21
  98.4 4.0 collective-permute-start.1
  102.4 9.8 %collective-permute-done.1 = bf16[128,2304]{1,0:T(8,128)(2,1)} collective-permute-done((bf16[128,2304]{1,0:T(8,128)(2,1)S(1)}, bf16[128,2304]{1,0:T(8,128)(2,1)}, u32[]{:S(2)}, u32[]{:S(2)}) %collective-permute-start.1) | collective-permute-done | bytes 589856 | tf_op jit(solution)/shard_map/ppermute | solution.py:45
  113.9 4.5 collective-permute-start.3
  119.1 9.1 %collective-permute-done.3 = bf16[128,2304]{1,0:T(8,128)(2,1)S(1)} collective-permute-done((bf16[128,2304]{1,0:T(8,128)(2,1)S(1)}, bf16[128,2304]{1,0:T(8,128)(2,1)S(1)}, u32[]{:S(2)}, u32[]{:S(2)}) %collective-permute-start.3) | collective-permute-done | bytes 589856 | tf_op jit(solution)/shard_map/ppermute | solution.py:45
  131.4 6.0 collective-permute-start.5
  137.4 7.9 collective-permute-done.6
  151.6 4.3 collective-permute-start.7
  165.0 16.2 %collective-permute-done.16 = bf16[288,512]{1,0:T(8,128)(2,1)S(1)} collective-permute-done((bf16[288,512]{1,0:T(8,128)(2,1)S(1)}, bf16[288,512]{1,0:T(8,128)(2,1)S(1)}, u32[]{:S(2)}, u32[]{:S(2)}) %collective-permute-start.16) | collective-permute-done | bytes 294944 | tf_op jit(solution)/shard_map/ppermute | solution.py:57
  182.1 9.2 %collective-permute-done.17 = bf16[288,512]{1,0:T(8,128)(2,1)S(1)} collective-permute-done((bf16[288,512]{1,0:T(8,128)(2,1)S(1)}, bf16[288,512]{1,0:T(8,128)(2,1)S(1)}, u32[]{:S(2)}, u32[]{:S(2)}) %collective-permute-start.17) | collective-permute-done | bytes 294944 | tf_op jit(solution)/shard_map/ppermute | solution.py:57
  202.4 6.2 collective-permute-done.10
  212.0 5.2 concatenate.77
  217.9 5.4 concatenate.72
  225.4 4.7 broadcast_in_dim.149
  232.7 16.1 %collective-permute-done.19 = bf16[288,2048]{1,0:T(8,128)(2,1)} collective-permute-done((bf16[288,2048]{1,0:T(8,128)(2,1)}, bf16[288,2048]{1,0:T(8,128)(2,1)}, u32[]{:S(2)}, u32[]{:S(2)}) %collective-permute-start.19) | collective-permute-done | bytes 1179680 | tf_op jit(solution)/shard_map/ppermute | solution.py:197
  248.8 19.2 %collective-permute-done.20 = bf16[288,2048]{1,0:T(8,128)(2,1)} collective-permute-done((bf16[288,2048]{1,0:T(8,128)(2,1)}, bf16[288,2048]{1,0:T(8,128)(2,1)}, u32[]{:S(2)}, u32[]{:S(2)}) %collective-permute-start.20) | collective-permute-done | bytes 1179680 | tf_op jit(solution)/shard_map/ppermute | solution.py:197
  279.0 5.9 multiply_convert_fusion.2
  284.9 15.2 %fusion.2 = f32[512,4608]{1,0:T(8,128)S(1)} fusion(bf16[512,2304]{1,0:T(8,128)(2,1)} %get-tuple-element.100, bf16[2304,6912]{1,0:T(8,128)(2,1)} %all-gather.5.cloned.1.call-done), kind=kOutput, calls=%fused_computation.4 | convolution fusion | flops 10871635968 | bytes 33030144 | tf_op jit(solution)/shard_map/dot_general | solution.py:33
  305.2 11.0 %fusion.29 = bf16[512,2304]{1,0:T(8,128)(2,1)} fusion(bf16[512,2304]{1,0:T(8,128)(2,1)S(1)} %multiply_convert_fusion.1, bf16[2304,6912]{1,0:T(8,128)(2,1)} %all-gather.5.cloned.1.call-done), kind=kOutput, calls=%fused_computation.52 | convolution fusion | flops 5436997632 | bytes 15335424 | tf_op jit(solution)/shard_map/dot_general | solution.py:41
  329.0 82.0 %all-reduce.4.cloned.1.call-done = bf16[512,2304]{1,0:T(8,128)(2,1)} async-done(((bf16[512,2304]{1,0:T(8,128)(2,1)}), bf16[512,2304]{1,0:T(8,128)(2,1)}) %all-reduce.4.cloned.1.call-update) | async-done | bytes 2359312 | tf_op jit(solution)/shard_map/psum | solution.py:337
  416.8 5.1 fusion.25
  423.3 8.3 convolution_convert_fusion.1
  431.6 14.4 %fusion.23 = (bf16[512,2304]{1,0:T(8,128)(2,1)S(1)}, bf16[512,2304]{1,0:T(8,128)(2,1)S(1)}) fusion(f32[512,4608]{1,0:T(8,128)} %copy-done.11, bf16[512,2304]{1,0:T(8,128)(2,1)} %copy-done.26, bf16[2304,6912]{1,0:T(8,128)(2,1)} %all-gather.5.cloned.1.call-done), kind=kOutput, calls=%fused_computation.38 | convolution fusion | flops 5464129536 | bytes 27131904 | tf_op jit(solution)/shard_map/dot_general | solution.py:33
  446.0 16.3 %fusion.32 = bf16[512,2304]{1,0:T(8,128)(2,1)S(1)} fusion(bf16[2304,6912]{1,0:T(8,128)(2,1)} %all-gather.5.cloned.1.call-done, bf16[512,2304]{1,0:T(8,128)(2,1)S(1)} %get-tuple-element.108, bf16[512,2304]{1,0:T(8,128)(2,1)S(1)} %get-tuple-element.107), kind=kOutput, calls=%fused_computation.53 | convolution fusion | flops 10882252800 | bytes 28311552 | tf_op jit(solution)/shard_map/dot_general | solution.py:41
  471.2 9.3 %collective-permute-done.15 = bf16[128,2304]{1,0:T(8,128)(2,1)S(1)} collective-permute-done((bf16[128,2304]{1,0:T(8,128)(2,1)S(1)}, bf16[128,2304]{1,0:T(8,128)(2,1)S(1)}, u32[]{:S(2)}, u32[]{:S(2)}) %collective-permute-start.15) | collective-permute-done | bytes 589856 | tf_op jit(solution)/shard_map/ppermute | solution.py:57
  480.6 9.6 %collective-permute-done.14 = bf16[128,2304]{1,0:T(8,128)(2,1)S(1)} collective-permute-done((bf16[128,2304]{1,0:T(8,128)(2,1)S(1)}, bf16[128,2304]{1,0:T(8,128)(2,1)S(1)}, u32[]{:S(2)}, u32[]{:S(2)}) %collective-permute-start.14) | collective-permute-done | bytes 589856 | tf_op jit(solution)/shard_map/ppermute | solution.py:57
  490.2 26.4 %collective-permute-done.13 = bf16[128,2304]{1,0:T(8,128)(2,1)S(1)} collective-permute-done((bf16[128,2304]{1,0:T(8,128)(2,1)S(1)}, bf16[128,2304]{1,0:T(8,128)(2,1)S(1)}, u32[]{:S(2)}, u32[]{:S(2)}) %collective-permute-start.13) | collective-permute-done | bytes 589856 | tf_op jit(solution)/shard_map/ppermute | solution.py:57
  521.4 5.1 convolution_convert_fusion.6
  531.0 15.3 %collective-permute-done.26 = bf16[128,512]{1,0:T(8,128)(2,1)S(1)} collective-permute-done((bf16[128,512]{1,0:T(8,128)(2,1)S(1)}, bf16[128,512]{1,0:T(8,128)(2,1)S(1)}, u32[]{:S(2)}, u32[]{:S(2)}) %collective-permute-start.26) | collective-permute-done | bytes 131104 | tf_op jit(solution)/shard_map/ppermute | solution.py:57
  553.1 3.9 fusion.57
  566.8 4.8 collective-permute-done.29
  594.6 10.3 %convolution_convert_fusion = bf16[1152,4608]{1,0:T(8,128)(2,1)} fusion(bf16[512,2304]{1,0:T(8,128)(2,1)} %copy-done.67, bf16[512,2304]{1,0:T(8,128)(2,1)} %copy-done.66, bf16[512,2304]{1,0:T(8,128)(2,1)S(1)} %copy-done.23, s32[]{:T(128)S(6)} %select_n.267), kind=kOutput, calls=%fused_computation.1 | convolution fusion | flops 5450563584 | bytes 16515076 | tf_op jit(solution)/shard_map/dot_general | solution.py:37
  605.1 16.5 %collective-permute-done.48 = bf16[1152,4608]{1,0:T(8,128)(2,1)} collective-permute-done((bf16[1152,4608]{1,0:T(8,128)(2,1)}, bf16[1152,4608]{1,0:T(8,128)(2,1)}, u32[]{:S(2)}, u32[]{:S(2)}) %collective-permute-start.48) | collective-permute-done | bytes 10616864 | tf_op jit(solution)/shard_map/ppermute | solution.py:225
  621.6 13.6 %add_convert_fusion = bf16[1152,4608]{1,0:T(8,128)(2,1)} fusion(bf16[1152,4608]{1,0:T(8,128)(2,1)} %collective-permute-done.48, bf16[512,2304]{1,0:T(8,128)(2,1)} %copy-done.67, bf16[512,2304]{1,0:T(8,128)(2,1)} %copy-done.66, bf16[512,2304]{1,0:T(8,128)(2,1)S(1)} %copy-done.23, s32[]{:T(128)S(6)} %select_n.266), kind=kOutput, calls=%fused_computation | convolution fusion | flops 5461180416 | bytes 27131908 | tf_op jit(solution)/shard_map/dot_general | solution.py:37
  638.2 6.5 fusion.15
  646.1 11.6 %collective-permute-start.33 = (bf16[128,2304]{1,0:T(8,128)(2,1)}, bf16[128,2304]{1,0:T(8,128)(2,1)}, u32[]{:S(2)}, u32[]{:S(2)}) collective-permute-start(bf16[128,2304]{1,0:T(8,128)(2,1)} %get-tuple-element.74), channel_id=1, source_target_pairs={{0,1},{1,2},{2,3},{3,0},{4,5},{5,6},{6,7},{7,4},{8,9},{9,10},{10,1... | collective-permute-start | bytes 1769480 | tf_op jit(solution)/shard_map/ppermute | solution.py:57
  663.9 10.9 %collective-permute-done.33 = bf16[128,2304]{1,0:T(8,128)(2,1)} collective-permute-done((bf16[128,2304]{1,0:T(8,128)(2,1)}, bf16[128,2304]{1,0:T(8,128)(2,1)}, u32[]{:S(2)}, u32[]{:S(2)}) %collective-permute-start.33) | collective-permute-done | bytes 589856 | tf_op jit(solution)/shard_map/ppermute | solution.py:57
  674.9 15.4 %collective-permute-start.39 = (f32[4,2304]{1,0:T(4,128)S(1)}, f32[4,2304]{1,0:T(4,128)}, u32[]{:S(2)}, u32[]{:S(2)}) collective-permute-start(f32[4,2304]{1,0:T(4,128)S(1)} %concatenate.82), channel_id=1, source_target_pairs={{0,3},{1,0},{2,1},{3,2},{4,7},{5,4},{6,5},{7,6},{8,11},{9,8},{10,9... | collective-permute-start | bytes 110600 | tf_op jit(solution)/shard_map/ppermute | solution.py:57
  690.3 23.5 %collective-permute-done.31 = bf16[128,2304]{1,0:T(8,128)(2,1)} collective-permute-done((bf16[128,2304]{1,0:T(8,128)(2,1)}, bf16[128,2304]{1,0:T(8,128)(2,1)}, u32[]{:S(2)}, u32[]{:S(2)}) %collective-permute-start.31) | collective-permute-done | bytes 589856 | tf_op jit(solution)/shard_map/ppermute | solution.py:57
  727.3 5.1 concatenate.76
  741.8 9.0 %collective-permute-done.34 = bf16[128,2304]{1,0:T(8,128)(2,1)S(1)} collective-permute-done((bf16[128,2304]{1,0:T(8,128)(2,1)}, bf16[128,2304]{1,0:T(8,128)(2,1)S(1)}, u32[]{:S(2)}, u32[]{:S(2)}) %collective-permute-start.34) | collective-permute-done | bytes 589856 | tf_op jit(solution)/shard_map/ppermute | solution.py:57
  750.8 24.2 %collective-permute-done.35 = bf16[128,2304]{1,0:T(8,128)(2,1)S(1)} collective-permute-done((bf16[128,2304]{1,0:T(8,128)(2,1)}, bf16[128,2304]{1,0:T(8,128)(2,1)S(1)}, u32[]{:S(2)}, u32[]{:S(2)}) %collective-permute-start.35) | collective-permute-done | bytes 589856 | tf_op jit(solution)/shard_map/ppermute | solution.py:57
  782.6 64.2 %reduce-scatter.6.cloned.1.call-done = bf16[288,4608]{1,0:T(8,128)(2,1)} async-done(((bf16[1152,4608]{1,0:T(8,128)(2,1)}), bf16[288,4608]{1,0:T(8,128)(2,1)}) %reduce-scatter.6.cloned.1.call-update) | async-done | bytes 2654224 | tf_op jit(solution)/shard_map/reduce_scatter | solution.py:234
  846.8 4.5 slice_convert_fusion
  (343 shorter events, 203.4 us)
Async XLA Ops:
  7.2 54.7 %all-gather.3.cloned.1.call-start = ((), (), s32[]{:S(2)}) async-start(), calls=%async_computation.3 | async-start | bytes 7962624 | tf_op jit(solution)/shard_map/all_gather | solution.py:185
  9.5 275.4 %all-gather.5.cloned.1.call-start = ((), (), s32[]{:S(2)}) async-start(), calls=%async_computation.4 | async-start | bytes 35831808 | tf_op jit(solution)/shard_map/all_gather | solution.py:185
  13.0 398.0 %all-reduce.4.cloned.1.call-start = ((), (), s32[]{:S(2)}) async-start(), calls=%async_computation.5 | async-start | bytes 4718592 | tf_op jit(solution)/shard_map/psum | solution.py:337
  68.4 18.3 %collective-permute-start = (bf16[384,512]{1,0:T(8,128)(2,1)}, bf16[384,512]{1,0:T(8,128)(2,1)}, u32[]{:S(2)}, u32[]{:S(2)}) collective-permute-start(bf16[384,512]{1,0:T(8,128)(2,1)} %slice.274), channel_id=1, source_target_pairs={{0,4},{1,5},{2,6},{3,7},{8,12},{9,13},{10,14},{11,15},{16,20},{17,... | collective-permute-start | bytes 1179656 | tf_op jit(solution)/shard_map/ppermute | solution.py:21
  98.4 13.8 %collective-permute-start.1 = (bf16[128,2304]{1,0:T(8,128)(2,1)S(1)}, bf16[128,2304]{1,0:T(8,128)(2,1)}, u32[]{:S(2)}, u32[]{:S(2)}) collective-permute-start(bf16[128,2304]{1,0:T(8,128)(2,1)S(1)} %get-tuple-element.49), channel_id=1, source_target_pairs={{0,1},{4,5},{8,9},{12,13},{16,17},{20,21},{24,25},{28,29}} | collective-permute-start | bytes 1769480 | tf_op jit(solution)/shard_map/ppermute | solution.py:45
  113.9 14.3 %collective-permute-start.3 = (bf16[128,2304]{1,0:T(8,128)(2,1)S(1)}, bf16[128,2304]{1,0:T(8,128)(2,1)S(1)}, u32[]{:S(2)}, u32[]{:S(2)}) collective-permute-start(bf16[128,2304]{1,0:T(8,128)(2,1)S(1)} %get-tuple-element.51), channel_id=1, source_target_pairs={{0,1},{1,2},{4,5},{5,6},{8,9},{9,10},{12,13},{13,14},{16,17},{17,1... | collective-permute-start | bytes 1769480 | tf_op jit(solution)/shard_map/ppermute | solution.py:45
  118.4 10.7 %collective-permute-start.4 = (bf16[128,2304]{1,0:T(8,128)(2,1)S(1)}, bf16[128,2304]{1,0:T(8,128)(2,1)S(1)}, u32[]{:S(2)}, u32[]{:S(2)}) collective-permute-start(bf16[128,2304]{1,0:T(8,128)(2,1)S(1)} %get-tuple-element.52), channel_id=1, source_target_pairs={{2,1},{3,2},{6,5},{7,6},{10,9},{11,10},{14,13},{15,14},{18,17},{19... | collective-permute-start | bytes 1769480 | tf_op jit(solution)/shard_map/ppermute | solution.py:45
  130.1 15.3 %collective-permute-start.6 = (bf16[128,2304]{1,0:T(8,128)(2,1)}, bf16[128,2304]{1,0:T(8,128)(2,1)S(1)}, u32[]{:S(2)}, u32[]{:S(2)}) collective-permute-start(bf16[128,2304]{1,0:T(8,128)(2,1)} %add_convert_fusion.2), channel_id=1, source_target_pairs={{1,0},{2,1},{3,2},{5,4},{6,5},{7,6},{9,8},{10,9},{11,10},{13,12},{... | collective-permute-start | bytes 1769480 | tf_op jit(solution)/shard_map/ppermute | solution.py:45
  131.4 15.3 %collective-permute-start.5 = (bf16[128,2304]{1,0:T(8,128)(2,1)}, bf16[128,2304]{1,0:T(8,128)(2,1)S(1)}, u32[]{:S(2)}, u32[]{:S(2)}) collective-permute-start(bf16[128,2304]{1,0:T(8,128)(2,1)} %add_convert_fusion.3), channel_id=1, source_target_pairs={{0,1},{1,2},{2,3},{4,5},{5,6},{6,7},{8,9},{9,10},{10,11},{12,13},{... | collective-permute-start | bytes 1769480 | tf_op jit(solution)/shard_map/ppermute | solution.py:45
  151.6 40.4 %collective-permute-start.7 = (bf16[128,2304]{1,0:T(8,128)(2,1)S(1)}, bf16[128,2304]{1,0:T(8,128)(2,1)S(1)}, u32[]{:S(2)}, u32[]{:S(2)}) collective-permute-start(bf16[128,2304]{1,0:T(8,128)(2,1)S(1)} %get-tuple-element.103), channel_id=1, source_target_pairs={{0,1},{1,2},{2,3},{4,5},{5,6},{6,7},{8,9},{9,10},{10,11},{12,13},{... | collective-permute-start | bytes 1769480 | tf_op jit(solution)/shard_map/ppermute | solution.py:45
  155.9 36.1 %collective-permute-start.8 = (bf16[128,2304]{1,0:T(8,128)(2,1)S(1)}, bf16[128,2304]{1,0:T(8,128)(2,1)S(1)}, u32[]{:S(2)}, u32[]{:S(2)}) collective-permute-start(bf16[128,2304]{1,0:T(8,128)(2,1)S(1)} %get-tuple-element.103), channel_id=1, source_target_pairs={{1,0},{2,1},{3,2},{5,4},{6,5},{7,6},{9,8},{10,9},{11,10},{13,12},{... | collective-permute-start | bytes 1769480 | tf_op jit(solution)/shard_map/ppermute | solution.py:45
  157.3 24.0 %collective-permute-start.16 = (bf16[288,512]{1,0:T(8,128)(2,1)S(1)}, bf16[288,512]{1,0:T(8,128)(2,1)S(1)}, u32[]{:S(2)}, u32[]{:S(2)}) collective-permute-start(bf16[288,512]{1,0:T(8,128)(2,1)S(1)} %copy-done.32), channel_id=1, source_target_pairs={{0,1},{1,2},{2,3},{3,0},{4,5},{5,6},{6,7},{7,4},{8,9},{9,10},{10,1... | collective-permute-start | bytes 884744 | tf_op jit(solution)/shard_map/ppermute | solution.py:57
  160.1 31.2 %collective-permute-start.17 = (bf16[288,512]{1,0:T(8,128)(2,1)S(1)}, bf16[288,512]{1,0:T(8,128)(2,1)S(1)}, u32[]{:S(2)}, u32[]{:S(2)}) collective-permute-start(bf16[288,512]{1,0:T(8,128)(2,1)S(1)} %copy-done.32), channel_id=1, source_target_pairs={{0,2},{1,3},{2,0},{3,1},{4,6},{5,7},{6,4},{7,5},{8,10},{9,11},{10,... | collective-permute-start | bytes 884744 | tf_op jit(solution)/shard_map/ppermute | solution.py:57
  161.6 33.3 %collective-permute-start.18 = (bf16[288,512]{1,0:T(8,128)(2,1)S(1)}, bf16[288,512]{1,0:T(8,128)(2,1)S(1)}, u32[]{:S(2)}, u32[]{:S(2)}) collective-permute-start(bf16[288,512]{1,0:T(8,128)(2,1)S(1)} %copy-done.32), channel_id=1, source_target_pairs={{0,3},{1,0},{2,1},{3,2},{4,7},{5,4},{6,5},{7,6},{8,11},{9,8},{10,9... | collective-permute-start | bytes 884744 | tf_op jit(solution)/shard_map/ppermute | solution.py:57
  193.6 15.0 %collective-permute-start.10 = (bf16[128,2304]{1,0:T(8,128)(2,1)S(1)}, bf16[128,2304]{1,0:T(8,128)(2,1)}, u32[]{:S(2)}, u32[]{:S(2)}) collective-permute-start(bf16[128,2304]{1,0:T(8,128)(2,1)S(1)} %collective-permute-done.8), channel_id=1, source_target_pairs={{1,0},{2,1},{5,4},{6,5},{9,8},{10,9},{13,12},{14,13},{17,16},{18,1... | collective-permute-start | bytes 1769480 | tf_op jit(solution)/shard_map/ppermute | solution.py:45
  195.7 53.1 %collective-permute-start.19 = (bf16[288,2048]{1,0:T(8,128)(2,1)}, bf16[288,2048]{1,0:T(8,128)(2,1)}, u32[]{:S(2)}, u32[]{:S(2)}) collective-permute-start(bf16[288,2048]{1,0:T(8,128)(2,1)} %constant_dynamic-update-slice_fusion), channel_id=1, source_target_pairs={{0,20},{4,16},{8,28},{12,24},{16,4},{20,0},{24,12},{28,8},{1,21},{... | collective-permute-start | bytes 3538952 | tf_op jit(solution)/shard_map/ppermute | solution.py:197
  197.2 70.8 %collective-permute-start.20 = (bf16[288,2048]{1,0:T(8,128)(2,1)}, bf16[288,2048]{1,0:T(8,128)(2,1)}, u32[]{:S(2)}, u32[]{:S(2)}) collective-permute-start(bf16[288,2048]{1,0:T(8,128)(2,1)} %constant_dynamic-update-slice_fusion), channel_id=1, source_target_pairs={{0,4},{4,0},{8,12},{12,8},{16,20},{20,16},{24,28},{28,24},{1,5},{5... | collective-permute-start | bytes 3538952 | tf_op jit(solution)/shard_map/ppermute | solution.py:197
  198.2 69.8 %collective-permute-start.21 = (bf16[288,2048]{1,0:T(8,128)(2,1)}, bf16[288,2048]{1,0:T(8,128)(2,1)}, u32[]{:S(2)}, u32[]{:S(2)}) collective-permute-start(bf16[288,2048]{1,0:T(8,128)(2,1)} %constant_dynamic-update-slice_fusion), channel_id=1, source_target_pairs={{0,16},{4,20},{8,24},{12,28},{16,0},{20,4},{24,8},{28,12},{1,17},{... | collective-permute-start | bytes 3538952 | tf_op jit(solution)/shard_map/ppermute | solution.py:197
  208.6 59.9 %collective-permute-start.11 = (bf16[128,2304]{1,0:T(8,128)(2,1)}, bf16[128,2304]{1,0:T(8,128)(2,1)}, u32[]{:S(2)}, u32[]{:S(2)}) collective-permute-start(bf16[128,2304]{1,0:T(8,128)(2,1)} %collective-permute-done.9), channel_id=1, source_target_pairs={{2,3},{6,7},{10,11},{14,15},{18,19},{22,23},{26,27},{30,31}} | collective-permute-start | bytes 1769480 | tf_op jit(solution)/shard_map/ppermute | solution.py:45
  210.0 58.5 %collective-permute-start.12 = (bf16[128,2304]{1,0:T(8,128)(2,1)}, bf16[128,2304]{1,0:T(8,128)(2,1)}, u32[]{:S(2)}, u32[]{:S(2)}) collective-permute-start(bf16[128,2304]{1,0:T(8,128)(2,1)} %collective-permute-done.10), channel_id=1, source_target_pairs={{1,0},{5,4},{9,8},{13,12},{17,16},{21,20},{25,24},{29,28}} | collective-permute-start | bytes 1769480 | tf_op jit(solution)/shard_map/ppermute | solution.py:45
  248.8 75.2 %collective-permute-start.22 = (bf16[288,2048]{1,0:T(8,128)(2,1)}, bf16[288,2048]{1,0:T(8,128)(2,1)}, u32[]{:S(2)}, u32[]{:S(2)}) collective-permute-start(bf16[288,2048]{1,0:T(8,128)(2,1)} %constant_dynamic-update-slice_fusion), channel_id=1, source_target_pairs={{0,8},{4,12},{8,0},{12,4},{16,24},{20,28},{24,16},{28,20},{1,9},{5... | collective-permute-start | bytes 3538952 | tf_op jit(solution)/shard_map/ppermute | solution.py:197
  268.0 58.5 %collective-permute-start.23 = (bf16[288,2048]{1,0:T(8,128)(2,1)}, bf16[288,2048]{1,0:T(8,128)(2,1)}, u32[]{:S(2)}, u32[]{:S(2)}) collective-permute-start(bf16[288,2048]{1,0:T(8,128)(2,1)} %collective-permute-done.20), channel_id=1, source_target_pairs={{0,8},{4,12},{8,0},{12,4},{16,24},{20,28},{24,16},{28,20},{1,9},{5... | collective-permute-start | bytes 3538952 | tf_op jit(solution)/shard_map/ppermute | solution.py:197
  268.0 198.4 %collective-permute-start.24 = (bf16[288,2048]{1,0:T(8,128)(2,1)}, bf16[288,2048]{1,0:T(8,128)(2,1)}, u32[]{:S(2)}, u32[]{:S(2)}) collective-permute-start(bf16[288,2048]{1,0:T(8,128)(2,1)} %collective-permute-done.21), channel_id=1, source_target_pairs={{0,8},{4,12},{8,0},{12,4},{16,24},{20,28},{24,16},{28,20},{1,9},{5... | collective-permute-start | bytes 3538952 | tf_op jit(solution)/shard_map/ppermute | solution.py:197
  268.5 200.3 %collective-permute-start.25 = (bf16[288,2048]{1,0:T(8,128)(2,1)}, bf16[288,2048]{1,0:T(8,128)(2,1)}, u32[]{:S(2)}, u32[]{:S(2)}) collective-permute-start(bf16[288,2048]{1,0:T(8,128)(2,1)} %collective-permute-done.19), channel_id=1, source_target_pairs={{0,8},{4,12},{8,0},{12,4},{16,24},{20,28},{24,16},{28,20},{1,9},{5... | collective-permute-start | bytes 3538952 | tf_op jit(solution)/shard_map/ppermute | solution.py:197
  316.2 459.0 %reduce-scatter.4.cloned.1.call-start = ((), (), s32[]{:S(2)}) async-start(), calls=%async_computation.6 | async-start | bytes 4423680 | tf_op jit(solution)/shard_map/reduce_scatter | solution.py:234
  462.5 18.1 %collective-permute-start.15 = (bf16[128,2304]{1,0:T(8,128)(2,1)S(1)}, bf16[128,2304]{1,0:T(8,128)(2,1)S(1)}, u32[]{:S(2)}, u32[]{:S(2)}) collective-permute-start(bf16[128,2304]{1,0:T(8,128)(2,1)S(1)} %get-tuple-element.65), channel_id=1, source_target_pairs={{0,1},{1,2},{2,3},{3,0},{4,5},{5,6},{6,7},{7,4},{8,9},{9,10},{10,1... | collective-permute-start | bytes 1769480 | tf_op jit(solution)/shard_map/ppermute | solution.py:57
  462.8 27.4 %collective-permute-start.14 = (bf16[128,2304]{1,0:T(8,128)(2,1)S(1)}, bf16[128,2304]{1,0:T(8,128)(2,1)S(1)}, u32[]{:S(2)}, u32[]{:S(2)}) collective-permute-start(bf16[128,2304]{1,0:T(8,128)(2,1)S(1)} %get-tuple-element.64), channel_id=1, source_target_pairs={{0,3},{1,0},{2,1},{3,2},{4,7},{5,4},{6,5},{7,6},{8,11},{9,8},{10,9... | collective-permute-start | bytes 1769480 | tf_op jit(solution)/shard_map/ppermute | solution.py:57
  466.4 50.2 %collective-permute-start.13 = (bf16[128,2304]{1,0:T(8,128)(2,1)S(1)}, bf16[128,2304]{1,0:T(8,128)(2,1)S(1)}, u32[]{:S(2)}, u32[]{:S(2)}) collective-permute-start(bf16[128,2304]{1,0:T(8,128)(2,1)S(1)} %get-tuple-element.63), channel_id=1, source_target_pairs={{0,2},{1,3},{2,0},{3,1},{4,6},{5,7},{6,4},{7,5},{8,10},{9,11},{10,... | collective-permute-start | bytes 1769480 | tf_op jit(solution)/shard_map/ppermute | solution.py:57
  521.1 53.5 %collective-permute-start.44 = (bf16[128,2304]{1,0:T(8,128)(2,1)S(1)}, bf16[128,2304]{1,0:T(8,128)(2,1)S(1)}, u32[]{:S(2)}, u32[]{:S(2)}) collective-permute-start(bf16[128,2304]{1,0:T(8,128)(2,1)S(1)} %fusion.69), channel_id=1, source_target_pairs={{0,1},{1,2},{2,3},{3,0},{4,5},{5,6},{6,7},{7,4},{8,9},{9,10},{10,1... | collective-permute-start | bytes 1769480 | tf_op jit(solution)/shard_map/ppermute | solution.py:57
  526.5 19.8 %collective-permute-start.26 = (bf16[128,512]{1,0:T(8,128)(2,1)S(1)}, bf16[128,512]{1,0:T(8,128)(2,1)S(1)}, u32[]{:S(2)}, u32[]{:S(2)}) collective-permute-start(bf16[128,512]{1,0:T(8,128)(2,1)S(1)} %get-tuple-element.67), channel_id=1, source_target_pairs={{0,2},{1,3},{2,0},{3,1},{4,6},{5,7},{6,4},{7,5},{8,10},{9,11},{10,... | collective-permute-start | bytes 393224 | tf_op jit(solution)/shard_map/ppermute | solution.py:57
  528.3 18.0 %collective-permute-start.27 = (bf16[128,512]{1,0:T(8,128)(2,1)S(1)}, bf16[128,512]{1,0:T(8,128)(2,1)S(1)}, u32[]{:S(2)}, u32[]{:S(2)}) collective-permute-start(bf16[128,512]{1,0:T(8,128)(2,1)S(1)} %get-tuple-element.68), channel_id=1, source_target_pairs={{0,3},{1,0},{2,1},{3,2},{4,7},{5,4},{6,5},{7,6},{8,11},{9,8},{10,9... | collective-permute-start | bytes 393224 | tf_op jit(solution)/shard_map/ppermute | solution.py:57
  530.4 15.9 %collective-permute-start.28 = (bf16[128,512]{1,0:T(8,128)(2,1)S(1)}, bf16[128,512]{1,0:T(8,128)(2,1)S(1)}, u32[]{:S(2)}, u32[]{:S(2)}) collective-permute-start(bf16[128,512]{1,0:T(8,128)(2,1)S(1)} %get-tuple-element.69), channel_id=1, source_target_pairs={{0,1},{1,2},{2,3},{3,0},{4,5},{5,6},{6,7},{7,4},{8,9},{9,10},{10,1... | collective-permute-start | bytes 393224 | tf_op jit(solution)/shard_map/ppermute | solution.py:57
  546.4 29.9 %collective-permute-start.45 = (bf16[128,2304]{1,0:T(8,128)(2,1)S(1)}, bf16[128,2304]{1,0:T(8,128)(2,1)}, u32[]{:S(2)}, u32[]{:S(2)}) collective-permute-start(bf16[128,2304]{1,0:T(8,128)(2,1)S(1)} %fusion.69), channel_id=1, source_target_pairs={{0,2},{1,3},{2,0},{3,1},{4,6},{5,7},{6,4},{7,5},{8,10},{9,11},{10,... | collective-permute-start | bytes 1769480 | tf_op jit(solution)/shard_map/ppermute | solution.py:57
  548.7 28.7 %collective-permute-start.46 = (bf16[128,2304]{1,0:T(8,128)(2,1)S(1)}, bf16[128,2304]{1,0:T(8,128)(2,1)}, u32[]{:S(2)}, u32[]{:S(2)}) collective-permute-start(bf16[128,2304]{1,0:T(8,128)(2,1)S(1)} %fusion.69), channel_id=1, source_target_pairs={{0,3},{1,0},{2,1},{3,2},{4,7},{5,4},{6,5},{7,6},{8,11},{9,8},{10,9... | collective-permute-start | bytes 1769480 | tf_op jit(solution)/shard_map/ppermute | solution.py:57
  574.5 13.1 %collective-permute-start.43 = (bf16[1152,1024]{1,0:T(8,128)(2,1)}, bf16[1152,1024]{1,0:T(8,128)(2,1)}, u32[]{:S(2)}, u32[]{:S(2)}) collective-permute-start(bf16[1152,1024]{1,0:T(8,128)(2,1)} %convolution_convert_fusion.4), channel_id=1, source_target_pairs={{0,8},{8,0},{16,24},{24,16},{1,9},{9,1},{17,25},{25,17},{2,10},{10... | collective-permute-start | bytes 7077896 | tf_op jit(solution)/shard_map/ppermute | solution.py:225
  593.0 186.7 %reduce-scatter.8.cloned.1.call-start = ((), (), s32[]{:S(2)}) async-start(), calls=%async_computation.8 | async-start | bytes 11943936 | tf_op jit(solution)/shard_map/reduce_scatter | solution.py:241
  593.5 253.2 %reduce-scatter.6.cloned.1.call-start = ((), (), s32[]{:S(2)}) async-start(), calls=%async_computation.7 | async-start | bytes 13271040 | tf_op jit(solution)/shard_map/reduce_scatter | solution.py:234
  604.9 16.7 %collective-permute-start.48 = (bf16[1152,4608]{1,0:T(8,128)(2,1)}, bf16[1152,4608]{1,0:T(8,128)(2,1)}, u32[]{:S(2)}, u32[]{:S(2)}) collective-permute-start(bf16[1152,4608]{1,0:T(8,128)(2,1)} %convolution_convert_fusion), channel_id=1, source_target_pairs={{0,8},{8,0},{16,24},{24,16},{1,9},{9,1},{17,25},{25,17},{2,10},{10... | collective-permute-start | bytes 31850504 | tf_op jit(solution)/shard_map/ppermute | solution.py:225
  646.1 28.7 %collective-permute-start.33 = (bf16[128,2304]{1,0:T(8,128)(2,1)}, bf16[128,2304]{1,0:T(8,128)(2,1)}, u32[]{:S(2)}, u32[]{:S(2)}) collective-permute-start(bf16[128,2304]{1,0:T(8,128)(2,1)} %get-tuple-element.74), channel_id=1, source_target_pairs={{0,1},{1,2},{2,3},{3,0},{4,5},{5,6},{6,7},{7,4},{8,9},{9,10},{10,1... | collective-permute-start | bytes 1769480 | tf_op jit(solution)/shard_map/ppermute | solution.py:57
  657.7 32.6 %collective-permute-start.32 = (bf16[128,2304]{1,0:T(8,128)(2,1)}, bf16[128,2304]{1,0:T(8,128)(2,1)}, u32[]{:S(2)}, u32[]{:S(2)}) collective-permute-start(bf16[128,2304]{1,0:T(8,128)(2,1)} %get-tuple-element.73), channel_id=1, source_target_pairs={{0,3},{1,0},{2,1},{3,2},{4,7},{5,4},{6,5},{7,6},{8,11},{9,8},{10,9... | collective-permute-start | bytes 1769480 | tf_op jit(solution)/shard_map/ppermute | solution.py:57
  660.3 53.5 %collective-permute-start.31 = (bf16[128,2304]{1,0:T(8,128)(2,1)}, bf16[128,2304]{1,0:T(8,128)(2,1)}, u32[]{:S(2)}, u32[]{:S(2)}) collective-permute-start(bf16[128,2304]{1,0:T(8,128)(2,1)} %get-tuple-element.72), channel_id=1, source_target_pairs={{0,2},{1,3},{2,0},{3,1},{4,6},{5,7},{6,4},{7,5},{8,10},{9,11},{10,... | collective-permute-start | bytes 1769480 | tf_op jit(solution)/shard_map/ppermute | solution.py:57
  661.4 59.9 %collective-permute-start.37 = (f32[4,2304]{1,0:T(4,128)S(1)}, f32[4,2304]{1,0:T(4,128)S(1)}, u32[]{:S(2)}, u32[]{:S(2)}) collective-permute-start(f32[4,2304]{1,0:T(4,128)S(1)} %concatenate.82), channel_id=1, source_target_pairs={{0,1},{1,2},{2,3},{3,0},{4,5},{5,6},{6,7},{7,4},{8,9},{9,10},{10,1... | collective-permute-start | bytes 110600 | tf_op jit(solution)/shard_map/ppermute | solution.py:57
  663.5 57.8 %collective-permute-start.38 = (f32[4,2304]{1,0:T(4,128)S(1)}, f32[4,2304]{1,0:T(4,128)}, u32[]{:S(2)}, u32[]{:S(2)}) collective-permute-start(f32[4,2304]{1,0:T(4,128)S(1)} %concatenate.82), channel_id=1, source_target_pairs={{0,2},{1,3},{2,0},{3,1},{4,6},{5,7},{6,4},{7,5},{8,10},{9,11},{10,... | collective-permute-start | bytes 110600 | tf_op jit(solution)/shard_map/ppermute | solution.py:57
  674.9 46.4 %collective-permute-start.39 = (f32[4,2304]{1,0:T(4,128)S(1)}, f32[4,2304]{1,0:T(4,128)}, u32[]{:S(2)}, u32[]{:S(2)}) collective-permute-start(f32[4,2304]{1,0:T(4,128)S(1)} %concatenate.82), channel_id=1, source_target_pairs={{0,3},{1,0},{2,1},{3,2},{4,7},{5,4},{6,5},{7,6},{8,11},{9,8},{10,9... | collective-permute-start | bytes 110600 | tf_op jit(solution)/shard_map/ppermute | solution.py:57
  724.0 12.3 %collective-permute-start.41 = (f32[4,2304]{1,0:T(4,128)}, f32[4,2304]{1,0:T(4,128)}, u32[]{:S(2)}, u32[]{:S(2)}) collective-permute-start(f32[4,2304]{1,0:T(4,128)} %add.436), channel_id=1, source_target_pairs={{0,16},{8,24},{16,0},{24,8},{1,17},{9,25},{17,1},{25,9},{2,18},{10... | collective-permute-start | bytes 110600 | tf_op jit(solution)/shard_map/ppermute | solution.py:145
  732.5 18.3 %collective-permute-start.34 = (bf16[128,2304]{1,0:T(8,128)(2,1)}, bf16[128,2304]{1,0:T(8,128)(2,1)S(1)}, u32[]{:S(2)}, u32[]{:S(2)}) collective-permute-start(bf16[128,2304]{1,0:T(8,128)(2,1)} %concatenate.81), channel_id=1, source_target_pairs={{0,1},{1,2},{2,3},{3,0},{4,5},{5,6},{6,7},{7,4},{8,9},{9,10},{10,1... | collective-permute-start | bytes 1769480 | tf_op jit(solution)/shard_map/ppermute | solution.py:57
  732.5 42.5 %collective-permute-start.35 = (bf16[128,2304]{1,0:T(8,128)(2,1)}, bf16[128,2304]{1,0:T(8,128)(2,1)S(1)}, u32[]{:S(2)}, u32[]{:S(2)}) collective-permute-start(bf16[128,2304]{1,0:T(8,128)(2,1)} %concatenate.81), channel_id=1, source_target_pairs={{0,2},{1,3},{2,0},{3,1},{4,6},{5,7},{6,4},{7,5},{8,10},{9,11},{10,... | collective-permute-start | bytes 1769480 | tf_op jit(solution)/shard_map/ppermute | solution.py:57
  733.3 41.7 %collective-permute-start.36 = (bf16[128,2304]{1,0:T(8,128)(2,1)}, bf16[128,2304]{1,0:T(8,128)(2,1)S(1)}, u32[]{:S(2)}, u32[]{:S(2)}) collective-permute-start(bf16[128,2304]{1,0:T(8,128)(2,1)} %concatenate.81), channel_id=1, source_target_pairs={{0,3},{1,0},{2,1},{3,2},{4,7},{5,4},{6,5},{7,6},{8,11},{9,8},{10,9... | collective-permute-start | bytes 1769480 | tf_op jit(solution)/shard_map/ppermute | solution.py:57
  (75 other events, 1033.5 us)
Sparse Core Ops, SparseCore 0:
  10.5 51.4 all-gather.2
  63.8 209.5 all-gather.4
  316.3 94.6 all-reduce.3
  593.1 59.3 reduce-scatter.3
  655.8 83.3 reduce-scatter.7
  742.2 104.5 reduce-scatter.5

commit v16 on v14

--- a/solution.py
+++ b/solution.py
@@ -349,8 +349,12 @@
     _, pull_glu = jax.vjp(geglu, gate_value, up_value)
     grad_gate, grad_up = pull_glu(product(grad_two_low, down_full))
     grad_gate_up = jnp.concatenate([grad_gate.astype(LOW), grad_up.astype(LOW)], axis=1)
-    grad_normed_two = transposed_product(grad_gate_up, gate_up_full).astype(LOW)
-    grad_normed_two = sent_scattered(ordered_blocks(grad_normed_two))
+    half = (gate_up_full.shape[0] // 256 + 1) // 2 * 256
+    first_half = transposed_product(grad_gate_up, gate_up_full[:half]).astype(LOW)
+    first_half = sent_scattered(ordered_blocks(first_half))
+    second_half = transposed_product(grad_gate_up, gate_up_full[half:]).astype(LOW)
+    second_half = sent_scattered(ordered_blocks(second_half))
+    grad_normed_two = jnp.concatenate([first_half, second_half], axis=1)
     outputs = by_chip((middle_all + rms(branch_two, post_feedforward_gain)).astype(LOW))
     gate_up_sent = sent_to_core(normed_two, grad_gate_up)
     gate_up_arrived = over_cores(gate_up_sent)

time: 869 us -> 863 us (level)
  waiting for transfers between devices: 448 us -> 422 us
    ppermute x21 -> x24, waiting for transfers between devices: 155 us -> 114 us  [shift(): lax.ppermute(block, 'tp', [(i, (i + distance) % size) for i in range(size)])]
    ppermute x7, waiting for transfers between devices: 35.3 us -> 49 us  [sent(): return lax.ppermute(block, ROWS, [(r, r ^ bits) for r in range(ranks)])]
    dot_general x4 -> x5, matrix products: 37 us -> 41.7 us  [transposed_product(): lax.dot_general(left, right, (((1,), (1,)), ((), ())), preferred_element_...]
    ppermute x21 -> x24, starting transfers between devices: 57.6 us -> 62.3 us  [shift(): lax.ppermute(block, 'tp', [(i, (i + distance) % size) for i in range(size)])]
    unnamed x139 -> x123, local copies, waits for them, and re-layouts: 16 us -> 17.8 us
  transfers between devices with their start and end apart: 55 -> 58, of which waited for: 27 -> 23; matrix products, arithmetic and copies ran while one was open for 31% -> 32% of each run, Pallas kernels for 0% -> 0%
where the time goes in v16:
time: 863 us; the launch traced here: 852 us
  waiting for transfers between devices  422 us (49%)
  matrix products  139 us (16%)
  starting transfers between devices  110 us (13%)
  local copies, waits for them, and re-layouts  90.1 us (10%)
  other arithmetic  74 us (9%)
  between operations  15.7 us (2%)
    ppermute x24, waiting for transfers between devices, shift(): lax.ppermute(block, 'tp', [(i, (i + distance) % size) for i in range(size)])  114 us
    psum x1, waiting for transfers between devices, shards(): lax.psum(transposed_product(hidden_low, down_full).astype(LOW), 'tp')  82 us
    reduce_scatter x2, waiting for transfers between devices, share_rows(): lax.psum_scatter(grad, ROWS, scatter_dimension=0, tiled=True, axis_index_...  64.2 us
    ppermute x24, starting transfers between devices, shift(): lax.ppermute(block, 'tp', [(i, (i + distance) % size) for i in range(size)])  62.3 us
    ppermute x7, waiting for transfers between devices, sent(): return lax.ppermute(block, ROWS, [(r, r ^ bits) for r in range(ranks)])  49 us
    dot_general x7, matrix products, rows_product(): lax.dot_general(left, right, (((0,), (0,)), ((), ())), preferred_element_...  42.8 us
    dot_general x5, matrix products, transposed_product(): lax.dot_general(left, right, (((1,), (1,)), ((), ())), preferred_element_...  41.7 us
    dot_general x4, matrix products, product(): return jnp.dot(left, right, preferred_element_type=F32)  40.2 us
  transfers between devices with their start and end apart: 58, of which 23 were waited for; matrix products, arithmetic and copies ran while one was open for 32% of the time, Pallas kernels for 0%

profile of v16, /device:TPU:0, one launch (start us, length us, event | category | flops | bytes accessed | tf_op | source)
XLA Modules:
  0.0 851.6 jit_solution(15946696554791769859)
XLA Ops:
  16.4 4.2 concatenate.65
  23.6 38.3 %all-gather.3.cloned.1.call-done = bf16[2304,1536]{1,0:T(8,128)(2,1)} async-done(((bf16[288,1536]{1,0:T(8,128)(2,1)}), bf16[2304,1536]{1,0:T(8,128)(2,1)}) %all-gather.3.cloned.1.call-update) | async-done | bytes 7077904 | tf_op jit(solution)/shard_map/all_gather | solution.py:185
  61.9 5.7 fusion.58
  68.4 4.1 collective-permute-start
  75.2 11.4 %collective-permute-done = bf16[384,512]{1,0:T(8,128)(2,1)} collective-permute-done((bf16[384,512]{1,0:T(8,128)(2,1)}, bf16[384,512]{1,0:T(8,128)(2,1)}, u32[]{:S(2)}, u32[]{:S(2)}) %collective-permute-start) | collective-permute-done | bytes 393248 | tf_op jit(solution)/shard_map/ppermute | solution.py:21
  98.4 4.0 collective-permute-start.1
  102.4 9.8 %collective-permute-done.1 = bf16[128,2304]{1,0:T(8,128)(2,1)} collective-permute-done((bf16[128,2304]{1,0:T(8,128)(2,1)S(1)}, bf16[128,2304]{1,0:T(8,128)(2,1)}, u32[]{:S(2)}, u32[]{:S(2)}) %collective-permute-start.1) | collective-permute-done | bytes 589856 | tf_op jit(solution)/shard_map/ppermute | solution.py:45
  113.9 4.5 collective-permute-start.3
  119.1 9.1 %collective-permute-done.3 = bf16[128,2304]{1,0:T(8,128)(2,1)S(1)} collective-permute-done((bf16[128,2304]{1,0:T(8,128)(2,1)S(1)}, bf16[128,2304]{1,0:T(8,128)(2,1)S(1)}, u32[]{:S(2)}, u32[]{:S(2)}) %collective-permute-start.3) | collective-permute-done | bytes 589856 | tf_op jit(solution)/shard_map/ppermute | solution.py:45
  131.4 6.0 collective-permute-start.5
  141.9 16.9 %collective-permute-done.6 = bf16[128,2304]{1,0:T(8,128)(2,1)S(1)} collective-permute-done((bf16[128,2304]{1,0:T(8,128)(2,1)}, bf16[128,2304]{1,0:T(8,128)(2,1)S(1)}, u32[]{:S(2)}, u32[]{:S(2)}) %collective-permute-start.6) | collective-permute-done | bytes 589856 | tf_op jit(solution)/shard_map/ppermute | solution.py:45
  164.7 8.5 collective-permute-start.7
  178.5 5.2 concatenate.80
  195.3 5.3 concatenate.75
  209.3 4.7 broadcast_in_dim.149
  216.5 27.8 %collective-permute-done.22 = bf16[288,2048]{1,0:T(8,128)(2,1)} collective-permute-done((bf16[288,2048]{1,0:T(8,128)(2,1)}, bf16[288,2048]{1,0:T(8,128)(2,1)}, u32[]{:S(2)}, u32[]{:S(2)}) %collective-permute-start.22) | collective-permute-done | bytes 1179680 | tf_op jit(solution)/shard_map/ppermute | solution.py:197
  246.7 21.3 %collective-permute-done.23 = bf16[288,2048]{1,0:T(8,128)(2,1)} collective-permute-done((bf16[288,2048]{1,0:T(8,128)(2,1)}, bf16[288,2048]{1,0:T(8,128)(2,1)}, u32[]{:S(2)}, u32[]{:S(2)}) %collective-permute-start.23) | collective-permute-done | bytes 1179680 | tf_op jit(solution)/shard_map/ppermute | solution.py:197
  279.0 5.9 multiply_convert_fusion.2
  284.9 15.2 %fusion = f32[512,4608]{1,0:T(8,128)S(1)} fusion(bf16[512,2304]{1,0:T(8,128)(2,1)} %get-tuple-element.107, bf16[2304,6912]{1,0:T(8,128)(2,1)} %all-gather.5.cloned.1.call-done), kind=kOutput, calls=%fused_computation | convolution fusion | flops 10871635968 | bytes 33030144 | tf_op jit(solution)/shard_map/dot_general | solution.py:33
  305.1 11.0 %fusion.31 = bf16[512,2304]{1,0:T(8,128)(2,1)} fusion(bf16[512,2304]{1,0:T(8,128)(2,1)S(1)} %multiply_convert_fusion.1, bf16[2304,6912]{1,0:T(8,128)(2,1)} %all-gather.5.cloned.1.call-done), kind=kOutput, calls=%fused_computation.54 | convolution fusion | flops 5436997632 | bytes 15335424 | tf_op jit(solution)/shard_map/dot_general | solution.py:41
  329.1 82.0 %all-reduce.4.cloned.1.call-done = bf16[512,2304]{1,0:T(8,128)(2,1)} async-done(((bf16[512,2304]{1,0:T(8,128)(2,1)}), bf16[512,2304]{1,0:T(8,128)(2,1)}) %all-reduce.4.cloned.1.call-update) | async-done | bytes 2359312 | tf_op jit(solution)/shard_map/psum | solution.py:337
  416.9 5.1 fusion.27
  423.4 8.3 convolution_convert_fusion.1
  431.7 14.2 %fusion.25 = (bf16[512,2304]{1,0:T(8,128)(2,1)S(1)}, bf16[512,2304]{1,0:T(8,128)(2,1)S(1)}) fusion(f32[512,4608]{1,0:T(8,128)} %copy-done.9, bf16[512,2304]{1,0:T(8,128)(2,1)} %copy-done.25, bf16[2304,6912]{1,0:T(8,128)(2,1)} %all-gather.5.cloned.1.call-done), kind=kOutput, calls=%fused_computation.40 | convolution fusion | flops 5464129536 | bytes 27131904 | tf_op jit(solution)/shard_map/dot_general | solution.py:33
  446.0 10.4 %fusion.55 = bf16[512,1024]{1,0:T(8,128)(2,1)S(1)} fusion(bf16[2304,6912]{1,0:T(8,128)(2,1)} %all-gather.5.cloned.1.call-done, bf16[512,2304]{1,0:T(8,128)(2,1)S(1)} %get-tuple-element.115, bf16[512,2304]{1,0:T(8,128)(2,1)S(1)} %get-tuple-element.114), kind=kOutput, calls=%fused_computation.96 | convolution fusion | flops 4841799680 | bytes 15204352 | tf_op jit(solution)/shard_map/dot_general | solution.py:41
  456.8 3.6 collective-permute-start.17
  460.4 10.6 %fusion.40 = bf16[512,1280]{1,0:T(8,128)(2,1)S(1)} fusion(bf16[2304,6912]{1,0:T(8,128)(2,1)} %all-gather.5.cloned.1.call-done, bf16[512,2304]{1,0:T(8,128)(2,1)S(1)} %get-tuple-element.115, bf16[512,2304]{1,0:T(8,128)(2,1)S(1)} %get-tuple-element.114), kind=kOutput, calls=%fused_computation.73 | convolution fusion | flops 6049890304 | bytes 17825792 | tf_op jit(solution)/shard_map/dot_general | solution.py:41
  475.0 3.5 collective-permute-start.13
  480.9 9.4 %collective-permute-done.16 = bf16[128,1024]{1,0:T(8,128)(2,1)S(1)} collective-permute-done((bf16[128,1024]{1,0:T(8,128)(2,1)S(1)}, bf16[128,1024]{1,0:T(8,128)(2,1)S(1)}, u32[]{:S(2)}, u32[]{:S(2)}) %collective-permute-start.16) | collective-permute-done | bytes 262176 | tf_op jit(solution)/shard_map/ppermute | solution.py:57
  492.9 17.7 %collective-permute-done.13 = bf16[128,1280]{1,0:T(8,128)(2,1)S(1)} collective-permute-done((bf16[128,1280]{1,0:T(8,128)(2,1)S(1)}, bf16[128,1280]{1,0:T(8,128)(2,1)S(1)}, u32[]{:S(2)}, u32[]{:S(2)}) %collective-permute-start.13) | collective-permute-done | bytes 327712 | tf_op jit(solution)/shard_map/ppermute | solution.py:57
  514.4 5.1 convolution_convert_fusion.6
  524.1 15.3 %collective-permute-done.29 = bf16[128,512]{1,0:T(8,128)(2,1)S(1)} collective-permute-done((bf16[128,512]{1,0:T(8,128)(2,1)S(1)}, bf16[128,512]{1,0:T(8,128)(2,1)S(1)}, u32[]{:S(2)}, u32[]{:S(2)}) %collective-permute-start.29) | collective-permute-done | bytes 131104 | tf_op jit(solution)/shard_map/ppermute | solution.py:57
  541.8 3.4 collective-permute-start.49
  546.2 3.9 fusion.61
  559.8 4.8 collective-permute-done.32
  587.7 10.3 %convolution_convert_fusion = bf16[1152,4608]{1,0:T(8,128)(2,1)} fusion(bf16[512,2304]{1,0:T(8,128)(2,1)S(1)} %copy-done.22, s32[]{:T(128)S(6)} %select_n.281, bf16[512,2304]{1,0:T(8,128)(2,1)} %copy-done.59, bf16[512,2304]{1,0:T(8,128)(2,1)} %copy-done.58), kind=kOutput, calls=%fused_computation.3 | convolution fusion | flops 5450563584 | bytes 16515076 | tf_op jit(solution)/shard_map/dot_general | solution.py:37
  598.1 16.5 %collective-permute-done.51 = bf16[1152,4608]{1,0:T(8,128)(2,1)} collective-permute-done((bf16[1152,4608]{1,0:T(8,128)(2,1)}, bf16[1152,4608]{1,0:T(8,128)(2,1)}, u32[]{:S(2)}, u32[]{:S(2)}) %collective-permute-start.51) | collective-permute-done | bytes 10616864 | tf_op jit(solution)/shard_map/ppermute | solution.py:225
  614.7 13.6 %add_convert_fusion = bf16[1152,4608]{1,0:T(8,128)(2,1)} fusion(bf16[1152,4608]{1,0:T(8,128)(2,1)} %collective-permute-done.51, bf16[512,2304]{1,0:T(8,128)(2,1)S(1)} %copy-done.22, s32[]{:T(128)S(6)} %select_n.280, bf16[512,2304]{1,0:T(8,128)(2,1)} %copy-done.59, bf16[512,2304]{1,0:T(8,128)(2,1)} %copy-done.58), kind=kOutput, calls=%fused_computation.2 | convolution fusion | flops 5461180416 | bytes 27131908 | tf_op jit(solution)/shard_map/dot_general | solution.py:37
  631.3 6.5 fusion.17
  639.2 11.6 %collective-permute-start.36 = (bf16[128,2304]{1,0:T(8,128)(2,1)}, bf16[128,2304]{1,0:T(8,128)(2,1)}, u32[]{:S(2)}, u32[]{:S(2)}) collective-permute-start(bf16[128,2304]{1,0:T(8,128)(2,1)} %get-tuple-element.82), channel_id=1, source_target_pairs={{0,1},{1,2},{2,3},{3,0},{4,5},{5,6},{6,7},{7,4},{8,9},{9,10},{10,1... | collective-permute-start | bytes 1769480 | tf_op jit(solution)/shard_map/ppermute | solution.py:57
  657.0 10.9 %collective-permute-done.36 = bf16[128,2304]{1,0:T(8,128)(2,1)} collective-permute-done((bf16[128,2304]{1,0:T(8,128)(2,1)}, bf16[128,2304]{1,0:T(8,128)(2,1)}, u32[]{:S(2)}, u32[]{:S(2)}) %collective-permute-start.36) | collective-permute-done | bytes 589856 | tf_op jit(solution)/shard_map/ppermute | solution.py:57
  667.9 15.4 %collective-permute-start.42 = (f32[4,2304]{1,0:T(4,128)S(1)}, f32[4,2304]{1,0:T(4,128)}, u32[]{:S(2)}, u32[]{:S(2)}) collective-permute-start(f32[4,2304]{1,0:T(4,128)S(1)} %concatenate.86), channel_id=1, source_target_pairs={{0,3},{1,0},{2,1},{3,2},{4,7},{5,4},{6,5},{7,6},{8,11},{9,8},{10,9... | collective-permute-start | bytes 110600 | tf_op jit(solution)/shard_map/ppermute | solution.py:57
  683.3 23.5 %collective-permute-done.34 = bf16[128,2304]{1,0:T(8,128)(2,1)} collective-permute-done((bf16[128,2304]{1,0:T(8,128)(2,1)}, bf16[128,2304]{1,0:T(8,128)(2,1)}, u32[]{:S(2)}, u32[]{:S(2)}) %collective-permute-start.34) | collective-permute-done | bytes 589856 | tf_op jit(solution)/shard_map/ppermute | solution.py:57
  720.4 5.1 concatenate.79
  734.9 9.0 %collective-permute-done.37 = bf16[128,2304]{1,0:T(8,128)(2,1)S(1)} collective-permute-done((bf16[128,2304]{1,0:T(8,128)(2,1)}, bf16[128,2304]{1,0:T(8,128)(2,1)S(1)}, u32[]{:S(2)}, u32[]{:S(2)}) %collective-permute-start.37) | collective-permute-done | bytes 589856 | tf_op jit(solution)/shard_map/ppermute | solution.py:57
  743.9 24.2 %collective-permute-done.38 = bf16[128,2304]{1,0:T(8,128)(2,1)S(1)} collective-permute-done((bf16[128,2304]{1,0:T(8,128)(2,1)}, bf16[128,2304]{1,0:T(8,128)(2,1)S(1)}, u32[]{:S(2)}, u32[]{:S(2)}) %collective-permute-start.38) | collective-permute-done | bytes 589856 | tf_op jit(solution)/shard_map/ppermute | solution.py:57
  775.7 64.2 %reduce-scatter.6.cloned.1.call-done = bf16[288,4608]{1,0:T(8,128)(2,1)} async-done(((bf16[1152,4608]{1,0:T(8,128)(2,1)}), bf16[288,4608]{1,0:T(8,128)(2,1)}) %reduce-scatter.6.cloned.1.call-update) | async-done | bytes 2654224 | tf_op jit(solution)/shard_map/reduce_scatter | solution.py:234
  839.8 4.5 slice_convert_fusion
  (337 shorter events, 204.3 us)
Async XLA Ops:
  7.2 54.7 %all-gather.3.cloned.1.call-start = ((), (), s32[]{:S(2)}) async-start(), calls=%async_computation.3 | async-start | bytes 7962624 | tf_op jit(solution)/shard_map/all_gather | solution.py:185
  9.5 275.4 %all-gather.5.cloned.1.call-start = ((), (), s32[]{:S(2)}) async-start(), calls=%async_computation.4 | async-start | bytes 35831808 | tf_op jit(solution)/shard_map/all_gather | solution.py:185
  12.9 398.2 %all-reduce.4.cloned.1.call-start = ((), (), s32[]{:S(2)}) async-start(), calls=%async_computation.5 | async-start | bytes 4718592 | tf_op jit(solution)/shard_map/psum | solution.py:337
  68.4 18.3 %collective-permute-start = (bf16[384,512]{1,0:T(8,128)(2,1)}, bf16[384,512]{1,0:T(8,128)(2,1)}, u32[]{:S(2)}, u32[]{:S(2)}) collective-permute-start(bf16[384,512]{1,0:T(8,128)(2,1)} %slice.284), channel_id=1, source_target_pairs={{0,4},{1,5},{2,6},{3,7},{8,12},{9,13},{10,14},{11,15},{16,20},{17,... | collective-permute-start | bytes 1179656 | tf_op jit(solution)/shard_map/ppermute | solution.py:21
  113.9 14.3 %collective-permute-start.3 = (bf16[128,2304]{1,0:T(8,128)(2,1)S(1)}, bf16[128,2304]{1,0:T(8,128)(2,1)S(1)}, u32[]{:S(2)}, u32[]{:S(2)}) collective-permute-start(bf16[128,2304]{1,0:T(8,128)(2,1)S(1)} %get-tuple-element.55), channel_id=1, source_target_pairs={{0,1},{1,2},{4,5},{5,6},{8,9},{9,10},{12,13},{13,14},{16,17},{17,1... | collective-permute-start | bytes 1769480 | tf_op jit(solution)/shard_map/ppermute | solution.py:45
  130.1 28.7 %collective-permute-start.6 = (bf16[128,2304]{1,0:T(8,128)(2,1)}, bf16[128,2304]{1,0:T(8,128)(2,1)S(1)}, u32[]{:S(2)}, u32[]{:S(2)}) collective-permute-start(bf16[128,2304]{1,0:T(8,128)(2,1)} %add_convert_fusion.2), channel_id=1, source_target_pairs={{1,0},{2,1},{3,2},{5,4},{6,5},{7,6},{9,8},{10,9},{11,10},{13,12},{... | collective-permute-start | bytes 1769480 | tf_op jit(solution)/shard_map/ppermute | solution.py:45
  131.4 27.4 %collective-permute-start.5 = (bf16[128,2304]{1,0:T(8,128)(2,1)}, bf16[128,2304]{1,0:T(8,128)(2,1)S(1)}, u32[]{:S(2)}, u32[]{:S(2)}) collective-permute-start(bf16[128,2304]{1,0:T(8,128)(2,1)} %add_convert_fusion.3), channel_id=1, source_target_pairs={{0,1},{1,2},{2,3},{4,5},{5,6},{6,7},{8,9},{9,10},{10,11},{12,13},{... | collective-permute-start | bytes 1769480 | tf_op jit(solution)/shard_map/ppermute | solution.py:45
  137.4 46.3 %collective-permute-start.19 = (bf16[288,512]{1,0:T(8,128)(2,1)}, bf16[288,512]{1,0:T(8,128)(2,1)}, u32[]{:S(2)}, u32[]{:S(2)}) collective-permute-start(bf16[288,512]{1,0:T(8,128)(2,1)} %param.24), channel_id=1, source_target_pairs={{0,1},{1,2},{2,3},{3,0},{4,5},{5,6},{6,7},{7,4},{8,9},{9,10},{10,1... | collective-permute-start | bytes 884744 | tf_op jit(solution)/shard_map/ppermute | solution.py:57
  139.4 46.0 %collective-permute-start.20 = (bf16[288,512]{1,0:T(8,128)(2,1)}, bf16[288,512]{1,0:T(8,128)(2,1)}, u32[]{:S(2)}, u32[]{:S(2)}) collective-permute-start(bf16[288,512]{1,0:T(8,128)(2,1)} %param.24), channel_id=1, source_target_pairs={{0,2},{1,3},{2,0},{3,1},{4,6},{5,7},{6,4},{7,5},{8,10},{9,11},{10,... | collective-permute-start | bytes 884744 | tf_op jit(solution)/shard_map/ppermute | solution.py:57
  139.4 47.8 %collective-permute-start.21 = (bf16[288,512]{1,0:T(8,128)(2,1)}, bf16[288,512]{1,0:T(8,128)(2,1)}, u32[]{:S(2)}, u32[]{:S(2)}) collective-permute-start(bf16[288,512]{1,0:T(8,128)(2,1)} %param.24), channel_id=1, source_target_pairs={{0,3},{1,0},{2,1},{3,2},{4,7},{5,4},{6,5},{7,6},{8,11},{9,8},{10,9... | collective-permute-start | bytes 884744 | tf_op jit(solution)/shard_map/ppermute | solution.py:57
  164.7 25.8 %collective-permute-start.7 = (bf16[128,2304]{1,0:T(8,128)(2,1)}, bf16[128,2304]{1,0:T(8,128)(2,1)}, u32[]{:S(2)}, u32[]{:S(2)}) collective-permute-start(bf16[128,2304]{1,0:T(8,128)(2,1)} %get-tuple-element.110), channel_id=1, source_target_pairs={{0,1},{1,2},{2,3},{4,5},{5,6},{6,7},{8,9},{9,10},{10,11},{12,13},{... | collective-permute-start | bytes 1769480 | tf_op jit(solution)/shard_map/ppermute | solution.py:45
  173.2 17.3 %collective-permute-start.8 = (bf16[128,2304]{1,0:T(8,128)(2,1)}, bf16[128,2304]{1,0:T(8,128)(2,1)}, u32[]{:S(2)}, u32[]{:S(2)}) collective-permute-start(bf16[128,2304]{1,0:T(8,128)(2,1)} %get-tuple-element.110), channel_id=1, source_target_pairs={{1,0},{2,1},{3,2},{5,4},{6,5},{7,6},{9,8},{10,9},{11,10},{13,12},{... | collective-permute-start | bytes 1769480 | tf_op jit(solution)/shard_map/ppermute | solution.py:45
  189.0 55.3 %collective-permute-start.22 = (bf16[288,2048]{1,0:T(8,128)(2,1)}, bf16[288,2048]{1,0:T(8,128)(2,1)}, u32[]{:S(2)}, u32[]{:S(2)}) collective-permute-start(bf16[288,2048]{1,0:T(8,128)(2,1)} %constant_dynamic-update-slice_fusion), channel_id=1, source_target_pairs={{0,20},{4,16},{8,28},{12,24},{16,4},{20,0},{24,12},{28,8},{1,21},{... | collective-permute-start | bytes 3538952 | tf_op jit(solution)/shard_map/ppermute | solution.py:197
  190.5 16.8 %collective-permute-start.9 = (bf16[128,2304]{1,0:T(8,128)(2,1)}, bf16[128,2304]{1,0:T(8,128)(2,1)}, u32[]{:S(2)}, u32[]{:S(2)}) collective-permute-start(bf16[128,2304]{1,0:T(8,128)(2,1)} %collective-permute-done.7), channel_id=1, source_target_pairs={{1,2},{2,3},{5,6},{6,7},{9,10},{10,11},{13,14},{14,15},{17,18},{18... | collective-permute-start | bytes 1769480 | tf_op jit(solution)/shard_map/ppermute | solution.py:45
  192.0 15.4 %collective-permute-start.10 = (bf16[128,2304]{1,0:T(8,128)(2,1)}, bf16[128,2304]{1,0:T(8,128)(2,1)}, u32[]{:S(2)}, u32[]{:S(2)}) collective-permute-start(bf16[128,2304]{1,0:T(8,128)(2,1)} %collective-permute-done.8), channel_id=1, source_target_pairs={{1,0},{2,1},{5,4},{6,5},{9,8},{10,9},{13,12},{14,13},{17,16},{18,1... | collective-permute-start | bytes 1769480 | tf_op jit(solution)/shard_map/ppermute | solution.py:45
  202.1 65.9 %collective-permute-start.23 = (bf16[288,2048]{1,0:T(8,128)(2,1)}, bf16[288,2048]{1,0:T(8,128)(2,1)}, u32[]{:S(2)}, u32[]{:S(2)}) collective-permute-start(bf16[288,2048]{1,0:T(8,128)(2,1)} %constant_dynamic-update-slice_fusion), channel_id=1, source_target_pairs={{0,4},{4,0},{8,12},{12,8},{16,20},{20,16},{24,28},{28,24},{1,5},{5... | collective-permute-start | bytes 3538952 | tf_op jit(solution)/shard_map/ppermute | solution.py:197
  203.1 64.9 %collective-permute-start.24 = (bf16[288,2048]{1,0:T(8,128)(2,1)}, bf16[288,2048]{1,0:T(8,128)(2,1)}, u32[]{:S(2)}, u32[]{:S(2)}) collective-permute-start(bf16[288,2048]{1,0:T(8,128)(2,1)} %constant_dynamic-update-slice_fusion), channel_id=1, source_target_pairs={{0,16},{4,20},{8,24},{12,28},{16,0},{20,4},{24,8},{28,12},{1,17},{... | collective-permute-start | bytes 3538952 | tf_op jit(solution)/shard_map/ppermute | solution.py:197
  207.3 61.2 %collective-permute-start.11 = (bf16[128,2304]{1,0:T(8,128)(2,1)}, bf16[128,2304]{1,0:T(8,128)(2,1)S(1)}, u32[]{:S(2)}, u32[]{:S(2)}) collective-permute-start(bf16[128,2304]{1,0:T(8,128)(2,1)} %collective-permute-done.9), channel_id=1, source_target_pairs={{2,3},{6,7},{10,11},{14,15},{18,19},{22,23},{26,27},{30,31}} | collective-permute-start | bytes 1769480 | tf_op jit(solution)/shard_map/ppermute | solution.py:45
  208.0 60.5 %collective-permute-start.12 = (bf16[128,2304]{1,0:T(8,128)(2,1)}, bf16[128,2304]{1,0:T(8,128)(2,1)S(1)}, u32[]{:S(2)}, u32[]{:S(2)}) collective-permute-start(bf16[128,2304]{1,0:T(8,128)(2,1)} %collective-permute-done.10), channel_id=1, source_target_pairs={{1,0},{5,4},{9,8},{13,12},{17,16},{21,20},{25,24},{29,28}} | collective-permute-start | bytes 1769480 | tf_op jit(solution)/shard_map/ppermute | solution.py:45
  244.3 77.1 %collective-permute-start.25 = (bf16[288,2048]{1,0:T(8,128)(2,1)}, bf16[288,2048]{1,0:T(8,128)(2,1)}, u32[]{:S(2)}, u32[]{:S(2)}) collective-permute-start(bf16[288,2048]{1,0:T(8,128)(2,1)} %constant_dynamic-update-slice_fusion), channel_id=1, source_target_pairs={{0,8},{4,12},{8,0},{12,4},{16,24},{20,28},{24,16},{28,20},{1,9},{5... | collective-permute-start | bytes 3538952 | tf_op jit(solution)/shard_map/ppermute | solution.py:197
  268.0 203.7 %collective-permute-start.28 = (bf16[288,2048]{1,0:T(8,128)(2,1)}, bf16[288,2048]{1,0:T(8,128)(2,1)}, u32[]{:S(2)}, u32[]{:S(2)}) collective-permute-start(bf16[288,2048]{1,0:T(8,128)(2,1)} %collective-permute-done.22), channel_id=1, source_target_pairs={{0,8},{4,12},{8,0},{12,4},{16,24},{20,28},{24,16},{28,20},{1,9},{5... | collective-permute-start | bytes 3538952 | tf_op jit(solution)/shard_map/ppermute | solution.py:197
  268.0 56.1 %collective-permute-start.26 = (bf16[288,2048]{1,0:T(8,128)(2,1)}, bf16[288,2048]{1,0:T(8,128)(2,1)}, u32[]{:S(2)}, u32[]{:S(2)}) collective-permute-start(bf16[288,2048]{1,0:T(8,128)(2,1)} %collective-permute-done.23), channel_id=1, source_target_pairs={{0,8},{4,12},{8,0},{12,4},{16,24},{20,28},{24,16},{28,20},{1,9},{5... | collective-permute-start | bytes 3538952 | tf_op jit(solution)/shard_map/ppermute | solution.py:197
  268.5 58.0 %collective-permute-start.27 = (bf16[288,2048]{1,0:T(8,128)(2,1)}, bf16[288,2048]{1,0:T(8,128)(2,1)}, u32[]{:S(2)}, u32[]{:S(2)}) collective-permute-start(bf16[288,2048]{1,0:T(8,128)(2,1)} %collective-permute-done.24), channel_id=1, source_target_pairs={{0,8},{4,12},{8,0},{12,4},{16,24},{20,28},{24,16},{28,20},{1,9},{5... | collective-permute-start | bytes 3538952 | tf_op jit(solution)/shard_map/ppermute | solution.py:197
  316.1 452.1 %reduce-scatter.4.cloned.1.call-start = ((), (), s32[]{:S(2)}) async-start(), calls=%async_computation.6 | async-start | bytes 4423680 | tf_op jit(solution)/shard_map/reduce_scatter | solution.py:234
  456.5 18.4 %collective-permute-start.18 = (bf16[128,1024]{1,0:T(8,128)(2,1)S(1)}, bf16[128,1024]{1,0:T(8,128)(2,1)S(1)}, u32[]{:S(2)}, u32[]{:S(2)}) collective-permute-start(bf16[128,1024]{1,0:T(8,128)(2,1)S(1)} %get-tuple-element.73), channel_id=1, source_target_pairs={{0,1},{1,2},{2,3},{3,0},{4,5},{5,6},{6,7},{7,4},{8,9},{9,10},{10,1... | collective-permute-start | bytes 786440 | tf_op jit(solution)/shard_map/ppermute | solution.py:57
  456.8 24.1 %collective-permute-start.17 = (bf16[128,1024]{1,0:T(8,128)(2,1)S(1)}, bf16[128,1024]{1,0:T(8,128)(2,1)S(1)}, u32[]{:S(2)}, u32[]{:S(2)}) collective-permute-start(bf16[128,1024]{1,0:T(8,128)(2,1)S(1)} %get-tuple-element.72), channel_id=1, source_target_pairs={{0,3},{1,0},{2,1},{3,2},{4,7},{5,4},{6,5},{7,6},{8,11},{9,8},{10,9... | collective-permute-start | bytes 786440 | tf_op jit(solution)/shard_map/ppermute | solution.py:57
  460.4 29.9 %collective-permute-start.16 = (bf16[128,1024]{1,0:T(8,128)(2,1)S(1)}, bf16[128,1024]{1,0:T(8,128)(2,1)S(1)}, u32[]{:S(2)}, u32[]{:S(2)}) collective-permute-start(bf16[128,1024]{1,0:T(8,128)(2,1)S(1)} %get-tuple-element.71), channel_id=1, source_target_pairs={{0,2},{1,3},{2,0},{3,1},{4,6},{5,7},{6,4},{7,5},{8,10},{9,11},{10,... | collective-permute-start | bytes 786440 | tf_op jit(solution)/shard_map/ppermute | solution.py:57
  471.1 19.4 %collective-permute-start.15 = (bf16[128,1280]{1,0:T(8,128)(2,1)S(1)}, bf16[128,1280]{1,0:T(8,128)(2,1)S(1)}, u32[]{:S(2)}, u32[]{:S(2)}) collective-permute-start(bf16[128,1280]{1,0:T(8,128)(2,1)S(1)} %get-tuple-element.69), channel_id=1, source_target_pairs={{0,1},{1,2},{2,3},{3,0},{4,5},{5,6},{6,7},{7,4},{8,9},{9,10},{10,1... | collective-permute-start | bytes 983048 | tf_op jit(solution)/shard_map/ppermute | solution.py:57
  471.7 21.2 %collective-permute-start.14 = (bf16[128,1280]{1,0:T(8,128)(2,1)S(1)}, bf16[128,1280]{1,0:T(8,128)(2,1)S(1)}, u32[]{:S(2)}, u32[]{:S(2)}) collective-permute-start(bf16[128,1280]{1,0:T(8,128)(2,1)S(1)} %get-tuple-element.68), channel_id=1, source_target_pairs={{0,3},{1,0},{2,1},{3,2},{4,7},{5,4},{6,5},{7,6},{8,11},{9,8},{10,9... | collective-permute-start | bytes 983048 | tf_op jit(solution)/shard_map/ppermute | solution.py:57
  475.0 35.7 %collective-permute-start.13 = (bf16[128,1280]{1,0:T(8,128)(2,1)S(1)}, bf16[128,1280]{1,0:T(8,128)(2,1)S(1)}, u32[]{:S(2)}, u32[]{:S(2)}) collective-permute-start(bf16[128,1280]{1,0:T(8,128)(2,1)S(1)} %get-tuple-element.67), channel_id=1, source_target_pairs={{0,2},{1,3},{2,0},{3,1},{4,6},{5,7},{6,4},{7,5},{8,10},{9,11},{10,... | collective-permute-start | bytes 983048 | tf_op jit(solution)/shard_map/ppermute | solution.py:57
  514.4 53.3 %collective-permute-start.47 = (bf16[128,2304]{1,0:T(8,128)(2,1)S(1)}, bf16[128,2304]{1,0:T(8,128)(2,1)S(1)}, u32[]{:S(2)}, u32[]{:S(2)}) collective-permute-start(bf16[128,2304]{1,0:T(8,128)(2,1)S(1)} %fusion.73), channel_id=1, source_target_pairs={{0,1},{1,2},{2,3},{3,0},{4,5},{5,6},{6,7},{7,4},{8,9},{9,10},{10,1... | collective-permute-start | bytes 1769480 | tf_op jit(solution)/shard_map/ppermute | solution.py:57
  519.6 19.8 %collective-permute-start.29 = (bf16[128,512]{1,0:T(8,128)(2,1)S(1)}, bf16[128,512]{1,0:T(8,128)(2,1)S(1)}, u32[]{:S(2)}, u32[]{:S(2)}) collective-permute-start(bf16[128,512]{1,0:T(8,128)(2,1)S(1)} %get-tuple-element.75), channel_id=1, source_target_pairs={{0,2},{1,3},{2,0},{3,1},{4,6},{5,7},{6,4},{7,5},{8,10},{9,11},{10,... | collective-permute-start | bytes 393224 | tf_op jit(solution)/shard_map/ppermute | solution.py:57
  521.4 18.0 %collective-permute-start.30 = (bf16[128,512]{1,0:T(8,128)(2,1)S(1)}, bf16[128,512]{1,0:T(8,128)(2,1)S(1)}, u32[]{:S(2)}, u32[]{:S(2)}) collective-permute-start(bf16[128,512]{1,0:T(8,128)(2,1)S(1)} %get-tuple-element.76), channel_id=1, source_target_pairs={{0,3},{1,0},{2,1},{3,2},{4,7},{5,4},{6,5},{7,6},{8,11},{9,8},{10,9... | collective-permute-start | bytes 393224 | tf_op jit(solution)/shard_map/ppermute | solution.py:57
  523.5 15.9 %collective-permute-start.31 = (bf16[128,512]{1,0:T(8,128)(2,1)S(1)}, bf16[128,512]{1,0:T(8,128)(2,1)S(1)}, u32[]{:S(2)}, u32[]{:S(2)}) collective-permute-start(bf16[128,512]{1,0:T(8,128)(2,1)S(1)} %get-tuple-element.77), channel_id=1, source_target_pairs={{0,1},{1,2},{2,3},{3,0},{4,5},{5,6},{6,7},{7,4},{8,9},{9,10},{10,1... | collective-permute-start | bytes 393224 | tf_op jit(solution)/shard_map/ppermute | solution.py:57
  539.5 29.9 %collective-permute-start.48 = (bf16[128,2304]{1,0:T(8,128)(2,1)S(1)}, bf16[128,2304]{1,0:T(8,128)(2,1)}, u32[]{:S(2)}, u32[]{:S(2)}) collective-permute-start(bf16[128,2304]{1,0:T(8,128)(2,1)S(1)} %fusion.73), channel_id=1, source_target_pairs={{0,2},{1,3},{2,0},{3,1},{4,6},{5,7},{6,4},{7,5},{8,10},{9,11},{10,... | collective-permute-start | bytes 1769480 | tf_op jit(solution)/shard_map/ppermute | solution.py:57
  541.8 28.7 %collective-permute-start.49 = (bf16[128,2304]{1,0:T(8,128)(2,1)S(1)}, bf16[128,2304]{1,0:T(8,128)(2,1)}, u32[]{:S(2)}, u32[]{:S(2)}) collective-permute-start(bf16[128,2304]{1,0:T(8,128)(2,1)S(1)} %fusion.73), channel_id=1, source_target_pairs={{0,3},{1,0},{2,1},{3,2},{4,7},{5,4},{6,5},{7,6},{8,11},{9,8},{10,9... | collective-permute-start | bytes 1769480 | tf_op jit(solution)/shard_map/ppermute | solution.py:57
  586.0 186.7 %reduce-scatter.8.cloned.1.call-start = ((), (), s32[]{:S(2)}) async-start(), calls=%async_computation.8 | async-start | bytes 11943936 | tf_op jit(solution)/shard_map/reduce_scatter | solution.py:241
  586.6 253.2 %reduce-scatter.6.cloned.1.call-start = ((), (), s32[]{:S(2)}) async-start(), calls=%async_computation.7 | async-start | bytes 13271040 | tf_op jit(solution)/shard_map/reduce_scatter | solution.py:234
  598.0 16.7 %collective-permute-start.51 = (bf16[1152,4608]{1,0:T(8,128)(2,1)}, bf16[1152,4608]{1,0:T(8,128)(2,1)}, u32[]{:S(2)}, u32[]{:S(2)}) collective-permute-start(bf16[1152,4608]{1,0:T(8,128)(2,1)} %convolution_convert_fusion), channel_id=1, source_target_pairs={{0,8},{8,0},{16,24},{24,16},{1,9},{9,1},{17,25},{25,17},{2,10},{10... | collective-permute-start | bytes 31850504 | tf_op jit(solution)/shard_map/ppermute | solution.py:225
  639.2 28.7 %collective-permute-start.36 = (bf16[128,2304]{1,0:T(8,128)(2,1)}, bf16[128,2304]{1,0:T(8,128)(2,1)}, u32[]{:S(2)}, u32[]{:S(2)}) collective-permute-start(bf16[128,2304]{1,0:T(8,128)(2,1)} %get-tuple-element.82), channel_id=1, source_target_pairs={{0,1},{1,2},{2,3},{3,0},{4,5},{5,6},{6,7},{7,4},{8,9},{9,10},{10,1... | collective-permute-start | bytes 1769480 | tf_op jit(solution)/shard_map/ppermute | solution.py:57
  650.8 32.6 %collective-permute-start.35 = (bf16[128,2304]{1,0:T(8,128)(2,1)}, bf16[128,2304]{1,0:T(8,128)(2,1)}, u32[]{:S(2)}, u32[]{:S(2)}) collective-permute-start(bf16[128,2304]{1,0:T(8,128)(2,1)} %get-tuple-element.81), channel_id=1, source_target_pairs={{0,3},{1,0},{2,1},{3,2},{4,7},{5,4},{6,5},{7,6},{8,11},{9,8},{10,9... | collective-permute-start | bytes 1769480 | tf_op jit(solution)/shard_map/ppermute | solution.py:57
  653.4 53.5 %collective-permute-start.34 = (bf16[128,2304]{1,0:T(8,128)(2,1)}, bf16[128,2304]{1,0:T(8,128)(2,1)}, u32[]{:S(2)}, u32[]{:S(2)}) collective-permute-start(bf16[128,2304]{1,0:T(8,128)(2,1)} %get-tuple-element.80), channel_id=1, source_target_pairs={{0,2},{1,3},{2,0},{3,1},{4,6},{5,7},{6,4},{7,5},{8,10},{9,11},{10,... | collective-permute-start | bytes 1769480 | tf_op jit(solution)/shard_map/ppermute | solution.py:57
  654.5 59.9 %collective-permute-start.40 = (f32[4,2304]{1,0:T(4,128)S(1)}, f32[4,2304]{1,0:T(4,128)S(1)}, u32[]{:S(2)}, u32[]{:S(2)}) collective-permute-start(f32[4,2304]{1,0:T(4,128)S(1)} %concatenate.86), channel_id=1, source_target_pairs={{0,1},{1,2},{2,3},{3,0},{4,5},{5,6},{6,7},{7,4},{8,9},{9,10},{10,1... | collective-permute-start | bytes 110600 | tf_op jit(solution)/shard_map/ppermute | solution.py:57
  656.6 57.8 %collective-permute-start.41 = (f32[4,2304]{1,0:T(4,128)S(1)}, f32[4,2304]{1,0:T(4,128)}, u32[]{:S(2)}, u32[]{:S(2)}) collective-permute-start(f32[4,2304]{1,0:T(4,128)S(1)} %concatenate.86), channel_id=1, source_target_pairs={{0,2},{1,3},{2,0},{3,1},{4,6},{5,7},{6,4},{7,5},{8,10},{9,11},{10,... | collective-permute-start | bytes 110600 | tf_op jit(solution)/shard_map/ppermute | solution.py:57
  667.9 46.4 %collective-permute-start.42 = (f32[4,2304]{1,0:T(4,128)S(1)}, f32[4,2304]{1,0:T(4,128)}, u32[]{:S(2)}, u32[]{:S(2)}) collective-permute-start(f32[4,2304]{1,0:T(4,128)S(1)} %concatenate.86), channel_id=1, source_target_pairs={{0,3},{1,0},{2,1},{3,2},{4,7},{5,4},{6,5},{7,6},{8,11},{9,8},{10,9... | collective-permute-start | bytes 110600 | tf_op jit(solution)/shard_map/ppermute | solution.py:57
  725.5 18.3 %collective-permute-start.37 = (bf16[128,2304]{1,0:T(8,128)(2,1)}, bf16[128,2304]{1,0:T(8,128)(2,1)S(1)}, u32[]{:S(2)}, u32[]{:S(2)}) collective-permute-start(bf16[128,2304]{1,0:T(8,128)(2,1)} %concatenate.85), channel_id=1, source_target_pairs={{0,1},{1,2},{2,3},{3,0},{4,5},{5,6},{6,7},{7,4},{8,9},{9,10},{10,1... | collective-permute-start | bytes 1769480 | tf_op jit(solution)/shard_map/ppermute | solution.py:57
  725.5 42.5 %collective-permute-start.38 = (bf16[128,2304]{1,0:T(8,128)(2,1)}, bf16[128,2304]{1,0:T(8,128)(2,1)S(1)}, u32[]{:S(2)}, u32[]{:S(2)}) collective-permute-start(bf16[128,2304]{1,0:T(8,128)(2,1)} %concatenate.85), channel_id=1, source_target_pairs={{0,2},{1,3},{2,0},{3,1},{4,6},{5,7},{6,4},{7,5},{8,10},{9,11},{10,... | collective-permute-start | bytes 1769480 | tf_op jit(solution)/shard_map/ppermute | solution.py:57
  726.3 41.7 %collective-permute-start.39 = (bf16[128,2304]{1,0:T(8,128)(2,1)}, bf16[128,2304]{1,0:T(8,128)(2,1)S(1)}, u32[]{:S(2)}, u32[]{:S(2)}) collective-permute-start(bf16[128,2304]{1,0:T(8,128)(2,1)} %concatenate.85), channel_id=1, source_target_pairs={{0,3},{1,0},{2,1},{3,2},{4,7},{5,4},{6,5},{7,6},{8,11},{9,8},{10,9... | collective-permute-start | bytes 1769480 | tf_op jit(solution)/shard_map/ppermute | solution.py:57
  (70 other events, 841.3 us)
Sparse Core Ops, SparseCore 0:
  10.5 51.4 all-gather.2
  63.8 209.7 all-gather.4
  316.2 94.8 all-reduce.3
  586.1 59.3 reduce-scatter.3
  648.9 83.4 reduce-scatter.7
  735.3 104.5 reduce-scatter.5

commit v17 on v16

--- a/solution.py
+++ b/solution.py
@@ -358,7 +358,10 @@
     outputs = by_chip((middle_all + rms(branch_two, post_feedforward_gain)).astype(LOW))
     gate_up_sent = sent_to_core(normed_two, grad_gate_up)
     gate_up_arrived = over_cores(gate_up_sent)
-    grad_gate_up_low = chip_rows(normed_two, grad_gate_up, gate_up_arrived)
+    own_rows = rows_of_core(normed_two, lax.axis_index("fsdp") % 2)
+    gate_up_own = rows_product(own_rows, grad_gate_up).astype(LOW)
+    gate_up_own = lax.optimization_barrier(gate_up_own)
+    grad_gate_up_low = (gate_up_own.astype(F32) + gate_up_arrived.astype(F32)).astype(LOW)
     gate_up_share = share_rows(grad_gate_up_low)
 
     _, pull_three = jax.vjp(rms, middle, pre_feedforward_gain)

time: 863 us -> 863 us (level)
  other arithmetic: 74 us -> 85.8 us
    convert_element_type x0 -> x1, other arithmetic: none -> 13.2 us  [shards(): (gate_up_own.astype(F32) + gate_up_arrived.astype(F32)).astype(LOW)]
    unnamed x123 -> x129, local copies, waits for them, and re-layouts: 17.8 us -> 17.8 us
  transfers between devices with their start and end apart: 58 -> 58, of which waited for: 23 -> 23; matrix products, arithmetic and copies ran while one was open for 32% -> 33% of each run, Pallas kernels for 0% -> 0%
where the time goes in v17:
time: 863 us; the launch traced here: 852 us
  waiting for transfers between devices  417 us (48%)
  matrix products  134 us (16%)
  starting transfers between devices  110 us (13%)
  local copies, waits for them, and re-layouts  89.2 us (10%)
  other arithmetic  85.8 us (10%)
  between operations  15.9 us (2%)
    ppermute x24, waiting for transfers between devices, shift(): lax.ppermute(block, 'tp', [(i, (i + distance) % size) for i in range(size)])  114 us
    psum x1, waiting for transfers between devices, shards(): lax.psum(transposed_product(hidden_low, down_full).astype(LOW), 'tp')  82.1 us
    reduce_scatter x2, waiting for transfers between devices, share_rows(): lax.psum_scatter(grad, ROWS, scatter_dimension=0, tiled=True, axis_index_...  66.9 us
    ppermute x24, starting transfers between devices, shift(): lax.ppermute(block, 'tp', [(i, (i + distance) % size) for i in range(size)])  61.7 us
    ppermute x7, waiting for transfers between devices, sent(): return lax.ppermute(block, ROWS, [(r, r ^ bits) for r in range(ranks)])  49 us
    dot_general x5, matrix products, transposed_product(): lax.dot_general(left, right, (((1,), (1,)), ((), ())), preferred_element_...  41.7 us
    dot_general x4, matrix products, product(): return jnp.dot(left, right, preferred_element_type=F32)  40.2 us
    all_gather x2, waiting for transfers between devices, gather_rows(): lax.all_gather(weight, ROWS, axis=0, tiled=True, axis_index_groups=[first...  38.4 us
  transfers between devices with their start and end apart: 58, of which 23 were waited for; matrix products, arithmetic and copies ran while one was open for 33% of the time, Pallas kernels for 0%

profile of v17, /device:TPU:0, one launch (start us, length us, event | category | flops | bytes accessed | tf_op | source)
XLA Modules:
  0.0 851.8 jit_solution(15710340761577283877)
XLA Ops:
  16.3 4.2 concatenate.65
  23.5 38.4 %all-gather.3.cloned.1.call-done = bf16[2304,1536]{1,0:T(8,128)(2,1)} async-done(((bf16[288,1536]{1,0:T(8,128)(2,1)}), bf16[2304,1536]{1,0:T(8,128)(2,1)}) %all-gather.3.cloned.1.call-update) | async-done | bytes 7077904 | tf_op jit(solution)/shard_map/all_gather | solution.py:185
  61.9 5.7 fusion.58
  68.4 4.1 collective-permute-start
  75.2 11.5 %collective-permute-done = bf16[384,512]{1,0:T(8,128)(2,1)} collective-permute-done((bf16[384,512]{1,0:T(8,128)(2,1)}, bf16[384,512]{1,0:T(8,128)(2,1)}, u32[]{:S(2)}, u32[]{:S(2)}) %collective-permute-start) | collective-permute-done | bytes 393248 | tf_op jit(solution)/shard_map/ppermute | solution.py:21
  98.4 4.0 collective-permute-start.1
  102.4 9.8 %collective-permute-done.1 = bf16[128,2304]{1,0:T(8,128)(2,1)} collective-permute-done((bf16[128,2304]{1,0:T(8,128)(2,1)S(1)}, bf16[128,2304]{1,0:T(8,128)(2,1)}, u32[]{:S(2)}, u32[]{:S(2)}) %collective-permute-start.1) | collective-permute-done | bytes 589856 | tf_op jit(solution)/shard_map/ppermute | solution.py:45
  113.9 4.5 collective-permute-start.3
  119.1 9.1 %collective-permute-done.3 = bf16[128,2304]{1,0:T(8,128)(2,1)S(1)} collective-permute-done((bf16[128,2304]{1,0:T(8,128)(2,1)S(1)}, bf16[128,2304]{1,0:T(8,128)(2,1)S(1)}, u32[]{:S(2)}, u32[]{:S(2)}) %collective-permute-start.3) | collective-permute-done | bytes 589856 | tf_op jit(solution)/shard_map/ppermute | solution.py:45
  131.4 6.0 collective-permute-start.5
  141.9 16.9 %collective-permute-done.6 = bf16[128,2304]{1,0:T(8,128)(2,1)S(1)} collective-permute-done((bf16[128,2304]{1,0:T(8,128)(2,1)}, bf16[128,2304]{1,0:T(8,128)(2,1)S(1)}, u32[]{:S(2)}, u32[]{:S(2)}) %collective-permute-start.6) | collective-permute-done | bytes 589856 | tf_op jit(solution)/shard_map/ppermute | solution.py:45
  164.8 8.5 collective-permute-start.7
  178.5 5.2 concatenate.80
  195.4 5.3 concatenate.75
  209.4 4.7 broadcast_in_dim.149
  216.5 27.7 %collective-permute-done.22 = bf16[288,2048]{1,0:T(8,128)(2,1)} collective-permute-done((bf16[288,2048]{1,0:T(8,128)(2,1)}, bf16[288,2048]{1,0:T(8,128)(2,1)}, u32[]{:S(2)}, u32[]{:S(2)}) %collective-permute-start.22) | collective-permute-done | bytes 1179680 | tf_op jit(solution)/shard_map/ppermute | solution.py:197
  246.7 21.3 %collective-permute-done.23 = bf16[288,2048]{1,0:T(8,128)(2,1)} collective-permute-done((bf16[288,2048]{1,0:T(8,128)(2,1)}, bf16[288,2048]{1,0:T(8,128)(2,1)}, u32[]{:S(2)}, u32[]{:S(2)}) %collective-permute-start.23) | collective-permute-done | bytes 1179680 | tf_op jit(solution)/shard_map/ppermute | solution.py:197
  279.0 5.9 multiply_convert_fusion.2
  284.9 15.2 %fusion = f32[512,4608]{1,0:T(8,128)S(1)} fusion(bf16[512,2304]{1,0:T(8,128)(2,1)} %get-tuple-element.107, bf16[2304,6912]{1,0:T(8,128)(2,1)} %all-gather.5.cloned.1.call-done), kind=kOutput, calls=%fused_computation | convolution fusion | flops 10871635968 | bytes 33030144 | tf_op jit(solution)/shard_map/dot_general | solution.py:33
  305.1 11.0 %fusion.31 = bf16[512,2304]{1,0:T(8,128)(2,1)} fusion(bf16[512,2304]{1,0:T(8,128)(2,1)S(1)} %multiply_convert_fusion.1, bf16[2304,6912]{1,0:T(8,128)(2,1)} %all-gather.5.cloned.1.call-done), kind=kOutput, calls=%fused_computation.55 | convolution fusion | flops 5436997632 | bytes 15335424 | tf_op jit(solution)/shard_map/dot_general | solution.py:41
  329.1 82.1 %all-reduce.4.cloned.1.call-done = bf16[512,2304]{1,0:T(8,128)(2,1)} async-done(((bf16[512,2304]{1,0:T(8,128)(2,1)}), bf16[512,2304]{1,0:T(8,128)(2,1)}) %all-reduce.4.cloned.1.call-update) | async-done | bytes 2359312 | tf_op jit(solution)/shard_map/psum | solution.py:337
  416.9 5.1 fusion.27
  423.5 8.3 convolution_convert_fusion.2
  431.8 14.2 %fusion.25 = (bf16[512,2304]{1,0:T(8,128)(2,1)S(1)}, bf16[512,2304]{1,0:T(8,128)(2,1)S(1)}) fusion(f32[512,4608]{1,0:T(8,128)} %copy-done.9, bf16[512,2304]{1,0:T(8,128)(2,1)} %copy-done.25, bf16[2304,6912]{1,0:T(8,128)(2,1)} %all-gather.5.cloned.1.call-done), kind=kOutput, calls=%fused_computation.41 | convolution fusion | flops 5464129536 | bytes 27131904 | tf_op jit(solution)/shard_map/dot_general | solution.py:33
  446.0 10.4 %fusion.55 = bf16[512,1024]{1,0:T(8,128)(2,1)S(1)} fusion(bf16[2304,6912]{1,0:T(8,128)(2,1)} %all-gather.5.cloned.1.call-done, bf16[512,2304]{1,0:T(8,128)(2,1)S(1)} %get-tuple-element.115, bf16[512,2304]{1,0:T(8,128)(2,1)S(1)} %get-tuple-element.114), kind=kOutput, calls=%fused_computation.97 | convolution fusion | flops 4841799680 | bytes 15204352 | tf_op jit(solution)/shard_map/dot_general | solution.py:41
  456.8 3.6 collective-permute-start.17
  460.4 10.6 %fusion.40 = bf16[512,1280]{1,0:T(8,128)(2,1)S(1)} fusion(bf16[2304,6912]{1,0:T(8,128)(2,1)} %all-gather.5.cloned.1.call-done, bf16[512,2304]{1,0:T(8,128)(2,1)S(1)} %get-tuple-element.115, bf16[512,2304]{1,0:T(8,128)(2,1)S(1)} %get-tuple-element.114), kind=kOutput, calls=%fused_computation.74 | convolution fusion | flops 6049890304 | bytes 17825792 | tf_op jit(solution)/shard_map/dot_general | solution.py:41
  475.0 3.5 collective-permute-start.13
  480.9 9.4 %collective-permute-done.16 = bf16[128,1024]{1,0:T(8,128)(2,1)S(1)} collective-permute-done((bf16[128,1024]{1,0:T(8,128)(2,1)S(1)}, bf16[128,1024]{1,0:T(8,128)(2,1)S(1)}, u32[]{:S(2)}, u32[]{:S(2)}) %collective-permute-start.16) | collective-permute-done | bytes 262176 | tf_op jit(solution)/shard_map/ppermute | solution.py:57
  492.9 17.7 %collective-permute-done.13 = bf16[128,1280]{1,0:T(8,128)(2,1)S(1)} collective-permute-done((bf16[128,1280]{1,0:T(8,128)(2,1)S(1)}, bf16[128,1280]{1,0:T(8,128)(2,1)S(1)}, u32[]{:S(2)}, u32[]{:S(2)}) %collective-permute-start.13) | collective-permute-done | bytes 327712 | tf_op jit(solution)/shard_map/ppermute | solution.py:57
  514.5 5.1 convolution_convert_fusion.7
  524.1 15.3 %collective-permute-done.29 = bf16[128,512]{1,0:T(8,128)(2,1)S(1)} collective-permute-done((bf16[128,512]{1,0:T(8,128)(2,1)S(1)}, bf16[128,512]{1,0:T(8,128)(2,1)S(1)}, u32[]{:S(2)}, u32[]{:S(2)}) %collective-permute-start.29) | collective-permute-done | bytes 131104 | tf_op jit(solution)/shard_map/ppermute | solution.py:57
  546.2 3.9 fusion.61
  560.1 4.5 collective-permute-done.32
  587.8 10.5 %convolution_convert_fusion = bf16[1152,4608]{1,0:T(8,128)(2,1)} fusion(bf16[512,2304]{1,0:T(8,128)(2,1)S(1)} %copy-done.22, s32[]{:T(128)S(6)} %select_n.281, bf16[512,2304]{1,0:T(8,128)(2,1)} %copy-done.61, bf16[512,2304]{1,0:T(8,128)(2,1)} %copy-done.59), kind=kOutput, calls=%fused_computation.3 | convolution fusion | flops 5450563584 | bytes 16515076 | tf_op jit(solution)/shard_map/dot_general | solution.py:37
  598.4 8.5 %convolution_convert_fusion.1 = bf16[1152,4608]{1,0:T(8,128)(2,1)} fusion(bf16[512,2304]{1,0:T(8,128)(2,1)S(1)} %copy-done.22, s32[]{:T(128)S(6)} %select_n.280, bf16[512,2304]{1,0:T(8,128)(2,1)S(1)} %copy-done.62, bf16[512,2304]{1,0:T(8,128)(2,1)S(1)} %copy-done.60), kind=kOutput, calls=%fused_computation.4 | convolution fusion | flops 5450563584 | bytes 16515076 | tf_op jit(solution)/shard_map/dot_general | solution.py:37
  606.9 8.0 collective-permute-done.51
  614.9 13.2 %add_convert_fusion = bf16[1152,4608]{1,0:T(8,128)(2,1)} fusion(bf16[1152,4608]{1,0:T(8,128)(2,1)} %collective-permute-done.51, bf16[1152,4608]{1,0:T(8,128)(2,1)} %convolution_convert_fusion.1), kind=kLoop, calls=%fused_computation.2 | loop fusion | flops 21233664 | bytes 31850496 | tf_op jit(solution)/shard_map/convert_element_type | solution.py:364
  631.1 6.5 fusion.17
  639.0 10.9 %collective-permute-start.36 = (bf16[128,2304]{1,0:T(8,128)(2,1)}, bf16[128,2304]{1,0:T(8,128)(2,1)}, u32[]{:S(2)}, u32[]{:S(2)}) collective-permute-start(bf16[128,2304]{1,0:T(8,128)(2,1)} %get-tuple-element.82), channel_id=1, source_target_pairs={{0,1},{1,2},{2,3},{3,0},{4,5},{5,6},{6,7},{7,4},{8,9},{9,10},{10,1... | collective-permute-start | bytes 1769480 | tf_op jit(solution)/shard_map/ppermute | solution.py:57
  656.6 10.5 %collective-permute-done.36 = bf16[128,2304]{1,0:T(8,128)(2,1)} collective-permute-done((bf16[128,2304]{1,0:T(8,128)(2,1)}, bf16[128,2304]{1,0:T(8,128)(2,1)}, u32[]{:S(2)}, u32[]{:S(2)}) %collective-permute-start.36) | collective-permute-done | bytes 589856 | tf_op jit(solution)/shard_map/ppermute | solution.py:57
  667.1 15.6 %collective-permute-start.42 = (f32[4,2304]{1,0:T(4,128)}, f32[4,2304]{1,0:T(4,128)}, u32[]{:S(2)}, u32[]{:S(2)}) collective-permute-start(f32[4,2304]{1,0:T(4,128)} %concatenate.86), channel_id=1, source_target_pairs={{0,3},{1,0},{2,1},{3,2},{4,7},{5,4},{6,5},{7,6},{8,11},{9,8},{10,9... | collective-permute-start | bytes 110600 | tf_op jit(solution)/shard_map/ppermute | solution.py:57
  682.7 23.4 %collective-permute-done.34 = bf16[128,2304]{1,0:T(8,128)(2,1)} collective-permute-done((bf16[128,2304]{1,0:T(8,128)(2,1)}, bf16[128,2304]{1,0:T(8,128)(2,1)}, u32[]{:S(2)}, u32[]{:S(2)}) %collective-permute-start.34) | collective-permute-done | bytes 589856 | tf_op jit(solution)/shard_map/ppermute | solution.py:57
  717.6 5.1 concatenate.79
  731.4 9.6 %collective-permute-done.37 = bf16[128,2304]{1,0:T(8,128)(2,1)S(1)} collective-permute-done((bf16[128,2304]{1,0:T(8,128)(2,1)}, bf16[128,2304]{1,0:T(8,128)(2,1)S(1)}, u32[]{:S(2)}, u32[]{:S(2)}) %collective-permute-start.37) | collective-permute-done | bytes 589856 | tf_op jit(solution)/shard_map/ppermute | solution.py:57
  741.1 24.2 %collective-permute-done.38 = bf16[128,2304]{1,0:T(8,128)(2,1)S(1)} collective-permute-done((bf16[128,2304]{1,0:T(8,128)(2,1)}, bf16[128,2304]{1,0:T(8,128)(2,1)S(1)}, u32[]{:S(2)}, u32[]{:S(2)}) %collective-permute-start.38) | collective-permute-done | bytes 589856 | tf_op jit(solution)/shard_map/ppermute | solution.py:57
  773.0 66.9 %reduce-scatter.6.cloned.1.call-done = bf16[288,4608]{1,0:T(8,128)(2,1)} async-done(((bf16[1152,4608]{1,0:T(8,128)(2,1)}), bf16[288,4608]{1,0:T(8,128)(2,1)}) %reduce-scatter.6.cloned.1.call-update) | async-done | bytes 2654224 | tf_op jit(solution)/shard_map/reduce_scatter | solution.py:234
  839.9 4.5 slice_convert_fusion
  (344 shorter events, 205.8 us)
Async XLA Ops:
  7.2 54.7 %all-gather.3.cloned.1.call-start = ((), (), s32[]{:S(2)}) async-start(), calls=%async_computation.3 | async-start | bytes 7962624 | tf_op jit(solution)/shard_map/all_gather | solution.py:185
  9.6 275.3 %all-gather.5.cloned.1.call-start = ((), (), s32[]{:S(2)}) async-start(), calls=%async_computation.4 | async-start | bytes 35831808 | tf_op jit(solution)/shard_map/all_gather | solution.py:185
  12.8 398.3 %all-reduce.4.cloned.1.call-start = ((), (), s32[]{:S(2)}) async-start(), calls=%async_computation.5 | async-start | bytes 4718592 | tf_op jit(solution)/shard_map/psum | solution.py:337
  68.4 18.3 %collective-permute-start = (bf16[384,512]{1,0:T(8,128)(2,1)}, bf16[384,512]{1,0:T(8,128)(2,1)}, u32[]{:S(2)}, u32[]{:S(2)}) collective-permute-start(bf16[384,512]{1,0:T(8,128)(2,1)} %slice.284), channel_id=1, source_target_pairs={{0,4},{1,5},{2,6},{3,7},{8,12},{9,13},{10,14},{11,15},{16,20},{17,... | collective-permute-start | bytes 1179656 | tf_op jit(solution)/shard_map/ppermute | solution.py:21
  113.9 14.3 %collective-permute-start.3 = (bf16[128,2304]{1,0:T(8,128)(2,1)S(1)}, bf16[128,2304]{1,0:T(8,128)(2,1)S(1)}, u32[]{:S(2)}, u32[]{:S(2)}) collective-permute-start(bf16[128,2304]{1,0:T(8,128)(2,1)S(1)} %get-tuple-element.55), channel_id=1, source_target_pairs={{0,1},{1,2},{4,5},{5,6},{8,9},{9,10},{12,13},{13,14},{16,17},{17,1... | collective-permute-start | bytes 1769480 | tf_op jit(solution)/shard_map/ppermute | solution.py:45
  130.1 28.7 %collective-permute-start.6 = (bf16[128,2304]{1,0:T(8,128)(2,1)}, bf16[128,2304]{1,0:T(8,128)(2,1)S(1)}, u32[]{:S(2)}, u32[]{:S(2)}) collective-permute-start(bf16[128,2304]{1,0:T(8,128)(2,1)} %add_convert_fusion.2), channel_id=1, source_target_pairs={{1,0},{2,1},{3,2},{5,4},{6,5},{7,6},{9,8},{10,9},{11,10},{13,12},{... | collective-permute-start | bytes 1769480 | tf_op jit(solution)/shard_map/ppermute | solution.py:45
  131.4 27.4 %collective-permute-start.5 = (bf16[128,2304]{1,0:T(8,128)(2,1)}, bf16[128,2304]{1,0:T(8,128)(2,1)S(1)}, u32[]{:S(2)}, u32[]{:S(2)}) collective-permute-start(bf16[128,2304]{1,0:T(8,128)(2,1)} %add_convert_fusion.3), channel_id=1, source_target_pairs={{0,1},{1,2},{2,3},{4,5},{5,6},{6,7},{8,9},{9,10},{10,11},{12,13},{... | collective-permute-start | bytes 1769480 | tf_op jit(solution)/shard_map/ppermute | solution.py:45
  137.4 46.3 %collective-permute-start.19 = (bf16[288,512]{1,0:T(8,128)(2,1)}, bf16[288,512]{1,0:T(8,128)(2,1)}, u32[]{:S(2)}, u32[]{:S(2)}) collective-permute-start(bf16[288,512]{1,0:T(8,128)(2,1)} %param.24), channel_id=1, source_target_pairs={{0,1},{1,2},{2,3},{3,0},{4,5},{5,6},{6,7},{7,4},{8,9},{9,10},{10,1... | collective-permute-start | bytes 884744 | tf_op jit(solution)/shard_map/ppermute | solution.py:57
  139.5 46.1 %collective-permute-start.20 = (bf16[288,512]{1,0:T(8,128)(2,1)}, bf16[288,512]{1,0:T(8,128)(2,1)}, u32[]{:S(2)}, u32[]{:S(2)}) collective-permute-start(bf16[288,512]{1,0:T(8,128)(2,1)} %param.24), channel_id=1, source_target_pairs={{0,2},{1,3},{2,0},{3,1},{4,6},{5,7},{6,4},{7,5},{8,10},{9,11},{10,... | collective-permute-start | bytes 884744 | tf_op jit(solution)/shard_map/ppermute | solution.py:57
  139.5 47.8 %collective-permute-start.21 = (bf16[288,512]{1,0:T(8,128)(2,1)}, bf16[288,512]{1,0:T(8,128)(2,1)}, u32[]{:S(2)}, u32[]{:S(2)}) collective-permute-start(bf16[288,512]{1,0:T(8,128)(2,1)} %param.24), channel_id=1, source_target_pairs={{0,3},{1,0},{2,1},{3,2},{4,7},{5,4},{6,5},{7,6},{8,11},{9,8},{10,9... | collective-permute-start | bytes 884744 | tf_op jit(solution)/shard_map/ppermute | solution.py:57
  164.8 25.8 %collective-permute-start.7 = (bf16[128,2304]{1,0:T(8,128)(2,1)}, bf16[128,2304]{1,0:T(8,128)(2,1)}, u32[]{:S(2)}, u32[]{:S(2)}) collective-permute-start(bf16[128,2304]{1,0:T(8,128)(2,1)} %get-tuple-element.110), channel_id=1, source_target_pairs={{0,1},{1,2},{2,3},{4,5},{5,6},{6,7},{8,9},{9,10},{10,11},{12,13},{... | collective-permute-start | bytes 1769480 | tf_op jit(solution)/shard_map/ppermute | solution.py:45
  173.2 17.4 %collective-permute-start.8 = (bf16[128,2304]{1,0:T(8,128)(2,1)}, bf16[128,2304]{1,0:T(8,128)(2,1)}, u32[]{:S(2)}, u32[]{:S(2)}) collective-permute-start(bf16[128,2304]{1,0:T(8,128)(2,1)} %get-tuple-element.110), channel_id=1, source_target_pairs={{1,0},{2,1},{3,2},{5,4},{6,5},{7,6},{9,8},{10,9},{11,10},{13,12},{... | collective-permute-start | bytes 1769480 | tf_op jit(solution)/shard_map/ppermute | solution.py:45
  189.0 55.3 %collective-permute-start.22 = (bf16[288,2048]{1,0:T(8,128)(2,1)}, bf16[288,2048]{1,0:T(8,128)(2,1)}, u32[]{:S(2)}, u32[]{:S(2)}) collective-permute-start(bf16[288,2048]{1,0:T(8,128)(2,1)} %constant_dynamic-update-slice_fusion), channel_id=1, source_target_pairs={{0,20},{4,16},{8,28},{12,24},{16,4},{20,0},{24,12},{28,8},{1,21},{... | collective-permute-start | bytes 3538952 | tf_op jit(solution)/shard_map/ppermute | solution.py:197
  190.6 16.8 %collective-permute-start.9 = (bf16[128,2304]{1,0:T(8,128)(2,1)}, bf16[128,2304]{1,0:T(8,128)(2,1)}, u32[]{:S(2)}, u32[]{:S(2)}) collective-permute-start(bf16[128,2304]{1,0:T(8,128)(2,1)} %collective-permute-done.7), channel_id=1, source_target_pairs={{1,2},{2,3},{5,6},{6,7},{9,10},{10,11},{13,14},{14,15},{17,18},{18... | collective-permute-start | bytes 1769480 | tf_op jit(solution)/shard_map/ppermute | solution.py:45
  192.1 15.3 %collective-permute-start.10 = (bf16[128,2304]{1,0:T(8,128)(2,1)}, bf16[128,2304]{1,0:T(8,128)(2,1)}, u32[]{:S(2)}, u32[]{:S(2)}) collective-permute-start(bf16[128,2304]{1,0:T(8,128)(2,1)} %collective-permute-done.8), channel_id=1, source_target_pairs={{1,0},{2,1},{5,4},{6,5},{9,8},{10,9},{13,12},{14,13},{17,16},{18,1... | collective-permute-start | bytes 1769480 | tf_op jit(solution)/shard_map/ppermute | solution.py:45
  202.2 65.8 %collective-permute-start.23 = (bf16[288,2048]{1,0:T(8,128)(2,1)}, bf16[288,2048]{1,0:T(8,128)(2,1)}, u32[]{:S(2)}, u32[]{:S(2)}) collective-permute-start(bf16[288,2048]{1,0:T(8,128)(2,1)} %constant_dynamic-update-slice_fusion), channel_id=1, source_target_pairs={{0,4},{4,0},{8,12},{12,8},{16,20},{20,16},{24,28},{28,24},{1,5},{5... | collective-permute-start | bytes 3538952 | tf_op jit(solution)/shard_map/ppermute | solution.py:197
  203.1 64.9 %collective-permute-start.24 = (bf16[288,2048]{1,0:T(8,128)(2,1)}, bf16[288,2048]{1,0:T(8,128)(2,1)}, u32[]{:S(2)}, u32[]{:S(2)}) collective-permute-start(bf16[288,2048]{1,0:T(8,128)(2,1)} %constant_dynamic-update-slice_fusion), channel_id=1, source_target_pairs={{0,16},{4,20},{8,24},{12,28},{16,0},{20,4},{24,8},{28,12},{1,17},{... | collective-permute-start | bytes 3538952 | tf_op jit(solution)/shard_map/ppermute | solution.py:197
  207.4 61.2 %collective-permute-start.11 = (bf16[128,2304]{1,0:T(8,128)(2,1)}, bf16[128,2304]{1,0:T(8,128)(2,1)S(1)}, u32[]{:S(2)}, u32[]{:S(2)}) collective-permute-start(bf16[128,2304]{1,0:T(8,128)(2,1)} %collective-permute-done.9), channel_id=1, source_target_pairs={{2,3},{6,7},{10,11},{14,15},{18,19},{22,23},{26,27},{30,31}} | collective-permute-start | bytes 1769480 | tf_op jit(solution)/shard_map/ppermute | solution.py:45
  208.1 60.5 %collective-permute-start.12 = (bf16[128,2304]{1,0:T(8,128)(2,1)}, bf16[128,2304]{1,0:T(8,128)(2,1)S(1)}, u32[]{:S(2)}, u32[]{:S(2)}) collective-permute-start(bf16[128,2304]{1,0:T(8,128)(2,1)} %collective-permute-done.10), channel_id=1, source_target_pairs={{1,0},{5,4},{9,8},{13,12},{17,16},{21,20},{25,24},{29,28}} | collective-permute-start | bytes 1769480 | tf_op jit(solution)/shard_map/ppermute | solution.py:45
  244.3 77.1 %collective-permute-start.25 = (bf16[288,2048]{1,0:T(8,128)(2,1)}, bf16[288,2048]{1,0:T(8,128)(2,1)}, u32[]{:S(2)}, u32[]{:S(2)}) collective-permute-start(bf16[288,2048]{1,0:T(8,128)(2,1)} %constant_dynamic-update-slice_fusion), channel_id=1, source_target_pairs={{0,8},{4,12},{8,0},{12,4},{16,24},{20,28},{24,16},{28,20},{1,9},{5... | collective-permute-start | bytes 3538952 | tf_op jit(solution)/shard_map/ppermute | solution.py:197
  268.0 203.7 %collective-permute-start.28 = (bf16[288,2048]{1,0:T(8,128)(2,1)}, bf16[288,2048]{1,0:T(8,128)(2,1)}, u32[]{:S(2)}, u32[]{:S(2)}) collective-permute-start(bf16[288,2048]{1,0:T(8,128)(2,1)} %collective-permute-done.22), channel_id=1, source_target_pairs={{0,8},{4,12},{8,0},{12,4},{16,24},{20,28},{24,16},{28,20},{1,9},{5... | collective-permute-start | bytes 3538952 | tf_op jit(solution)/shard_map/ppermute | solution.py:197
  268.0 56.1 %collective-permute-start.26 = (bf16[288,2048]{1,0:T(8,128)(2,1)}, bf16[288,2048]{1,0:T(8,128)(2,1)}, u32[]{:S(2)}, u32[]{:S(2)}) collective-permute-start(bf16[288,2048]{1,0:T(8,128)(2,1)} %collective-permute-done.23), channel_id=1, source_target_pairs={{0,8},{4,12},{8,0},{12,4},{16,24},{20,28},{24,16},{28,20},{1,9},{5... | collective-permute-start | bytes 3538952 | tf_op jit(solution)/shard_map/ppermute | solution.py:197
  268.5 58.0 %collective-permute-start.27 = (bf16[288,2048]{1,0:T(8,128)(2,1)}, bf16[288,2048]{1,0:T(8,128)(2,1)}, u32[]{:S(2)}, u32[]{:S(2)}) collective-permute-start(bf16[288,2048]{1,0:T(8,128)(2,1)} %collective-permute-done.24), channel_id=1, source_target_pairs={{0,8},{4,12},{8,0},{12,4},{16,24},{20,28},{24,16},{28,20},{1,9},{5... | collective-permute-start | bytes 3538952 | tf_op jit(solution)/shard_map/ppermute | solution.py:197
  316.1 449.3 %reduce-scatter.4.cloned.1.call-start = ((), (), s32[]{:S(2)}) async-start(), calls=%async_computation.6 | async-start | bytes 4423680 | tf_op jit(solution)/shard_map/reduce_scatter | solution.py:234
  456.6 18.4 %collective-permute-start.18 = (bf16[128,1024]{1,0:T(8,128)(2,1)S(1)}, bf16[128,1024]{1,0:T(8,128)(2,1)S(1)}, u32[]{:S(2)}, u32[]{:S(2)}) collective-permute-start(bf16[128,1024]{1,0:T(8,128)(2,1)S(1)} %get-tuple-element.73), channel_id=1, source_target_pairs={{0,1},{1,2},{2,3},{3,0},{4,5},{5,6},{6,7},{7,4},{8,9},{9,10},{10,1... | collective-permute-start | bytes 786440 | tf_op jit(solution)/shard_map/ppermute | solution.py:57
  456.8 24.1 %collective-permute-start.17 = (bf16[128,1024]{1,0:T(8,128)(2,1)S(1)}, bf16[128,1024]{1,0:T(8,128)(2,1)S(1)}, u32[]{:S(2)}, u32[]{:S(2)}) collective-permute-start(bf16[128,1024]{1,0:T(8,128)(2,1)S(1)} %get-tuple-element.72), channel_id=1, source_target_pairs={{0,3},{1,0},{2,1},{3,2},{4,7},{5,4},{6,5},{7,6},{8,11},{9,8},{10,9... | collective-permute-start | bytes 786440 | tf_op jit(solution)/shard_map/ppermute | solution.py:57
  460.4 29.9 %collective-permute-start.16 = (bf16[128,1024]{1,0:T(8,128)(2,1)S(1)}, bf16[128,1024]{1,0:T(8,128)(2,1)S(1)}, u32[]{:S(2)}, u32[]{:S(2)}) collective-permute-start(bf16[128,1024]{1,0:T(8,128)(2,1)S(1)} %get-tuple-element.71), channel_id=1, source_target_pairs={{0,2},{1,3},{2,0},{3,1},{4,6},{5,7},{6,4},{7,5},{8,10},{9,11},{10,... | collective-permute-start | bytes 786440 | tf_op jit(solution)/shard_map/ppermute | solution.py:57
  471.1 19.4 %collective-permute-start.15 = (bf16[128,1280]{1,0:T(8,128)(2,1)S(1)}, bf16[128,1280]{1,0:T(8,128)(2,1)S(1)}, u32[]{:S(2)}, u32[]{:S(2)}) collective-permute-start(bf16[128,1280]{1,0:T(8,128)(2,1)S(1)} %get-tuple-element.69), channel_id=1, source_target_pairs={{0,1},{1,2},{2,3},{3,0},{4,5},{5,6},{6,7},{7,4},{8,9},{9,10},{10,1... | collective-permute-start | bytes 983048 | tf_op jit(solution)/shard_map/ppermute | solution.py:57
  471.7 21.2 %collective-permute-start.14 = (bf16[128,1280]{1,0:T(8,128)(2,1)S(1)}, bf16[128,1280]{1,0:T(8,128)(2,1)S(1)}, u32[]{:S(2)}, u32[]{:S(2)}) collective-permute-start(bf16[128,1280]{1,0:T(8,128)(2,1)S(1)} %get-tuple-element.68), channel_id=1, source_target_pairs={{0,3},{1,0},{2,1},{3,2},{4,7},{5,4},{6,5},{7,6},{8,11},{9,8},{10,9... | collective-permute-start | bytes 983048 | tf_op jit(solution)/shard_map/ppermute | solution.py:57
  475.0 35.6 %collective-permute-start.13 = (bf16[128,1280]{1,0:T(8,128)(2,1)S(1)}, bf16[128,1280]{1,0:T(8,128)(2,1)S(1)}, u32[]{:S(2)}, u32[]{:S(2)}) collective-permute-start(bf16[128,1280]{1,0:T(8,128)(2,1)S(1)} %get-tuple-element.67), channel_id=1, source_target_pairs={{0,2},{1,3},{2,0},{3,1},{4,6},{5,7},{6,4},{7,5},{8,10},{9,11},{10,... | collective-permute-start | bytes 983048 | tf_op jit(solution)/shard_map/ppermute | solution.py:57
  514.4 53.3 %collective-permute-start.47 = (bf16[128,2304]{1,0:T(8,128)(2,1)S(1)}, bf16[128,2304]{1,0:T(8,128)(2,1)S(1)}, u32[]{:S(2)}, u32[]{:S(2)}) collective-permute-start(bf16[128,2304]{1,0:T(8,128)(2,1)S(1)} %fusion.73), channel_id=1, source_target_pairs={{0,1},{1,2},{2,3},{3,0},{4,5},{5,6},{6,7},{7,4},{8,9},{9,10},{10,1... | collective-permute-start | bytes 1769480 | tf_op jit(solution)/shard_map/ppermute | solution.py:57
  519.7 19.8 %collective-permute-start.29 = (bf16[128,512]{1,0:T(8,128)(2,1)S(1)}, bf16[128,512]{1,0:T(8,128)(2,1)S(1)}, u32[]{:S(2)}, u32[]{:S(2)}) collective-permute-start(bf16[128,512]{1,0:T(8,128)(2,1)S(1)} %get-tuple-element.75), channel_id=1, source_target_pairs={{0,2},{1,3},{2,0},{3,1},{4,6},{5,7},{6,4},{7,5},{8,10},{9,11},{10,... | collective-permute-start | bytes 393224 | tf_op jit(solution)/shard_map/ppermute | solution.py:57
  521.4 18.0 %collective-permute-start.30 = (bf16[128,512]{1,0:T(8,128)(2,1)S(1)}, bf16[128,512]{1,0:T(8,128)(2,1)S(1)}, u32[]{:S(2)}, u32[]{:S(2)}) collective-permute-start(bf16[128,512]{1,0:T(8,128)(2,1)S(1)} %get-tuple-element.76), channel_id=1, source_target_pairs={{0,3},{1,0},{2,1},{3,2},{4,7},{5,4},{6,5},{7,6},{8,11},{9,8},{10,9... | collective-permute-start | bytes 393224 | tf_op jit(solution)/shard_map/ppermute | solution.py:57
  523.6 15.9 %collective-permute-start.31 = (bf16[128,512]{1,0:T(8,128)(2,1)S(1)}, bf16[128,512]{1,0:T(8,128)(2,1)S(1)}, u32[]{:S(2)}, u32[]{:S(2)}) collective-permute-start(bf16[128,512]{1,0:T(8,128)(2,1)S(1)} %get-tuple-element.77), channel_id=1, source_target_pairs={{0,1},{1,2},{2,3},{3,0},{4,5},{5,6},{6,7},{7,4},{8,9},{9,10},{10,1... | collective-permute-start | bytes 393224 | tf_op jit(solution)/shard_map/ppermute | solution.py:57
  539.5 29.9 %collective-permute-start.48 = (bf16[128,2304]{1,0:T(8,128)(2,1)S(1)}, bf16[128,2304]{1,0:T(8,128)(2,1)}, u32[]{:S(2)}, u32[]{:S(2)}) collective-permute-start(bf16[128,2304]{1,0:T(8,128)(2,1)S(1)} %fusion.73), channel_id=1, source_target_pairs={{0,2},{1,3},{2,0},{3,1},{4,6},{5,7},{6,4},{7,5},{8,10},{9,11},{10,... | collective-permute-start | bytes 1769480 | tf_op jit(solution)/shard_map/ppermute | solution.py:57
  541.8 28.7 %collective-permute-start.49 = (bf16[128,2304]{1,0:T(8,128)(2,1)S(1)}, bf16[128,2304]{1,0:T(8,128)(2,1)}, u32[]{:S(2)}, u32[]{:S(2)}) collective-permute-start(bf16[128,2304]{1,0:T(8,128)(2,1)S(1)} %fusion.73), channel_id=1, source_target_pairs={{0,3},{1,0},{2,1},{3,2},{4,7},{5,4},{6,5},{7,6},{8,11},{9,8},{10,9... | collective-permute-start | bytes 1769480 | tf_op jit(solution)/shard_map/ppermute | solution.py:57
  586.1 183.7 %reduce-scatter.8.cloned.1.call-start = ((), (), s32[]{:S(2)}) async-start(), calls=%async_computation.8 | async-start | bytes 11943936 | tf_op jit(solution)/shard_map/reduce_scatter | solution.py:241
  586.7 253.2 %reduce-scatter.6.cloned.1.call-start = ((), (), s32[]{:S(2)}) async-start(), calls=%async_computation.7 | async-start | bytes 13271040 | tf_op jit(solution)/shard_map/reduce_scatter | solution.py:234
  598.3 16.7 %collective-permute-start.51 = (bf16[1152,4608]{1,0:T(8,128)(2,1)}, bf16[1152,4608]{1,0:T(8,128)(2,1)}, u32[]{:S(2)}, u32[]{:S(2)}) collective-permute-start(bf16[1152,4608]{1,0:T(8,128)(2,1)} %convolution_convert_fusion), channel_id=1, source_target_pairs={{0,8},{8,0},{16,24},{24,16},{1,9},{9,1},{17,25},{25,17},{2,10},{10... | collective-permute-start | bytes 31850504 | tf_op jit(solution)/shard_map/ppermute | solution.py:225
  639.0 28.1 %collective-permute-start.36 = (bf16[128,2304]{1,0:T(8,128)(2,1)}, bf16[128,2304]{1,0:T(8,128)(2,1)}, u32[]{:S(2)}, u32[]{:S(2)}) collective-permute-start(bf16[128,2304]{1,0:T(8,128)(2,1)} %get-tuple-element.82), channel_id=1, source_target_pairs={{0,1},{1,2},{2,3},{3,0},{4,5},{5,6},{6,7},{7,4},{8,9},{9,10},{10,1... | collective-permute-start | bytes 1769480 | tf_op jit(solution)/shard_map/ppermute | solution.py:57
  650.0 32.7 %collective-permute-start.35 = (bf16[128,2304]{1,0:T(8,128)(2,1)}, bf16[128,2304]{1,0:T(8,128)(2,1)}, u32[]{:S(2)}, u32[]{:S(2)}) collective-permute-start(bf16[128,2304]{1,0:T(8,128)(2,1)} %get-tuple-element.81), channel_id=1, source_target_pairs={{0,3},{1,0},{2,1},{3,2},{4,7},{5,4},{6,5},{7,6},{8,11},{9,8},{10,9... | collective-permute-start | bytes 1769480 | tf_op jit(solution)/shard_map/ppermute | solution.py:57
  652.6 53.5 %collective-permute-start.34 = (bf16[128,2304]{1,0:T(8,128)(2,1)}, bf16[128,2304]{1,0:T(8,128)(2,1)}, u32[]{:S(2)}, u32[]{:S(2)}) collective-permute-start(bf16[128,2304]{1,0:T(8,128)(2,1)} %get-tuple-element.80), channel_id=1, source_target_pairs={{0,2},{1,3},{2,0},{3,1},{4,6},{5,7},{6,4},{7,5},{8,10},{9,11},{10,... | collective-permute-start | bytes 1769480 | tf_op jit(solution)/shard_map/ppermute | solution.py:57
  654.3 57.8 %collective-permute-start.40 = (f32[4,2304]{1,0:T(4,128)}, f32[4,2304]{1,0:T(4,128)}, u32[]{:S(2)}, u32[]{:S(2)}) collective-permute-start(f32[4,2304]{1,0:T(4,128)} %concatenate.86), channel_id=1, source_target_pairs={{0,1},{1,2},{2,3},{3,0},{4,5},{5,6},{6,7},{7,4},{8,9},{9,10},{10,1... | collective-permute-start | bytes 110600 | tf_op jit(solution)/shard_map/ppermute | solution.py:57
  656.3 55.8 %collective-permute-start.41 = (f32[4,2304]{1,0:T(4,128)}, f32[4,2304]{1,0:T(4,128)}, u32[]{:S(2)}, u32[]{:S(2)}) collective-permute-start(f32[4,2304]{1,0:T(4,128)} %concatenate.86), channel_id=1, source_target_pairs={{0,2},{1,3},{2,0},{3,1},{4,6},{5,7},{6,4},{7,5},{8,10},{9,11},{10,... | collective-permute-start | bytes 110600 | tf_op jit(solution)/shard_map/ppermute | solution.py:57
  667.1 45.0 %collective-permute-start.42 = (f32[4,2304]{1,0:T(4,128)}, f32[4,2304]{1,0:T(4,128)}, u32[]{:S(2)}, u32[]{:S(2)}) collective-permute-start(f32[4,2304]{1,0:T(4,128)} %concatenate.86), channel_id=1, source_target_pairs={{0,3},{1,0},{2,1},{3,2},{4,7},{5,4},{6,5},{7,6},{8,11},{9,8},{10,9... | collective-permute-start | bytes 110600 | tf_op jit(solution)/shard_map/ppermute | solution.py:57
  722.7 18.3 %collective-permute-start.37 = (bf16[128,2304]{1,0:T(8,128)(2,1)}, bf16[128,2304]{1,0:T(8,128)(2,1)S(1)}, u32[]{:S(2)}, u32[]{:S(2)}) collective-permute-start(bf16[128,2304]{1,0:T(8,128)(2,1)} %concatenate.85), channel_id=1, source_target_pairs={{0,1},{1,2},{2,3},{3,0},{4,5},{5,6},{6,7},{7,4},{8,9},{9,10},{10,1... | collective-permute-start | bytes 1769480 | tf_op jit(solution)/shard_map/ppermute | solution.py:57
  722.7 42.6 %collective-permute-start.38 = (bf16[128,2304]{1,0:T(8,128)(2,1)}, bf16[128,2304]{1,0:T(8,128)(2,1)S(1)}, u32[]{:S(2)}, u32[]{:S(2)}) collective-permute-start(bf16[128,2304]{1,0:T(8,128)(2,1)} %concatenate.85), channel_id=1, source_target_pairs={{0,2},{1,3},{2,0},{3,1},{4,6},{5,7},{6,4},{7,5},{8,10},{9,11},{10,... | collective-permute-start | bytes 1769480 | tf_op jit(solution)/shard_map/ppermute | solution.py:57
  723.7 41.6 %collective-permute-start.39 = (bf16[128,2304]{1,0:T(8,128)(2,1)}, bf16[128,2304]{1,0:T(8,128)(2,1)S(1)}, u32[]{:S(2)}, u32[]{:S(2)}) collective-permute-start(bf16[128,2304]{1,0:T(8,128)(2,1)} %concatenate.85), channel_id=1, source_target_pairs={{0,3},{1,0},{2,1},{3,2},{4,7},{5,4},{6,5},{7,6},{8,11},{9,8},{10,9... | collective-permute-start | bytes 1769480 | tf_op jit(solution)/shard_map/ppermute | solution.py:57
  (73 other events, 862.0 us)
Sparse Core Ops, SparseCore 0:
  10.5 51.4 all-gather.2
  63.8 209.7 all-gather.4
  316.3 94.8 all-reduce.3
  586.2 59.3 reduce-scatter.3
  649.0 83.4 reduce-scatter.7
  735.4 104.4 reduce-scatter.5
